TPU v7x, 32 devices: a whole 2x2x4 slice. The times are simulated.
32 devices in a mesh: rep: 8 (over y, x, core), shard: 4 (over z).
Axes of the slice: x: 2, y: 2, z: 4, core: 2. Of those that a mesh axis runs over, the one named last changes fastest.
Arguments:
- tokens: bfloat16 [2, 8192, 2048], P(None, ('rep', 'shard')), may hold values from -6 to 6
- cotangent: bfloat16 [2, 8192, 2048], P(None, ('rep', 'shard')), may hold values from -6 to 6
- lengths: int32 [2, 8, 2], P(None, 'rep'), may hold values from 1 to 768, 1024 in all within a row
- decay_rates: float32 [16], replicated, may hold values from 0.00048828125 to 0.05
- w_query: bfloat16 [2048, 2048], P('shard'), may hold values from -0.125 to 0.125
- w_key: bfloat16 [2048, 2048], P('shard'), may hold values from -0.125 to 0.125
- w_value: bfloat16 [2048, 2048], P('shard'), may hold values from -0.125 to 0.125
- w_gate: bfloat16 [2048, 2048], P('shard'), may hold values from -0.125 to 0.125
- w_out: bfloat16 [2048, 2048], P('shard'), may hold values from -0.125 to 0.125
- w_one: bfloat16 [2048, 5632], P('shard'), may hold values from -0.125 to 0.125
- w_two: bfloat16 [2048, 5632], P('shard'), may hold values from -0.125 to 0.125
- w_down: bfloat16 [2048, 5632], P('shard'), may hold values from -0.078125 to 0.078125
Outputs:
- output: bfloat16 [2, 8192, 2048], P(None, ('rep', 'shard'))
- input_grad: bfloat16 [2, 8192, 2048], P(None, ('rep', 'shard'))
- grad_query: float32 [2048, 2048], P('shard')
- grad_key: float32 [2048, 2048], P('shard')
- grad_value: float32 [2048, 2048], P('shard')
- grad_gate: float32 [2048, 2048], P('shard')
- grad_out: float32 [2048, 2048], P('shard')
- grad_one: float32 [2048, 5632], P('shard')
- grad_two: float32 [2048, 5632], P('shard')
- grad_down: float32 [2048, 5632], P('shard')
Inputs may be any that keep to these rules, and one draw needn't show every extreme that they name: Each row of lengths sums to 1024, and its largest entry is at most 768.
All inputs are finite; a program needn't handle non-finite values.
Results may differ from a plain program's by a relative error of at most 0.022.
Values may be sent and summed in bfloat16 or wider, within the bound.
No kernel may reach another device: no remote copies, remote signals or barrier semaphores. Data moves between devices by JAX's collectives and lax.ppermute only.
A program may use at most 640 MiB of HBM per device.

v0:
```python
import jax
import jax.numpy as jnp
from jax import lax
from jax.sharding import PartitionSpec as P

HEADS = 16
HEAD_DIM = 128


epsilon = 1e-06
highest = lax.Precision.HIGHEST


def carried_in(x, axis, join, neutral, backward):
    count = lax.axis_size(axis)
    place = lax.axis_index(axis)
    ahead = count - 1 - place if backward else place
    gathered = jax.tree.map(
        lambda a, kind: lax.all_gather(a.astype(kind), axis), x, (jnp.bfloat16, jnp.bfloat16)
    )
    state = jax.tree.map(lambda a, e: jnp.zeros_like(a) + jnp.asarray(e, a.dtype), x, neutral)

    def one(turn, state):
        source = count - 1 - turn if backward else turn
        return join(
            state,
            jax.tree.map(
                lambda a, own: lax.dynamic_index_in_dim(a, source, 0, False).astype(own.dtype),
                gathered,
                x,
            ),
        )

    return lax.fori_loop(0, ahead, one, state)


def normed(values):
    return values * lax.rsqrt(jnp.mean(values * values, axis=-1, keepdims=True) + epsilon)


def norm_back(source, upstream):
    factor = lax.rsqrt(jnp.mean(source * source, axis=-1, keepdims=True) + epsilon)
    scaled = source * factor
    return factor * (upstream - scaled * jnp.mean(scaled * upstream, axis=-1, keepdims=True))


def silu_back(preact, upstream):
    sigmoid = jax.nn.sigmoid(preact)
    return upstream * sigmoid * (1.0 + preact * (1.0 - sigmoid))


def matmul(former, latter):
    return jnp.dot(former, latter, preferred_element_type=jnp.float32)


def times_transposed(former, latter):
    return lax.dot_general(
        former, latter, (((1,), (1,)), ((), ())), preferred_element_type=jnp.float32
    )


def cross_tokens(former, latter):
    return lax.dot_general(
        former, latter, (((0,), (0,)), ((), ())), preferred_element_type=jnp.float32
    )


def carry_state(earlier, latter):
    return (earlier[0] * latter[0], latter[1] + latter[0][:, None, None] * earlier[1])


def segment_ids(lengths_row, positions):
    seq_ends = jnp.cumsum(lengths_row)
    return jnp.sum((seq_ends[None, :] <= positions[:, None]).astype(jnp.int32), axis=1)


def fold_rows(inputs, portions):
    return tuple((matmul(inputs, portion) for portion in portions))


def fold_columns(upstreams, portions):
    column_block = times_transposed(upstreams[0], portions[0])
    for member in range(1, len(upstreams)):
        column_block = column_block + times_transposed(upstreams[member], portions[member])
    return column_block


def body(
    tokens,
    cotangent,
    lengths,
    decay_rates,
    w_query,
    w_key,
    w_value,
    w_gate,
    w_out,
    w_one,
    w_two,
    w_down,
):
    micro_count, tok_rows, width = tokens.shape
    hidden_units = w_one.shape[1]
    local_pos = jnp.arange(tok_rows, dtype=jnp.int32)
    global_pos = lax.axis_index("shard") * tok_rows + local_pos
    gap = local_pos[:, None] - local_pos[None, :]
    decay_gap = jnp.exp(
        -decay_rates[:, None, None] * jnp.maximum(gap, 0).astype(jnp.float32)[None, :, :]
    )
    inflow_decay = jnp.exp(-decay_rates[:, None] * (local_pos + 1).astype(jnp.float32)[None, :])
    tail_decay = jnp.exp(
        -decay_rates[:, None] * (tok_rows - 1 - local_pos).astype(jnp.float32)[None, :]
    )
    block_decay = jnp.exp(-decay_rates * jnp.float32(tok_rows))
    identity = (
        jnp.ones((HEADS,), jnp.float32),
        jnp.zeros((HEADS, HEAD_DIM, HEAD_DIM), jnp.float32),
    )
    outputs = []
    input_grads = []
    kept_hidden_one = []
    kept_attn_factors = []
    kept_hidden_two = []
    kept_ffn_factors = []
    kept_tail_left = []
    kept_branch = []
    kept_product = []
    for micro_batch in range(micro_count):
        lengths_row = lengths[micro_batch, 0]
        segments = segment_ids(lengths_row, global_pos)
        seg_before = segment_ids(lengths_row, global_pos[:1] - 1)[0]
        seg_last = segments[tok_rows - 1]
        same_seg = (gap >= 0) & (segments[:, None] == segments[None, :])
        mask = jnp.where(same_seg[None, :, :], decay_gap, jnp.float32(0.0))
        inflow = inflow_decay * (segments == seg_before).astype(jnp.float32)[None, :]
        tail = tail_decay * (segments == seg_last).astype(jnp.float32)[None, :]
        keep_factor = block_decay * (seg_last == seg_before).astype(jnp.float32)
        inflow_rows = jnp.transpose(inflow)[:, :, None]
        tail_rows = jnp.transpose(tail)[:, :, None]
        source = tokens[micro_batch].astype(jnp.float32)
        hidden_one = normed(source).astype(jnp.bfloat16)
        query_pre, key_pre, value_pre, gate_pre = fold_rows(
            hidden_one,
            (
                lax.all_gather(w_query, "shard", axis=0, tiled=True),
                lax.all_gather(w_key, "shard", axis=0, tiled=True),
                lax.all_gather(w_value, "shard", axis=0, tiled=True),
                lax.all_gather(w_gate, "shard", axis=0, tiled=True),
            ),
        )
        q_heads = jax.nn.silu(query_pre).astype(jnp.bfloat16).reshape(tok_rows, HEADS, HEAD_DIM)
        k_heads = jax.nn.silu(key_pre).astype(jnp.bfloat16).reshape(tok_rows, HEADS, HEAD_DIM)
        v_heads = value_pre.astype(jnp.bfloat16).reshape(tok_rows, HEADS, HEAD_DIM)
        q_float = q_heads.astype(jnp.float32)
        k_float = k_heads.astype(jnp.float32)
        v_float = v_heads.astype(jnp.float32)
        scores = jnp.einsum("thd,shd->hts", q_heads, k_heads, preferred_element_type=jnp.float32)
        attn_weights = (scores * mask).astype(jnp.bfloat16)
        intra = jnp.einsum(
            "hts,shd->thd", attn_weights, v_heads, preferred_element_type=jnp.float32
        )
        state_local = jnp.einsum("shd,she->hde", k_float * tail_rows, v_float, precision=highest)
        scanned = carried_in((keep_factor, state_local), "shard", carry_state, identity, False)
        state_in = scanned[1]
        inter = inflow_rows * jnp.einsum("thd,hde->the", q_float, state_in, precision=highest)
        attended = (intra + inter).reshape(tok_rows, width)
        attn_normed = normed(attended)
        gated = (attn_normed * gate_pre).astype(jnp.bfloat16)
        middle = source + fold_rows(gated, (lax.all_gather(w_out, "shard", axis=0, tiled=True),))[0]
        hidden_two = normed(middle).astype(jnp.bfloat16)
        first_pre, second_pre = fold_rows(
            hidden_two,
            (
                lax.all_gather(w_one, "shard", axis=0, tiled=True),
                lax.all_gather(w_two, "shard", axis=0, tiled=True),
            ),
        )
        product = (first_pre * second_pre).astype(jnp.bfloat16)
        result = middle + times_transposed(
            product, lax.all_gather(w_down, "shard", axis=0, tiled=True)
        )
        outputs.append(result.astype(jnp.bfloat16))
        upstream = cotangent[micro_batch]
        d_product = fold_rows(upstream, (lax.all_gather(w_down, "shard", axis=0, tiled=True),))[0]
        d_first = (d_product * second_pre).astype(jnp.bfloat16)
        d_second = (d_product * first_pre).astype(jnp.bfloat16)
        d_hidden_two = fold_columns(
            (d_first, d_second),
            (
                lax.all_gather(w_one, "shard", axis=0, tiled=True),
                lax.all_gather(w_two, "shard", axis=0, tiled=True),
            ),
        )
        d_middle = upstream.astype(jnp.float32) + norm_back(middle, d_hidden_two)
        d_branch = d_middle.astype(jnp.bfloat16)
        d_gated = times_transposed(d_branch, lax.all_gather(w_out, "shard", axis=0, tiled=True))
        d_gate_pre = (d_gated * attn_normed).astype(jnp.bfloat16)
        d_attended = norm_back(attended, d_gated * gate_pre).astype(jnp.bfloat16)
        d_heads = d_attended.reshape(tok_rows, HEADS, HEAD_DIM)
        d_float = d_heads.astype(jnp.float32)
        d_weights = jnp.einsum("thd,shd->hts", d_heads, v_heads, preferred_element_type=jnp.float32)
        d_values = jnp.einsum(
            "hts,thd->shd", attn_weights, d_heads, preferred_element_type=jnp.float32
        )
        d_scores = (d_weights * mask).astype(jnp.bfloat16)
        d_queries = jnp.einsum(
            "hts,shd->thd", d_scores, k_heads, preferred_element_type=jnp.float32
        )
        d_queries = d_queries + inflow_rows * jnp.einsum(
            "the,hde->thd", d_float, state_in, precision=highest
        )
        d_keys = jnp.einsum("hts,thd->shd", d_scores, q_heads, preferred_element_type=jnp.float32)
        grad_in = jnp.einsum("thd,the->hde", q_float * inflow_rows, d_float, precision=highest)
        reversed_scan = carried_in((keep_factor, grad_in), "shard", carry_state, identity, True)
        grad_tail = reversed_scan[1]
        d_keys = d_keys + tail_rows * jnp.einsum(
            "she,hde->shd", v_float, grad_tail, precision=highest
        )
        d_values = d_values + tail_rows * jnp.einsum(
            "shd,hde->she", k_float, grad_tail, precision=highest
        )
        d_query_pre = silu_back(query_pre, d_queries.reshape(tok_rows, width)).astype(jnp.bfloat16)
        d_key_pre = silu_back(key_pre, d_keys.reshape(tok_rows, width)).astype(jnp.bfloat16)
        d_value_pre = d_values.reshape(tok_rows, width).astype(jnp.bfloat16)
        d_hidden_one = fold_columns(
            (d_query_pre, d_key_pre, d_value_pre, d_gate_pre),
            (
                lax.all_gather(w_query, "shard", axis=0, tiled=True),
                lax.all_gather(w_key, "shard", axis=0, tiled=True),
                lax.all_gather(w_value, "shard", axis=0, tiled=True),
                lax.all_gather(w_gate, "shard", axis=0, tiled=True),
            ),
        )
        input_grads.append((d_middle + norm_back(source, d_hidden_one)).astype(jnp.bfloat16))
        kept_hidden_one.append(hidden_one)
        kept_attn_factors.append(
            jnp.concatenate([d_query_pre, d_key_pre, d_value_pre, d_gate_pre], axis=1)
        )
        kept_hidden_two.append(hidden_two)
        kept_ffn_factors.append(jnp.concatenate([d_first, d_second], axis=1))
        kept_tail_left.append(gated)
        kept_tail_left.append(upstream)
        kept_branch.append(d_branch)
        kept_product.append(product)
    all_hidden_one = jnp.concatenate(kept_hidden_one, axis=0)
    all_attn_factors = jnp.concatenate(kept_attn_factors, axis=0)
    all_hidden_two = jnp.concatenate(kept_hidden_two, axis=0)
    all_ffn_factors = jnp.concatenate(kept_ffn_factors, axis=0)
    all_tail_left = jnp.concatenate(kept_tail_left, axis=0)
    tail_blocks = []
    for micro_batch in range(micro_count):
        tail_blocks.append(
            jnp.concatenate(
                [kept_branch[micro_batch], jnp.zeros((tok_rows, hidden_units), jnp.bfloat16)],
                axis=1,
            )
        )
        tail_blocks.append(
            jnp.concatenate(
                [jnp.zeros((tok_rows, width), jnp.bfloat16), kept_product[micro_batch]], axis=1
            )
        )
    all_tail_right = jnp.concatenate(tail_blocks, axis=0)
    attn_total = lax.psum_scatter(
        cross_tokens(all_hidden_one, all_attn_factors).astype(jnp.bfloat16),
        "shard",
        scatter_dimension=0,
        tiled=True,
    ).astype(jnp.float32)
    ffn_total = lax.psum_scatter(
        cross_tokens(all_hidden_two, all_ffn_factors).astype(jnp.bfloat16),
        "shard",
        scatter_dimension=0,
        tiled=True,
    ).astype(jnp.float32)
    tail_total = lax.psum_scatter(
        cross_tokens(all_tail_left, all_tail_right).astype(jnp.bfloat16),
        "shard",
        scatter_dimension=0,
        tiled=True,
    ).astype(jnp.float32)
    summed = (
        lax.psum(attn_total[:, 0:width].astype(jnp.bfloat16), "rep").astype(jnp.float32),
        lax.psum(attn_total[:, width : 2 * width].astype(jnp.bfloat16), "rep").astype(jnp.float32),
        lax.psum(attn_total[:, 2 * width : 3 * width].astype(jnp.bfloat16), "rep").astype(
            jnp.float32
        ),
        lax.psum(attn_total[:, 3 * width : 4 * width].astype(jnp.bfloat16), "rep").astype(
            jnp.float32
        ),
        lax.psum(tail_total[:, 0:width].astype(jnp.bfloat16), "rep").astype(jnp.float32),
        lax.psum(ffn_total[:, 0:hidden_units].astype(jnp.bfloat16), "rep").astype(jnp.float32),
        lax.psum(ffn_total[:, hidden_units : 2 * hidden_units].astype(jnp.bfloat16), "rep").astype(
            jnp.float32
        ),
        lax.psum(tail_total[:, width : width + hidden_units].astype(jnp.bfloat16), "rep").astype(
            jnp.float32
        ),
    )
    return (
        jnp.stack(outputs),
        jnp.stack(input_grads),
        summed[0],
        summed[1],
        summed[2],
        summed[3],
        summed[4],
        summed[5],
        summed[6],
        summed[7],
    )


def solution(mesh):
    placed = (
        P(None, ("rep", "shard"), None),
        P(None, ("rep", "shard"), None),
        P(None, "rep", None),
        P(),
        P("shard", None),
        P("shard", None),
        P("shard", None),
        P("shard", None),
        P("shard", None),
        P("shard", None),
        P("shard", None),
        P("shard", None),
    )
    return jax.shard_map(
        body,
        mesh=mesh,
        in_specs=placed,
        out_specs=(
            P(None, ("rep", "shard"), None),
            P(None, ("rep", "shard"), None),
            P("shard", None),
            P("shard", None),
            P("shard", None),
            P("shard", None),
            P("shard", None),
            P("shard", None),
            P("shard", None),
            P("shard", None),
        ),
        check_vma=False,
    )
```

profile of v0, /device:TPU:17, one launch (start us, length us, event | category | flops | bytes accessed | tf_op | source)
XLA Modules:
  0.0 5603.8 jit_solution(6157925069724339974)
XLA Ops:
  20.8 137.8 %all-gather.23.cloned.1.call-done = bf16[2048,2048]{1,0:T(8,128)(2,1)} async-done(((bf16[512,2048]{1,0:T(8,128)(2,1)}), bf16[2048,2048]{1,0:T(8,128)(2,1)}) %all-gather.23.cloned.1.call-update) | async-done | bytes 8388624 | tf_op jit(solution)/shard_map/all_gather | solution.py:146
  158.6 7.4 multiply_convert_fusion.19
  168.0 140.0 %all-gather.19.cloned.1.call-done = bf16[2048,2048]{1,0:T(8,128)(2,1)} async-done(((bf16[512,2048]{1,0:T(8,128)(2,1)}), bf16[2048,2048]{1,0:T(8,128)(2,1)}) %all-gather.19.cloned.1.call-update) | async-done | bytes 8388624 | tf_op jit(solution)/shard_map/all_gather | solution.py:147
  308.0 6.1 fusion.103
  317.4 8.0 multiply_convert_fusion.22
  327.5 6.2 fusion.102
  342.0 11.2 all-reduce.9
  355.7 102.0 %all-gather.21.cloned.1.call-done = bf16[2048,2048]{1,0:T(8,128)(2,1)} async-done(((bf16[512,2048]{1,0:T(8,128)(2,1)}), bf16[2048,2048]{1,0:T(8,128)(2,1)}) %all-gather.21.cloned.1.call-update) | async-done | bytes 8388624 | tf_op jit(solution)/shard_map/all_gather | solution.py:145
  457.7 7.4 multiply_convert_fusion.20
  466.4 8.2 multiply_convert_fusion.23
  486.3 18.1 all-gather.37.cloned.1.call-done
  514.9 36.2 all-gather.35.cloned.1.call-done
  562.3 138.1 %all-gather.25.cloned.1.call-done = bf16[2048,2048]{1,0:T(8,128)(2,1)} async-done(((bf16[512,2048]{1,0:T(8,128)(2,1)}), bf16[2048,2048]{1,0:T(8,128)(2,1)}) %all-gather.25.cloned.1.call-update) | async-done | bytes 8388624 | tf_op jit(solution)/shard_map/all_gather | solution.py:148
  700.4 8.1 multiply_convert_fusion.18
  708.5 141.4 %all-gather.27.cloned.1.call-done = bf16[2048,2048]{1,0:T(8,128)(2,1)} async-done(((bf16[512,2048]{1,0:T(8,128)(2,1)}), bf16[2048,2048]{1,0:T(8,128)(2,1)}) %all-gather.27.cloned.1.call-update) | async-done | bytes 8388624 | tf_op jit(solution)/shard_map/all_gather | solution.py:169
  849.9 6.5 multiply_reduce_fusion.4
  868.7 372.3 %all-gather.29.cloned.1.call-done = bf16[2048,5632]{1,0:T(8,128)(2,1)} async-done(((bf16[512,5632]{1,0:T(8,128)(2,1)}), bf16[2048,5632]{1,0:T(8,128)(2,1)}) %all-gather.29.cloned.1.call-update) | async-done | bytes 23068688 | tf_op jit(solution)/shard_map/all_gather | solution.py:174
  1240.9 12.9 fusion.173
  1253.8 378.1 %all-gather.31.cloned.1.call-done = bf16[2048,5632]{1,0:T(8,128)(2,1)} async-done(((bf16[512,5632]{1,0:T(8,128)(2,1)}), bf16[2048,5632]{1,0:T(8,128)(2,1)}) %all-gather.31.cloned.1.call-update) | async-done | bytes 23068688 | tf_op jit(solution)/shard_map/all_gather | solution.py:175
  1631.9 13.0 fusion.174
  1645.0 377.8 %all-gather.33.cloned.1.call-done = bf16[2048,5632]{1,0:T(8,128)(2,1)} async-done(((bf16[512,5632]{1,0:T(8,128)(2,1)}), bf16[2048,5632]{1,0:T(8,128)(2,1)}) %all-gather.33.cloned.1.call-update) | async-done | bytes 23068688 | tf_op jit(solution)/shard_map/all_gather | solution.py:180
  2022.8 18.1 multiply_convert_fusion.2
  2040.9 12.5 fusion.177
  2053.4 13.8 multiply_reduce_fusion.3
  2067.2 13.5 fusion.175
  2080.7 13.2 fusion.176
  2093.9 18.1 multiply_convert_fusion
  2112.0 12.5 fusion.182
  2124.5 14.2 multiply_reduce_fusion.1
  2144.3 7.5 multiply_reduce_fusion
  2163.5 7.9 multiply_reduce_fusion.2
  2199.9 39.6 convolution_convert_fusion.1
  2278.8 47.9 convolution_convert_fusion.2
  2328.5 36.0 convolution_convert_fusion
  2365.3 2090.2 %all-reduce.16.cloned.1.call-done = (bf16[2048,8192]{1,0:T(8,128)(2,1)}, bf16[2048,7680]{1,0:T(8,128)(2,1)}) async-done(((bf16[2048,8192]{1,0:T(8,128)(2,1)}, bf16[2048,7680]{1,0:T(8,128)(2,1)}), (bf16[2048,8192]{1,0:T(8,128)(2,1)}, bf16[2048,7680]{1,0:T(8,128)(2,1)})) %all-reduce.16.cloned.1.call-update) | async-done | bytes 65011728
  4455.5 8.4 dynamic-slice.11
  4467.7 11.0 fusion.170
  4478.7 734.4 %reduce-scatter.2.cloned.1.call-done = bf16[512,11264]{1,0:T(8,128)(2,1)} async-done(((bf16[2048,11264]{1,0:T(8,128)(2,1)}), bf16[512,11264]{1,0:T(8,128)(2,1)}) %reduce-scatter.2.cloned.1.call-update) | async-done | bytes 11534352 | tf_op jit(solution)/shard_map/reduce_scatter | solution.py:270
  5213.2 9.5 fusion.171
  5224.3 12.9 fusion.60
  5237.1 13.5 fusion.61
  5253.5 6.3 fusion.184
  5259.9 7.6 fusion.179
  5276.7 6.5 convolution_add_fusion.4
  5285.9 7.9 convolution_add_fusion.8
  5293.9 7.1 fusion.67
  5305.2 258.0 %all-reduce.14.cloned.1.call-done = (bf16[512,2048]{1,0:T(8,128)(2,1)}, bf16[512,2048]{1,0:T(8,128)(2,1)}, bf16[512,2048]{1,0:T(8,128)(2,1)}, bf16[512,2048]{1,0...) async-done(((bf16[512,2048]{1,0:T(8,128)(2,1)}, bf16[512,2048]{1,0:T(8,128)(2,1)}, ...) | async-done | bytes 27787280 | tf_op jit(solution)/shard_map/psum | solution.py:283
  5579.2 5.9 convert_element_type.464
  (414 shorter events, 220.4 us)
Async XLA Ops:
  7.2 151.4 %all-gather.23.cloned.1.call-start = ((), (), s32[]{:S(2)}) async-start(), calls=%async_computation.3 | async-start | bytes 10485760 | tf_op jit(solution)/shard_map/all_gather | solution.py:146
  7.9 8.2 copy-start.107
  7.9 8.3 copy-start.9
  7.9 300.0 %all-gather.19.cloned.1.call-start = ((), (), s32[]{:S(2)}) async-start(), calls=%async_computation.1 | async-start | bytes 10485760 | tf_op jit(solution)/shard_map/all_gather | solution.py:147
  8.7 449.0 %all-gather.21.cloned.1.call-start = ((), (), s32[]{:S(2)}) async-start(), calls=%async_computation.2 | async-start | bytes 10485760 | tf_op jit(solution)/shard_map/all_gather | solution.py:145
  9.4 494.9 %all-gather.37.cloned.1.call-start = ((), (), s32[]{:S(2)}) async-start(), calls=%async_computation.11 | async-start | bytes 2621440 | tf_op jit(solution)/shard_map/all_gather | solution.py:19
  16.2 465.3 %copy-start.103 = (f32[16]{0:T(128)}, f32[16]{0:T(128)S(1)}, u32[]{:S(2)}) copy-start(f32[16]{0:T(128)S(1)} %get-tuple-element.370) | copy-start | bytes 196
  19.4 294.6 %copy-start.82 = (f32[256,16]{0,1:T(8,128)}, f32[256,16]{0,1:T(8,128)S(1)}, u32[]{:S(2)}) copy-start(f32[256,16]{0,1:T(8,128)S(1)} %get-tuple-element.366) | copy-start | bytes 49156
  19.4 314.2 %copy-start.80 = (f32[256,16]{0,1:T(8,128)}, f32[256,16]{0,1:T(8,128)S(1)}, u32[]{:S(2)}) copy-start(f32[256,16]{0,1:T(8,128)S(1)} %get-tuple-element.367) | copy-start | bytes 49156
  19.4 487.7 %copy-start.76 = (f32[256,16]{0,1:T(8,128)}, f32[256,16]{0,1:T(8,128)S(1)}, u32[]{:S(2)}) copy-start(f32[256,16]{0,1:T(8,128)S(1)} %get-tuple-element.355) | copy-start | bytes 49156
  19.5 534.4 %copy-start.74 = (f32[256,16]{0,1:T(8,128)}, f32[256,16]{0,1:T(8,128)S(1)}, u32[]{:S(2)}) copy-start(f32[256,16]{0,1:T(8,128)S(1)} %get-tuple-element.354) | copy-start | bytes 49156
  20.8 306.6 %copy-start.71 = (bf16[256,2048]{1,0:T(8,128)(2,1)}, bf16[256,2048]{1,0:T(8,128)(2,1)S(1)}, u32[]{:S(2)}) copy-start(bf16[256,2048]{1,0:T(8,128)(2,1)S(1)} %get-tuple-element.352) | copy-start | bytes 3145732
  168.0 146.1 %copy-start.43 = (bf16[256,16,128]{0,2,1:T(8,128)(2,1)}, bf16[256,16,128]{0,2,1:T(8,128)(2,1)S(1)}, u32[]{:S(2)}) copy-start(bf16[256,16,128]{0,2,1:T(8,128)(2,1)S(1)} %copy.121) | copy-start | bytes 3145732
  317.2 233.9 %all-gather.35.cloned.1.call-start = ((), (), s32[]{:S(2)}) async-start(), calls=%async_computation.10 | async-start | bytes 2621440 | tf_op jit(solution)/shard_map/all_gather | solution.py:19
  336.7 363.7 %all-gather.25.cloned.1.call-start = ((), (), s32[]{:S(2)}) async-start(), calls=%async_computation.4 | async-start | bytes 10485760 | tf_op jit(solution)/shard_map/all_gather | solution.py:148
  337.3 512.6 %all-gather.27.cloned.1.call-start = ((), (), s32[]{:S(2)}) async-start(), calls=%async_computation.5 | async-start | bytes 10485760 | tf_op jit(solution)/shard_map/all_gather | solution.py:169
  338.1 902.9 %all-gather.29.cloned.1.call-start = ((), (), s32[]{:S(2)}) async-start(), calls=%async_computation.6 | async-start | bytes 28835840 | tf_op jit(solution)/shard_map/all_gather | solution.py:174
  338.8 1293.1 %all-gather.31.cloned.1.call-start = ((), (), s32[]{:S(2)}) async-start(), calls=%async_computation.7 | async-start | bytes 28835840 | tf_op jit(solution)/shard_map/all_gather | solution.py:175
  339.5 14.7 copy-start.4
  339.6 1683.2 %all-gather.33.cloned.1.call-start = ((), (), s32[]{:S(2)}) async-start(), calls=%async_computation.8 | async-start | bytes 28835840 | tf_op jit(solution)/shard_map/all_gather | solution.py:180
  340.1 1904.8 %all-gather.41.cloned.1.call-start = ((), (), s32[]{:S(2)}) async-start(), calls=%async_computation.13 | async-start | bytes 2621440 | tf_op jit(solution)/shard_map/all_gather | solution.py:19
  353.5 128.0 %copy-start.78 = (f32[256,256]{1,0:T(8,128)}, f32[256,256]{1,0:T(8,128)S(1)}, u32[]{:S(2)}) copy-start(f32[256,256]{1,0:T(8,128)S(1)} %maximum_convert_fusion) | copy-start | bytes 786436
  354.2 127.3 %copy-start.84 = (pred[256,256]{1,0:T(8,128)(4,1)}, pred[256,256]{1,0:T(8,128)(4,1)S(1)}, u32[]{:S(2)}) copy-start(pred[256,256]{1,0:T(8,128)(4,1)S(1)} %get-tuple-element.399) | copy-start | bytes 196612
  558.7 141.7 %copy-start.73 = (bf16[256,2048]{1,0:T(8,128)(2,1)S(1)}, bf16[256,2048]{1,0:T(8,128)(2,1)}, u32[]{:S(2)}) copy-start(bf16[256,2048]{1,0:T(8,128)(2,1)} %get-tuple-element.353) | copy-start | bytes 3145732
  562.3 146.2 %copy-start.97 = (f32[256]{0:T(256)}, f32[256]{0:T(256)S(1)}, u32[]{:S(2)}) copy-start(f32[256]{0:T(256)S(1)} %add_rsqrt_fusion.1) | copy-start | bytes 3076
  849.9 11.1 slice-start
  856.4 9.8 copy-start.12
  856.4 1282.3 %copy-start.87 = (f32[256]{0:T(256)}, f32[256]{0:T(256)S(1)}, u32[]{:S(2)}) copy-start(f32[256]{0:T(256)S(1)} %add_rsqrt_fusion) | copy-start | bytes 3076
  866.2 1272.6 %copy-start.89 = (f32[256]{0:T(256)}, f32[256]{0:T(256)S(1)}, u32[]{:S(2)}) copy-start(f32[256]{0:T(256)S(1)} %add_rsqrt_fusion.3) | copy-start | bytes 3076
  866.4 1214.3 %copy-start.70 = (bf16[256,2048]{1,0:T(8,128)(2,1)}, bf16[256,2048]{1,0:T(8,128)(2,1)S(1)}, u32[]{:S(2)}) copy-start(bf16[256,2048]{1,0:T(8,128)(2,1)S(1)} %multiply_convert_fusion.24) | copy-start | bytes 3145732
  2067.2 71.6 %copy-start.91 = (f32[256]{0:T(256)}, f32[256]{0:T(256)S(1)}, u32[]{:S(2)}) copy-start(f32[256]{0:T(256)S(1)} %broadcast_multiply_fusion.5) | copy-start | bytes 3076
  2163.2 94.3 %all-gather.39.cloned.1.call-start = ((), (), s32[]{:S(2)}) async-start(), calls=%async_computation.12 | async-start | bytes 2621440 | tf_op jit(solution)/shard_map/all_gather | solution.py:19
  2178.7 9.2 copy-start.22
  2199.4 2256.1 %all-reduce.16.cloned.1.call-start = ((), (), s32[]{:S(2)}) async-start(), calls=%async_computation.15 | async-start | bytes 130023424
  2199.9 39.7 copy-start.23
  2326.7 2886.4 %reduce-scatter.2.cloned.1.call-start = ((), (), s32[]{:S(2)}) async-start(), calls=%async_computation.9 | async-start | bytes 57671680 | tf_op jit(solution)/shard_map/reduce_scatter | solution.py:270
  2364.6 3198.6 %all-reduce.14.cloned.1.call-start = ((), (), s32[]{:S(2)}) async-start(), calls=%async_computation.14 | async-start | bytes 55574528 | tf_op jit(solution)/shard_map/psum | solution.py:283
  5253.5 14.0 slice-start.8
  5259.9 7.6 copy-start.69
  5259.9 7.6 slice-start.9
  5259.9 11.3 slice-start.10
  5285.9 7.9 copy-start.11
  5285.9 7.9 copy-start.64
  5285.9 7.9 copy-start.100
  5285.9 7.9 copy-start.102
  5570.0 9.1 slice-start.6
  5576.5 8.6 slice-start.4
  5579.2 11.9 slice-start.2
  (94 other events, 353.3 us)
Sparse Core Ops, SparseCore 0:
  9.6 148.9 all-gather.22
  160.1 147.8 all-gather.18
  309.6 148.1 all-gather.20
  459.7 44.5 all-gather.36
  506.3 44.6 all-gather.34
  552.5 147.8 all-gather.24
  702.0 147.8 all-gather.26
  851.5 389.4 all-gather.28
  1242.5 389.3 all-gather.30
  1633.4 389.3 all-gather.32
  2163.4 44.5 all-gather.40
  2209.4 44.6 all-gather.38
  2326.8 2128.6 all-reduce.15
  4457.8 755.2 reduce-scatter.1
  5222.8 340.3 all-reduce.13
where the time goes:
time: 5610 us; the launch traced here: 5600 us
  waiting for transfers between devices  4930 us (88%)
  matrix products  484 us (9%)
  local copies, waits for them, and re-layouts  85.7 us (2%)
  other arithmetic  71.7 us (1%)
    unnamed x16, waiting for transfers between devices  2100 us
    reduce_scatter x1, waiting for transfers between devices, body(): lax.psum_scatter(cross_tokens(all_hidden_two, all_ffn_factors).astype(jnp...  734 us
    all_gather x1, waiting for transfers between devices, body(): lax.all_gather(w_two, 'shard', axis=0, tiled=True)  378 us
    all_gather x1, waiting for transfers between devices, body(): lax.all_gather(w_down, 'shard', axis=0, tiled=True)  378 us
    all_gather x1, waiting for transfers between devices, body(): lax.all_gather(w_one, 'shard', axis=0, tiled=True)  372 us
    psum x1, waiting for transfers between devices, body(): lax.psum(attn_total[:, 0:width].astype(jnp.bfloat16), 'rep')  258 us
    dot_general x16, matrix products, matmul(): return jnp.dot(former, latter, preferred_element_type=jnp.float32)  153 us
    dot_general x16, matrix products, times_transposed(): lax.dot_general(former, latter, (((1,), (1,)), ((), ())), preferred_eleme...  142 us
  transfers between devices with their start and end apart: 15, of which 13 were waited for; matrix products, arithmetic and copies ran while one was open for 7% of the time, Pallas kernels for 0%

commit v1 on v0

v1 whole, which is shorter than its diff:
```python
import functools

import jax
import jax.numpy as jnp
from jax import lax
from jax.experimental import pallas as pl
from jax.experimental.pallas import tpu as pltpu
from jax.sharding import PartitionSpec as P

HEADS = 16
HEAD_DIM = 128
STREAM = 1024
GROUP = 4
BLOCK = 256
EPSILON = 1e-06
AXES = ("rep", "shard")
LOW = jnp.bfloat16
F32 = jnp.float32


def matmul(former, latter):
    return jnp.dot(former, latter, preferred_element_type=F32)


def times_transposed(former, latter):
    return lax.dot_general(former, latter, (((1,), (1,)), ((), ())), preferred_element_type=F32)


def cross_tokens(former, latter):
    return lax.dot_general(former, latter, (((0,), (0,)), ((), ())), preferred_element_type=F32)


def masked_decay(rate, ends, first, columns):
    row = first + lax.broadcasted_iota(jnp.int32, (BLOCK, 1), 0)
    column = lax.broadcasted_iota(jnp.int32, (1, columns), 1)
    begin = jnp.zeros((BLOCK, 1), jnp.int32)
    for end in ends:
        begin = jnp.where(row >= end, end, begin)
    falling = jnp.exp(-rate * (row - first).astype(F32))
    rising = jnp.exp(rate * (column - first).astype(F32))
    allowed = (column <= row) & (column >= begin)
    return jnp.where(allowed, falling * rising, 0.0)


def attend_kernel(rates, ends, zq_ref, zk_ref, zv_ref, out_ref):
    stream, head = pl.program_id(0), pl.program_id(1)
    rate = rates[head]
    bounds = [ends[stream, i] for i in range(ends.shape[1])]
    zq, zk = zq_ref[...], zk_ref[...]
    q = (zq * jax.nn.sigmoid(zq)).astype(LOW)
    k = (zk * jax.nn.sigmoid(zk)).astype(LOW)
    v = zv_ref[...].astype(LOW)
    for first in range(0, STREAM, BLOCK):
        columns = first + BLOCK
        mask = masked_decay(rate, bounds, first, columns)
        scores = times_transposed(q[first:columns], k[:columns])
        weights = (scores * mask).astype(LOW)
        out_ref[first:columns, :] = matmul(weights, v[:columns])


def attend_back_kernel(
    rates, ends, zq_ref, zk_ref, zv_ref, do_ref, dzq_ref, dzk_ref, dzv_ref, dk_ref, dv_ref
):
    stream, head = pl.program_id(0), pl.program_id(1)
    rate = rates[head]
    bounds = [ends[stream, i] for i in range(ends.shape[1])]
    zq, zk = zq_ref[...], zk_ref[...]
    sig_q, sig_k = jax.nn.sigmoid(zq), jax.nn.sigmoid(zk)
    q = (zq * sig_q).astype(LOW)
    k = (zk * sig_k).astype(LOW)
    slope_q = sig_q * (1.0 + zq * (1.0 - sig_q))
    v = zv_ref[...].astype(LOW)
    d_o = do_ref[...]
    dk_ref[...] = jnp.zeros_like(dk_ref)
    dv_ref[...] = jnp.zeros_like(dv_ref)
    for first in range(0, STREAM, BLOCK):
        columns = first + BLOCK
        rows = slice(first, columns)
        mask = masked_decay(rate, bounds, first, columns)
        weights = (times_transposed(q[rows], k[:columns]) * mask).astype(LOW)
        d_scores = (times_transposed(d_o[rows], v[:columns]) * mask).astype(LOW)
        dzq_ref[rows, :] = (matmul(d_scores, k[:columns]) * slope_q[rows]).astype(LOW)
        dk_ref[:columns, :] += cross_tokens(d_scores, q[rows])
        dv_ref[:columns, :] += cross_tokens(weights, d_o[rows])
    dzk_ref[...] = (dk_ref[...] * (sig_k * (1.0 + zk * (1.0 - sig_k)))).astype(LOW)
    dzv_ref[...] = dv_ref[...].astype(LOW)


def head_block(offset=0):
    return pl.BlockSpec((STREAM, HEAD_DIM), lambda g, h, *_: (g, h + offset))


def attend(rates, ends, z_qk, z_vg):
    heads, streams = rates.shape[0], ends.shape[0]
    work = streams * heads * STREAM * STREAM
    return pl.pallas_call(
        attend_kernel,
        out_shape=jax.ShapeDtypeStruct((streams * STREAM, heads * HEAD_DIM), F32),
        grid_spec=pltpu.PrefetchScalarGridSpec(
            num_scalar_prefetch=2,
            grid=(streams, heads),
            in_specs=[head_block(), head_block(heads), head_block()],
            out_specs=head_block(),
        ),
        compiler_params=pltpu.CompilerParams(vmem_limit_bytes=40 << 20),
        cost_estimate=pl.CostEstimate(
            flops=4 * work * HEAD_DIM, transcendentals=work // 64,
            bytes_accessed=streams * heads * STREAM * HEAD_DIM * 16,
        ),
        name="attend",
    )(rates, ends, z_qk, z_qk, z_vg)


def attend_back(rates, ends, z_qk, z_vg, d_o):
    heads, streams = rates.shape[0], ends.shape[0]
    work = streams * heads * STREAM * STREAM
    return pl.pallas_call(
        attend_back_kernel,
        out_shape=[jax.ShapeDtypeStruct((streams * STREAM, heads * HEAD_DIM), LOW)] * 3,
        grid_spec=pltpu.PrefetchScalarGridSpec(
            num_scalar_prefetch=2,
            grid=(streams, heads),
            in_specs=[head_block(), head_block(heads), head_block(), head_block()],
            out_specs=[head_block()] * 3,
            scratch_shapes=[pltpu.VMEM((STREAM, HEAD_DIM), F32)] * 2,
        ),
        compiler_params=pltpu.CompilerParams(vmem_limit_bytes=40 << 20),
        cost_estimate=pl.CostEstimate(
            flops=10 * work * HEAD_DIM, transcendentals=work // 64,
            bytes_accessed=streams * heads * STREAM * HEAD_DIM * 20,
        ),
        name="attend_back",
    )(rates, ends, z_qk, z_qk, z_vg, d_o)


def body(reps, shards, tokens, cotangent, lengths, decay_rates, *weights):
    spread = reps // GROUP
    rep, place = lax.axis_index("rep"), lax.axis_index("shard")
    c, b, a = rep % 2, (rep // 2) % 2, rep // GROUP
    quarter = rep % GROUP
    micro, run, width = tokens.shape
    streams = micro * GROUP // shards
    per_block = STREAM // run // GROUP * streams

    def move(x, target):
        pairs = [(r * shards + s, target(r) * shards + s) for r in range(reps) for s in range(shards)]
        return lax.ppermute(x, AXES, pairs)

    def swap_c(x):
        return move(x, lambda r: r ^ 1)

    def swap_b(x):
        return move(x, lambda r: r ^ 2)

    def shift_a(x, k):
        return move(x, lambda r: (r + GROUP * k) % reps)

    def ordered(index, own, other, axis):
        return jnp.where(
            index == 0, jnp.stack([own, other], axis), jnp.stack([other, own], axis)
        )


    def origin(r, s, p):
        run_id = (r % GROUP) * per_block + p
        stream, part = run_id // shards, run_id % shards
        index = s * streams + stream if streams == 1 else s
        if streams == 1:
            batch, member = index // GROUP, index % GROUP
        else:
            batch, member = s // 2, 2 * stream + s % 2
        return (r // GROUP) * GROUP + member, part, batch

    def routes(p, batch):
        found = []
        for r in range(reps):
            for s in range(shards):
                from_r, from_s, from_batch = origin(r, s, p)
                if from_batch == batch:
                    found.append((from_r * shards + from_s, r * shards + s))
        return found

    def bring(x):
        slots = []
        for p in range(per_block):
            arrived = [lax.ppermute(x[m], AXES, routes(p, m)) for m in range(micro)]
            slots.append(functools.reduce(jnp.add, arrived))
        return jnp.concatenate(slots, axis=0)

    def bring_back(x):
        slots = x.reshape(per_block, run, width)
        batches = []
        for m in range(micro):
            arrived = [
                lax.ppermute(slots[p], AXES, [(d, o) for o, d in routes(p, m)])
                for p in range(per_block)
            ]
            batches.append(functools.reduce(jnp.add, arrived))
        return jnp.stack(batches)


    def gather_rows(x):
        both = ordered(b, x, swap_b(x), 0)
        return ordered(c, both, swap_c(both), 1).reshape(-1, x.shape[1])

    def gather_columns(x):
        both = ordered(b, x, swap_b(x), 0)
        four = ordered(c, both, swap_c(both), 1)
        return jnp.concatenate([four[i, j] for i in range(2) for j in range(2)], axis=1)

    def scatter_columns(x):
        cut = x.reshape(x.shape[0], 2, 2, -1)
        pick = functools.partial(lax.dynamic_index_in_dim, keepdims=False)
        kept = pick(cut, c, 2) + swap_c(pick(cut, 1 - c, 2).astype(LOW)).astype(F32)
        return pick(kept, b, 1) + swap_b(pick(kept, 1 - b, 1).astype(LOW)).astype(F32)

    def total(x):
        x = x + swap_c(x)
        return x + swap_b(x)

    def to_runs(x):
        cut = x.reshape(2, 2, -1, x.shape[1])
        pick = functools.partial(lax.dynamic_index_in_dim, keepdims=False)
        both = ordered(b, pick(cut, b, 0), swap_b(pick(cut, 1 - b, 0)), 0)
        four = ordered(c, pick(both, c, 1), swap_c(pick(both, 1 - c, 1)), 1)
        return bring_back(
            jnp.concatenate([four[i, j] for i in range(2) for j in range(2)], axis=1)
        )

    def own_columns(x):
        size = x.shape[1] // GROUP
        return lax.dynamic_slice_in_dim(x, quarter * size, size, 1)


    rows = weights[0].shape[0]
    part = rows // spread

    def whole(members):
        cut = [
            lax.dynamic_slice(
                w, (a * part, quarter * (w.shape[1] // GROUP)), (part, w.shape[1] // GROUP)
            )
            for w in members
        ]
        piece = jnp.concatenate(cut, axis=1) if len(cut) > 1 else cut[0]
        mine = lax.all_gather(piece, "shard", axis=0, tiled=True).reshape(shards, part, -1)
        relative = [mine] + [shift_a(mine, k) for k in range(1, spread)]
        if spread == 2:
            full = ordered(a, relative[0], relative[1], 1)
        else:
            stacked = jnp.stack(relative, 0)
            full = jnp.stack(
                [
                    lax.dynamic_index_in_dim(stacked, (a - j) % spread, 0, False)
                    for j in range(spread)
                ],
                1,
            )
        return full.reshape(shards * rows, -1)

    def by_owner(x):
        cut = x.reshape(x.shape[0], shards, spread, part)
        return [
            lax.dynamic_index_in_dim(cut, (a + k) % spread, 2, False).reshape(x.shape[0], -1)
            for k in range(spread)
        ]

    def summed(left, right):
        products = [cross_tokens(x, right).astype(LOW) for x in left]
        kept = products[0].astype(F32)
        for k in range(1, spread):
            kept = kept + shift_a(products[k], k).astype(F32)
        return lax.psum_scatter(kept.astype(LOW), "shard", scatter_dimension=0, tiled=True)

    def spread_out(x):
        relative = [x] + [shift_a(x, k) for k in range(1, spread)]
        if spread == 2:
            full = ordered(a, relative[0], relative[1], 0)
        else:
            stacked = jnp.stack(relative, 0)
            full = jnp.stack(
                [
                    lax.dynamic_index_in_dim(stacked, (a - j) % spread, 0, False)
                    for j in range(spread)
                ],
                0,
            )
        full = full.reshape(rows, -1)
        both = ordered(b, full, swap_b(full), 0)
        return ordered(c, both, swap_c(both), 1)

    def as_outputs(four, count):
        size = four.shape[3] // count
        return [
            jnp.concatenate(
                [four[i, j][:, n * size : (n + 1) * size] for i in range(2) for j in range(2)],
                axis=1,
            ).astype(F32)
            for n in range(count)
        ]


    w_query, w_key, w_value, w_gate, w_out, w_one, w_two, w_down = weights
    x_run = bring(tokens)
    x_all = gather_rows(x_run)
    w_qk = whole((w_query, w_key))
    w_vg = whole((w_value, w_gate))
    w_o = whole((w_out,))
    w_1 = whole((w_one,))
    w_2 = whole((w_two,))
    w_d = whole((w_down,))
    dy_all = gather_rows(bring(cotangent))

    heads = HEADS // GROUP
    rates = lax.dynamic_slice_in_dim(decay_rates, quarter * heads, heads, 0)
    cuts = lengths.reshape(1, -1)
    cuts = gather_rows(cuts).reshape(GROUP, micro, -1)
    if streams == 1:
        batch = place // GROUP
        chosen = lax.dynamic_slice_in_dim(cuts, place % GROUP, 1, 0)
    else:
        batch = place // 2
        chosen = lax.dynamic_index_in_dim(cuts.reshape(2, 2, micro, -1), place % 2, 1, False)
    chosen = lax.dynamic_index_in_dim(chosen, batch, 1, False)
    seq_ends = [chosen[:, 0]]
    for i in range(1, chosen.shape[1]):
        seq_ends.append(seq_ends[-1] + chosen[:, i])
    ends = jnp.stack(seq_ends, axis=1)


    x_float = x_all.astype(F32)
    x_scale = lax.rsqrt(jnp.mean(x_float * x_float, axis=-1, keepdims=True) + EPSILON)
    hidden_one = (x_float * x_scale).astype(LOW)
    z_qk = matmul(hidden_one, w_qk)
    z_vg = matmul(hidden_one, w_vg)
    attended = attend(rates, ends, z_qk, z_vg)
    gate = z_vg[:, z_vg.shape[1] // 2 :]
    o_scale = lax.rsqrt(total(jnp.sum(attended * attended, axis=-1)) / width + EPSILON)[:, None]
    o_normed = attended * o_scale
    gated = gather_columns((o_normed * gate).astype(LOW))
    x_own = own_columns(x_all).astype(F32)
    middle = x_own + matmul(gated, w_o)
    m_scale = lax.rsqrt(total(jnp.sum(middle * middle, axis=-1)) / width + EPSILON)[:, None]
    m_normed = middle * m_scale
    hidden_two = gather_columns(m_normed.astype(LOW))
    z_one = matmul(hidden_two, w_1)
    z_two = matmul(hidden_two, w_2)
    product = (z_one * z_two).astype(LOW)
    output = to_runs((middle + scatter_columns(times_transposed(product, w_d))).astype(LOW))


    g_down = summed(by_owner(dy_all), product)
    d_product = matmul(dy_all, w_d)
    d_one = (d_product * z_two).astype(LOW)
    d_two = (d_product * z_one).astype(LOW)
    second_left = by_owner(hidden_two)
    g_one = summed(second_left, d_one)
    g_two = summed(second_left, d_two)
    d_hidden = scatter_columns(times_transposed(d_one, w_1) + times_transposed(d_two, w_2))
    lean = total(jnp.sum(m_normed * d_hidden, axis=-1))[:, None] / width
    d_middle = own_columns(dy_all).astype(F32) + m_scale * (d_hidden - m_normed * lean)
    d_branch = d_middle.astype(LOW)
    d_gated = scatter_columns(times_transposed(d_branch, w_o))
    g_out = summed(by_owner(gated), d_branch)
    d_gate = (d_gated * o_normed).astype(LOW)
    d_normed = d_gated * gate
    lean = total(jnp.sum(o_normed * d_normed, axis=-1))[:, None] / width
    d_attended = (o_scale * (d_normed - o_normed * lean)).astype(LOW)
    d_query, d_key, d_value = attend_back(rates, ends, z_qk, z_vg, d_attended)
    d_qk = jnp.concatenate([d_query, d_key], axis=1)
    d_vg = jnp.concatenate([d_value, d_gate], axis=1)
    first_left = by_owner(hidden_one)
    g_qk = summed(first_left, d_qk)
    g_vg = summed(first_left, d_vg)
    d_hidden = scatter_columns(times_transposed(d_qk, w_qk) + times_transposed(d_vg, w_vg))
    x_normed = x_own * x_scale
    lean = total(jnp.sum(x_normed * d_hidden, axis=-1))[:, None] / width
    input_grad = to_runs((d_middle + x_scale * (d_hidden - x_normed * lean)).astype(LOW))

    grads = []
    for reduced, count in ((g_qk, 2), (g_vg, 2), (g_out, 1), (g_one, 1), (g_two, 1), (g_down, 1)):
        grads += as_outputs(spread_out(reduced), count)
    return (output, input_grad, *grads)


def solution(mesh):
    by_tokens = P(None, ("rep", "shard"), None)
    by_rows = P("shard", None)
    return jax.shard_map(
        functools.partial(body, mesh.shape["rep"], mesh.shape["shard"]),
        mesh=mesh,
        in_specs=(by_tokens, by_tokens, P(None, "rep", None), P(), *[by_rows] * 8),
        out_specs=(by_tokens, by_tokens, *[by_rows] * 8),
        check_vma=False,
    )
```

time: 5610 us -> 1890 us (0.34)
  waiting for transfers between devices: 4930 us -> 728 us
  local copies, waits for them, and re-layouts: 85.7 us -> 339 us
  other arithmetic: 71.7 us -> 290 us
  matrix products: 484 us -> 305 us
  starting transfers between devices: 1.35 us -> 151 us
    unnamed x16 -> x12, waiting for transfers between devices: 2100 us -> 0.2 us
    all_gather x12 -> x6, waiting for transfers between devices: 1840 us -> 0.01 us  [whole(): lax.all_gather(piece, 'shard', axis=0, tiled=True).reshape(shards, part, -1)]
    reduce_scatter x1 -> x6, waiting for transfers between devices: 734 us -> 15.9 us  [summed(): lax.psum_scatter(kept.astype(LOW), 'shard', scatter_dimension=0, tiled=True)]
    ppermute x0 -> x78, waiting for transfers between devices: none -> 711 us  [the longest x62 582 us: move(): return lax.ppermute(x, AXES, pairs)]
    psum x1 -> x0, waiting for transfers between devices: 258 us -> none  [body(): lax.psum(attn_total[:, 0:width].astype(jnp.bfloat16), 'rep')]
    dynamic_slice x0 -> x30, local copies, waits for them, and re-layouts: none -> 211 us  [the longest x8 133 us: by_owner(): lax.dynamic_index_in_dim(cut, (a + k) % spread, 2, False)]
    ppermute x0 -> x78, starting transfers between devices: none -> 151 us  [the longest x62 105 us: move(): return lax.ppermute(x, AXES, pairs)]
    select_n x0 -> x47, other arithmetic: none -> 137 us  [ordered(): jnp.where(index == 0, jnp.stack([own, other], axis), jnp.stack([other, ow...]
  transfers between devices with their start and end apart: 15 -> 90, of which waited for: 13 -> 37; matrix products, arithmetic and copies ran while one was open for 7% -> 42% of each run, Pallas kernels for 0% -> 2%
where the time goes in v1:
time: 1890 us; the launch traced here: 1860 us
  waiting for transfers between devices  728 us (39%)
  local copies, waits for them, and re-layouts  339 us (18%)
  matrix products  305 us (16%)
  other arithmetic  290 us (15%)
  starting transfers between devices  151 us (8%)
  Pallas kernels  34.1 us (2%)
    ppermute x62, waiting for transfers between devices, move(): return lax.ppermute(x, AXES, pairs)  582 us
    select_n x47, other arithmetic, ordered(): jnp.where(index == 0, jnp.stack([own, other], axis), jnp.stack([other, ow...  137 us
    dynamic_slice x8, local copies, waits for them, and re-layouts, by_owner(): lax.dynamic_index_in_dim(cut, (a + k) % spread, 2, False)  133 us
    dot_general x12, matrix products, cross_tokens(): lax.dot_general(former, latter, (((0,), (0,)), ((), ())), preferred_eleme...  107 us
    ppermute x62, starting transfers between devices, move(): return lax.ppermute(x, AXES, pairs)  105 us
    dot_general x6, matrix products, times_transposed(): lax.dot_general(former, latter, (((1,), (1,)), ((), ())), preferred_eleme...  105 us
    ppermute x8, waiting for transfers between devices, bring(): arrived = [lax.ppermute(x[m], AXES, routes(p, m)) for m in range(micro)]  100 us
    dot_general x6, matrix products, matmul(): return jnp.dot(former, latter, preferred_element_type=F32)  92.8 us
  transfers between devices with their start and end apart: 90, of which 37 were waited for; matrix products, arithmetic and copies ran while one was open for 42% of the time, Pallas kernels for 2%

profile of v1, /device:TPU:17, one launch (start us, length us, event | category | flops | bytes accessed | tf_op | source)
XLA Modules:
  0.0 1862.9 jit_solution(2956117436731913331)
XLA Ops:
  31.8 55.1 %collective-permute-done.3 = bf16[256,2048]{1,0:T(8,128)(2,1)} collective-permute-done((bf16[256,2048]{1,0:T(8,128)(2,1)}, bf16[256,2048]{1,0:T(8,128)(2,1)}, u32[]{:S(2)}, u32[]{:S(2)}) %collective-permute-start.3) | collective-permute-done | bytes 1048608 | tf_op jit(solution)/shard_map/ppermute | solution.py:186
  103.4 39.5 %collective-permute-done.4 = bf16[512,2048]{1,0:T(8,128)(2,1)} collective-permute-done((bf16[512,2048]{1,0:T(8,128)(2,1)}, bf16[512,2048]{1,0:T(8,128)(2,1)}, u32[]{:S(2)}, u32[]{:S(2)}) %collective-permute-start.4) | collective-permute-done | bytes 2097184 | tf_op jit(solution)/shard_map/ppermute | solution.py:147
  167.1 34.9 %collective-permute-done.8 = bf16[4,256,1024]{2,1,0:T(8,128)(2,1)} collective-permute-done((bf16[4,256,1024]{2,1,0:T(8,128)(2,1)}, bf16[4,256,1024]{2,1,0:T(8,128)(2,1)}, u32[]{:S(2)}, u32[]{:S(2)}) %collective-permute-start.8) | collective-permute-done | bytes 2097184 | tf_op jit(solution)/shard_map/ppermute | solution.py:147
  202.0 44.9 %collective-permute-done.9 = bf16[4,256,1024]{2,1,0:T(8,128)(2,1)} collective-permute-done((bf16[4,256,1024]{2,1,0:T(8,128)(2,1)}, bf16[4,256,1024]{2,1,0:T(8,128)(2,1)}, u32[]{:S(2)}, u32[]{:S(2)}) %collective-permute-start.9) | collective-permute-done | bytes 2097184 | tf_op jit(solution)/shard_map/ppermute | solution.py:147
  272.2 14.8 fusion.61.zv_ref
  296.2 12.7 attend.1
  334.0 28.1 %collective-permute-done.12 = bf16[2048,512]{1,0:T(8,128)(2,1)} collective-permute-done((bf16[2048,512]{1,0:T(8,128)(2,1)S(1)}, bf16[2048,512]{1,0:T(8,128)(2,1)}, u32[]{:S(2)}, u32[]{:S(2)}) %collective-permute-start.12) | collective-permute-done | bytes 2097184 | tf_op jit(solution)/shard_map/ppermute | solution.py:147
  369.8 36.6 %collective-permute-done.30 = bf16[256,2048]{1,0:T(8,128)(2,1)S(1)} collective-permute-done((bf16[256,2048]{1,0:T(8,128)(2,1)S(1)}, bf16[256,2048]{1,0:T(8,128)(2,1)S(1)}, u32[]{:S(2)}, u32[]{:S(2)}) %collective-permute-start.30) | collective-permute-done | bytes 1048608 | tf_op jit(solution)/shard_map/ppermute | solution.py:186
  411.7 12.5 collective-permute-done.14
  427.4 15.1 collective-permute-done.34
  446.9 16.2 collective-permute-start.35
  489.8 42.2 %collective-permute-done.19 = bf16[4,256,1408]{2,1,0:T(8,128)(2,1)} collective-permute-done((bf16[4,256,1408]{2,1,0:T(8,128)(2,1)}, bf16[4,256,1408]{2,1,0:T(8,128)(2,1)}, u32[]{:S(2)}, u32[]{:S(2)}) %collective-permute-start.19) | collective-permute-done | bytes 2883616 | tf_op jit(solution)/shard_map/ppermute | solution.py:147
  538.9 54.9 %collective-permute-done.20 = bf16[4,256,1408]{2,1,0:T(8,128)(2,1)} collective-permute-done((bf16[4,256,1408]{2,1,0:T(8,128)(2,1)}, bf16[4,256,1408]{2,1,0:T(8,128)(2,1)}, u32[]{:S(2)}, u32[]{:S(2)}) %collective-permute-start.20) | collective-permute-done | bytes 2883616 | tf_op jit(solution)/shard_map/ppermute | solution.py:147
  602.1 53.3 %collective-permute-done.21 = bf16[4,256,1408]{2,1,0:T(8,128)(2,1)S(1)} collective-permute-done((bf16[4,256,1408]{2,1,0:T(8,128)(2,1)}, bf16[4,256,1408]{2,1,0:T(8,128)(2,1)S(1)}, u32[]{:S(2)}, u32[]{:S(2)}) %collective-permute-start.21) | collective-permute-done | bytes 2883616 | tf_op jit(solution)/shard_map/ppermute | solution.py:147
  659.2 21.4 %reshape.1249 = f32[2048,4,2,256]{3,2,1,0:T(2,128)} reshape(bf16[2,2,512,2048]{3,2,1,0:T(8,128)(2,1)} %get-tuple-element.17) | data formatting | bytes 25165824 | tf_op jit(solution)/shard_map/convert_element_type | solution.py:331
  699.3 14.4 select_n.822
  721.1 18.9 %constant_dynamic-slice_fusion.4 = (bf16[2048,4,1,256]{3,2,1,0:T(2,128)(2,1)}, bf16[2048,4,1,256]{3,2,1,0:T(2,128)(2,1)}) fusion(bf16[2048,4,2,256]{3,2,1,0:T(2,128)(2,1)S(1)} %copy-done.8, s32[]{:T(128)S(6)} %select_n.781, s32[]{:T(128)S(6)} %select_n.783), kind=kLoop, calls=%fused_computation.211 | loop fusion | bytes 16777224 | tf_op jit(solution)/shard_map/jit(dynamic_index_in_dim)/dynamic_slice | solution.py:264
  740.0 20.1 %copy.117 = bf16[2048,4,1,256]{0,3,1,2:T(8,128)(2,1)} copy(bf16[2048,4,1,256]{3,2,1,0:T(2,128)(2,1)} %get-tuple-element.24) | data formatting | bytes 8388608 | tf_op jit(solution)/shard_map/jit(dynamic_index_in_dim)/dynamic_slice | solution.py:264
  760.1 12.0 multiply_convert_fusion
  784.0 18.9 %fusion.31 = f32[2048,1408]{1,0:T(8,128)} fusion(bf16[2048,1408]{1,0:T(8,128)(2,1)} %bitcast.471, bf16[2048,512]{1,0:T(8,128)(2,1)S(1)} %get-tuple-element.28, bf16[2048,512]{1,0:T(8,128)(2,1)} %get-tuple-element.31, bf16[2048,512]{1,0:T(8,128)(2,1)} %get-tuple-element.30, bf16[2048,512]{1,0:T(8,128)(2,1)} %get-tuple-element.29), kind=kOutput, calls=%fused_computation.166 | convolution fusion | flops 11844714496 | bytes 25690112 | tf_op jit(solution)/shard_map/dot_general | solution.py:22
  803.0 17.0 fusion.30
  820.0 26.0 %multiply_convert_fusion.2 = (bf16[2048,1408]{1,0:T(8,128)(2,1)}, bf16[2048,1408]{1,0:T(8,128)(2,1)}, bf16[2048,1408]{1,0:T(8,128)(2,1)}) fusion(f32[2048,1408]{1,0:T(8,128)} %fusion.31, f32[2048,1408]{1,0:T(8,128)} %fusion.30, bf16[2048,2048]{1,0:T(8,128)(2,1)} %bitcast.422, bf16[2048,1408]{1,0:T(8,128)(2,1)} %bitcast.465), kind=kOutput, calls=%fused_computation.3 | convolution fusion | flops 11828461568 | bytes 54525952 | tf_op jit(solution)/shard_map/dot_general | solution.py:22
  846.0 19.4 %fusion.62 = f32[2048,2048]{0,1:T(8,128)} fusion(bf16[2048,1408]{1,0:T(8,128)(2,1)} %get-tuple-element.22, bf16[2048,1408]{1,0:T(8,128)(2,1)} %bitcast.472), kind=kOutput, calls=%fused_computation.273 | convolution fusion | flops 11811160064 | bytes 28311552 | tf_op jit(solution)/shard_map/dot_general | solution.py:26
  888.1 11.2 convolution_convert_fusion.4
  900.5 23.0 %convolution_add_fusion = f32[2048,2048]{0,1:T(8,128)} fusion(f32[2048,2048]{0,1:T(8,128)} %fusion.62, bf16[2048,1408]{1,0:T(8,128)(2,1)} %get-tuple-element.20, bf16[2048,1408]{1,0:T(8,128)(2,1)} %bitcast.467), kind=kOutput, calls=%fused_computation.27 | convolution fusion | flops 11815354368 | bytes 45088768 | tf_op jit(solution)/shard_map/dot_general | solution.py:26
  936.9 11.9 convolution_convert_fusion.2
  949.0 13.9 collective-permute-done.66
  972.3 25.0 %fusion.8 = f32[2048,2,2,512]{3,0,2,1:T(8,128)S(1)} fusion(bf16[2,2,512,1408]{3,2,1,0:T(8,128)(2,1)} %bitcast.466, bf16[2048,1408]{1,0:T(8,128)(2,1)} %get-tuple-element.21), kind=kOutput, calls=%fused_computation.38 | convolution fusion | flops 11811160064 | bytes 28311552 | tf_op jit(solution)/shard_map/dot_general | solution.py:26
  1003.2 12.5 convolution_convert_fusion
  1035.8 20.3 %constant_dynamic-slice_fusion.10 = (bf16[2048,4,1,256]{3,2,1,0:T(2,128)(2,1)}, bf16[2048,4,1,256]{3,2,1,0:T(2,128)(2,1)}) fusion(bf16[2048,4,2,256]{3,2,1,0:T(2,128)(2,1)} %multiply_convert_fusion, s32[]{:T(128)S(6)} %select_n.781, s32[]{:T(128)S(6)} %select_n.783), kind=kLoop, calls=%fused_computation.217 | loop fusion | bytes 16777224 | tf_op jit(solution)/shard_map/jit(dynamic_index_in_dim)/dynamic_slice | solution.py:264
  1056.1 20.1 %copy.89 = bf16[2048,4,1,256]{0,3,1,2:T(8,128)(2,1)} copy(bf16[2048,4,1,256]{3,2,1,0:T(2,128)(2,1)} %get-tuple-element.46) | data formatting | bytes 8388608 | tf_op jit(solution)/shard_map/jit(dynamic_index_in_dim)/dynamic_slice | solution.py:264
  1076.2 20.1 %copy.88 = bf16[2048,4,1,256]{0,3,1,2:T(8,128)(2,1)} copy(bf16[2048,4,1,256]{3,2,1,0:T(2,128)(2,1)} %get-tuple-element.45) | data formatting | bytes 8388608 | tf_op jit(solution)/shard_map/jit(dynamic_index_in_dim)/dynamic_slice | solution.py:264
  1096.3 20.2 %copy.116 = bf16[2048,4,1,256]{0,3,1,2:T(8,128)(2,1)} copy(bf16[2048,4,1,256]{3,2,1,0:T(2,128)(2,1)} %get-tuple-element.23) | data formatting | bytes 8388608 | tf_op jit(solution)/shard_map/jit(dynamic_index_in_dim)/dynamic_slice | solution.py:264
  1154.3 11.1 bitcast_add_fusion.3
  1180.6 18.2 collective-permute-done.37
  1223.9 20.0 %collective-permute-done.39 = f32[2048]{0:T(1024)S(1)} collective-permute-done((f32[2048]{0:T(1024)S(1)}, f32[2048]{0:T(1024)S(1)}, u32[]{:S(2)}, u32[]{:S(2)}) %collective-permute-start.39) | collective-permute-done | bytes 8224 | tf_op jit(solution)/shard_map/ppermute | solution.py:147
  1362.1 13.2 collective-permute-done.26
  1380.0 72.3 %collective-permute-done.64 = bf16[512,512]{1,0:T(8,128)(2,1)S(1)} collective-permute-done((bf16[512,512]{1,0:T(8,128)(2,1)S(1)}, bf16[512,512]{1,0:T(8,128)(2,1)S(1)}, u32[]{:S(2)}, u32[]{:S(2)}) %collective-permute-start.64) | collective-permute-done | bytes 524320 | tf_op jit(solution)/shard_map/ppermute | solution.py:147
  1496.0 20.8 %collective-permute-done.41 = bf16[2048,512]{1,0:T(8,128)(2,1)S(1)} collective-permute-done((bf16[2048,512]{1,0:T(8,128)(2,1)S(1)}, bf16[2048,512]{1,0:T(8,128)(2,1)S(1)}, u32[]{:S(2)}, u32[]{:S(2)}) %collective-permute-start.41) | collective-permute-done | bytes 2097184 | tf_op jit(solution)/shard_map/ppermute | solution.py:147
  1525.3 21.3 %attend_back.1 = (bf16[2048,512]{1,0:T(8,128)(2,1)S(1)}, bf16[2048,512]{1,0:T(8,128)(2,1)S(1)}, bf16[2048,512]{1,0:T(8,128)(2,1)S(1)}) custom-call(f32[4]{0:T(128)S(1)} %dynamic_slice.141.rates, s32[2,2]{1,0:T(2,128)S(1)} %copy-done.4, f32[2048,1024]{1,0:T(8,128)} %copy-done.2, f32[2048,1024]{1,0:T(8,128)} %copy-done.2, f32[2048,1024]{1,0:T(8,128)} %fusion.61.zv_ref, ...), custom_call_target="tpu_custom_call" | custom-call | flops 10737418240 | bytes 20971520 | tf_op jit(solution)/shard_map/attend_back/pallas_call | solution.py:117
  1548.8 11.7 fusion.63
  1560.5 17.9 convolution_add_fusion.1
  1627.1 21.8 %collective-permute-done.54 = bf16[1024,1024]{1,0:T(8,128)(2,1)} collective-permute-done((bf16[1024,1024]{1,0:T(8,128)(2,1)}, bf16[1024,1024]{1,0:T(8,128)(2,1)}, u32[]{:S(2)}, u32[]{:S(2)}) %collective-permute-start.54) | collective-permute-done | bytes 2097184 | tf_op jit(solution)/shard_map/ppermute | solution.py:147
  1680.1 15.4 collective-permute-done.58
  1699.5 14.7 collective-permute-done.45
  1744.9 15.9 reduce-scatter.9.cloned.1.call-done
  1775.3 12.1 collective-permute-done.56
  1817.2 13.2 collective-permute-start.61
  (523 shorter events, 740.1 us)
Async XLA Ops:
  7.2 147.3 %all-gather.7.cloned.1.call-start = ((), (), s32[]{:S(2)}) async-start(), calls=%async_computation.6 | async-start | bytes 2621440 | tf_op jit(solution)/shard_map/all_gather | solution.py:246
  10.2 145.5 %all-gather.9.cloned.1.call-start = ((), (), s32[]{:S(2)}) async-start(), calls=%async_computation.7 | async-start | bytes 2621440 | tf_op jit(solution)/shard_map/all_gather | solution.py:246
  13.1 397.2 %all-gather.11.cloned.1.call-start = ((), (), s32[]{:S(2)}) async-start(), calls=%async_computation.8 | async-start | bytes 1310720 | tf_op jit(solution)/shard_map/all_gather | solution.py:246
  15.4 71.5 %collective-permute-start.3 = (bf16[256,2048]{1,0:T(8,128)(2,1)}, bf16[256,2048]{1,0:T(8,128)(2,1)}, u32[]{:S(2)}, u32[]{:S(2)}) collective-permute-start(bf16[256,2048]{1,0:T(8,128)(2,1)} %get-tuple-element.101), channel_id=1, source_target_pairs={{1,2},{5,3},{3,6},{7,7},{9,10},{13,11},{11,14},{15,15},{17,18},{21... | collective-permute-start | bytes 3145736 | tf_op jit(solution)/shard_map/ppermute | solution.py:186
  16.7 80.4 %collective-permute-start = (bf16[256,2048]{1,0:T(8,128)(2,1)}, bf16[256,2048]{1,0:T(8,128)(2,1)S(1)}, u32[]{:S(2)}, u32[]{:S(2)}) collective-permute-start(bf16[256,2048]{1,0:T(8,128)(2,1)} %get-tuple-element.102), channel_id=1, source_target_pairs={{0,0},{4,1},{2,4},{6,5},{8,8},{12,9},{10,12},{14,13},{16,16},{20,1... | collective-permute-start | bytes 3145736 | tf_op jit(solution)/shard_map/ppermute | solution.py:186
  23.9 73.2 %collective-permute-start.1 = (bf16[256,2048]{1,0:T(8,128)(2,1)}, bf16[256,2048]{1,0:T(8,128)(2,1)S(1)}, u32[]{:S(2)}, u32[]{:S(2)}) collective-permute-start(bf16[256,2048]{1,0:T(8,128)(2,1)} %get-tuple-element.101), channel_id=1, source_target_pairs={{0,2},{4,3},{2,6},{6,7},{8,10},{12,11},{10,14},{14,15},{16,18},{20... | collective-permute-start | bytes 3145736 | tf_op jit(solution)/shard_map/ppermute | solution.py:186
  31.8 435.7 %all-gather.13.cloned.1.call-start = ((), (), s32[]{:S(2)}) async-start(), calls=%async_computation.9 | async-start | bytes 3604480 | tf_op jit(solution)/shard_map/all_gather | solution.py:246
  103.3 365.4 %all-gather.15.cloned.1.call-start = ((), (), s32[]{:S(2)}) async-start(), calls=%async_computation.10 | async-start | bytes 3604480 | tf_op jit(solution)/shard_map/all_gather | solution.py:246
  149.0 105.5 %collective-permute-start.5 = (bf16[2,512,2048]{2,1,0:T(8,128)(2,1)}, bf16[2,512,2048]{2,1,0:T(8,128)(2,1)}, u32[]{:S(2)}, u32[]{:S(2)}) collective-permute-start(bf16[2,512,2048]{2,1,0:T(8,128)(2,1)} %maximum_select_fusion.10), channel_id=1, source_target_pairs={{0,4},{1,5},{2,6},{3,7},{4,0},{5,1},{6,2},{7,3},{8,12},{9,13},{10,... | collective-permute-start | bytes 12582920 | tf_op jit(solution)/shard_map/ppermute | solution.py:147
  154.5 47.5 %collective-permute-start.8 = (bf16[4,256,1024]{2,1,0:T(8,128)(2,1)}, bf16[4,256,1024]{2,1,0:T(8,128)(2,1)}, u32[]{:S(2)}, u32[]{:S(2)}) collective-permute-start(bf16[4,256,1024]{2,1,0:T(8,128)(2,1)} %bitcast.506), channel_id=1, source_target_pairs={{0,16},{1,17},{2,18},{3,19},{4,20},{5,21},{6,22},{7,23},{8,24},{9,... | collective-permute-start | bytes 6291464 | tf_op jit(solution)/shard_map/ppermute | solution.py:147
  155.8 91.2 %collective-permute-start.9 = (bf16[4,256,1024]{2,1,0:T(8,128)(2,1)}, bf16[4,256,1024]{2,1,0:T(8,128)(2,1)}, u32[]{:S(2)}, u32[]{:S(2)}) collective-permute-start(bf16[4,256,1024]{2,1,0:T(8,128)(2,1)} %bitcast.508), channel_id=1, source_target_pairs={{0,16},{1,17},{2,18},{3,19},{4,20},{5,21},{6,22},{7,23},{8,24},{9,... | collective-permute-start | bytes 6291464 | tf_op jit(solution)/shard_map/ppermute | solution.py:147
  160.5 308.5 %all-gather.17.cloned.1.call-start = ((), (), s32[]{:S(2)}) async-start(), calls=%async_computation.11 | async-start | bytes 3604480 | tf_op jit(solution)/shard_map/all_gather | solution.py:246
  319.6 979.1 %reduce-scatter.13.cloned.1.call-start = ((), (), s32[]{:S(2)}) async-start(), calls=%async_computation.15 | async-start | bytes 3604480 | tf_op jit(solution)/shard_map/reduce_scatter | solution.py:273
  321.3 48.1 %collective-permute-start.32 = (bf16[256,2048]{1,0:T(8,128)(2,1)S(1)}, bf16[256,2048]{1,0:T(8,128)(2,1)S(1)}, u32[]{:S(2)}, u32[]{:S(2)}) collective-permute-start(bf16[256,2048]{1,0:T(8,128)(2,1)S(1)} %get-tuple-element.87), channel_id=1, source_target_pairs={{1,0},{5,1},{3,4},{7,5},{9,8},{13,9},{11,12},{15,13},{17,16},{21,1... | collective-permute-start | bytes 3145736 | tf_op jit(solution)/shard_map/ppermute | solution.py:186
  323.3 83.1 %collective-permute-start.30 = (bf16[256,2048]{1,0:T(8,128)(2,1)S(1)}, bf16[256,2048]{1,0:T(8,128)(2,1)S(1)}, u32[]{:S(2)}, u32[]{:S(2)}) collective-permute-start(bf16[256,2048]{1,0:T(8,128)(2,1)S(1)} %get-tuple-element.87), channel_id=1, source_target_pairs={{0,0},{4,1},{2,4},{6,5},{8,8},{12,9},{10,12},{14,13},{16,16},{20,1... | collective-permute-start | bytes 3145736 | tf_op jit(solution)/shard_map/ppermute | solution.py:186
  332.0 74.4 %collective-permute-start.31 = (bf16[256,2048]{1,0:T(8,128)(2,1)S(1)}, bf16[256,2048]{1,0:T(8,128)(2,1)S(1)}, u32[]{:S(2)}, u32[]{:S(2)}) collective-permute-start(bf16[256,2048]{1,0:T(8,128)(2,1)S(1)} %get-tuple-element.86), channel_id=1, source_target_pairs={{0,2},{4,3},{2,6},{6,7},{8,10},{12,11},{10,14},{14,15},{16,18},{20... | collective-permute-start | bytes 3145736 | tf_op jit(solution)/shard_map/ppermute | solution.py:186
  366.9 106.2 %collective-permute-start.13 = (bf16[2,2048,512]{2,1,0:T(8,128)(2,1)}, bf16[2,2048,512]{2,1,0:T(8,128)(2,1)}, u32[]{:S(2)}, u32[]{:S(2)}) collective-permute-start(bf16[2,2048,512]{2,1,0:T(8,128)(2,1)} %maximum_select_fusion.14), channel_id=1, source_target_pairs={{0,4},{1,5},{2,6},{3,7},{4,0},{5,1},{6,2},{7,3},{8,12},{9,13},{10,... | collective-permute-start | bytes 12582920 | tf_op jit(solution)/shard_map/ppermute | solution.py:147
  446.9 233.7 %collective-permute-start.35 = (bf16[2,512,2048]{2,1,0:T(8,128)(2,1)}, bf16[2,512,2048]{2,1,0:T(8,128)(2,1)}, u32[]{:S(2)}, u32[]{:S(2)}) collective-permute-start(bf16[2,512,2048]{2,1,0:T(8,128)(2,1)} %maximum_select_fusion.17), channel_id=1, source_target_pairs={{0,4},{1,5},{2,6},{3,7},{4,0},{5,1},{6,2},{7,3},{8,12},{9,13},{10,... | collective-permute-start | bytes 12582920 | tf_op jit(solution)/shard_map/ppermute | solution.py:147
  467.5 64.4 %collective-permute-start.19 = (bf16[4,256,1408]{2,1,0:T(8,128)(2,1)}, bf16[4,256,1408]{2,1,0:T(8,128)(2,1)}, u32[]{:S(2)}, u32[]{:S(2)}) collective-permute-start(bf16[4,256,1408]{2,1,0:T(8,128)(2,1)} %bitcast.499), channel_id=1, source_target_pairs={{0,16},{1,17},{2,18},{3,19},{4,20},{5,21},{6,22},{7,23},{8,24},{9,... | collective-permute-start | bytes 8650760 | tf_op jit(solution)/shard_map/ppermute | solution.py:147
  468.8 125.0 %collective-permute-start.20 = (bf16[4,256,1408]{2,1,0:T(8,128)(2,1)}, bf16[4,256,1408]{2,1,0:T(8,128)(2,1)}, u32[]{:S(2)}, u32[]{:S(2)}) collective-permute-start(bf16[4,256,1408]{2,1,0:T(8,128)(2,1)} %bitcast.501), channel_id=1, source_target_pairs={{0,16},{1,17},{2,18},{3,19},{4,20},{5,21},{6,22},{7,23},{8,24},{9,... | collective-permute-start | bytes 8650760 | tf_op jit(solution)/shard_map/ppermute | solution.py:147
  469.0 186.4 %collective-permute-start.21 = (bf16[4,256,1408]{2,1,0:T(8,128)(2,1)}, bf16[4,256,1408]{2,1,0:T(8,128)(2,1)S(1)}, u32[]{:S(2)}, u32[]{:S(2)}) collective-permute-start(bf16[4,256,1408]{2,1,0:T(8,128)(2,1)} %bitcast.503), channel_id=1, source_target_pairs={{0,16},{1,17},{2,18},{3,19},{4,20},{5,21},{6,22},{7,23},{8,24},{9,... | collective-permute-start | bytes 8650760 | tf_op jit(solution)/shard_map/ppermute | solution.py:147
  488.9 49.9 %collective-permute-start.15 = (f32[2048]{0:T(1024)S(1)}, f32[2048]{0:T(1024)S(1)}, u32[]{:S(2)}, u32[]{:S(2)}) collective-permute-start(f32[2048]{0:T(1024)S(1)} %get-tuple-element.123), channel_id=1, source_target_pairs={{0,4},{1,5},{2,6},{3,7},{4,0},{5,1},{6,2},{7,3},{8,12},{9,13},{10,... | collective-permute-start | bytes 24584 | tf_op jit(solution)/shard_map/ppermute | solution.py:147
  538.7 61.7 %collective-permute-start.16 = (f32[2048]{0:T(1024)S(1)}, f32[2048]{0:T(1024)S(1)}, u32[]{:S(2)}, u32[]{:S(2)}) collective-permute-start(f32[2048]{0:T(1024)S(1)} %add.291), channel_id=1, source_target_pairs={{0,8},{1,9},{2,10},{3,11},{4,12},{5,13},{6,14},{7,15},{8,0},{9,1},... | collective-permute-start | bytes 24584 | tf_op jit(solution)/shard_map/ppermute | solution.py:147
  602.1 114.1 %collective-permute-start.17 = (bf16[2048,512]{1,0:T(8,128)(2,1)}, bf16[2048,512]{1,0:T(8,128)(2,1)S(1)}, u32[]{:S(2)}, u32[]{:S(2)}) collective-permute-start(bf16[2048,512]{1,0:T(8,128)(2,1)} %multiply_convert_fusion.8), channel_id=1, source_target_pairs={{0,8},{1,9},{2,10},{3,11},{4,12},{5,13},{6,14},{7,15},{8,0},{9,1},... | collective-permute-start | bytes 6291464 | tf_op jit(solution)/shard_map/ppermute | solution.py:147
  718.7 54.4 %collective-permute-start.18 = (bf16[2,2048,512]{2,1,0:T(8,128)(2,1)}, bf16[2,2048,512]{2,1,0:T(8,128)(2,1)}, u32[]{:S(2)}, u32[]{:S(2)}) collective-permute-start(bf16[2,2048,512]{2,1,0:T(8,128)(2,1)} %maximum_select_fusion.15), channel_id=1, source_target_pairs={{0,4},{1,5},{2,6},{3,7},{4,0},{5,1},{6,2},{7,3},{8,12},{9,13},{10,... | collective-permute-start | bytes 12582920 | tf_op jit(solution)/shard_map/ppermute | solution.py:147
  899.3 63.5 %collective-permute-start.66 = (bf16[1024,1408]{1,0:T(8,128)(2,1)}, bf16[1024,1408]{1,0:T(8,128)(2,1)}, u32[]{:S(2)}, u32[]{:S(2)}) collective-permute-start(bf16[1024,1408]{1,0:T(8,128)(2,1)} %convolution_convert_fusion.4), channel_id=1, source_target_pairs={{0,16},{1,17},{2,18},{3,19},{4,20},{5,21},{6,22},{7,23},{8,24},{9,... | collective-permute-start | bytes 8650760 | tf_op jit(solution)/shard_map/ppermute | solution.py:147
  935.8 210.3 %collective-permute-start.36 = (bf16[2048,2,512]{2,0,1:T(8,128)(2,1)}, bf16[2048,2,512]{2,0,1:T(8,128)(2,1)}, u32[]{:S(2)}, u32[]{:S(2)}) collective-permute-start(bf16[2048,2,512]{2,0,1:T(8,128)(2,1)} %bitcast.491), channel_id=1, source_target_pairs={{0,4},{1,5},{2,6},{3,7},{4,0},{5,1},{6,2},{7,3},{8,12},{9,13},{10,... | collective-permute-start | bytes 12582920 | tf_op jit(solution)/shard_map/ppermute | solution.py:147
  948.8 75.9 %collective-permute-start.70 = (bf16[1024,1408]{1,0:T(8,128)(2,1)}, bf16[1024,1408]{1,0:T(8,128)(2,1)S(1)}, u32[]{:S(2)}, u32[]{:S(2)}) collective-permute-start(bf16[1024,1408]{1,0:T(8,128)(2,1)} %convolution_convert_fusion.2), channel_id=1, source_target_pairs={{0,16},{1,17},{2,18},{3,19},{4,20},{5,21},{6,22},{7,23},{8,24},{9,... | collective-permute-start | bytes 8650760 | tf_op jit(solution)/shard_map/ppermute | solution.py:147
  972.3 329.0 %reduce-scatter.15.cloned.1.call-start = ((), (), s32[]{:S(2)}) async-start(), calls=%async_computation.16 | async-start | bytes 3604480 | tf_op jit(solution)/shard_map/reduce_scatter | solution.py:273
  1000.2 154.0 %collective-permute-start.22 = (bf16[2048,2,512]{2,0,1:T(8,128)(2,1)}, bf16[2048,2,512]{2,0,1:T(8,128)(2,1)}, u32[]{:S(2)}, u32[]{:S(2)}) collective-permute-start(bf16[2048,2,512]{2,0,1:T(8,128)(2,1)} %fusion.17), channel_id=1, source_target_pairs={{0,4},{1,5},{2,6},{3,7},{4,0},{5,1},{6,2},{7,3},{8,12},{9,13},{10,... | collective-permute-start | bytes 12582920 | tf_op jit(solution)/shard_map/ppermute | solution.py:147
  1015.7 153.6 %collective-permute-start.74 = (bf16[1024,1408]{1,0:T(8,128)(2,1)}, bf16[1024,1408]{1,0:T(8,128)(2,1)}, u32[]{:S(2)}, u32[]{:S(2)}) collective-permute-start(bf16[1024,1408]{1,0:T(8,128)(2,1)} %convolution_convert_fusion), channel_id=1, source_target_pairs={{0,16},{1,17},{2,18},{3,19},{4,20},{5,21},{6,22},{7,23},{8,24},{9,... | collective-permute-start | bytes 8650760 | tf_op jit(solution)/shard_map/ppermute | solution.py:147
  1035.7 265.9 %reduce-scatter.17.cloned.1.call-start = ((), (), s32[]{:S(2)}) async-start(), calls=%async_computation.17 | async-start | bytes 3604480 | tf_op jit(solution)/shard_map/reduce_scatter | solution.py:273
  1169.3 74.6 %collective-permute-start.23 = (bf16[2048,512]{1,0:T(8,128)(2,1)}, bf16[2048,512]{1,0:T(8,128)(2,1)}, u32[]{:S(2)}, u32[]{:S(2)}) collective-permute-start(bf16[2048,512]{1,0:T(8,128)(2,1)} %fusion.24), channel_id=1, source_target_pairs={{0,8},{1,9},{2,10},{3,11},{4,12},{5,13},{6,14},{7,15},{8,0},{9,1},... | collective-permute-start | bytes 6291464 | tf_op jit(solution)/shard_map/ppermute | solution.py:147
  1180.5 173.3 %reduce-scatter.11.cloned.1.call-start = ((), (), s32[]{:S(2)}) async-start(), calls=%async_computation.14 | async-start | bytes 1310720 | tf_op jit(solution)/shard_map/reduce_scatter | solution.py:273
  1288.7 174.2 %collective-permute-start.40 = (bf16[2048,2,512]{2,0,1:T(8,128)(2,1)}, bf16[2048,2,512]{2,0,1:T(8,128)(2,1)}, u32[]{:S(2)}, u32[]{:S(2)}) collective-permute-start(bf16[2048,2,512]{2,0,1:T(8,128)(2,1)} %bitcast.490), channel_id=1, source_target_pairs={{0,4},{1,5},{2,6},{3,7},{4,0},{5,1},{6,2},{7,3},{8,12},{9,13},{10,... | collective-permute-start | bytes 12582920 | tf_op jit(solution)/shard_map/ppermute | solution.py:147
  1297.1 440.8 %reduce-scatter.7.cloned.1.call-start = ((), (), s32[]{:S(2)}) async-start(), calls=%async_computation.12 | async-start | bytes 2621440 | tf_op jit(solution)/shard_map/reduce_scatter | solution.py:273
  1304.3 49.4 %collective-permute-start.28 = (bf16[256,2048]{1,0:T(8,128)(2,1)}, bf16[256,2048]{1,0:T(8,128)(2,1)}, u32[]{:S(2)}, u32[]{:S(2)}) collective-permute-start(bf16[256,2048]{1,0:T(8,128)(2,1)} %get-tuple-element.89), channel_id=1, source_target_pairs={{2,0},{3,4},{6,2},{7,6},{10,8},{11,12},{14,10},{15,14},{18,16},{19... | collective-permute-start | bytes 3145736 | tf_op jit(solution)/shard_map/ppermute | solution.py:195
  1353.7 116.0 %collective-permute-start.68 = (bf16[512,1408]{1,0:T(8,128)(2,1)S(1)}, bf16[512,1408]{1,0:T(8,128)(2,1)}, u32[]{:S(2)}, u32[]{:S(2)}) collective-permute-start(bf16[512,1408]{1,0:T(8,128)(2,1)S(1)} %bitcast.430), channel_id=1, source_target_pairs={{0,8},{1,9},{2,10},{3,11},{4,12},{5,13},{6,14},{7,15},{8,0},{9,1},... | collective-permute-start | bytes 4325384 | tf_op jit(solution)/shard_map/ppermute | solution.py:147
  1359.7 115.7 %collective-permute-start.72 = (bf16[512,1408]{1,0:T(8,128)(2,1)S(1)}, bf16[512,1408]{1,0:T(8,128)(2,1)}, u32[]{:S(2)}, u32[]{:S(2)}) collective-permute-start(bf16[512,1408]{1,0:T(8,128)(2,1)S(1)} %bitcast.433), channel_id=1, source_target_pairs={{0,8},{1,9},{2,10},{3,11},{4,12},{5,13},{6,14},{7,15},{8,0},{9,1},... | collective-permute-start | bytes 4325384 | tf_op jit(solution)/shard_map/ppermute | solution.py:147
  1375.4 104.2 %collective-permute-start.76 = (bf16[512,1408]{1,0:T(8,128)(2,1)S(1)}, bf16[512,1408]{1,0:T(8,128)(2,1)}, u32[]{:S(2)}, u32[]{:S(2)}) collective-permute-start(bf16[512,1408]{1,0:T(8,128)(2,1)S(1)} %bitcast.436), channel_id=1, source_target_pairs={{0,8},{1,9},{2,10},{3,11},{4,12},{5,13},{6,14},{7,15},{8,0},{9,1},... | collective-permute-start | bytes 4325384 | tf_op jit(solution)/shard_map/ppermute | solution.py:147
  1375.4 76.9 %collective-permute-start.64 = (bf16[512,512]{1,0:T(8,128)(2,1)S(1)}, bf16[512,512]{1,0:T(8,128)(2,1)S(1)}, u32[]{:S(2)}, u32[]{:S(2)}) collective-permute-start(bf16[512,512]{1,0:T(8,128)(2,1)S(1)} %bitcast.473), channel_id=1, source_target_pairs={{0,8},{1,9},{2,10},{3,11},{4,12},{5,13},{6,14},{7,15},{8,0},{9,1},... | collective-permute-start | bytes 1572872 | tf_op jit(solution)/shard_map/ppermute | solution.py:147
  1475.4 193.2 %collective-permute-start.69 = (bf16[2,512,1408]{2,1,0:T(8,128)(2,1)}, bf16[2,512,1408]{2,1,0:T(8,128)(2,1)}, u32[]{:S(2)}, u32[]{:S(2)}) collective-permute-start(bf16[2,512,1408]{2,1,0:T(8,128)(2,1)} %maximum_select_fusion.20), channel_id=1, source_target_pairs={{0,4},{1,5},{2,6},{3,7},{4,0},{5,1},{6,2},{7,3},{8,12},{9,13},{10,... | collective-permute-start | bytes 8650760 | tf_op jit(solution)/shard_map/ppermute | solution.py:147
  1479.1 241.2 %collective-permute-start.73 = (bf16[2,512,1408]{2,1,0:T(8,128)(2,1)}, bf16[2,512,1408]{2,1,0:T(8,128)(2,1)}, u32[]{:S(2)}, u32[]{:S(2)}) collective-permute-start(bf16[2,512,1408]{2,1,0:T(8,128)(2,1)} %maximum_select_fusion.22), channel_id=1, source_target_pairs={{0,4},{1,5},{2,6},{3,7},{4,0},{5,1},{6,2},{7,3},{8,12},{9,13},{10,... | collective-permute-start | bytes 8650760 | tf_op jit(solution)/shard_map/ppermute | solution.py:147
  1483.1 255.3 %collective-permute-start.77 = (bf16[2,512,1408]{2,1,0:T(8,128)(2,1)}, bf16[2,512,1408]{2,1,0:T(8,128)(2,1)}, u32[]{:S(2)}, u32[]{:S(2)}) collective-permute-start(bf16[2,512,1408]{2,1,0:T(8,128)(2,1)} %maximum_select_fusion.23), channel_id=1, source_target_pairs={{0,4},{1,5},{2,6},{3,7},{4,0},{5,1},{6,2},{7,3},{8,12},{9,13},{10,... | collective-permute-start | bytes 8650760 | tf_op jit(solution)/shard_map/ppermute | solution.py:147
  1590.6 69.4 %collective-permute-start.44 = (bf16[2048,2,512]{2,0,1:T(8,128)(2,1)}, bf16[2048,2,512]{2,0,1:T(8,128)(2,1)}, u32[]{:S(2)}, u32[]{:S(2)}) collective-permute-start(bf16[2048,2,512]{2,0,1:T(8,128)(2,1)} %bitcast.492), channel_id=1, source_target_pairs={{0,4},{1,5},{2,6},{3,7},{4,0},{5,1},{6,2},{7,3},{8,12},{9,13},{10,... | collective-permute-start | bytes 12582920 | tf_op jit(solution)/shard_map/ppermute | solution.py:147
  1601.3 47.6 %collective-permute-start.54 = (bf16[1024,1024]{1,0:T(8,128)(2,1)}, bf16[1024,1024]{1,0:T(8,128)(2,1)}, u32[]{:S(2)}, u32[]{:S(2)}) collective-permute-start(bf16[1024,1024]{1,0:T(8,128)(2,1)} %convolution_convert_fusion.7), channel_id=1, source_target_pairs={{0,16},{1,17},{2,18},{3,19},{4,20},{5,21},{6,22},{7,23},{8,24},{9,... | collective-permute-start | bytes 6291464 | tf_op jit(solution)/shard_map/ppermute | solution.py:147
  1660.0 100.8 %reduce-scatter.9.cloned.1.call-start = ((), (), s32[]{:S(2)}) async-start(), calls=%async_computation.13 | async-start | bytes 2621440 | tf_op jit(solution)/shard_map/reduce_scatter | solution.py:273
  1787.7 54.8 %collective-permute-start.57 = (bf16[2,512,1024]{2,1,0:T(8,128)(2,1)S(1)}, bf16[2,512,1024]{2,1,0:T(8,128)(2,1)S(1)}, u32[]{:S(2)}, u32[]{:S(2)}) collective-permute-start(bf16[2,512,1024]{2,1,0:T(8,128)(2,1)S(1)} %maximum_select_fusion.30), channel_id=1, source_target_pairs={{0,4},{1,5},{2,6},{3,7},{4,0},{5,1},{6,2},{7,3},{8,12},{9,13},{10,... | collective-permute-start | bytes 6291464 | tf_op jit(solution)/shard_map/ppermute | solution.py:147
  (121 other events, 2965.4 us)
Sparse Core Ops, SparseCore 0:
  10.4 81.0 all-gather.6
  93.6 48.3 all-gather.8
  143.5 27.4 all-gather.10
  173.0 57.8 all-gather.12
  232.4 57.8 all-gather.14
  319.7 89.8 all-gather.16
  972.4 69.6 reduce-scatter.12
  1044.3 61.0 reduce-scatter.14
  1180.7 70.9 reduce-scatter.16
  1297.2 47.5 reduce-scatter.10
  1660.1 54.6 reduce-scatter.6
  1717.5 43.1 reduce-scatter.8

commit v2 on v1

v2 whole, which is shorter than its diff:
```python
import functools

import jax
import jax.numpy as jnp
from jax import lax
from jax.experimental import pallas as pl
from jax.experimental.pallas import tpu as pltpu
from jax.sharding import PartitionSpec as P

HEADS = 16
HEAD_DIM = 128
STREAM = 1024
GROUP = 4
BLOCK = 256
EPSILON = 1e-06
AXES = ("rep", "shard")
LOW = jnp.bfloat16
F32 = jnp.float32


def matmul(former, latter):
    return jnp.dot(former, latter, preferred_element_type=F32)


def times_transposed(former, latter):
    return lax.dot_general(former, latter, (((1,), (1,)), ((), ())), preferred_element_type=F32)


def cross_tokens(former, latter):
    return lax.dot_general(former, latter, (((0,), (0,)), ((), ())), preferred_element_type=F32)


def masked_decay(rate, ends, first, columns):
    row = first + lax.broadcasted_iota(jnp.int32, (BLOCK, 1), 0)
    column = lax.broadcasted_iota(jnp.int32, (1, columns), 1)
    begin = jnp.zeros((BLOCK, 1), jnp.int32)
    for end in ends:
        begin = jnp.where(row >= end, end, begin)
    falling = jnp.exp(-rate * (row - first).astype(F32))
    rising = jnp.exp(rate * (column - first).astype(F32))
    allowed = (column <= row) & (column >= begin)
    return jnp.where(allowed, falling * rising, 0.0)


def attend_kernel(rates, ends, zq_ref, zk_ref, zv_ref, out_ref):
    stream, head = pl.program_id(0), pl.program_id(1)
    rate = rates[head]
    bounds = [ends[stream, i] for i in range(ends.shape[1])]
    zq, zk = zq_ref[...], zk_ref[...]
    q = (zq * jax.nn.sigmoid(zq)).astype(LOW)
    k = (zk * jax.nn.sigmoid(zk)).astype(LOW)
    v = zv_ref[...].astype(LOW)
    for first in range(0, STREAM, BLOCK):
        columns = first + BLOCK
        mask = masked_decay(rate, bounds, first, columns)
        scores = times_transposed(q[first:columns], k[:columns])
        weights = (scores * mask).astype(LOW)
        out_ref[first:columns, :] = matmul(weights, v[:columns])


def attend_back_kernel(
    rates, ends, zq_ref, zk_ref, zv_ref, do_ref, dzq_ref, dzk_ref, dzv_ref, dk_ref, dv_ref
):
    stream, head = pl.program_id(0), pl.program_id(1)
    rate = rates[head]
    bounds = [ends[stream, i] for i in range(ends.shape[1])]
    zq, zk = zq_ref[...], zk_ref[...]
    sig_q, sig_k = jax.nn.sigmoid(zq), jax.nn.sigmoid(zk)
    q = (zq * sig_q).astype(LOW)
    k = (zk * sig_k).astype(LOW)
    slope_q = sig_q * (1.0 + zq * (1.0 - sig_q))
    v = zv_ref[...].astype(LOW)
    d_o = do_ref[...]
    dk_ref[...] = jnp.zeros_like(dk_ref)
    dv_ref[...] = jnp.zeros_like(dv_ref)
    for first in range(0, STREAM, BLOCK):
        columns = first + BLOCK
        rows = slice(first, columns)
        mask = masked_decay(rate, bounds, first, columns)
        weights = (times_transposed(q[rows], k[:columns]) * mask).astype(LOW)
        d_scores = (times_transposed(d_o[rows], v[:columns]) * mask).astype(LOW)
        dzq_ref[rows, :] = (matmul(d_scores, k[:columns]) * slope_q[rows]).astype(LOW)
        dk_ref[:columns, :] += cross_tokens(d_scores, q[rows])
        dv_ref[:columns, :] += cross_tokens(weights, d_o[rows])
    dzk_ref[...] = (dk_ref[...] * (sig_k * (1.0 + zk * (1.0 - sig_k)))).astype(LOW)
    dzv_ref[...] = dv_ref[...].astype(LOW)


def head_block(offset=0):
    return pl.BlockSpec((STREAM, HEAD_DIM), lambda g, h, *_: (g, h + offset))


def attend(rates, ends, z_qk, z_vg):
    heads, streams = rates.shape[0], ends.shape[0]
    work = streams * heads * STREAM * STREAM
    return pl.pallas_call(
        attend_kernel,
        out_shape=jax.ShapeDtypeStruct((streams * STREAM, heads * HEAD_DIM), F32),
        grid_spec=pltpu.PrefetchScalarGridSpec(
            num_scalar_prefetch=2,
            grid=(streams, heads),
            in_specs=[head_block(), head_block(heads), head_block()],
            out_specs=head_block(),
        ),
        compiler_params=pltpu.CompilerParams(vmem_limit_bytes=40 << 20),
        cost_estimate=pl.CostEstimate(
            flops=4 * work * HEAD_DIM, transcendentals=work // 64,
            bytes_accessed=streams * heads * STREAM * HEAD_DIM * 16,
        ),
        name="attend",
    )(rates, ends, z_qk, z_qk, z_vg)


def attend_back(rates, ends, z_qk, z_vg, d_o):
    heads, streams = rates.shape[0], ends.shape[0]
    work = streams * heads * STREAM * STREAM
    return pl.pallas_call(
        attend_back_kernel,
        out_shape=[jax.ShapeDtypeStruct((streams * STREAM, heads * HEAD_DIM), LOW)] * 3,
        grid_spec=pltpu.PrefetchScalarGridSpec(
            num_scalar_prefetch=2,
            grid=(streams, heads),
            in_specs=[head_block(), head_block(heads), head_block(), head_block()],
            out_specs=[head_block()] * 3,
            scratch_shapes=[pltpu.VMEM((STREAM, HEAD_DIM), F32)] * 2,
        ),
        compiler_params=pltpu.CompilerParams(vmem_limit_bytes=40 << 20),
        cost_estimate=pl.CostEstimate(
            flops=10 * work * HEAD_DIM, transcendentals=work // 64,
            bytes_accessed=streams * heads * STREAM * HEAD_DIM * 20,
        ),
        name="attend_back",
    )(rates, ends, z_qk, z_qk, z_vg, d_o)


def tie(*values):
    return lax.optimization_barrier(values)


def body(reps, shards, tokens, cotangent, lengths, decay_rates, *weights):
    spread = reps // GROUP
    rep, place = lax.axis_index("rep"), lax.axis_index("shard")
    c, b, a = rep % 2, (rep // 2) % 2, rep // GROUP
    quarter = 2 * c + b
    micro, run, width = tokens.shape
    half, own = width // 2, width // GROUP
    streams = micro * GROUP // shards
    per_block = STREAM // run // GROUP * streams
    rows = width // shards
    part = rows // spread
    columns = functools.partial(lax.dynamic_slice_in_dim, axis=1)

    def move(x, target):
        pairs = [(r * shards + s, target(r) * shards + s) for r in range(reps) for s in range(shards)]
        return lax.ppermute(x, AXES, pairs)

    def swap_c(x):
        return move(x, lambda r: r ^ 1)

    def swap_b(x):
        return move(x, lambda r: r ^ 2)

    def shift_a(x, k):
        return move(x, lambda r: (r + GROUP * k) % reps)

    def ordered(index, mine, other, axis):
        return jnp.where(
            index == 0,
            jnp.concatenate([mine, other], axis),
            jnp.concatenate([other, mine], axis),
        )


    def origin(r, s, p):
        run_id = (2 * (r % 2) + (r // 2) % 2) * per_block + p
        stream, piece = run_id // shards, run_id % shards
        if streams == 1:
            batch, member = s // GROUP, s % GROUP
        else:
            batch, member = s // 2, 2 * stream + s % 2
        return (r // GROUP) * GROUP + member, piece, batch

    def routes(p, batch):
        found = []
        for r in range(reps):
            for s in range(shards):
                from_r, from_s, from_batch = origin(r, s, p)
                if from_batch == batch:
                    found.append((from_r * shards + from_s, r * shards + s))
        return found

    def permuted(x):
        return jnp.concatenate(
            [
                x[:, (z * spread + k) * part : (z * spread + k + 1) * part]
                for k in range(spread)
                for z in range(shards)
            ],
            axis=1,
        )

    def natural(x):
        return jnp.concatenate(
            [
                x[:, (k * shards + z) * part : (k * shards + z + 1) * part]
                for z in range(shards)
                for k in range(spread)
            ],
            axis=1,
        )

    def bring(x):
        slots = []
        for p in range(per_block):
            arrived = [lax.ppermute(x[m], AXES, routes(p, m)) for m in range(micro)]
            slots.append(functools.reduce(jnp.add, arrived))
        return permuted(jnp.concatenate(slots, axis=0))

    def bring_back(x):
        slots = natural(x).reshape(per_block, run, width)
        batches = []
        for m in range(micro):
            arrived = [
                lax.ppermute(slots[p], AXES, [(d, o) for o, d in routes(p, m)])
                for p in range(per_block)
            ]
            batches.append(functools.reduce(jnp.add, arrived))
        return jnp.stack(batches)


    def gather_b(x):
        return ordered(b, x, swap_b(x), 1)

    def gather_c(x):
        return ordered(c, x, swap_c(x), 1)

    def gather_rows_b(x):
        return ordered(b, x, swap_b(x), 0)

    def gather_rows_c(x):
        return ordered(c, x, swap_c(x), 0)

    def total(x):
        x = x + swap_c(x)
        return x + swap_b(x)

    def fold_c(product):
        sent = swap_c(product(1 - c).astype(LOW))
        return product(c) + sent.astype(F32)

    def fold_b(x):
        sent = swap_b(columns(x, (1 - b) * own, own).astype(LOW))
        return columns(x, b * own, own) + sent.astype(F32)

    def to_runs(x):
        cut = x.reshape(2, 2, -1, own)
        pick = functools.partial(lax.dynamic_index_in_dim, keepdims=False)
        both = ordered(b, pick(cut, b, 1), swap_b(pick(cut, 1 - b, 1)), 2)
        four = ordered(c, pick(both, c, 0), swap_c(pick(both, 1 - c, 0)), 1)
        return bring_back(four)


    def own_features(w):
        count = shards * spread // GROUP
        cut = []
        for i in range(count):
            block = quarter * count + i
            cut.append(columns(w, (block % shards) * rows + (block // shards) * part, part))
        return jnp.concatenate(cut, axis=1)

    def own_units(w):
        return columns(w, quarter * (w.shape[1] // GROUP), w.shape[1] // GROUP)

    def over_shards(*members):
        cut = jnp.concatenate(members, axis=1) if len(members) > 1 else members[0]
        piece = lax.dynamic_slice_in_dim(cut, a * part, part, 0)
        return lax.all_gather(piece, "shard", axis=0, tiled=True)

    def over_spread(x):
        return [shift_a(x, k) for k in range(1, spread)]

    def by_spread(relative):
        if spread == 2:
            return ordered(a, relative[0], relative[1], 0)
        stacked = jnp.stack(relative, 0)
        pick = functools.partial(lax.dynamic_index_in_dim, axis=0, keepdims=False)
        return jnp.concatenate([pick(stacked, (a - j) % spread) for j in range(spread)], axis=0)

    def in_row_order(x):
        cut = x.reshape(spread, shards, part, -1)
        return jnp.transpose(cut, (1, 0, 2, 3)).reshape(width, -1)

    def row_half(w, h):
        return lax.dynamic_slice_in_dim(w, h * half, half, 0)


    def owned_by(x, k):
        return columns(x, ((a + k) % spread) * (width // spread), width // spread)

    def away(left, right):
        return [cross_tokens(owned_by(left, k), right).astype(LOW) for k in range(1, spread)]

    def kept(left, right):
        return cross_tokens(owned_by(left, 0), right).astype(LOW)

    def sent_a(terms):
        return [shift_a(x, k + 1) for k, x in enumerate(terms)]

    def summed(mine, arrived):
        whole = mine.astype(F32)
        for x in arrived:
            whole = whole + x.astype(F32)
        return lax.psum_scatter(whole.astype(LOW), "shard", scatter_dimension=0, tiled=True)

    def spread_out(x):
        full = by_spread([x] + over_spread(x))
        return gather_quarters(full)

    def gather_quarters(full):
        pair = ordered(b, full[None], swap_b(full)[None], 0)
        return ordered(c, pair[None], swap_c(pair)[None], 0)

    def as_outputs(four, count, unpermute):
        size = four.shape[3] // count
        found = []
        for n in range(count):
            flat = jnp.concatenate(
                [four[i, j][:, n * size : (n + 1) * size] for i in range(2) for j in range(2)],
                axis=1,
            )
            found.append((natural(flat) if unpermute else flat).astype(F32))
        return found


    w_query, w_key, w_value, w_gate, w_out, w_one, w_two, w_down = weights
    g_qk = over_shards(own_units(w_query), own_units(w_key))
    g_vg = over_shards(own_units(w_value), own_units(w_gate))
    g_o = over_shards(own_features(w_out))
    g_1 = over_shards(own_units(w_one))
    g_2 = over_shards(own_units(w_two))
    g_d = over_shards(own_units(w_down))

    heads = HEADS // GROUP
    rates = lax.dynamic_slice_in_dim(decay_rates, quarter * heads, heads, 0)
    cuts = gather_rows_c(gather_rows_b(lengths.reshape(1, -1))).reshape(GROUP, micro, -1)
    if streams == 1:
        batch = place // GROUP
        member = place % GROUP
        chosen = lax.dynamic_slice_in_dim(cuts, 2 * (member % 2) + member // 2, 1, 0)
    else:
        batch = place // 2
        chosen = lax.dynamic_index_in_dim(cuts.reshape(2, 2, micro, -1), place % 2, 0, False)
    chosen = lax.dynamic_index_in_dim(chosen, batch, 1, False)
    seq_ends = [chosen[:, 0]]
    for i in range(1, chosen.shape[1]):
        seq_ends.append(seq_ends[-1] + chosen[:, i])
    ends = jnp.stack(seq_ends, axis=1)

    x_run = bring(tokens)
    x_run, g_qk = tie(x_run, g_qk)

    x_pair = gather_rows_b(x_run)
    s_qk = over_spread(g_qk)
    x_pair, s_qk, g_vg = tie(x_pair, s_qk, g_vg)

    s_vg = over_spread(g_vg)
    x_all = gather_rows_c(x_pair)
    x_float = x_all.astype(F32)
    x_scale = lax.rsqrt(jnp.mean(x_float * x_float, axis=-1, keepdims=True) + EPSILON)
    hidden_one = (x_float * x_scale).astype(LOW)
    w_qk = by_spread([g_qk, *s_qk])
    z_qk = matmul(hidden_one, w_qk)
    z_qk, s_vg, g_o = tie(z_qk, s_vg, g_o)

    s_o = over_spread(g_o)
    w_vg = by_spread([g_vg, *s_vg])
    z_vg = matmul(hidden_one, w_vg)
    attended = attend(rates, ends, z_qk, z_vg)
    gate = z_vg[:, own:]
    o_scale = lax.rsqrt(total(jnp.sum(attended * attended, axis=-1)) / width + EPSILON)[:, None]
    o_normed = attended * o_scale
    gated = (o_normed * gate).astype(LOW)
    gated, s_o, g_1 = tie(gated, s_o, g_1)

    s_1 = over_spread(g_1)
    dy_run = bring(cotangent)
    gated = gather_b(gated)
    w_o = in_row_order(by_spread([g_o, *s_o]))
    gated, s_1, g_2, dy_run = tie(gated, s_1, g_2, dy_run)

    s_2 = over_spread(g_2)
    gated = gather_c(gated)
    x_own = columns(x_all, quarter * own, own).astype(F32)
    middle = x_own + matmul(gated, w_o)
    m_scale = lax.rsqrt(total(jnp.sum(middle * middle, axis=-1)) / width + EPSILON)[:, None]
    m_normed = middle * m_scale
    hidden_two = gather_b(m_normed.astype(LOW))
    w_1 = by_spread([g_1, *s_1])
    hidden_two, s_2, g_d = tie(hidden_two, s_2, g_d)

    s_d = over_spread(g_d)
    hidden_two = gather_c(hidden_two)
    dy_all = gather_rows_c(gather_rows_b(dy_run))
    z_one = matmul(hidden_two, w_1)
    w_2 = by_spread([g_2, *s_2])
    z_two = matmul(hidden_two, w_2)
    product = (z_one * z_two).astype(LOW)
    t_down = away(dy_all, product)
    z_one, z_two, product, t_down, s_d = tie(z_one, z_two, product, t_down, s_d)

    r_down = sent_a(t_down)
    w_d = by_spread([g_d, *s_d])
    d_product = matmul(dy_all, w_d)
    d_one = (d_product * z_two).astype(LOW)
    d_two = (d_product * z_one).astype(LOW)
    t_one = away(hidden_two, d_one)
    k_down = kept(dy_all, product)
    d_hidden = fold_c(
        lambda h: times_transposed(d_one, row_half(w_1, h)) + times_transposed(d_two, row_half(w_2, h))
    )
    d_hidden, d_one, d_two, t_one, r_down, k_down = tie(
        d_hidden, d_one, d_two, t_one, r_down, k_down
    )

    r_one = sent_a(t_one)
    f_down = summed(k_down, r_down)
    d_hidden = fold_b(d_hidden)
    k_one = kept(hidden_two, d_one)
    t_two = away(hidden_two, d_two)
    d_hidden, r_one, k_one, t_two = tie(d_hidden, r_one, k_one, t_two)

    r_two = sent_a(t_two)
    f_one = summed(k_one, r_one)
    lean = total(jnp.sum(m_normed * d_hidden, axis=-1))[:, None] / width
    dy_own = columns(dy_all, quarter * own, own).astype(F32)
    d_middle = dy_own + m_scale * (d_hidden - m_normed * lean)
    d_branch = d_middle.astype(LOW)
    d_gated = fold_b(fold_c(lambda h: times_transposed(d_branch, row_half(w_o, h))))
    k_two = kept(hidden_two, d_two)
    p_out = cross_tokens(gated, d_branch).astype(LOW).reshape(shards, spread, part, -1)
    p_out = jnp.transpose(p_out, (1, 0, 2, 3)).reshape(spread, width // spread, -1)
    t_out = [lax.dynamic_index_in_dim(p_out, (a + k) % spread, 0, False) for k in range(spread)]
    d_gated, r_two, k_two, t_out = tie(d_gated, r_two, k_two, t_out)

    r_out = sent_a(t_out[1:])
    f_two = summed(k_two, r_two)
    d_gate = (d_gated * o_normed).astype(LOW)
    d_normed = d_gated * gate
    lean = total(jnp.sum(o_normed * d_normed, axis=-1))[:, None] / width
    d_attended = (o_scale * (d_normed - o_normed * lean)).astype(LOW)
    d_query, d_key, d_value = attend_back(rates, ends, z_qk, z_vg, d_attended)
    d_qk = jnp.concatenate([d_query, d_key], axis=1)
    d_vg = jnp.concatenate([d_value, d_gate], axis=1)
    t_qk = away(hidden_one, d_qk)
    d_qk, d_vg, r_out, t_qk = tie(d_qk, d_vg, r_out, t_qk)

    r_qk = sent_a(t_qk)
    f_out = summed(t_out[0], r_out)
    t_vg = away(hidden_one, d_vg)
    r_vg = sent_a(t_vg)
    k_qk = kept(hidden_one, d_qk)
    k_vg = kept(hidden_one, d_vg)
    f_qk = summed(k_qk, r_qk)
    f_vg = summed(k_vg, r_vg)
    d_hidden = fold_b(
        fold_c(
            lambda h: times_transposed(d_qk, row_half(w_qk, h))
            + times_transposed(d_vg, row_half(w_vg, h))
        )
    )
    x_normed = x_own * x_scale
    lean = total(jnp.sum(x_normed * d_hidden, axis=-1))[:, None] / width
    input_grad = to_runs((d_middle + x_scale * (d_hidden - x_normed * lean)).astype(LOW))

    result = fold_b(fold_c(lambda h: times_transposed(product, row_half(w_d, h))))
    output = to_runs((middle + result).astype(LOW))

    grads = []
    for reduced, count in ((f_qk, 2), (f_vg, 2), (f_out, 1), (f_one, 1), (f_two, 1), (f_down, 1)):
        grads += as_outputs(spread_out(reduced), count, reduced is f_out)
    return (output, input_grad, *grads)


def solution(mesh):
    by_tokens = P(None, ("rep", "shard"), None)
    by_rows = P("shard", None)
    return jax.shard_map(
        functools.partial(body, mesh.shape["rep"], mesh.shape["shard"]),
        mesh=mesh,
        in_specs=(by_tokens, by_tokens, P(None, "rep", None), P(), *[by_rows] * 8),
        out_specs=(by_tokens, by_tokens, *[by_rows] * 8),
        check_vma=False,
    )
```

time: 1890 us -> 1510 us (0.80)
  local copies, waits for them, and re-layouts: 339 us -> 64.2 us
  waiting for transfers between devices: 728 us -> 676 us
  other arithmetic: 290 us -> 249 us
  starting transfers between devices: 151 us -> 123 us
    dynamic_slice x29 -> x7, local copies, waits for them, and re-layouts: 210 us -> 10.9 us  [the longest x3 7.16 us: over_shards(): piece = lax.dynamic_slice_in_dim(cut, a * part, part, 0)]
    ppermute x62, waiting for transfers between devices: 582 us -> 426 us  [move(): return lax.ppermute(x, AXES, pairs)]
    ppermute x8, waiting for transfers between devices: 28.9 us -> 129 us  [bring_back(): lax.ppermute(slots[p], AXES, [(d, o) for o, d in routes(p, m)])]
    ppermute x62, starting transfers between devices: 105 us -> 70.1 us  [move(): return lax.ppermute(x, AXES, pairs)]
    concatenate x8 -> x3, local copies, waits for them, and re-layouts: 27.1 us -> 0.81 us  [natural(): jnp.concatenate([x[:, (k * shards + z) * part:(k * shards + z + 1) * part...]
    select_n x2 -> x1, local copies, waits for them, and re-layouts: 22.7 us -> 0.08 us  [ordered(): jnp.where(index == 0, jnp.concatenate([mine, other], axis), jnp.concatena...]
    convert_element_type x6 -> x4, local copies, waits for them, and re-layouts: 32 us -> 10.9 us  [fold_b(): sent = swap_b(columns(x, (1 - b) * own, own).astype(LOW))]
    select_n x47 -> x48, other arithmetic: 137 us -> 116 us  [ordered(): jnp.where(index == 0, jnp.concatenate([mine, other], axis), jnp.concatena...]
  transfers between devices with their start and end apart: 90 -> 90, of which waited for: 37 -> 35; matrix products, arithmetic and copies ran while one was open for 42% -> 37% of each run, Pallas kernels for 2% -> 2%
where the time goes in v2:
time: 1510 us; the launch traced here: 1480 us
  waiting for transfers between devices  676 us (45%)
  matrix products  317 us (21%)
  other arithmetic  249 us (16%)
  starting transfers between devices  123 us (8%)
  local copies, waits for them, and re-layouts  64.2 us (4%)
  Pallas kernels  34.3 us (2%)
  between operations  16.3 us (1%)
    ppermute x62, waiting for transfers between devices, move(): return lax.ppermute(x, AXES, pairs)  426 us
    ppermute x8, waiting for transfers between devices, bring_back(): lax.ppermute(slots[p], AXES, [(d, o) for o, d in routes(p, m)])  129 us
    ppermute x8, waiting for transfers between devices, bring(): arrived = [lax.ppermute(x[m], AXES, routes(p, m)) for m in range(micro)]  121 us
    dot_general x12, matrix products, times_transposed(): lax.dot_general(former, latter, (((1,), (1,)), ((), ())), preferred_eleme...  119 us
    select_n x48, other arithmetic, ordered(): jnp.where(index == 0, jnp.concatenate([mine, other], axis), jnp.concatena...  116 us
    dot_general x11, matrix products, cross_tokens(): lax.dot_general(former, latter, (((0,), (0,)), ((), ())), preferred_eleme...  103 us
    dot_general x6, matrix products, matmul(): return jnp.dot(former, latter, preferred_element_type=F32)  95.3 us
    ppermute x62, starting transfers between devices, move(): return lax.ppermute(x, AXES, pairs)  70.1 us
  transfers between devices with their start and end apart: 90, of which 35 were waited for; matrix products, arithmetic and copies ran while one was open for 37% of the time, Pallas kernels for 2%

profile of v2, /device:TPU:17, one launch (start us, length us, event | category | flops | bytes accessed | tf_op | source)
XLA Modules:
  0.0 1479.1 jit_solution(7877858122881876540)
XLA Ops:
  23.5 68.2 %collective-permute-done.3 = bf16[256,2048]{1,0:T(8,128)(2,1)} collective-permute-done((bf16[256,2048]{1,0:T(8,128)(2,1)}, bf16[256,2048]{1,0:T(8,128)(2,1)}, u32[]{:S(2)}, u32[]{:S(2)}) %collective-permute-start.3) | collective-permute-done | bytes 1048608 | tf_op jit(solution)/shard_map/ppermute | solution.py:215
  97.2 45.7 %collective-permute-done.4 = bf16[512,2048]{1,0:T(8,128)(2,1)} collective-permute-done((bf16[512,2048]{1,0:T(8,128)(2,1)S(1)}, bf16[512,2048]{1,0:T(8,128)(2,1)}, u32[]{:S(2)}, u32[]{:S(2)}) %collective-permute-start.4) | collective-permute-done | bytes 2097184 | tf_op jit(solution)/shard_map/ppermute | solution.py:155
  180.2 14.5 fusion.128.zq_ref.zk_ref
  194.8 9.8 collective-permute-done.9
  210.1 11.1 fusion.129.zv_ref
  221.2 12.8 attend.1
  248.6 16.1 %collective-permute-done.12 = bf16[1024,512]{1,0:T(8,128)(2,1)} collective-permute-done((bf16[1024,512]{1,0:T(8,128)(2,1)S(1)}, bf16[1024,512]{1,0:T(8,128)(2,1)}, u32[]{:S(2)}, u32[]{:S(2)}) %collective-permute-start.12) | collective-permute-done | bytes 1048608 | tf_op jit(solution)/shard_map/ppermute | solution.py:155
  274.4 19.9 %collective-permute-start.16 = (bf16[256,2048]{1,0:T(8,128)(2,1)}, bf16[256,2048]{1,0:T(8,128)(2,1)S(1)}, u32[]{:S(2)}, u32[]{:S(2)}) collective-permute-start(bf16[256,2048]{1,0:T(8,128)(2,1)} %get-tuple-element.146), channel_id=1, source_target_pairs={{0,2},{4,3},{8,6},{12,7},{2,10},{6,11},{10,14},{14,15},{16,18},{20... | collective-permute-start | bytes 3145736 | tf_op jit(solution)/shard_map/ppermute | solution.py:215
  294.3 51.0 %collective-permute-done.18 = bf16[256,2048]{1,0:T(8,128)(2,1)S(1)} collective-permute-done((bf16[256,2048]{1,0:T(8,128)(2,1)}, bf16[256,2048]{1,0:T(8,128)(2,1)S(1)}, u32[]{:S(2)}, u32[]{:S(2)}) %collective-permute-start.18) | collective-permute-done | bytes 1048608 | tf_op jit(solution)/shard_map/ppermute | solution.py:215
  370.0 33.8 %collective-permute-done.21 = f32[2048]{0:T(1024)S(1)} collective-permute-done((f32[2048]{0:T(1024)S(1)}, f32[2048]{0:T(1024)S(1)}, u32[]{:S(2)}, u32[]{:S(2)}) %collective-permute-start.21) | collective-permute-done | bytes 8224 | tf_op jit(solution)/shard_map/ppermute | solution.py:155
  409.3 40.7 %collective-permute-done.22 = bf16[2048,512]{1,0:T(8,128)(2,1)S(1)} collective-permute-done((bf16[2048,512]{1,0:T(8,128)(2,1)S(1)}, bf16[2048,512]{1,0:T(8,128)(2,1)S(1)}, u32[]{:S(2)}, u32[]{:S(2)}) %collective-permute-start.22) | collective-permute-done | bytes 2097184 | tf_op jit(solution)/shard_map/ppermute | solution.py:155
  460.3 12.0 maximum_select_fusion.3
  490.5 15.8 %fusion.130 = f32[2048,1408]{1,0:T(8,128)} fusion(bf16[2048,2048]{1,0:T(8,128)(2,1)S(1)} %maximum_select_fusion.2, bf16[2048,1408]{1,0:T(8,128)(2,1)S(1)} %maximum_select_fusion.5), kind=kOutput, calls=%fused_computation.343 | convolution fusion | flops 11811160064 | bytes 25690112 | tf_op jit(solution)/shard_map/dot_general | solution.py:22
  506.3 20.9 %multiply_convert_fusion.2 = (bf16[2048,1408]{1,0:T(8,128)(2,1)}, f32[2048,1408]{1,0:T(8,128)}) fusion(f32[2048,1408]{1,0:T(8,128)} %fusion.130, bf16[2048,2048]{1,0:T(8,128)(2,1)} %copy-done.12, bf16[2048,1408]{1,0:T(8,128)(2,1)S(1)} %maximum_select_fusion.4), kind=kOutput, calls=%fused_computation.6 | convolution fusion | flops 11816927232 | bytes 42991616 | tf_op jit(solution)/shard_map/dot_general | solution.py:22
  527.2 11.3 fusion.13
  546.1 24.7 %multiply_convert_fusion.1 = (bf16[2048,1408]{1,0:T(8,128)(2,1)}, bf16[2048,1408]{1,0:T(8,128)(2,1)}) fusion(f32[2048,1408]{1,0:T(8,128)} %fusion.130, f32[2048,1408]{1,0:T(8,128)} %get-tuple-element.76, bf16[2048,2048]{1,0:T(8,128)(2,1)} %maximum_select_fusion.3, bf16[2048,1408]{1,0:T(8,128)(2,1)} %maximum_select_fusion.6), kind=kOutput, calls=%fused_computation.5 | convolution fusion | flops 11822694400 | bytes 48758784 | tf_op jit(solution)/shard_map/dot_general | solution.py:22
  570.7 12.4 fusion.31
  583.2 11.4 add_convert_fusion.1
  595.0 10.7 fusion.34
  605.8 11.0 convolution_convert_fusion.3
  617.4 12.2 convolution_convert_fusion.5
  629.7 10.9 fusion.16
  640.9 13.5 convert_add_fusion.2
  654.5 26.4 %collective-permute-done.37 = bf16[1024,1408]{1,0:T(8,128)(2,1)S(1)} collective-permute-done((bf16[1024,1408]{1,0:T(8,128)(2,1)S(1)}, bf16[1024,1408]{1,0:T(8,128)(2,1)S(1)}, u32[]{:S(2)}, u32[]{:S(2)}) %collective-permute-start.37) | collective-permute-done | bytes 2883616 | tf_op jit(solution)/shard_map/ppermute | solution.py:155
  686.6 10.8 convolution_convert_fusion.2
  697.4 9.6 convert_add_fusion.3
  710.1 12.4 convolution_convert_fusion.1
  736.2 12.9 collective-permute-done.39
  754.7 22.6 %collective-permute-done.41 = f32[2048]{0:T(1024)S(1)} collective-permute-done((f32[2048]{0:T(1024)S(1)}, f32[2048]{0:T(1024)S(1)}, u32[]{:S(2)}, u32[]{:S(2)}) %collective-permute-start.41) | collective-permute-done | bytes 8224 | tf_op jit(solution)/shard_map/ppermute | solution.py:155
  796.6 14.0 collective-permute-done.30
  816.8 11.4 convolution_convert_fusion
  853.2 11.7 convolution_convert_fusion.6
  867.4 83.6 %collective-permute-done.34 = bf16[256,2048]{1,0:T(8,128)(2,1)S(1)} collective-permute-done((bf16[256,2048]{1,0:T(8,128)(2,1)}, bf16[256,2048]{1,0:T(8,128)(2,1)S(1)}, u32[]{:S(2)}, u32[]{:S(2)}) %collective-permute-start.34) | collective-permute-done | bytes 1048608 | tf_op jit(solution)/shard_map/ppermute | solution.py:224
  952.6 21.0 %collective-permute-done.35 = bf16[256,2048]{1,0:T(8,128)(2,1)} collective-permute-done((bf16[256,2048]{1,0:T(8,128)(2,1)}, bf16[256,2048]{1,0:T(8,128)(2,1)}, u32[]{:S(2)}, u32[]{:S(2)}) %collective-permute-start.35) | collective-permute-done | bytes 1048608 | tf_op jit(solution)/shard_map/ppermute | solution.py:224
  995.9 21.6 %attend_back.1 = (bf16[2048,512]{1,0:T(8,128)(2,1)S(1)}, bf16[2048,512]{1,0:T(8,128)(2,1)S(1)}, bf16[2048,512]{1,0:T(8,128)(2,1)S(1)}) custom-call(f32[4]{0:T(128)S(1)} %dynamic_slice.176.rates, s32[2,2]{1,0:T(2,128)S(1)} %pad_add_fusion.ends, f32[2048,1024]{1,0:T(8,128)} %fusion.128.zq_ref.zk_ref, f32[2048,1024]{1,0:T(8,128)} %fusion.128.zq_ref.zk_ref, ...), custom_call_target="tpu_custom_call" | custom-call | flops 10737418240 | bytes 20971520 | tf_op jit(solution)/shard_map/attend_back/pallas_call | solution.py:117
  1045.1 12.5 collective-permute-done.69
  1063.2 9.6 fusion.39
  1078.7 9.8 add_convert_fusion
  1107.3 11.5 collective-permute-done.58
  1121.2 10.8 fusion.42
  1152.0 35.4 %collective-permute-done.66 = bf16[256,512]{1,0:T(8,128)(2,1)S(1)} collective-permute-done((bf16[256,512]{1,0:T(8,128)(2,1)}, bf16[256,512]{1,0:T(8,128)(2,1)S(1)}, u32[]{:S(2)}, u32[]{:S(2)}) %collective-permute-start.66) | collective-permute-done | bytes 262176 | tf_op jit(solution)/shard_map/ppermute | solution.py:155
  1211.7 13.8 convert_add_fusion
  1241.2 34.1 %collective-permute-done.49 = bf16[2048,512]{1,0:T(8,128)(2,1)S(1)} collective-permute-done((bf16[2048,512]{1,0:T(8,128)(2,1)S(1)}, bf16[2048,512]{1,0:T(8,128)(2,1)S(1)}, u32[]{:S(2)}, u32[]{:S(2)}) %collective-permute-start.49) | collective-permute-done | bytes 2097184 | tf_op jit(solution)/shard_map/ppermute | solution.py:155
  1332.7 10.2 collective-permute-done.73
  1353.2 23.5 %collective-permute-done.60 = bf16[512,1024]{1,0:T(8,128)(2,1)S(1)} collective-permute-done((bf16[512,1024]{1,0:T(8,128)(2,1)S(1)}, bf16[512,1024]{1,0:T(8,128)(2,1)S(1)}, u32[]{:S(2)}, u32[]{:S(2)}) %collective-permute-start.60) | collective-permute-done | bytes 1048608 | tf_op jit(solution)/shard_map/ppermute | solution.py:155
  1378.3 33.4 %collective-permute-done.64 = bf16[512,1024]{1,0:T(8,128)(2,1)S(1)} collective-permute-done((bf16[512,1024]{1,0:T(8,128)(2,1)S(1)}, bf16[512,1024]{1,0:T(8,128)(2,1)S(1)}, u32[]{:S(2)}, u32[]{:S(2)}) %collective-permute-start.64) | collective-permute-done | bytes 1048608 | tf_op jit(solution)/shard_map/ppermute | solution.py:155
  1413.4 11.8 collective-permute-start.61
  1427.3 23.0 %collective-permute-done.54 = bf16[256,2048]{1,0:T(8,128)(2,1)S(1)} collective-permute-done((bf16[256,2048]{1,0:T(8,128)(2,1)S(1)}, bf16[256,2048]{1,0:T(8,128)(2,1)S(1)}, u32[]{:S(2)}, u32[]{:S(2)}) %collective-permute-start.54) | collective-permute-done | bytes 1048608 | tf_op jit(solution)/shard_map/ppermute | solution.py:224
  (547 shorter events, 474.9 us)
Async XLA Ops:
  7.2 88.6 %all-gather.7.cloned.1.call-start = ((), (), s32[]{:S(2)}) async-start(), calls=%async_computation.6 | async-start | bytes 2621440 | tf_op jit(solution)/shard_map/all_gather | solution.py:277
  9.6 138.5 %all-gather.9.cloned.1.call-start = ((), (), s32[]{:S(2)}) async-start(), calls=%async_computation.7 | async-start | bytes 2621440 | tf_op jit(solution)/shard_map/all_gather | solution.py:277
  11.8 79.9 %collective-permute-start.3 = (bf16[256,2048]{1,0:T(8,128)(2,1)}, bf16[256,2048]{1,0:T(8,128)(2,1)}, u32[]{:S(2)}, u32[]{:S(2)}) collective-permute-start(bf16[256,2048]{1,0:T(8,128)(2,1)} %get-tuple-element.150), channel_id=1, source_target_pairs={{1,2},{5,3},{9,6},{13,7},{3,10},{7,11},{11,14},{15,15},{17,18},{21... | collective-permute-start | bytes 3145736 | tf_op jit(solution)/shard_map/ppermute | solution.py:215
  13.1 81.9 %collective-permute-start = (bf16[256,2048]{1,0:T(8,128)(2,1)}, bf16[256,2048]{1,0:T(8,128)(2,1)S(1)}, u32[]{:S(2)}, u32[]{:S(2)}) collective-permute-start(bf16[256,2048]{1,0:T(8,128)(2,1)} %get-tuple-element.151), channel_id=1, source_target_pairs={{0,0},{4,1},{8,4},{12,5},{2,8},{6,9},{10,12},{14,13},{16,16},{20,1... | collective-permute-start | bytes 3145736 | tf_op jit(solution)/shard_map/ppermute | solution.py:215
  19.3 75.7 %collective-permute-start.1 = (bf16[256,2048]{1,0:T(8,128)(2,1)}, bf16[256,2048]{1,0:T(8,128)(2,1)S(1)}, u32[]{:S(2)}, u32[]{:S(2)}) collective-permute-start(bf16[256,2048]{1,0:T(8,128)(2,1)} %get-tuple-element.150), channel_id=1, source_target_pairs={{0,2},{4,3},{8,6},{12,7},{2,10},{6,11},{10,14},{14,15},{16,18},{20... | collective-permute-start | bytes 3145736 | tf_op jit(solution)/shard_map/ppermute | solution.py:215
  23.4 171.3 %all-gather.11.cloned.1.call-start = ((), (), s32[]{:S(2)}) async-start(), calls=%async_computation.8 | async-start | bytes 1310720 | tf_op jit(solution)/shard_map/all_gather | solution.py:277
  95.8 47.1 %collective-permute-start.4 = (bf16[512,2048]{1,0:T(8,128)(2,1)S(1)}, bf16[512,2048]{1,0:T(8,128)(2,1)}, u32[]{:S(2)}, u32[]{:S(2)}) collective-permute-start(bf16[512,2048]{1,0:T(8,128)(2,1)S(1)} %fusion.89), channel_id=1, source_target_pairs={{0,8},{1,9},{2,10},{3,11},{4,12},{5,13},{6,14},{7,15},{8,0},{9,1},... | collective-permute-start | bytes 6291464 | tf_op jit(solution)/shard_map/ppermute | solution.py:155
  95.9 52.2 %collective-permute-start.5 = (bf16[1024,1024]{1,0:T(8,128)(2,1)}, bf16[1024,1024]{1,0:T(8,128)(2,1)}, u32[]{:S(2)}, u32[]{:S(2)}) collective-permute-start(bf16[1024,1024]{1,0:T(8,128)(2,1)} %all-gather.7.cloned.1.call-done), channel_id=1, source_target_pairs={{0,16},{1,17},{2,18},{3,19},{4,20},{5,21},{6,22},{7,23},{8,24},{9,... | collective-permute-start | bytes 6291464 | tf_op jit(solution)/shard_map/ppermute | solution.py:155
  151.1 97.5 %all-gather.13.cloned.1.call-start = ((), (), s32[]{:S(2)}) async-start(), calls=%async_computation.9 | async-start | bytes 3604480 | tf_op jit(solution)/shard_map/all_gather | solution.py:277
  154.9 196.8 %all-gather.15.cloned.1.call-start = ((), (), s32[]{:S(2)}) async-start(), calls=%async_computation.10 | async-start | bytes 3604480 | tf_op jit(solution)/shard_map/all_gather | solution.py:277
  157.3 47.2 %collective-permute-start.9 = (bf16[1024,1024]{1,0:T(8,128)(2,1)}, bf16[1024,1024]{1,0:T(8,128)(2,1)}, u32[]{:S(2)}, u32[]{:S(2)}) collective-permute-start(bf16[1024,1024]{1,0:T(8,128)(2,1)} %all-gather.9.cloned.1.call-done), channel_id=1, source_target_pairs={{0,16},{1,17},{2,18},{3,19},{4,20},{5,21},{6,22},{7,23},{8,24},{9,... | collective-permute-start | bytes 6291464 | tf_op jit(solution)/shard_map/ppermute | solution.py:155
  240.0 212.8 %all-gather.17.cloned.1.call-start = ((), (), s32[]{:S(2)}) async-start(), calls=%async_computation.11 | async-start | bytes 3604480 | tf_op jit(solution)/shard_map/all_gather | solution.py:277
  264.7 86.9 %collective-permute-start.14 = (bf16[1024,1408]{1,0:T(8,128)(2,1)}, bf16[1024,1408]{1,0:T(8,128)(2,1)}, u32[]{:S(2)}, u32[]{:S(2)}) collective-permute-start(bf16[1024,1408]{1,0:T(8,128)(2,1)} %all-gather.13.cloned.1.call-done), channel_id=1, source_target_pairs={{0,16},{1,17},{2,18},{3,19},{4,20},{5,21},{6,22},{7,23},{8,24},{9,... | collective-permute-start | bytes 8650760 | tf_op jit(solution)/shard_map/ppermute | solution.py:155
  265.9 83.0 %collective-permute-start.13 = (bf16[2048,512]{1,0:T(8,128)(2,1)S(1)}, bf16[2048,512]{1,0:T(8,128)(2,1)S(1)}, u32[]{:S(2)}, u32[]{:S(2)}) collective-permute-start(bf16[2048,512]{1,0:T(8,128)(2,1)S(1)} %multiply_convert_fusion.5), channel_id=1, source_target_pairs={{0,8},{1,9},{2,10},{3,11},{4,12},{5,13},{6,14},{7,15},{8,0},{9,1},... | collective-permute-start | bytes 6291464 | tf_op jit(solution)/shard_map/ppermute | solution.py:155
  266.7 78.6 %collective-permute-start.18 = (bf16[256,2048]{1,0:T(8,128)(2,1)}, bf16[256,2048]{1,0:T(8,128)(2,1)S(1)}, u32[]{:S(2)}, u32[]{:S(2)}) collective-permute-start(bf16[256,2048]{1,0:T(8,128)(2,1)} %get-tuple-element.146), channel_id=1, source_target_pairs={{1,2},{5,3},{9,6},{13,7},{3,10},{7,11},{11,14},{15,15},{17,18},{21... | collective-permute-start | bytes 3145736 | tf_op jit(solution)/shard_map/ppermute | solution.py:215
  268.0 78.9 %collective-permute-start.15 = (bf16[256,2048]{1,0:T(8,128)(2,1)}, bf16[256,2048]{1,0:T(8,128)(2,1)S(1)}, u32[]{:S(2)}, u32[]{:S(2)}) collective-permute-start(bf16[256,2048]{1,0:T(8,128)(2,1)} %get-tuple-element.147), channel_id=1, source_target_pairs={{0,0},{4,1},{8,4},{12,5},{2,8},{6,9},{10,12},{14,13},{16,16},{20,1... | collective-permute-start | bytes 3145736 | tf_op jit(solution)/shard_map/ppermute | solution.py:215
  274.4 72.5 %collective-permute-start.16 = (bf16[256,2048]{1,0:T(8,128)(2,1)}, bf16[256,2048]{1,0:T(8,128)(2,1)S(1)}, u32[]{:S(2)}, u32[]{:S(2)}) collective-permute-start(bf16[256,2048]{1,0:T(8,128)(2,1)} %get-tuple-element.146), channel_id=1, source_target_pairs={{0,2},{4,3},{8,6},{12,7},{2,10},{6,11},{10,14},{14,15},{16,18},{20... | collective-permute-start | bytes 3145736 | tf_op jit(solution)/shard_map/ppermute | solution.py:215
  354.1 598.5 %reduce-scatter.17.cloned.1.call-start = ((), (), s32[]{:S(2)}) async-start(), calls=%async_computation.17 | async-start | bytes 3604480 | tf_op jit(solution)/shard_map/reduce_scatter | solution.py:313
  356.7 47.8 %collective-permute-start.25 = (bf16[512,2048]{1,0:T(8,128)(2,1)S(1)}, bf16[512,2048]{1,0:T(8,128)(2,1)S(1)}, u32[]{:S(2)}, u32[]{:S(2)}) collective-permute-start(bf16[512,2048]{1,0:T(8,128)(2,1)S(1)} %copy-done.41), channel_id=1, source_target_pairs={{0,8},{1,9},{2,10},{3,11},{4,12},{5,13},{6,14},{7,15},{8,0},{9,1},... | collective-permute-start | bytes 6291464 | tf_op jit(solution)/shard_map/ppermute | solution.py:155
  368.8 84.0 %collective-permute-start.23 = (bf16[1024,1408]{1,0:T(8,128)(2,1)}, bf16[1024,1408]{1,0:T(8,128)(2,1)}, u32[]{:S(2)}, u32[]{:S(2)}) collective-permute-start(bf16[1024,1408]{1,0:T(8,128)(2,1)} %all-gather.15.cloned.1.call-done), channel_id=1, source_target_pairs={{0,16},{1,17},{2,18},{3,19},{4,20},{5,21},{6,22},{7,23},{8,24},{9,... | collective-permute-start | bytes 8650760 | tf_op jit(solution)/shard_map/ppermute | solution.py:155
  408.1 52.3 %collective-permute-start.26 = (bf16[1024,2048]{1,0:T(8,128)(2,1)}, bf16[1024,2048]{1,0:T(8,128)(2,1)}, u32[]{:S(2)}, u32[]{:S(2)}) collective-permute-start(bf16[1024,2048]{1,0:T(8,128)(2,1)} %maximum_select_fusion.15), channel_id=1, source_target_pairs={{0,4},{1,5},{2,6},{3,7},{4,0},{5,1},{6,2},{7,3},{8,12},{9,13},{10,... | collective-permute-start | bytes 12582920 | tf_op jit(solution)/shard_map/ppermute | solution.py:155
  472.4 66.1 %collective-permute-start.27 = (bf16[1024,1408]{1,0:T(8,128)(2,1)S(1)}, bf16[1024,1408]{1,0:T(8,128)(2,1)}, u32[]{:S(2)}, u32[]{:S(2)}) collective-permute-start(bf16[1024,1408]{1,0:T(8,128)(2,1)S(1)} %copy-done.32), channel_id=1, source_target_pairs={{0,16},{1,17},{2,18},{3,19},{4,20},{5,21},{6,22},{7,23},{8,24},{9,... | collective-permute-start | bytes 8650760 | tf_op jit(solution)/shard_map/ppermute | solution.py:155
  616.8 64.0 %collective-permute-start.37 = (bf16[1024,1408]{1,0:T(8,128)(2,1)S(1)}, bf16[1024,1408]{1,0:T(8,128)(2,1)S(1)}, u32[]{:S(2)}, u32[]{:S(2)}) collective-permute-start(bf16[1024,1408]{1,0:T(8,128)(2,1)S(1)} %copy-done.66), channel_id=1, source_target_pairs={{0,16},{1,17},{2,18},{3,19},{4,20},{5,21},{6,22},{7,23},{8,24},{9,... | collective-permute-start | bytes 8650760 | tf_op jit(solution)/shard_map/ppermute | solution.py:155
  640.5 56.9 %collective-permute-start.28 = (bf16[2048,1024]{1,0:T(8,128)(2,1)}, bf16[2048,1024]{1,0:T(8,128)(2,1)}, u32[]{:S(2)}, u32[]{:S(2)}) collective-permute-start(bf16[2048,1024]{1,0:T(8,128)(2,1)} %convolution_convert_fusion.5), channel_id=1, source_target_pairs={{0,4},{1,5},{2,6},{3,7},{4,0},{5,1},{6,2},{7,3},{8,12},{9,13},{10,... | collective-permute-start | bytes 12582920 | tf_op jit(solution)/shard_map/ppermute | solution.py:155
  686.0 63.0 %collective-permute-start.39 = (bf16[1024,1408]{1,0:T(8,128)(2,1)}, bf16[1024,1408]{1,0:T(8,128)(2,1)S(1)}, u32[]{:S(2)}, u32[]{:S(2)}) collective-permute-start(bf16[1024,1408]{1,0:T(8,128)(2,1)} %convolution_convert_fusion.3), channel_id=1, source_target_pairs={{0,16},{1,17},{2,18},{3,19},{4,20},{5,21},{6,22},{7,23},{8,24},{9,... | collective-permute-start | bytes 8650760 | tf_op jit(solution)/shard_map/ppermute | solution.py:155
  709.0 68.3 %collective-permute-start.29 = (bf16[2048,512]{1,0:T(8,128)(2,1)}, bf16[2048,512]{1,0:T(8,128)(2,1)}, u32[]{:S(2)}, u32[]{:S(2)}) collective-permute-start(bf16[2048,512]{1,0:T(8,128)(2,1)} %dynamic-slice_convert_fusion.3), channel_id=1, source_target_pairs={{0,8},{1,9},{2,10},{3,11},{4,12},{5,13},{6,14},{7,15},{8,0},{9,1},... | collective-permute-start | bytes 6291464 | tf_op jit(solution)/shard_map/ppermute | solution.py:155
  724.9 314.7 %reduce-scatter.13.cloned.1.call-start = ((), (), s32[]{:S(2)}) async-start(), calls=%async_computation.15 | async-start | bytes 3604480 | tf_op jit(solution)/shard_map/reduce_scatter | solution.py:313
  828.2 151.8 %collective-permute-start.44 = (bf16[1024,1408]{1,0:T(8,128)(2,1)}, bf16[1024,1408]{1,0:T(8,128)(2,1)}, u32[]{:S(2)}, u32[]{:S(2)}) collective-permute-start(bf16[1024,1408]{1,0:T(8,128)(2,1)} %convolution_convert_fusion.1), channel_id=1, source_target_pairs={{0,16},{1,17},{2,18},{3,19},{4,20},{5,21},{6,22},{7,23},{8,24},{9,... | collective-permute-start | bytes 8650760 | tf_op jit(solution)/shard_map/ppermute | solution.py:155
  831.1 312.5 %reduce-scatter.11.cloned.1.call-start = ((), (), s32[]{:S(2)}) async-start(), calls=%async_computation.14 | async-start | bytes 1310720 | tf_op jit(solution)/shard_map/reduce_scatter | solution.py:313
  835.5 115.5 %collective-permute-start.34 = (bf16[256,2048]{1,0:T(8,128)(2,1)}, bf16[256,2048]{1,0:T(8,128)(2,1)S(1)}, u32[]{:S(2)}, u32[]{:S(2)}) collective-permute-start(bf16[256,2048]{1,0:T(8,128)(2,1)} %get-tuple-element.141), channel_id=1, source_target_pairs={{2,0},{3,4},{6,8},{7,12},{10,2},{11,6},{14,10},{15,14},{18,16},{19... | collective-permute-start | bytes 3145736 | tf_op jit(solution)/shard_map/ppermute | solution.py:224
  837.5 136.1 %collective-permute-start.35 = (bf16[256,2048]{1,0:T(8,128)(2,1)}, bf16[256,2048]{1,0:T(8,128)(2,1)}, u32[]{:S(2)}, u32[]{:S(2)}) collective-permute-start(bf16[256,2048]{1,0:T(8,128)(2,1)} %get-tuple-element.140), channel_id=1, source_target_pairs={{2,1},{3,5},{6,9},{7,13},{10,3},{11,7},{14,11},{15,15},{18,17},{19... | collective-permute-start | bytes 3145736 | tf_op jit(solution)/shard_map/ppermute | solution.py:224
  849.6 126.8 %collective-permute-start.43 = (bf16[2048,512]{1,0:T(8,128)(2,1)}, bf16[2048,512]{1,0:T(8,128)(2,1)}, u32[]{:S(2)}, u32[]{:S(2)}) collective-permute-start(bf16[2048,512]{1,0:T(8,128)(2,1)} %dynamic-slice_convert_fusion.1), channel_id=1, source_target_pairs={{0,8},{1,9},{2,10},{3,11},{4,12},{5,13},{6,14},{7,15},{8,0},{9,1},... | collective-permute-start | bytes 6291464 | tf_op jit(solution)/shard_map/ppermute | solution.py:155
  866.1 118.2 %collective-permute-start.32 = (bf16[256,2048]{1,0:T(8,128)(2,1)}, bf16[256,2048]{1,0:T(8,128)(2,1)}, u32[]{:S(2)}, u32[]{:S(2)}) collective-permute-start(bf16[256,2048]{1,0:T(8,128)(2,1)} %get-tuple-element.141), channel_id=1, source_target_pairs={{0,0},{1,4},{4,8},{5,12},{8,2},{9,6},{12,10},{13,14},{16,16},{17,2... | collective-permute-start | bytes 3145736 | tf_op jit(solution)/shard_map/ppermute | solution.py:224
  1029.0 251.6 %reduce-scatter.15.cloned.1.call-start = ((), (), s32[]{:S(2)}) async-start(), calls=%async_computation.16 | async-start | bytes 3604480 | tf_op jit(solution)/shard_map/reduce_scatter | solution.py:313
  1036.1 100.8 %collective-permute-start.77 = (bf16[2,512,1408]{2,1,0:T(8,128)(2,1)}, bf16[2,512,1408]{2,1,0:T(8,128)(2,1)}, u32[]{:S(2)}, u32[]{:S(2)}) collective-permute-start(bf16[2,512,1408]{2,1,0:T(8,128)(2,1)} %maximum_select_fusion.23), channel_id=1, source_target_pairs={{0,4},{1,5},{2,6},{3,7},{4,0},{5,1},{6,2},{7,3},{8,12},{9,13},{10,... | collective-permute-start | bytes 8650760 | tf_op jit(solution)/shard_map/ppermute | solution.py:155
  1045.0 261.9 %reduce-scatter.7.cloned.1.call-start = ((), (), s32[]{:S(2)}) async-start(), calls=%async_computation.12 | async-start | bytes 2621440 | tf_op jit(solution)/shard_map/reduce_scatter | solution.py:313
  1059.3 75.1 %collective-permute-start.70 = (bf16[512,1408]{1,0:T(8,128)(2,1)}, bf16[512,1408]{1,0:T(8,128)(2,1)S(1)}, u32[]{:S(2)}, u32[]{:S(2)}) collective-permute-start(bf16[512,1408]{1,0:T(8,128)(2,1)} %maximum_select_fusion.35), channel_id=1, source_target_pairs={{0,8},{1,9},{2,10},{3,11},{4,12},{5,13},{6,14},{7,15},{8,0},{9,1},... | collective-permute-start | bytes 4325384 | tf_op jit(solution)/shard_map/ppermute | solution.py:155
  1121.2 185.7 %reduce-scatter.9.cloned.1.call-start = ((), (), s32[]{:S(2)}) async-start(), calls=%async_computation.13 | async-start | bytes 2621440 | tf_op jit(solution)/shard_map/reduce_scatter | solution.py:313
  1132.1 79.7 %collective-permute-start.48 = (bf16[2048,1024]{1,0:T(8,128)(2,1)}, bf16[2048,1024]{1,0:T(8,128)(2,1)}, u32[]{:S(2)}, u32[]{:S(2)}) collective-permute-start(bf16[2048,1024]{1,0:T(8,128)(2,1)} %add_convert_fusion), channel_id=1, source_target_pairs={{0,4},{1,5},{2,6},{3,7},{4,0},{5,1},{6,2},{7,3},{8,12},{9,13},{10,... | collective-permute-start | bytes 12582920 | tf_op jit(solution)/shard_map/ppermute | solution.py:155
  1134.3 55.9 %collective-permute-start.62 = (bf16[1024,1024]{1,0:T(8,128)(2,1)}, bf16[1024,1024]{1,0:T(8,128)(2,1)}, u32[]{:S(2)}, u32[]{:S(2)}) collective-permute-start(bf16[1024,1024]{1,0:T(8,128)(2,1)} %fusion.49), channel_id=1, source_target_pairs={{0,16},{1,17},{2,18},{3,19},{4,20},{5,21},{6,22},{7,23},{8,24},{9,... | collective-permute-start | bytes 6291464 | tf_op jit(solution)/shard_map/ppermute | solution.py:155
  1136.6 68.7 %collective-permute-start.71 = (bf16[2,512,1408]{2,1,0:T(8,128)(2,1)}, bf16[2,512,1408]{2,1,0:T(8,128)(2,1)}, u32[]{:S(2)}, u32[]{:S(2)}) collective-permute-start(bf16[2,512,1408]{2,1,0:T(8,128)(2,1)} %maximum_select_fusion.19), channel_id=1, source_target_pairs={{0,4},{1,5},{2,6},{3,7},{4,0},{5,1},{6,2},{7,3},{8,12},{9,13},{10,... | collective-permute-start | bytes 8650760 | tf_op jit(solution)/shard_map/ppermute | solution.py:155
  1228.0 47.4 %collective-permute-start.49 = (bf16[2048,512]{1,0:T(8,128)(2,1)S(1)}, bf16[2048,512]{1,0:T(8,128)(2,1)S(1)}, u32[]{:S(2)}, u32[]{:S(2)}) collective-permute-start(bf16[2048,512]{1,0:T(8,128)(2,1)S(1)} %dynamic-slice_convert_fusion), channel_id=1, source_target_pairs={{0,8},{1,9},{2,10},{3,11},{4,12},{5,13},{6,14},{7,15},{8,0},{9,1},... | collective-permute-start | bytes 6291464 | tf_op jit(solution)/shard_map/ppermute | solution.py:155
  1321.2 55.4 %collective-permute-start.60 = (bf16[512,1024]{1,0:T(8,128)(2,1)S(1)}, bf16[512,1024]{1,0:T(8,128)(2,1)S(1)}, u32[]{:S(2)}, u32[]{:S(2)}) collective-permute-start(bf16[512,1024]{1,0:T(8,128)(2,1)S(1)} %maximum_select_fusion.43), channel_id=1, source_target_pairs={{0,8},{1,9},{2,10},{3,11},{4,12},{5,13},{6,14},{7,15},{8,0},{9,1},... | collective-permute-start | bytes 3145736 | tf_op jit(solution)/shard_map/ppermute | solution.py:155
  1330.5 81.1 %collective-permute-start.64 = (bf16[512,1024]{1,0:T(8,128)(2,1)S(1)}, bf16[512,1024]{1,0:T(8,128)(2,1)S(1)}, u32[]{:S(2)}, u32[]{:S(2)}) collective-permute-start(bf16[512,1024]{1,0:T(8,128)(2,1)S(1)} %maximum_select_fusion.45), channel_id=1, source_target_pairs={{0,8},{1,9},{2,10},{3,11},{4,12},{5,13},{6,14},{7,15},{8,0},{9,1},... | collective-permute-start | bytes 3145736 | tf_op jit(solution)/shard_map/ppermute | solution.py:155
  1343.5 108.3 %collective-permute-start.74 = (bf16[2,512,1408]{2,1,0:T(8,128)(2,1)S(1)}, bf16[2,512,1408]{2,1,0:T(8,128)(2,1)S(1)}, u32[]{:S(2)}, u32[]{:S(2)}) collective-permute-start(bf16[2,512,1408]{2,1,0:T(8,128)(2,1)S(1)} %maximum_select_fusion.21), channel_id=1, source_target_pairs={{0,4},{1,5},{2,6},{3,7},{4,0},{5,1},{6,2},{7,3},{8,12},{9,13},{10,... | collective-permute-start | bytes 8650760 | tf_op jit(solution)/shard_map/ppermute | solution.py:155
  1349.2 64.2 %collective-permute-start.56 = (bf16[256,2048]{1,0:T(8,128)(2,1)S(1)}, bf16[256,2048]{1,0:T(8,128)(2,1)S(1)}, u32[]{:S(2)}, u32[]{:S(2)}) collective-permute-start(bf16[256,2048]{1,0:T(8,128)(2,1)S(1)} %get-tuple-element.133), channel_id=1, source_target_pairs={{2,0},{3,4},{6,8},{7,12},{10,2},{11,6},{14,10},{15,14},{18,16},{19... | collective-permute-start | bytes 3145736 | tf_op jit(solution)/shard_map/ppermute | solution.py:224
  1351.2 75.5 %collective-permute-start.57 = (bf16[256,2048]{1,0:T(8,128)(2,1)S(1)}, bf16[256,2048]{1,0:T(8,128)(2,1)S(1)}, u32[]{:S(2)}, u32[]{:S(2)}) collective-permute-start(bf16[256,2048]{1,0:T(8,128)(2,1)S(1)} %get-tuple-element.132), channel_id=1, source_target_pairs={{2,1},{3,5},{6,9},{7,13},{10,3},{11,7},{14,11},{15,15},{18,17},{19... | collective-permute-start | bytes 3145736 | tf_op jit(solution)/shard_map/ppermute | solution.py:224
  1377.0 73.3 %collective-permute-start.54 = (bf16[256,2048]{1,0:T(8,128)(2,1)S(1)}, bf16[256,2048]{1,0:T(8,128)(2,1)S(1)}, u32[]{:S(2)}, u32[]{:S(2)}) collective-permute-start(bf16[256,2048]{1,0:T(8,128)(2,1)S(1)} %get-tuple-element.133), channel_id=1, source_target_pairs={{0,0},{1,4},{4,8},{5,12},{8,2},{9,6},{12,10},{13,14},{16,16},{17,2... | collective-permute-start | bytes 3145736 | tf_op jit(solution)/shard_map/ppermute | solution.py:224
  (130 other events, 2255.4 us)
Sparse Core Ops, SparseCore 0:
  10.2 79.2 all-gather.6
  91.6 49.3 all-gather.8
  151.3 30.1 all-gather.10
  183.5 57.9 all-gather.12
  243.4 94.3 all-gather.14
  354.2 57.8 all-gather.16
  725.0 57.5 reduce-scatter.16
  831.2 120.7 reduce-scatter.12
  1029.2 26.5 reduce-scatter.10
  1058.6 56.0 reduce-scatter.14
  1121.3 42.9 reduce-scatter.6
  1194.3 42.9 reduce-scatter.8

commit v3 on v2

--- a/solution.py
+++ b/solution.py
@@ -12,6 +12,7 @@
 STREAM = 1024
 GROUP = 4
 BLOCK = 256
+TILE = 256
 EPSILON = 1e-06
 AXES = ("rep", "shard")
 LOW = jnp.bfloat16
@@ -133,6 +134,351 @@
     )(rates, ends, z_qk, z_qk, z_vg, d_o)
 
 
+def chunk_copies(chunks, buffer, sems, turn, half=None):
+    count, size = len(chunks), chunks[0].shape[0]
+    copies = []
+    for k, chunk in enumerate(chunks):
+        index = lax.rem(turn - k + count, count)
+        wanted = None
+        if half is not None:
+            wanted = lax.div(index, count // 2) == half
+            index = lax.rem(index, count // 2)
+        target = buffer.at[pl.ds(pl.multiple_of(index * size, size), size)]
+        copies.append((wanted, pltpu.make_async_copy(chunk, target, sems.at[k])))
+    return copies
+
+
+def each(copies, act):
+    for wanted, copy in copies:
+        if wanted is None:
+            act(copy)
+        else:
+            pl.when(wanted)(functools.partial(act, copy))
+
+
+def start(copies):
+    each(copies, lambda copy: copy.start())
+
+
+def finish(copies):
+    each(copies, lambda copy: copy.wait())
+
+
+def estimate(flops, *arrays):
+    moved = sum(x.size * x.dtype.itemsize for x in arrays)
+    return pl.CostEstimate(flops=flops, transcendentals=0, bytes_accessed=moved)
+
+
+def limit(mebibytes):
+    return pltpu.CompilerParams(vmem_limit_bytes=mebibytes << 20)
+
+
+ANYWHERE = pl.BlockSpec(memory_space=pl.ANY)
+
+
+def weight_buffer(chunks, share=1):
+    size = len(chunks) * chunks[0].shape[0] // share
+    return [pltpu.VMEM((size, chunks[0].shape[1]), LOW), pltpu.SemaphoreType.DMA((len(chunks),))]
+
+
+def tile_rows(width, column=0):
+    return pl.BlockSpec((TILE, width), lambda i, *_: (i, column))
+
+
+def joined_rows(width, tiles):
+    own = pl.BlockSpec((TILE, width), lambda i, s: (jnp.clip(i - s[0] * tiles, 0, tiles - 1), 0))
+    other = pl.BlockSpec(
+        (TILE, width), lambda i, s: (jnp.clip(i - (1 - s[0]) * tiles, 0, tiles - 1), 0)
+    )
+    return [own, other]
+
+
+def enter_kernel(tiles, blocks, project, spots, own_ref, other_ref, *refs):
+    i = pl.program_id(0)
+    rows = jnp.where(i // tiles == spots[0], own_ref[...], other_ref[...])
+    part = rows.shape[1] // len(blocks)
+    permuted = jnp.concatenate([rows[:, n * part : (n + 1) * part] for n in blocks], axis=1)
+    if not project:
+        all_ref, quarter_ref = refs
+        all_ref[...] = permuted
+        held = all_ref
+    else:
+        chunks, (h_ref, z_ref, scale_ref, quarter_ref, held, buffer, sems) = refs[:-7], refs[-7:]
+        held[...] = permuted
+        copies = chunk_copies(chunks, buffer, sems, spots[2])
+
+        @pl.when(i == 0)
+        def _():
+            start(copies)
+
+        x = rows.astype(F32)
+        scale = lax.rsqrt(jnp.mean(x * x, axis=-1, keepdims=True) + EPSILON)
+        scale_ref[...] = scale
+        hidden = (permuted.astype(F32) * scale).astype(LOW)
+        h_ref[...] = hidden
+
+        @pl.when(i == 0)
+        def _():
+            finish(copies)
+
+        z_ref[...] = matmul(hidden, buffer[...])
+    size = quarter_ref.shape[1]
+    quarter_ref[...] = held[:, pl.ds(pl.multiple_of(spots[1] * size, size), size)]
+
+
+def enter(spots, blocks, own, other, chunks=()):
+    width = own.shape[1]
+    count, tiles = 2 * own.shape[0], own.shape[0] // TILE
+    shape = jax.ShapeDtypeStruct
+    quarter = shape((count, width // GROUP), LOW)
+    if chunks:
+        columns = chunks[0].shape[1]
+        outs = [shape((count, width), LOW), shape((count, columns), F32), shape((count, 1), F32), quarter]
+        scratch = [pltpu.VMEM((TILE, width), LOW), *weight_buffer(chunks)]
+    else:
+        columns, scratch = 0, []
+        outs = [shape((count, width), LOW), quarter]
+    return pl.pallas_call(
+        functools.partial(enter_kernel, tiles, blocks, bool(chunks)),
+        out_shape=outs,
+        grid_spec=pltpu.PrefetchScalarGridSpec(
+            num_scalar_prefetch=1,
+            grid=(2 * tiles,),
+            in_specs=joined_rows(width, tiles) + [ANYWHERE] * len(chunks),
+            out_specs=[tile_rows(o.shape[1]) for o in outs],
+            scratch_shapes=scratch,
+        ),
+        compiler_params=limit(40),
+        cost_estimate=estimate(2 * count * width * columns, own, other, *chunks, *outs),
+        name="enter",
+    )(spots, own, other, *chunks)
+
+
+def project_kernel(spots, h_ref, *refs):
+    chunks, (z_ref, buffer, sems) = refs[:-3], refs[-3:]
+    copies = chunk_copies(chunks, buffer, sems, spots[2])
+
+    @pl.when(pl.program_id(0) == 0)
+    def _():
+        start(copies)
+        finish(copies)
+
+    z_ref[...] = matmul(h_ref[...], buffer[...])
+
+
+def project(spots, hidden, chunks):
+    count, width = hidden.shape
+    out = jax.ShapeDtypeStruct((count, chunks[0].shape[1]), F32)
+    return pl.pallas_call(
+        project_kernel,
+        out_shape=out,
+        grid_spec=pltpu.PrefetchScalarGridSpec(
+            num_scalar_prefetch=1,
+            grid=(count // TILE,),
+            in_specs=[tile_rows(width)] + [ANYWHERE] * len(chunks),
+            out_specs=tile_rows(out.shape[1]),
+            scratch_shapes=weight_buffer(chunks),
+        ),
+        compiler_params=limit(40),
+        cost_estimate=estimate(2 * count * width * out.shape[1], hidden, *chunks, out),
+        name="project",
+    )(spots, hidden, *chunks)
+
+
+def unit_kernel(spots, own_ref, other_ref, *refs):
+    chunks, rest = refs[:-9], refs[-9:]
+    h_ref, one_ref, two_ref, product_ref, scale_ref, first, second, sem_one, sem_two = rest
+    split = len(chunks) // 2
+    copies = [
+        chunk_copies(chunks[:split], first, sem_one, spots[2]),
+        chunk_copies(chunks[split:], second, sem_two, spots[2]),
+    ]
+    begins = pl.program_id(0) == 0
+
+    @pl.when(begins)
+    def _():
+        start(copies[0])
+        start(copies[1])
+
+    mine, other = own_ref[...], other_ref[...]
+    swapped = spots[0] == 1
+    middle = jnp.concatenate(
+        [jnp.where(swapped, other, mine), jnp.where(swapped, mine, other)], axis=1
+    ).astype(F32)
+    scale = lax.rsqrt(jnp.mean(middle * middle, axis=-1, keepdims=True) + EPSILON)
+    scale_ref[...] = scale
+    hidden = (middle * scale).astype(LOW)
+    h_ref[...] = hidden
+
+    @pl.when(begins)
+    def _():
+        finish(copies[0])
+
+    z_one = matmul(hidden, first[...])
+
+    @pl.when(begins)
+    def _():
+        finish(copies[1])
+
+    z_two = matmul(hidden, second[...])
+    one_ref[...] = z_one.astype(LOW)
+    two_ref[...] = z_two.astype(LOW)
+    product_ref[...] = (z_one * z_two).astype(LOW)
+
+
+def gated_unit(spots, own, other, first, second):
+    count, width, units = own.shape[0], 2 * own.shape[1], first[0].shape[1]
+    shape = jax.ShapeDtypeStruct
+    outs = [shape((count, width), LOW)] + [shape((count, units), LOW)] * 3 + [shape((count, 1), F32)]
+    (buffer, sems) = weight_buffer(first)
+    return pl.pallas_call(
+        unit_kernel,
+        out_shape=outs,
+        grid_spec=pltpu.PrefetchScalarGridSpec(
+            num_scalar_prefetch=1,
+            grid=(count // TILE,),
+            in_specs=[tile_rows(width // 2)] * 2 + [ANYWHERE] * (2 * len(first)),
+            out_specs=[tile_rows(o.shape[1]) for o in outs],
+            scratch_shapes=[buffer, buffer, sems, sems],
+        ),
+        compiler_params=limit(48),
+        cost_estimate=estimate(4 * count * width * units, own, other, *first, *second, *outs),
+        name="gated_unit",
+    )(spots, own, other, *first, *second)
+
+
+def unit_back_kernel(spots, dy_ref, one_ref, two_ref, *refs):
+    chunks, (d_one_ref, d_two_ref, sum_ref, buffer, sems) = refs[:-5], refs[-5:]
+    copies = chunk_copies(chunks, buffer, sems, spots[2])
+
+    @pl.when(pl.program_id(0) == 0)
+    def _():
+        start(copies)
+        finish(copies)
+
+    d_product = matmul(dy_ref[...], buffer[...])
+    z_one, z_two = one_ref[...].astype(F32), two_ref[...].astype(F32)
+    d_one = d_product * z_two
+    d_one_ref[...] = d_one.astype(LOW)
+    d_two_ref[...] = (d_product * z_one).astype(LOW)
+    sum_ref[...] = jnp.sum(d_one * z_one, axis=-1, keepdims=True)
+
+
+def gated_unit_back(spots, dy, z_one, z_two, chunks):
+    count, width, units = dy.shape[0], dy.shape[1], z_one.shape[1]
+    shape = jax.ShapeDtypeStruct
+    outs = [shape((count, units), LOW)] * 2 + [shape((count, 1), F32)]
+    return pl.pallas_call(
+        unit_back_kernel,
+        out_shape=outs,
+        grid_spec=pltpu.PrefetchScalarGridSpec(
+            num_scalar_prefetch=1,
+            grid=(count // TILE,),
+            in_specs=[tile_rows(width), tile_rows(units), tile_rows(units)] + [ANYWHERE] * len(chunks),
+            out_specs=[tile_rows(o.shape[1]) for o in outs],
+            scratch_shapes=weight_buffer(chunks),
+        ),
+        compiler_params=limit(40),
+        cost_estimate=estimate(2 * count * width * units, dy, z_one, z_two, *chunks, *outs),
+        name="gated_unit_back",
+    )(spots, dy, z_one, z_two, *chunks)
+
+
+def fold_kernel(members, keeps, spots, *refs):
+    values, refs = refs[:members], refs[members:]
+    arrived, refs = (refs[0], refs[1:]) if keeps else (None, refs)
+    outs = 2 if keeps else 1
+    chunks, refs = refs[: -outs - 2 * members], refs[-outs - 2 * members :]
+    outs, buffers, sems = refs[:outs], refs[outs : outs + members], refs[outs + members :]
+    each_count = len(chunks) // members
+    half = spots[0] if keeps else 1 - spots[0]
+    begins = pl.program_id(0) == 0
+    copies = [
+        chunk_copies(chunks[m * each_count : (m + 1) * each_count], buffers[m], sems[m], spots[2], half)
+        for m in range(members)
+    ]
+
+    @pl.when(begins)
+    def _():
+        for m in range(members):
+            start(copies[m])
+
+    whole = None
+    for m in range(members):
+        pl.when(begins)(functools.partial(finish, copies[m]))
+        term = times_transposed(values[m][...], buffers[m][...])
+        whole = term if whole is None else whole + term
+    if not keeps:
+        outs[0][...] = whole.astype(LOW)
+    else:
+        whole = whole + arrived[...].astype(F32)
+        size = whole.shape[1] // 2
+        upper = spots[3] == 1
+        outs[0][...] = jnp.where(upper, whole[:, :size], whole[:, size:]).astype(LOW)
+        outs[1][...] = jnp.where(upper, whole[:, size:], whole[:, :size])
+
+
+def fold_half(spots, values, weights, arrived=None):
+    count = values[0].shape[0]
+    half = len(weights[0]) * weights[0][0].shape[0] // 2
+    shape = jax.ShapeDtypeStruct
+    if arrived is None:
+        outs, extra = [shape((count, half), LOW)], []
+    else:
+        outs, extra = [shape((count, half // 2), LOW), shape((count, half // 2), F32)], [arrived]
+    buffers, sems = zip(*[weight_buffer(w, 2) for w in weights])
+    chunks = [x for w in weights for x in w]
+    flops = sum(2 * count * half * v.shape[1] for v in values)
+    found = pl.pallas_call(
+        functools.partial(fold_kernel, len(values), arrived is not None),
+        out_shape=outs,
+        grid_spec=pltpu.PrefetchScalarGridSpec(
+            num_scalar_prefetch=1,
+            grid=(count // TILE,),
+            in_specs=[tile_rows(v.shape[1]) for v in values]
+            + [tile_rows(half)] * len(extra)
+            + [ANYWHERE] * len(chunks),
+            out_specs=[tile_rows(o.shape[1]) for o in outs],
+            scratch_shapes=[*buffers, *sems],
+        ),
+        compiler_params=limit(40),
+        cost_estimate=estimate(flops, *values, *extra, *chunks[: len(chunks) // 2], *outs),
+        name="fold_half",
+    )(spots, *values, *extra, *chunks)
+    return found[0] if arrived is None else found
+
+
+def place_kernel(count, spots, *refs):
+    quarter = pl.program_id(0)
+    cross = lax.rem(lax.div(quarter, 2) + spots[0], 2) * 2 + lax.rem(lax.rem(quarter, 2) + spots[3], 2)
+    for n in range(4):
+
+        @pl.when(cross == n)
+        def _():
+            size = refs[n].shape[1] // count
+            for m in range(count):
+                refs[4 + m][...] = refs[n][:, m * size : (m + 1) * size].astype(F32)
+
+
+def place_quarters(spots, four, count):
+    rows, columns = four[0].shape
+    size = columns // count
+    outs = [jax.ShapeDtypeStruct((rows, GROUP * size), F32)] * count
+    return pl.pallas_call(
+        functools.partial(place_kernel, count),
+        out_shape=outs,
+        grid_spec=pltpu.PrefetchScalarGridSpec(
+            num_scalar_prefetch=1,
+            grid=(GROUP,),
+            in_specs=[pl.BlockSpec((rows, columns), lambda q, s: (0, 0))] * 4,
+            out_specs=[pl.BlockSpec((rows, size), lambda q, s: (0, q))] * count,
+        ),
+        compiler_params=limit(40),
+        cost_estimate=estimate(0, *four, *outs),
+        name="place_quarters",
+    )(spots, *four)
+
+
 def tie(*values):
     return lax.optimization_barrier(values)
 
@@ -149,6 +495,8 @@
     rows = width // shards
     part = rows // spread
     columns = functools.partial(lax.dynamic_slice_in_dim, axis=1)
+    spots = jnp.stack([c, quarter, a, b]).astype(jnp.int32)
+    blocks = [z * spread + k for k in range(spread) for z in range(shards)]
 
     def move(x, target):
         pairs = [(r * shards + s, target(r) * shards + s) for r in range(reps) for s in range(shards)]
@@ -188,16 +536,6 @@
                 if from_batch == batch:
                     found.append((from_r * shards + from_s, r * shards + s))
         return found
-
-    def permuted(x):
-        return jnp.concatenate(
-            [
-                x[:, (z * spread + k) * part : (z * spread + k + 1) * part]
-                for k in range(spread)
-                for z in range(shards)
-            ],
-            axis=1,
-        )
 
     def natural(x):
         return jnp.concatenate(
@@ -214,7 +552,7 @@
         for p in range(per_block):
             arrived = [lax.ppermute(x[m], AXES, routes(p, m)) for m in range(micro)]
             slots.append(functools.reduce(jnp.add, arrived))
-        return permuted(jnp.concatenate(slots, axis=0))
+        return jnp.concatenate(slots, axis=0)
 
     def bring_back(x):
         slots = natural(x).reshape(per_block, run, width)
@@ -237,9 +575,6 @@
     def gather_rows_b(x):
         return ordered(b, x, swap_b(x), 0)
 
-    def gather_rows_c(x):
-        return ordered(c, x, swap_c(x), 0)
-
     def total(x):
         x = x + swap_c(x)
         return x + swap_b(x)
@@ -247,6 +582,13 @@
     def fold_c(product):
         sent = swap_c(product(1 - c).astype(LOW))
         return product(c) + sent.astype(F32)
+
+    def fold_sent(values, members):
+        return swap_c(fold_half(spots, values, members))
+
+    def fold_kept(values, members, arrived):
+        sent, mine = fold_half(spots, values, members, arrived)
+        return mine, swap_b(sent)
 
     def fold_b(x):
         sent = swap_b(columns(x, (1 - b) * own, own).astype(LOW))
@@ -312,24 +654,18 @@
             whole = whole + x.astype(F32)
         return lax.psum_scatter(whole.astype(LOW), "shard", scatter_dimension=0, tiled=True)
 
-    def spread_out(x):
-        full = by_spread([x] + over_spread(x))
-        return gather_quarters(full)
-
-    def gather_quarters(full):
-        pair = ordered(b, full[None], swap_b(full)[None], 0)
-        return ordered(c, pair[None], swap_c(pair)[None], 0)
-
-    def as_outputs(four, count, unpermute):
-        size = four.shape[3] // count
-        found = []
-        for n in range(count):
-            flat = jnp.concatenate(
-                [four[i, j][:, n * size : (n + 1) * size] for i in range(2) for j in range(2)],
-                axis=1,
-            )
-            found.append((natural(flat) if unpermute else flat).astype(F32))
-        return found
+    def spread_a(x):
+        return by_spread([x] + over_spread(x))
+
+    def spread_b(x):
+        return (x, swap_b(x))
+
+    def spread_c(two):
+        return [*two, swap_c(two[0]), swap_c(two[1])]
+
+    def features_in_order(four):
+        pair = [ordered(b, four[n], four[n + 1], 1) for n in (0, 2)]
+        return natural(ordered(c, pair[0], pair[1], 1)).astype(F32)
 
 
     w_query, w_key, w_value, w_gate, w_out, w_one, w_two, w_down = weights
@@ -342,7 +678,8 @@
 
     heads = HEADS // GROUP
     rates = lax.dynamic_slice_in_dim(decay_rates, quarter * heads, heads, 0)
-    cuts = gather_rows_c(gather_rows_b(lengths.reshape(1, -1))).reshape(GROUP, micro, -1)
+    cuts = gather_rows_b(lengths.reshape(1, -1))
+    cuts = ordered(c, cuts, swap_c(cuts), 0).reshape(GROUP, micro, -1)
     if streams == 1:
         batch = place // GROUP
         member = place % GROUP
@@ -364,121 +701,135 @@
     x_pair, s_qk, g_vg = tie(x_pair, s_qk, g_vg)
 
     s_vg = over_spread(g_vg)
-    x_all = gather_rows_c(x_pair)
-    x_float = x_all.astype(F32)
-    x_scale = lax.rsqrt(jnp.mean(x_float * x_float, axis=-1, keepdims=True) + EPSILON)
-    hidden_one = (x_float * x_scale).astype(LOW)
-    w_qk = by_spread([g_qk, *s_qk])
-    z_qk = matmul(hidden_one, w_qk)
-    z_qk, s_vg, g_o = tie(z_qk, s_vg, g_o)
+    dy_run = bring(cotangent)
+    w_qk = [g_qk, *s_qk]
+    hidden_one, z_qk, x_scale, x_own = enter(spots, blocks, x_pair, swap_c(x_pair), w_qk)
+    z_qk, hidden_one, s_vg, g_o, dy_run = tie(z_qk, hidden_one, s_vg, g_o, dy_run)
 
     s_o = over_spread(g_o)
-    w_vg = by_spread([g_vg, *s_vg])
-    z_vg = matmul(hidden_one, w_vg)
+    dy_pair = gather_rows_b(dy_run)
+    w_vg = [g_vg, *s_vg]
+    z_vg = project(spots, hidden_one, w_vg)
     attended = attend(rates, ends, z_qk, z_vg)
     gate = z_vg[:, own:]
     o_scale = lax.rsqrt(total(jnp.sum(attended * attended, axis=-1)) / width + EPSILON)[:, None]
-    o_normed = attended * o_scale
-    gated = (o_normed * gate).astype(LOW)
-    gated, s_o, g_1 = tie(gated, s_o, g_1)
+    lifted = (attended * gate).astype(LOW)
+    lifted, dy_pair, s_o, g_1 = tie(lifted, dy_pair, s_o, g_1)
 
     s_1 = over_spread(g_1)
-    dy_run = bring(cotangent)
-    gated = gather_b(gated)
+    lifted = gather_b(lifted)
+    dy_all, dy_own = enter(spots, blocks, dy_pair, swap_c(dy_pair))
     w_o = in_row_order(by_spread([g_o, *s_o]))
-    gated, s_1, g_2, dy_run = tie(gated, s_1, g_2, dy_run)
+    lifted, s_1, g_2, dy_all, o_scale = tie(lifted, s_1, g_2, dy_all, o_scale)
 
     s_2 = over_spread(g_2)
-    gated = gather_c(gated)
-    x_own = columns(x_all, quarter * own, own).astype(F32)
-    middle = x_own + matmul(gated, w_o)
-    m_scale = lax.rsqrt(total(jnp.sum(middle * middle, axis=-1)) / width + EPSILON)[:, None]
-    m_normed = middle * m_scale
-    hidden_two = gather_b(m_normed.astype(LOW))
-    w_1 = by_spread([g_1, *s_1])
-    hidden_two, s_2, g_d = tie(hidden_two, s_2, g_d)
+    lifted = gather_c(lifted)
+    branch = o_scale * matmul(lifted, w_o)
+    middle = x_own.astype(F32) + branch
+    low_middle = gather_b(middle.astype(LOW))
+    low_middle, s_2, g_d = tie(low_middle, s_2, g_d)
 
     s_d = over_spread(g_d)
-    hidden_two = gather_c(hidden_two)
-    dy_all = gather_rows_c(gather_rows_b(dy_run))
-    z_one = matmul(hidden_two, w_1)
-    w_2 = by_spread([g_2, *s_2])
-    z_two = matmul(hidden_two, w_2)
-    product = (z_one * z_two).astype(LOW)
+    w_1, w_2 = [g_1, *s_1], [g_2, *s_2]
+    hidden_two, z_one, z_two, product, m_scale = gated_unit(
+        spots, low_middle, swap_c(low_middle), w_1, w_2
+    )
     t_down = away(dy_all, product)
     z_one, z_two, product, t_down, s_d = tie(z_one, z_two, product, t_down, s_d)
 
     r_down = sent_a(t_down)
-    w_d = by_spread([g_d, *s_d])
-    d_product = matmul(dy_all, w_d)
-    d_one = (d_product * z_two).astype(LOW)
-    d_two = (d_product * z_one).astype(LOW)
+    w_d = [g_d, *s_d]
+    d_one, d_two, lean_m = gated_unit_back(spots, dy_all, z_one, z_two, w_d)
+    arrived = fold_sent([d_one, d_two], [w_1, w_2])
     t_one = away(hidden_two, d_one)
+    lean_m = total(lean_m[:, 0])
+    d_one, d_two, t_one, arrived, lean_m = tie(d_one, d_two, t_one, arrived, lean_m)
+
+    mine, crossed = fold_kept([d_one, d_two], [w_1, w_2], arrived)
     k_down = kept(dy_all, product)
-    d_hidden = fold_c(
-        lambda h: times_transposed(d_one, row_half(w_1, h)) + times_transposed(d_two, row_half(w_2, h))
-    )
-    d_hidden, d_one, d_two, t_one, r_down, k_down = tie(
-        d_hidden, d_one, d_two, t_one, r_down, k_down
-    )
-
     r_one = sent_a(t_one)
+    t_two = away(hidden_two, d_two)
+    k_one = kept(hidden_two, d_one)
+    r_down, k_down, crossed, t_two = tie(r_down, k_down, crossed, t_two)
+
     f_down = summed(k_down, r_down)
-    d_hidden = fold_b(d_hidden)
-    k_one = kept(hidden_two, d_one)
-    t_two = away(hidden_two, d_two)
-    d_hidden, r_one, k_one, t_two = tie(d_hidden, r_one, k_one, t_two)
-
+    d_hidden = mine + crossed.astype(F32)
+    m_normed = middle * m_scale
+    lean = lean_m[:, None] * (2.0 / width)
+    d_middle = dy_own.astype(F32) + m_scale * (d_hidden - m_normed * lean)
+    d_branch = d_middle.astype(LOW)
+    lean_o = total(jnp.sum(d_middle * branch, axis=-1))
+    d_gated = fold_c(lambda h: times_transposed(d_branch, row_half(w_o, h)))
     r_two = sent_a(t_two)
+    k_two = kept(hidden_two, d_two)
+    r_one, k_one, d_gated, lean_o = tie(r_one, k_one, d_gated, lean_o)
+
     f_one = summed(k_one, r_one)
-    lean = total(jnp.sum(m_normed * d_hidden, axis=-1))[:, None] / width
-    dy_own = columns(dy_all, quarter * own, own).astype(F32)
-    d_middle = dy_own + m_scale * (d_hidden - m_normed * lean)
-    d_branch = d_middle.astype(LOW)
-    d_gated = fold_b(fold_c(lambda h: times_transposed(d_branch, row_half(w_o, h))))
-    k_two = kept(hidden_two, d_two)
-    p_out = cross_tokens(gated, d_branch).astype(LOW).reshape(shards, spread, part, -1)
-    p_out = jnp.transpose(p_out, (1, 0, 2, 3)).reshape(spread, width // spread, -1)
+    d_gated = fold_b(d_gated)
+    p_out = cross_tokens(lifted, (o_scale * d_middle).astype(LOW)).astype(LOW)
+    p_out = jnp.transpose(p_out.reshape(shards, spread, part, -1), (1, 0, 2, 3))
+    p_out = p_out.reshape(spread, width // spread, -1)
     t_out = [lax.dynamic_index_in_dim(p_out, (a + k) % spread, 0, False) for k in range(spread)]
-    d_gated, r_two, k_two, t_out = tie(d_gated, r_two, k_two, t_out)
+    result = fold_sent([product], [w_d])
+    d_gated, r_two, k_two, t_out, f_down, result = tie(d_gated, r_two, k_two, t_out, f_down, result)
 
     r_out = sent_a(t_out[1:])
     f_two = summed(k_two, r_two)
+    y_down = spread_a(f_down)
+    o_normed = attended * o_scale
     d_gate = (d_gated * o_normed).astype(LOW)
-    d_normed = d_gated * gate
-    lean = total(jnp.sum(o_normed * d_normed, axis=-1))[:, None] / width
-    d_attended = (o_scale * (d_normed - o_normed * lean)).astype(LOW)
+    lean = lean_o[:, None] / width
+    d_attended = (o_scale * (d_gated * gate - o_normed * lean)).astype(LOW)
+    result, result_b = fold_kept([product], [w_d], result)
     d_query, d_key, d_value = attend_back(rates, ends, z_qk, z_vg, d_attended)
     d_qk = jnp.concatenate([d_query, d_key], axis=1)
     d_vg = jnp.concatenate([d_value, d_gate], axis=1)
     t_qk = away(hidden_one, d_qk)
-    d_qk, d_vg, r_out, t_qk = tie(d_qk, d_vg, r_out, t_qk)
+    d_qk, d_vg, t_qk, r_out, f_one, y_down, result_b = tie(
+        d_qk, d_vg, t_qk, r_out, f_one, y_down, result_b
+    )
 
     r_qk = sent_a(t_qk)
     f_out = summed(t_out[0], r_out)
     t_vg = away(hidden_one, d_vg)
     r_vg = sent_a(t_vg)
+    arrived = fold_sent([d_qk, d_vg], [w_qk, w_vg])
+    lean_x = total(
+        jnp.sum(z_qk * d_qk.astype(F32), axis=-1) + jnp.sum(z_vg * d_vg.astype(F32), axis=-1)
+    )
     k_qk = kept(hidden_one, d_qk)
-    k_vg = kept(hidden_one, d_vg)
+    mine, crossed = fold_kept([d_qk, d_vg], [w_qk, w_vg], arrived)
+    k_qk, r_qk, k_vg_in, f_two = tie(k_qk, r_qk, hidden_one, f_two)
+
     f_qk = summed(k_qk, r_qk)
+    k_vg = kept(k_vg_in, d_vg)
+    output = (middle + (result + result_b.astype(F32))).astype(LOW)
+    d_hidden = mine + crossed.astype(F32)
+    x_normed = x_own.astype(F32) * x_scale
+    lean = lean_x[:, None] / width
+    input_grad = (d_middle + x_scale * (d_hidden - x_normed * lean)).astype(LOW)
+    k_vg, r_vg, f_one, f_two, f_out, output, input_grad = tie(
+        k_vg, r_vg, f_one, f_two, f_out, output, input_grad
+    )
+
     f_vg = summed(k_vg, r_vg)
-    d_hidden = fold_b(
-        fold_c(
-            lambda h: times_transposed(d_qk, row_half(w_qk, h))
-            + times_transposed(d_vg, row_half(w_vg, h))
-        )
+    input_grad, output = to_runs(input_grad), to_runs(output)
+    g_down = spread_c(spread_b(y_down))
+    g_one = spread_c(spread_b(spread_a(f_one)))
+    g_two = spread_c(spread_b(spread_a(f_two)))
+    g_out = spread_c(spread_b(spread_a(f_out)))
+    g_qk = spread_c(spread_b(spread_a(f_qk)))
+    g_vg = spread_c(spread_b(spread_a(f_vg)))
+    return (
+        output,
+        input_grad,
+        *place_quarters(spots, g_qk, 2),
+        *place_quarters(spots, g_vg, 2),
+        features_in_order(g_out),
+        *place_quarters(spots, g_one, 1),
+        *place_quarters(spots, g_two, 1),
+        *place_quarters(spots, g_down, 1),
     )
-    x_normed = x_own * x_scale
-    lean = total(jnp.sum(x_normed * d_hidden, axis=-1))[:, None] / width
-    input_grad = to_runs((d_middle + x_scale * (d_hidden - x_normed * lean)).astype(LOW))
-
-    result = fold_b(fold_c(lambda h: times_transposed(product, row_half(w_d, h))))
-    output = to_runs((middle + result).astype(LOW))
-
-    grads = []
-    for reduced, count in ((f_qk, 2), (f_vg, 2), (f_out, 1), (f_one, 1), (f_two, 1), (f_down, 1)):
-        grads += as_outputs(spread_out(reduced), count, reduced is f_out)
-    return (output, input_grad, *grads)
 
 
 def solution(mesh):

time: 1510 us -> 1430 us (0.947); the launches traced: 1480 us -> 1420 us
  Pallas kernels: 34.3 us -> 260 us
  matrix products: 317 us -> 128 us
  other arithmetic: 249 us -> 123 us
    pallas_call x0 -> x16, Pallas kernels: none -> 226 us  [the longest x6 102 us: fold_half(): pl.pallas_call(functools.partial(fold_kernel, len(values), arrived is not...]
    dot_general x12 -> x2, matrix products: 119 us -> 12.4 us  [times_transposed(): lax.dot_general(former, latter, (((1,), (1,)), ((), ())), preferred_eleme...]
    dot_general x6 -> x1, matrix products: 95.3 us -> 10.1 us  [matmul(): return jnp.dot(former, latter, preferred_element_type=F32)]
    select_n x48 -> x20, other arithmetic: 116 us -> 35.3 us  [ordered(): jnp.where(index == 0, jnp.concatenate([mine, other], axis), jnp.concatena...]
    convert_element_type x12 -> x2, other arithmetic: 48.1 us -> 9.11 us  [the longest x1 6.57 us: body(): input_grad = (d_middle + x_scale * (d_hidden - x_normed * lean)).astype(LOW)]
    ppermute x8, starting transfers between devices: 12.5 us -> 49.2 us  [bring_back(): lax.ppermute(slots[p], AXES, [(d, o) for o, d in routes(p, m)])]
    ppermute x8, waiting for transfers between devices: 121 us -> 147 us  [bring(): arrived = [lax.ppermute(x[m], AXES, routes(p, m)) for m in range(micro)]]
    add x2 -> x3, other arithmetic: 22.7 us -> 0.01 us  [the longest x2 0.01 us: total(): return x + swap_b(x)]
  transfers between devices with their start and end apart: 90 -> 94, of which waited for: 35 -> 33; matrix products, arithmetic and copies ran while one was open for 37% -> 19% of each run, Pallas kernels for 2% -> 15%
where the time goes in v3:
time: 1430 us; the launch traced here: 1420 us
  waiting for transfers between devices  691 us (48%)
  Pallas kernels  260 us (18%)
  starting transfers between devices  138 us (10%)
  matrix products  128 us (9%)
  other arithmetic  123 us (9%)
  local copies, waits for them, and re-layouts  67.6 us (5%)
  between operations  16.1 us (1%)
    ppermute x66, waiting for transfers between devices, move(): return lax.ppermute(x, AXES, pairs)  409 us
    ppermute x8, waiting for transfers between devices, bring(): arrived = [lax.ppermute(x[m], AXES, routes(p, m)) for m in range(micro)]  147 us
    ppermute x8, waiting for transfers between devices, bring_back(): lax.ppermute(slots[p], AXES, [(d, o) for o, d in routes(p, m)])  134 us
    dot_general x11, matrix products, cross_tokens(): lax.dot_general(former, latter, (((0,), (0,)), ((), ())), preferred_eleme...  106 us
    pallas_call x6, Pallas kernels, fold_half(): pl.pallas_call(functools.partial(fold_kernel, len(values), arrived is not...  102 us
    ppermute x66, starting transfers between devices, move(): return lax.ppermute(x, AXES, pairs)  69.5 us
    ppermute x8, starting transfers between devices, bring_back(): lax.ppermute(slots[p], AXES, [(d, o) for o, d in routes(p, m)])  49.2 us
    unnamed x185, local copies, waits for them, and re-layouts  38.4 us
  transfers between devices with their start and end apart: 94, of which 33 were waited for; matrix products, arithmetic and copies ran while one was open for 19% of the time, Pallas kernels for 15%

profile of v3, /device:TPU:17, one launch (start us, length us, event | category | flops | bytes accessed | tf_op | source)
XLA Modules:
  0.0 1424.2 jit_solution(1442285546866439142)
XLA Ops:
  21.4 74.7 %collective-permute-done.3 = bf16[256,2048]{1,0:T(8,128)(2,1)S(1)} collective-permute-done((bf16[256,2048]{1,0:T(8,128)(2,1)S(1)}, bf16[256,2048]{1,0:T(8,128)(2,1)S(1)}, u32[]{:S(2)}, u32[]{:S(2)}) %collective-permute-start.3) | collective-permute-done | bytes 1048608 | tf_op jit(solution)/shard_map/ppermute | solution.py:553
  106.8 40.9 %collective-permute-done.4 = bf16[512,2048]{1,0:T(8,128)(2,1)} collective-permute-done((bf16[512,2048]{1,0:T(8,128)(2,1)}, bf16[512,2048]{1,0:T(8,128)(2,1)}, u32[]{:S(2)}, u32[]{:S(2)}) %collective-permute-start.4) | collective-permute-done | bytes 2097184 | tf_op jit(solution)/shard_map/ppermute | solution.py:503
  172.0 11.3 collective-permute-start.13
  186.3 47.1 %collective-permute-done.11 = bf16[256,2048]{1,0:T(8,128)(2,1)} collective-permute-done((bf16[256,2048]{1,0:T(8,128)(2,1)}, bf16[256,2048]{1,0:T(8,128)(2,1)}, u32[]{:S(2)}, u32[]{:S(2)}) %collective-permute-start.11) | collective-permute-done | bytes 1048608 | tf_op jit(solution)/shard_map/ppermute | solution.py:553
  239.8 22.9 %collective-permute-done.8 = bf16[256,2048]{1,0:T(8,128)(2,1)} collective-permute-done((bf16[256,2048]{1,0:T(8,128)(2,1)}, bf16[256,2048]{1,0:T(8,128)(2,1)}, u32[]{:S(2)}, u32[]{:S(2)}) %collective-permute-start.8) | collective-permute-done | bytes 1048608 | tf_op jit(solution)/shard_map/ppermute | solution.py:553
  267.5 18.7 %enter.2 = (bf16[2048,2048]{1,0:T(8,128)(2,1)}, f32[2048,1024]{1,0:T(8,128)}, f32[2048,1]{1,0:T(8,128)S(1)}, bf16[2048,512]{1,0:T(8,128)(2,1)S(1)}) custom-call(s32[4]{0:T(128)S(1)} %pad_add_fusion.1.spots, bf16[1024,2048]{1,0:T(8,128)(2,1)S(1)} %copy-done.8, bf16[1024,2048]{1,0:T(8,128)(2,1)} %collective-permute-done.6.other_ref, ...), custom_call_target="tpu_custom_call" | custom-call | flops 8589934592 | bytes 31465472 | tf_op jit(solution)/shard_map/enter/pallas_call | solution.py:241
  290.2 14.7 %project.1.zv_ref = f32[2048,1024]{1,0:T(8,128)S(1)} custom-call(s32[4]{0:T(128)S(1)} %pad_add_fusion.1.spots, bf16[2048,2048]{1,0:T(8,128)(2,1)} %get-tuple-element.169.h_ref, bf16[1024,1024]{1,0:T(8,128)(2,1)} %all-gather.9.cloned.1.call-done.refs_0_.refs_4_.refs_5_, bf16[1024,1024]{1,0:T(8,128)(2,1)} %collective-permute-done.7.refs_1_.refs_5_.refs_6_), custom_call_target="tpu_custom_call" | custom-call | flops 8589934592 | bytes 20971520 | tf_op jit(solution)/shard_map/project/pallas_call | solution.py:272
  308.4 12.3 attend.1
  326.2 7.7 collective-permute-done.14
  349.1 40.4 %collective-permute-done.20 = f32[2048]{0:T(1024)S(1)} collective-permute-done((f32[2048]{0:T(1024)S(1)}, f32[2048]{0:T(1024)S(1)}, u32[]{:S(2)}, u32[]{:S(2)}) %collective-permute-start.20) | collective-permute-done | bytes 8224 | tf_op jit(solution)/shard_map/ppermute | solution.py:503
  414.4 10.1 fusion.65
  426.0 45.9 %collective-permute-done.22 = bf16[2048,512]{1,0:T(8,128)(2,1)S(1)} collective-permute-done((bf16[2048,512]{1,0:T(8,128)(2,1)S(1)}, bf16[2048,512]{1,0:T(8,128)(2,1)S(1)}, u32[]{:S(2)}, u32[]{:S(2)}) %collective-permute-start.22) | collective-permute-done | bytes 2097184 | tf_op jit(solution)/shard_map/ppermute | solution.py:503
  486.0 38.0 %gated_unit.1 = (bf16[2048,2048]{1,0:T(8,128)(2,1)}, bf16[2048,1408]{1,0:T(8,128)(2,1)}, bf16[2048,1408]{1,0:T(8,128)(2,1)}, bf16[2048,1408]{1,0:T(8,128)(2,1)}, f32[2048,1]{1,0:T(8,128)S(1)}) custom-call(s32[4]{0:T(128)S(1)} %pad_add_fusion.1.spots, bf16[2048,1024]{1,0:T(8,128)(2,1)} %maximum_select_fusion.4.own_ref, ...), custom_call_target="tpu_custom_call" | custom-call | flops 23622320128 | bytes 45621248 | tf_op jit(solution)/shard_map/gated_unit/pallas_call | solution.py:334
  524.0 11.7 fusion.13
  541.3 21.1 %gated_unit_back.1 = (bf16[2048,1408]{1,0:T(8,128)(2,1)S(1)}, bf16[2048,1408]{1,0:T(8,128)(2,1)}, f32[2048,1]{1,0:T(8,128)S(1)}) custom-call(s32[4]{0:T(128)S(1)} %pad_add_fusion.1.spots, bf16[2048,2048]{1,0:T(8,128)(2,1)} %get-tuple-element.119.dy_ref, bf16[2048,1408]{1,0:T(8,128)(2,1)} %get-tuple-element.131.one_ref, ...), custom_call_target="tpu_custom_call" | custom-call | flops 11811160064 | bytes 37232640 | tf_op jit(solution)/shard_map/gated_unit_back/pallas_call | solution.py:371
  565.9 21.4 %fold_half.6 = bf16[2048,1024]{1,0:T(8,128)(2,1)} custom-call(s32[4]{0:T(128)S(1)} %pad_add_fusion.1.spots, bf16[2048,1408]{1,0:T(8,128)(2,1)} %copy-done.44, bf16[2048,1408]{1,0:T(8,128)(2,1)} %get-tuple-element.142.refs_1_, bf16[1024,1408]{1,0:T(8,128)(2,1)S(1)} %copy-done.29, bf16[1024,1408]{1,0:T(8,128)(2,1)} %collective-permute-done.17.refs_1_.refs_3_.refs_4_, ...), custom_call_target="tpu_custom_call" | custom-call | flops 11811160064 | bytes 21495808 | tf_op jit(solution)/shard_map/fold_half/pallas_call | solution.py:432
  597.1 11.5 convolution_convert_fusion.3
  609.5 23.3 %fold_half.7 = (bf16[2048,512]{1,0:T(8,128)(2,1)}, f32[2048,512]{1,0:T(8,128)}) custom-call(s32[4]{0:T(128)S(1)} %pad_add_fusion.1.spots, bf16[2048,1408]{1,0:T(8,128)(2,1)} %copy-done.44, bf16[2048,1408]{1,0:T(8,128)(2,1)} %get-tuple-element.142.refs_1_, bf16[2048,1024]{1,0:T(8,128)(2,1)} %collective-permute-done.26.refs_2_, ...), custom_call_target="tpu_custom_call" | custom-call | flops 11811160064 | bytes 27787264 | tf_op jit(solution)/shard_map/fold_half/pallas_call | solution.py:432
  632.9 9.6 fusion.16
  644.1 11.5 convolution_convert_fusion.1
  655.6 16.7 %collective-permute-done.30 = bf16[1024,1408]{1,0:T(8,128)(2,1)} collective-permute-done((bf16[1024,1408]{1,0:T(8,128)(2,1)}, bf16[1024,1408]{1,0:T(8,128)(2,1)}, u32[]{:S(2)}, u32[]{:S(2)}) %collective-permute-start.30) | collective-permute-done | bytes 2883616 | tf_op jit(solution)/shard_map/ppermute | solution.py:503
  672.3 8.3 collective-permute-done.31
  700.0 11.9 fold_half.8
  712.5 10.5 convolution_convert_fusion.2
  723.0 8.0 convert_add_fusion
  731.0 29.6 %collective-permute-done.29 = bf16[1024,1408]{1,0:T(8,128)(2,1)S(1)} collective-permute-done((bf16[1024,1408]{1,0:T(8,128)(2,1)}, bf16[1024,1408]{1,0:T(8,128)(2,1)S(1)}, u32[]{:S(2)}, u32[]{:S(2)}) %collective-permute-start.29) | collective-permute-done | bytes 2883616 | tf_op jit(solution)/shard_map/ppermute | solution.py:503
  762.9 11.8 convolution_convert_fusion
  778.9 13.5 convolution_convert_fusion.5
  795.7 29.8 %collective-permute-done.35 = bf16[2048,512]{1,0:T(8,128)(2,1)} collective-permute-done((bf16[2048,512]{1,0:T(8,128)(2,1)}, bf16[2048,512]{1,0:T(8,128)(2,1)}, u32[]{:S(2)}, u32[]{:S(2)}) %collective-permute-start.35) | collective-permute-done | bytes 2097184 | tf_op jit(solution)/shard_map/ppermute | solution.py:503
  829.9 8.3 collective-permute-done.36
  843.3 12.4 fold_half.9
  867.3 21.3 %attend_back.1 = (bf16[2048,512]{1,0:T(8,128)(2,1)S(1)}, bf16[2048,512]{1,0:T(8,128)(2,1)S(1)}, bf16[2048,512]{1,0:T(8,128)(2,1)S(1)}) custom-call(f32[4]{0:T(128)S(1)} %dynamic_slice.127.rates, s32[2,2]{1,0:T(2,128)S(1)} %copy-done.27, f32[2048,1024]{1,0:T(8,128)} %get-tuple-element.110.zq_ref.zk_ref, f32[2048,1024]{1,0:T(8,128)} %get-tuple-element.110.zq_ref.zk_ref, ...), custom_call_target="tpu_custom_call" | custom-call | flops 10737418240 | bytes 20971520 | tf_op jit(solution)/shard_map/attend_back/pallas_call | solution.py:118
  906.1 16.0 %fold_half.10 = bf16[2048,1024]{1,0:T(8,128)(2,1)} custom-call(s32[4]{0:T(128)S(1)} %pad_add_fusion.1.spots, bf16[2048,1024]{1,0:T(8,128)(2,1)} %copy-done.50, bf16[2048,1024]{1,0:T(8,128)(2,1)} %pad_maximum_fusion.refs_1_, bf16[1024,1024]{1,0:T(8,128)(2,1)S(1)} %copy-done.38, bf16[1024,1024]{1,0:T(8,128)(2,1)S(1)} %copy-done.42, ...), custom_call_target="tpu_custom_call" | custom-call | flops 8589934592 | bytes 16777216 | tf_op jit(solution)/shard_map/fold_half/pallas_call | solution.py:432
  947.7 20.5 %collective-permute-done.79.refs_1_ = bf16[512,1408]{1,0:T(8,128)(2,1)} collective-permute-done((bf16[512,1408]{1,0:T(8,128)(2,1)S(1)}, bf16[512,1408]{1,0:T(8,128)(2,1)}, u32[]{:S(2)}, u32[]{:S(2)}) %collective-permute-start.79) | collective-permute-done | bytes 1441824 | tf_op jit(solution)/shard_map/ppermute | solution.py:503
  981.1 16.8 %fold_half.11 = (bf16[2048,512]{1,0:T(8,128)(2,1)S(1)}, f32[2048,512]{1,0:T(8,128)}) custom-call(s32[4]{0:T(128)S(1)} %pad_add_fusion.1.spots, bf16[2048,1024]{1,0:T(8,128)(2,1)} %copy-done.50, bf16[2048,1024]{1,0:T(8,128)(2,1)} %pad_maximum_fusion.refs_1_, bf16[2048,1024]{1,0:T(8,128)(2,1)} %collective-permute-done.43.refs_2_, ...), custom_call_target="tpu_custom_call" | custom-call | flops 8589934592 | bytes 23068672 | tf_op jit(solution)/shard_map/fold_half/pallas_call | solution.py:432
  998.5 8.3 fusion.31
  1013.1 7.8 place_quarters.9
  1020.9 23.5 %collective-permute-done.44 = bf16[2048,512]{1,0:T(8,128)(2,1)S(1)} collective-permute-done((bf16[2048,512]{1,0:T(8,128)(2,1)S(1)}, bf16[2048,512]{1,0:T(8,128)(2,1)S(1)}, u32[]{:S(2)}, u32[]{:S(2)}) %collective-permute-start.44) | collective-permute-done | bytes 2097184 | tf_op jit(solution)/shard_map/ppermute | solution.py:503
  1065.7 35.4 %collective-permute-done.59 = bf16[256,1024]{1,0:T(8,128)(2,1)} collective-permute-done((bf16[256,1024]{1,0:T(8,128)(2,1)}, bf16[256,1024]{1,0:T(8,128)(2,1)}, u32[]{:S(2)}, u32[]{:S(2)}) %collective-permute-start.59) | collective-permute-done | bytes 524320 | tf_op jit(solution)/shard_map/ppermute | solution.py:503
  1111.0 8.5 collective-permute-done.68
  1133.5 9.9 collective-permute-done.60.refs_1_
  1154.8 50.4 %collective-permute-done.76.refs_1_ = bf16[512,1408]{1,0:T(8,128)(2,1)S(1)} collective-permute-done((bf16[512,1408]{1,0:T(8,128)(2,1)S(1)}, bf16[512,1408]{1,0:T(8,128)(2,1)S(1)}, u32[]{:S(2)}, u32[]{:S(2)}) %collective-permute-start.76) | collective-permute-done | bytes 1441824 | tf_op jit(solution)/shard_map/ppermute | solution.py:503
  1205.2 8.8 collective-permute-start.51
  1227.3 23.4 %collective-permute-start.58 = (bf16[256,2048]{1,0:T(8,128)(2,1)S(1)}, bf16[256,2048]{1,0:T(8,128)(2,1)S(1)}, u32[]{:S(2)}, u32[]{:S(2)}) collective-permute-start(bf16[256,2048]{1,0:T(8,128)(2,1)S(1)} %get-tuple-element.200), channel_id=1, source_target_pairs={{2,1},{3,5},{6,9},{7,13},{10,3},{11,7},{14,11},{15,15},{18,17},{19... | collective-permute-start | bytes 3145736 | tf_op jit(solution)/shard_map/ppermute | solution.py:562
  1250.6 53.5 %collective-permute-done.51 = bf16[256,2048]{1,0:T(8,128)(2,1)} collective-permute-done((bf16[256,2048]{1,0:T(8,128)(2,1)}, bf16[256,2048]{1,0:T(8,128)(2,1)}, u32[]{:S(2)}, u32[]{:S(2)}) %collective-permute-start.51) | collective-permute-done | bytes 1048608 | tf_op jit(solution)/shard_map/ppermute | solution.py:562
  1304.9 7.0 collective-permute-start.57
  1315.5 38.8 %collective-permute-done.49 = bf16[256,2048]{1,0:T(8,128)(2,1)} collective-permute-done((bf16[256,2048]{1,0:T(8,128)(2,1)}, bf16[256,2048]{1,0:T(8,128)(2,1)}, u32[]{:S(2)}, u32[]{:S(2)}) %collective-permute-start.49) | collective-permute-done | bytes 1048608 | tf_op jit(solution)/shard_map/ppermute | solution.py:562
  1356.9 42.2 %collective-permute-done.55 = bf16[256,2048]{1,0:T(8,128)(2,1)S(1)} collective-permute-done((bf16[256,2048]{1,0:T(8,128)(2,1)S(1)}, bf16[256,2048]{1,0:T(8,128)(2,1)S(1)}, u32[]{:S(2)}, u32[]{:S(2)}) %collective-permute-start.55) | collective-permute-done | bytes 1048608 | tf_op jit(solution)/shard_map/ppermute | solution.py:562
  (468 shorter events, 360.3 us)
Async XLA Ops:
  7.2 93.5 %all-gather.7.cloned.1.call-start = ((), (), s32[]{:S(2)}) async-start(), calls=%async_computation.6 | async-start | bytes 2621440 | tf_op jit(solution)/shard_map/all_gather | solution.py:619
  9.5 144.3 %all-gather.9.cloned.1.call-start = ((), (), s32[]{:S(2)}) async-start(), calls=%async_computation.7 | async-start | bytes 2621440 | tf_op jit(solution)/shard_map/all_gather | solution.py:619
  11.7 274.5 %all-gather.11.cloned.1.call-start = ((), (), s32[]{:S(2)}) async-start(), calls=%async_computation.8 | async-start | bytes 1310720 | tf_op jit(solution)/shard_map/all_gather | solution.py:619
  12.0 84.1 %collective-permute-start.3 = (bf16[256,2048]{1,0:T(8,128)(2,1)S(1)}, bf16[256,2048]{1,0:T(8,128)(2,1)S(1)}, u32[]{:S(2)}, u32[]{:S(2)}) collective-permute-start(bf16[256,2048]{1,0:T(8,128)(2,1)S(1)} %get-tuple-element.220), channel_id=1, source_target_pairs={{1,2},{5,3},{9,6},{13,7},{3,10},{7,11},{11,14},{15,15},{17,18},{21... | collective-permute-start | bytes 3145736 | tf_op jit(solution)/shard_map/ppermute | solution.py:553
  13.3 82.8 %collective-permute-start.2 = (bf16[256,2048]{1,0:T(8,128)(2,1)S(1)}, bf16[256,2048]{1,0:T(8,128)(2,1)S(1)}, u32[]{:S(2)}, u32[]{:S(2)}) collective-permute-start(bf16[256,2048]{1,0:T(8,128)(2,1)S(1)} %get-tuple-element.221), channel_id=1, source_target_pairs={{1,0},{5,1},{9,4},{13,5},{3,8},{7,9},{11,12},{15,13},{17,16},{21,1... | collective-permute-start | bytes 3145736 | tf_op jit(solution)/shard_map/ppermute | solution.py:553
  14.0 82.4 %collective-permute-start.1 = (bf16[256,2048]{1,0:T(8,128)(2,1)S(1)}, bf16[256,2048]{1,0:T(8,128)(2,1)S(1)}, u32[]{:S(2)}, u32[]{:S(2)}) collective-permute-start(bf16[256,2048]{1,0:T(8,128)(2,1)S(1)} %get-tuple-element.220), channel_id=1, source_target_pairs={{0,2},{4,3},{8,6},{12,7},{2,10},{6,11},{10,14},{14,15},{16,18},{20... | collective-permute-start | bytes 3145736 | tf_op jit(solution)/shard_map/ppermute | solution.py:553
  20.0 78.7 %collective-permute-start = (bf16[256,2048]{1,0:T(8,128)(2,1)S(1)}, bf16[256,2048]{1,0:T(8,128)(2,1)S(1)}, u32[]{:S(2)}, u32[]{:S(2)}) collective-permute-start(bf16[256,2048]{1,0:T(8,128)(2,1)S(1)} %get-tuple-element.221), channel_id=1, source_target_pairs={{0,0},{4,1},{8,4},{12,5},{2,8},{6,9},{10,12},{14,13},{16,16},{20,1... | collective-permute-start | bytes 3145736 | tf_op jit(solution)/shard_map/ppermute | solution.py:553
  102.9 236.1 %all-gather.13.cloned.1.call-start = ((), (), s32[]{:S(2)}) async-start(), calls=%async_computation.9 | async-start | bytes 3604480 | tf_op jit(solution)/shard_map/all_gather | solution.py:619
  106.7 294.4 %all-gather.15.cloned.1.call-start = ((), (), s32[]{:S(2)}) async-start(), calls=%async_computation.10 | async-start | bytes 3604480 | tf_op jit(solution)/shard_map/all_gather | solution.py:619
  153.8 112.3 %collective-permute-start.6 = (bf16[1024,2048]{1,0:T(8,128)(2,1)}, bf16[1024,2048]{1,0:T(8,128)(2,1)}, u32[]{:S(2)}, u32[]{:S(2)}) collective-permute-start(bf16[1024,2048]{1,0:T(8,128)(2,1)} %maximum_select_fusion.1.own_ref), channel_id=1, source_target_pairs={{0,4},{1,5},{2,6},{3,7},{4,0},{5,1},{6,2},{7,3},{8,12},{9,13},{10,... | collective-permute-start | bytes 12582920 | tf_op jit(solution)/shard_map/ppermute | solution.py:503
  158.4 75.1 %collective-permute-start.11 = (bf16[256,2048]{1,0:T(8,128)(2,1)}, bf16[256,2048]{1,0:T(8,128)(2,1)}, u32[]{:S(2)}, u32[]{:S(2)}) collective-permute-start(bf16[256,2048]{1,0:T(8,128)(2,1)} %get-tuple-element.216), channel_id=1, source_target_pairs={{1,2},{5,3},{9,6},{13,7},{3,10},{7,11},{11,14},{15,15},{17,18},{21... | collective-permute-start | bytes 3145736 | tf_op jit(solution)/shard_map/ppermute | solution.py:553
  159.7 80.1 %collective-permute-start.9 = (bf16[256,2048]{1,0:T(8,128)(2,1)}, bf16[256,2048]{1,0:T(8,128)(2,1)S(1)}, u32[]{:S(2)}, u32[]{:S(2)}) collective-permute-start(bf16[256,2048]{1,0:T(8,128)(2,1)} %get-tuple-element.216), channel_id=1, source_target_pairs={{0,2},{4,3},{8,6},{12,7},{2,10},{6,11},{10,14},{14,15},{16,18},{20... | collective-permute-start | bytes 3145736 | tf_op jit(solution)/shard_map/ppermute | solution.py:553
  170.3 67.4 %collective-permute-start.10 = (bf16[256,2048]{1,0:T(8,128)(2,1)}, bf16[256,2048]{1,0:T(8,128)(2,1)}, u32[]{:S(2)}, u32[]{:S(2)}) collective-permute-start(bf16[256,2048]{1,0:T(8,128)(2,1)} %get-tuple-element.217), channel_id=1, source_target_pairs={{1,0},{5,1},{9,4},{13,5},{3,8},{7,9},{11,12},{15,13},{17,16},{21,1... | collective-permute-start | bytes 3145736 | tf_op jit(solution)/shard_map/ppermute | solution.py:553
  184.1 78.7 %collective-permute-start.8 = (bf16[256,2048]{1,0:T(8,128)(2,1)}, bf16[256,2048]{1,0:T(8,128)(2,1)}, u32[]{:S(2)}, u32[]{:S(2)}) collective-permute-start(bf16[256,2048]{1,0:T(8,128)(2,1)} %get-tuple-element.217), channel_id=1, source_target_pairs={{0,0},{4,1},{8,4},{12,5},{2,8},{6,9},{10,12},{14,13},{16,16},{20,1... | collective-permute-start | bytes 3145736 | tf_op jit(solution)/shard_map/ppermute | solution.py:553
  237.1 237.5 %all-gather.17.cloned.1.call-start = ((), (), s32[]{:S(2)}) async-start(), calls=%async_computation.11 | async-start | bytes 3604480 | tf_op jit(solution)/shard_map/all_gather | solution.py:619
  339.0 55.4 %collective-permute-start.18 = (bf16[1024,2048]{1,0:T(8,128)(2,1)}, bf16[1024,2048]{1,0:T(8,128)(2,1)S(1)}, u32[]{:S(2)}, u32[]{:S(2)}) collective-permute-start(bf16[1024,2048]{1,0:T(8,128)(2,1)} %maximum_select_fusion.2.own_ref), channel_id=1, source_target_pairs={{0,4},{1,5},{2,6},{3,7},{4,0},{5,1},{6,2},{7,3},{8,12},{9,13},{10,... | collective-permute-start | bytes 12582920 | tf_op jit(solution)/shard_map/ppermute | solution.py:503
  340.8 64.4 %collective-permute-start.17 = (bf16[1024,1408]{1,0:T(8,128)(2,1)}, bf16[1024,1408]{1,0:T(8,128)(2,1)}, u32[]{:S(2)}, u32[]{:S(2)}) collective-permute-start(bf16[1024,1408]{1,0:T(8,128)(2,1)} %all-gather.13.cloned.1.call-done.refs_0_.refs_2_.refs_3_), channel_id=1, source_target_pairs={{0,16},{1,17},{2,18},{3,19},{4,20},{5,21},{6,22},{7,23},{8,24},{9,... | collective-permute-start | bytes 8650760 | tf_op jit(solution)/shard_map/ppermute | solution.py:503
  408.5 429.8 %reduce-scatter.7.cloned.1.call-start = ((), (), s32[]{:S(2)}) async-start(), calls=%async_computation.12 | async-start | bytes 3604480 | tf_op jit(solution)/shard_map/reduce_scatter | solution.py:655
  411.7 64.5 %collective-permute-start.23 = (bf16[1024,1408]{1,0:T(8,128)(2,1)}, bf16[1024,1408]{1,0:T(8,128)(2,1)}, u32[]{:S(2)}, u32[]{:S(2)}) collective-permute-start(bf16[1024,1408]{1,0:T(8,128)(2,1)} %all-gather.15.cloned.1.call-done.refs_2_.refs_4_.refs_5_), channel_id=1, source_target_pairs={{0,16},{1,17},{2,18},{3,19},{4,20},{5,21},{6,22},{7,23},{8,24},{9,... | collective-permute-start | bytes 8650760 | tf_op jit(solution)/shard_map/ppermute | solution.py:503
  477.0 64.3 %collective-permute-start.25 = (bf16[1024,1408]{1,0:T(8,128)(2,1)}, bf16[1024,1408]{1,0:T(8,128)(2,1)S(1)}, u32[]{:S(2)}, u32[]{:S(2)}) collective-permute-start(bf16[1024,1408]{1,0:T(8,128)(2,1)} %all-gather.17.cloned.1.call-done.refs_0_.refs_1_.refs_2_), channel_id=1, source_target_pairs={{0,16},{1,17},{2,18},{3,19},{4,20},{5,21},{6,22},{7,23},{8,24},{9,... | collective-permute-start | bytes 8650760 | tf_op jit(solution)/shard_map/ppermute | solution.py:503
  608.6 63.7 %collective-permute-start.30 = (bf16[1024,1408]{1,0:T(8,128)(2,1)}, bf16[1024,1408]{1,0:T(8,128)(2,1)}, u32[]{:S(2)}, u32[]{:S(2)}) collective-permute-start(bf16[1024,1408]{1,0:T(8,128)(2,1)} %fusion.13), channel_id=1, source_target_pairs={{0,16},{1,17},{2,18},{3,19},{4,20},{5,21},{6,22},{7,23},{8,24},{9,... | collective-permute-start | bytes 8650760 | tf_op jit(solution)/shard_map/ppermute | solution.py:503
  684.7 218.2 %reduce-scatter.9.cloned.1.call-start = ((), (), s32[]{:S(2)}) async-start(), calls=%async_computation.13 | async-start | bytes 3604480 | tf_op jit(solution)/shard_map/reduce_scatter | solution.py:655
  696.2 64.3 %collective-permute-start.29 = (bf16[1024,1408]{1,0:T(8,128)(2,1)}, bf16[1024,1408]{1,0:T(8,128)(2,1)S(1)}, u32[]{:S(2)}, u32[]{:S(2)}) collective-permute-start(bf16[1024,1408]{1,0:T(8,128)(2,1)} %convolution_convert_fusion.3), channel_id=1, source_target_pairs={{0,16},{1,17},{2,18},{3,19},{4,20},{5,21},{6,22},{7,23},{8,24},{9,... | collective-permute-start | bytes 8650760 | tf_op jit(solution)/shard_map/ppermute | solution.py:503
  711.9 118.0 %collective-permute-start.37 = (bf16[2048,1024]{1,0:T(8,128)(2,1)}, bf16[2048,1024]{1,0:T(8,128)(2,1)}, u32[]{:S(2)}, u32[]{:S(2)}) collective-permute-start(bf16[2048,1024]{1,0:T(8,128)(2,1)} %fold_half.8), channel_id=1, source_target_pairs={{0,4},{1,5},{2,6},{3,7},{4,0},{5,1},{6,2},{7,3},{8,12},{9,13},{10,... | collective-permute-start | bytes 12582920 | tf_op jit(solution)/shard_map/ppermute | solution.py:503
  762.9 206.4 %reduce-scatter.11.cloned.1.call-start = ((), (), s32[]{:S(2)}) async-start(), calls=%async_computation.14 | async-start | bytes 3604480 | tf_op jit(solution)/shard_map/reduce_scatter | solution.py:655
  774.7 63.5 %collective-permute-start.36 = (bf16[1024,1408]{1,0:T(8,128)(2,1)}, bf16[1024,1408]{1,0:T(8,128)(2,1)}, u32[]{:S(2)}, u32[]{:S(2)}) collective-permute-start(bf16[1024,1408]{1,0:T(8,128)(2,1)} %convolution_convert_fusion.1), channel_id=1, source_target_pairs={{0,16},{1,17},{2,18},{3,19},{4,20},{5,21},{6,22},{7,23},{8,24},{9,... | collective-permute-start | bytes 8650760 | tf_op jit(solution)/shard_map/ppermute | solution.py:503
  838.2 62.6 %collective-permute-start.39 = (bf16[256,1408]{1,0:T(8,128)(2,1)}, bf16[256,1408]{1,0:T(8,128)(2,1)}, u32[]{:S(2)}, u32[]{:S(2)}) collective-permute-start(bf16[256,1408]{1,0:T(8,128)(2,1)} %reduce-scatter.7.cloned.1.call-done), channel_id=1, source_target_pairs={{0,16},{1,17},{2,18},{3,19},{4,20},{5,21},{6,22},{7,23},{8,24},{9,... | collective-permute-start | bytes 2162696 | tf_op jit(solution)/shard_map/ppermute | solution.py:503
  838.7 63.8 %collective-permute-start.38 = (bf16[1024,512]{1,0:T(8,128)(2,1)}, bf16[1024,512]{1,0:T(8,128)(2,1)}, u32[]{:S(2)}, u32[]{:S(2)}) collective-permute-start(bf16[1024,512]{1,0:T(8,128)(2,1)} %get-tuple-element.159), channel_id=1, source_target_pairs={{0,16},{1,17},{2,18},{3,19},{4,20},{5,21},{6,22},{7,23},{8,24},{9,... | collective-permute-start | bytes 3145736 | tf_op jit(solution)/shard_map/ppermute | solution.py:503
  861.8 189.2 %reduce-scatter.13.cloned.1.call-start = ((), (), s32[]{:S(2)}) async-start(), calls=%async_computation.15 | async-start | bytes 1310720 | tf_op jit(solution)/shard_map/reduce_scatter | solution.py:655
  922.1 55.8 %collective-permute-start.43 = (bf16[2048,1024]{1,0:T(8,128)(2,1)}, bf16[2048,1024]{1,0:T(8,128)(2,1)}, u32[]{:S(2)}, u32[]{:S(2)}) collective-permute-start(bf16[2048,1024]{1,0:T(8,128)(2,1)} %fold_half.10), channel_id=1, source_target_pairs={{0,4},{1,5},{2,6},{3,7},{4,0},{5,1},{6,2},{7,3},{8,12},{9,13},{10,... | collective-permute-start | bytes 12582920 | tf_op jit(solution)/shard_map/ppermute | solution.py:503
  929.0 130.0 %reduce-scatter.15.cloned.1.call-start = ((), (), s32[]{:S(2)}) async-start(), calls=%async_computation.16 | async-start | bytes 2621440 | tf_op jit(solution)/shard_map/reduce_scatter | solution.py:655
  934.7 78.4 %collective-permute-start.80 = (bf16[512,1408]{1,0:T(8,128)(2,1)S(1)}, bf16[512,1408]{1,0:T(8,128)(2,1)S(1)}, u32[]{:S(2)}, u32[]{:S(2)}) collective-permute-start(bf16[512,1408]{1,0:T(8,128)(2,1)S(1)} %maximum_select_fusion.11.refs_0_), channel_id=1, source_target_pairs={{0,4},{1,5},{2,6},{3,7},{4,0},{5,1},{6,2},{7,3},{8,12},{9,13},{10,... | collective-permute-start | bytes 4325384 | tf_op jit(solution)/shard_map/ppermute | solution.py:503
  947.3 60.0 %collective-permute-start.46 = (f32[2048]{0:T(1024)S(1)}, f32[2048]{0:T(1024)S(1)}, u32[]{:S(2)}, u32[]{:S(2)}) collective-permute-start(f32[2048]{0:T(1024)S(1)} %add.328), channel_id=1, source_target_pairs={{0,8},{1,9},{2,10},{3,11},{4,12},{5,13},{6,14},{7,15},{8,0},{9,1},... | collective-permute-start | bytes 24584 | tf_op jit(solution)/shard_map/ppermute | solution.py:503
  977.8 242.5 %reduce-scatter.17.cloned.1.call-start = ((), (), s32[]{:S(2)}) async-start(), calls=%async_computation.17 | async-start | bytes 2621440 | tf_op jit(solution)/shard_map/reduce_scatter | solution.py:655
  1054.6 54.3 %collective-permute-start.75 = (bf16[256,1408]{1,0:T(8,128)(2,1)}, bf16[256,1408]{1,0:T(8,128)(2,1)}, u32[]{:S(2)}, u32[]{:S(2)}) collective-permute-start(bf16[256,1408]{1,0:T(8,128)(2,1)} %reduce-scatter.11.cloned.1.call-done), channel_id=1, source_target_pairs={{0,16},{1,17},{2,18},{3,19},{4,20},{5,21},{6,22},{7,23},{8,24},{9,... | collective-permute-start | bytes 2162696 | tf_op jit(solution)/shard_map/ppermute | solution.py:503
  1058.2 62.7 %collective-permute-start.53 = (bf16[2,512,512]{2,1,0:T(8,128)(2,1)}, bf16[2,512,512]{2,1,0:T(8,128)(2,1)}, u32[]{:S(2)}, u32[]{:S(2)}) collective-permute-start(bf16[2,512,512]{2,1,0:T(8,128)(2,1)} %get-tuple-element.205), channel_id=1, source_target_pairs={{0,8},{1,9},{2,10},{3,11},{4,12},{5,13},{6,14},{7,15},{8,0},{9,1},... | collective-permute-start | bytes 3145736 | tf_op jit(solution)/shard_map/ppermute | solution.py:503
  1064.8 59.7 %collective-permute-start.47 = (bf16[2,512,512]{2,1,0:T(8,128)(2,1)S(1)}, bf16[2,512,512]{2,1,0:T(8,128)(2,1)S(1)}, u32[]{:S(2)}, u32[]{:S(2)}) collective-permute-start(bf16[2,512,512]{2,1,0:T(8,128)(2,1)S(1)} %get-tuple-element.211), channel_id=1, source_target_pairs={{0,8},{1,9},{2,10},{3,11},{4,12},{5,13},{6,14},{7,15},{8,0},{9,1},... | collective-permute-start | bytes 3145736 | tf_op jit(solution)/shard_map/ppermute | solution.py:503
  1124.5 89.6 %collective-permute-start.73 = (bf16[512,1408]{1,0:T(8,128)(2,1)S(1)}, bf16[512,1408]{1,0:T(8,128)(2,1)S(1)}, u32[]{:S(2)}, u32[]{:S(2)}) collective-permute-start(bf16[512,1408]{1,0:T(8,128)(2,1)S(1)} %maximum_select_fusion.12.refs_0_), channel_id=1, source_target_pairs={{0,4},{1,5},{2,6},{3,7},{4,0},{5,1},{6,2},{7,3},{8,12},{9,13},{10,... | collective-permute-start | bytes 4325384 | tf_op jit(solution)/shard_map/ppermute | solution.py:503
  1125.5 91.4 %collective-permute-start.72 = (bf16[512,1408]{1,0:T(8,128)(2,1)S(1)}, bf16[512,1408]{1,0:T(8,128)(2,1)S(1)}, u32[]{:S(2)}, u32[]{:S(2)}) collective-permute-start(bf16[512,1408]{1,0:T(8,128)(2,1)S(1)} %maximum_select_fusion.12.refs_0_), channel_id=1, source_target_pairs={{0,8},{1,9},{2,10},{3,11},{4,12},{5,13},{6,14},{7,15},{8,0},{9,1},... | collective-permute-start | bytes 4325384 | tf_op jit(solution)/shard_map/ppermute | solution.py:503
  1143.4 61.8 %collective-permute-start.76 = (bf16[512,1408]{1,0:T(8,128)(2,1)S(1)}, bf16[512,1408]{1,0:T(8,128)(2,1)S(1)}, u32[]{:S(2)}, u32[]{:S(2)}) collective-permute-start(bf16[512,1408]{1,0:T(8,128)(2,1)S(1)} %maximum_select_fusion.13.refs_0_), channel_id=1, source_target_pairs={{0,8},{1,9},{2,10},{3,11},{4,12},{5,13},{6,14},{7,15},{8,0},{9,1},... | collective-permute-start | bytes 4325384 | tf_op jit(solution)/shard_map/ppermute | solution.py:503
  1144.5 74.9 %collective-permute-start.62 = (bf16[512,1024]{1,0:T(8,128)(2,1)S(1)}, bf16[512,1024]{1,0:T(8,128)(2,1)S(1)}, u32[]{:S(2)}, u32[]{:S(2)}) collective-permute-start(bf16[512,1024]{1,0:T(8,128)(2,1)S(1)} %collective-permute-done.60.refs_1_), channel_id=1, source_target_pairs={{0,4},{1,5},{2,6},{3,7},{4,0},{5,1},{6,2},{7,3},{8,12},{9,13},{10,... | collective-permute-start | bytes 3145736 | tf_op jit(solution)/shard_map/ppermute | solution.py:503
  1149.8 77.4 %collective-permute-start.52 = (bf16[256,2048]{1,0:T(8,128)(2,1)}, bf16[256,2048]{1,0:T(8,128)(2,1)}, u32[]{:S(2)}, u32[]{:S(2)}) collective-permute-start(bf16[256,2048]{1,0:T(8,128)(2,1)} %get-tuple-element.206), channel_id=1, source_target_pairs={{2,1},{3,5},{6,9},{7,13},{10,3},{11,7},{14,11},{15,15},{18,17},{19... | collective-permute-start | bytes 3145736 | tf_op jit(solution)/shard_map/ppermute | solution.py:562
  1205.2 98.9 %collective-permute-start.51 = (bf16[256,2048]{1,0:T(8,128)(2,1)}, bf16[256,2048]{1,0:T(8,128)(2,1)}, u32[]{:S(2)}, u32[]{:S(2)}) collective-permute-start(bf16[256,2048]{1,0:T(8,128)(2,1)} %get-tuple-element.207), channel_id=1, source_target_pairs={{2,0},{3,4},{6,8},{7,12},{10,2},{11,6},{14,10},{15,14},{18,16},{19... | collective-permute-start | bytes 3145736 | tf_op jit(solution)/shard_map/ppermute | solution.py:562
  1215.3 98.8 %collective-permute-start.50 = (bf16[256,2048]{1,0:T(8,128)(2,1)}, bf16[256,2048]{1,0:T(8,128)(2,1)}, u32[]{:S(2)}, u32[]{:S(2)}) collective-permute-start(bf16[256,2048]{1,0:T(8,128)(2,1)} %get-tuple-element.206), channel_id=1, source_target_pairs={{0,1},{1,5},{4,9},{5,13},{8,3},{9,7},{12,11},{13,15},{16,17},{17,2... | collective-permute-start | bytes 3145736 | tf_op jit(solution)/shard_map/ppermute | solution.py:562
  1218.0 136.3 %collective-permute-start.49 = (bf16[256,2048]{1,0:T(8,128)(2,1)}, bf16[256,2048]{1,0:T(8,128)(2,1)}, u32[]{:S(2)}, u32[]{:S(2)}) collective-permute-start(bf16[256,2048]{1,0:T(8,128)(2,1)} %get-tuple-element.207), channel_id=1, source_target_pairs={{0,0},{1,4},{4,8},{5,12},{8,2},{9,6},{12,10},{13,14},{16,16},{17,2... | collective-permute-start | bytes 3145736 | tf_op jit(solution)/shard_map/ppermute | solution.py:562
  1220.3 84.5 %collective-permute-start.63 = (bf16[256,1024]{1,0:T(8,128)(2,1)}, bf16[256,1024]{1,0:T(8,128)(2,1)S(1)}, u32[]{:S(2)}, u32[]{:S(2)}) collective-permute-start(bf16[256,1024]{1,0:T(8,128)(2,1)} %reduce-scatter.17.cloned.1.call-done), channel_id=1, source_target_pairs={{0,16},{1,17},{2,18},{3,19},{4,20},{5,21},{6,22},{7,23},{8,24},{9,... | collective-permute-start | bytes 1572872 | tf_op jit(solution)/shard_map/ppermute | solution.py:503
  1227.3 128.8 %collective-permute-start.58 = (bf16[256,2048]{1,0:T(8,128)(2,1)S(1)}, bf16[256,2048]{1,0:T(8,128)(2,1)S(1)}, u32[]{:S(2)}, u32[]{:S(2)}) collective-permute-start(bf16[256,2048]{1,0:T(8,128)(2,1)S(1)} %get-tuple-element.200), channel_id=1, source_target_pairs={{2,1},{3,5},{6,9},{7,13},{10,3},{11,7},{14,11},{15,15},{18,17},{19... | collective-permute-start | bytes 3145736 | tf_op jit(solution)/shard_map/ppermute | solution.py:562
  1314.1 85.0 %collective-permute-start.55 = (bf16[256,2048]{1,0:T(8,128)(2,1)S(1)}, bf16[256,2048]{1,0:T(8,128)(2,1)S(1)}, u32[]{:S(2)}, u32[]{:S(2)}) collective-permute-start(bf16[256,2048]{1,0:T(8,128)(2,1)S(1)} %get-tuple-element.201), channel_id=1, source_target_pairs={{0,0},{1,4},{4,8},{5,12},{8,2},{9,6},{12,10},{13,14},{16,16},{17,2... | collective-permute-start | bytes 3145736 | tf_op jit(solution)/shard_map/ppermute | solution.py:562
  (127 other events, 3033.4 us)
Sparse Core Ops, SparseCore 0:
  10.2 82.5 all-gather.6
  94.9 46.1 all-gather.8
  143.3 30.8 all-gather.10
  176.2 94.3 all-gather.12
  272.6 59.5 all-gather.14
  408.6 58.6 all-gather.16
  684.9 54.9 reduce-scatter.6
  763.0 55.4 reduce-scatter.8
  861.9 59.2 reduce-scatter.10
  929.1 27.1 reduce-scatter.12
  978.0 44.3 reduce-scatter.14
  1064.7 47.5 reduce-scatter.16

commit v4 on v3

--- a/solution.py
+++ b/solution.py
@@ -5,7 +5,7 @@
 from jax import lax
 from jax.experimental import pallas as pl
 from jax.experimental.pallas import tpu as pltpu
-from jax.sharding import PartitionSpec as P
+from jax.sharding import Mesh, PartitionSpec as P
 
 HEADS = 16
 HEAD_DIM = 128
@@ -14,7 +14,8 @@
 BLOCK = 256
 TILE = 256
 EPSILON = 1e-06
-AXES = ("rep", "shard")
+AXES = ("a", "b", "c", "shard")
+OWNERS = ("a", "shard")
 LOW = jnp.bfloat16
 F32 = jnp.float32
 
@@ -136,6 +137,10 @@
 
 def chunk_copies(chunks, buffer, sems, turn, half=None):
     count, size = len(chunks), chunks[0].shape[0]
+    if count == 1:
+        rows = buffer.shape[0]
+        first = 0 if half is None else pl.multiple_of(half * rows, rows)
+        return [(None, pltpu.make_async_copy(chunks[0].at[pl.ds(first, rows)], buffer, sems.at[0]))]
     copies = []
     for k, chunk in enumerate(chunks):
         index = lax.rem(turn - k + count, count)
@@ -448,6 +453,41 @@
     return found[0] if arrived is None else found
 
 
+def gradient_kernel(spots, left_ref, right_ref, *refs):
+    found = cross_tokens(left_ref[...], right_ref[...])
+    for arrived_ref in refs[:-1]:
+        found = found + arrived_ref[...].astype(F32)
+    refs[-1][...] = found.astype(LOW)
+
+
+def gradient_rows(spots, spread, k, left, right, arrived=()):
+    count, columns = right.shape
+    rows = left.shape[1] // (1 if k is None else spread)
+    tiles = rows // TILE
+
+    def block(i, s):
+        return (0, i if k is None else lax.rem(s[2] + k, spread) * tiles + i)
+
+    out = jax.ShapeDtypeStruct((rows, columns), LOW)
+    return pl.pallas_call(
+        gradient_kernel,
+        out_shape=out,
+        grid_spec=pltpu.PrefetchScalarGridSpec(
+            num_scalar_prefetch=1,
+            grid=(tiles,),
+            in_specs=[
+                pl.BlockSpec((count, TILE), block),
+                pl.BlockSpec((count, columns), lambda i, s: (0, 0), pipeline_mode=pl.Buffered(1)),
+            ]
+            + [tile_rows(columns)] * len(arrived),
+            out_specs=tile_rows(columns),
+        ),
+        compiler_params=limit(40),
+        cost_estimate=estimate(2 * count * rows * columns, right, out, out, *arrived),
+        name="gradient_rows",
+    )(spots, left, right, *arrived)
+
+
 def place_kernel(count, spots, *refs):
     quarter = pl.program_id(0)
     cross = lax.rem(lax.div(quarter, 2) + spots[0], 2) * 2 + lax.rem(lax.rem(quarter, 2) + spots[3], 2)
@@ -461,22 +501,26 @@
 
 
 def place_quarters(spots, four, count):
-    rows, columns = four[0].shape
+    rows, columns = four[0][0].shape[0], four[0][2]
     size = columns // count
     outs = [jax.ShapeDtypeStruct((rows, GROUP * size), F32)] * count
+
+    def block(index):
+        return pl.BlockSpec((rows, columns), lambda q, s: (0, index))
+
     return pl.pallas_call(
         functools.partial(place_kernel, count),
         out_shape=outs,
         grid_spec=pltpu.PrefetchScalarGridSpec(
             num_scalar_prefetch=1,
             grid=(GROUP,),
-            in_specs=[pl.BlockSpec((rows, columns), lambda q, s: (0, 0))] * 4,
+            in_specs=[block(index) for _, index, _ in four],
             out_specs=[pl.BlockSpec((rows, size), lambda q, s: (0, q))] * count,
         ),
         compiler_params=limit(40),
-        cost_estimate=estimate(0, *four, *outs),
+        cost_estimate=estimate(0, *[x for x, _, _ in four], *outs),
         name="place_quarters",
-    )(spots, *four)
+    )(spots, *[x for x, _, _ in four])
 
 
 def tie(*values):
@@ -485,8 +529,8 @@
 
 def body(reps, shards, tokens, cotangent, lengths, decay_rates, *weights):
     spread = reps // GROUP
-    rep, place = lax.axis_index("rep"), lax.axis_index("shard")
-    c, b, a = rep % 2, (rep // 2) % 2, rep // GROUP
+    place = lax.axis_index("shard")
+    a, b, c = lax.axis_index("a"), lax.axis_index("b"), lax.axis_index("c")
     quarter = 2 * c + b
     micro, run, width = tokens.shape
     half, own = width // 2, width // GROUP
@@ -583,13 +627,6 @@
         sent = swap_c(product(1 - c).astype(LOW))
         return product(c) + sent.astype(F32)
 
-    def fold_sent(values, members):
-        return swap_c(fold_half(spots, values, members))
-
-    def fold_kept(values, members, arrived):
-        sent, mine = fold_half(spots, values, members, arrived)
-        return mine, swap_b(sent)
-
     def fold_b(x):
         sent = swap_b(columns(x, (1 - b) * own, own).astype(LOW))
         return columns(x, b * own, own) + sent.astype(F32)
@@ -598,8 +635,7 @@
         cut = x.reshape(2, 2, -1, own)
         pick = functools.partial(lax.dynamic_index_in_dim, keepdims=False)
         both = ordered(b, pick(cut, b, 1), swap_b(pick(cut, 1 - b, 1)), 2)
-        four = ordered(c, pick(both, c, 0), swap_c(pick(both, 1 - c, 0)), 1)
-        return bring_back(four)
+        return ordered(c, pick(both, c, 0), swap_c(pick(both, 1 - c, 0)), 1)
 
 
     def own_features(w):
@@ -618,6 +654,10 @@
         piece = lax.dynamic_slice_in_dim(cut, a * part, part, 0)
         return lax.all_gather(piece, "shard", axis=0, tiled=True)
 
+    def over_owners(w):
+        piece = lax.dynamic_slice_in_dim(w, a * part, part, 0)
+        return lax.all_gather(piece, OWNERS, axis=0, tiled=True)
+
     def over_spread(x):
         return [shift_a(x, k) for k in range(1, spread)]
 
@@ -636,35 +676,37 @@
         return lax.dynamic_slice_in_dim(w, h * half, half, 0)
 
 
-    def owned_by(x, k):
-        return columns(x, ((a + k) % spread) * (width // spread), width // spread)
-
     def away(left, right):
-        return [cross_tokens(owned_by(left, k), right).astype(LOW) for k in range(1, spread)]
-
-    def kept(left, right):
-        return cross_tokens(owned_by(left, 0), right).astype(LOW)
+        return [gradient_rows(spots, spread, k, left, right) for k in range(1, spread)]
 
     def sent_a(terms):
         return [shift_a(x, k + 1) for k, x in enumerate(terms)]
 
-    def summed(mine, arrived):
-        whole = mine.astype(F32)
-        for x in arrived:
-            whole = whole + x.astype(F32)
-        return lax.psum_scatter(whole.astype(LOW), "shard", scatter_dimension=0, tiled=True)
+    def scattered(x):
+        return lax.psum_scatter(x, "shard", scatter_dimension=0, tiled=True)
+
+    def whole_rows(left, right):
+        return gradient_rows(spots, spread, None, left, right)
+
+    def scattered_all(x):
+        return lax.psum_scatter(x, OWNERS, scatter_dimension=0, tiled=True)
+
+    def summed(left, right, arrived):
+        return scattered(gradient_rows(spots, spread, 0, left, right, arrived))
 
     def spread_a(x):
         return by_spread([x] + over_spread(x))
 
     def spread_b(x):
-        return (x, swap_b(x))
-
-    def spread_c(two):
-        return [*two, swap_c(two[0]), swap_c(two[1])]
+        return jnp.concatenate([x, swap_b(x)], axis=1)
+
+    def spread_c(pair):
+        other, size = swap_c(pair), pair.shape[1] // 2
+        return [(pair, 0, size), (pair, 1, size), (other, 0, size), (other, 1, size)]
 
     def features_in_order(four):
-        pair = [ordered(b, four[n], four[n + 1], 1) for n in (0, 2)]
+        cut = [x[:, index * size : (index + 1) * size] for x, index, size in four]
+        pair = [ordered(b, cut[n], cut[n + 1], 1) for n in (0, 2)]
         return natural(ordered(c, pair[0], pair[1], 1)).astype(F32)
 
 
@@ -674,7 +716,7 @@
     g_o = over_shards(own_features(w_out))
     g_1 = over_shards(own_units(w_one))
     g_2 = over_shards(own_units(w_two))
-    g_d = over_shards(own_units(w_down))
+    w_d = [over_owners(own_units(w_down))]
 
     heads = HEADS // GROUP
     rates = lax.dynamic_slice_in_dim(decay_rates, quarter * heads, heads, 0)
@@ -701,144 +743,180 @@
     x_pair, s_qk, g_vg = tie(x_pair, s_qk, g_vg)
 
     s_vg = over_spread(g_vg)
-    dy_run = bring(cotangent)
     w_qk = [g_qk, *s_qk]
     hidden_one, z_qk, x_scale, x_own = enter(spots, blocks, x_pair, swap_c(x_pair), w_qk)
-    z_qk, hidden_one, s_vg, g_o, dy_run = tie(z_qk, hidden_one, s_vg, g_o, dy_run)
+    z_qk, hidden_one, s_vg, g_o, cotangent = tie(z_qk, hidden_one, s_vg, g_o, cotangent)
 
     s_o = over_spread(g_o)
-    dy_pair = gather_rows_b(dy_run)
+    dy_run = bring(cotangent)
     w_vg = [g_vg, *s_vg]
     z_vg = project(spots, hidden_one, w_vg)
     attended = attend(rates, ends, z_qk, z_vg)
     gate = z_vg[:, own:]
     o_scale = lax.rsqrt(total(jnp.sum(attended * attended, axis=-1)) / width + EPSILON)[:, None]
     lifted = (attended * gate).astype(LOW)
-    lifted, dy_pair, s_o, g_1 = tie(lifted, dy_pair, s_o, g_1)
+    lifted, s_o, g_1 = tie(lifted, s_o, g_1)
 
     s_1 = over_spread(g_1)
-    lifted = gather_b(lifted)
-    dy_all, dy_own = enter(spots, blocks, dy_pair, swap_c(dy_pair))
+    lifted = gather_c(gather_b(lifted))
     w_o = in_row_order(by_spread([g_o, *s_o]))
-    lifted, s_1, g_2, dy_all, o_scale = tie(lifted, s_1, g_2, dy_all, o_scale)
-
-    s_2 = over_spread(g_2)
-    lifted = gather_c(lifted)
     branch = o_scale * matmul(lifted, w_o)
     middle = x_own.astype(F32) + branch
-    low_middle = gather_b(middle.astype(LOW))
-    low_middle, s_2, g_d = tie(low_middle, s_2, g_d)
-
-    s_d = over_spread(g_d)
+    low_middle = middle.astype(LOW)
+    low_middle, s_1, g_2 = tie(low_middle, s_1, g_2)
+
+    s_2 = over_spread(g_2)
+    low_middle = gather_b(low_middle)
+    low_middle, dy_run = tie(low_middle, dy_run)
+
+    other_middle = swap_c(low_middle)
+    dy_pair = gather_rows_b(dy_run)
+    other_middle, dy_pair, s_2 = tie(other_middle, dy_pair, s_2)
+
+    dy_all, dy_own = enter(spots, blocks, dy_pair, swap_c(dy_pair))
     w_1, w_2 = [g_1, *s_1], [g_2, *s_2]
-    hidden_two, z_one, z_two, product, m_scale = gated_unit(
-        spots, low_middle, swap_c(low_middle), w_1, w_2
-    )
-    t_down = away(dy_all, product)
-    z_one, z_two, product, t_down, s_d = tie(z_one, z_two, product, t_down, s_d)
-
-    r_down = sent_a(t_down)
-    w_d = [g_d, *s_d]
+    hidden_two, z_one, z_two, product, m_scale = gated_unit(spots, low_middle, other_middle, w_1, w_2)
+    f_down = scattered_all(whole_rows(dy_all, product))
+    z_one, z_two, product, w_d[0] = tie(z_one, z_two, product, w_d[0])
+
+
     d_one, d_two, lean_m = gated_unit_back(spots, dy_all, z_one, z_two, w_d)
-    arrived = fold_sent([d_one, d_two], [w_1, w_2])
-    t_one = away(hidden_two, d_one)
+    sent = fold_half(spots, [d_one, d_two], [w_1, w_2])
+    sent, d_two, lean_m = tie(sent, d_two, lean_m)
+
+    arrived = swap_c(sent)
+    t_two = away(hidden_two, d_two)
     lean_m = total(lean_m[:, 0])
-    d_one, d_two, t_one, arrived, lean_m = tie(d_one, d_two, t_one, arrived, lean_m)
-
-    mine, crossed = fold_kept([d_one, d_two], [w_1, w_2], arrived)
-    k_down = kept(dy_all, product)
-    r_one = sent_a(t_one)
-    t_two = away(hidden_two, d_two)
-    k_one = kept(hidden_two, d_one)
-    r_down, k_down, crossed, t_two = tie(r_down, k_down, crossed, t_two)
-
-    f_down = summed(k_down, r_down)
+    sent, mine = fold_half(spots, [d_one, d_two], [w_1, w_2], arrived)
+    sent, d_one, t_two, product = tie(sent, d_one, t_two, product)
+
+    crossed = swap_b(sent)
+    cut = [(x[: x.shape[0] // 2], x[x.shape[0] // 2 :]) for x in t_two]
+    upper = sent_a([x for x, _ in cut])
+    f_one = whole_rows(hidden_two, d_one)
+    result = fold_half(spots, [product], [w_d])
+    crossed, result, lean_m, f_one, upper = tie(crossed, result, lean_m, f_one, upper)
+
+    f_one = scattered_all(f_one)
     d_hidden = mine + crossed.astype(F32)
     m_normed = middle * m_scale
     lean = lean_m[:, None] * (2.0 / width)
     d_middle = dy_own.astype(F32) + m_scale * (d_hidden - m_normed * lean)
     d_branch = d_middle.astype(LOW)
-    lean_o = total(jnp.sum(d_middle * branch, axis=-1))
-    d_gated = fold_c(lambda h: times_transposed(d_branch, row_half(w_o, h)))
-    r_two = sent_a(t_two)
-    k_two = kept(hidden_two, d_two)
-    r_one, k_one, d_gated, lean_o = tie(r_one, k_one, d_gated, lean_o)
-
-    f_one = summed(k_one, r_one)
-    d_gated = fold_b(d_gated)
+    lean_o = jnp.sum(d_middle * branch, axis=-1)
+    sent = times_transposed(d_branch, row_half(w_o, 1 - c)).astype(LOW)
+    sent, result, d_middle, lean_o = tie(sent, result, d_middle, lean_o)
+
+    arrived = swap_c(sent)
+    r_result = swap_c(result)
+    lean_o = total(lean_o)
     p_out = cross_tokens(lifted, (o_scale * d_middle).astype(LOW)).astype(LOW)
     p_out = jnp.transpose(p_out.reshape(shards, spread, part, -1), (1, 0, 2, 3))
     p_out = p_out.reshape(spread, width // spread, -1)
     t_out = [lax.dynamic_index_in_dim(p_out, (a + k) % spread, 0, False) for k in range(spread)]
-    result = fold_sent([product], [w_d])
-    d_gated, r_two, k_two, t_out, f_down, result = tie(d_gated, r_two, k_two, t_out, f_down, result)
-
+    d_gated = times_transposed(d_branch, row_half(w_o, c)) + arrived.astype(F32)
+    sent = columns(d_gated, (1 - b) * own, own).astype(LOW)
+    mine = columns(d_gated, b * own, own)
+    lower = [x for _, x in cut]
+    sent, mine, lower, r_result, t_out = tie(sent, mine, lower, r_result, t_out)
+
+    crossed = swap_b(sent)
+    lower = sent_a(lower)
+    result, result_mine = fold_half(spots, [product], [w_d], r_result)
+    crossed, result, f_down, lean_o, lower, t_out = tie(crossed, result, f_down, lean_o, lower, t_out)
+
+    r_two = [jnp.concatenate(pair, axis=0) for pair in zip(upper, lower)]
+    f_two = summed(hidden_two, d_two, r_two)
     r_out = sent_a(t_out[1:])
-    f_two = summed(k_two, r_two)
+    result = swap_b(result)
     y_down = spread_a(f_down)
+    d_gated = mine + crossed.astype(F32)
     o_normed = attended * o_scale
     d_gate = (d_gated * o_normed).astype(LOW)
     lean = lean_o[:, None] / width
     d_attended = (o_scale * (d_gated * gate - o_normed * lean)).astype(LOW)
-    result, result_b = fold_kept([product], [w_d], result)
     d_query, d_key, d_value = attend_back(rates, ends, z_qk, z_vg, d_attended)
     d_qk = jnp.concatenate([d_query, d_key], axis=1)
     d_vg = jnp.concatenate([d_value, d_gate], axis=1)
     t_qk = away(hidden_one, d_qk)
-    d_qk, d_vg, t_qk, r_out, f_one, y_down, result_b = tie(
-        d_qk, d_vg, t_qk, r_out, f_one, y_down, result_b
-    )
+    d_qk, d_vg, t_qk, r_out, y_down = tie(d_qk, d_vg, t_qk, r_out, y_down)
 
     r_qk = sent_a(t_qk)
-    f_out = summed(t_out[0], r_out)
+    f_out = scattered(sum([x.astype(F32) for x in r_out], t_out[0].astype(F32)).astype(LOW))
     t_vg = away(hidden_one, d_vg)
+    sent = fold_half(spots, [d_qk, d_vg], [w_qk, w_vg])
+    sent, t_vg, result, d_qk, d_vg = tie(sent, t_vg, result, d_qk, d_vg)
+
     r_vg = sent_a(t_vg)
-    arrived = fold_sent([d_qk, d_vg], [w_qk, w_vg])
+    arrived = swap_c(sent)
+    x_down = spread_b(y_down)
     lean_x = total(
         jnp.sum(z_qk * d_qk.astype(F32), axis=-1) + jnp.sum(z_vg * d_vg.astype(F32), axis=-1)
     )
-    k_qk = kept(hidden_one, d_qk)
-    mine, crossed = fold_kept([d_qk, d_vg], [w_qk, w_vg], arrived)
-    k_qk, r_qk, k_vg_in, f_two = tie(k_qk, r_qk, hidden_one, f_two)
-
-    f_qk = summed(k_qk, r_qk)
-    k_vg = kept(k_vg_in, d_vg)
-    output = (middle + (result + result_b.astype(F32))).astype(LOW)
+    sent, mine = fold_half(spots, [d_qk, d_vg], [w_qk, w_vg], arrived)
+    output = (middle + (result_mine + result.astype(F32))).astype(LOW)
+    sent, mine, r_qk, d_qk, d_vg, f_one, x_down, output = tie(
+        sent, mine, r_qk, d_qk, d_vg, f_one, x_down, output
+    )
+
+    crossed = swap_b(sent)
+    f_qk = summed(hidden_one, d_qk, r_qk)
+    x_one = spread_b(f_one)
+    output = to_runs(output)
+    crossed, d_vg, r_vg, x_one, f_two, lean_x, output = tie(
+        crossed, d_vg, r_vg, x_one, f_two, lean_x, output
+    )
+
+    vg_rows = gradient_rows(spots, spread, 0, hidden_one, d_vg, r_vg)
+    vg_rows, crossed, x_one, f_two, f_out, output = tie(
+        vg_rows, crossed, x_one, f_two, f_out, output
+    )
+
+    f_vg = scattered(vg_rows)
     d_hidden = mine + crossed.astype(F32)
     x_normed = x_own.astype(F32) * x_scale
     lean = lean_x[:, None] / width
     input_grad = (d_middle + x_scale * (d_hidden - x_normed * lean)).astype(LOW)
-    k_vg, r_vg, f_one, f_two, f_out, output, input_grad = tie(
-        k_vg, r_vg, f_one, f_two, f_out, output, input_grad
+    output = bring_back(output)
+    x_two = spread_b(f_two)
+    y_one = spread_a(x_one)
+    y_out = spread_a(f_out)
+    input_grad = to_runs(input_grad)
+    y_qk = spread_a(f_qk)
+    output, input_grad, x_two, y_one, y_out, y_qk, f_vg = tie(
+        output, input_grad, x_two, y_one, y_out, y_qk, f_vg
     )
 
-    f_vg = summed(k_vg, r_vg)
-    input_grad, output = to_runs(input_grad), to_runs(output)
-    g_down = spread_c(spread_b(y_down))
-    g_one = spread_c(spread_b(spread_a(f_one)))
-    g_two = spread_c(spread_b(spread_a(f_two)))
-    g_out = spread_c(spread_b(spread_a(f_out)))
-    g_qk = spread_c(spread_b(spread_a(f_qk)))
-    g_vg = spread_c(spread_b(spread_a(f_vg)))
+    y_vg = spread_a(f_vg)
+    x_qk = spread_b(y_qk)
+    y_vg, x_qk = tie(y_vg, x_qk)
+
+    x_vg = spread_b(y_vg)
+    input_grad = bring_back(input_grad)
+    y_two = spread_a(x_two)
+    x_out = spread_b(y_out)
     return (
         output,
         input_grad,
-        *place_quarters(spots, g_qk, 2),
-        *place_quarters(spots, g_vg, 2),
-        features_in_order(g_out),
-        *place_quarters(spots, g_one, 1),
-        *place_quarters(spots, g_two, 1),
-        *place_quarters(spots, g_down, 1),
+        *place_quarters(spots, spread_c(x_qk), 2),
+        *place_quarters(spots, spread_c(x_vg), 2),
+        features_in_order(spread_c(x_out)),
+        *place_quarters(spots, spread_c(y_one), 1),
+        *place_quarters(spots, spread_c(y_two), 1),
+        *place_quarters(spots, spread_c(x_down), 1),
     )
 
 
 def solution(mesh):
-    by_tokens = P(None, ("rep", "shard"), None)
+    reps, shards = mesh.shape["rep"], mesh.shape["shard"]
+    devices = mesh.devices.reshape(reps // GROUP, 2, 2, shards)
+    rep = ("a", "b", "c")
+    by_tokens = P(None, (*rep, "shard"), None)
     by_rows = P("shard", None)
     return jax.shard_map(
-        functools.partial(body, mesh.shape["rep"], mesh.shape["shard"]),
-        mesh=mesh,
-        in_specs=(by_tokens, by_tokens, P(None, "rep", None), P(), *[by_rows] * 8),
+        functools.partial(body, reps, shards),
+        mesh=Mesh(devices, AXES),
+        in_specs=(by_tokens, by_tokens, P(None, rep, None), P(), *[by_rows] * 8),
         out_specs=(by_tokens, by_tokens, *[by_rows] * 8),
         check_vma=False,
     )

time: 1430 us -> 1450 us (1.014)
  matrix products: 128 us -> 33.5 us
  Pallas kernels: 260 us -> 340 us
  starting transfers between devices: 138 us -> 89.3 us
  local copies, waits for them, and re-layouts: 67.6 us -> 109 us
  waiting for transfers between devices: 691 us -> 730 us
    dot_general x11 -> x1, matrix products: 106 us -> 11.9 us  [cross_tokens(): lax.dot_general(former, latter, (((0,), (0,)), ((), ())), preferred_eleme...]
    pallas_call x0 -> x8, Pallas kernels: none -> 81.3 us  [gradient_rows(): pl.pallas_call(gradient_kernel, out_shape=out, grid_spec=pltpu.PrefetchSc...]
    all_gather x6 -> x5, waiting for transfers between devices: 0.04 us -> 34.3 us  [over_shards(): return lax.all_gather(piece, 'shard', axis=0, tiled=True)]
    unnamed x185 -> x179, local copies, waits for them, and re-layouts: 38.4 us -> 72.5 us
    ppermute x8, waiting for transfers between devices: 134 us -> 166 us  [bring_back(): lax.ppermute(slots[p], AXES, [(d, o) for o, d in routes(p, m)])]
    ppermute x8, starting transfers between devices: 49.2 us -> 18.8 us  [bring_back(): lax.ppermute(slots[p], AXES, [(d, o) for o, d in routes(p, m)])]
    ppermute x66 -> x58, starting transfers between devices: 69.5 us -> 47.8 us  [move(): return lax.ppermute(x, AXES, pairs)]
    ppermute x66 -> x58, waiting for transfers between devices: 409 us -> 396 us  [move(): return lax.ppermute(x, AXES, pairs)]
  transfers between devices with their start and end apart: 94 -> 86, of which waited for: 33 -> 34; matrix products, arithmetic and copies ran while one was open for 19% -> 13% of each run, Pallas kernels for 15% -> 23%
where the time goes in v4:
time: 1450 us; the launch traced here: 1430 us
  waiting for transfers between devices  730 us (50%)
  Pallas kernels  340 us (23%)
  other arithmetic  115 us (8%)
  local copies, waits for them, and re-layouts  109 us (8%)
  starting transfers between devices  89.3 us (6%)
  matrix products  33.5 us (2%)
  between operations  17.1 us (1%)
    ppermute x58, waiting for transfers between devices, move(): return lax.ppermute(x, AXES, pairs)  396 us
    ppermute x8, waiting for transfers between devices, bring_back(): lax.ppermute(slots[p], AXES, [(d, o) for o, d in routes(p, m)])  166 us
    ppermute x8, waiting for transfers between devices, bring(): arrived = [lax.ppermute(x[m], AXES, routes(p, m)) for m in range(micro)]  134 us
    pallas_call x6, Pallas kernels, fold_half(): pl.pallas_call(functools.partial(fold_kernel, len(values), arrived is not...  99.3 us
    pallas_call x8, Pallas kernels, gradient_rows(): pl.pallas_call(gradient_kernel, out_shape=out, grid_spec=pltpu.PrefetchSc...  81.3 us
    unnamed x179, local copies, waits for them, and re-layouts  72.5 us
    ppermute x58, starting transfers between devices, move(): return lax.ppermute(x, AXES, pairs)  47.8 us
    select_n x20, other arithmetic, ordered(): jnp.where(index == 0, jnp.concatenate([mine, other], axis), jnp.concatena...  43.9 us
  transfers between devices with their start and end apart: 86, of which 34 were waited for; matrix products, arithmetic and copies ran while one was open for 13% of the time, Pallas kernels for 23%

profile of v4, /device:TPU:17, one launch (start us, length us, event | category | flops | bytes accessed | tf_op | source)
XLA Modules:
  0.0 1433.9 jit_solution(13515706698920389418)
XLA Ops:
  24.4 71.8 %collective-permute-done.3 = bf16[256,2048]{1,0:T(8,128)(2,1)S(1)} collective-permute-done((bf16[256,2048]{1,0:T(8,128)(2,1)}, bf16[256,2048]{1,0:T(8,128)(2,1)S(1)}, u32[]{:S(2)}, u32[]{:S(2)}) %collective-permute-start.3) | collective-permute-done | bytes 1048608 | tf_op jit(solution)/shard_map/ppermute | solution.py:597
  102.9 45.3 %collective-permute-done.4 = bf16[512,2048]{1,0:T(8,128)(2,1)} collective-permute-done((bf16[512,2048]{1,0:T(8,128)(2,1)}, bf16[512,2048]{1,0:T(8,128)(2,1)}, u32[]{:S(2)}, u32[]{:S(2)}) %collective-permute-start.4) | collective-permute-done | bytes 2097184 | tf_op jit(solution)/shard_map/ppermute | solution.py:547
  148.2 6.2 maximum_select_fusion.1.own_ref
  173.7 18.7 %enter.2 = (bf16[2048,2048]{1,0:T(8,128)(2,1)}, f32[2048,1024]{1,0:T(8,128)}, f32[2048,1]{1,0:T(8,128)S(1)}, bf16[2048,512]{1,0:T(8,128)(2,1)S(1)}) custom-call(s32[4]{0:T(128)S(1)} %pad_add_fusion.1.spots, bf16[1024,2048]{1,0:T(8,128)(2,1)S(1)} %copy-done.14, bf16[1024,2048]{1,0:T(8,128)(2,1)} %collective-permute-done.6.other_ref, ...), custom_call_target="tpu_custom_call" | custom-call | flops 8589934592 | bytes 31465472 | tf_op jit(solution)/shard_map/enter/pallas_call | solution.py:246
  193.4 14.0 collective-permute-done.7.refs_1_.refs_5_.refs_6_
  208.6 14.7 %project.1.zv_ref = f32[2048,1024]{1,0:T(8,128)S(1)} custom-call(s32[4]{0:T(128)S(1)} %pad_add_fusion.1.spots, bf16[2048,2048]{1,0:T(8,128)(2,1)} %get-tuple-element.138.h_ref.left_ref, bf16[1024,1024]{1,0:T(8,128)(2,1)} %all-gather.9.cloned.1.call-done.refs_0_.refs_4_.refs_5_, bf16[1024,1024]{1,0:T(8,128)(2,1)} %collective-permute-done.7.refs_1_.refs_5_.refs_6_), custom_call_target="tpu_custom_call" | custom-call | flops 8589934592 | bytes 20971520 | tf_op jit(solution)/shard_map/project/pallas_call | solution.py:277
  226.7 12.3 attend.1
  247.1 45.5 %collective-permute-done.13 = bf16[2048,512]{1,0:T(8,128)(2,1)S(1)} collective-permute-done((bf16[2048,512]{1,0:T(8,128)(2,1)}, bf16[2048,512]{1,0:T(8,128)(2,1)S(1)}, u32[]{:S(2)}, u32[]{:S(2)}) %collective-permute-start.13) | collective-permute-done | bytes 2097184 | tf_op jit(solution)/shard_map/ppermute | solution.py:547
  313.4 12.3 fusion.21
  325.7 33.4 %all-gather.15.cloned.1.call-done.refs_2_.refs_4_.refs_5_ = bf16[1024,1408]{1,0:T(8,128)(2,1)} async-done(((bf16[256,1408]{1,0:T(8,128)(2,1)}), bf16[1024,1408]{1,0:T(8,128)(2,1)}) %all-gather.15.cloned.1.call-update) | async-done | bytes 2883600 | tf_op jit(solution)/shard_map/all_gather | solution.py:655
  359.1 12.1 collective-permute-done.15.refs_1_.refs_3_.refs_4_
  389.1 60.0 %collective-permute-done.20 = bf16[256,2048]{1,0:T(8,128)(2,1)S(1)} collective-permute-done((bf16[256,2048]{1,0:T(8,128)(2,1)}, bf16[256,2048]{1,0:T(8,128)(2,1)S(1)}, u32[]{:S(2)}, u32[]{:S(2)}) %collective-permute-start.20) | collective-permute-done | bytes 1048608 | tf_op jit(solution)/shard_map/ppermute | solution.py:597
  463.7 46.3 %collective-permute-done.22 = bf16[512,2048]{1,0:T(8,128)(2,1)S(1)} collective-permute-done((bf16[512,2048]{1,0:T(8,128)(2,1)S(1)}, bf16[512,2048]{1,0:T(8,128)(2,1)S(1)}, u32[]{:S(2)}, u32[]{:S(2)}) %collective-permute-start.22) | collective-permute-done | bytes 2097184 | tf_op jit(solution)/shard_map/ppermute | solution.py:547
  512.2 39.3 %collective-permute-done.23.refs_3_.refs_5_.refs_6_ = bf16[1024,1408]{1,0:T(8,128)(2,1)S(1)} collective-permute-done((bf16[1024,1408]{1,0:T(8,128)(2,1)S(1)}, bf16[1024,1408]{1,0:T(8,128)(2,1)S(1)}, u32[]{:S(2)}, u32[]{:S(2)}) %collective-permute-start.23) | collective-permute-done | bytes 2883616 | tf_op jit(solution)/shard_map/ppermute | solution.py:547
  555.8 37.9 %gated_unit.1 = (bf16[2048,2048]{1,0:T(8,128)(2,1)}, bf16[2048,1408]{1,0:T(8,128)(2,1)}, bf16[2048,1408]{1,0:T(8,128)(2,1)}, bf16[2048,1408]{1,0:T(8,128)(2,1)}, f32[2048,1]{1,0:T(8,128)S(1)}) custom-call(s32[4]{0:T(128)S(1)} %pad_add_fusion.1.spots, bf16[2048,1024]{1,0:T(8,128)(2,1)} %copy-done.63, bf16[2048,1024]{1,0:T(8,128)(2,1)} %copy-done.75, ...), custom_call_target="tpu_custom_call" | custom-call | flops 23622320128 | bytes 45621248 | tf_op jit(solution)/shard_map/gated_unit/pallas_call | solution.py:339
  603.0 16.4 %gradient_rows.10 = bf16[2048,1408]{1,0:T(8,128)(2,1)S(1)} custom-call(s32[4]{0:T(128)S(1)} %pad_add_fusion.1.spots, bf16[2048,2048]{1,0:T(8,128)(2,1)} %get-tuple-element.157.dy_ref.left_ref, bf16[2048,1408]{1,0:T(8,128)(2,1)S(1)} %copy-done.46), custom_call_target="tpu_custom_call" | custom-call | flops 11811160064 | bytes 17301504 | tf_op jit(solution)/shard_map/gradient_rows/pallas_call | solution.py:472
  622.4 22.4 %gated_unit_back.1 = (bf16[2048,1408]{1,0:T(8,128)(2,1)S(1)}, bf16[2048,1408]{1,0:T(8,128)(2,1)S(1)}, f32[2048,1]{1,0:T(8,128)S(1)}) custom-call(s32[4]{0:T(128)S(1)} %pad_add_fusion.1.spots, bf16[2048,2048]{1,0:T(8,128)(2,1)} %get-tuple-element.157.dy_ref.left_ref, bf16[2048,1408]{1,0:T(8,128)(2,1)} %get-tuple-element.161.one_ref, ...), custom_call_target="tpu_custom_call" | custom-call | flops 11811160064 | bytes 37232640 | tf_op jit(solution)/shard_map/gated_unit_back/pallas_call | solution.py:376
  650.7 19.9 %fold_half.6 = bf16[2048,1024]{1,0:T(8,128)(2,1)} custom-call(s32[4]{0:T(128)S(1)} %pad_add_fusion.1.spots, bf16[2048,1408]{1,0:T(8,128)(2,1)} %copy-done.48, bf16[2048,1408]{1,0:T(8,128)(2,1)} %copy-done.43, bf16[1024,1408]{1,0:T(8,128)(2,1)S(1)} %copy-done.24, bf16[1024,1408]{1,0:T(8,128)(2,1)} %collective-permute-done.15.refs_1_.refs_3_.refs_4_, ...), custom_call_target="tpu_custom_call" | custom-call | flops 11811160064 | bytes 21495808 | tf_op jit(solution)/shard_map/fold_half/pallas_call | solution.py:437
  683.0 9.5 gradient_rows.8
  692.5 21.9 %fold_half.7 = (bf16[2048,512]{1,0:T(8,128)(2,1)}, f32[2048,512]{1,0:T(8,128)}) custom-call(s32[4]{0:T(128)S(1)} %pad_add_fusion.1.spots, bf16[2048,1408]{1,0:T(8,128)(2,1)} %copy-done.48, bf16[2048,1408]{1,0:T(8,128)(2,1)} %copy-done.43, bf16[2048,1024]{1,0:T(8,128)(2,1)} %collective-permute-done.25.refs_2_, bf16[1024,1408]{1,0:T(8,128)(2,1)S(1)} %copy-done.25, ...), custom_call_target="tpu_custom_call" | custom-call | flops 11811160064 | bytes 27787264 | tf_op jit(solution)/shard_map/fold_half/pallas_call | solution.py:437
  719.3 11.4 fold_half.8
  733.4 16.4 %gradient_rows.9 = bf16[2048,1408]{1,0:T(8,128)(2,1)S(1)} custom-call(s32[4]{0:T(128)S(1)} %pad_add_fusion.1.spots, bf16[2048,2048]{1,0:T(8,128)(2,1)} %get-tuple-element.171.left_ref, bf16[2048,1408]{1,0:T(8,128)(2,1)S(1)} %copy-done.49), custom_call_target="tpu_custom_call" | custom-call | flops 11811160064 | bytes 17301504 | tf_op jit(solution)/shard_map/gradient_rows/pallas_call | solution.py:472
  752.3 9.4 collective-permute-done.26
  762.3 6.0 multiply_reduce_fusion.2
  773.2 11.9 convolution_convert_fusion.1
  801.0 44.7 %collective-permute-done.34 = f32[2048]{0:T(1024)S(1)} collective-permute-done((f32[2048]{0:T(1024)S(1)}, f32[2048]{0:T(1024)S(1)}, u32[]{:S(2)}, u32[]{:S(2)}) %collective-permute-start.34) | collective-permute-done | bytes 8224 | tf_op jit(solution)/shard_map/ppermute | solution.py:547
  845.7 13.0 fold_half.9
  868.2 9.4 gradient_rows.13
  879.3 6.0 multiply_convert_fusion
  885.3 21.3 %attend_back.1 = (bf16[2048,512]{1,0:T(8,128)(2,1)S(1)}, bf16[2048,512]{1,0:T(8,128)(2,1)S(1)}, bf16[2048,512]{1,0:T(8,128)(2,1)S(1)}) custom-call(f32[4]{0:T(128)S(1)} %copy-done.22, s32[2,2]{1,0:T(2,128)S(1)} %copy-done.20, f32[2048,1024]{1,0:T(8,128)} %get-tuple-element.139.zq_ref.zk_ref, f32[2048,1024]{1,0:T(8,128)} %get-tuple-element.139.zq_ref.zk_ref, ...), custom_call_target="tpu_custom_call" | custom-call | flops 10737418240 | bytes 20971520 | tf_op jit(solution)/shard_map/attend_back/pallas_call | solution.py:119
  907.7 8.0 gradient_rows.11
  919.3 7.3 gradient_rows.12
  926.7 16.5 %fold_half.10 = bf16[2048,1024]{1,0:T(8,128)(2,1)} custom-call(s32[4]{0:T(128)S(1)} %pad_add_fusion.1.spots, bf16[2048,1024]{1,0:T(8,128)(2,1)} %copy-done.5, bf16[2048,1024]{1,0:T(8,128)(2,1)} %copy-done.3, bf16[1024,1024]{1,0:T(8,128)(2,1)S(1)} %copy-done.33, bf16[1024,1024]{1,0:T(8,128)(2,1)S(1)} %copy-done.37, ...), custom_call_target="tpu_custom_call" | custom-call | flops 8589934592 | bytes 16777216 | tf_op jit(solution)/shard_map/fold_half/pallas_call | solution.py:437
  955.1 23.6 %collective-permute-done.41 = bf16[512,1408]{1,0:T(8,128)(2,1)} collective-permute-done((bf16[512,1408]{1,0:T(8,128)(2,1)}, bf16[512,1408]{1,0:T(8,128)(2,1)}, u32[]{:S(2)}, u32[]{:S(2)}) %collective-permute-start.41) | collective-permute-done | bytes 1441824 | tf_op jit(solution)/shard_map/ppermute | solution.py:547
  980.8 16.5 %fold_half.11 = (bf16[2048,512]{1,0:T(8,128)(2,1)S(1)}, f32[2048,512]{1,0:T(8,128)}) custom-call(s32[4]{0:T(128)S(1)} %pad_add_fusion.1.spots, bf16[2048,1024]{1,0:T(8,128)(2,1)} %copy-done.5, bf16[2048,1024]{1,0:T(8,128)(2,1)} %copy-done.3, bf16[2048,1024]{1,0:T(8,128)(2,1)} %collective-permute-done.39.refs_2_, bf16[1024,1024]{1,0:T(8,128)(2,1)S(1)} %copy-done.34, ...), custom_call_target="tpu_custom_call" | custom-call | flops 8589934592 | bytes 23068672 | tf_op jit(solution)/shard_map/fold_half/pallas_call | solution.py:437
  1009.9 16.0 %collective-permute-done.47 = bf16[2,512,512]{2,1,0:T(8,128)(2,1)} collective-permute-done((bf16[2,512,512]{2,1,0:T(8,128)(2,1)}, bf16[2,512,512]{2,1,0:T(8,128)(2,1)}, u32[]{:S(2)}, u32[]{:S(2)}) %collective-permute-start.47) | collective-permute-done | bytes 1048608 | tf_op jit(solution)/shard_map/ppermute | solution.py:547
  1032.5 7.2 gradient_rows.15
  1052.0 34.5 %collective-permute-done.46 = f32[2048]{0:T(1024)S(1)} collective-permute-done((f32[2048]{0:T(1024)S(1)}, f32[2048]{0:T(1024)S(1)}, u32[]{:S(2)}, u32[]{:S(2)}) %collective-permute-start.46) | collective-permute-done | bytes 8224 | tf_op jit(solution)/shard_map/ppermute | solution.py:547
  1094.9 7.2 gradient_rows.14
  1134.3 11.1 collective-permute-done.53
  1150.3 75.3 %collective-permute-done.52 = bf16[256,2048]{1,0:T(8,128)(2,1)S(1)} collective-permute-done((bf16[256,2048]{1,0:T(8,128)(2,1)S(1)}, bf16[256,2048]{1,0:T(8,128)(2,1)S(1)}, u32[]{:S(2)}, u32[]{:S(2)}) %collective-permute-start.52) | collective-permute-done | bytes 1048608 | tf_op jit(solution)/shard_map/ppermute | solution.py:606
  1226.0 22.1 %collective-permute-done.51 = bf16[256,2048]{1,0:T(8,128)(2,1)S(1)} collective-permute-done((bf16[256,2048]{1,0:T(8,128)(2,1)S(1)}, bf16[256,2048]{1,0:T(8,128)(2,1)S(1)}, u32[]{:S(2)}, u32[]{:S(2)}) %collective-permute-start.51) | collective-permute-done | bytes 1048608 | tf_op jit(solution)/shard_map/ppermute | solution.py:606
  1284.5 7.1 place_quarters.9
  1294.8 19.3 %collective-permute-done.64 = bf16[512,1024]{1,0:T(8,128)(2,1)S(1)} collective-permute-done((bf16[512,1024]{1,0:T(8,128)(2,1)}, bf16[512,1024]{1,0:T(8,128)(2,1)S(1)}, u32[]{:S(2)}, u32[]{:S(2)}) %collective-permute-start.64) | collective-permute-done | bytes 1048608 | tf_op jit(solution)/shard_map/ppermute | solution.py:547
  1314.6 32.2 %collective-permute-done.62 = bf16[256,2048]{1,0:T(8,128)(2,1)S(1)} collective-permute-done((bf16[256,2048]{1,0:T(8,128)(2,1)S(1)}, bf16[256,2048]{1,0:T(8,128)(2,1)S(1)}, u32[]{:S(2)}, u32[]{:S(2)}) %collective-permute-start.62) | collective-permute-done | bytes 1048608 | tf_op jit(solution)/shard_map/ppermute | solution.py:606
  1347.1 22.2 %collective-permute-done.61 = bf16[256,2048]{1,0:T(8,128)(2,1)S(1)} collective-permute-done((bf16[256,2048]{1,0:T(8,128)(2,1)S(1)}, bf16[256,2048]{1,0:T(8,128)(2,1)S(1)}, u32[]{:S(2)}, u32[]{:S(2)}) %collective-permute-start.61) | collective-permute-done | bytes 1048608 | tf_op jit(solution)/shard_map/ppermute | solution.py:606
  1369.7 13.1 collective-permute-done.59
  1386.4 15.6 %collective-permute-done.66 = bf16[512,1024]{1,0:T(8,128)(2,1)S(1)} collective-permute-done((bf16[512,1024]{1,0:T(8,128)(2,1)S(1)}, bf16[512,1024]{1,0:T(8,128)(2,1)S(1)}, u32[]{:S(2)}, u32[]{:S(2)}) %collective-permute-start.66) | collective-permute-done | bytes 1048608 | tf_op jit(solution)/shard_map/ppermute | solution.py:547
  (445 shorter events, 352.5 us)
Async XLA Ops:
  8.0 93.2 %all-gather.7.cloned.1.call-start = ((), (), s32[]{:S(2)}) async-start(), calls=%async_computation.6 | async-start | bytes 2621440 | tf_op jit(solution)/shard_map/all_gather | solution.py:655
  10.4 144.1 %all-gather.9.cloned.1.call-start = ((), (), s32[]{:S(2)}) async-start(), calls=%async_computation.7 | async-start | bytes 2621440 | tf_op jit(solution)/shard_map/all_gather | solution.py:655
  11.9 84.3 %collective-permute-start.3 = (bf16[256,2048]{1,0:T(8,128)(2,1)}, bf16[256,2048]{1,0:T(8,128)(2,1)S(1)}, u32[]{:S(2)}, u32[]{:S(2)}) collective-permute-start(bf16[256,2048]{1,0:T(8,128)(2,1)} %get-tuple-element.278), channel_id=1, source_target_pairs={{1,2},{5,3},{9,6},{13,7},{3,10},{7,11},{11,14},{15,15},{17,18},{21... | collective-permute-start | bytes 3145736 | tf_op jit(solution)/shard_map/ppermute | solution.py:597
  13.2 83.0 %collective-permute-start.2 = (bf16[256,2048]{1,0:T(8,128)(2,1)}, bf16[256,2048]{1,0:T(8,128)(2,1)}, u32[]{:S(2)}, u32[]{:S(2)}) collective-permute-start(bf16[256,2048]{1,0:T(8,128)(2,1)} %get-tuple-element.279), channel_id=1, source_target_pairs={{1,0},{5,1},{9,4},{13,5},{3,8},{7,9},{11,12},{15,13},{17,16},{21,1... | collective-permute-start | bytes 3145736 | tf_op jit(solution)/shard_map/ppermute | solution.py:597
  14.8 83.0 %collective-permute-start.1 = (bf16[256,2048]{1,0:T(8,128)(2,1)}, bf16[256,2048]{1,0:T(8,128)(2,1)S(1)}, u32[]{:S(2)}, u32[]{:S(2)}) collective-permute-start(bf16[256,2048]{1,0:T(8,128)(2,1)} %get-tuple-element.278), channel_id=1, source_target_pairs={{0,2},{4,3},{8,6},{12,7},{2,10},{6,11},{10,14},{14,15},{16,18},{20... | collective-permute-start | bytes 3145736 | tf_op jit(solution)/shard_map/ppermute | solution.py:597
  20.8 78.5 %collective-permute-start = (bf16[256,2048]{1,0:T(8,128)(2,1)}, bf16[256,2048]{1,0:T(8,128)(2,1)S(1)}, u32[]{:S(2)}, u32[]{:S(2)}) collective-permute-start(bf16[256,2048]{1,0:T(8,128)(2,1)} %get-tuple-element.279), channel_id=1, source_target_pairs={{0,0},{4,1},{8,4},{12,5},{2,8},{6,9},{10,12},{14,13},{16,16},{20,1... | collective-permute-start | bytes 3145736 | tf_op jit(solution)/shard_map/ppermute | solution.py:597
  24.3 169.0 %all-gather.11.cloned.1.call-start = ((), (), s32[]{:S(2)}) async-start(), calls=%async_computation.8 | async-start | bytes 1310720 | tf_op jit(solution)/shard_map/all_gather | solution.py:655
  101.7 52.8 %collective-permute-start.5 = (bf16[1024,1024]{1,0:T(8,128)(2,1)}, bf16[1024,1024]{1,0:T(8,128)(2,1)S(1)}, u32[]{:S(2)}, u32[]{:S(2)}) collective-permute-start(bf16[1024,1024]{1,0:T(8,128)(2,1)} %all-gather.7.cloned.1.call-done.refs_0_.refs_2_.refs_3_), channel_id=1, source_target_pairs={{0,16},{1,17},{2,18},{3,19},{4,20},{5,21},{6,22},{7,23},{8,24},{9,... | collective-permute-start | bytes 6291464 | tf_op jit(solution)/shard_map/ppermute | solution.py:547
  157.7 88.2 %all-gather.13.cloned.1.call-start = ((), (), s32[]{:S(2)}) async-start(), calls=%async_computation.9 | async-start | bytes 3604480 | tf_op jit(solution)/shard_map/all_gather | solution.py:655
  160.2 198.9 %all-gather.15.cloned.1.call-start = ((), (), s32[]{:S(2)}) async-start(), calls=%async_computation.10 | async-start | bytes 3604480 | tf_op jit(solution)/shard_map/all_gather | solution.py:655
  301.5 320.9 %all-gather.17.cloned.1.call-start = ((), (), s32[]{:S(2)}) async-start(), calls=%async_computation.11 | async-start | bytes 6488064 | tf_op jit(solution)/shard_map/all_gather | solution.py:659
  308.4 62.8 %collective-permute-start.15 = (bf16[1024,1408]{1,0:T(8,128)(2,1)}, bf16[1024,1408]{1,0:T(8,128)(2,1)}, u32[]{:S(2)}, u32[]{:S(2)}) collective-permute-start(bf16[1024,1408]{1,0:T(8,128)(2,1)} %all-gather.13.cloned.1.call-done.refs_0_.refs_2_.refs_3_), channel_id=1, source_target_pairs={{0,16},{1,17},{2,18},{3,19},{4,20},{5,21},{6,22},{7,23},{8,24},{9,... | collective-permute-start | bytes 8650760 | tf_op jit(solution)/shard_map/ppermute | solution.py:547
  371.2 83.4 %collective-permute-start.16 = (bf16[2048,512]{1,0:T(8,128)(2,1)}, bf16[2048,512]{1,0:T(8,128)(2,1)}, u32[]{:S(2)}, u32[]{:S(2)}) collective-permute-start(bf16[2048,512]{1,0:T(8,128)(2,1)} %get-tuple-element.146), channel_id=1, source_target_pairs={{0,8},{1,9},{2,10},{3,11},{4,12},{5,13},{6,14},{7,15},{8,0},{9,1},... | collective-permute-start | bytes 6291464 | tf_op jit(solution)/shard_map/ppermute | solution.py:547
  375.5 73.7 %collective-permute-start.20 = (bf16[256,2048]{1,0:T(8,128)(2,1)}, bf16[256,2048]{1,0:T(8,128)(2,1)S(1)}, u32[]{:S(2)}, u32[]{:S(2)}) collective-permute-start(bf16[256,2048]{1,0:T(8,128)(2,1)} %get-tuple-element.274), channel_id=1, source_target_pairs={{1,2},{5,3},{9,6},{13,7},{3,10},{7,11},{11,14},{15,15},{17,18},{21... | collective-permute-start | bytes 3145736 | tf_op jit(solution)/shard_map/ppermute | solution.py:597
  376.8 73.4 %collective-permute-start.19 = (bf16[256,2048]{1,0:T(8,128)(2,1)}, bf16[256,2048]{1,0:T(8,128)(2,1)}, u32[]{:S(2)}, u32[]{:S(2)}) collective-permute-start(bf16[256,2048]{1,0:T(8,128)(2,1)} %get-tuple-element.275), channel_id=1, source_target_pairs={{1,0},{5,1},{9,4},{13,5},{3,8},{7,9},{11,12},{15,13},{17,16},{21,1... | collective-permute-start | bytes 3145736 | tf_op jit(solution)/shard_map/ppermute | solution.py:597
  378.4 73.7 %collective-permute-start.18 = (bf16[256,2048]{1,0:T(8,128)(2,1)}, bf16[256,2048]{1,0:T(8,128)(2,1)}, u32[]{:S(2)}, u32[]{:S(2)}) collective-permute-start(bf16[256,2048]{1,0:T(8,128)(2,1)} %get-tuple-element.274), channel_id=1, source_target_pairs={{0,2},{4,3},{8,6},{12,7},{2,10},{6,11},{10,14},{14,15},{16,18},{20... | collective-permute-start | bytes 3145736 | tf_op jit(solution)/shard_map/ppermute | solution.py:597
  384.3 68.0 %collective-permute-start.17 = (bf16[256,2048]{1,0:T(8,128)(2,1)}, bf16[256,2048]{1,0:T(8,128)(2,1)}, u32[]{:S(2)}, u32[]{:S(2)}) collective-permute-start(bf16[256,2048]{1,0:T(8,128)(2,1)} %get-tuple-element.275), channel_id=1, source_target_pairs={{0,0},{4,1},{8,4},{12,5},{2,8},{6,9},{10,12},{14,13},{16,16},{20,1... | collective-permute-start | bytes 3145736 | tf_op jit(solution)/shard_map/ppermute | solution.py:597
  389.1 472.9 %reduce-scatter.7.cloned.1.call-start = ((), (), s32[]{:S(2)}) async-start(), calls=%async_computation.12 | async-start | bytes 6488064 | tf_op jit(solution)/shard_map/reduce_scatter | solution.py:692
  459.5 92.0 %collective-permute-start.21 = (bf16[2048,1024]{1,0:T(8,128)(2,1)S(1)}, bf16[2048,1024]{1,0:T(8,128)(2,1)S(1)}, u32[]{:S(2)}, u32[]{:S(2)}) collective-permute-start(bf16[2048,1024]{1,0:T(8,128)(2,1)S(1)} %maximum_select_fusion.3.own_ref), channel_id=1, source_target_pairs={{0,4},{1,5},{2,6},{3,7},{4,0},{5,1},{6,2},{7,3},{8,12},{9,13},{10,... | collective-permute-start | bytes 12582920 | tf_op jit(solution)/shard_map/ppermute | solution.py:547
  461.8 89.7 %collective-permute-start.23 = (bf16[1024,1408]{1,0:T(8,128)(2,1)S(1)}, bf16[1024,1408]{1,0:T(8,128)(2,1)S(1)}, u32[]{:S(2)}, u32[]{:S(2)}) collective-permute-start(bf16[1024,1408]{1,0:T(8,128)(2,1)S(1)} %copy-done.26), channel_id=1, source_target_pairs={{0,16},{1,17},{2,18},{3,19},{4,20},{5,21},{6,22},{7,23},{8,24},{9,... | collective-permute-start | bytes 8650760 | tf_op jit(solution)/shard_map/ppermute | solution.py:547
  621.9 376.7 %reduce-scatter.9.cloned.1.call-start = ((), (), s32[]{:S(2)}) async-start(), calls=%async_computation.13 | async-start | bytes 6488064 | tf_op jit(solution)/shard_map/reduce_scatter | solution.py:692
  714.5 47.2 %collective-permute-start.26 = (bf16[2048,512]{1,0:T(8,128)(2,1)}, bf16[2048,512]{1,0:T(8,128)(2,1)}, u32[]{:S(2)}, u32[]{:S(2)}) collective-permute-start(bf16[2048,512]{1,0:T(8,128)(2,1)} %get-tuple-element.173), channel_id=1, source_target_pairs={{0,8},{1,9},{2,10},{3,11},{4,12},{5,13},{6,14},{7,15},{8,0},{9,1},... | collective-permute-start | bytes 6291464 | tf_op jit(solution)/shard_map/ppermute | solution.py:547
  761.7 331.1 %reduce-scatter.11.cloned.1.call-start = ((), (), s32[]{:S(2)}) async-start(), calls=%async_computation.14 | async-start | bytes 3604480 | tf_op jit(solution)/shard_map/reduce_scatter | solution.py:686
  797.9 64.1 %collective-permute-start.32 = (bf16[2048,512]{1,0:T(8,128)(2,1)}, bf16[2048,512]{1,0:T(8,128)(2,1)}, u32[]{:S(2)}, u32[]{:S(2)}) collective-permute-start(bf16[2048,512]{1,0:T(8,128)(2,1)} %dynamic-slice_convert_fusion), channel_id=1, source_target_pairs={{0,8},{1,9},{2,10},{3,11},{4,12},{5,13},{6,14},{7,15},{8,0},{9,1},... | collective-permute-start | bytes 6291464 | tf_op jit(solution)/shard_map/ppermute | solution.py:547
  798.0 64.0 %collective-permute-start.35 = (bf16[512,1408]{1,0:T(8,128)(2,1)}, bf16[512,1408]{1,0:T(8,128)(2,1)}, u32[]{:S(2)}, u32[]{:S(2)}) collective-permute-start(bf16[512,1408]{1,0:T(8,128)(2,1)} %get-tuple-element.189), channel_id=1, source_target_pairs={{0,16},{1,17},{2,18},{3,19},{4,20},{5,21},{6,22},{7,23},{8,24},{9,... | collective-permute-start | bytes 4325384 | tf_op jit(solution)/shard_map/ppermute | solution.py:547
  862.0 53.8 %collective-permute-start.37 = (bf16[256,1408]{1,0:T(8,128)(2,1)}, bf16[256,1408]{1,0:T(8,128)(2,1)}, u32[]{:S(2)}, u32[]{:S(2)}) collective-permute-start(bf16[256,1408]{1,0:T(8,128)(2,1)} %reduce-scatter.7.cloned.1.call-done), channel_id=1, source_target_pairs={{0,16},{1,17},{2,18},{3,19},{4,20},{5,21},{6,22},{7,23},{8,24},{9,... | collective-permute-start | bytes 2162696 | tf_op jit(solution)/shard_map/ppermute | solution.py:547
  862.1 57.3 %collective-permute-start.36 = (bf16[1024,512]{1,0:T(8,128)(2,1)}, bf16[1024,512]{1,0:T(8,128)(2,1)}, u32[]{:S(2)}, u32[]{:S(2)}) collective-permute-start(bf16[1024,512]{1,0:T(8,128)(2,1)} %get-tuple-element.197), channel_id=1, source_target_pairs={{0,16},{1,17},{2,18},{3,19},{4,20},{5,21},{6,22},{7,23},{8,24},{9,... | collective-permute-start | bytes 3145736 | tf_op jit(solution)/shard_map/ppermute | solution.py:547
  863.5 79.8 %collective-permute-start.38 = (bf16[2048,512]{1,0:T(8,128)(2,1)}, bf16[2048,512]{1,0:T(8,128)(2,1)}, u32[]{:S(2)}, u32[]{:S(2)}) collective-permute-start(bf16[2048,512]{1,0:T(8,128)(2,1)} %copy-done.41), channel_id=1, source_target_pairs={{0,8},{1,9},{2,10},{3,11},{4,12},{5,13},{6,14},{7,15},{8,0},{9,1},... | collective-permute-start | bytes 6291464 | tf_op jit(solution)/shard_map/ppermute | solution.py:547
  879.2 224.2 %reduce-scatter.13.cloned.1.call-start = ((), (), s32[]{:S(2)}) async-start(), calls=%async_computation.15 | async-start | bytes 1310720 | tf_op jit(solution)/shard_map/reduce_scatter | solution.py:686
  946.6 52.1 %collective-permute-start.40 = (bf16[1024,1024]{1,0:T(8,128)(2,1)}, bf16[1024,1024]{1,0:T(8,128)(2,1)}, u32[]{:S(2)}, u32[]{:S(2)}) collective-permute-start(bf16[1024,1024]{1,0:T(8,128)(2,1)} %copy-done.42), channel_id=1, source_target_pairs={{0,16},{1,17},{2,18},{3,19},{4,20},{5,21},{6,22},{7,23},{8,24},{9,... | collective-permute-start | bytes 6291464 | tf_op jit(solution)/shard_map/ppermute | solution.py:547
  949.1 302.1 %reduce-scatter.15.cloned.1.call-start = ((), (), s32[]{:S(2)}) async-start(), calls=%async_computation.16 | async-start | bytes 2621440 | tf_op jit(solution)/shard_map/reduce_scatter | solution.py:686
  1002.9 89.8 %collective-permute-start.43 = (bf16[1024,1024]{1,0:T(8,128)(2,1)}, bf16[1024,1024]{1,0:T(8,128)(2,1)}, u32[]{:S(2)}, u32[]{:S(2)}) collective-permute-start(bf16[1024,1024]{1,0:T(8,128)(2,1)} %copy-done.39), channel_id=1, source_target_pairs={{0,16},{1,17},{2,18},{3,19},{4,20},{5,21},{6,22},{7,23},{8,24},{9,... | collective-permute-start | bytes 6291464 | tf_op jit(solution)/shard_map/ppermute | solution.py:547
  1002.9 89.8 %collective-permute-start.42 = (bf16[2048,512]{1,0:T(8,128)(2,1)}, bf16[2048,512]{1,0:T(8,128)(2,1)}, u32[]{:S(2)}, u32[]{:S(2)}) collective-permute-start(bf16[2048,512]{1,0:T(8,128)(2,1)} %copy-done.40), channel_id=1, source_target_pairs={{0,8},{1,9},{2,10},{3,11},{4,12},{5,13},{6,14},{7,15},{8,0},{9,1},... | collective-permute-start | bytes 6291464 | tf_op jit(solution)/shard_map/ppermute | solution.py:547
  1008.6 77.9 %collective-permute-start.44 = (bf16[256,1408]{1,0:T(8,128)(2,1)}, bf16[256,1408]{1,0:T(8,128)(2,1)}, u32[]{:S(2)}, u32[]{:S(2)}) collective-permute-start(bf16[256,1408]{1,0:T(8,128)(2,1)} %reduce-scatter.9.cloned.1.call-done), channel_id=1, source_target_pairs={{0,8},{1,9},{2,10},{3,11},{4,12},{5,13},{6,14},{7,15},{8,0},{9,1},... | collective-permute-start | bytes 2162696 | tf_op jit(solution)/shard_map/ppermute | solution.py:547
  1029.8 59.2 %collective-permute-start.48 = (bf16[512,1024]{1,0:T(8,128)(2,1)}, bf16[512,1024]{1,0:T(8,128)(2,1)}, u32[]{:S(2)}, u32[]{:S(2)}) collective-permute-start(bf16[512,1024]{1,0:T(8,128)(2,1)} %get-tuple-element.269), channel_id=1, source_target_pairs={{0,4},{1,5},{2,6},{3,7},{4,0},{5,1},{6,2},{7,3},{8,12},{9,13},{10,... | collective-permute-start | bytes 3145736 | tf_op jit(solution)/shard_map/ppermute | solution.py:547
  1041.0 225.1 %reduce-scatter.17.cloned.1.call-start = ((), (), s32[]{:S(2)}) async-start(), calls=%async_computation.17 | async-start | bytes 2621440 | tf_op jit(solution)/shard_map/reduce_scatter | solution.py:686
  1121.9 103.8 %collective-permute-start.52 = (bf16[256,2048]{1,0:T(8,128)(2,1)S(1)}, bf16[256,2048]{1,0:T(8,128)(2,1)S(1)}, u32[]{:S(2)}, u32[]{:S(2)}) collective-permute-start(bf16[256,2048]{1,0:T(8,128)(2,1)S(1)} %get-tuple-element.266), channel_id=1, source_target_pairs={{2,1},{3,5},{6,9},{7,13},{10,3},{11,7},{14,11},{15,15},{18,17},{19... | collective-permute-start | bytes 3145736 | tf_op jit(solution)/shard_map/ppermute | solution.py:606
  1126.8 121.3 %collective-permute-start.51 = (bf16[256,2048]{1,0:T(8,128)(2,1)S(1)}, bf16[256,2048]{1,0:T(8,128)(2,1)S(1)}, u32[]{:S(2)}, u32[]{:S(2)}) collective-permute-start(bf16[256,2048]{1,0:T(8,128)(2,1)S(1)} %get-tuple-element.267), channel_id=1, source_target_pairs={{2,0},{3,4},{6,8},{7,12},{10,2},{11,6},{14,10},{15,14},{18,16},{19... | collective-permute-start | bytes 3145736 | tf_op jit(solution)/shard_map/ppermute | solution.py:606
  1128.8 119.8 %collective-permute-start.50 = (bf16[256,2048]{1,0:T(8,128)(2,1)S(1)}, bf16[256,2048]{1,0:T(8,128)(2,1)S(1)}, u32[]{:S(2)}, u32[]{:S(2)}) collective-permute-start(bf16[256,2048]{1,0:T(8,128)(2,1)S(1)} %get-tuple-element.266), channel_id=1, source_target_pairs={{0,1},{1,5},{4,9},{5,13},{8,3},{9,7},{12,11},{13,15},{16,17},{17,2... | collective-permute-start | bytes 3145736 | tf_op jit(solution)/shard_map/ppermute | solution.py:606
  1130.5 119.0 %collective-permute-start.49 = (bf16[256,2048]{1,0:T(8,128)(2,1)S(1)}, bf16[256,2048]{1,0:T(8,128)(2,1)S(1)}, u32[]{:S(2)}, u32[]{:S(2)}) collective-permute-start(bf16[256,2048]{1,0:T(8,128)(2,1)S(1)} %get-tuple-element.267), channel_id=1, source_target_pairs={{0,0},{1,4},{4,8},{5,12},{8,2},{9,6},{12,10},{13,14},{16,16},{17,2... | collective-permute-start | bytes 3145736 | tf_op jit(solution)/shard_map/ppermute | solution.py:606
  1145.4 107.0 %collective-permute-start.56 = (bf16[256,2816]{1,0:T(8,128)(2,1)}, bf16[256,2816]{1,0:T(8,128)(2,1)}, u32[]{:S(2)}, u32[]{:S(2)}) collective-permute-start(bf16[256,2816]{1,0:T(8,128)(2,1)} %pad_maximum_fusion.8), channel_id=1, source_target_pairs={{0,16},{1,17},{2,18},{3,19},{4,20},{5,21},{6,22},{7,23},{8,24},{9,... | collective-permute-start | bytes 4325384 | tf_op jit(solution)/shard_map/ppermute | solution.py:547
  1225.6 54.7 %collective-permute-start.73 = (bf16[512,2816]{1,0:T(8,128)(2,1)S(1)}, bf16[512,2816]{1,0:T(8,128)(2,1)}, u32[]{:S(2)}, u32[]{:S(2)}) collective-permute-start(bf16[512,2816]{1,0:T(8,128)(2,1)S(1)} %pad_maximum_fusion.1.refs_0_.refs_1_), channel_id=1, source_target_pairs={{0,4},{1,5},{2,6},{3,7},{4,0},{5,1},{6,2},{7,3},{8,12},{9,13},{10,... | collective-permute-start | bytes 8650760 | tf_op jit(solution)/shard_map/ppermute | solution.py:547
  1276.9 69.9 %collective-permute-start.62 = (bf16[256,2048]{1,0:T(8,128)(2,1)S(1)}, bf16[256,2048]{1,0:T(8,128)(2,1)S(1)}, u32[]{:S(2)}, u32[]{:S(2)}) collective-permute-start(bf16[256,2048]{1,0:T(8,128)(2,1)S(1)} %get-tuple-element.260), channel_id=1, source_target_pairs={{2,1},{3,5},{6,9},{7,13},{10,3},{11,7},{14,11},{15,15},{18,17},{19... | collective-permute-start | bytes 3145736 | tf_op jit(solution)/shard_map/ppermute | solution.py:606
  1280.4 88.9 %collective-permute-start.61 = (bf16[256,2048]{1,0:T(8,128)(2,1)S(1)}, bf16[256,2048]{1,0:T(8,128)(2,1)S(1)}, u32[]{:S(2)}, u32[]{:S(2)}) collective-permute-start(bf16[256,2048]{1,0:T(8,128)(2,1)S(1)} %get-tuple-element.261), channel_id=1, source_target_pairs={{2,0},{3,4},{6,8},{7,12},{10,2},{11,6},{14,10},{15,14},{18,16},{19... | collective-permute-start | bytes 3145736 | tf_op jit(solution)/shard_map/ppermute | solution.py:606
  1291.7 78.0 %collective-permute-start.60 = (bf16[256,2048]{1,0:T(8,128)(2,1)S(1)}, bf16[256,2048]{1,0:T(8,128)(2,1)S(1)}, u32[]{:S(2)}, u32[]{:S(2)}) collective-permute-start(bf16[256,2048]{1,0:T(8,128)(2,1)S(1)} %get-tuple-element.260), channel_id=1, source_target_pairs={{0,1},{1,5},{4,9},{5,13},{8,3},{9,7},{12,11},{13,15},{16,17},{17,2... | collective-permute-start | bytes 3145736 | tf_op jit(solution)/shard_map/ppermute | solution.py:606
  1292.5 90.3 %collective-permute-start.59 = (bf16[256,2048]{1,0:T(8,128)(2,1)S(1)}, bf16[256,2048]{1,0:T(8,128)(2,1)S(1)}, u32[]{:S(2)}, u32[]{:S(2)}) collective-permute-start(bf16[256,2048]{1,0:T(8,128)(2,1)S(1)} %get-tuple-element.261), channel_id=1, source_target_pairs={{0,0},{1,4},{4,8},{5,12},{8,2},{9,6},{12,10},{13,14},{16,16},{17,2... | collective-permute-start | bytes 3145736 | tf_op jit(solution)/shard_map/ppermute | solution.py:606
  1314.1 70.4 %collective-permute-start.71 = (bf16[256,2816]{1,0:T(8,128)(2,1)S(1)}, bf16[256,2816]{1,0:T(8,128)(2,1)S(1)}, u32[]{:S(2)}, u32[]{:S(2)}) collective-permute-start(bf16[256,2816]{1,0:T(8,128)(2,1)S(1)} %copy-done.53), channel_id=1, source_target_pairs={{0,16},{1,17},{2,18},{3,19},{4,20},{5,21},{6,22},{7,23},{8,24},{9,... | collective-permute-start | bytes 4325384 | tf_op jit(solution)/shard_map/ppermute | solution.py:547
  1346.8 59.7 %collective-permute-start.70 = (bf16[512,2816]{1,0:T(8,128)(2,1)S(1)}, bf16[512,2816]{1,0:T(8,128)(2,1)S(1)}, u32[]{:S(2)}, u32[]{:S(2)}) collective-permute-start(bf16[512,2816]{1,0:T(8,128)(2,1)S(1)} %copy-done.7), channel_id=1, source_target_pairs={{0,4},{1,5},{2,6},{3,7},{4,0},{5,1},{6,2},{7,3},{8,12},{9,13},{10,... | collective-permute-start | bytes 8650760 | tf_op jit(solution)/shard_map/ppermute | solution.py:547
  (115 other events, 2611.9 us)
Sparse Core Ops, SparseCore 0:
  11.0 82.1 all-gather.6
  95.3 46.7 all-gather.8
  157.8 28.1 all-gather.10
  188.1 57.8 all-gather.12
  301.6 57.4 all-gather.14
Sparse Core Ops, SparseCore 1:
  389.2 147.1 all-gather.16
  622.0 108.0 reduce-scatter.6
  761.8 120.3 reduce-scatter.8
  884.4 56.6 reduce-scatter.10
  949.2 25.2 reduce-scatter.12
  1041.1 42.8 reduce-scatter.14
  1116.7 102.7 reduce-scatter.16

commit v5 on v4

--- a/solution.py
+++ b/solution.py
@@ -488,34 +488,32 @@
     )(spots, left, right, *arrived)
 
 
-def place_kernel(count, spots, *refs):
+def place_kernel(cuts, spots, *refs):
     quarter = pl.program_id(0)
     cross = lax.rem(lax.div(quarter, 2) + spots[0], 2) * 2 + lax.rem(lax.rem(quarter, 2) + spots[3], 2)
     for n in range(4):
 
         @pl.when(cross == n)
         def _():
-            size = refs[n].shape[1] // count
-            for m in range(count):
-                refs[4 + m][...] = refs[n][:, m * size : (m + 1) * size].astype(F32)
-
-
-def place_quarters(spots, four, count):
+            for (first, size), out_ref in zip(cuts, refs[4:]):
+                out_ref[...] = refs[n][:, first : first + size].astype(F32)
+
+
+def place_quarters(spots, four, *cuts):
     rows, columns = four[0][0].shape[0], four[0][2]
-    size = columns // count
-    outs = [jax.ShapeDtypeStruct((rows, GROUP * size), F32)] * count
+    outs = [jax.ShapeDtypeStruct((rows, GROUP * size), F32) for _, size in cuts]
 
     def block(index):
-        return pl.BlockSpec((rows, columns), lambda q, s: (0, index))
+        return pl.BlockSpec((rows, columns), lambda q, s: (0, index), pipeline_mode=pl.Buffered(1))
 
     return pl.pallas_call(
-        functools.partial(place_kernel, count),
+        functools.partial(place_kernel, cuts),
         out_shape=outs,
         grid_spec=pltpu.PrefetchScalarGridSpec(
             num_scalar_prefetch=1,
             grid=(GROUP,),
             in_specs=[block(index) for _, index, _ in four],
-            out_specs=[pl.BlockSpec((rows, size), lambda q, s: (0, q))] * count,
+            out_specs=[pl.BlockSpec((rows, size), lambda q, s: (0, q)) for _, size in cuts],
         ),
         compiler_params=limit(40),
         cost_estimate=estimate(0, *[x for x, _, _ in four], *outs),
@@ -552,6 +550,9 @@
     def swap_b(x):
         return move(x, lambda r: r ^ 2)
 
+    def joined(*parts):
+        return jnp.concatenate(parts, axis=1)
+
     def shift_a(x, k):
         return move(x, lambda r: (r + GROUP * k) % reps)
 
@@ -563,22 +564,21 @@
         )
 
 
+    def batch_of(s):
+        return s // (shards // micro)
+
     def origin(r, s, p):
         run_id = (2 * (r % 2) + (r // 2) % 2) * per_block + p
         stream, piece = run_id // shards, run_id % shards
-        if streams == 1:
-            batch, member = s // GROUP, s % GROUP
-        else:
-            batch, member = s // 2, 2 * stream + s % 2
-        return (r // GROUP) * GROUP + member, piece, batch
-
-    def routes(p, batch):
+        member = s % GROUP if streams == 1 else 2 * stream + s % 2
+        return (r // GROUP) * GROUP + member, piece
+
+    def routes(p):
         found = []
         for r in range(reps):
             for s in range(shards):
-                from_r, from_s, from_batch = origin(r, s, p)
-                if from_batch == batch:
-                    found.append((from_r * shards + from_s, r * shards + s))
+                from_r, from_s = origin(r, s, p ^ batch_of(s))
+                found.append((from_r * shards + from_s, r * shards + s))
         return found
 
     def natural(x):
@@ -592,22 +592,23 @@
         )
 
     def bring(x):
-        slots = []
-        for p in range(per_block):
-            arrived = [lax.ppermute(x[m], AXES, routes(p, m)) for m in range(micro)]
-            slots.append(functools.reduce(jnp.add, arrived))
-        return jnp.concatenate(slots, axis=0)
+        arrived = [
+            lax.ppermute(lax.dynamic_index_in_dim(x, (place + p) % 2, 0, False), AXES, routes(p))
+            for p in range(2)
+        ]
+        return ordered(batch_of(place), *arrived, 0)
 
     def bring_back(x):
-        slots = natural(x).reshape(per_block, run, width)
-        batches = []
-        for m in range(micro):
-            arrived = [
-                lax.ppermute(slots[p], AXES, [(d, o) for o, d in routes(p, m)])
-                for p in range(per_block)
-            ]
-            batches.append(functools.reduce(jnp.add, arrived))
-        return jnp.stack(batches)
+        slots = natural(x).reshape(2, run, width)
+        arrived = [
+            lax.ppermute(
+                lax.dynamic_index_in_dim(slots, (batch_of(place) + p) % 2, 0, False),
+                AXES,
+                [(to, origin) for origin, to in routes(p)],
+            )
+            for p in range(2)
+        ]
+        return ordered(place % 2, arrived[0][None], arrived[1][None], 0)
 
 
     def gather_b(x):
@@ -704,8 +705,8 @@
         other, size = swap_c(pair), pair.shape[1] // 2
         return [(pair, 0, size), (pair, 1, size), (other, 0, size), (other, 1, size)]
 
-    def features_in_order(four):
-        cut = [x[:, index * size : (index + 1) * size] for x, index, size in four]
+    def features_in_order(four, first, size):
+        cut = [x[:, index * full + first : index * full + first + size] for x, index, full in four]
         pair = [ordered(b, cut[n], cut[n + 1], 1) for n in (0, 2)]
         return natural(ordered(c, pair[0], pair[1], 1)).astype(F32)
 
@@ -745,41 +746,42 @@
     s_vg = over_spread(g_vg)
     w_qk = [g_qk, *s_qk]
     hidden_one, z_qk, x_scale, x_own = enter(spots, blocks, x_pair, swap_c(x_pair), w_qk)
-    z_qk, hidden_one, s_vg, g_o, cotangent = tie(z_qk, hidden_one, s_vg, g_o, cotangent)
+    z_qk, hidden_one, s_vg, g_o = tie(z_qk, hidden_one, s_vg, g_o)
 
     s_o = over_spread(g_o)
-    dy_run = bring(cotangent)
     w_vg = [g_vg, *s_vg]
     z_vg = project(spots, hidden_one, w_vg)
     attended = attend(rates, ends, z_qk, z_vg)
     gate = z_vg[:, own:]
     o_scale = lax.rsqrt(total(jnp.sum(attended * attended, axis=-1)) / width + EPSILON)[:, None]
     lifted = (attended * gate).astype(LOW)
-    lifted, s_o, g_1 = tie(lifted, s_o, g_1)
+    lifted, s_o, g_1, cotangent = tie(lifted, s_o, g_1, cotangent)
 
     s_1 = over_spread(g_1)
-    lifted = gather_c(gather_b(lifted))
+    lifted = gather_b(lifted)
+    lifted, s_1, g_2, o_scale, cotangent = tie(lifted, s_1, g_2, o_scale, cotangent)
+
+    s_2 = over_spread(g_2)
+    dy_run = bring(cotangent)
+    lifted = gather_c(lifted)
     w_o = in_row_order(by_spread([g_o, *s_o]))
     branch = o_scale * matmul(lifted, w_o)
     middle = x_own.astype(F32) + branch
-    low_middle = middle.astype(LOW)
-    low_middle, s_1, g_2 = tie(low_middle, s_1, g_2)
-
-    s_2 = over_spread(g_2)
-    low_middle = gather_b(low_middle)
-    low_middle, dy_run = tie(low_middle, dy_run)
+    low_middle = gather_b(middle.astype(LOW))
+    low_middle, s_2, dy_run = tie(low_middle, s_2, dy_run)
 
     other_middle = swap_c(low_middle)
     dy_pair = gather_rows_b(dy_run)
-    other_middle, dy_pair, s_2 = tie(other_middle, dy_pair, s_2)
-
-    dy_all, dy_own = enter(spots, blocks, dy_pair, swap_c(dy_pair))
     w_1, w_2 = [g_1, *s_1], [g_2, *s_2]
     hidden_two, z_one, z_two, product, m_scale = gated_unit(spots, low_middle, other_middle, w_1, w_2)
-    f_down = scattered_all(whole_rows(dy_all, product))
-    z_one, z_two, product, w_d[0] = tie(z_one, z_two, product, w_d[0])
-
-
+    z_one, z_two, product, dy_pair = tie(z_one, z_two, product, dy_pair)
+
+    dy_all, dy_own = enter(spots, blocks, dy_pair, swap_c(dy_pair))
+    f_down = whole_rows(dy_all, product)
+    z_one, z_two, product, f_down, w_d[0] = tie(z_one, z_two, product, f_down, w_d[0])
+
+
+    f_down = scattered_all(f_down)
     d_one, d_two, lean_m = gated_unit_back(spots, dy_all, z_one, z_two, w_d)
     sent = fold_half(spots, [d_one, d_two], [w_1, w_2])
     sent, d_two, lean_m = tie(sent, d_two, lean_m)
@@ -788,14 +790,14 @@
     t_two = away(hidden_two, d_two)
     lean_m = total(lean_m[:, 0])
     sent, mine = fold_half(spots, [d_one, d_two], [w_1, w_2], arrived)
-    sent, d_one, t_two, product = tie(sent, d_one, t_two, product)
+    sent, d_one, t_two, product, lean_m = tie(sent, d_one, t_two, product, lean_m)
 
     crossed = swap_b(sent)
     cut = [(x[: x.shape[0] // 2], x[x.shape[0] // 2 :]) for x in t_two]
     upper = sent_a([x for x, _ in cut])
     f_one = whole_rows(hidden_two, d_one)
     result = fold_half(spots, [product], [w_d])
-    crossed, result, lean_m, f_one, upper = tie(crossed, result, lean_m, f_one, upper)
+    crossed, result, f_one, upper = tie(crossed, result, f_one, upper)
 
     f_one = scattered_all(f_one)
     d_hidden = mine + crossed.astype(F32)
@@ -818,93 +820,85 @@
     sent = columns(d_gated, (1 - b) * own, own).astype(LOW)
     mine = columns(d_gated, b * own, own)
     lower = [x for _, x in cut]
-    sent, mine, lower, r_result, t_out = tie(sent, mine, lower, r_result, t_out)
+    sent, mine, lower, r_result, t_out, lean_o = tie(sent, mine, lower, r_result, t_out, lean_o)
 
     crossed = swap_b(sent)
     lower = sent_a(lower)
     result, result_mine = fold_half(spots, [product], [w_d], r_result)
-    crossed, result, f_down, lean_o, lower, t_out = tie(crossed, result, f_down, lean_o, lower, t_out)
-
     r_two = [jnp.concatenate(pair, axis=0) for pair in zip(upper, lower)]
-    f_two = summed(hidden_two, d_two, r_two)
+    crossed, result, r_two, t_out, f_down = tie(crossed, result, r_two, t_out, f_down)
+
+    f_two = gradient_rows(spots, spread, 0, hidden_two, d_two, r_two)
     r_out = sent_a(t_out[1:])
     result = swap_b(result)
     y_down = spread_a(f_down)
+    o_normed = attended * o_scale
     d_gated = mine + crossed.astype(F32)
-    o_normed = attended * o_scale
     d_gate = (d_gated * o_normed).astype(LOW)
     lean = lean_o[:, None] / width
     d_attended = (o_scale * (d_gated * gate - o_normed * lean)).astype(LOW)
     d_query, d_key, d_value = attend_back(rates, ends, z_qk, z_vg, d_attended)
-    d_qk = jnp.concatenate([d_query, d_key], axis=1)
-    d_vg = jnp.concatenate([d_value, d_gate], axis=1)
+    d_qk = joined(d_query, d_key)
+    d_vg = joined(d_value, d_gate)
     t_qk = away(hidden_one, d_qk)
-    d_qk, d_vg, t_qk, r_out, y_down = tie(d_qk, d_vg, t_qk, r_out, y_down)
+    d_qk, d_vg, t_qk, f_two, r_out, result, y_down = tie(d_qk, d_vg, t_qk, f_two, r_out, result, y_down)
 
     r_qk = sent_a(t_qk)
+    f_two = scattered(f_two)
     f_out = scattered(sum([x.astype(F32) for x in r_out], t_out[0].astype(F32)).astype(LOW))
+    output = to_runs((middle + (result_mine + result.astype(F32))).astype(LOW))
     t_vg = away(hidden_one, d_vg)
     sent = fold_half(spots, [d_qk, d_vg], [w_qk, w_vg])
-    sent, t_vg, result, d_qk, d_vg = tie(sent, t_vg, result, d_qk, d_vg)
-
-    r_vg = sent_a(t_vg)
+    sent, t_vg, d_qk, d_vg = tie(sent, t_vg, d_qk, d_vg)
+
     arrived = swap_c(sent)
-    x_down = spread_b(y_down)
     lean_x = total(
         jnp.sum(z_qk * d_qk.astype(F32), axis=-1) + jnp.sum(z_vg * d_vg.astype(F32), axis=-1)
     )
     sent, mine = fold_half(spots, [d_qk, d_vg], [w_qk, w_vg], arrived)
-    output = (middle + (result_mine + result.astype(F32))).astype(LOW)
-    sent, mine, r_qk, d_qk, d_vg, f_one, x_down, output = tie(
-        sent, mine, r_qk, d_qk, d_vg, f_one, x_down, output
+    sent, mine, r_qk, t_vg, f_one, output, lean_x, y_down = tie(
+        sent, mine, r_qk, t_vg, f_one, output, lean_x, y_down
     )
 
     crossed = swap_b(sent)
-    f_qk = summed(hidden_one, d_qk, r_qk)
+    r_vg = sent_a(t_vg)
+    f_qk = scattered(gradient_rows(spots, spread, 0, hidden_one, d_qk, r_qk))
+    output = bring_back(output)
     x_one = spread_b(f_one)
-    output = to_runs(output)
-    crossed, d_vg, r_vg, x_one, f_two, lean_x, output = tie(
-        crossed, d_vg, r_vg, x_one, f_two, lean_x, output
-    )
-
-    vg_rows = gradient_rows(spots, spread, 0, hidden_one, d_vg, r_vg)
-    vg_rows, crossed, x_one, f_two, f_out, output = tie(
-        vg_rows, crossed, x_one, f_two, f_out, output
-    )
-
-    f_vg = scattered(vg_rows)
+    crossed, d_vg, r_vg, x_one, output, y_down = tie(crossed, d_vg, r_vg, x_one, output, y_down)
+
+    f_vg = gradient_rows(spots, spread, 0, hidden_one, d_vg, r_vg)
+    f_vg, crossed, x_one, f_two, f_out, y_down = tie(f_vg, crossed, x_one, f_two, f_out, y_down)
+
+    f_vg = scattered(f_vg)
     d_hidden = mine + crossed.astype(F32)
     x_normed = x_own.astype(F32) * x_scale
     lean = lean_x[:, None] / width
-    input_grad = (d_middle + x_scale * (d_hidden - x_normed * lean)).astype(LOW)
-    output = bring_back(output)
+    input_grad = to_runs((d_middle + x_scale * (d_hidden - x_normed * lean)).astype(LOW))
+    x_down = spread_b(y_down)
+    y_one = spread_a(x_one)
     x_two = spread_b(f_two)
-    y_one = spread_a(x_one)
-    y_out = spread_a(f_out)
-    input_grad = to_runs(input_grad)
-    y_qk = spread_a(f_qk)
-    output, input_grad, x_two, y_one, y_out, y_qk, f_vg = tie(
-        output, input_grad, x_two, y_one, y_out, y_qk, f_vg
-    )
+    y_oqk = spread_a(joined(f_out, f_qk))
+    input_grad, x_down, y_one, x_two, y_oqk, f_vg = tie(input_grad, x_down, y_one, x_two, y_oqk, f_vg)
 
     y_vg = spread_a(f_vg)
-    x_qk = spread_b(y_qk)
-    y_vg, x_qk = tie(y_vg, x_qk)
-
-    x_vg = spread_b(y_vg)
+    x_oqk = spread_b(y_oqk)
+    y_vg, x_oqk = tie(y_vg, x_oqk)
+
+    four_vg = spread_c(spread_b(y_vg))
     input_grad = bring_back(input_grad)
-    y_two = spread_a(x_two)
-    x_out = spread_b(y_out)
-    return (
-        output,
-        input_grad,
-        *place_quarters(spots, spread_c(x_qk), 2),
-        *place_quarters(spots, spread_c(x_vg), 2),
-        features_in_order(spread_c(x_out)),
-        *place_quarters(spots, spread_c(y_one), 1),
-        *place_quarters(spots, spread_c(y_two), 1),
-        *place_quarters(spots, spread_c(x_down), 1),
-    )
+    four_two = spread_c(spread_a(x_two))
+    four_one = spread_c(y_one)
+    four_down = spread_c(x_down)
+    four_oqk = spread_c(x_oqk)
+    units = f_one.shape[1]
+    g_query, g_key = place_quarters(spots, four_oqk, (own, own), (2 * own, own))
+    g_value, g_gate = place_quarters(spots, four_vg, (0, own), (own, own))
+    [g_one] = place_quarters(spots, four_one, (0, units))
+    [g_two] = place_quarters(spots, four_two, (0, units))
+    [g_down] = place_quarters(spots, four_down, (0, units))
+    g_out = features_in_order(four_oqk, 0, own)
+    return output, input_grad, g_query, g_key, g_value, g_gate, g_out, g_one, g_two, g_down
 
 
 def solution(mesh):

time: 1450 us -> 1350 us (0.931)
  waiting for transfers between devices: 730 us -> 669 us
    all_gather x5, waiting for transfers between devices: 34.3 us -> 1.75 us  [over_shards(): return lax.all_gather(piece, 'shard', axis=0, tiled=True)]
    ppermute x16 -> x8, waiting for transfers between devices: 299 us -> 277 us  [the longest x4 154 us: bring_back(): lax.ppermute(lax.dynamic_index_in_dim(slots, (batch_of(place) + p) % 2, 0...]
    ppermute x16 -> x8, starting transfers between devices: 40.2 us -> 20.5 us  [the longest x4 10.5 us: bring_back(): lax.ppermute(lax.dynamic_index_in_dim(slots, (batch_of(place) + p) % 2, 0...]
    unnamed x179 -> x181, local copies, waits for them, and re-layouts: 72.5 us -> 64.2 us
    ppermute x58 -> x55, waiting for transfers between devices: 396 us -> 389 us  [move(): return lax.ppermute(x, AXES, pairs)]
    ppermute x58 -> x55, starting transfers between devices: 47.8 us -> 54.5 us  [move(): return lax.ppermute(x, AXES, pairs)]
    select_n x20 -> x22, other arithmetic: 43.9 us -> 48.4 us  [ordered(): jnp.where(index == 0, jnp.concatenate([mine, other], axis), jnp.concatena...]
  transfers between devices with their start and end apart: 86 -> 75, of which waited for: 34 -> 31; matrix products, arithmetic and copies ran while one was open for 13% -> 13% of each run, Pallas kernels for 23% -> 25%
where the time goes in v5:
time: 1350 us; the launch traced here: 1340 us
  waiting for transfers between devices  669 us (50%)
  Pallas kernels  343 us (25%)
  other arithmetic  104 us (8%)
  local copies, waits for them, and re-layouts  95 us (7%)
  starting transfers between devices  76 us (6%)
  matrix products  33.2 us (2%)
  between operations  17 us (1%)
    ppermute x55, waiting for transfers between devices, move(): return lax.ppermute(x, AXES, pairs)  389 us
    ppermute x4, waiting for transfers between devices, bring_back(): lax.ppermute(lax.dynamic_index_in_dim(slots, (batch_of(place) + p) % 2, 0...  154 us
    ppermute x4, waiting for transfers between devices, bring(): lax.ppermute(lax.dynamic_index_in_dim(x, (place + p) % 2, 0, False), AXES...  123 us
    pallas_call x6, Pallas kernels, fold_half(): pl.pallas_call(functools.partial(fold_kernel, len(values), arrived is not...  98.3 us
    pallas_call x8, Pallas kernels, gradient_rows(): pl.pallas_call(gradient_kernel, out_shape=out, grid_spec=pltpu.PrefetchSc...  82.6 us
    unnamed x181, local copies, waits for them, and re-layouts  64.2 us
    ppermute x55, starting transfers between devices, move(): return lax.ppermute(x, AXES, pairs)  54.5 us
    select_n x22, other arithmetic, ordered(): jnp.where(index == 0, jnp.concatenate([mine, other], axis), jnp.concatena...  48.4 us
  transfers between devices with their start and end apart: 75, of which 31 were waited for; matrix products, arithmetic and copies ran while one was open for 13% of the time, Pallas kernels for 25%

profile of v5, /device:TPU:17, one launch (start us, length us, event | category | flops | bytes accessed | tf_op | source)
XLA Modules:
  0.0 1337.5 jit_solution(14062761076715693895)
XLA Ops:
  22.6 77.7 %collective-permute-done.2 = bf16[256,2048]{1,0:T(8,128)(2,1)S(1)} collective-permute-done((bf16[256,2048]{1,0:T(8,128)(2,1)}, bf16[256,2048]{1,0:T(8,128)(2,1)S(1)}, u32[]{:S(2)}, u32[]{:S(2)}) %collective-permute-start.2) | collective-permute-done | bytes 1048608 | tf_op jit(solution)/shard_map/ppermute | solution.py:596
  107.2 42.6 %collective-permute-done.4 = bf16[512,2048]{1,0:T(8,128)(2,1)} collective-permute-done((bf16[512,2048]{1,0:T(8,128)(2,1)}, bf16[512,2048]{1,0:T(8,128)(2,1)}, u32[]{:S(2)}, u32[]{:S(2)}) %collective-permute-start.4) | collective-permute-done | bytes 2097184 | tf_op jit(solution)/shard_map/ppermute | solution.py:545
  149.8 6.1 maximum_select_fusion.1.own_ref
  167.0 19.7 %enter.2 = (bf16[2048,2048]{1,0:T(8,128)(2,1)}, f32[2048,1024]{1,0:T(8,128)}, f32[2048,1]{1,0:T(8,128)S(1)}, bf16[2048,512]{1,0:T(8,128)(2,1)S(1)}) custom-call(s32[4]{0:T(128)S(1)} %pad_add_fusion.1.spots, bf16[1024,2048]{1,0:T(8,128)(2,1)S(1)} %copy-done.21, bf16[1024,2048]{1,0:T(8,128)(2,1)} %collective-permute-done.6.other_ref, ...), custom_call_target="tpu_custom_call" | custom-call | flops 8589934592 | bytes 31465472 | tf_op jit(solution)/shard_map/enter/pallas_call | solution.py:246
  188.0 16.7 %collective-permute-done.7.refs_1_.refs_5_.refs_6_ = bf16[1024,1024]{1,0:T(8,128)(2,1)} collective-permute-done((bf16[1024,1024]{1,0:T(8,128)(2,1)}, bf16[1024,1024]{1,0:T(8,128)(2,1)}, u32[]{:S(2)}, u32[]{:S(2)}) %collective-permute-start.7) | collective-permute-done | bytes 2097184 | tf_op jit(solution)/shard_map/ppermute | solution.py:545
  207.6 14.2 %project.1.zv_ref = f32[2048,1024]{1,0:T(8,128)S(1)} custom-call(s32[4]{0:T(128)S(1)} %pad_add_fusion.1.spots, bf16[2048,2048]{1,0:T(8,128)(2,1)} %get-tuple-element.143.h_ref.left_ref, bf16[1024,1024]{1,0:T(8,128)(2,1)S(1)} %copy-done.43, bf16[1024,1024]{1,0:T(8,128)(2,1)} %collective-permute-done.7.refs_1_.refs_5_.refs_6_), custom_call_target="tpu_custom_call" | custom-call | flops 8589934592 | bytes 20971520 | tf_op jit(solution)/shard_map/project/pallas_call | solution.py:277
  225.2 12.3 attend.1
  246.6 42.0 %collective-permute-done.12 = f32[2048]{0:T(1024)S(1)} collective-permute-done((f32[2048]{0:T(1024)S(1)}, f32[2048]{0:T(1024)S(1)}, u32[]{:S(2)}, u32[]{:S(2)}) %collective-permute-start.12) | collective-permute-done | bytes 8224 | tf_op jit(solution)/shard_map/ppermute | solution.py:545
  293.0 12.4 collective-permute-done.10.refs_1_.refs_3_.refs_4_
  314.8 12.0 fusion.21
  332.3 44.9 %collective-permute-done.16 = bf16[256,2048]{1,0:T(8,128)(2,1)S(1)} collective-permute-done((bf16[256,2048]{1,0:T(8,128)(2,1)S(1)}, bf16[256,2048]{1,0:T(8,128)(2,1)S(1)}, u32[]{:S(2)}, u32[]{:S(2)}) %collective-permute-start.16) | collective-permute-done | bytes 1048608 | tf_op jit(solution)/shard_map/ppermute | solution.py:596
  378.2 17.9 %collective-permute-done.14 = bf16[2048,512]{1,0:T(8,128)(2,1)S(1)} collective-permute-done((bf16[2048,512]{1,0:T(8,128)(2,1)S(1)}, bf16[2048,512]{1,0:T(8,128)(2,1)S(1)}, u32[]{:S(2)}, u32[]{:S(2)}) %collective-permute-start.14) | collective-permute-done | bytes 2097184 | tf_op jit(solution)/shard_map/ppermute | solution.py:545
  405.5 46.4 %collective-permute-done.19 = bf16[512,2048]{1,0:T(8,128)(2,1)S(1)} collective-permute-done((bf16[512,2048]{1,0:T(8,128)(2,1)S(1)}, bf16[512,2048]{1,0:T(8,128)(2,1)S(1)}, u32[]{:S(2)}, u32[]{:S(2)}) %collective-permute-start.19) | collective-permute-done | bytes 2097184 | tf_op jit(solution)/shard_map/ppermute | solution.py:545
  454.5 38.0 %gated_unit.1 = (bf16[2048,2048]{1,0:T(8,128)(2,1)}, bf16[2048,1408]{1,0:T(8,128)(2,1)}, bf16[2048,1408]{1,0:T(8,128)(2,1)}, bf16[2048,1408]{1,0:T(8,128)(2,1)}, f32[2048,1]{1,0:T(8,128)S(1)}) custom-call(s32[4]{0:T(128)S(1)} %pad_add_fusion.1.spots, bf16[2048,1024]{1,0:T(8,128)(2,1)} %maximum_select_fusion.3.own_ref, ...), custom_call_target="tpu_custom_call" | custom-call | flops 23622320128 | bytes 45621248 | tf_op jit(solution)/shard_map/gated_unit/pallas_call | solution.py:339
  494.2 6.8 collective-permute-done.20.other_ref
  507.6 16.4 %gradient_rows.8 = bf16[2048,1408]{1,0:T(8,128)(2,1)S(1)} custom-call(s32[4]{0:T(128)S(1)} %pad_add_fusion.1.spots, bf16[2048,2048]{1,0:T(8,128)(2,1)} %get-tuple-element.165.left_ref.dy_ref, bf16[2048,1408]{1,0:T(8,128)(2,1)S(1)} %copy-done.50), custom_call_target="tpu_custom_call" | custom-call | flops 11811160064 | bytes 17301504 | tf_op jit(solution)/shard_map/gradient_rows/pallas_call | solution.py:472
  526.6 22.4 %gated_unit_back.1 = (bf16[2048,1408]{1,0:T(8,128)(2,1)S(1)}, bf16[2048,1408]{1,0:T(8,128)(2,1)S(1)}, f32[2048,1]{1,0:T(8,128)S(1)}) custom-call(s32[4]{0:T(128)S(1)} %pad_add_fusion.1.spots, bf16[2048,2048]{1,0:T(8,128)(2,1)} %get-tuple-element.165.left_ref.dy_ref, bf16[2048,1408]{1,0:T(8,128)(2,1)} %get-tuple-element.169.one_ref, ...), custom_call_target="tpu_custom_call" | custom-call | flops 11811160064 | bytes 37232640 | tf_op jit(solution)/shard_map/gated_unit_back/pallas_call | solution.py:376
  555.1 20.0 %fold_half.6 = bf16[2048,1024]{1,0:T(8,128)(2,1)} custom-call(s32[4]{0:T(128)S(1)} %pad_add_fusion.1.spots, bf16[2048,1408]{1,0:T(8,128)(2,1)} %copy-done.52, bf16[2048,1408]{1,0:T(8,128)(2,1)} %copy-done.48, bf16[1024,1408]{1,0:T(8,128)(2,1)S(1)} %copy-done.32, bf16[1024,1408]{1,0:T(8,128)(2,1)} %collective-permute-done.10.refs_1_.refs_3_.refs_4_, ...), custom_call_target="tpu_custom_call" | custom-call | flops 11811160064 | bytes 21495808 | tf_op jit(solution)/shard_map/fold_half/pallas_call | solution.py:437
  587.4 9.4 gradient_rows.9
  596.9 21.8 %fold_half.7 = (bf16[2048,512]{1,0:T(8,128)(2,1)S(1)}, f32[2048,512]{1,0:T(8,128)}) custom-call(s32[4]{0:T(128)S(1)} %pad_add_fusion.1.spots, bf16[2048,1408]{1,0:T(8,128)(2,1)} %copy-done.52, bf16[2048,1408]{1,0:T(8,128)(2,1)} %copy-done.48, bf16[2048,1024]{1,0:T(8,128)(2,1)} %collective-permute-done.21.refs_2_, bf16[1024,1408]{1,0:T(8,128)(2,1)S(1)} %copy-done.33, ...), custom_call_target="tpu_custom_call" | custom-call | flops 11811160064 | bytes 27787264 | tf_op jit(solution)/shard_map/fold_half/pallas_call | solution.py:437
  623.6 10.6 fold_half.8
  638.9 16.4 %gradient_rows.10 = bf16[2048,1408]{1,0:T(8,128)(2,1)S(1)} custom-call(s32[4]{0:T(128)S(1)} %pad_add_fusion.1.spots, bf16[2048,2048]{1,0:T(8,128)(2,1)} %get-tuple-element.179.left_ref, bf16[2048,1408]{1,0:T(8,128)(2,1)S(1)} %copy-done.53), custom_call_target="tpu_custom_call" | custom-call | flops 11811160064 | bytes 17301504 | tf_op jit(solution)/shard_map/gradient_rows/pallas_call | solution.py:472
  657.8 8.0 collective-permute-done.24
  665.7 6.6 multiply_reduce_fusion.2
  677.6 12.0 convolution_convert_fusion.1
  702.6 14.0 %fold_half.9 = (bf16[2048,512]{1,0:T(8,128)(2,1)}, f32[2048,512]{1,0:T(8,128)S(1)}) custom-call(s32[4]{0:T(128)S(1)} %pad_add_fusion.1.spots, bf16[2048,1408]{1,0:T(8,128)(2,1)} %get-tuple-element.183.right_ref.refs_0_, bf16[2048,1024]{1,0:T(8,128)(2,1)} %collective-permute-done.27.refs_1_, ...), custom_call_target="tpu_custom_call" | custom-call | flops 5905580032 | bytes 16252928 | tf_op jit(solution)/shard_map/fold_half/pallas_call | solution.py:437
  718.6 33.0 %collective-permute-done.31 = bf16[512,1408]{1,0:T(8,128)(2,1)S(1)} collective-permute-done((bf16[512,1408]{1,0:T(8,128)(2,1)S(1)}, bf16[512,1408]{1,0:T(8,128)(2,1)S(1)}, u32[]{:S(2)}, u32[]{:S(2)}) %collective-permute-start.31) | collective-permute-done | bytes 1441824 | tf_op jit(solution)/shard_map/ppermute | solution.py:545
  757.1 6.1 multiply_convert_fusion
  763.2 21.3 %attend_back.1 = (bf16[2048,512]{1,0:T(8,128)(2,1)S(1)}, bf16[2048,512]{1,0:T(8,128)(2,1)S(1)}, bf16[2048,512]{1,0:T(8,128)(2,1)S(1)}) custom-call(f32[4]{0:T(128)S(1)} %dynamic_slice.118.rates, s32[2,2]{1,0:T(2,128)S(1)} %pad_add_fusion.ends, f32[2048,1024]{1,0:T(8,128)} %get-tuple-element.142.zq_ref.zk_ref, f32[2048,1024]{1,0:T(8,128)} %get-tuple-element.142.zq_ref.zk_ref, ...), custom_call_target="tpu_custom_call" | custom-call | flops 10737418240 | bytes 20971520 | tf_op jit(solution)/shard_map/attend_back/pallas_call | solution.py:119
  785.2 9.8 gradient_rows.11
  797.8 9.3 gradient_rows.12
  816.9 15.0 %fold_half.10 = bf16[2048,1024]{1,0:T(8,128)(2,1)} custom-call(s32[4]{0:T(128)S(1)} %pad_add_fusion.1.spots, bf16[2048,1024]{1,0:T(8,128)(2,1)} %copy-done.8, bf16[2048,1024]{1,0:T(8,128)(2,1)} %pad_maximum_fusion.refs_1_.right_ref, bf16[1024,1024]{1,0:T(8,128)(2,1)S(1)} %copy-done.41, bf16[1024,1024]{1,0:T(8,128)(2,1)} %collective-permute-done.5.refs_1_.refs_3_.refs_4_, ...), custom_call_target="tpu_custom_call" | custom-call | flops 8589934592 | bytes 16777216 | tf_op jit(solution)/shard_map/fold_half/pallas_call | solution.py:437
  831.9 6.9 gradient_rows.13
  851.3 23.7 %collective-permute-done.37 = bf16[2,512,512]{2,1,0:T(8,128)(2,1)S(1)} collective-permute-done((bf16[2,512,512]{2,1,0:T(8,128)(2,1)S(1)}, bf16[2,512,512]{2,1,0:T(8,128)(2,1)S(1)}, u32[]{:S(2)}, u32[]{:S(2)}) %collective-permute-start.37) | collective-permute-done | bytes 1048608 | tf_op jit(solution)/shard_map/ppermute | solution.py:545
  897.3 17.1 %fold_half.11 = (bf16[2048,512]{1,0:T(8,128)(2,1)S(1)}, f32[2048,512]{1,0:T(8,128)}) custom-call(s32[4]{0:T(128)S(1)} %pad_add_fusion.1.spots, bf16[2048,1024]{1,0:T(8,128)(2,1)} %copy-done.8, bf16[2048,1024]{1,0:T(8,128)(2,1)} %pad_maximum_fusion.refs_1_.right_ref, bf16[2048,1024]{1,0:T(8,128)(2,1)} %collective-permute-done.35.refs_2_, ...), custom_call_target="tpu_custom_call" | custom-call | flops 8589934592 | bytes 23068672 | tf_op jit(solution)/shard_map/fold_half/pallas_call | solution.py:437
  920.8 6.9 gradient_rows.15
  951.0 87.2 %collective-permute-done.44 = bf16[256,2048]{1,0:T(8,128)(2,1)} collective-permute-done((bf16[256,2048]{1,0:T(8,128)(2,1)}, bf16[256,2048]{1,0:T(8,128)(2,1)}, u32[]{:S(2)}, u32[]{:S(2)}) %collective-permute-start.44) | collective-permute-done | bytes 1048608 | tf_op jit(solution)/shard_map/ppermute | solution.py:604
  1038.2 20.6 %collective-permute-done.45 = bf16[256,2048]{1,0:T(8,128)(2,1)} collective-permute-done((bf16[256,2048]{1,0:T(8,128)(2,1)}, bf16[256,2048]{1,0:T(8,128)(2,1)}, u32[]{:S(2)}, u32[]{:S(2)}) %collective-permute-start.45) | collective-permute-done | bytes 1048608 | tf_op jit(solution)/shard_map/ppermute | solution.py:604
  1062.7 7.4 gradient_rows.14
  1081.4 21.0 %collective-permute-done.46 = bf16[2,512,512]{2,1,0:T(8,128)(2,1)S(1)} collective-permute-done((bf16[2,512,512]{2,1,0:T(8,128)(2,1)S(1)}, bf16[2,512,512]{2,1,0:T(8,128)(2,1)S(1)}, u32[]{:S(2)}, u32[]{:S(2)}) %collective-permute-start.46) | collective-permute-done | bytes 1048608 | tf_op jit(solution)/shard_map/ppermute | solution.py:545
  1106.2 42.5 %collective-permute-done.50 = bf16[256,1408]{1,0:T(8,128)(2,1)S(1)} collective-permute-done((bf16[256,1408]{1,0:T(8,128)(2,1)S(1)}, bf16[256,1408]{1,0:T(8,128)(2,1)S(1)}, u32[]{:S(2)}, u32[]{:S(2)}) %collective-permute-start.50) | collective-permute-done | bytes 720928 | tf_op jit(solution)/shard_map/ppermute | solution.py:545
  1163.9 5.8 collective-permute-done.51
  1190.4 29.5 %collective-permute-done.55 = bf16[512,1536]{1,0:T(8,128)(2,1)S(1)} collective-permute-done((bf16[512,1536]{1,0:T(8,128)(2,1)}, bf16[512,1536]{1,0:T(8,128)(2,1)S(1)}, u32[]{:S(2)}, u32[]{:S(2)}) %collective-permute-start.55) | collective-permute-done | bytes 1572896 | tf_op jit(solution)/shard_map/ppermute | solution.py:545
  1225.0 24.1 %collective-permute-done.52 = bf16[256,2048]{1,0:T(8,128)(2,1)S(1)} collective-permute-done((bf16[256,2048]{1,0:T(8,128)(2,1)S(1)}, bf16[256,2048]{1,0:T(8,128)(2,1)S(1)}, u32[]{:S(2)}, u32[]{:S(2)}) %collective-permute-start.52) | collective-permute-done | bytes 1048608 | tf_op jit(solution)/shard_map/ppermute | solution.py:604
  1249.1 22.3 %collective-permute-done.53 = bf16[256,2048]{1,0:T(8,128)(2,1)S(1)} collective-permute-done((bf16[256,2048]{1,0:T(8,128)(2,1)S(1)}, bf16[256,2048]{1,0:T(8,128)(2,1)S(1)}, u32[]{:S(2)}, u32[]{:S(2)}) %collective-permute-start.53) | collective-permute-done | bytes 1048608 | tf_op jit(solution)/shard_map/ppermute | solution.py:604
  1273.2 21.0 %collective-permute-done.57 = bf16[512,1024]{1,0:T(8,128)(2,1)S(1)} collective-permute-done((bf16[512,1024]{1,0:T(8,128)(2,1)S(1)}, bf16[512,1024]{1,0:T(8,128)(2,1)S(1)}, u32[]{:S(2)}, u32[]{:S(2)}) %collective-permute-start.57) | collective-permute-done | bytes 1048608 | tf_op jit(solution)/shard_map/ppermute | solution.py:545
  1308.4 7.1 place_quarters.8
  1324.4 5.8 place_quarters.6
  (420 shorter events, 309.7 us)
Async XLA Ops:
  8.0 94.6 %all-gather.7.cloned.1.call-start = ((), (), s32[]{:S(2)}) async-start(), calls=%async_computation.6 | async-start | bytes 2621440 | tf_op jit(solution)/shard_map/all_gather | solution.py:656
  11.6 144.3 %all-gather.9.cloned.1.call-start = ((), (), s32[]{:S(2)}) async-start(), calls=%async_computation.7 | async-start | bytes 2621440 | tf_op jit(solution)/shard_map/all_gather | solution.py:656
  14.8 173.2 %all-gather.11.cloned.1.call-start = ((), (), s32[]{:S(2)}) async-start(), calls=%async_computation.8 | async-start | bytes 1310720 | tf_op jit(solution)/shard_map/all_gather | solution.py:656
  16.0 84.3 %collective-permute-start.2 = (bf16[256,2048]{1,0:T(8,128)(2,1)}, bf16[256,2048]{1,0:T(8,128)(2,1)S(1)}, u32[]{:S(2)}, u32[]{:S(2)}) collective-permute-start(bf16[256,2048]{1,0:T(8,128)(2,1)} %get-tuple-element.290), channel_id=1, source_target_pairs={{0,0},{4,1},{1,2},{5,3},{8,4},{12,5},{9,6},{13,7},{2,8},{6,9},{3,1... | collective-permute-start | bytes 3145736 | tf_op jit(solution)/shard_map/ppermute | solution.py:596
  19.6 80.7 %collective-permute-start.3 = (bf16[256,2048]{1,0:T(8,128)(2,1)S(1)}, bf16[256,2048]{1,0:T(8,128)(2,1)S(1)}, u32[]{:S(2)}, u32[]{:S(2)}) collective-permute-start(bf16[256,2048]{1,0:T(8,128)(2,1)S(1)} %get-tuple-element.291), channel_id=1, source_target_pairs={{1,0},{5,1},{0,2},{4,3},{9,4},{13,5},{8,6},{12,7},{3,8},{7,9},{2,1... | collective-permute-start | bytes 3145736 | tf_op jit(solution)/shard_map/ppermute | solution.py:596
  102.6 47.2 %collective-permute-start.4 = (bf16[512,2048]{1,0:T(8,128)(2,1)}, bf16[512,2048]{1,0:T(8,128)(2,1)}, u32[]{:S(2)}, u32[]{:S(2)}) collective-permute-start(bf16[512,2048]{1,0:T(8,128)(2,1)} %maximum_select_fusion.7), channel_id=1, source_target_pairs={{0,8},{1,9},{2,10},{3,11},{4,12},{5,13},{6,14},{7,15},{8,0},{9,1},... | collective-permute-start | bytes 6291464 | tf_op jit(solution)/shard_map/ppermute | solution.py:545
  103.4 139.0 %all-gather.13.cloned.1.call-start = ((), (), s32[]{:S(2)}) async-start(), calls=%async_computation.9 | async-start | bytes 3604480 | tf_op jit(solution)/shard_map/all_gather | solution.py:656
  103.4 52.5 %collective-permute-start.5 = (bf16[1024,1024]{1,0:T(8,128)(2,1)}, bf16[1024,1024]{1,0:T(8,128)(2,1)}, u32[]{:S(2)}, u32[]{:S(2)}) collective-permute-start(bf16[1024,1024]{1,0:T(8,128)(2,1)} %all-gather.7.cloned.1.call-done.refs_0_.refs_2_.refs_3_), channel_id=1, source_target_pairs={{0,16},{1,17},{2,18},{3,19},{4,20},{5,21},{6,22},{7,23},{8,24},{9,... | collective-permute-start | bytes 6291464 | tf_op jit(solution)/shard_map/ppermute | solution.py:545
  107.1 185.9 %all-gather.15.cloned.1.call-start = ((), (), s32[]{:S(2)}) async-start(), calls=%async_computation.10 | async-start | bytes 3604480 | tf_op jit(solution)/shard_map/all_gather | solution.py:656
  157.2 47.5 %collective-permute-start.7 = (bf16[1024,1024]{1,0:T(8,128)(2,1)}, bf16[1024,1024]{1,0:T(8,128)(2,1)}, u32[]{:S(2)}, u32[]{:S(2)}) collective-permute-start(bf16[1024,1024]{1,0:T(8,128)(2,1)} %all-gather.9.cloned.1.call-done.refs_0_.refs_4_.refs_5_), channel_id=1, source_target_pairs={{0,16},{1,17},{2,18},{3,19},{4,20},{5,21},{6,22},{7,23},{8,24},{9,... | collective-permute-start | bytes 6291464 | tf_op jit(solution)/shard_map/ppermute | solution.py:545
  162.1 364.4 %all-gather.17.cloned.1.call-start = ((), (), s32[]{:S(2)}) async-start(), calls=%async_computation.11 | async-start | bytes 6488064 | tf_op jit(solution)/shard_map/all_gather | solution.py:660
  242.4 63.1 %collective-permute-start.10 = (bf16[1024,1408]{1,0:T(8,128)(2,1)}, bf16[1024,1408]{1,0:T(8,128)(2,1)}, u32[]{:S(2)}, u32[]{:S(2)}) collective-permute-start(bf16[1024,1408]{1,0:T(8,128)(2,1)} %all-gather.13.cloned.1.call-done.refs_0_.refs_2_.refs_3_), channel_id=1, source_target_pairs={{0,16},{1,17},{2,18},{3,19},{4,20},{5,21},{6,22},{7,23},{8,24},{9,... | collective-permute-start | bytes 8650760 | tf_op jit(solution)/shard_map/ppermute | solution.py:545
  242.6 46.0 %collective-permute-start.9 = (bf16[2048,512]{1,0:T(8,128)(2,1)S(1)}, bf16[2048,512]{1,0:T(8,128)(2,1)S(1)}, u32[]{:S(2)}, u32[]{:S(2)}) collective-permute-start(bf16[2048,512]{1,0:T(8,128)(2,1)S(1)} %get-tuple-element.146), channel_id=1, source_target_pairs={{0,8},{1,9},{2,10},{3,11},{4,12},{5,13},{6,14},{7,15},{8,0},{9,1},... | collective-permute-start | bytes 6291464 | tf_op jit(solution)/shard_map/ppermute | solution.py:545
  310.8 88.0 %collective-permute-start.15 = (bf16[1024,1408]{1,0:T(8,128)(2,1)S(1)}, bf16[1024,1408]{1,0:T(8,128)(2,1)S(1)}, u32[]{:S(2)}, u32[]{:S(2)}) collective-permute-start(bf16[1024,1408]{1,0:T(8,128)(2,1)S(1)} %copy-done.34), channel_id=1, source_target_pairs={{0,16},{1,17},{2,18},{3,19},{4,20},{5,21},{6,22},{7,23},{8,24},{9,... | collective-permute-start | bytes 8650760 | tf_op jit(solution)/shard_map/ppermute | solution.py:545
  326.8 69.3 %collective-permute-start.14 = (bf16[2048,512]{1,0:T(8,128)(2,1)S(1)}, bf16[2048,512]{1,0:T(8,128)(2,1)S(1)}, u32[]{:S(2)}, u32[]{:S(2)}) collective-permute-start(bf16[2048,512]{1,0:T(8,128)(2,1)S(1)} %get-tuple-element.294), channel_id=1, source_target_pairs={{0,8},{1,9},{2,10},{3,11},{4,12},{5,13},{6,14},{7,15},{8,0},{9,1},... | collective-permute-start | bytes 6291464 | tf_op jit(solution)/shard_map/ppermute | solution.py:545
  327.1 50.1 %collective-permute-start.16 = (bf16[256,2048]{1,0:T(8,128)(2,1)S(1)}, bf16[256,2048]{1,0:T(8,128)(2,1)S(1)}, u32[]{:S(2)}, u32[]{:S(2)}) collective-permute-start(bf16[256,2048]{1,0:T(8,128)(2,1)S(1)} %get-tuple-element.286), channel_id=1, source_target_pairs={{0,0},{4,1},{1,2},{5,3},{8,4},{12,5},{9,6},{13,7},{2,8},{6,9},{3,1... | collective-permute-start | bytes 3145736 | tf_op jit(solution)/shard_map/ppermute | solution.py:596
  330.4 46.8 %collective-permute-start.17 = (bf16[256,2048]{1,0:T(8,128)(2,1)S(1)}, bf16[256,2048]{1,0:T(8,128)(2,1)S(1)}, u32[]{:S(2)}, u32[]{:S(2)}) collective-permute-start(bf16[256,2048]{1,0:T(8,128)(2,1)S(1)} %get-tuple-element.287), channel_id=1, source_target_pairs={{1,0},{5,1},{0,2},{4,3},{9,4},{13,5},{8,6},{12,7},{3,8},{7,9},{2,1... | collective-permute-start | bytes 3145736 | tf_op jit(solution)/shard_map/ppermute | solution.py:596
  400.3 54.2 %collective-permute-start.18 = (bf16[2048,1024]{1,0:T(8,128)(2,1)}, bf16[2048,1024]{1,0:T(8,128)(2,1)}, u32[]{:S(2)}, u32[]{:S(2)}) collective-permute-start(bf16[2048,1024]{1,0:T(8,128)(2,1)} %maximum_select_fusion.3.own_ref), channel_id=1, source_target_pairs={{0,4},{1,5},{2,6},{3,7},{4,0},{5,1},{6,2},{7,3},{8,12},{9,13},{10,... | collective-permute-start | bytes 12582920 | tf_op jit(solution)/shard_map/ppermute | solution.py:545
  404.0 350.8 %reduce-scatter.7.cloned.1.call-start = ((), (), s32[]{:S(2)}) async-start(), calls=%async_computation.12 | async-start | bytes 6488064 | tf_op jit(solution)/shard_map/reduce_scatter | solution.py:693
  404.4 47.4 %collective-permute-start.19 = (bf16[512,2048]{1,0:T(8,128)(2,1)S(1)}, bf16[512,2048]{1,0:T(8,128)(2,1)S(1)}, u32[]{:S(2)}, u32[]{:S(2)}) collective-permute-start(bf16[512,2048]{1,0:T(8,128)(2,1)S(1)} %maximum_select_fusion.9), channel_id=1, source_target_pairs={{0,8},{1,9},{2,10},{3,11},{4,12},{5,13},{6,14},{7,15},{8,0},{9,1},... | collective-permute-start | bytes 6291464 | tf_op jit(solution)/shard_map/ppermute | solution.py:545
  526.6 390.5 %reduce-scatter.9.cloned.1.call-start = ((), (), s32[]{:S(2)}) async-start(), calls=%async_computation.13 | async-start | bytes 6488064 | tf_op jit(solution)/shard_map/reduce_scatter | solution.py:693
  618.7 47.0 %collective-permute-start.24 = (bf16[2048,512]{1,0:T(8,128)(2,1)S(1)}, bf16[2048,512]{1,0:T(8,128)(2,1)}, u32[]{:S(2)}, u32[]{:S(2)}) collective-permute-start(bf16[2048,512]{1,0:T(8,128)(2,1)S(1)} %get-tuple-element.182), channel_id=1, source_target_pairs={{0,8},{1,9},{2,10},{3,11},{4,12},{5,13},{6,14},{7,15},{8,0},{9,1},... | collective-permute-start | bytes 6291464 | tf_op jit(solution)/shard_map/ppermute | solution.py:545
  677.0 394.5 %reduce-scatter.13.cloned.1.call-start = ((), (), s32[]{:S(2)}) async-start(), calls=%async_computation.15 | async-start | bytes 1310720 | tf_op jit(solution)/shard_map/reduce_scatter | solution.py:687
  702.1 52.7 %collective-permute-start.30 = (bf16[2048,512]{1,0:T(8,128)(2,1)}, bf16[2048,512]{1,0:T(8,128)(2,1)}, u32[]{:S(2)}, u32[]{:S(2)}) collective-permute-start(bf16[2048,512]{1,0:T(8,128)(2,1)} %dynamic-slice_convert_fusion), channel_id=1, source_target_pairs={{0,8},{1,9},{2,10},{3,11},{4,12},{5,13},{6,14},{7,15},{8,0},{9,1},... | collective-permute-start | bytes 6291464 | tf_op jit(solution)/shard_map/ppermute | solution.py:545
  702.6 49.0 %collective-permute-start.31 = (bf16[512,1408]{1,0:T(8,128)(2,1)S(1)}, bf16[512,1408]{1,0:T(8,128)(2,1)S(1)}, u32[]{:S(2)}, u32[]{:S(2)}) collective-permute-start(bf16[512,1408]{1,0:T(8,128)(2,1)S(1)} %copy-done.64), channel_id=1, source_target_pairs={{0,16},{1,17},{2,18},{3,19},{4,20},{5,21},{6,22},{7,23},{8,24},{9,... | collective-permute-start | bytes 4325384 | tf_op jit(solution)/shard_map/ppermute | solution.py:545
  754.8 53.9 %collective-permute-start.34 = (bf16[256,1408]{1,0:T(8,128)(2,1)}, bf16[256,1408]{1,0:T(8,128)(2,1)}, u32[]{:S(2)}, u32[]{:S(2)}) collective-permute-start(bf16[256,1408]{1,0:T(8,128)(2,1)} %reduce-scatter.7.cloned.1.call-done), channel_id=1, source_target_pairs={{0,16},{1,17},{2,18},{3,19},{4,20},{5,21},{6,22},{7,23},{8,24},{9,... | collective-permute-start | bytes 2162696 | tf_op jit(solution)/shard_map/ppermute | solution.py:545
  754.8 56.7 %collective-permute-start.32 = (bf16[1024,512]{1,0:T(8,128)(2,1)}, bf16[1024,512]{1,0:T(8,128)(2,1)}, u32[]{:S(2)}, u32[]{:S(2)}) collective-permute-start(bf16[1024,512]{1,0:T(8,128)(2,1)} %get-tuple-element.208), channel_id=1, source_target_pairs={{0,16},{1,17},{2,18},{3,19},{4,20},{5,21},{6,22},{7,23},{8,24},{9,... | collective-permute-start | bytes 3145736 | tf_op jit(solution)/shard_map/ppermute | solution.py:545
  756.3 55.3 %collective-permute-start.33 = (bf16[2048,512]{1,0:T(8,128)(2,1)}, bf16[2048,512]{1,0:T(8,128)(2,1)}, u32[]{:S(2)}, u32[]{:S(2)}) collective-permute-start(bf16[2048,512]{1,0:T(8,128)(2,1)} %get-tuple-element.209), channel_id=1, source_target_pairs={{0,8},{1,9},{2,10},{3,11},{4,12},{5,13},{6,14},{7,15},{8,0},{9,1},... | collective-permute-start | bytes 6291464 | tf_op jit(solution)/shard_map/ppermute | solution.py:545
  814.5 256.9 %reduce-scatter.11.cloned.1.call-start = ((), (), s32[]{:S(2)}) async-start(), calls=%async_computation.14 | async-start | bytes 3604480 | tf_op jit(solution)/shard_map/reduce_scatter | solution.py:687
  815.3 334.6 %reduce-scatter.15.cloned.1.call-start = ((), (), s32[]{:S(2)}) async-start(), calls=%async_computation.16 | async-start | bytes 2621440 | tf_op jit(solution)/shard_map/reduce_scatter | solution.py:687
  838.9 58.4 %collective-permute-start.35 = (bf16[2048,1024]{1,0:T(8,128)(2,1)}, bf16[2048,1024]{1,0:T(8,128)(2,1)}, u32[]{:S(2)}, u32[]{:S(2)}) collective-permute-start(bf16[2048,1024]{1,0:T(8,128)(2,1)} %fold_half.10), channel_id=1, source_target_pairs={{0,4},{1,5},{2,6},{3,7},{4,0},{5,1},{6,2},{7,3},{8,12},{9,13},{10,... | collective-permute-start | bytes 12582920 | tf_op jit(solution)/shard_map/ppermute | solution.py:545
  851.3 64.4 %collective-permute-start.36 = (bf16[1024,1024]{1,0:T(8,128)(2,1)}, bf16[1024,1024]{1,0:T(8,128)(2,1)S(1)}, u32[]{:S(2)}, u32[]{:S(2)}) collective-permute-start(bf16[1024,1024]{1,0:T(8,128)(2,1)} %gradient_rows.11), channel_id=1, source_target_pairs={{0,16},{1,17},{2,18},{3,19},{4,20},{5,21},{6,22},{7,23},{8,24},{9,... | collective-permute-start | bytes 6291464 | tf_op jit(solution)/shard_map/ppermute | solution.py:545
  929.1 243.6 %reduce-scatter.17.cloned.1.call-start = ((), (), s32[]{:S(2)}) async-start(), calls=%async_computation.17 | async-start | bytes 2621440 | tf_op jit(solution)/shard_map/reduce_scatter | solution.py:687
  929.7 133.0 %collective-permute-start.41 = (bf16[2048,512]{1,0:T(8,128)(2,1)}, bf16[2048,512]{1,0:T(8,128)(2,1)}, u32[]{:S(2)}, u32[]{:S(2)}) collective-permute-start(bf16[2048,512]{1,0:T(8,128)(2,1)} %copy-done.47), channel_id=1, source_target_pairs={{0,8},{1,9},{2,10},{3,11},{4,12},{5,13},{6,14},{7,15},{8,0},{9,1},... | collective-permute-start | bytes 6291464 | tf_op jit(solution)/shard_map/ppermute | solution.py:545
  930.7 132.0 %collective-permute-start.42 = (bf16[1024,1024]{1,0:T(8,128)(2,1)}, bf16[1024,1024]{1,0:T(8,128)(2,1)S(1)}, u32[]{:S(2)}, u32[]{:S(2)}) collective-permute-start(bf16[1024,1024]{1,0:T(8,128)(2,1)} %copy-done.46), channel_id=1, source_target_pairs={{0,16},{1,17},{2,18},{3,19},{4,20},{5,21},{6,22},{7,23},{8,24},{9,... | collective-permute-start | bytes 6291464 | tf_op jit(solution)/shard_map/ppermute | solution.py:545
  940.1 98.1 %collective-permute-start.44 = (bf16[256,2048]{1,0:T(8,128)(2,1)}, bf16[256,2048]{1,0:T(8,128)(2,1)}, u32[]{:S(2)}, u32[]{:S(2)}) collective-permute-start(bf16[256,2048]{1,0:T(8,128)(2,1)} %get-tuple-element.278), channel_id=1, source_target_pairs={{0,0},{1,4},{2,1},{3,5},{4,8},{5,12},{6,9},{7,13},{8,2},{9,6},{10,... | collective-permute-start | bytes 3145736 | tf_op jit(solution)/shard_map/ppermute | solution.py:604
  942.1 116.8 %collective-permute-start.45 = (bf16[256,2048]{1,0:T(8,128)(2,1)}, bf16[256,2048]{1,0:T(8,128)(2,1)}, u32[]{:S(2)}, u32[]{:S(2)}) collective-permute-start(bf16[256,2048]{1,0:T(8,128)(2,1)} %get-tuple-element.279), channel_id=1, source_target_pairs={{0,1},{1,5},{2,0},{3,4},{4,9},{5,13},{6,8},{7,12},{8,3},{9,7},{10,... | collective-permute-start | bytes 3145736 | tf_op jit(solution)/shard_map/ppermute | solution.py:604
  1078.0 74.9 %collective-permute-start.48 = (bf16[512,1408]{1,0:T(8,128)(2,1)}, bf16[512,1408]{1,0:T(8,128)(2,1)}, u32[]{:S(2)}, u32[]{:S(2)}) collective-permute-start(bf16[512,1408]{1,0:T(8,128)(2,1)} %maximum_select_fusion.18), channel_id=1, source_target_pairs={{0,8},{1,9},{2,10},{3,11},{4,12},{5,13},{6,14},{7,15},{8,0},{9,1},... | collective-permute-start | bytes 4325384 | tf_op jit(solution)/shard_map/ppermute | solution.py:545
  1079.4 69.2 %collective-permute-start.50 = (bf16[256,1408]{1,0:T(8,128)(2,1)S(1)}, bf16[256,1408]{1,0:T(8,128)(2,1)S(1)}, u32[]{:S(2)}, u32[]{:S(2)}) collective-permute-start(bf16[256,1408]{1,0:T(8,128)(2,1)S(1)} %copy-done.68), channel_id=1, source_target_pairs={{0,8},{1,9},{2,10},{3,11},{4,12},{5,13},{6,14},{7,15},{8,0},{9,1},... | collective-permute-start | bytes 2162696 | tf_op jit(solution)/shard_map/ppermute | solution.py:545
  1079.5 76.9 %collective-permute-start.49 = (bf16[256,2816]{1,0:T(8,128)(2,1)}, bf16[256,2816]{1,0:T(8,128)(2,1)}, u32[]{:S(2)}, u32[]{:S(2)}) collective-permute-start(bf16[256,2816]{1,0:T(8,128)(2,1)} %pad_maximum_fusion.4), channel_id=1, source_target_pairs={{0,16},{1,17},{2,18},{3,19},{4,20},{5,21},{6,22},{7,23},{8,24},{9,... | collective-permute-start | bytes 4325384 | tf_op jit(solution)/shard_map/ppermute | solution.py:545
  1104.2 56.4 %collective-permute-start.47 = (bf16[512,1024]{1,0:T(8,128)(2,1)}, bf16[512,1024]{1,0:T(8,128)(2,1)S(1)}, u32[]{:S(2)}, u32[]{:S(2)}) collective-permute-start(bf16[512,1024]{1,0:T(8,128)(2,1)} %get-tuple-element.275), channel_id=1, source_target_pairs={{0,4},{1,5},{2,6},{3,7},{4,0},{5,1},{6,2},{7,3},{8,12},{9,13},{10,... | collective-permute-start | bytes 3145736 | tf_op jit(solution)/shard_map/ppermute | solution.py:545
  1173.7 50.3 %collective-permute-start.60 = (bf16[256,2816]{1,0:T(8,128)(2,1)}, bf16[256,2816]{1,0:T(8,128)(2,1)S(1)}, u32[]{:S(2)}, u32[]{:S(2)}) collective-permute-start(bf16[256,2816]{1,0:T(8,128)(2,1)} %pad_maximum_fusion.5), channel_id=1, source_target_pairs={{0,16},{1,17},{2,18},{3,19},{4,20},{5,21},{6,22},{7,23},{8,24},{9,... | collective-permute-start | bytes 4325384 | tf_op jit(solution)/shard_map/ppermute | solution.py:545
  1174.1 45.7 %collective-permute-start.55 = (bf16[512,1536]{1,0:T(8,128)(2,1)}, bf16[512,1536]{1,0:T(8,128)(2,1)S(1)}, u32[]{:S(2)}, u32[]{:S(2)}) collective-permute-start(bf16[512,1536]{1,0:T(8,128)(2,1)} %maximum_select_fusion.17), channel_id=1, source_target_pairs={{0,8},{1,9},{2,10},{3,11},{4,12},{5,13},{6,14},{7,15},{8,0},{9,1},... | collective-permute-start | bytes 4718600 | tf_op jit(solution)/shard_map/ppermute | solution.py:545
  1175.5 73.6 %collective-permute-start.52 = (bf16[256,2048]{1,0:T(8,128)(2,1)S(1)}, bf16[256,2048]{1,0:T(8,128)(2,1)S(1)}, u32[]{:S(2)}, u32[]{:S(2)}) collective-permute-start(bf16[256,2048]{1,0:T(8,128)(2,1)S(1)} %get-tuple-element.272), channel_id=1, source_target_pairs={{0,0},{1,4},{2,1},{3,5},{4,8},{5,12},{6,9},{7,13},{8,2},{9,6},{10,... | collective-permute-start | bytes 3145736 | tf_op jit(solution)/shard_map/ppermute | solution.py:604
  1180.8 122.0 %collective-permute-start.59 = (bf16[512,2816]{1,0:T(8,128)(2,1)S(1)}, bf16[512,2816]{1,0:T(8,128)(2,1)S(1)}, u32[]{:S(2)}, u32[]{:S(2)}) collective-permute-start(bf16[512,2816]{1,0:T(8,128)(2,1)S(1)} %copy-done.12), channel_id=1, source_target_pairs={{0,4},{1,5},{2,6},{3,7},{4,0},{5,1},{6,2},{7,3},{8,12},{9,13},{10,... | collective-permute-start | bytes 8650760 | tf_op jit(solution)/shard_map/ppermute | solution.py:545
  1184.2 112.9 %collective-permute-start.62 = (bf16[512,2816]{1,0:T(8,128)(2,1)S(1)}, bf16[512,2816]{1,0:T(8,128)(2,1)S(1)}, u32[]{:S(2)}, u32[]{:S(2)}) collective-permute-start(bf16[512,2816]{1,0:T(8,128)(2,1)S(1)} %copy-done.11), channel_id=1, source_target_pairs={{0,4},{1,5},{2,6},{3,7},{4,0},{5,1},{6,2},{7,3},{8,12},{9,13},{10,... | collective-permute-start | bytes 8650760 | tf_op jit(solution)/shard_map/ppermute | solution.py:545
  1220.3 95.1 %collective-permute-start.56 = (bf16[512,3072]{1,0:T(8,128)(2,1)S(1)}, bf16[512,3072]{1,0:T(8,128)(2,1)S(1)}, u32[]{:S(2)}, u32[]{:S(2)}) collective-permute-start(bf16[512,3072]{1,0:T(8,128)(2,1)S(1)} %pad_maximum_fusion.1.refs_0_.refs_1_), channel_id=1, source_target_pairs={{0,4},{1,5},{2,6},{3,7},{4,0},{5,1},{6,2},{7,3},{8,12},{9,13},{10,... | collective-permute-start | bytes 9437192 | tf_op jit(solution)/shard_map/ppermute | solution.py:545
  1224.8 83.5 %collective-permute-start.61 = (bf16[512,2816]{1,0:T(8,128)(2,1)S(1)}, bf16[512,2816]{1,0:T(8,128)(2,1)}, u32[]{:S(2)}, u32[]{:S(2)}) collective-permute-start(bf16[512,2816]{1,0:T(8,128)(2,1)S(1)} %maximum_select_fusion.6.refs_0_.refs_1_), channel_id=1, source_target_pairs={{0,4},{1,5},{2,6},{3,7},{4,0},{5,1},{6,2},{7,3},{8,12},{9,13},{10,... | collective-permute-start | bytes 8650760 | tf_op jit(solution)/shard_map/ppermute | solution.py:545
  (105 other events, 1310.5 us)
Sparse Core Ops, SparseCore 0:
  11.8 83.2 all-gather.6
  97.2 46.2 all-gather.8
  145.7 27.5 all-gather.10
  175.2 57.8 all-gather.12
  235.1 57.8 all-gather.14
Sparse Core Ops, SparseCore 1:
  404.1 90.4 all-gather.16
  526.6 109.3 reduce-scatter.6
  677.1 123.6 reduce-scatter.8
  814.6 29.0 reduce-scatter.12
  846.1 56.0 reduce-scatter.10
  929.2 98.1 reduce-scatter.14
  1071.6 43.8 reduce-scatter.16

commit v6 on v5

--- a/solution.py
+++ b/solution.py
@@ -191,16 +191,14 @@
 
 
 def joined_rows(width, tiles):
-    own = pl.BlockSpec((TILE, width), lambda i, s: (jnp.clip(i - s[0] * tiles, 0, tiles - 1), 0))
-    other = pl.BlockSpec(
-        (TILE, width), lambda i, s: (jnp.clip(i - (1 - s[0]) * tiles, 0, tiles - 1), 0)
-    )
-    return [own, other]
+    spec = pl.BlockSpec((TILE, width), lambda i, s: (i // (2 * tiles) * tiles + i % tiles, 0))
+    return [spec, spec]
 
 
 def enter_kernel(tiles, blocks, project, spots, own_ref, other_ref, *refs):
     i = pl.program_id(0)
-    rows = jnp.where(i // tiles == spots[0], own_ref[...], other_ref[...])
+    mine = lax.rem(lax.div(i, tiles), 2) == spots[0]
+    rows = jnp.where(mine, own_ref[...], other_ref[...])
     part = rows.shape[1] // len(blocks)
     permuted = jnp.concatenate([rows[:, n * part : (n + 1) * part] for n in blocks], axis=1)
     if not project:
@@ -233,7 +231,7 @@
 
 def enter(spots, blocks, own, other, chunks=()):
     width = own.shape[1]
-    count, tiles = 2 * own.shape[0], own.shape[0] // TILE
+    count, tiles = 2 * own.shape[0], own.shape[0] // TILE // 2
     shape = jax.ShapeDtypeStruct
     quarter = shape((count, width // GROUP), LOW)
     if chunks:
@@ -248,7 +246,7 @@
         out_shape=outs,
         grid_spec=pltpu.PrefetchScalarGridSpec(
             num_scalar_prefetch=1,
-            grid=(2 * tiles,),
+            grid=(count // TILE,),
             in_specs=joined_rows(width, tiles) + [ANYWHERE] * len(chunks),
             out_specs=[tile_rows(o.shape[1]) for o in outs],
             scratch_shapes=scratch,
@@ -568,7 +566,7 @@
         return s // (shards // micro)
 
     def origin(r, s, p):
-        run_id = (2 * (r % 2) + (r // 2) % 2) * per_block + p
+        run_id = (r % GROUP) * per_block + p
         stream, piece = run_id // shards, run_id % shards
         member = s % GROUP if streams == 1 else 2 * stream + s % 2
         return (r // GROUP) * GROUP + member, piece
@@ -635,7 +633,7 @@
     def to_runs(x):
         cut = x.reshape(2, 2, -1, own)
         pick = functools.partial(lax.dynamic_index_in_dim, keepdims=False)
-        both = ordered(b, pick(cut, b, 1), swap_b(pick(cut, 1 - b, 1)), 2)
+        both = ordered(b, pick(cut, b, 0), swap_b(pick(cut, 1 - b, 0)), 2)
         return ordered(c, pick(both, c, 0), swap_c(pick(both, 1 - c, 0)), 1)
 
 
@@ -679,6 +677,13 @@
 
     def away(left, right):
         return [gradient_rows(spots, spread, k, left, right) for k in range(1, spread)]
+
+    def in_two(terms):
+        middles = [x.shape[0] // 2 for x in terms]
+        return [x[:m] for x, m in zip(terms, middles)], [x[m:] for x, m in zip(terms, middles)]
+
+    def stacked(upper, lower):
+        return [jnp.concatenate(pair, axis=0) for pair in zip(upper, lower)]
 
     def sent_a(terms):
         return [shift_a(x, k + 1) for k, x in enumerate(terms)]
@@ -771,11 +776,12 @@
     low_middle, s_2, dy_run = tie(low_middle, s_2, dy_run)
 
     other_middle = swap_c(low_middle)
-    dy_pair = gather_rows_b(dy_run)
+    dy_other = swap_b(dy_run)
     w_1, w_2 = [g_1, *s_1], [g_2, *s_2]
     hidden_two, z_one, z_two, product, m_scale = gated_unit(spots, low_middle, other_middle, w_1, w_2)
-    z_one, z_two, product, dy_pair = tie(z_one, z_two, product, dy_pair)
-
+    z_one, z_two, product, dy_other = tie(z_one, z_two, product, dy_other)
+
+    dy_pair = ordered(b, dy_run, dy_other, 0)
     dy_all, dy_own = enter(spots, blocks, dy_pair, swap_c(dy_pair))
     f_down = whole_rows(dy_all, product)
     z_one, z_two, product, f_down, w_d[0] = tie(z_one, z_two, product, f_down, w_d[0])
@@ -793,11 +799,11 @@
     sent, d_one, t_two, product, lean_m = tie(sent, d_one, t_two, product, lean_m)
 
     crossed = swap_b(sent)
-    cut = [(x[: x.shape[0] // 2], x[x.shape[0] // 2 :]) for x in t_two]
-    upper = sent_a([x for x, _ in cut])
+    upper, lower = in_two(t_two)
+    upper = sent_a(upper)
     f_one = whole_rows(hidden_two, d_one)
     result = fold_half(spots, [product], [w_d])
-    crossed, result, f_one, upper = tie(crossed, result, f_one, upper)
+    crossed, result, f_one, upper, f_down = tie(crossed, result, f_one, upper, f_down)
 
     f_one = scattered_all(f_one)
     d_hidden = mine + crossed.astype(F32)
@@ -811,6 +817,7 @@
 
     arrived = swap_c(sent)
     r_result = swap_c(result)
+    y_down = spread_a(f_down)
     lean_o = total(lean_o)
     p_out = cross_tokens(lifted, (o_scale * d_middle).astype(LOW)).astype(LOW)
     p_out = jnp.transpose(p_out.reshape(shards, spread, part, -1), (1, 0, 2, 3))
@@ -819,19 +826,16 @@
     d_gated = times_transposed(d_branch, row_half(w_o, c)) + arrived.astype(F32)
     sent = columns(d_gated, (1 - b) * own, own).astype(LOW)
     mine = columns(d_gated, b * own, own)
-    lower = [x for _, x in cut]
-    sent, mine, lower, r_result, t_out, lean_o = tie(sent, mine, lower, r_result, t_out, lean_o)
+    sent, mine, r_result, t_out, lean_o, y_down = tie(sent, mine, r_result, t_out, lean_o, y_down)
 
     crossed = swap_b(sent)
+    r_out = sent_a(t_out[1:])
+    result, result_mine = fold_half(spots, [product], [w_d], r_result)
+    crossed, result, r_out, lower = tie(crossed, result, r_out, lower)
+
     lower = sent_a(lower)
-    result, result_mine = fold_half(spots, [product], [w_d], r_result)
-    r_two = [jnp.concatenate(pair, axis=0) for pair in zip(upper, lower)]
-    crossed, result, r_two, t_out, f_down = tie(crossed, result, r_two, t_out, f_down)
-
-    f_two = gradient_rows(spots, spread, 0, hidden_two, d_two, r_two)
-    r_out = sent_a(t_out[1:])
     result = swap_b(result)
-    y_down = spread_a(f_down)
+    f_out = scattered(sum([x.astype(F32) for x in r_out], t_out[0].astype(F32)).astype(LOW))
     o_normed = attended * o_scale
     d_gated = mine + crossed.astype(F32)
     d_gate = (d_gated * o_normed).astype(LOW)
@@ -841,28 +845,32 @@
     d_qk = joined(d_query, d_key)
     d_vg = joined(d_value, d_gate)
     t_qk = away(hidden_one, d_qk)
-    d_qk, d_vg, t_qk, f_two, r_out, result, y_down = tie(d_qk, d_vg, t_qk, f_two, r_out, result, y_down)
-
-    r_qk = sent_a(t_qk)
-    f_two = scattered(f_two)
-    f_out = scattered(sum([x.astype(F32) for x in r_out], t_out[0].astype(F32)).astype(LOW))
+    d_qk, d_vg, t_qk, lower, result = tie(d_qk, d_vg, t_qk, lower, result)
+
+    upper_qk, lower_qk = in_two(t_qk)
+    upper_qk = sent_a(upper_qk)
+    f_two = gradient_rows(spots, spread, 0, hidden_two, d_two, stacked(upper, lower))
     output = to_runs((middle + (result_mine + result.astype(F32))).astype(LOW))
     t_vg = away(hidden_one, d_vg)
     sent = fold_half(spots, [d_qk, d_vg], [w_qk, w_vg])
-    sent, t_vg, d_qk, d_vg = tie(sent, t_vg, d_qk, d_vg)
-
+    sent, t_vg, d_qk, d_vg, f_two, output, upper_qk, lower_qk = tie(
+        sent, t_vg, d_qk, d_vg, f_two, output, upper_qk, lower_qk
+    )
+
+    f_two = scattered(f_two)
+    lower_qk = sent_a(lower_qk)
     arrived = swap_c(sent)
     lean_x = total(
         jnp.sum(z_qk * d_qk.astype(F32), axis=-1) + jnp.sum(z_vg * d_vg.astype(F32), axis=-1)
     )
     sent, mine = fold_half(spots, [d_qk, d_vg], [w_qk, w_vg], arrived)
-    sent, mine, r_qk, t_vg, f_one, output, lean_x, y_down = tie(
-        sent, mine, r_qk, t_vg, f_one, output, lean_x, y_down
+    sent, mine, lower_qk, t_vg, f_one, lean_x, y_down = tie(
+        sent, mine, lower_qk, t_vg, f_one, lean_x, y_down
     )
 
     crossed = swap_b(sent)
     r_vg = sent_a(t_vg)
-    f_qk = scattered(gradient_rows(spots, spread, 0, hidden_one, d_qk, r_qk))
+    f_qk = scattered(gradient_rows(spots, spread, 0, hidden_one, d_qk, stacked(upper_qk, lower_qk)))
     output = bring_back(output)
     x_one = spread_b(f_one)
     crossed, d_vg, r_vg, x_one, output, y_down = tie(crossed, d_vg, r_vg, x_one, output, y_down)

time: 1350 us -> 1210 us (0.90)
  waiting for transfers between devices: 669 us -> 445 us
  starting transfers between devices: 76 us -> 149 us
    ppermute x55 -> x56, waiting for transfers between devices: 389 us -> 218 us  [move(): return lax.ppermute(x, AXES, pairs)]
    ppermute x4, waiting for transfers between devices: 154 us -> 99.6 us  [bring_back(): lax.ppermute(lax.dynamic_index_in_dim(slots, (batch_of(place) + p) % 2, 0...]
    ppermute x55 -> x56, starting transfers between devices: 54.5 us -> 103 us  [move(): return lax.ppermute(x, AXES, pairs)]
    ppermute x4, starting transfers between devices: 10.5 us -> 36.8 us  [bring_back(): lax.ppermute(lax.dynamic_index_in_dim(slots, (batch_of(place) + p) % 2, 0...]
    unnamed x181 -> x195, local copies, waits for them, and re-layouts: 64.2 us -> 66.8 us
  transfers between devices with their start and end apart: 75 -> 76, of which waited for: 31 -> 29; matrix products, arithmetic and copies ran while one was open for 13% -> 15% of each run, Pallas kernels for 25% -> 28%
where the time goes in v6:
time: 1210 us; the launch traced here: 1190 us
  waiting for transfers between devices  445 us (37%)
  Pallas kernels  343 us (28%)
  starting transfers between devices  149 us (12%)
  other arithmetic  106 us (9%)
  local copies, waits for them, and re-layouts  100 us (8%)
  matrix products  32.9 us (3%)
  between operations  17.1 us (1%)
    ppermute x56, waiting for transfers between devices, move(): return lax.ppermute(x, AXES, pairs)  218 us
    ppermute x4, waiting for transfers between devices, bring(): lax.ppermute(lax.dynamic_index_in_dim(x, (place + p) % 2, 0, False), AXES...  119 us
    ppermute x56, starting transfers between devices, move(): return lax.ppermute(x, AXES, pairs)  103 us
    pallas_call x6, Pallas kernels, fold_half(): pl.pallas_call(functools.partial(fold_kernel, len(values), arrived is not...  99.7 us
    ppermute x4, waiting for transfers between devices, bring_back(): lax.ppermute(lax.dynamic_index_in_dim(slots, (batch_of(place) + p) % 2, 0...  99.6 us
    pallas_call x8, Pallas kernels, gradient_rows(): pl.pallas_call(gradient_kernel, out_shape=out, grid_spec=pltpu.PrefetchSc...  80.4 us
    unnamed x195, local copies, waits for them, and re-layouts  66.8 us
    select_n x22, other arithmetic, ordered(): jnp.where(index == 0, jnp.concatenate([mine, other], axis), jnp.concatena...  49.6 us
  transfers between devices with their start and end apart: 76, of which 29 were waited for; matrix products, arithmetic and copies ran while one was open for 15% of the time, Pallas kernels for 28%

profile of v6, /device:TPU:17, one launch (start us, length us, event | category | flops | bytes accessed | tf_op | source)
XLA Modules:
  0.0 1193.9 jit_solution(8832387671239279733)
XLA Ops:
  21.0 75.9 %collective-permute-done.2 = bf16[256,2048]{1,0:T(8,128)(2,1)S(1)} collective-permute-done((bf16[256,2048]{1,0:T(8,128)(2,1)}, bf16[256,2048]{1,0:T(8,128)(2,1)S(1)}, u32[]{:S(2)}, u32[]{:S(2)}) %collective-permute-start.2) | collective-permute-done | bytes 1048608 | tf_op jit(solution)/shard_map/ppermute | solution.py:594
  105.0 37.9 %collective-permute-done.4 = bf16[512,2048]{1,0:T(8,128)(2,1)} collective-permute-done((bf16[512,2048]{1,0:T(8,128)(2,1)}, bf16[512,2048]{1,0:T(8,128)(2,1)}, u32[]{:S(2)}, u32[]{:S(2)}) %collective-permute-start.4) | collective-permute-done | bytes 2097184 | tf_op jit(solution)/shard_map/ppermute | solution.py:543
  142.9 6.1 maximum_select_fusion.1.own_ref
  164.3 19.8 %enter.2 = (bf16[2048,2048]{1,0:T(8,128)(2,1)}, f32[2048,1024]{1,0:T(8,128)}, f32[2048,1]{1,0:T(8,128)S(1)}, bf16[2048,512]{1,0:T(8,128)(2,1)S(1)}) custom-call(s32[4]{0:T(128)S(1)} %pad_add_fusion.1.spots, bf16[1024,2048]{1,0:T(8,128)(2,1)S(1)} %copy-done.24, bf16[1024,2048]{1,0:T(8,128)(2,1)} %collective-permute-done.6.other_ref, ...), custom_call_target="tpu_custom_call" | custom-call | flops 8589934592 | bytes 31465472 | tf_op jit(solution)/shard_map/enter/pallas_call | solution.py:244
  185.5 15.9 %collective-permute-done.7.refs_1_.refs_5_.refs_6_ = bf16[1024,1024]{1,0:T(8,128)(2,1)} collective-permute-done((bf16[1024,1024]{1,0:T(8,128)(2,1)}, bf16[1024,1024]{1,0:T(8,128)(2,1)}, u32[]{:S(2)}, u32[]{:S(2)}) %collective-permute-start.7) | collective-permute-done | bytes 2097184 | tf_op jit(solution)/shard_map/ppermute | solution.py:543
  204.2 14.3 %project.1.zv_ref = f32[2048,1024]{1,0:T(8,128)S(1)} custom-call(s32[4]{0:T(128)S(1)} %pad_add_fusion.1.spots, bf16[2048,2048]{1,0:T(8,128)(2,1)} %get-tuple-element.143.h_ref.left_ref, bf16[1024,1024]{1,0:T(8,128)(2,1)S(1)} %copy-done.49, bf16[1024,1024]{1,0:T(8,128)(2,1)} %collective-permute-done.7.refs_1_.refs_5_.refs_6_), custom_call_target="tpu_custom_call" | custom-call | flops 8589934592 | bytes 20971520 | tf_op jit(solution)/shard_map/project/pallas_call | solution.py:275
  221.9 12.3 %attend.1 = f32[2048,512]{1,0:T(8,128)S(1)} custom-call(f32[4]{0:T(128)S(1)} %dynamic_slice.118.rates, s32[2,2]{1,0:T(2,128)S(1)} %pad_add_fusion.ends, f32[2048,1024]{1,0:T(8,128)S(1)} %copy-done.2, f32[2048,1024]{1,0:T(8,128)S(1)} %copy-done.2, f32[2048,1024]{1,0:T(8,128)} %copy-done.3), custom_call_target="tpu_custom_call" | custom-call | flops 4294967296 | bytes 16777216 | tf_op jit(solution)/shard_map/attend/pallas_call | solution.py:98
  243.3 42.0 %collective-permute-done.12 = f32[2048]{0:T(1024)S(1)} collective-permute-done((f32[2048]{0:T(1024)S(1)}, f32[2048]{0:T(1024)S(1)}, u32[]{:S(2)}, u32[]{:S(2)}) %collective-permute-start.12) | collective-permute-done | bytes 8224 | tf_op jit(solution)/shard_map/ppermute | solution.py:543
  293.0 9.2 collective-permute-done.10.refs_1_.refs_3_.refs_4_
  311.4 11.9 fusion.21
  329.8 43.1 %collective-permute-done.16 = bf16[256,2048]{1,0:T(8,128)(2,1)S(1)} collective-permute-done((bf16[256,2048]{1,0:T(8,128)(2,1)S(1)}, bf16[256,2048]{1,0:T(8,128)(2,1)S(1)}, u32[]{:S(2)}, u32[]{:S(2)}) %collective-permute-start.16) | collective-permute-done | bytes 1048608 | tf_op jit(solution)/shard_map/ppermute | solution.py:594
  392.1 38.1 %gated_unit.1 = (bf16[2048,2048]{1,0:T(8,128)(2,1)}, bf16[2048,1408]{1,0:T(8,128)(2,1)}, bf16[2048,1408]{1,0:T(8,128)(2,1)}, bf16[2048,1408]{1,0:T(8,128)(2,1)}, f32[2048,1]{1,0:T(8,128)S(1)}) custom-call(s32[4]{0:T(128)S(1)} %pad_add_fusion.1.spots, bf16[2048,1024]{1,0:T(8,128)(2,1)} %maximum_select_fusion.3.own_ref, ...), custom_call_target="tpu_custom_call" | custom-call | flops 23622320128 | bytes 45621248 | tf_op jit(solution)/shard_map/gated_unit/pallas_call | solution.py:337
  438.1 6.8 collective-permute-done.20.other_ref
  444.9 5.5 enter.3
  451.7 16.7 %gradient_rows.8 = bf16[2048,1408]{1,0:T(8,128)(2,1)S(1)} custom-call(s32[4]{0:T(128)S(1)} %pad_add_fusion.1.spots, bf16[2048,2048]{1,0:T(8,128)(2,1)} %get-tuple-element.165.left_ref.dy_ref, bf16[2048,1408]{1,0:T(8,128)(2,1)S(1)} %bitcast.65), custom_call_target="tpu_custom_call" | custom-call | flops 11811160064 | bytes 17301504 | tf_op jit(solution)/shard_map/gradient_rows/pallas_call | solution.py:470
  474.4 22.4 %gated_unit_back.1 = (bf16[2048,1408]{1,0:T(8,128)(2,1)S(1)}, bf16[2048,1408]{1,0:T(8,128)(2,1)S(1)}, f32[2048,1]{1,0:T(8,128)S(1)}) custom-call(s32[4]{0:T(128)S(1)} %pad_add_fusion.1.spots, bf16[2048,2048]{1,0:T(8,128)(2,1)} %get-tuple-element.165.left_ref.dy_ref, bf16[2048,1408]{1,0:T(8,128)(2,1)} %get-tuple-element.169.one_ref, ...), custom_call_target="tpu_custom_call" | custom-call | flops 11811160064 | bytes 37232640 | tf_op jit(solution)/shard_map/gated_unit_back/pallas_call | solution.py:374
  502.7 19.8 %fold_half.6 = bf16[2048,1024]{1,0:T(8,128)(2,1)} custom-call(s32[4]{0:T(128)S(1)} %pad_add_fusion.1.spots, bf16[2048,1408]{1,0:T(8,128)(2,1)} %copy-done.56, bf16[2048,1408]{1,0:T(8,128)(2,1)} %copy-done.53, bf16[1024,1408]{1,0:T(8,128)(2,1)S(1)} %copy-done.38, bf16[1024,1408]{1,0:T(8,128)(2,1)} %collective-permute-done.10.refs_1_.refs_3_.refs_4_, ...), custom_call_target="tpu_custom_call" | custom-call | flops 11811160064 | bytes 21495808 | tf_op jit(solution)/shard_map/fold_half/pallas_call | solution.py:435
  525.9 6.2 collective-permute-done.22
  536.1 9.4 gradient_rows.9
  545.6 21.9 %fold_half.7 = (bf16[2048,512]{1,0:T(8,128)(2,1)}, f32[2048,512]{1,0:T(8,128)}) custom-call(s32[4]{0:T(128)S(1)} %pad_add_fusion.1.spots, bf16[2048,1408]{1,0:T(8,128)(2,1)} %copy-done.56, bf16[2048,1408]{1,0:T(8,128)(2,1)} %copy-done.53, bf16[2048,1024]{1,0:T(8,128)(2,1)} %collective-permute-done.21.refs_2_, bf16[1024,1408]{1,0:T(8,128)(2,1)S(1)} %copy-done.39, ...), custom_call_target="tpu_custom_call" | custom-call | flops 11811160064 | bytes 27787264 | tf_op jit(solution)/shard_map/fold_half/pallas_call | solution.py:435
  572.2 11.4 fold_half.8
  586.4 16.4 %gradient_rows.10 = bf16[2048,1408]{1,0:T(8,128)(2,1)S(1)} custom-call(s32[4]{0:T(128)S(1)} %pad_add_fusion.1.spots, bf16[2048,2048]{1,0:T(8,128)(2,1)} %get-tuple-element.179.left_ref, bf16[2048,1408]{1,0:T(8,128)(2,1)S(1)} %copy-done.57), custom_call_target="tpu_custom_call" | custom-call | flops 11811160064 | bytes 17301504 | tf_op jit(solution)/shard_map/gradient_rows/pallas_call | solution.py:470
  605.3 9.2 collective-permute-done.24
  616.2 6.7 multiply_reduce_fusion.2
  627.8 11.8 convolution_convert_fusion.1
  642.8 6.4 collective-permute-done.30
  661.1 15.0 %fold_half.9 = (bf16[2048,512]{1,0:T(8,128)(2,1)}, f32[2048,512]{1,0:T(8,128)S(1)}) custom-call(s32[4]{0:T(128)S(1)} %pad_add_fusion.1.spots, bf16[2048,1408]{1,0:T(8,128)(2,1)} %get-tuple-element.183.right_ref.refs_0_, bf16[2048,1024]{1,0:T(8,128)(2,1)} %collective-permute-done.27.refs_1_, ...), custom_call_target="tpu_custom_call" | custom-call | flops 5905580032 | bytes 16252928 | tf_op jit(solution)/shard_map/fold_half/pallas_call | solution.py:435
  676.1 23.5 %collective-permute-done.32 = bf16[1024,512]{1,0:T(8,128)(2,1)} collective-permute-done((bf16[1024,512]{1,0:T(8,128)(2,1)}, bf16[1024,512]{1,0:T(8,128)(2,1)}, u32[]{:S(2)}, u32[]{:S(2)}) %collective-permute-start.32) | collective-permute-done | bytes 1048608 | tf_op jit(solution)/shard_map/ppermute | solution.py:543
  699.6 7.2 collective-permute-done.31
  712.8 21.3 %attend_back.1 = (bf16[2048,512]{1,0:T(8,128)(2,1)S(1)}, bf16[2048,512]{1,0:T(8,128)(2,1)S(1)}, bf16[2048,512]{1,0:T(8,128)(2,1)S(1)}) custom-call(f32[4]{0:T(128)S(1)} %dynamic_slice.118.rates, s32[2,2]{1,0:T(2,128)S(1)} %pad_add_fusion.ends, f32[2048,1024]{1,0:T(8,128)} %get-tuple-element.142.zq_ref.zk_ref, f32[2048,1024]{1,0:T(8,128)} %get-tuple-element.142.zq_ref.zk_ref, ...), custom_call_target="tpu_custom_call" | custom-call | flops 10737418240 | bytes 20971520 | tf_op jit(solution)/shard_map/attend_back/pallas_call | solution.py:119
  749.2 8.1 gradient_rows.11
  764.8 9.1 gradient_rows.13
  791.5 6.9 gradient_rows.12
  798.5 14.0 %fold_half.10 = bf16[2048,1024]{1,0:T(8,128)(2,1)S(1)} custom-call(s32[4]{0:T(128)S(1)} %pad_add_fusion.1.spots, bf16[2048,1024]{1,0:T(8,128)(2,1)} %copy-done.8, bf16[2048,1024]{1,0:T(8,128)(2,1)} %pad_maximum_fusion.refs_1_.right_ref, bf16[1024,1024]{1,0:T(8,128)(2,1)S(1)} %copy-done.47, bf16[1024,1024]{1,0:T(8,128)(2,1)} %collective-permute-done.5.refs_1_.refs_3_.refs_4_, ...), custom_call_target="tpu_custom_call" | custom-call | flops 8589934592 | bytes 16777216 | tf_op jit(solution)/shard_map/fold_half/pallas_call | solution.py:435
  836.6 17.5 %fold_half.11 = (bf16[2048,512]{1,0:T(8,128)(2,1)}, f32[2048,512]{1,0:T(8,128)}) custom-call(s32[4]{0:T(128)S(1)} %pad_add_fusion.1.spots, bf16[2048,1024]{1,0:T(8,128)(2,1)} %copy-done.8, bf16[2048,1024]{1,0:T(8,128)(2,1)} %pad_maximum_fusion.refs_1_.right_ref, bf16[2048,1024]{1,0:T(8,128)(2,1)} %collective-permute-done.38.refs_2_, ...), custom_call_target="tpu_custom_call" | custom-call | flops 8589934592 | bytes 23068672 | tf_op jit(solution)/shard_map/fold_half/pallas_call | solution.py:435
  857.7 6.9 gradient_rows.15
  883.2 56.5 %collective-permute-done.45 = bf16[256,2048]{1,0:T(8,128)(2,1)} collective-permute-done((bf16[256,2048]{1,0:T(8,128)(2,1)}, bf16[256,2048]{1,0:T(8,128)(2,1)}, u32[]{:S(2)}, u32[]{:S(2)}) %collective-permute-start.45) | collective-permute-done | bytes 1048608 | tf_op jit(solution)/shard_map/ppermute | solution.py:602
  946.4 6.9 gradient_rows.14
  965.4 9.3 collective-permute-done.47
  976.5 34.2 %collective-permute-start.48 = (bf16[512,1024]{1,0:T(8,128)(2,1)}, bf16[512,1024]{1,0:T(8,128)(2,1)S(1)}, u32[]{:S(2)}, u32[]{:S(2)}) collective-permute-start(bf16[512,1024]{1,0:T(8,128)(2,1)} %get-tuple-element.275), channel_id=1, source_target_pairs={{0,4},{1,5},{2,6},{3,7},{4,0},{5,1},{6,2},{7,3},{8,12},{9,13},{10,... | collective-permute-start | bytes 3145736 | tf_op jit(solution)/shard_map/ppermute | solution.py:543
  1032.6 32.4 %collective-permute-start.53 = (bf16[256,2048]{1,0:T(8,128)(2,1)S(1)}, bf16[256,2048]{1,0:T(8,128)(2,1)S(1)}, u32[]{:S(2)}, u32[]{:S(2)}) collective-permute-start(bf16[256,2048]{1,0:T(8,128)(2,1)S(1)} %get-tuple-element.272), channel_id=1, source_target_pairs={{0,0},{1,4},{2,1},{3,5},{4,2},{5,6},{6,3},{7,7},{8,8},{9,12},{10,9... | collective-permute-start | bytes 3145736 | tf_op jit(solution)/shard_map/ppermute | solution.py:602
  1070.1 12.8 %collective-permute-start.57 = (bf16[512,3072]{1,0:T(8,128)(2,1)S(1)}, bf16[512,3072]{1,0:T(8,128)(2,1)S(1)}, u32[]{:S(2)}, u32[]{:S(2)}) collective-permute-start(bf16[512,3072]{1,0:T(8,128)(2,1)S(1)} %pad_maximum_fusion.1.refs_0_.refs_1_), channel_id=1, source_target_pairs={{0,4},{1,5},{2,6},{3,7},{4,0},{5,1},{6,2},{7,3},{8,12},{9,13},{10,... | collective-permute-start | bytes 9437192 | tf_op jit(solution)/shard_map/ppermute | solution.py:543
  1085.5 5.7 collective-permute-done.53
  1091.3 37.4 %collective-permute-done.54 = bf16[256,2048]{1,0:T(8,128)(2,1)S(1)} collective-permute-done((bf16[256,2048]{1,0:T(8,128)(2,1)S(1)}, bf16[256,2048]{1,0:T(8,128)(2,1)S(1)}, u32[]{:S(2)}, u32[]{:S(2)}) %collective-permute-start.54) | collective-permute-done | bytes 1048608 | tf_op jit(solution)/shard_map/ppermute | solution.py:602
  1130.9 22.1 %collective-permute-done.58 = bf16[512,1024]{1,0:T(8,128)(2,1)S(1)} collective-permute-done((bf16[512,1024]{1,0:T(8,128)(2,1)S(1)}, bf16[512,1024]{1,0:T(8,128)(2,1)S(1)}, u32[]{:S(2)}, u32[]{:S(2)}) %collective-permute-start.58) | collective-permute-done | bytes 1048608 | tf_op jit(solution)/shard_map/ppermute | solution.py:543
  1153.3 5.6 place_quarters.9
  1158.9 7.1 place_quarters.7
  1166.0 7.1 place_quarters.8
  (439 shorter events, 312.9 us)
Async XLA Ops:
  8.0 91.2 %all-gather.7.cloned.1.call-start = ((), (), s32[]{:S(2)}) async-start(), calls=%async_computation.6 | async-start | bytes 2621440 | tf_op jit(solution)/shard_map/all_gather | solution.py:654
  11.6 137.4 %all-gather.9.cloned.1.call-start = ((), (), s32[]{:S(2)}) async-start(), calls=%async_computation.7 | async-start | bytes 2621440 | tf_op jit(solution)/shard_map/all_gather | solution.py:654
  14.8 170.7 %all-gather.11.cloned.1.call-start = ((), (), s32[]{:S(2)}) async-start(), calls=%async_computation.8 | async-start | bytes 1310720 | tf_op jit(solution)/shard_map/all_gather | solution.py:654
  16.0 80.9 %collective-permute-start.2 = (bf16[256,2048]{1,0:T(8,128)(2,1)}, bf16[256,2048]{1,0:T(8,128)(2,1)S(1)}, u32[]{:S(2)}, u32[]{:S(2)}) collective-permute-start(bf16[256,2048]{1,0:T(8,128)(2,1)} %get-tuple-element.292), channel_id=1, source_target_pairs={{0,0},{4,1},{1,2},{5,3},{2,4},{6,5},{3,6},{7,7},{8,8},{12,9},{9,10... | collective-permute-start | bytes 3145736 | tf_op jit(solution)/shard_map/ppermute | solution.py:594
  18.1 78.8 %collective-permute-start.3 = (bf16[256,2048]{1,0:T(8,128)(2,1)S(1)}, bf16[256,2048]{1,0:T(8,128)(2,1)S(1)}, u32[]{:S(2)}, u32[]{:S(2)}) collective-permute-start(bf16[256,2048]{1,0:T(8,128)(2,1)S(1)} %get-tuple-element.293), channel_id=1, source_target_pairs={{1,0},{5,1},{0,2},{4,3},{3,4},{7,5},{2,6},{6,7},{9,8},{13,9},{8,10... | collective-permute-start | bytes 3145736 | tf_op jit(solution)/shard_map/ppermute | solution.py:594
  99.2 43.7 %collective-permute-start.4 = (bf16[512,2048]{1,0:T(8,128)(2,1)}, bf16[512,2048]{1,0:T(8,128)(2,1)}, u32[]{:S(2)}, u32[]{:S(2)}) collective-permute-start(bf16[512,2048]{1,0:T(8,128)(2,1)} %maximum_select_fusion.7), channel_id=1, source_target_pairs={{0,8},{1,9},{2,10},{3,11},{4,12},{5,13},{6,14},{7,15},{8,0},{9,1},... | collective-permute-start | bytes 6291464 | tf_op jit(solution)/shard_map/ppermute | solution.py:543
  101.2 137.8 %all-gather.13.cloned.1.call-start = ((), (), s32[]{:S(2)}) async-start(), calls=%async_computation.9 | async-start | bytes 3604480 | tf_op jit(solution)/shard_map/all_gather | solution.py:654
  101.2 47.8 %collective-permute-start.5 = (bf16[1024,1024]{1,0:T(8,128)(2,1)}, bf16[1024,1024]{1,0:T(8,128)(2,1)}, u32[]{:S(2)}, u32[]{:S(2)}) collective-permute-start(bf16[1024,1024]{1,0:T(8,128)(2,1)} %all-gather.7.cloned.1.call-done.refs_0_.refs_2_.refs_3_), channel_id=1, source_target_pairs={{0,16},{1,17},{2,18},{3,19},{4,20},{5,21},{6,22},{7,23},{8,24},{9,... | collective-permute-start | bytes 6291464 | tf_op jit(solution)/shard_map/ppermute | solution.py:543
  104.9 188.1 %all-gather.15.cloned.1.call-start = ((), (), s32[]{:S(2)}) async-start(), calls=%async_computation.10 | async-start | bytes 3604480 | tf_op jit(solution)/shard_map/all_gather | solution.py:654
  153.8 47.5 %collective-permute-start.7 = (bf16[1024,1024]{1,0:T(8,128)(2,1)}, bf16[1024,1024]{1,0:T(8,128)(2,1)}, u32[]{:S(2)}, u32[]{:S(2)}) collective-permute-start(bf16[1024,1024]{1,0:T(8,128)(2,1)} %all-gather.9.cloned.1.call-done.refs_0_.refs_4_.refs_5_), channel_id=1, source_target_pairs={{0,16},{1,17},{2,18},{3,19},{4,20},{5,21},{6,22},{7,23},{8,24},{9,... | collective-permute-start | bytes 6291464 | tf_op jit(solution)/shard_map/ppermute | solution.py:543
  159.9 314.4 %all-gather.17.cloned.1.call-start = ((), (), s32[]{:S(2)}) async-start(), calls=%async_computation.11 | async-start | bytes 6488064 | tf_op jit(solution)/shard_map/all_gather | solution.py:658
  201.3 37.7 %collective-permute-start.8 = (bf16[1024,512]{1,0:T(8,128)(2,1)}, bf16[1024,512]{1,0:T(8,128)(2,1)}, u32[]{:S(2)}, u32[]{:S(2)}) collective-permute-start(bf16[1024,512]{1,0:T(8,128)(2,1)} %all-gather.11.cloned.1.call-done), channel_id=1, source_target_pairs={{0,16},{1,17},{2,18},{3,19},{4,20},{5,21},{6,22},{7,23},{8,24},{9,... | collective-permute-start | bytes 3145736 | tf_op jit(solution)/shard_map/ppermute | solution.py:543
  239.0 63.2 %collective-permute-start.10 = (bf16[1024,1408]{1,0:T(8,128)(2,1)}, bf16[1024,1408]{1,0:T(8,128)(2,1)}, u32[]{:S(2)}, u32[]{:S(2)}) collective-permute-start(bf16[1024,1408]{1,0:T(8,128)(2,1)} %all-gather.13.cloned.1.call-done.refs_0_.refs_2_.refs_3_), channel_id=1, source_target_pairs={{0,16},{1,17},{2,18},{3,19},{4,20},{5,21},{6,22},{7,23},{8,24},{9,... | collective-permute-start | bytes 8650760 | tf_op jit(solution)/shard_map/ppermute | solution.py:543
  239.2 46.0 %collective-permute-start.9 = (bf16[2048,512]{1,0:T(8,128)(2,1)S(1)}, bf16[2048,512]{1,0:T(8,128)(2,1)S(1)}, u32[]{:S(2)}, u32[]{:S(2)}) collective-permute-start(bf16[2048,512]{1,0:T(8,128)(2,1)S(1)} %get-tuple-element.146), channel_id=1, source_target_pairs={{0,8},{1,9},{2,10},{3,11},{4,12},{5,13},{6,14},{7,15},{8,0},{9,1},... | collective-permute-start | bytes 6291464 | tf_op jit(solution)/shard_map/ppermute | solution.py:543
  243.0 42.2 %collective-permute-start.12 = (f32[2048]{0:T(1024)S(1)}, f32[2048]{0:T(1024)S(1)}, u32[]{:S(2)}, u32[]{:S(2)}) collective-permute-start(f32[2048]{0:T(1024)S(1)} %add.256), channel_id=1, source_target_pairs={{0,8},{1,9},{2,10},{3,11},{4,12},{5,13},{6,14},{7,15},{8,0},{9,1},... | collective-permute-start | bytes 24584 | tf_op jit(solution)/shard_map/ppermute | solution.py:543
  307.4 70.5 %collective-permute-start.15 = (bf16[1024,1408]{1,0:T(8,128)(2,1)S(1)}, bf16[1024,1408]{1,0:T(8,128)(2,1)S(1)}, u32[]{:S(2)}, u32[]{:S(2)}) collective-permute-start(bf16[1024,1408]{1,0:T(8,128)(2,1)S(1)} %copy-done.40), channel_id=1, source_target_pairs={{0,16},{1,17},{2,18},{3,19},{4,20},{5,21},{6,22},{7,23},{8,24},{9,... | collective-permute-start | bytes 8650760 | tf_op jit(solution)/shard_map/ppermute | solution.py:543
  323.3 51.9 %collective-permute-start.14 = (bf16[2048,512]{1,0:T(8,128)(2,1)S(1)}, bf16[2048,512]{1,0:T(8,128)(2,1)S(1)}, u32[]{:S(2)}, u32[]{:S(2)}) collective-permute-start(bf16[2048,512]{1,0:T(8,128)(2,1)S(1)} %get-tuple-element.296), channel_id=1, source_target_pairs={{0,8},{1,9},{2,10},{3,11},{4,12},{5,13},{6,14},{7,15},{8,0},{9,1},... | collective-permute-start | bytes 6291464 | tf_op jit(solution)/shard_map/ppermute | solution.py:543
  324.7 48.2 %collective-permute-start.16 = (bf16[256,2048]{1,0:T(8,128)(2,1)S(1)}, bf16[256,2048]{1,0:T(8,128)(2,1)S(1)}, u32[]{:S(2)}, u32[]{:S(2)}) collective-permute-start(bf16[256,2048]{1,0:T(8,128)(2,1)S(1)} %get-tuple-element.288), channel_id=1, source_target_pairs={{0,0},{4,1},{1,2},{5,3},{2,4},{6,5},{3,6},{7,7},{8,8},{12,9},{9,10... | collective-permute-start | bytes 3145736 | tf_op jit(solution)/shard_map/ppermute | solution.py:594
  329.8 43.2 %collective-permute-start.17 = (bf16[256,2048]{1,0:T(8,128)(2,1)S(1)}, bf16[256,2048]{1,0:T(8,128)(2,1)S(1)}, u32[]{:S(2)}, u32[]{:S(2)}) collective-permute-start(bf16[256,2048]{1,0:T(8,128)(2,1)S(1)} %get-tuple-element.289), channel_id=1, source_target_pairs={{1,0},{5,1},{0,2},{4,3},{3,4},{7,5},{2,6},{6,7},{9,8},{13,9},{8,10... | collective-permute-start | bytes 3145736 | tf_op jit(solution)/shard_map/ppermute | solution.py:594
  385.3 229.2 %reduce-scatter.7.cloned.1.call-start = ((), (), s32[]{:S(2)}) async-start(), calls=%async_computation.12 | async-start | bytes 6488064 | tf_op jit(solution)/shard_map/reduce_scatter | solution.py:698
  385.8 47.6 %collective-permute-start.19 = (bf16[512,2048]{1,0:T(8,128)(2,1)}, bf16[512,2048]{1,0:T(8,128)(2,1)S(1)}, u32[]{:S(2)}, u32[]{:S(2)}) collective-permute-start(bf16[512,2048]{1,0:T(8,128)(2,1)} %maximum_select_fusion.9), channel_id=1, source_target_pairs={{0,8},{1,9},{2,10},{3,11},{4,12},{5,13},{6,14},{7,15},{8,0},{9,1},... | collective-permute-start | bytes 6291464 | tf_op jit(solution)/shard_map/ppermute | solution.py:543
  474.3 379.7 %reduce-scatter.9.cloned.1.call-start = ((), (), s32[]{:S(2)}) async-start(), calls=%async_computation.13 | async-start | bytes 6488064 | tf_op jit(solution)/shard_map/reduce_scatter | solution.py:698
  567.5 47.0 %collective-permute-start.24 = (bf16[2048,512]{1,0:T(8,128)(2,1)}, bf16[2048,512]{1,0:T(8,128)(2,1)}, u32[]{:S(2)}, u32[]{:S(2)}) collective-permute-start(bf16[2048,512]{1,0:T(8,128)(2,1)} %get-tuple-element.182), channel_id=1, source_target_pairs={{0,8},{1,9},{2,10},{3,11},{4,12},{5,13},{6,14},{7,15},{8,0},{9,1},... | collective-permute-start | bytes 6291464 | tf_op jit(solution)/shard_map/ppermute | solution.py:543
  614.5 340.1 %reduce-scatter.13.cloned.1.call-start = ((), (), s32[]{:S(2)}) async-start(), calls=%async_computation.15 | async-start | bytes 1310720 | tf_op jit(solution)/shard_map/reduce_scatter | solution.py:692
  660.9 46.0 %collective-permute-start.31 = (bf16[2048,512]{1,0:T(8,128)(2,1)}, bf16[2048,512]{1,0:T(8,128)(2,1)}, u32[]{:S(2)}, u32[]{:S(2)}) collective-permute-start(bf16[2048,512]{1,0:T(8,128)(2,1)} %dynamic-slice_convert_fusion), channel_id=1, source_target_pairs={{0,8},{1,9},{2,10},{3,11},{4,12},{5,13},{6,14},{7,15},{8,0},{9,1},... | collective-permute-start | bytes 6291464 | tf_op jit(solution)/shard_map/ppermute | solution.py:543
  660.9 38.7 %collective-permute-start.32 = (bf16[1024,512]{1,0:T(8,128)(2,1)}, bf16[1024,512]{1,0:T(8,128)(2,1)}, u32[]{:S(2)}, u32[]{:S(2)}) collective-permute-start(bf16[1024,512]{1,0:T(8,128)(2,1)} %get-tuple-element.199), channel_id=1, source_target_pairs={{0,16},{1,17},{2,18},{3,19},{4,20},{5,21},{6,22},{7,23},{8,24},{9,... | collective-permute-start | bytes 3145736 | tf_op jit(solution)/shard_map/ppermute | solution.py:543
  706.9 50.5 %collective-permute-start.33 = (bf16[512,1408]{1,0:T(8,128)(2,1)}, bf16[512,1408]{1,0:T(8,128)(2,1)}, u32[]{:S(2)}, u32[]{:S(2)}) collective-permute-start(bf16[512,1408]{1,0:T(8,128)(2,1)} %get-tuple-element.205), channel_id=1, source_target_pairs={{0,16},{1,17},{2,18},{3,19},{4,20},{5,21},{6,22},{7,23},{8,24},{9,... | collective-permute-start | bytes 4325384 | tf_op jit(solution)/shard_map/ppermute | solution.py:543
  707.6 49.7 %collective-permute-start.34 = (bf16[2048,512]{1,0:T(8,128)(2,1)}, bf16[2048,512]{1,0:T(8,128)(2,1)}, u32[]{:S(2)}, u32[]{:S(2)}) collective-permute-start(bf16[2048,512]{1,0:T(8,128)(2,1)} %get-tuple-element.206), channel_id=1, source_target_pairs={{0,8},{1,9},{2,10},{3,11},{4,12},{5,13},{6,14},{7,15},{8,0},{9,1},... | collective-permute-start | bytes 6291464 | tf_op jit(solution)/shard_map/ppermute | solution.py:543
  740.6 214.0 %reduce-scatter.11.cloned.1.call-start = ((), (), s32[]{:S(2)}) async-start(), calls=%async_computation.14 | async-start | bytes 3604480 | tf_op jit(solution)/shard_map/reduce_scatter | solution.py:692
  778.3 38.4 %collective-permute-start.37 = (bf16[512,1024]{1,0:T(8,128)(2,1)S(1)}, bf16[512,1024]{1,0:T(8,128)(2,1)}, u32[]{:S(2)}, u32[]{:S(2)}) collective-permute-start(bf16[512,1024]{1,0:T(8,128)(2,1)S(1)} %get-tuple-element.281), channel_id=1, source_target_pairs={{0,16},{1,17},{2,18},{3,19},{4,20},{5,21},{6,22},{7,23},{8,24},{9,... | collective-permute-start | bytes 3145736 | tf_op jit(solution)/shard_map/ppermute | solution.py:543
  816.7 195.3 %reduce-scatter.15.cloned.1.call-start = ((), (), s32[]{:S(2)}) async-start(), calls=%async_computation.16 | async-start | bytes 2621440 | tf_op jit(solution)/shard_map/reduce_scatter | solution.py:692
  866.0 163.3 %reduce-scatter.17.cloned.1.call-start = ((), (), s32[]{:S(2)}) async-start(), calls=%async_computation.17 | async-start | bytes 2621440 | tf_op jit(solution)/shard_map/reduce_scatter | solution.py:692
  873.2 73.2 %collective-permute-start.42 = (bf16[2048,512]{1,0:T(8,128)(2,1)}, bf16[2048,512]{1,0:T(8,128)(2,1)}, u32[]{:S(2)}, u32[]{:S(2)}) collective-permute-start(bf16[2048,512]{1,0:T(8,128)(2,1)} %get-tuple-element.223), channel_id=1, source_target_pairs={{0,8},{1,9},{2,10},{3,11},{4,12},{5,13},{6,14},{7,15},{8,0},{9,1},... | collective-permute-start | bytes 6291464 | tf_op jit(solution)/shard_map/ppermute | solution.py:543
  874.3 72.0 %collective-permute-start.43 = (bf16[1024,1024]{1,0:T(8,128)(2,1)}, bf16[1024,1024]{1,0:T(8,128)(2,1)S(1)}, u32[]{:S(2)}, u32[]{:S(2)}) collective-permute-start(bf16[1024,1024]{1,0:T(8,128)(2,1)} %copy-done.52), channel_id=1, source_target_pairs={{0,16},{1,17},{2,18},{3,19},{4,20},{5,21},{6,22},{7,23},{8,24},{9,... | collective-permute-start | bytes 6291464 | tf_op jit(solution)/shard_map/ppermute | solution.py:543
  877.9 61.9 %collective-permute-start.45 = (bf16[256,2048]{1,0:T(8,128)(2,1)}, bf16[256,2048]{1,0:T(8,128)(2,1)}, u32[]{:S(2)}, u32[]{:S(2)}) collective-permute-start(bf16[256,2048]{1,0:T(8,128)(2,1)} %get-tuple-element.278), channel_id=1, source_target_pairs={{0,0},{1,4},{2,1},{3,5},{4,2},{5,6},{6,3},{7,7},{8,8},{9,12},{10,9... | collective-permute-start | bytes 3145736 | tf_op jit(solution)/shard_map/ppermute | solution.py:602
  882.0 57.8 %collective-permute-start.46 = (bf16[256,2048]{1,0:T(8,128)(2,1)}, bf16[256,2048]{1,0:T(8,128)(2,1)}, u32[]{:S(2)}, u32[]{:S(2)}) collective-permute-start(bf16[256,2048]{1,0:T(8,128)(2,1)} %get-tuple-element.279), channel_id=1, source_target_pairs={{0,1},{1,5},{2,0},{3,4},{4,3},{5,7},{6,2},{7,6},{8,9},{9,13},{10,8... | collective-permute-start | bytes 3145736 | tf_op jit(solution)/shard_map/ppermute | solution.py:602
  882.1 61.8 %collective-permute-start.44 = (bf16[256,1408]{1,0:T(8,128)(2,1)}, bf16[256,1408]{1,0:T(8,128)(2,1)}, u32[]{:S(2)}, u32[]{:S(2)}) collective-permute-start(bf16[256,1408]{1,0:T(8,128)(2,1)} %reduce-scatter.9.cloned.1.call-done), channel_id=1, source_target_pairs={{0,8},{1,9},{2,10},{3,11},{4,12},{5,13},{6,14},{7,15},{8,0},{9,1},... | collective-permute-start | bytes 2162696 | tf_op jit(solution)/shard_map/ppermute | solution.py:543
  962.5 52.6 %collective-permute-start.49 = (bf16[512,1408]{1,0:T(8,128)(2,1)}, bf16[512,1408]{1,0:T(8,128)(2,1)}, u32[]{:S(2)}, u32[]{:S(2)}) collective-permute-start(bf16[512,1408]{1,0:T(8,128)(2,1)} %maximum_select_fusion.18), channel_id=1, source_target_pairs={{0,8},{1,9},{2,10},{3,11},{4,12},{5,13},{6,14},{7,15},{8,0},{9,1},... | collective-permute-start | bytes 4325384 | tf_op jit(solution)/shard_map/ppermute | solution.py:543
  962.6 48.2 %collective-permute-start.51 = (bf16[256,1408]{1,0:T(8,128)(2,1)S(1)}, bf16[256,1408]{1,0:T(8,128)(2,1)S(1)}, u32[]{:S(2)}, u32[]{:S(2)}) collective-permute-start(bf16[256,1408]{1,0:T(8,128)(2,1)S(1)} %copy-done.74), channel_id=1, source_target_pairs={{0,8},{1,9},{2,10},{3,11},{4,12},{5,13},{6,14},{7,15},{8,0},{9,1},... | collective-permute-start | bytes 2162696 | tf_op jit(solution)/shard_map/ppermute | solution.py:543
  964.0 54.8 %collective-permute-start.50 = (bf16[256,2816]{1,0:T(8,128)(2,1)}, bf16[256,2816]{1,0:T(8,128)(2,1)}, u32[]{:S(2)}, u32[]{:S(2)}) collective-permute-start(bf16[256,2816]{1,0:T(8,128)(2,1)} %pad_maximum_fusion.5), channel_id=1, source_target_pairs={{0,16},{1,17},{2,18},{3,19},{4,20},{5,21},{6,22},{7,23},{8,24},{9,... | collective-permute-start | bytes 4325384 | tf_op jit(solution)/shard_map/ppermute | solution.py:543
  976.5 46.3 %collective-permute-start.48 = (bf16[512,1024]{1,0:T(8,128)(2,1)}, bf16[512,1024]{1,0:T(8,128)(2,1)S(1)}, u32[]{:S(2)}, u32[]{:S(2)}) collective-permute-start(bf16[512,1024]{1,0:T(8,128)(2,1)} %get-tuple-element.275), channel_id=1, source_target_pairs={{0,4},{1,5},{2,6},{3,7},{4,0},{5,1},{6,2},{7,3},{8,12},{9,13},{10,... | collective-permute-start | bytes 3145736 | tf_op jit(solution)/shard_map/ppermute | solution.py:543
  1029.4 53.5 %collective-permute-start.61 = (bf16[256,2816]{1,0:T(8,128)(2,1)}, bf16[256,2816]{1,0:T(8,128)(2,1)S(1)}, u32[]{:S(2)}, u32[]{:S(2)}) collective-permute-start(bf16[256,2816]{1,0:T(8,128)(2,1)} %pad_maximum_fusion.6), channel_id=1, source_target_pairs={{0,16},{1,17},{2,18},{3,19},{4,20},{5,21},{6,22},{7,23},{8,24},{9,... | collective-permute-start | bytes 4325384 | tf_op jit(solution)/shard_map/ppermute | solution.py:543
  1030.8 38.9 %collective-permute-start.56 = (bf16[512,1536]{1,0:T(8,128)(2,1)}, bf16[512,1536]{1,0:T(8,128)(2,1)S(1)}, u32[]{:S(2)}, u32[]{:S(2)}) collective-permute-start(bf16[512,1536]{1,0:T(8,128)(2,1)} %maximum_select_fusion.17), channel_id=1, source_target_pairs={{0,8},{1,9},{2,10},{3,11},{4,12},{5,13},{6,14},{7,15},{8,0},{9,1},... | collective-permute-start | bytes 4718600 | tf_op jit(solution)/shard_map/ppermute | solution.py:543
  1032.6 58.6 %collective-permute-start.53 = (bf16[256,2048]{1,0:T(8,128)(2,1)S(1)}, bf16[256,2048]{1,0:T(8,128)(2,1)S(1)}, u32[]{:S(2)}, u32[]{:S(2)}) collective-permute-start(bf16[256,2048]{1,0:T(8,128)(2,1)S(1)} %get-tuple-element.272), channel_id=1, source_target_pairs={{0,0},{1,4},{2,1},{3,5},{4,2},{5,6},{6,3},{7,7},{8,8},{9,12},{10,9... | collective-permute-start | bytes 3145736 | tf_op jit(solution)/shard_map/ppermute | solution.py:602
  1065.0 93.9 %collective-permute-start.60 = (bf16[512,2816]{1,0:T(8,128)(2,1)S(1)}, bf16[512,2816]{1,0:T(8,128)(2,1)}, u32[]{:S(2)}, u32[]{:S(2)}) collective-permute-start(bf16[512,2816]{1,0:T(8,128)(2,1)S(1)} %copy-done.12), channel_id=1, source_target_pairs={{0,4},{1,5},{2,6},{3,7},{4,0},{5,1},{6,2},{7,3},{8,12},{9,13},{10,... | collective-permute-start | bytes 8650760 | tf_op jit(solution)/shard_map/ppermute | solution.py:543
  1066.6 86.8 %collective-permute-start.63 = (bf16[512,2816]{1,0:T(8,128)(2,1)S(1)}, bf16[512,2816]{1,0:T(8,128)(2,1)S(1)}, u32[]{:S(2)}, u32[]{:S(2)}) collective-permute-start(bf16[512,2816]{1,0:T(8,128)(2,1)S(1)} %copy-done.11), channel_id=1, source_target_pairs={{0,4},{1,5},{2,6},{3,7},{4,0},{5,1},{6,2},{7,3},{8,12},{9,13},{10,... | collective-permute-start | bytes 8650760 | tf_op jit(solution)/shard_map/ppermute | solution.py:543
  1070.1 103.0 %collective-permute-start.57 = (bf16[512,3072]{1,0:T(8,128)(2,1)S(1)}, bf16[512,3072]{1,0:T(8,128)(2,1)S(1)}, u32[]{:S(2)}, u32[]{:S(2)}) collective-permute-start(bf16[512,3072]{1,0:T(8,128)(2,1)S(1)} %pad_maximum_fusion.1.refs_0_.refs_1_), channel_id=1, source_target_pairs={{0,4},{1,5},{2,6},{3,7},{4,0},{5,1},{6,2},{7,3},{8,12},{9,13},{10,... | collective-permute-start | bytes 9437192 | tf_op jit(solution)/shard_map/ppermute | solution.py:543
  1083.8 82.3 %collective-permute-start.62 = (bf16[512,2816]{1,0:T(8,128)(2,1)S(1)}, bf16[512,2816]{1,0:T(8,128)(2,1)}, u32[]{:S(2)}, u32[]{:S(2)}) collective-permute-start(bf16[512,2816]{1,0:T(8,128)(2,1)S(1)} %maximum_select_fusion.6.refs_0_.refs_1_), channel_id=1, source_target_pairs={{0,4},{1,5},{2,6},{3,7},{4,0},{5,1},{6,2},{7,3},{8,12},{9,13},{10,... | collective-permute-start | bytes 8650760 | tf_op jit(solution)/shard_map/ppermute | solution.py:543
  (113 other events, 1476.6 us)
Sparse Core Ops, SparseCore 0:
  11.8 83.3 all-gather.6
  97.3 46.1 all-gather.8
  145.7 27.5 all-gather.10
  175.2 57.8 all-gather.12
  235.1 57.8 all-gather.14
Sparse Core Ops, SparseCore 1:
  385.4 88.9 all-gather.16
  477.8 109.1 reduce-scatter.6
  614.6 126.9 reduce-scatter.8
  743.9 25.0 reduce-scatter.12
  816.8 58.4 reduce-scatter.10
  878.2 71.1 reduce-scatter.14
  954.7 63.9 reduce-scatter.16

commit v7 on v6

--- a/solution.py
+++ b/solution.py
@@ -497,8 +497,8 @@
                 out_ref[...] = refs[n][:, first : first + size].astype(F32)
 
 
-def place_quarters(spots, four, *cuts):
-    rows, columns = four[0][0].shape[0], four[0][2]
+def place_quarters(spots, pairs, *cuts):
+    rows, columns = pairs[0].shape[0], pairs[0].shape[1] // 2
     outs = [jax.ShapeDtypeStruct((rows, GROUP * size), F32) for _, size in cuts]
 
     def block(index):
@@ -510,13 +510,13 @@
         grid_spec=pltpu.PrefetchScalarGridSpec(
             num_scalar_prefetch=1,
             grid=(GROUP,),
-            in_specs=[block(index) for _, index, _ in four],
+            in_specs=[block(0), block(1), block(0), block(1)],
             out_specs=[pl.BlockSpec((rows, size), lambda q, s: (0, q)) for _, size in cuts],
         ),
         compiler_params=limit(40),
-        cost_estimate=estimate(0, *[x for x, _, _ in four], *outs),
+        cost_estimate=estimate(0, *pairs, *outs),
         name="place_quarters",
-    )(spots, *[x for x, _, _ in four])
+    )(spots, pairs[0], pairs[0], pairs[1], pairs[1])
 
 
 def tie(*values):
@@ -678,12 +678,15 @@
     def away(left, right):
         return [gradient_rows(spots, spread, k, left, right) for k in range(1, spread)]
 
-    def in_two(terms):
-        middles = [x.shape[0] // 2 for x in terms]
-        return [x[:m] for x, m in zip(terms, middles)], [x[m:] for x, m in zip(terms, middles)]
-
-    def stacked(upper, lower):
-        return [jnp.concatenate(pair, axis=0) for pair in zip(upper, lower)]
+    def pieces(terms, *eighths):
+        marks = [0, *eighths, 8]
+        return [
+            [x[x.shape[0] * i // 8 : x.shape[0] * j // 8] for x in terms]
+            for i, j in zip(marks[:-1], marks[1:])
+        ]
+
+    def stacked(*arrived):
+        return [jnp.concatenate(cut, axis=0) for cut in zip(*arrived)]
 
     def sent_a(terms):
         return [shift_a(x, k + 1) for k, x in enumerate(terms)]
@@ -691,14 +694,8 @@
     def scattered(x):
         return lax.psum_scatter(x, "shard", scatter_dimension=0, tiled=True)
 
-    def whole_rows(left, right):
-        return gradient_rows(spots, spread, None, left, right)
-
-    def scattered_all(x):
-        return lax.psum_scatter(x, OWNERS, scatter_dimension=0, tiled=True)
-
-    def summed(left, right, arrived):
-        return scattered(gradient_rows(spots, spread, 0, left, right, arrived))
+    def kept(left, right, *arrived):
+        return gradient_rows(spots, spread, 0, left, right, stacked(*arrived))
 
     def spread_a(x):
         return by_spread([x] + over_spread(x))
@@ -707,11 +704,11 @@
         return jnp.concatenate([x, swap_b(x)], axis=1)
 
     def spread_c(pair):
-        other, size = swap_c(pair), pair.shape[1] // 2
-        return [(pair, 0, size), (pair, 1, size), (other, 0, size), (other, 1, size)]
-
-    def features_in_order(four, first, size):
-        cut = [x[:, index * full + first : index * full + first + size] for x, index, full in four]
+        return pair, swap_c(pair)
+
+    def features_in_order(pairs, first, size):
+        full = pairs[0].shape[1] // 2
+        cut = [x[:, i * full + first : i * full + first + size] for x in pairs for i in range(2)]
         pair = [ordered(b, cut[n], cut[n + 1], 1) for n in (0, 2)]
         return natural(ordered(c, pair[0], pair[1], 1)).astype(F32)
 
@@ -783,29 +780,35 @@
 
     dy_pair = ordered(b, dy_run, dy_other, 0)
     dy_all, dy_own = enter(spots, blocks, dy_pair, swap_c(dy_pair))
-    f_down = whole_rows(dy_all, product)
-    z_one, z_two, product, f_down, w_d[0] = tie(z_one, z_two, product, f_down, w_d[0])
-
-
-    f_down = scattered_all(f_down)
+    t_down = away(dy_all, product)
+    z_one, z_two, product, t_down, w_d[0] = tie(z_one, z_two, product, t_down, w_d[0])
+
+
+    down_a, down_b = pieces(t_down, 6)
+    down_a = sent_a(down_a)
     d_one, d_two, lean_m = gated_unit_back(spots, dy_all, z_one, z_two, w_d)
     sent = fold_half(spots, [d_one, d_two], [w_1, w_2])
-    sent, d_two, lean_m = tie(sent, d_two, lean_m)
+    sent, d_one, d_two, lean_m, down_a = tie(sent, d_one, d_two, lean_m, down_a)
 
     arrived = swap_c(sent)
-    t_two = away(hidden_two, d_two)
+    down_b = sent_a(down_b)
+    t_one = away(hidden_two, d_one)
     lean_m = total(lean_m[:, 0])
     sent, mine = fold_half(spots, [d_one, d_two], [w_1, w_2], arrived)
-    sent, d_one, t_two, product, lean_m = tie(sent, d_one, t_two, product, lean_m)
+    sent, d_two, t_one, product, lean_m, down_b = tie(sent, d_two, t_one, product, lean_m, down_b)
 
     crossed = swap_b(sent)
-    upper, lower = in_two(t_two)
-    upper = sent_a(upper)
-    f_one = whole_rows(hidden_two, d_one)
+    one_a, one_b = pieces(t_one, 6)
+    one_a = sent_a(one_a)
+    f_down = kept(dy_all, product, down_a, down_b)
+    t_two = away(hidden_two, d_two)
     result = fold_half(spots, [product], [w_d])
-    crossed, result, f_one, upper, f_down = tie(crossed, result, f_one, upper, f_down)
-
-    f_one = scattered_all(f_one)
+    crossed, result, f_down, t_two, one_a = tie(crossed, result, f_down, t_two, one_a)
+
+    f_down = scattered(f_down)
+    one_b = sent_a(one_b)
+    two_a, two_b = pieces(t_two, 3)
+    two_a = sent_a(two_a)
     d_hidden = mine + crossed.astype(F32)
     m_normed = middle * m_scale
     lean = lean_m[:, None] * (2.0 / width)
@@ -817,7 +820,6 @@
 
     arrived = swap_c(sent)
     r_result = swap_c(result)
-    y_down = spread_a(f_down)
     lean_o = total(lean_o)
     p_out = cross_tokens(lifted, (o_scale * d_middle).astype(LOW)).astype(LOW)
     p_out = jnp.transpose(p_out.reshape(shards, spread, part, -1), (1, 0, 2, 3))
@@ -826,16 +828,21 @@
     d_gated = times_transposed(d_branch, row_half(w_o, c)) + arrived.astype(F32)
     sent = columns(d_gated, (1 - b) * own, own).astype(LOW)
     mine = columns(d_gated, b * own, own)
-    sent, mine, r_result, t_out, lean_o, y_down = tie(sent, mine, r_result, t_out, lean_o, y_down)
+    sent, mine, d_one, r_result, t_out, lean_o, one_b, two_a = tie(
+        sent, mine, d_one, r_result, t_out, lean_o, one_b, two_a
+    )
 
     crossed = swap_b(sent)
+    two_b = sent_a(two_b)
+    f_one = kept(hidden_two, d_one, one_a, one_b)
+    result, result_mine = fold_half(spots, [product], [w_d], r_result)
+    crossed, result, f_one, f_down, two_b = tie(crossed, result, f_one, f_down, two_b)
+
+    f_one = scattered(f_one)
     r_out = sent_a(t_out[1:])
-    result, result_mine = fold_half(spots, [product], [w_d], r_result)
-    crossed, result, r_out, lower = tie(crossed, result, r_out, lower)
-
-    lower = sent_a(lower)
+    y_down = spread_a(f_down)
     result = swap_b(result)
-    f_out = scattered(sum([x.astype(F32) for x in r_out], t_out[0].astype(F32)).astype(LOW))
+    f_two = kept(hidden_two, d_two, two_a, two_b)
     o_normed = attended * o_scale
     d_gated = mine + crossed.astype(F32)
     d_gate = (d_gated * o_normed).astype(LOW)
@@ -845,66 +852,69 @@
     d_qk = joined(d_query, d_key)
     d_vg = joined(d_value, d_gate)
     t_qk = away(hidden_one, d_qk)
-    d_qk, d_vg, t_qk, lower, result = tie(d_qk, d_vg, t_qk, lower, result)
-
-    upper_qk, lower_qk = in_two(t_qk)
-    upper_qk = sent_a(upper_qk)
-    f_two = gradient_rows(spots, spread, 0, hidden_two, d_two, stacked(upper, lower))
+    d_qk, d_vg, t_qk, f_two, r_out, y_down, result = tie(d_qk, d_vg, t_qk, f_two, r_out, y_down, result)
+
+    f_two = scattered(f_two)
+    qk_a, qk_b = pieces(t_qk, 4)
+    qk_a = sent_a(qk_a)
     output = to_runs((middle + (result_mine + result.astype(F32))).astype(LOW))
+    x_down = swap_b(y_down)
+    y_one = over_spread(f_one)
     t_vg = away(hidden_one, d_vg)
     sent = fold_half(spots, [d_qk, d_vg], [w_qk, w_vg])
-    sent, t_vg, d_qk, d_vg, f_two, output, upper_qk, lower_qk = tie(
-        sent, t_vg, d_qk, d_vg, f_two, output, upper_qk, lower_qk
+    sent, t_vg, d_qk, d_vg, output, qk_a, x_down, y_one = tie(
+        sent, t_vg, d_qk, d_vg, output, qk_a, x_down, y_one
     )
 
-    f_two = scattered(f_two)
-    lower_qk = sent_a(lower_qk)
+    f_out = scattered(sum([x.astype(F32) for x in r_out], t_out[0].astype(F32)).astype(LOW))
     arrived = swap_c(sent)
+    qk_b = sent_a(qk_b)
+    x_down = joined(y_down, x_down)
+    y_one = by_spread([f_one, *y_one])
+    x_one = swap_b(y_one)
     lean_x = total(
         jnp.sum(z_qk * d_qk.astype(F32), axis=-1) + jnp.sum(z_vg * d_vg.astype(F32), axis=-1)
     )
     sent, mine = fold_half(spots, [d_qk, d_vg], [w_qk, w_vg], arrived)
-    sent, mine, lower_qk, t_vg, f_one, lean_x, y_down = tie(
-        sent, mine, lower_qk, t_vg, f_one, lean_x, y_down
-    )
+    sent, mine, qk_b, t_vg, lean_x, x_one = tie(sent, mine, qk_b, t_vg, lean_x, x_one)
 
     crossed = swap_b(sent)
     r_vg = sent_a(t_vg)
-    f_qk = scattered(gradient_rows(spots, spread, 0, hidden_one, d_qk, stacked(upper_qk, lower_qk)))
+    f_qk = scattered(kept(hidden_one, d_qk, qk_a, qk_b))
     output = bring_back(output)
-    x_one = spread_b(f_one)
-    crossed, d_vg, r_vg, x_one, output, y_down = tie(crossed, d_vg, r_vg, x_one, output, y_down)
-
-    f_vg = gradient_rows(spots, spread, 0, hidden_one, d_vg, r_vg)
-    f_vg, crossed, x_one, f_two, f_out, y_down = tie(f_vg, crossed, x_one, f_two, f_out, y_down)
+    four_down = spread_c(x_down)
+    crossed, d_vg, r_vg, output, f_two, four_down = tie(crossed, d_vg, r_vg, output, f_two, four_down)
+
+    f_vg = kept(hidden_one, d_vg, r_vg)
+    x_one = joined(y_one, x_one)
+    f_vg, crossed, f_two, f_out, x_one = tie(f_vg, crossed, f_two, f_out, x_one)
 
     f_vg = scattered(f_vg)
     d_hidden = mine + crossed.astype(F32)
     x_normed = x_own.astype(F32) * x_scale
     lean = lean_x[:, None] / width
     input_grad = to_runs((d_middle + x_scale * (d_hidden - x_normed * lean)).astype(LOW))
-    x_down = spread_b(y_down)
-    y_one = spread_a(x_one)
-    x_two = spread_b(f_two)
-    y_oqk = spread_a(joined(f_out, f_qk))
-    input_grad, x_down, y_one, x_two, y_oqk, f_vg = tie(input_grad, x_down, y_one, x_two, y_oqk, f_vg)
-
-    y_vg = spread_a(f_vg)
-    x_oqk = spread_b(y_oqk)
-    y_vg, x_oqk = tie(y_vg, x_oqk)
-
-    four_vg = spread_c(spread_b(y_vg))
+    f_oqk = joined(f_out, f_qk)
+    x_oqk = swap_b(f_oqk)
+    y_two = over_spread(f_two)
+    four_one = spread_c(x_one)
+    units = f_one.shape[1]
+    [g_down] = place_quarters(spots, four_down, (0, units))
+    [g_one] = place_quarters(spots, four_one, (0, units))
+    input_grad, x_oqk, y_two, f_vg, g_down, g_one = tie(input_grad, x_oqk, y_two, f_vg, g_down, g_one)
+
+    x_vg = spread_b(f_vg)
+    y_two = by_spread([f_two, *y_two])
+    y_oqk = spread_a(joined(f_oqk, x_oqk))
+    x_vg, y_oqk = tie(x_vg, y_oqk)
+
+    four_vg = spread_c(spread_a(x_vg))
     input_grad = bring_back(input_grad)
-    four_two = spread_c(spread_a(x_two))
-    four_one = spread_c(y_one)
-    four_down = spread_c(x_down)
-    four_oqk = spread_c(x_oqk)
-    units = f_one.shape[1]
+    four_two = spread_c(spread_b(y_two))
+    four_oqk = spread_c(y_oqk)
     g_query, g_key = place_quarters(spots, four_oqk, (own, own), (2 * own, own))
     g_value, g_gate = place_quarters(spots, four_vg, (0, own), (own, own))
-    [g_one] = place_quarters(spots, four_one, (0, units))
     [g_two] = place_quarters(spots, four_two, (0, units))
-    [g_down] = place_quarters(spots, four_down, (0, units))
     g_out = features_in_order(four_oqk, 0, own)
     return output, input_grad, g_query, g_key, g_value, g_gate, g_out, g_one, g_two, g_down
 

time: 1210 us -> 1210 us (level)
  waiting for transfers between devices: 445 us -> 484 us
  starting transfers between devices: 149 us -> 111 us
    ppermute x56 -> x60, waiting for transfers between devices: 218 us -> 260 us  [move(): return lax.ppermute(x, AXES, pairs)]
    ppermute x4, starting transfers between devices: 36.8 us -> 7.51 us  [bring_back(): lax.ppermute(lax.dynamic_index_in_dim(slots, (batch_of(place) + p) % 2, 0...]
    unnamed x195 -> x204, local copies, waits for them, and re-layouts: 66.8 us -> 55.5 us
    ppermute x56 -> x60, starting transfers between devices: 103 us -> 94.4 us  [move(): return lax.ppermute(x, AXES, pairs)]
    pallas_call x8 -> x10, Pallas kernels: 80.4 us -> 83.2 us  [gradient_rows(): pl.pallas_call(gradient_kernel, out_shape=out, grid_spec=pltpu.PrefetchSc...]
  transfers between devices with their start and end apart: 76 -> 80, of which waited for: 29 -> 30; matrix products, arithmetic and copies ran while one was open for 15% -> 15% of each run, Pallas kernels for 28% -> 28%
where the time goes in v7:
time: 1210 us; the launch traced here: 1200 us
  waiting for transfers between devices  484 us (40%)
  Pallas kernels  346 us (29%)
  starting transfers between devices  111 us (9%)
  other arithmetic  110 us (9%)
  local copies, waits for them, and re-layouts  99.5 us (8%)
  matrix products  33.8 us (3%)
  between operations  17.5 us (1%)
    ppermute x60, waiting for transfers between devices, move(): return lax.ppermute(x, AXES, pairs)  260 us
    ppermute x4, waiting for transfers between devices, bring(): lax.ppermute(lax.dynamic_index_in_dim(x, (place + p) % 2, 0, False), AXES...  119 us
    pallas_call x6, Pallas kernels, fold_half(): pl.pallas_call(functools.partial(fold_kernel, len(values), arrived is not...  99.4 us
    ppermute x60, starting transfers between devices, move(): return lax.ppermute(x, AXES, pairs)  94.4 us
    ppermute x4, waiting for transfers between devices, bring_back(): lax.ppermute(lax.dynamic_index_in_dim(slots, (batch_of(place) + p) % 2, 0...  87.5 us
    pallas_call x10, Pallas kernels, gradient_rows(): pl.pallas_call(gradient_kernel, out_shape=out, grid_spec=pltpu.PrefetchSc...  83.2 us
    unnamed x204, local copies, waits for them, and re-layouts  55.5 us
    select_n x22, other arithmetic, ordered(): jnp.where(index == 0, jnp.concatenate([mine, other], axis), jnp.concatena...  49.4 us
  transfers between devices with their start and end apart: 80, of which 30 were waited for; matrix products, arithmetic and copies ran while one was open for 15% of the time, Pallas kernels for 28%

profile of v7, /device:TPU:17, one launch (start us, length us, event | category | flops | bytes accessed | tf_op | source)
XLA Modules:
  0.0 1201.4 jit_solution(16491831726498630225)
XLA Ops:
  21.0 75.9 %collective-permute-done.2 = bf16[256,2048]{1,0:T(8,128)(2,1)S(1)} collective-permute-done((bf16[256,2048]{1,0:T(8,128)(2,1)}, bf16[256,2048]{1,0:T(8,128)(2,1)S(1)}, u32[]{:S(2)}, u32[]{:S(2)}) %collective-permute-start.2) | collective-permute-done | bytes 1048608 | tf_op jit(solution)/shard_map/ppermute | solution.py:594
  105.0 37.9 %collective-permute-done.4 = bf16[512,2048]{1,0:T(8,128)(2,1)} collective-permute-done((bf16[512,2048]{1,0:T(8,128)(2,1)}, bf16[512,2048]{1,0:T(8,128)(2,1)}, u32[]{:S(2)}, u32[]{:S(2)}) %collective-permute-start.4) | collective-permute-done | bytes 2097184 | tf_op jit(solution)/shard_map/ppermute | solution.py:543
  164.6 19.8 %enter.2 = (bf16[2048,2048]{1,0:T(8,128)(2,1)}, f32[2048,1024]{1,0:T(8,128)}, f32[2048,1]{1,0:T(8,128)S(1)}, bf16[2048,512]{1,0:T(8,128)(2,1)S(1)}) custom-call(s32[4]{0:T(128)S(1)} %pad_add_fusion.1.spots, bf16[1024,2048]{1,0:T(8,128)(2,1)S(1)} %copy-done.19, bf16[1024,2048]{1,0:T(8,128)(2,1)} %collective-permute-done.6.other_ref, ...), custom_call_target="tpu_custom_call" | custom-call | flops 8589934592 | bytes 31465472 | tf_op jit(solution)/shard_map/enter/pallas_call | solution.py:244
  185.7 15.5 %collective-permute-done.7.refs_1_.refs_5_.refs_6_ = bf16[1024,1024]{1,0:T(8,128)(2,1)} collective-permute-done((bf16[1024,1024]{1,0:T(8,128)(2,1)}, bf16[1024,1024]{1,0:T(8,128)(2,1)}, u32[]{:S(2)}, u32[]{:S(2)}) %collective-permute-start.7) | collective-permute-done | bytes 2097184 | tf_op jit(solution)/shard_map/ppermute | solution.py:543
  204.1 14.2 %project.1.zv_ref = f32[2048,1024]{1,0:T(8,128)S(1)} custom-call(s32[4]{0:T(128)S(1)} %pad_add_fusion.1.spots, bf16[2048,2048]{1,0:T(8,128)(2,1)} %get-tuple-element.150.h_ref.left_ref, bf16[1024,1024]{1,0:T(8,128)(2,1)S(1)} %copy-done.46, bf16[1024,1024]{1,0:T(8,128)(2,1)} %collective-permute-done.7.refs_1_.refs_5_.refs_6_), custom_call_target="tpu_custom_call" | custom-call | flops 8589934592 | bytes 20971520 | tf_op jit(solution)/shard_map/project/pallas_call | solution.py:275
  221.8 12.3 %attend.1 = f32[2048,512]{1,0:T(8,128)S(1)} custom-call(f32[4]{0:T(128)S(1)} %dynamic_slice.118.rates, s32[2,2]{1,0:T(2,128)S(1)} %pad_add_fusion.ends, f32[2048,1024]{1,0:T(8,128)S(1)} %copy-done.2, f32[2048,1024]{1,0:T(8,128)S(1)} %copy-done.2, f32[2048,1024]{1,0:T(8,128)} %copy-done.3), custom_call_target="tpu_custom_call" | custom-call | flops 4294967296 | bytes 16777216 | tf_op jit(solution)/shard_map/attend/pallas_call | solution.py:98
  243.2 42.0 %collective-permute-done.12 = f32[2048]{0:T(1024)S(1)} collective-permute-done((f32[2048]{0:T(1024)S(1)}, f32[2048]{0:T(1024)S(1)}, u32[]{:S(2)}, u32[]{:S(2)}) %collective-permute-start.12) | collective-permute-done | bytes 8224 | tf_op jit(solution)/shard_map/ppermute | solution.py:543
  293.0 9.1 collective-permute-done.10.refs_1_.refs_3_.refs_4_
  311.3 12.2 %fusion.21 = (bf16[2048,512]{1,0:T(8,128)(2,1)S(1)}, f32[2048,512]{1,0:T(8,128)}) fusion(f32[2048]{0:T(1024)S(1)} %add_rsqrt_fusion, bf16[2048,512]{1,0:T(8,128)(2,1)S(1)} %copy-done.12, bf16[2048,512]{1,0:T(8,128)(2,1)S(1)} %bitcast.70, bf16[2048,1024]{1,0:T(8,128)(2,1)} %collective-permute-done.13, bf16[2048,1024]{1,0:T(8,128)(2,1)} %maximum_select_fusion.2, ...), kind=kOutput, calls=%fused_computation.140 | convolution fusion | flops 4336910336 | bytes 18882560 | tf_op jit(solution)/shard_map/dot_general | solution.py:24
  330.0 43.1 %collective-permute-done.16 = bf16[256,2048]{1,0:T(8,128)(2,1)S(1)} collective-permute-done((bf16[256,2048]{1,0:T(8,128)(2,1)S(1)}, bf16[256,2048]{1,0:T(8,128)(2,1)S(1)}, u32[]{:S(2)}, u32[]{:S(2)}) %collective-permute-start.16) | collective-permute-done | bytes 1048608 | tf_op jit(solution)/shard_map/ppermute | solution.py:594
  392.3 38.1 %gated_unit.1 = (bf16[2048,2048]{1,0:T(8,128)(2,1)}, bf16[2048,1408]{1,0:T(8,128)(2,1)}, bf16[2048,1408]{1,0:T(8,128)(2,1)}, bf16[2048,1408]{1,0:T(8,128)(2,1)}, f32[2048,1]{1,0:T(8,128)S(1)}) custom-call(s32[4]{0:T(128)S(1)} %pad_add_fusion.1.spots, bf16[2048,1024]{1,0:T(8,128)(2,1)} %maximum_select_fusion.3.own_ref, ...), custom_call_target="tpu_custom_call" | custom-call | flops 23622320128 | bytes 45621248 | tf_op jit(solution)/shard_map/gated_unit/pallas_call | solution.py:337
  438.2 6.8 collective-permute-done.20.other_ref
  451.6 9.2 gradient_rows.10
  462.4 12.1 %all-gather.17.cloned.1.call-done.refs_0_.refs_1_.refs_2_ = bf16[2048,1408]{1,0:T(8,128)(2,1)} async-done(((bf16[256,1408]{1,0:T(8,128)(2,1)}), bf16[2048,1408]{1,0:T(8,128)(2,1)}) %all-gather.17.cloned.1.call-update) | async-done | bytes 5767184 | tf_op jit(solution)/shard_map/all_gather | solution.py:658
  477.9 22.5 %gated_unit_back.1 = (bf16[2048,1408]{1,0:T(8,128)(2,1)S(1)}, bf16[2048,1408]{1,0:T(8,128)(2,1)S(1)}, f32[2048,1]{1,0:T(8,128)S(1)}) custom-call(s32[4]{0:T(128)S(1)} %pad_add_fusion.1.spots, bf16[2048,2048]{1,0:T(8,128)(2,1)} %get-tuple-element.172.left_ref.dy_ref, bf16[2048,1408]{1,0:T(8,128)(2,1)} %get-tuple-element.176.one_ref, ...), custom_call_target="tpu_custom_call" | custom-call | flops 11811160064 | bytes 37232640 | tf_op jit(solution)/shard_map/gated_unit_back/pallas_call | solution.py:374
  506.3 19.8 %fold_half.6 = bf16[2048,1024]{1,0:T(8,128)(2,1)} custom-call(s32[4]{0:T(128)S(1)} %pad_add_fusion.1.spots, bf16[2048,1408]{1,0:T(8,128)(2,1)} %copy-done.53, bf16[2048,1408]{1,0:T(8,128)(2,1)} %copy-done.50, bf16[1024,1408]{1,0:T(8,128)(2,1)S(1)} %copy-done.35, bf16[1024,1408]{1,0:T(8,128)(2,1)} %collective-permute-done.10.refs_1_.refs_3_.refs_4_, ...), custom_call_target="tpu_custom_call" | custom-call | flops 11811160064 | bytes 21495808 | tf_op jit(solution)/shard_map/fold_half/pallas_call | solution.py:435
  540.0 9.4 gradient_rows.11
  549.5 22.1 %fold_half.7 = (bf16[2048,512]{1,0:T(8,128)(2,1)S(1)}, f32[2048,512]{1,0:T(8,128)}) custom-call(s32[4]{0:T(128)S(1)} %pad_add_fusion.1.spots, bf16[2048,1408]{1,0:T(8,128)(2,1)} %copy-done.53, bf16[2048,1408]{1,0:T(8,128)(2,1)} %copy-done.50, bf16[2048,1024]{1,0:T(8,128)(2,1)} %collective-permute-done.22.refs_2_, bf16[1024,1408]{1,0:T(8,128)(2,1)S(1)} %copy-done.36, ...), custom_call_target="tpu_custom_call" | custom-call | flops 11811160064 | bytes 27787264 | tf_op jit(solution)/shard_map/fold_half/pallas_call | solution.py:435
  577.9 11.4 fold_half.8
  589.3 9.1 gradient_rows.12
  602.6 9.4 gradient_rows.13
  612.0 8.4 collective-permute-done.26
  637.8 12.6 %convolution_convert_fusion.1 = bf16[2048,512]{1,0:T(8,128)(2,1)S(1)} fusion(f32[2048,512]{1,0:T(8,128)} %copy-done.55, f32[2048]{0:T(1024)S(1)} %add_rsqrt_fusion, bf16[2048,1024]{1,0:T(8,128)(2,1)} %collective-permute-done.13, bf16[2048,1024]{1,0:T(8,128)(2,1)} %maximum_select_fusion.2, pred[]{:T(512)S(6)} %eq.50), kind=kOutput, calls=%fused_computation.28 | convolution fusion | flops 4335861760 | bytes 14688257 | tf_op jit(solution)/shard_map/dot_general | solution.py:32
  662.8 11.9 collective-permute-done.33
  679.6 13.9 %fold_half.9 = (bf16[2048,512]{1,0:T(8,128)(2,1)}, f32[2048,512]{1,0:T(8,128)S(1)}) custom-call(s32[4]{0:T(128)S(1)} %pad_add_fusion.1.spots, bf16[2048,1408]{1,0:T(8,128)(2,1)} %get-tuple-element.192.right_ref.refs_0_, bf16[2048,1024]{1,0:T(8,128)(2,1)} %collective-permute-done.29.refs_1_, ...), custom_call_target="tpu_custom_call" | custom-call | flops 5905580032 | bytes 16252928 | tf_op jit(solution)/shard_map/fold_half/pallas_call | solution.py:435
  695.6 9.1 gradient_rows.14
  706.4 10.6 collective-permute-done.35
  723.8 6.6 multiply_convert_fusion
  730.4 21.3 %attend_back.1 = (bf16[2048,512]{1,0:T(8,128)(2,1)S(1)}, bf16[2048,512]{1,0:T(8,128)(2,1)S(1)}, bf16[2048,512]{1,0:T(8,128)(2,1)S(1)}) custom-call(f32[4]{0:T(128)S(1)} %dynamic_slice.118.rates, s32[2,2]{1,0:T(2,128)S(1)} %pad_add_fusion.ends, f32[2048,1024]{1,0:T(8,128)} %get-tuple-element.149.zq_ref.zk_ref, f32[2048,1024]{1,0:T(8,128)} %get-tuple-element.149.zq_ref.zk_ref, ...), custom_call_target="tpu_custom_call" | custom-call | flops 10737418240 | bytes 20971520 | tf_op jit(solution)/shard_map/attend_back/pallas_call | solution.py:119
  756.6 6.9 gradient_rows.15
  767.5 9.3 gradient_rows.16
  791.2 19.0 %collective-permute-done.39 = bf16[2,512,512]{2,1,0:T(8,128)(2,1)} collective-permute-done((bf16[2,512,512]{2,1,0:T(8,128)(2,1)}, bf16[2,512,512]{2,1,0:T(8,128)(2,1)}, u32[]{:S(2)}, u32[]{:S(2)}) %collective-permute-start.39) | collective-permute-done | bytes 1048608 | tf_op jit(solution)/shard_map/ppermute | solution.py:543
  814.0 7.4 collective-permute-start.40
  823.3 14.7 %fold_half.10 = bf16[2048,1024]{1,0:T(8,128)(2,1)} custom-call(s32[4]{0:T(128)S(1)} %pad_add_fusion.1.spots, bf16[2048,1024]{1,0:T(8,128)(2,1)} %copy-done.7, bf16[2048,1024]{1,0:T(8,128)(2,1)} %pad_maximum_fusion.refs_1_.right_ref, bf16[1024,1024]{1,0:T(8,128)(2,1)S(1)} %copy-done.44, bf16[1024,1024]{1,0:T(8,128)(2,1)} %collective-permute-done.5.refs_1_.refs_3_.refs_4_, ...), custom_call_target="tpu_custom_call" | custom-call | flops 8589934592 | bytes 16777216 | tf_op jit(solution)/shard_map/fold_half/pallas_call | solution.py:435
  838.0 6.9 gradient_rows.17
  874.3 16.4 %collective-permute-done.47 = f32[2048]{0:T(1024)S(1)} collective-permute-done((f32[2048]{0:T(1024)S(1)}, f32[2048]{0:T(1024)S(1)}, u32[]{:S(2)}, u32[]{:S(2)}) %collective-permute-start.47) | collective-permute-done | bytes 8224 | tf_op jit(solution)/shard_map/ppermute | solution.py:543
  890.7 17.5 %fold_half.11 = (bf16[2048,512]{1,0:T(8,128)(2,1)}, f32[2048,512]{1,0:T(8,128)}) custom-call(s32[4]{0:T(128)S(1)} %pad_add_fusion.1.spots, bf16[2048,1024]{1,0:T(8,128)(2,1)} %copy-done.7, bf16[2048,1024]{1,0:T(8,128)(2,1)} %pad_maximum_fusion.refs_1_.right_ref, bf16[2048,1024]{1,0:T(8,128)(2,1)} %collective-permute-done.44.refs_2_, ...), custom_call_target="tpu_custom_call" | custom-call | flops 8589934592 | bytes 23068672 | tf_op jit(solution)/shard_map/fold_half/pallas_call | solution.py:435
  911.2 6.9 gradient_rows.19
  929.0 63.6 %collective-permute-done.51 = bf16[256,2048]{1,0:T(8,128)(2,1)} collective-permute-done((bf16[256,2048]{1,0:T(8,128)(2,1)}, bf16[256,2048]{1,0:T(8,128)(2,1)}, u32[]{:S(2)}, u32[]{:S(2)}) %collective-permute-start.51) | collective-permute-done | bytes 1048608 | tf_op jit(solution)/shard_map/ppermute | solution.py:602
  1000.4 6.9 gradient_rows.18
  1009.1 11.0 collective-permute-start.58
  1026.1 22.4 %collective-permute-done.54 = bf16[2,512,512]{2,1,0:T(8,128)(2,1)S(1)} collective-permute-done((bf16[2,512,512]{2,1,0:T(8,128)(2,1)S(1)}, bf16[2,512,512]{2,1,0:T(8,128)(2,1)S(1)}, u32[]{:S(2)}, u32[]{:S(2)}) %collective-permute-start.54) | collective-permute-done | bytes 1048608 | tf_op jit(solution)/shard_map/ppermute | solution.py:543
  1055.9 7.8 place_quarters.5
  1067.5 7.1 place_quarters.6
  1080.5 9.3 collective-permute-done.61
  1089.9 22.5 %collective-permute-done.62 = bf16[256,3072]{1,0:T(8,128)(2,1)S(1)} collective-permute-done((bf16[256,3072]{1,0:T(8,128)(2,1)}, bf16[256,3072]{1,0:T(8,128)(2,1)S(1)}, u32[]{:S(2)}, u32[]{:S(2)}) %collective-permute-start.62) | collective-permute-done | bytes 1572896 | tf_op jit(solution)/shard_map/ppermute | solution.py:543
  1128.9 22.3 %collective-permute-done.59 = bf16[256,2048]{1,0:T(8,128)(2,1)S(1)} collective-permute-done((bf16[256,2048]{1,0:T(8,128)(2,1)S(1)}, bf16[256,2048]{1,0:T(8,128)(2,1)S(1)}, u32[]{:S(2)}, u32[]{:S(2)}) %collective-permute-start.59) | collective-permute-done | bytes 1048608 | tf_op jit(solution)/shard_map/ppermute | solution.py:602
  1155.6 19.3 %collective-permute-start.65 = (bf16[512,2048]{1,0:T(8,128)(2,1)S(1)}, bf16[512,2048]{1,0:T(8,128)(2,1)S(1)}, u32[]{:S(2)}, u32[]{:S(2)}) collective-permute-start(bf16[512,2048]{1,0:T(8,128)(2,1)S(1)} %maximum_select_fusion.15.refs_0_.refs_1_), channel_id=1, source_target_pairs={{0,4},{1,5},{2,6},{3,7},{4,0},{5,1},{6,2},{7,3},{8,12},{9,13},{10,... | collective-permute-start | bytes 6291464 | tf_op jit(solution)/shard_map/ppermute | solution.py:543
  (465 shorter events, 340.1 us)
Async XLA Ops:
  8.0 91.2 %all-gather.7.cloned.1.call-start = ((), (), s32[]{:S(2)}) async-start(), calls=%async_computation.6 | async-start | bytes 2621440 | tf_op jit(solution)/shard_map/all_gather | solution.py:654
  11.6 137.3 %all-gather.9.cloned.1.call-start = ((), (), s32[]{:S(2)}) async-start(), calls=%async_computation.7 | async-start | bytes 2621440 | tf_op jit(solution)/shard_map/all_gather | solution.py:654
  14.8 171.0 %all-gather.11.cloned.1.call-start = ((), (), s32[]{:S(2)}) async-start(), calls=%async_computation.8 | async-start | bytes 1310720 | tf_op jit(solution)/shard_map/all_gather | solution.py:654
  16.0 80.9 %collective-permute-start.2 = (bf16[256,2048]{1,0:T(8,128)(2,1)}, bf16[256,2048]{1,0:T(8,128)(2,1)S(1)}, u32[]{:S(2)}, u32[]{:S(2)}) collective-permute-start(bf16[256,2048]{1,0:T(8,128)(2,1)} %get-tuple-element.304), channel_id=1, source_target_pairs={{0,0},{4,1},{1,2},{5,3},{2,4},{6,5},{3,6},{7,7},{8,8},{12,9},{9,10... | collective-permute-start | bytes 3145736 | tf_op jit(solution)/shard_map/ppermute | solution.py:594
  18.1 78.8 %collective-permute-start.3 = (bf16[256,2048]{1,0:T(8,128)(2,1)S(1)}, bf16[256,2048]{1,0:T(8,128)(2,1)S(1)}, u32[]{:S(2)}, u32[]{:S(2)}) collective-permute-start(bf16[256,2048]{1,0:T(8,128)(2,1)S(1)} %get-tuple-element.305), channel_id=1, source_target_pairs={{1,0},{5,1},{0,2},{4,3},{3,4},{7,5},{2,6},{6,7},{9,8},{13,9},{8,10... | collective-permute-start | bytes 3145736 | tf_op jit(solution)/shard_map/ppermute | solution.py:594
  99.2 43.7 %collective-permute-start.4 = (bf16[512,2048]{1,0:T(8,128)(2,1)}, bf16[512,2048]{1,0:T(8,128)(2,1)}, u32[]{:S(2)}, u32[]{:S(2)}) collective-permute-start(bf16[512,2048]{1,0:T(8,128)(2,1)} %maximum_select_fusion.6), channel_id=1, source_target_pairs={{0,8},{1,9},{2,10},{3,11},{4,12},{5,13},{6,14},{7,15},{8,0},{9,1},... | collective-permute-start | bytes 6291464 | tf_op jit(solution)/shard_map/ppermute | solution.py:543
  101.2 137.7 %all-gather.13.cloned.1.call-start = ((), (), s32[]{:S(2)}) async-start(), calls=%async_computation.9 | async-start | bytes 3604480 | tf_op jit(solution)/shard_map/all_gather | solution.py:654
  101.2 47.8 %collective-permute-start.5 = (bf16[1024,1024]{1,0:T(8,128)(2,1)}, bf16[1024,1024]{1,0:T(8,128)(2,1)}, u32[]{:S(2)}, u32[]{:S(2)}) collective-permute-start(bf16[1024,1024]{1,0:T(8,128)(2,1)} %all-gather.7.cloned.1.call-done.refs_0_.refs_2_.refs_3_), channel_id=1, source_target_pairs={{0,16},{1,17},{2,18},{3,19},{4,20},{5,21},{6,22},{7,23},{8,24},{9,... | collective-permute-start | bytes 6291464 | tf_op jit(solution)/shard_map/ppermute | solution.py:543
  104.9 188.1 %all-gather.15.cloned.1.call-start = ((), (), s32[]{:S(2)}) async-start(), calls=%async_computation.10 | async-start | bytes 3604480 | tf_op jit(solution)/shard_map/all_gather | solution.py:654
  153.7 47.5 %collective-permute-start.7 = (bf16[1024,1024]{1,0:T(8,128)(2,1)}, bf16[1024,1024]{1,0:T(8,128)(2,1)}, u32[]{:S(2)}, u32[]{:S(2)}) collective-permute-start(bf16[1024,1024]{1,0:T(8,128)(2,1)} %all-gather.9.cloned.1.call-done.refs_0_.refs_4_.refs_5_), channel_id=1, source_target_pairs={{0,16},{1,17},{2,18},{3,19},{4,20},{5,21},{6,22},{7,23},{8,24},{9,... | collective-permute-start | bytes 6291464 | tf_op jit(solution)/shard_map/ppermute | solution.py:543
  159.9 314.6 %all-gather.17.cloned.1.call-start = ((), (), s32[]{:S(2)}) async-start(), calls=%async_computation.11 | async-start | bytes 6488064 | tf_op jit(solution)/shard_map/all_gather | solution.py:658
  238.9 63.2 %collective-permute-start.10 = (bf16[1024,1408]{1,0:T(8,128)(2,1)}, bf16[1024,1408]{1,0:T(8,128)(2,1)}, u32[]{:S(2)}, u32[]{:S(2)}) collective-permute-start(bf16[1024,1408]{1,0:T(8,128)(2,1)} %all-gather.13.cloned.1.call-done.refs_0_.refs_2_.refs_3_), channel_id=1, source_target_pairs={{0,16},{1,17},{2,18},{3,19},{4,20},{5,21},{6,22},{7,23},{8,24},{9,... | collective-permute-start | bytes 8650760 | tf_op jit(solution)/shard_map/ppermute | solution.py:543
  239.2 46.0 %collective-permute-start.9 = (bf16[2048,512]{1,0:T(8,128)(2,1)S(1)}, bf16[2048,512]{1,0:T(8,128)(2,1)S(1)}, u32[]{:S(2)}, u32[]{:S(2)}) collective-permute-start(bf16[2048,512]{1,0:T(8,128)(2,1)S(1)} %get-tuple-element.153), channel_id=1, source_target_pairs={{0,8},{1,9},{2,10},{3,11},{4,12},{5,13},{6,14},{7,15},{8,0},{9,1},... | collective-permute-start | bytes 6291464 | tf_op jit(solution)/shard_map/ppermute | solution.py:543
  242.9 42.2 %collective-permute-start.12 = (f32[2048]{0:T(1024)S(1)}, f32[2048]{0:T(1024)S(1)}, u32[]{:S(2)}, u32[]{:S(2)}) collective-permute-start(f32[2048]{0:T(1024)S(1)} %add.256), channel_id=1, source_target_pairs={{0,8},{1,9},{2,10},{3,11},{4,12},{5,13},{6,14},{7,15},{8,0},{9,1},... | collective-permute-start | bytes 24584 | tf_op jit(solution)/shard_map/ppermute | solution.py:543
  307.3 70.8 %collective-permute-start.15 = (bf16[1024,1408]{1,0:T(8,128)(2,1)S(1)}, bf16[1024,1408]{1,0:T(8,128)(2,1)S(1)}, u32[]{:S(2)}, u32[]{:S(2)}) collective-permute-start(bf16[1024,1408]{1,0:T(8,128)(2,1)S(1)} %copy-done.37), channel_id=1, source_target_pairs={{0,16},{1,17},{2,18},{3,19},{4,20},{5,21},{6,22},{7,23},{8,24},{9,... | collective-permute-start | bytes 8650760 | tf_op jit(solution)/shard_map/ppermute | solution.py:543
  323.5 51.9 %collective-permute-start.14 = (bf16[2048,512]{1,0:T(8,128)(2,1)S(1)}, bf16[2048,512]{1,0:T(8,128)(2,1)S(1)}, u32[]{:S(2)}, u32[]{:S(2)}) collective-permute-start(bf16[2048,512]{1,0:T(8,128)(2,1)S(1)} %get-tuple-element.308), channel_id=1, source_target_pairs={{0,8},{1,9},{2,10},{3,11},{4,12},{5,13},{6,14},{7,15},{8,0},{9,1},... | collective-permute-start | bytes 6291464 | tf_op jit(solution)/shard_map/ppermute | solution.py:543
  324.9 48.2 %collective-permute-start.16 = (bf16[256,2048]{1,0:T(8,128)(2,1)S(1)}, bf16[256,2048]{1,0:T(8,128)(2,1)S(1)}, u32[]{:S(2)}, u32[]{:S(2)}) collective-permute-start(bf16[256,2048]{1,0:T(8,128)(2,1)S(1)} %get-tuple-element.300), channel_id=1, source_target_pairs={{0,0},{4,1},{1,2},{5,3},{2,4},{6,5},{3,6},{7,7},{8,8},{12,9},{9,10... | collective-permute-start | bytes 3145736 | tf_op jit(solution)/shard_map/ppermute | solution.py:594
  330.0 43.2 %collective-permute-start.17 = (bf16[256,2048]{1,0:T(8,128)(2,1)S(1)}, bf16[256,2048]{1,0:T(8,128)(2,1)S(1)}, u32[]{:S(2)}, u32[]{:S(2)}) collective-permute-start(bf16[256,2048]{1,0:T(8,128)(2,1)S(1)} %get-tuple-element.301), channel_id=1, source_target_pairs={{1,0},{5,1},{0,2},{4,3},{3,4},{7,5},{2,6},{6,7},{9,8},{13,9},{8,10... | collective-permute-start | bytes 3145736 | tf_op jit(solution)/shard_map/ppermute | solution.py:594
  385.5 331.4 %reduce-scatter.7.cloned.1.call-start = ((), (), s32[]{:S(2)}) async-start(), calls=%async_computation.12 | async-start | bytes 3604480 | tf_op jit(solution)/shard_map/reduce_scatter | solution.py:695
  385.7 47.6 %collective-permute-start.19 = (bf16[512,2048]{1,0:T(8,128)(2,1)}, bf16[512,2048]{1,0:T(8,128)(2,1)S(1)}, u32[]{:S(2)}, u32[]{:S(2)}) collective-permute-start(bf16[512,2048]{1,0:T(8,128)(2,1)} %maximum_select_fusion.8), channel_id=1, source_target_pairs={{0,8},{1,9},{2,10},{3,11},{4,12},{5,13},{6,14},{7,15},{8,0},{9,1},... | collective-permute-start | bytes 6291464 | tf_op jit(solution)/shard_map/ppermute | solution.py:543
  477.6 48.6 %collective-permute-start.21 = (bf16[768,1408]{1,0:T(8,128)(2,1)}, bf16[768,1408]{1,0:T(8,128)(2,1)}, u32[]{:S(2)}, u32[]{:S(2)}) collective-permute-start(bf16[768,1408]{1,0:T(8,128)(2,1)} %slice.120), channel_id=1, source_target_pairs={{0,16},{1,17},{2,18},{3,19},{4,20},{5,21},{6,22},{7,23},{8,24},{9,... | collective-permute-start | bytes 6488072 | tf_op jit(solution)/shard_map/ppermute | solution.py:543
  573.1 47.3 %collective-permute-start.26 = (bf16[2048,512]{1,0:T(8,128)(2,1)S(1)}, bf16[2048,512]{1,0:T(8,128)(2,1)}, u32[]{:S(2)}, u32[]{:S(2)}) collective-permute-start(bf16[2048,512]{1,0:T(8,128)(2,1)S(1)} %get-tuple-element.191), channel_id=1, source_target_pairs={{0,8},{1,9},{2,10},{3,11},{4,12},{5,13},{6,14},{7,15},{8,0},{9,1},... | collective-permute-start | bytes 6291464 | tf_op jit(solution)/shard_map/ppermute | solution.py:543
  573.4 49.0 %collective-permute-start.27 = (bf16[768,1408]{1,0:T(8,128)(2,1)}, bf16[768,1408]{1,0:T(8,128)(2,1)}, u32[]{:S(2)}, u32[]{:S(2)}) collective-permute-start(bf16[768,1408]{1,0:T(8,128)(2,1)} %slice.122), channel_id=1, source_target_pairs={{0,16},{1,17},{2,18},{3,19},{4,20},{5,21},{6,22},{7,23},{8,24},{9,... | collective-permute-start | bytes 6488072 | tf_op jit(solution)/shard_map/ppermute | solution.py:543
  631.7 43.0 %collective-permute-start.29 = (bf16[2048,1024]{1,0:T(8,128)(2,1)}, bf16[2048,1024]{1,0:T(8,128)(2,1)}, u32[]{:S(2)}, u32[]{:S(2)}) collective-permute-start(bf16[2048,1024]{1,0:T(8,128)(2,1)} %fold_half.8), channel_id=1, source_target_pairs={{0,4},{1,5},{2,6},{3,7},{4,0},{5,1},{6,2},{7,3},{8,12},{9,13},{10,... | collective-permute-start | bytes 12582920 | tf_op jit(solution)/shard_map/ppermute | solution.py:543
  634.2 187.2 %reduce-scatter.9.cloned.1.call-start = ((), (), s32[]{:S(2)}) async-start(), calls=%async_computation.13 | async-start | bytes 3604480 | tf_op jit(solution)/shard_map/reduce_scatter | solution.py:695
  635.5 39.2 %collective-permute-start.33 = (bf16[384,1408]{1,0:T(8,128)(2,1)S(1)}, bf16[384,1408]{1,0:T(8,128)(2,1)S(1)}, u32[]{:S(2)}, u32[]{:S(2)}) collective-permute-start(bf16[384,1408]{1,0:T(8,128)(2,1)S(1)} %slice.124), channel_id=1, source_target_pairs={{0,16},{1,17},{2,18},{3,19},{4,20},{5,21},{6,22},{7,23},{8,24},{9,... | collective-permute-start | bytes 3244040 | tf_op jit(solution)/shard_map/ppermute | solution.py:543
  674.7 46.3 %collective-permute-start.34 = (bf16[2048,512]{1,0:T(8,128)(2,1)}, bf16[2048,512]{1,0:T(8,128)(2,1)}, u32[]{:S(2)}, u32[]{:S(2)}) collective-permute-start(bf16[2048,512]{1,0:T(8,128)(2,1)} %dynamic-slice_convert_fusion), channel_id=1, source_target_pairs={{0,8},{1,9},{2,10},{3,11},{4,12},{5,13},{6,14},{7,15},{8,0},{9,1},... | collective-permute-start | bytes 6291464 | tf_op jit(solution)/shard_map/ppermute | solution.py:543
  677.3 39.7 %collective-permute-start.35 = (bf16[640,1408]{1,0:T(8,128)(2,1)}, bf16[640,1408]{1,0:T(8,128)(2,1)}, u32[]{:S(2)}, u32[]{:S(2)}) collective-permute-start(bf16[640,1408]{1,0:T(8,128)(2,1)} %slice.125), channel_id=1, source_target_pairs={{0,16},{1,17},{2,18},{3,19},{4,20},{5,21},{6,22},{7,23},{8,24},{9,... | collective-permute-start | bytes 5406728 | tf_op jit(solution)/shard_map/ppermute | solution.py:543
  721.0 277.2 %reduce-scatter.11.cloned.1.call-start = ((), (), s32[]{:S(2)}) async-start(), calls=%async_computation.14 | async-start | bytes 3604480 | tf_op jit(solution)/shard_map/reduce_scatter | solution.py:695
  721.1 60.7 %collective-permute-start.36 = (bf16[1024,512]{1,0:T(8,128)(2,1)}, bf16[1024,512]{1,0:T(8,128)(2,1)}, u32[]{:S(2)}, u32[]{:S(2)}) collective-permute-start(bf16[1024,512]{1,0:T(8,128)(2,1)} %get-tuple-element.220), channel_id=1, source_target_pairs={{0,16},{1,17},{2,18},{3,19},{4,20},{5,21},{6,22},{7,23},{8,24},{9,... | collective-permute-start | bytes 3145736 | tf_op jit(solution)/shard_map/ppermute | solution.py:543
  721.2 57.2 %collective-permute-start.37 = (bf16[256,1408]{1,0:T(8,128)(2,1)}, bf16[256,1408]{1,0:T(8,128)(2,1)}, u32[]{:S(2)}, u32[]{:S(2)}) collective-permute-start(bf16[256,1408]{1,0:T(8,128)(2,1)} %reduce-scatter.7.cloned.1.call-done), channel_id=1, source_target_pairs={{0,16},{1,17},{2,18},{3,19},{4,20},{5,21},{6,22},{7,23},{8,24},{9,... | collective-permute-start | bytes 2162696 | tf_op jit(solution)/shard_map/ppermute | solution.py:543
  722.6 59.2 %collective-permute-start.38 = (bf16[2048,512]{1,0:T(8,128)(2,1)}, bf16[2048,512]{1,0:T(8,128)(2,1)}, u32[]{:S(2)}, u32[]{:S(2)}) collective-permute-start(bf16[2048,512]{1,0:T(8,128)(2,1)} %get-tuple-element.222), channel_id=1, source_target_pairs={{0,8},{1,9},{2,10},{3,11},{4,12},{5,13},{6,14},{7,15},{8,0},{9,1},... | collective-permute-start | bytes 6291464 | tf_op jit(solution)/shard_map/ppermute | solution.py:543
  781.8 226.9 %reduce-scatter.13.cloned.1.call-start = ((), (), s32[]{:S(2)}) async-start(), calls=%async_computation.15 | async-start | bytes 1310720 | tf_op jit(solution)/shard_map/reduce_scatter | solution.py:695
  788.2 61.2 %collective-permute-start.42 = (bf16[512,1408]{1,0:T(8,128)(2,1)}, bf16[512,1408]{1,0:T(8,128)(2,1)}, u32[]{:S(2)}, u32[]{:S(2)}) collective-permute-start(bf16[512,1408]{1,0:T(8,128)(2,1)} %maximum_select_fusion.17), channel_id=1, source_target_pairs={{0,8},{1,9},{2,10},{3,11},{4,12},{5,13},{6,14},{7,15},{8,0},{9,1},... | collective-permute-start | bytes 4325384 | tf_op jit(solution)/shard_map/ppermute | solution.py:543
  791.2 58.2 %collective-permute-start.41 = (bf16[512,1024]{1,0:T(8,128)(2,1)}, bf16[512,1024]{1,0:T(8,128)(2,1)}, u32[]{:S(2)}, u32[]{:S(2)}) collective-permute-start(bf16[512,1024]{1,0:T(8,128)(2,1)} %get-tuple-element.293), channel_id=1, source_target_pairs={{0,16},{1,17},{2,18},{3,19},{4,20},{5,21},{6,22},{7,23},{8,24},{9,... | collective-permute-start | bytes 3145736 | tf_op jit(solution)/shard_map/ppermute | solution.py:543
  849.4 41.3 %collective-permute-start.44 = (bf16[2048,1024]{1,0:T(8,128)(2,1)}, bf16[2048,1024]{1,0:T(8,128)(2,1)}, u32[]{:S(2)}, u32[]{:S(2)}) collective-permute-start(bf16[2048,1024]{1,0:T(8,128)(2,1)} %fold_half.10), channel_id=1, source_target_pairs={{0,4},{1,5},{2,6},{3,7},{4,0},{5,1},{6,2},{7,3},{8,12},{9,13},{10,... | collective-permute-start | bytes 12582920 | tf_op jit(solution)/shard_map/ppermute | solution.py:543
  855.1 197.3 %reduce-scatter.15.cloned.1.call-start = ((), (), s32[]{:S(2)}) async-start(), calls=%async_computation.16 | async-start | bytes 2621440 | tf_op jit(solution)/shard_map/reduce_scatter | solution.py:695
  857.3 50.9 %collective-permute-start.48 = (bf16[512,1408]{1,0:T(8,128)(2,1)S(1)}, bf16[512,1408]{1,0:T(8,128)(2,1)S(1)}, u32[]{:S(2)}, u32[]{:S(2)}) collective-permute-start(bf16[512,1408]{1,0:T(8,128)(2,1)S(1)} %maximum_select_fusion.18), channel_id=1, source_target_pairs={{0,8},{1,9},{2,10},{3,11},{4,12},{5,13},{6,14},{7,15},{8,0},{9,1},... | collective-permute-start | bytes 4325384 | tf_op jit(solution)/shard_map/ppermute | solution.py:543
  919.5 155.2 %reduce-scatter.17.cloned.1.call-start = ((), (), s32[]{:S(2)}) async-start(), calls=%async_computation.17 | async-start | bytes 2621440 | tf_op jit(solution)/shard_map/reduce_scatter | solution.py:695
  920.6 77.6 %collective-permute-start.53 = (bf16[512,2816]{1,0:T(8,128)(2,1)}, bf16[512,2816]{1,0:T(8,128)(2,1)}, u32[]{:S(2)}, u32[]{:S(2)}) collective-permute-start(bf16[512,2816]{1,0:T(8,128)(2,1)} %constant_dynamic-update-slice_fusion.2.refs_0_.refs_1_), channel_id=1, source_target_pairs={{0,4},{1,5},{2,6},{3,7},{4,0},{5,1},{6,2},{7,3},{8,12},{9,13},{10,... | collective-permute-start | bytes 8650760 | tf_op jit(solution)/shard_map/ppermute | solution.py:543
  921.9 76.3 %collective-permute-start.49 = (bf16[2048,512]{1,0:T(8,128)(2,1)}, bf16[2048,512]{1,0:T(8,128)(2,1)}, u32[]{:S(2)}, u32[]{:S(2)}) collective-permute-start(bf16[2048,512]{1,0:T(8,128)(2,1)} %get-tuple-element.237), channel_id=1, source_target_pairs={{0,8},{1,9},{2,10},{3,11},{4,12},{5,13},{6,14},{7,15},{8,0},{9,1},... | collective-permute-start | bytes 6291464 | tf_op jit(solution)/shard_map/ppermute | solution.py:543
  922.3 75.9 %collective-permute-start.50 = (bf16[1024,1024]{1,0:T(8,128)(2,1)}, bf16[1024,1024]{1,0:T(8,128)(2,1)S(1)}, u32[]{:S(2)}, u32[]{:S(2)}) collective-permute-start(bf16[1024,1024]{1,0:T(8,128)(2,1)} %copy-done.49), channel_id=1, source_target_pairs={{0,16},{1,17},{2,18},{3,19},{4,20},{5,21},{6,22},{7,23},{8,24},{9,... | collective-permute-start | bytes 6291464 | tf_op jit(solution)/shard_map/ppermute | solution.py:543
  925.9 66.6 %collective-permute-start.51 = (bf16[256,2048]{1,0:T(8,128)(2,1)}, bf16[256,2048]{1,0:T(8,128)(2,1)}, u32[]{:S(2)}, u32[]{:S(2)}) collective-permute-start(bf16[256,2048]{1,0:T(8,128)(2,1)} %get-tuple-element.290), channel_id=1, source_target_pairs={{0,0},{1,4},{2,1},{3,5},{4,2},{5,6},{6,3},{7,7},{8,8},{9,12},{10,9... | collective-permute-start | bytes 3145736 | tf_op jit(solution)/shard_map/ppermute | solution.py:602
  928.5 64.0 %collective-permute-start.52 = (bf16[256,2048]{1,0:T(8,128)(2,1)}, bf16[256,2048]{1,0:T(8,128)(2,1)}, u32[]{:S(2)}, u32[]{:S(2)}) collective-permute-start(bf16[256,2048]{1,0:T(8,128)(2,1)} %get-tuple-element.291), channel_id=1, source_target_pairs={{0,1},{1,5},{2,0},{3,4},{4,3},{5,7},{6,2},{7,6},{8,9},{9,13},{10,8... | collective-permute-start | bytes 3145736 | tf_op jit(solution)/shard_map/ppermute | solution.py:602
  1009.1 58.4 %collective-permute-start.58 = (bf16[512,2816]{1,0:T(8,128)(2,1)}, bf16[512,2816]{1,0:T(8,128)(2,1)}, u32[]{:S(2)}, u32[]{:S(2)}) collective-permute-start(bf16[512,2816]{1,0:T(8,128)(2,1)} %pad_maximum_fusion.4.refs_0_.refs_1_), channel_id=1, source_target_pairs={{0,4},{1,5},{2,6},{3,7},{4,0},{5,1},{6,2},{7,3},{8,12},{9,13},{10,... | collective-permute-start | bytes 8650760 | tf_op jit(solution)/shard_map/ppermute | solution.py:543
  1079.1 41.6 %collective-permute-start.66 = (bf16[512,1408]{1,0:T(8,128)(2,1)S(1)}, bf16[512,1408]{1,0:T(8,128)(2,1)S(1)}, u32[]{:S(2)}, u32[]{:S(2)}) collective-permute-start(bf16[512,1408]{1,0:T(8,128)(2,1)S(1)} %maximum_select_fusion.19), channel_id=1, source_target_pairs={{0,8},{1,9},{2,10},{3,11},{4,12},{5,13},{6,14},{7,15},{8,0},{9,1},... | collective-permute-start | bytes 4325384 | tf_op jit(solution)/shard_map/ppermute | solution.py:543
  1113.7 66.7 %collective-permute-start.63 = (bf16[512,3072]{1,0:T(8,128)(2,1)S(1)}, bf16[512,3072]{1,0:T(8,128)(2,1)S(1)}, u32[]{:S(2)}, u32[]{:S(2)}) collective-permute-start(bf16[512,3072]{1,0:T(8,128)(2,1)S(1)} %maximum_select_fusion.5.refs_0_.refs_1_), channel_id=1, source_target_pairs={{0,4},{1,5},{2,6},{3,7},{4,0},{5,1},{6,2},{7,3},{8,12},{9,13},{10,... | collective-permute-start | bytes 9437192 | tf_op jit(solution)/shard_map/ppermute | solution.py:543
  1120.9 53.9 %collective-permute-start.67 = (bf16[512,2816]{1,0:T(8,128)(2,1)S(1)}, bf16[512,2816]{1,0:T(8,128)(2,1)S(1)}, u32[]{:S(2)}, u32[]{:S(2)}) collective-permute-start(bf16[512,2816]{1,0:T(8,128)(2,1)S(1)} %pad_maximum_fusion.5.refs_0_.refs_1_), channel_id=1, source_target_pairs={{0,4},{1,5},{2,6},{3,7},{4,0},{5,1},{6,2},{7,3},{8,12},{9,13},{10,... | collective-permute-start | bytes 8650760 | tf_op jit(solution)/shard_map/ppermute | solution.py:543
  (121 other events, 1644.4 us)
Sparse Core Ops, SparseCore 0:
  11.8 83.3 all-gather.6
  97.3 46.1 all-gather.8
  145.7 27.5 all-gather.10
  175.2 57.8 all-gather.12
  235.1 57.8 all-gather.14
  634.3 56.1 reduce-scatter.6
  721.2 56.5 reduce-scatter.8
  782.0 56.5 reduce-scatter.10
  855.2 23.8 reduce-scatter.12
  919.6 66.9 reduce-scatter.14
  1008.8 54.8 reduce-scatter.16
Sparse Core Ops, SparseCore 1:
  385.6 88.8 all-gather.16

commit v8 on v7

--- a/solution.py
+++ b/solution.py
@@ -596,9 +596,9 @@
         ]
         return ordered(batch_of(place), *arrived, 0)
 
-    def bring_back(x):
+    def send_back(x):
         slots = natural(x).reshape(2, run, width)
-        arrived = [
+        return [
             lax.ppermute(
                 lax.dynamic_index_in_dim(slots, (batch_of(place) + p) % 2, 0, False),
                 AXES,
@@ -606,6 +606,8 @@
             )
             for p in range(2)
         ]
+
+    def as_batches(arrived):
         return ordered(place % 2, arrived[0][None], arrived[1][None], 0)
 
 
@@ -630,11 +632,19 @@
         sent = swap_b(columns(x, (1 - b) * own, own).astype(LOW))
         return columns(x, b * own, own) + sent.astype(F32)
 
+
+    pick = functools.partial(lax.dynamic_index_in_dim, keepdims=False)
+
+    def away_b(x):
+        cut = x.reshape(2, 2, -1, own)
+        return pick(cut, b, 0), swap_b(pick(cut, 1 - b, 0))
+
+    def away_c(mine, arrived):
+        both = ordered(b, mine, arrived, 2)
+        return pick(both, c, 0), swap_c(pick(both, 1 - c, 0))
+
     def to_runs(x):
-        cut = x.reshape(2, 2, -1, own)
-        pick = functools.partial(lax.dynamic_index_in_dim, keepdims=False)
-        both = ordered(b, pick(cut, b, 0), swap_b(pick(cut, 1 - b, 0)), 2)
-        return ordered(c, pick(both, c, 0), swap_c(pick(both, 1 - c, 0)), 1)
+        return ordered(c, *away_c(*away_b(x)), 1)
 
 
     def own_features(w):
@@ -793,22 +803,29 @@
     arrived = swap_c(sent)
     down_b = sent_a(down_b)
     t_one = away(hidden_two, d_one)
+    result = fold_half(spots, [product], [w_d])
     lean_m = total(lean_m[:, 0])
+    arrived, result, t_one = tie(arrived, result, t_one)
+
+    r_result = swap_c(result)
+    one_a, one_b = pieces(t_one, 2)
+    one_a = sent_a(one_a)
     sent, mine = fold_half(spots, [d_one, d_two], [w_1, w_2], arrived)
-    sent, d_two, t_one, product, lean_m, down_b = tie(sent, d_two, t_one, product, lean_m, down_b)
+    sent, d_two, one_a, one_b, product, lean_m, down_b, r_result = tie(
+        sent, d_two, one_a, one_b, product, lean_m, down_b, r_result
+    )
 
     crossed = swap_b(sent)
-    one_a, one_b = pieces(t_one, 6)
-    one_a = sent_a(one_a)
+    one_b = sent_a(one_b)
     f_down = kept(dy_all, product, down_a, down_b)
     t_two = away(hidden_two, d_two)
-    result = fold_half(spots, [product], [w_d])
-    crossed, result, f_down, t_two, one_a = tie(crossed, result, f_down, t_two, one_a)
+    result, result_mine = fold_half(spots, [product], [w_d], r_result)
+    crossed, result, f_down, t_two, one_b = tie(crossed, result, f_down, t_two, one_b)
 
     f_down = scattered(f_down)
-    one_b = sent_a(one_b)
-    two_a, two_b = pieces(t_two, 3)
+    two_a, two_b = pieces(t_two, 5)
     two_a = sent_a(two_a)
+    result_b = swap_b(result)
     d_hidden = mine + crossed.astype(F32)
     m_normed = middle * m_scale
     lean = lean_m[:, None] * (2.0 / width)
@@ -816,10 +833,9 @@
     d_branch = d_middle.astype(LOW)
     lean_o = jnp.sum(d_middle * branch, axis=-1)
     sent = times_transposed(d_branch, row_half(w_o, 1 - c)).astype(LOW)
-    sent, result, d_middle, lean_o = tie(sent, result, d_middle, lean_o)
+    sent, d_middle, lean_o = tie(sent, d_middle, lean_o)
 
     arrived = swap_c(sent)
-    r_result = swap_c(result)
     lean_o = total(lean_o)
     p_out = cross_tokens(lifted, (o_scale * d_middle).astype(LOW)).astype(LOW)
     p_out = jnp.transpose(p_out.reshape(shards, spread, part, -1), (1, 0, 2, 3))
@@ -828,21 +844,22 @@
     d_gated = times_transposed(d_branch, row_half(w_o, c)) + arrived.astype(F32)
     sent = columns(d_gated, (1 - b) * own, own).astype(LOW)
     mine = columns(d_gated, b * own, own)
-    sent, mine, d_one, r_result, t_out, lean_o, one_b, two_a = tie(
-        sent, mine, d_one, r_result, t_out, lean_o, one_b, two_a
+    sent, mine, d_one, result_b, t_out, lean_o, two_a = tie(
+        sent, mine, d_one, result_b, t_out, lean_o, two_a
     )
 
     crossed = swap_b(sent)
     two_b = sent_a(two_b)
+    r_out = sent_a(t_out[1:])
     f_one = kept(hidden_two, d_one, one_a, one_b)
-    result, result_mine = fold_half(spots, [product], [w_d], r_result)
-    crossed, result, f_one, f_down, two_b = tie(crossed, result, f_one, f_down, two_b)
+    output = (middle + (result_mine + result_b.astype(F32))).astype(LOW)
+    crossed, output, f_one, f_down, two_b, r_out = tie(crossed, output, f_one, f_down, two_b, r_out)
 
     f_one = scattered(f_one)
-    r_out = sent_a(t_out[1:])
-    y_down = spread_a(f_down)
-    result = swap_b(result)
+    f_out = scattered(sum([x.astype(F32) for x in r_out], t_out[0].astype(F32)).astype(LOW))
+    y_down = over_spread(f_down)
     f_two = kept(hidden_two, d_two, two_a, two_b)
+    output, out_b = away_b(output)
     o_normed = attended * o_scale
     d_gated = mine + crossed.astype(F32)
     d_gate = (d_gated * o_normed).astype(LOW)
@@ -852,38 +869,37 @@
     d_qk = joined(d_query, d_key)
     d_vg = joined(d_value, d_gate)
     t_qk = away(hidden_one, d_qk)
-    d_qk, d_vg, t_qk, f_two, r_out, y_down, result = tie(d_qk, d_vg, t_qk, f_two, r_out, y_down, result)
+    d_qk, d_vg, t_qk, f_two, y_down, out_b = tie(d_qk, d_vg, t_qk, f_two, y_down, out_b)
 
     f_two = scattered(f_two)
+    y_down = by_spread([f_down, *y_down])
     qk_a, qk_b = pieces(t_qk, 4)
     qk_a = sent_a(qk_a)
-    output = to_runs((middle + (result_mine + result.astype(F32))).astype(LOW))
+    output, out_c = away_c(output, out_b)
     x_down = swap_b(y_down)
     y_one = over_spread(f_one)
     t_vg = away(hidden_one, d_vg)
     sent = fold_half(spots, [d_qk, d_vg], [w_qk, w_vg])
-    sent, t_vg, d_qk, d_vg, output, qk_a, x_down, y_one = tie(
-        sent, t_vg, d_qk, d_vg, output, qk_a, x_down, y_one
+    sent, t_vg, d_qk, d_vg, out_c, qk_a, x_down, y_one, f_out = tie(
+        sent, t_vg, d_qk, d_vg, out_c, qk_a, x_down, y_one, f_out
     )
 
-    f_out = scattered(sum([x.astype(F32) for x in r_out], t_out[0].astype(F32)).astype(LOW))
     arrived = swap_c(sent)
+    output = send_back(ordered(c, output, out_c, 1))
     qk_b = sent_a(qk_b)
     x_down = joined(y_down, x_down)
     y_one = by_spread([f_one, *y_one])
     x_one = swap_b(y_one)
-    lean_x = total(
-        jnp.sum(z_qk * d_qk.astype(F32), axis=-1) + jnp.sum(z_vg * d_vg.astype(F32), axis=-1)
-    )
+    lean_x = jnp.sum(z_qk * d_qk.astype(F32), axis=-1) + jnp.sum(z_vg * d_vg.astype(F32), axis=-1)
     sent, mine = fold_half(spots, [d_qk, d_vg], [w_qk, w_vg], arrived)
-    sent, mine, qk_b, t_vg, lean_x, x_one = tie(sent, mine, qk_b, t_vg, lean_x, x_one)
+    sent, mine, qk_b, t_vg, lean_x, x_one, output = tie(sent, mine, qk_b, t_vg, lean_x, x_one, output)
 
     crossed = swap_b(sent)
+    lean_x = total(lean_x)
     r_vg = sent_a(t_vg)
     f_qk = scattered(kept(hidden_one, d_qk, qk_a, qk_b))
-    output = bring_back(output)
     four_down = spread_c(x_down)
-    crossed, d_vg, r_vg, output, f_two, four_down = tie(crossed, d_vg, r_vg, output, f_two, four_down)
+    crossed, d_vg, r_vg, lean_x, f_two, four_down = tie(crossed, d_vg, r_vg, lean_x, f_two, four_down)
 
     f_vg = kept(hidden_one, d_vg, r_vg)
     x_one = joined(y_one, x_one)
@@ -909,13 +925,14 @@
     x_vg, y_oqk = tie(x_vg, y_oqk)
 
     four_vg = spread_c(spread_a(x_vg))
-    input_grad = bring_back(input_grad)
+    input_grad = send_back(input_grad)
     four_two = spread_c(spread_b(y_two))
     four_oqk = spread_c(y_oqk)
     g_query, g_key = place_quarters(spots, four_oqk, (own, own), (2 * own, own))
     g_value, g_gate = place_quarters(spots, four_vg, (0, own), (own, own))
     [g_two] = place_quarters(spots, four_two, (0, units))
     g_out = features_in_order(four_oqk, 0, own)
+    output, input_grad = as_batches(output), as_batches(input_grad)
     return output, input_grad, g_query, g_key, g_value, g_gate, g_out, g_one, g_two, g_down
 
 

time: 1210 us -> 1240 us (1.025)
  waiting for transfers between devices: 484 us -> 498 us
    ppermute x60, waiting for transfers between devices: 260 us -> 310 us  [move(): return lax.ppermute(x, AXES, pairs)]
    ppermute x4, waiting for transfers between devices: 87.5 us -> 52.1 us  [send_back(): lax.ppermute(lax.dynamic_index_in_dim(slots, (batch_of(place) + p) % 2, 0...]
    unnamed x204 -> x227, local copies, waits for them, and re-layouts: 55.5 us -> 64.3 us
  transfers between devices with their start and end apart: 80 -> 80, of which waited for: 30 -> 33; matrix products, arithmetic and copies ran while one was open for 15% -> 14% of each run, Pallas kernels for 28% -> 28%
where the time goes in v8:
time: 1240 us; the launch traced here: 1230 us
  waiting for transfers between devices  498 us (40%)
  Pallas kernels  350 us (28%)
  other arithmetic  112 us (9%)
  local copies, waits for them, and re-layouts  111 us (9%)
  starting transfers between devices  103 us (8%)
  matrix products  33.7 us (3%)
  between operations  17.5 us (1%)
    ppermute x60, waiting for transfers between devices, move(): return lax.ppermute(x, AXES, pairs)  310 us
    ppermute x4, waiting for transfers between devices, bring(): lax.ppermute(lax.dynamic_index_in_dim(x, (place + p) % 2, 0, False), AXES...  119 us
    pallas_call x6, Pallas kernels, fold_half(): pl.pallas_call(functools.partial(fold_kernel, len(values), arrived is not...  97.4 us
    ppermute x60, starting transfers between devices, move(): return lax.ppermute(x, AXES, pairs)  85.1 us
    pallas_call x10, Pallas kernels, gradient_rows(): pl.pallas_call(gradient_kernel, out_shape=out, grid_spec=pltpu.PrefetchSc...  84.4 us
    unnamed x227, local copies, waits for them, and re-layouts  64.3 us
    ppermute x4, waiting for transfers between devices, send_back(): lax.ppermute(lax.dynamic_index_in_dim(slots, (batch_of(place) + p) % 2, 0...  52.1 us
    select_n x22, other arithmetic, ordered(): jnp.where(index == 0, jnp.concatenate([mine, other], axis), jnp.concatena...  51.3 us
  transfers between devices with their start and end apart: 80, of which 33 were waited for; matrix products, arithmetic and copies ran while one was open for 14% of the time, Pallas kernels for 28%

profile of v8, /device:TPU:17, one launch (start us, length us, event | category | flops | bytes accessed | tf_op | source)
XLA Modules:
  0.0 1225.2 jit_solution(7797817181437538124)
XLA Ops:
  21.0 75.9 %collective-permute-done.2 = bf16[256,2048]{1,0:T(8,128)(2,1)S(1)} collective-permute-done((bf16[256,2048]{1,0:T(8,128)(2,1)}, bf16[256,2048]{1,0:T(8,128)(2,1)S(1)}, u32[]{:S(2)}, u32[]{:S(2)}) %collective-permute-start.2) | collective-permute-done | bytes 1048608 | tf_op jit(solution)/shard_map/ppermute | solution.py:594
  105.0 37.9 %collective-permute-done.4 = bf16[512,2048]{1,0:T(8,128)(2,1)} collective-permute-done((bf16[512,2048]{1,0:T(8,128)(2,1)}, bf16[512,2048]{1,0:T(8,128)(2,1)}, u32[]{:S(2)}, u32[]{:S(2)}) %collective-permute-start.4) | collective-permute-done | bytes 2097184 | tf_op jit(solution)/shard_map/ppermute | solution.py:543
  142.9 6.2 maximum_select_fusion.1.own_ref
  164.7 19.8 %enter.2 = (bf16[2048,2048]{1,0:T(8,128)(2,1)}, f32[2048,1024]{1,0:T(8,128)}, f32[2048,1]{1,0:T(8,128)S(1)}, bf16[2048,512]{1,0:T(8,128)(2,1)S(1)}) custom-call(s32[4]{0:T(128)S(1)} %pad_add_fusion.1.spots, bf16[1024,2048]{1,0:T(8,128)(2,1)S(1)} %copy-done.21, bf16[1024,2048]{1,0:T(8,128)(2,1)} %collective-permute-done.6.other_ref, ...), custom_call_target="tpu_custom_call" | custom-call | flops 8589934592 | bytes 31465472 | tf_op jit(solution)/shard_map/enter/pallas_call | solution.py:244
  185.8 15.5 %collective-permute-done.7.refs_1_.refs_5_.refs_6_ = bf16[1024,1024]{1,0:T(8,128)(2,1)} collective-permute-done((bf16[1024,1024]{1,0:T(8,128)(2,1)}, bf16[1024,1024]{1,0:T(8,128)(2,1)}, u32[]{:S(2)}, u32[]{:S(2)}) %collective-permute-start.7) | collective-permute-done | bytes 2097184 | tf_op jit(solution)/shard_map/ppermute | solution.py:543
  204.2 14.3 %project.1.zv_ref = f32[2048,1024]{1,0:T(8,128)S(1)} custom-call(s32[4]{0:T(128)S(1)} %pad_add_fusion.1.spots, bf16[2048,2048]{1,0:T(8,128)(2,1)} %get-tuple-element.156.h_ref.left_ref, bf16[1024,1024]{1,0:T(8,128)(2,1)S(1)} %copy-done.51, bf16[1024,1024]{1,0:T(8,128)(2,1)} %collective-permute-done.7.refs_1_.refs_5_.refs_6_), custom_call_target="tpu_custom_call" | custom-call | flops 8589934592 | bytes 20971520 | tf_op jit(solution)/shard_map/project/pallas_call | solution.py:275
  221.9 12.3 %attend.1 = f32[2048,512]{1,0:T(8,128)S(1)} custom-call(f32[4]{0:T(128)S(1)} %dynamic_slice.118.rates, s32[2,2]{1,0:T(2,128)S(1)} %pad_add_fusion.ends, f32[2048,1024]{1,0:T(8,128)S(1)} %copy-done.2, f32[2048,1024]{1,0:T(8,128)S(1)} %copy-done.2, f32[2048,1024]{1,0:T(8,128)} %copy-done.3), custom_call_target="tpu_custom_call" | custom-call | flops 4294967296 | bytes 16777216 | tf_op jit(solution)/shard_map/attend/pallas_call | solution.py:98
  243.4 42.0 %collective-permute-done.12 = f32[2048]{0:T(1024)S(1)} collective-permute-done((f32[2048]{0:T(1024)S(1)}, f32[2048]{0:T(1024)S(1)}, u32[]{:S(2)}, u32[]{:S(2)}) %collective-permute-start.12) | collective-permute-done | bytes 8224 | tf_op jit(solution)/shard_map/ppermute | solution.py:543
  293.0 9.3 collective-permute-done.10.refs_1_.refs_3_.refs_4_
  311.5 12.1 fusion.21
  330.1 43.1 %collective-permute-done.16 = bf16[256,2048]{1,0:T(8,128)(2,1)S(1)} collective-permute-done((bf16[256,2048]{1,0:T(8,128)(2,1)S(1)}, bf16[256,2048]{1,0:T(8,128)(2,1)S(1)}, u32[]{:S(2)}, u32[]{:S(2)}) %collective-permute-start.16) | collective-permute-done | bytes 1048608 | tf_op jit(solution)/shard_map/ppermute | solution.py:594
  392.4 38.1 %gated_unit.1 = (bf16[2048,2048]{1,0:T(8,128)(2,1)}, bf16[2048,1408]{1,0:T(8,128)(2,1)}, bf16[2048,1408]{1,0:T(8,128)(2,1)}, bf16[2048,1408]{1,0:T(8,128)(2,1)}, f32[2048,1]{1,0:T(8,128)S(1)}) custom-call(s32[4]{0:T(128)S(1)} %pad_add_fusion.1.spots, bf16[2048,1024]{1,0:T(8,128)(2,1)} %maximum_select_fusion.3.own_ref, ...), custom_call_target="tpu_custom_call" | custom-call | flops 23622320128 | bytes 45621248 | tf_op jit(solution)/shard_map/gated_unit/pallas_call | solution.py:337
  438.2 6.8 collective-permute-done.20.other_ref
  451.8 9.2 gradient_rows.10
  462.6 12.0 all-gather.17.cloned.1.call-done.refs_0_.refs_1_.refs_2_
  478.0 22.5 %gated_unit_back.1 = (bf16[2048,1408]{1,0:T(8,128)(2,1)S(1)}, bf16[2048,1408]{1,0:T(8,128)(2,1)S(1)}, f32[2048,1]{1,0:T(8,128)S(1)}) custom-call(s32[4]{0:T(128)S(1)} %pad_add_fusion.1.spots, bf16[2048,2048]{1,0:T(8,128)(2,1)} %get-tuple-element.178.left_ref.dy_ref, bf16[2048,1408]{1,0:T(8,128)(2,1)} %get-tuple-element.182.one_ref, ...), custom_call_target="tpu_custom_call" | custom-call | flops 11811160064 | bytes 37232640 | tf_op jit(solution)/shard_map/gated_unit_back/pallas_call | solution.py:374
  506.5 19.8 %fold_half.6 = bf16[2048,1024]{1,0:T(8,128)(2,1)} custom-call(s32[4]{0:T(128)S(1)} %pad_add_fusion.1.spots, bf16[2048,1408]{1,0:T(8,128)(2,1)} %copy-done.58, bf16[2048,1408]{1,0:T(8,128)(2,1)} %copy-done.56, bf16[1024,1408]{1,0:T(8,128)(2,1)S(1)} %copy-done.40, bf16[1024,1408]{1,0:T(8,128)(2,1)} %collective-permute-done.10.refs_1_.refs_3_.refs_4_, ...), custom_call_target="tpu_custom_call" | custom-call | flops 11811160064 | bytes 21495808 | tf_op jit(solution)/shard_map/fold_half/pallas_call | solution.py:435
  532.2 11.4 fold_half.7
  543.6 9.3 gradient_rows.11
  574.6 21.8 %fold_half.8 = (bf16[2048,512]{1,0:T(8,128)(2,1)}, f32[2048,512]{1,0:T(8,128)}) custom-call(s32[4]{0:T(128)S(1)} %pad_add_fusion.1.spots, bf16[2048,1408]{1,0:T(8,128)(2,1)} %copy-done.58, bf16[2048,1408]{1,0:T(8,128)(2,1)} %copy-done.56, bf16[2048,1024]{1,0:T(8,128)(2,1)} %copy-done.87, bf16[1024,1408]{1,0:T(8,128)(2,1)S(1)} %copy-done.41, ...), custom_call_target="tpu_custom_call" | custom-call | flops 11811160064 | bytes 27787264 | tf_op jit(solution)/shard_map/fold_half/pallas_call | solution.py:435
  602.3 12.8 %fold_half.9 = (bf16[2048,512]{1,0:T(8,128)(2,1)S(1)}, f32[2048,512]{1,0:T(8,128)S(1)}) custom-call(s32[4]{0:T(128)S(1)} %pad_add_fusion.1.spots, bf16[2048,1408]{1,0:T(8,128)(2,1)} %get-tuple-element.201.right_ref.refs_0_, bf16[2048,1024]{1,0:T(8,128)(2,1)} %collective-permute-done.27.refs_1_, ...), custom_call_target="tpu_custom_call" | custom-call | flops 5905580032 | bytes 16252928 | tf_op jit(solution)/shard_map/fold_half/pallas_call | solution.py:435
  617.1 9.3 gradient_rows.12
  630.7 9.4 gradient_rows.13
  663.6 12.5 %convolution_convert_fusion.1 = bf16[2048,512]{1,0:T(8,128)(2,1)S(1)} fusion(f32[2048,512]{1,0:T(8,128)} %copy-done.60, f32[2048]{0:T(1024)S(1)} %add_rsqrt_fusion, bf16[2048,1024]{1,0:T(8,128)(2,1)} %collective-permute-done.13, bf16[2048,1024]{1,0:T(8,128)(2,1)} %maximum_select_fusion.2, pred[]{:T(512)S(6)} %eq.51), kind=kOutput, calls=%fused_computation.28 | convolution fusion | flops 4335861760 | bytes 14688257 | tf_op jit(solution)/shard_map/dot_general | solution.py:32
  678.1 30.9 %collective-permute-done.33 = f32[2048]{0:T(1024)S(1)} collective-permute-done((f32[2048]{0:T(1024)S(1)}, f32[2048]{0:T(1024)S(1)}, u32[]{:S(2)}, u32[]{:S(2)}) %collective-permute-start.33) | collective-permute-done | bytes 8224 | tf_op jit(solution)/shard_map/ppermute | solution.py:543
  725.1 9.1 gradient_rows.14
  746.1 22.5 %collective-permute-done.37 = bf16[1024,512]{1,0:T(8,128)(2,1)} collective-permute-done((bf16[1024,512]{1,0:T(8,128)(2,1)}, bf16[1024,512]{1,0:T(8,128)(2,1)}, u32[]{:S(2)}, u32[]{:S(2)}) %collective-permute-start.37) | collective-permute-done | bytes 1048608 | tf_op jit(solution)/shard_map/ppermute | solution.py:543
  778.5 21.3 %attend_back.1 = (bf16[2048,512]{1,0:T(8,128)(2,1)S(1)}, bf16[2048,512]{1,0:T(8,128)(2,1)S(1)}, bf16[2048,512]{1,0:T(8,128)(2,1)S(1)}) custom-call(f32[4]{0:T(128)S(1)} %dynamic_slice.118.rates, s32[2,2]{1,0:T(2,128)S(1)} %pad_add_fusion.ends, f32[2048,1024]{1,0:T(8,128)} %get-tuple-element.155.zq_ref.zk_ref, f32[2048,1024]{1,0:T(8,128)} %get-tuple-element.155.zq_ref.zk_ref, ...), custom_call_target="tpu_custom_call" | custom-call | flops 10737418240 | bytes 20971520 | tf_op jit(solution)/shard_map/attend_back/pallas_call | solution.py:119
  808.2 6.9 gradient_rows.15
  822.9 9.1 gradient_rows.16
  850.6 14.1 %fold_half.10 = bf16[2048,1024]{1,0:T(8,128)(2,1)S(1)} custom-call(s32[4]{0:T(128)S(1)} %pad_add_fusion.1.spots, bf16[2048,1024]{1,0:T(8,128)(2,1)} %copy-done.9, bf16[2048,1024]{1,0:T(8,128)(2,1)} %pad_maximum_fusion.refs_1_.right_ref, bf16[1024,1024]{1,0:T(8,128)(2,1)S(1)} %copy-done.49, bf16[1024,1024]{1,0:T(8,128)(2,1)} %collective-permute-done.5.refs_1_.refs_3_.refs_4_, ...), custom_call_target="tpu_custom_call" | custom-call | flops 8589934592 | bytes 16777216 | tf_op jit(solution)/shard_map/fold_half/pallas_call | solution.py:435
  866.7 7.9 gradient_rows.17
  876.6 9.2 collective-permute-done.43
  905.4 17.5 %fold_half.11 = (bf16[2048,512]{1,0:T(8,128)(2,1)}, f32[2048,512]{1,0:T(8,128)}) custom-call(s32[4]{0:T(128)S(1)} %pad_add_fusion.1.spots, bf16[2048,1024]{1,0:T(8,128)(2,1)} %copy-done.9, bf16[2048,1024]{1,0:T(8,128)(2,1)} %pad_maximum_fusion.refs_1_.right_ref, bf16[2048,1024]{1,0:T(8,128)(2,1)} %collective-permute-done.44.refs_2_, ...), custom_call_target="tpu_custom_call" | custom-call | flops 8589934592 | bytes 23068672 | tf_op jit(solution)/shard_map/fold_half/pallas_call | solution.py:435
  922.9 10.9 collective-permute-done.48
  933.8 21.1 %collective-permute-done.47 = bf16[256,2048]{1,0:T(8,128)(2,1)} collective-permute-done((bf16[256,2048]{1,0:T(8,128)(2,1)}, bf16[256,2048]{1,0:T(8,128)(2,1)}, u32[]{:S(2)}, u32[]{:S(2)}) %collective-permute-start.47) | collective-permute-done | bytes 1048608 | tf_op jit(solution)/shard_map/ppermute | solution.py:602
  957.8 6.9 gradient_rows.19
  978.1 38.9 %collective-permute-done.52 = f32[2048]{0:T(1024)S(1)} collective-permute-done((f32[2048]{0:T(1024)S(1)}, f32[2048]{0:T(1024)S(1)}, u32[]{:S(2)}, u32[]{:S(2)}) %collective-permute-start.52) | collective-permute-done | bytes 8224 | tf_op jit(solution)/shard_map/ppermute | solution.py:543
  1019.9 7.2 gradient_rows.18
  1035.6 23.3 %collective-permute-done.54 = bf16[2,512,512]{2,1,0:T(8,128)(2,1)S(1)} collective-permute-done((bf16[2,512,512]{2,1,0:T(8,128)(2,1)S(1)}, bf16[2,512,512]{2,1,0:T(8,128)(2,1)S(1)}, u32[]{:S(2)}, u32[]{:S(2)}) %collective-permute-start.54) | collective-permute-done | bytes 1048608 | tf_op jit(solution)/shard_map/ppermute | solution.py:543
  1065.4 7.8 place_quarters.5
  1077.0 7.1 place_quarters.6
  1090.0 9.2 collective-permute-done.61
  1099.2 22.6 %collective-permute-done.62 = bf16[256,3072]{1,0:T(8,128)(2,1)S(1)} collective-permute-done((bf16[256,3072]{1,0:T(8,128)(2,1)}, bf16[256,3072]{1,0:T(8,128)(2,1)S(1)}, u32[]{:S(2)}, u32[]{:S(2)}) %collective-permute-start.62) | collective-permute-done | bytes 1572896 | tf_op jit(solution)/shard_map/ppermute | solution.py:543
  1145.0 20.1 %collective-permute-done.59 = bf16[256,2048]{1,0:T(8,128)(2,1)} collective-permute-done((bf16[256,2048]{1,0:T(8,128)(2,1)}, bf16[256,2048]{1,0:T(8,128)(2,1)}, u32[]{:S(2)}, u32[]{:S(2)}) %collective-permute-start.59) | collective-permute-done | bytes 1048608 | tf_op jit(solution)/shard_map/ppermute | solution.py:602
  1171.2 21.1 %collective-permute-start.65 = (bf16[512,2048]{1,0:T(8,128)(2,1)S(1)}, bf16[512,2048]{1,0:T(8,128)(2,1)S(1)}, u32[]{:S(2)}, u32[]{:S(2)}) collective-permute-start(bf16[512,2048]{1,0:T(8,128)(2,1)S(1)} %maximum_select_fusion.15.refs_0_.refs_1_), channel_id=1, source_target_pairs={{0,4},{1,5},{2,6},{3,7},{4,0},{5,1},{6,2},{7,3},{8,12},{9,13},{10,... | collective-permute-start | bytes 6291464 | tf_op jit(solution)/shard_map/ppermute | solution.py:543
  1192.3 8.1 place_quarters.9
  1206.1 7.0 place_quarters.7
  (491 shorter events, 364.5 us)
Async XLA Ops:
  8.0 91.2 %all-gather.7.cloned.1.call-start = ((), (), s32[]{:S(2)}) async-start(), calls=%async_computation.6 | async-start | bytes 2621440 | tf_op jit(solution)/shard_map/all_gather | solution.py:664
  11.6 137.4 %all-gather.9.cloned.1.call-start = ((), (), s32[]{:S(2)}) async-start(), calls=%async_computation.7 | async-start | bytes 2621440 | tf_op jit(solution)/shard_map/all_gather | solution.py:664
  14.8 171.1 %all-gather.11.cloned.1.call-start = ((), (), s32[]{:S(2)}) async-start(), calls=%async_computation.8 | async-start | bytes 1310720 | tf_op jit(solution)/shard_map/all_gather | solution.py:664
  16.0 80.9 %collective-permute-start.2 = (bf16[256,2048]{1,0:T(8,128)(2,1)}, bf16[256,2048]{1,0:T(8,128)(2,1)S(1)}, u32[]{:S(2)}, u32[]{:S(2)}) collective-permute-start(bf16[256,2048]{1,0:T(8,128)(2,1)} %get-tuple-element.316), channel_id=1, source_target_pairs={{0,0},{4,1},{1,2},{5,3},{2,4},{6,5},{3,6},{7,7},{8,8},{12,9},{9,10... | collective-permute-start | bytes 3145736 | tf_op jit(solution)/shard_map/ppermute | solution.py:594
  18.1 78.8 %collective-permute-start.3 = (bf16[256,2048]{1,0:T(8,128)(2,1)S(1)}, bf16[256,2048]{1,0:T(8,128)(2,1)S(1)}, u32[]{:S(2)}, u32[]{:S(2)}) collective-permute-start(bf16[256,2048]{1,0:T(8,128)(2,1)S(1)} %get-tuple-element.317), channel_id=1, source_target_pairs={{1,0},{5,1},{0,2},{4,3},{3,4},{7,5},{2,6},{6,7},{9,8},{13,9},{8,10... | collective-permute-start | bytes 3145736 | tf_op jit(solution)/shard_map/ppermute | solution.py:594
  99.2 43.7 %collective-permute-start.4 = (bf16[512,2048]{1,0:T(8,128)(2,1)}, bf16[512,2048]{1,0:T(8,128)(2,1)}, u32[]{:S(2)}, u32[]{:S(2)}) collective-permute-start(bf16[512,2048]{1,0:T(8,128)(2,1)} %maximum_select_fusion.6), channel_id=1, source_target_pairs={{0,8},{1,9},{2,10},{3,11},{4,12},{5,13},{6,14},{7,15},{8,0},{9,1},... | collective-permute-start | bytes 6291464 | tf_op jit(solution)/shard_map/ppermute | solution.py:543
  101.2 137.9 %all-gather.13.cloned.1.call-start = ((), (), s32[]{:S(2)}) async-start(), calls=%async_computation.9 | async-start | bytes 3604480 | tf_op jit(solution)/shard_map/all_gather | solution.py:664
  101.2 47.9 %collective-permute-start.5 = (bf16[1024,1024]{1,0:T(8,128)(2,1)}, bf16[1024,1024]{1,0:T(8,128)(2,1)}, u32[]{:S(2)}, u32[]{:S(2)}) collective-permute-start(bf16[1024,1024]{1,0:T(8,128)(2,1)} %all-gather.7.cloned.1.call-done.refs_0_.refs_2_.refs_3_), channel_id=1, source_target_pairs={{0,16},{1,17},{2,18},{3,19},{4,20},{5,21},{6,22},{7,23},{8,24},{9,... | collective-permute-start | bytes 6291464 | tf_op jit(solution)/shard_map/ppermute | solution.py:543
  104.9 188.1 %all-gather.15.cloned.1.call-start = ((), (), s32[]{:S(2)}) async-start(), calls=%async_computation.10 | async-start | bytes 3604480 | tf_op jit(solution)/shard_map/all_gather | solution.py:664
  153.8 47.5 %collective-permute-start.7 = (bf16[1024,1024]{1,0:T(8,128)(2,1)}, bf16[1024,1024]{1,0:T(8,128)(2,1)}, u32[]{:S(2)}, u32[]{:S(2)}) collective-permute-start(bf16[1024,1024]{1,0:T(8,128)(2,1)} %all-gather.9.cloned.1.call-done.refs_0_.refs_4_.refs_5_), channel_id=1, source_target_pairs={{0,16},{1,17},{2,18},{3,19},{4,20},{5,21},{6,22},{7,23},{8,24},{9,... | collective-permute-start | bytes 6291464 | tf_op jit(solution)/shard_map/ppermute | solution.py:543
  160.0 314.6 %all-gather.17.cloned.1.call-start = ((), (), s32[]{:S(2)}) async-start(), calls=%async_computation.11 | async-start | bytes 6488064 | tf_op jit(solution)/shard_map/all_gather | solution.py:668
  239.1 63.2 %collective-permute-start.10 = (bf16[1024,1408]{1,0:T(8,128)(2,1)}, bf16[1024,1408]{1,0:T(8,128)(2,1)}, u32[]{:S(2)}, u32[]{:S(2)}) collective-permute-start(bf16[1024,1408]{1,0:T(8,128)(2,1)} %all-gather.13.cloned.1.call-done.refs_0_.refs_2_.refs_3_), channel_id=1, source_target_pairs={{0,16},{1,17},{2,18},{3,19},{4,20},{5,21},{6,22},{7,23},{8,24},{9,... | collective-permute-start | bytes 8650760 | tf_op jit(solution)/shard_map/ppermute | solution.py:543
  239.4 46.0 %collective-permute-start.9 = (bf16[2048,512]{1,0:T(8,128)(2,1)S(1)}, bf16[2048,512]{1,0:T(8,128)(2,1)S(1)}, u32[]{:S(2)}, u32[]{:S(2)}) collective-permute-start(bf16[2048,512]{1,0:T(8,128)(2,1)S(1)} %get-tuple-element.159), channel_id=1, source_target_pairs={{0,8},{1,9},{2,10},{3,11},{4,12},{5,13},{6,14},{7,15},{8,0},{9,1},... | collective-permute-start | bytes 6291464 | tf_op jit(solution)/shard_map/ppermute | solution.py:543
  243.1 42.2 %collective-permute-start.12 = (f32[2048]{0:T(1024)S(1)}, f32[2048]{0:T(1024)S(1)}, u32[]{:S(2)}, u32[]{:S(2)}) collective-permute-start(f32[2048]{0:T(1024)S(1)} %add.256), channel_id=1, source_target_pairs={{0,8},{1,9},{2,10},{3,11},{4,12},{5,13},{6,14},{7,15},{8,0},{9,1},... | collective-permute-start | bytes 24584 | tf_op jit(solution)/shard_map/ppermute | solution.py:543
  307.5 70.8 %collective-permute-start.15 = (bf16[1024,1408]{1,0:T(8,128)(2,1)S(1)}, bf16[1024,1408]{1,0:T(8,128)(2,1)S(1)}, u32[]{:S(2)}, u32[]{:S(2)}) collective-permute-start(bf16[1024,1408]{1,0:T(8,128)(2,1)S(1)} %copy-done.42), channel_id=1, source_target_pairs={{0,16},{1,17},{2,18},{3,19},{4,20},{5,21},{6,22},{7,23},{8,24},{9,... | collective-permute-start | bytes 8650760 | tf_op jit(solution)/shard_map/ppermute | solution.py:543
  323.7 51.9 %collective-permute-start.14 = (bf16[2048,512]{1,0:T(8,128)(2,1)S(1)}, bf16[2048,512]{1,0:T(8,128)(2,1)S(1)}, u32[]{:S(2)}, u32[]{:S(2)}) collective-permute-start(bf16[2048,512]{1,0:T(8,128)(2,1)S(1)} %get-tuple-element.320), channel_id=1, source_target_pairs={{0,8},{1,9},{2,10},{3,11},{4,12},{5,13},{6,14},{7,15},{8,0},{9,1},... | collective-permute-start | bytes 6291464 | tf_op jit(solution)/shard_map/ppermute | solution.py:543
  325.1 48.2 %collective-permute-start.16 = (bf16[256,2048]{1,0:T(8,128)(2,1)S(1)}, bf16[256,2048]{1,0:T(8,128)(2,1)S(1)}, u32[]{:S(2)}, u32[]{:S(2)}) collective-permute-start(bf16[256,2048]{1,0:T(8,128)(2,1)S(1)} %get-tuple-element.312), channel_id=1, source_target_pairs={{0,0},{4,1},{1,2},{5,3},{2,4},{6,5},{3,6},{7,7},{8,8},{12,9},{9,10... | collective-permute-start | bytes 3145736 | tf_op jit(solution)/shard_map/ppermute | solution.py:594
  330.1 43.2 %collective-permute-start.17 = (bf16[256,2048]{1,0:T(8,128)(2,1)S(1)}, bf16[256,2048]{1,0:T(8,128)(2,1)S(1)}, u32[]{:S(2)}, u32[]{:S(2)}) collective-permute-start(bf16[256,2048]{1,0:T(8,128)(2,1)S(1)} %get-tuple-element.313), channel_id=1, source_target_pairs={{1,0},{5,1},{0,2},{4,3},{3,4},{7,5},{2,6},{6,7},{9,8},{13,9},{8,10... | collective-permute-start | bytes 3145736 | tf_op jit(solution)/shard_map/ppermute | solution.py:594
  385.6 383.0 %reduce-scatter.7.cloned.1.call-start = ((), (), s32[]{:S(2)}) async-start(), calls=%async_computation.12 | async-start | bytes 3604480 | tf_op jit(solution)/shard_map/reduce_scatter | solution.py:705
  385.8 47.6 %collective-permute-start.19 = (bf16[512,2048]{1,0:T(8,128)(2,1)}, bf16[512,2048]{1,0:T(8,128)(2,1)S(1)}, u32[]{:S(2)}, u32[]{:S(2)}) collective-permute-start(bf16[512,2048]{1,0:T(8,128)(2,1)} %maximum_select_fusion.8), channel_id=1, source_target_pairs={{0,8},{1,9},{2,10},{3,11},{4,12},{5,13},{6,14},{7,15},{8,0},{9,1},... | collective-permute-start | bytes 6291464 | tf_op jit(solution)/shard_map/ppermute | solution.py:543
  477.7 48.6 %collective-permute-start.21 = (bf16[768,1408]{1,0:T(8,128)(2,1)}, bf16[768,1408]{1,0:T(8,128)(2,1)}, u32[]{:S(2)}, u32[]{:S(2)}) collective-permute-start(bf16[768,1408]{1,0:T(8,128)(2,1)} %slice.120), channel_id=1, source_target_pairs={{0,16},{1,17},{2,18},{3,19},{4,20},{5,21},{6,22},{7,23},{8,24},{9,... | collective-permute-start | bytes 6488072 | tf_op jit(solution)/shard_map/ppermute | solution.py:543
  556.6 42.8 %collective-permute-start.27 = (bf16[2048,1024]{1,0:T(8,128)(2,1)}, bf16[2048,1024]{1,0:T(8,128)(2,1)}, u32[]{:S(2)}, u32[]{:S(2)}) collective-permute-start(bf16[2048,1024]{1,0:T(8,128)(2,1)} %fold_half.7), channel_id=1, source_target_pairs={{0,4},{1,5},{2,6},{3,7},{4,0},{5,1},{6,2},{7,3},{8,12},{9,13},{10,... | collective-permute-start | bytes 12582920 | tf_op jit(solution)/shard_map/ppermute | solution.py:543
  599.4 46.2 %collective-permute-start.28 = (bf16[2048,512]{1,0:T(8,128)(2,1)}, bf16[2048,512]{1,0:T(8,128)(2,1)}, u32[]{:S(2)}, u32[]{:S(2)}) collective-permute-start(bf16[2048,512]{1,0:T(8,128)(2,1)} %get-tuple-element.200), channel_id=1, source_target_pairs={{0,8},{1,9},{2,10},{3,11},{4,12},{5,13},{6,14},{7,15},{8,0},{9,1},... | collective-permute-start | bytes 6291464 | tf_op jit(solution)/shard_map/ppermute | solution.py:543
  599.7 47.3 %collective-permute-start.29 = (bf16[768,1408]{1,0:T(8,128)(2,1)}, bf16[768,1408]{1,0:T(8,128)(2,1)}, u32[]{:S(2)}, u32[]{:S(2)}) collective-permute-start(bf16[768,1408]{1,0:T(8,128)(2,1)} %slice.122), channel_id=1, source_target_pairs={{0,16},{1,17},{2,18},{3,19},{4,20},{5,21},{6,22},{7,23},{8,24},{9,... | collective-permute-start | bytes 6488072 | tf_op jit(solution)/shard_map/ppermute | solution.py:543
  656.2 52.9 %collective-permute-start.30 = (bf16[2048,1024]{1,0:T(8,128)(2,1)}, bf16[2048,1024]{1,0:T(8,128)(2,1)}, u32[]{:S(2)}, u32[]{:S(2)}) collective-permute-start(bf16[2048,1024]{1,0:T(8,128)(2,1)} %convolution_convert_fusion), channel_id=1, source_target_pairs={{0,4},{1,5},{2,6},{3,7},{4,0},{5,1},{6,2},{7,3},{8,12},{9,13},{10,... | collective-permute-start | bytes 12582920 | tf_op jit(solution)/shard_map/ppermute | solution.py:543
  658.7 187.4 %reduce-scatter.9.cloned.1.call-start = ((), (), s32[]{:S(2)}) async-start(), calls=%async_computation.13 | async-start | bytes 3604480 | tf_op jit(solution)/shard_map/reduce_scatter | solution.py:705
  661.7 56.4 %collective-permute-start.34 = (bf16[640,1408]{1,0:T(8,128)(2,1)}, bf16[640,1408]{1,0:T(8,128)(2,1)}, u32[]{:S(2)}, u32[]{:S(2)}) collective-permute-start(bf16[640,1408]{1,0:T(8,128)(2,1)} %slice.124), channel_id=1, source_target_pairs={{0,16},{1,17},{2,18},{3,19},{4,20},{5,21},{6,22},{7,23},{8,24},{9,... | collective-permute-start | bytes 5406728 | tf_op jit(solution)/shard_map/ppermute | solution.py:543
  661.8 56.3 %collective-permute-start.31 = (bf16[2048,512]{1,0:T(8,128)(2,1)S(1)}, bf16[2048,512]{1,0:T(8,128)(2,1)S(1)}, u32[]{:S(2)}, u32[]{:S(2)}) collective-permute-start(bf16[2048,512]{1,0:T(8,128)(2,1)S(1)} %copy-done.55), channel_id=1, source_target_pairs={{0,8},{1,9},{2,10},{3,11},{4,12},{5,13},{6,14},{7,15},{8,0},{9,1},... | collective-permute-start | bytes 6291464 | tf_op jit(solution)/shard_map/ppermute | solution.py:543
  718.1 50.5 %collective-permute-start.35 = (bf16[2048,512]{1,0:T(8,128)(2,1)}, bf16[2048,512]{1,0:T(8,128)(2,1)}, u32[]{:S(2)}, u32[]{:S(2)}) collective-permute-start(bf16[2048,512]{1,0:T(8,128)(2,1)} %dynamic-slice_convert_fusion), channel_id=1, source_target_pairs={{0,8},{1,9},{2,10},{3,11},{4,12},{5,13},{6,14},{7,15},{8,0},{9,1},... | collective-permute-start | bytes 6291464 | tf_op jit(solution)/shard_map/ppermute | solution.py:543
  724.9 43.7 %collective-permute-start.37 = (bf16[1024,512]{1,0:T(8,128)(2,1)}, bf16[1024,512]{1,0:T(8,128)(2,1)}, u32[]{:S(2)}, u32[]{:S(2)}) collective-permute-start(bf16[1024,512]{1,0:T(8,128)(2,1)} %get-tuple-element.223), channel_id=1, source_target_pairs={{0,16},{1,17},{2,18},{3,19},{4,20},{5,21},{6,22},{7,23},{8,24},{9,... | collective-permute-start | bytes 3145736 | tf_op jit(solution)/shard_map/ppermute | solution.py:543
  768.6 106.0 %reduce-scatter.11.cloned.1.call-start = ((), (), s32[]{:S(2)}) async-start(), calls=%async_computation.14 | async-start | bytes 1310720 | tf_op jit(solution)/shard_map/reduce_scatter | solution.py:705
  768.7 65.0 %collective-permute-start.38 = (bf16[256,1408]{1,0:T(8,128)(2,1)}, bf16[256,1408]{1,0:T(8,128)(2,1)}, u32[]{:S(2)}, u32[]{:S(2)}) collective-permute-start(bf16[256,1408]{1,0:T(8,128)(2,1)} %reduce-scatter.7.cloned.1.call-done), channel_id=1, source_target_pairs={{0,16},{1,17},{2,18},{3,19},{4,20},{5,21},{6,22},{7,23},{8,24},{9,... | collective-permute-start | bytes 2162696 | tf_op jit(solution)/shard_map/ppermute | solution.py:543
  771.5 62.1 %collective-permute-start.39 = (bf16[2,512,512]{2,1,0:T(8,128)(2,1)}, bf16[2,512,512]{2,1,0:T(8,128)(2,1)}, u32[]{:S(2)}, u32[]{:S(2)}) collective-permute-start(bf16[2,512,512]{2,1,0:T(8,128)(2,1)} %get-tuple-element.309), channel_id=1, source_target_pairs={{0,8},{1,9},{2,10},{3,11},{4,12},{5,13},{6,14},{7,15},{8,0},{9,1},... | collective-permute-start | bytes 3145736 | tf_op jit(solution)/shard_map/ppermute | solution.py:543
  815.2 201.9 %reduce-scatter.13.cloned.1.call-start = ((), (), s32[]{:S(2)}) async-start(), calls=%async_computation.15 | async-start | bytes 3604480 | tf_op jit(solution)/shard_map/reduce_scatter | solution.py:705
  846.0 216.7 %reduce-scatter.15.cloned.1.call-start = ((), (), s32[]{:S(2)}) async-start(), calls=%async_computation.16 | async-start | bytes 2621440 | tf_op jit(solution)/shard_map/reduce_scatter | solution.py:705
  846.1 39.7 %collective-permute-start.43 = (bf16[256,1408]{1,0:T(8,128)(2,1)}, bf16[256,1408]{1,0:T(8,128)(2,1)}, u32[]{:S(2)}, u32[]{:S(2)}) collective-permute-start(bf16[256,1408]{1,0:T(8,128)(2,1)} %reduce-scatter.9.cloned.1.call-done), channel_id=1, source_target_pairs={{0,16},{1,17},{2,18},{3,19},{4,20},{5,21},{6,22},{7,23},{8,24},{9,... | collective-permute-start | bytes 2162696 | tf_op jit(solution)/shard_map/ppermute | solution.py:543
  889.5 65.5 %collective-permute-start.46 = (bf16[512,1408]{1,0:T(8,128)(2,1)S(1)}, bf16[512,1408]{1,0:T(8,128)(2,1)S(1)}, u32[]{:S(2)}, u32[]{:S(2)}) collective-permute-start(bf16[512,1408]{1,0:T(8,128)(2,1)S(1)} %maximum_select_fusion.18), channel_id=1, source_target_pairs={{0,8},{1,9},{2,10},{3,11},{4,12},{5,13},{6,14},{7,15},{8,0},{9,1},... | collective-permute-start | bytes 4325384 | tf_op jit(solution)/shard_map/ppermute | solution.py:543
  900.5 54.4 %collective-permute-start.47 = (bf16[256,2048]{1,0:T(8,128)(2,1)}, bf16[256,2048]{1,0:T(8,128)(2,1)}, u32[]{:S(2)}, u32[]{:S(2)}) collective-permute-start(bf16[256,2048]{1,0:T(8,128)(2,1)} %get-tuple-element.303), channel_id=1, source_target_pairs={{0,0},{1,4},{2,1},{3,5},{4,2},{5,6},{6,3},{7,7},{8,8},{9,12},{10,9... | collective-permute-start | bytes 3145736 | tf_op jit(solution)/shard_map/ppermute | solution.py:602
  966.1 118.1 %reduce-scatter.17.cloned.1.call-start = ((), (), s32[]{:S(2)}) async-start(), calls=%async_computation.17 | async-start | bytes 2621440 | tf_op jit(solution)/shard_map/reduce_scatter | solution.py:705
  969.9 47.2 %collective-permute-start.53 = (bf16[512,2816]{1,0:T(8,128)(2,1)}, bf16[512,2816]{1,0:T(8,128)(2,1)}, u32[]{:S(2)}, u32[]{:S(2)}) collective-permute-start(bf16[512,2816]{1,0:T(8,128)(2,1)} %pad_maximum_fusion.4.refs_0_.refs_1_), channel_id=1, source_target_pairs={{0,4},{1,5},{2,6},{3,7},{4,0},{5,1},{6,2},{7,3},{8,12},{9,13},{10,... | collective-permute-start | bytes 8650760 | tf_op jit(solution)/shard_map/ppermute | solution.py:543
  969.9 47.2 %collective-permute-start.49 = (bf16[2048,512]{1,0:T(8,128)(2,1)}, bf16[2048,512]{1,0:T(8,128)(2,1)}, u32[]{:S(2)}, u32[]{:S(2)}) collective-permute-start(bf16[2048,512]{1,0:T(8,128)(2,1)} %get-tuple-element.253), channel_id=1, source_target_pairs={{0,8},{1,9},{2,10},{3,11},{4,12},{5,13},{6,14},{7,15},{8,0},{9,1},... | collective-permute-start | bytes 6291464 | tf_op jit(solution)/shard_map/ppermute | solution.py:543
  971.1 46.7 %collective-permute-start.50 = (bf16[1024,1024]{1,0:T(8,128)(2,1)}, bf16[1024,1024]{1,0:T(8,128)(2,1)S(1)}, u32[]{:S(2)}, u32[]{:S(2)}) collective-permute-start(bf16[1024,1024]{1,0:T(8,128)(2,1)} %gradient_rows.17), channel_id=1, source_target_pairs={{0,16},{1,17},{2,18},{3,19},{4,20},{5,21},{6,22},{7,23},{8,24},{9,... | collective-permute-start | bytes 6291464 | tf_op jit(solution)/shard_map/ppermute | solution.py:543
  975.2 41.9 %collective-permute-start.52 = (f32[2048]{0:T(1024)S(1)}, f32[2048]{0:T(1024)S(1)}, u32[]{:S(2)}, u32[]{:S(2)}) collective-permute-start(f32[2048]{0:T(1024)S(1)} %add.291), channel_id=1, source_target_pairs={{0,8},{1,9},{2,10},{3,11},{4,12},{5,13},{6,14},{7,15},{8,0},{9,1},... | collective-permute-start | bytes 24584 | tf_op jit(solution)/shard_map/ppermute | solution.py:543
  1028.8 48.2 %collective-permute-start.58 = (bf16[512,2816]{1,0:T(8,128)(2,1)}, bf16[512,2816]{1,0:T(8,128)(2,1)}, u32[]{:S(2)}, u32[]{:S(2)}) collective-permute-start(bf16[512,2816]{1,0:T(8,128)(2,1)} %pad_maximum_fusion.5.refs_0_.refs_1_), channel_id=1, source_target_pairs={{0,4},{1,5},{2,6},{3,7},{4,0},{5,1},{6,2},{7,3},{8,12},{9,13},{10,... | collective-permute-start | bytes 8650760 | tf_op jit(solution)/shard_map/ppermute | solution.py:543
  1089.4 40.6 %collective-permute-start.66 = (bf16[512,1408]{1,0:T(8,128)(2,1)S(1)}, bf16[512,1408]{1,0:T(8,128)(2,1)S(1)}, u32[]{:S(2)}, u32[]{:S(2)}) collective-permute-start(bf16[512,1408]{1,0:T(8,128)(2,1)S(1)} %maximum_select_fusion.19), channel_id=1, source_target_pairs={{0,8},{1,9},{2,10},{3,11},{4,12},{5,13},{6,14},{7,15},{8,0},{9,1},... | collective-permute-start | bytes 4325384 | tf_op jit(solution)/shard_map/ppermute | solution.py:543
  1124.3 76.1 %collective-permute-start.63 = (bf16[512,3072]{1,0:T(8,128)(2,1)}, bf16[512,3072]{1,0:T(8,128)(2,1)}, u32[]{:S(2)}, u32[]{:S(2)}) collective-permute-start(bf16[512,3072]{1,0:T(8,128)(2,1)} %maximum_select_fusion.5.refs_0_.refs_1_), channel_id=1, source_target_pairs={{0,4},{1,5},{2,6},{3,7},{4,0},{5,1},{6,2},{7,3},{8,12},{9,13},{10,... | collective-permute-start | bytes 9437192 | tf_op jit(solution)/shard_map/ppermute | solution.py:543
  1131.8 60.5 %collective-permute-start.67 = (bf16[512,2816]{1,0:T(8,128)(2,1)}, bf16[512,2816]{1,0:T(8,128)(2,1)}, u32[]{:S(2)}, u32[]{:S(2)}) collective-permute-start(bf16[512,2816]{1,0:T(8,128)(2,1)} %pad_maximum_fusion.6.refs_0_.refs_1_), channel_id=1, source_target_pairs={{0,4},{1,5},{2,6},{3,7},{4,0},{5,1},{6,2},{7,3},{8,12},{9,13},{10,... | collective-permute-start | bytes 8650760 | tf_op jit(solution)/shard_map/ppermute | solution.py:543
  1171.2 41.9 %collective-permute-start.65 = (bf16[512,2048]{1,0:T(8,128)(2,1)S(1)}, bf16[512,2048]{1,0:T(8,128)(2,1)S(1)}, u32[]{:S(2)}, u32[]{:S(2)}) collective-permute-start(bf16[512,2048]{1,0:T(8,128)(2,1)S(1)} %maximum_select_fusion.15.refs_0_.refs_1_), channel_id=1, source_target_pairs={{0,4},{1,5},{2,6},{3,7},{4,0},{5,1},{6,2},{7,3},{8,12},{9,13},{10,... | collective-permute-start | bytes 6291464 | tf_op jit(solution)/shard_map/ppermute | solution.py:543
  (133 other events, 1632.6 us)
Sparse Core Ops, SparseCore 0:
  11.8 83.3 all-gather.6
  97.3 46.1 all-gather.8
  145.7 27.5 all-gather.10
  175.2 57.8 all-gather.12
  235.1 57.8 all-gather.14
  658.8 54.6 reduce-scatter.6
  768.7 57.2 reduce-scatter.8
  828.3 25.7 reduce-scatter.10
  856.5 63.9 reduce-scatter.12
  966.2 43.2 reduce-scatter.14
  1028.6 43.9 reduce-scatter.16
Sparse Core Ops, SparseCore 1:
  385.7 88.8 all-gather.16

commit v9 on v8

--- a/solution.py
+++ b/solution.py
@@ -836,7 +836,7 @@
     sent, d_middle, lean_o = tie(sent, d_middle, lean_o)
 
     arrived = swap_c(sent)
-    lean_o = total(lean_o)
+    lean_o = lean_o + swap_c(lean_o)
     p_out = cross_tokens(lifted, (o_scale * d_middle).astype(LOW)).astype(LOW)
     p_out = jnp.transpose(p_out.reshape(shards, spread, part, -1), (1, 0, 2, 3))
     p_out = p_out.reshape(spread, width // spread, -1)
@@ -849,29 +849,32 @@
     )
 
     crossed = swap_b(sent)
+    lean_b = swap_b(lean_o)
     two_b = sent_a(two_b)
-    r_out = sent_a(t_out[1:])
     f_one = kept(hidden_two, d_one, one_a, one_b)
     output = (middle + (result_mine + result_b.astype(F32))).astype(LOW)
-    crossed, output, f_one, f_down, two_b, r_out = tie(crossed, output, f_one, f_down, two_b, r_out)
+    crossed, output, f_one, f_down, two_b, t_out, lean_b = tie(
+        crossed, output, f_one, f_down, two_b, t_out, lean_b
+    )
 
     f_one = scattered(f_one)
-    f_out = scattered(sum([x.astype(F32) for x in r_out], t_out[0].astype(F32)).astype(LOW))
+    r_out = sent_a(t_out[1:])
     y_down = over_spread(f_down)
     f_two = kept(hidden_two, d_two, two_a, two_b)
     output, out_b = away_b(output)
     o_normed = attended * o_scale
     d_gated = mine + crossed.astype(F32)
     d_gate = (d_gated * o_normed).astype(LOW)
-    lean = lean_o[:, None] / width
+    lean = (lean_o + lean_b)[:, None] / width
     d_attended = (o_scale * (d_gated * gate - o_normed * lean)).astype(LOW)
     d_query, d_key, d_value = attend_back(rates, ends, z_qk, z_vg, d_attended)
     d_qk = joined(d_query, d_key)
     d_vg = joined(d_value, d_gate)
     t_qk = away(hidden_one, d_qk)
-    d_qk, d_vg, t_qk, f_two, y_down, out_b = tie(d_qk, d_vg, t_qk, f_two, y_down, out_b)
+    d_qk, d_vg, t_qk, f_two, y_down, out_b, r_out = tie(d_qk, d_vg, t_qk, f_two, y_down, out_b, r_out)
 
     f_two = scattered(f_two)
+    f_out = scattered(sum([x.astype(F32) for x in r_out], t_out[0].astype(F32)).astype(LOW))
     y_down = by_spread([f_down, *y_down])
     qk_a, qk_b = pieces(t_qk, 4)
     qk_a = sent_a(qk_a)
@@ -880,8 +883,8 @@
     y_one = over_spread(f_one)
     t_vg = away(hidden_one, d_vg)
     sent = fold_half(spots, [d_qk, d_vg], [w_qk, w_vg])
-    sent, t_vg, d_qk, d_vg, out_c, qk_a, x_down, y_one, f_out = tie(
-        sent, t_vg, d_qk, d_vg, out_c, qk_a, x_down, y_one, f_out
+    sent, t_vg, d_qk, d_vg, out_c, qk_a, x_down, y_one = tie(
+        sent, t_vg, d_qk, d_vg, out_c, qk_a, x_down, y_one
     )
 
     arrived = swap_c(sent)
@@ -892,14 +895,15 @@
     x_one = swap_b(y_one)
     lean_x = jnp.sum(z_qk * d_qk.astype(F32), axis=-1) + jnp.sum(z_vg * d_vg.astype(F32), axis=-1)
     sent, mine = fold_half(spots, [d_qk, d_vg], [w_qk, w_vg], arrived)
+    lean_x = lean_x + swap_c(lean_x)
     sent, mine, qk_b, t_vg, lean_x, x_one, output = tie(sent, mine, qk_b, t_vg, lean_x, x_one, output)
 
     crossed = swap_b(sent)
-    lean_x = total(lean_x)
+    lean_b = swap_b(lean_x)
     r_vg = sent_a(t_vg)
     f_qk = scattered(kept(hidden_one, d_qk, qk_a, qk_b))
     four_down = spread_c(x_down)
-    crossed, d_vg, r_vg, lean_x, f_two, four_down = tie(crossed, d_vg, r_vg, lean_x, f_two, four_down)
+    crossed, d_vg, r_vg, lean_b, f_two, four_down = tie(crossed, d_vg, r_vg, lean_b, f_two, four_down)
 
     f_vg = kept(hidden_one, d_vg, r_vg)
     x_one = joined(y_one, x_one)
@@ -908,7 +912,7 @@
     f_vg = scattered(f_vg)
     d_hidden = mine + crossed.astype(F32)
     x_normed = x_own.astype(F32) * x_scale
-    lean = lean_x[:, None] / width
+    lean = (lean_x + lean_b)[:, None] / width
     input_grad = to_runs((d_middle + x_scale * (d_hidden - x_normed * lean)).astype(LOW))
     f_oqk = joined(f_out, f_qk)
     x_oqk = swap_b(f_oqk)
@@ -919,15 +923,17 @@
     [g_one] = place_quarters(spots, four_one, (0, units))
     input_grad, x_oqk, y_two, f_vg, g_down, g_one = tie(input_grad, x_oqk, y_two, f_vg, g_down, g_one)
 
-    x_vg = spread_b(f_vg)
+    y_vg = over_spread(f_vg)
+    f_oqk = joined(f_oqk, x_oqk)
+    y_oqk = over_spread(f_oqk)
     y_two = by_spread([f_two, *y_two])
-    y_oqk = spread_a(joined(f_oqk, x_oqk))
-    x_vg, y_oqk = tie(x_vg, y_oqk)
-
-    four_vg = spread_c(spread_a(x_vg))
+    x_two = swap_b(y_two)
     input_grad = send_back(input_grad)
-    four_two = spread_c(spread_b(y_two))
-    four_oqk = spread_c(y_oqk)
+    y_vg, y_oqk, x_two, input_grad = tie(y_vg, y_oqk, x_two, input_grad)
+
+    four_vg = spread_c(spread_b(by_spread([f_vg, *y_vg])))
+    four_two = spread_c(joined(y_two, x_two))
+    four_oqk = spread_c(by_spread([f_oqk, *y_oqk]))
     g_query, g_key = place_quarters(spots, four_oqk, (own, own), (2 * own, own))
     g_value, g_gate = place_quarters(spots, four_vg, (0, own), (own, own))
     [g_two] = place_quarters(spots, four_two, (0, units))

time: 1240 us -> 1200 us (0.968)
  starting transfers between devices: 103 us -> 81.1 us
    ppermute x60, waiting for transfers between devices: 310 us -> 337 us  [move(): return lax.ppermute(x, AXES, pairs)]
    ppermute x4, waiting for transfers between devices: 52.1 us -> 26.2 us  [send_back(): lax.ppermute(lax.dynamic_index_in_dim(slots, (batch_of(place) + p) % 2, 0...]
    ppermute x60, starting transfers between devices: 85.1 us -> 63.8 us  [move(): return lax.ppermute(x, AXES, pairs)]
    select_n x22 -> x23, other arithmetic: 51.3 us -> 48.9 us  [ordered(): jnp.where(index == 0, jnp.concatenate([mine, other], axis), jnp.concatena...]
    unnamed x227 -> x229, local copies, waits for them, and re-layouts: 64.3 us -> 63.5 us
  transfers between devices with their start and end apart: 80 -> 80, of which waited for: 33 -> 32; matrix products, arithmetic and copies ran while one was open for 14% -> 14% of each run, Pallas kernels for 28% -> 29%
where the time goes in v9:
time: 1200 us; the launch traced here: 1190 us
  waiting for transfers between devices  496 us (41%)
  Pallas kernels  350 us (29%)
  other arithmetic  112 us (9%)
  local copies, waits for them, and re-layouts  107 us (9%)
  starting transfers between devices  81.1 us (7%)
  matrix products  31.3 us (3%)
  between operations  17.3 us (1%)
    ppermute x60, waiting for transfers between devices, move(): return lax.ppermute(x, AXES, pairs)  337 us
    ppermute x4, waiting for transfers between devices, bring(): lax.ppermute(lax.dynamic_index_in_dim(x, (place + p) % 2, 0, False), AXES...  119 us
    pallas_call x6, Pallas kernels, fold_half(): pl.pallas_call(functools.partial(fold_kernel, len(values), arrived is not...  96.7 us
    pallas_call x10, Pallas kernels, gradient_rows(): pl.pallas_call(gradient_kernel, out_shape=out, grid_spec=pltpu.PrefetchSc...  88.1 us
    ppermute x60, starting transfers between devices, move(): return lax.ppermute(x, AXES, pairs)  63.8 us
    unnamed x229, local copies, waits for them, and re-layouts  63.5 us
    select_n x23, other arithmetic, ordered(): jnp.where(index == 0, jnp.concatenate([mine, other], axis), jnp.concatena...  48.9 us
    pallas_call x1, Pallas kernels, gated_unit(): pl.pallas_call(unit_kernel, out_shape=outs, grid_spec=pltpu.PrefetchScala...  38.3 us
  transfers between devices with their start and end apart: 80, of which 32 were waited for; matrix products, arithmetic and copies ran while one was open for 14% of the time, Pallas kernels for 29%

profile of v9, /device:TPU:17, one launch (start us, length us, event | category | flops | bytes accessed | tf_op | source)
XLA Modules:
  0.0 1194.4 jit_solution(6716369950660495954)
XLA Ops:
  18.7 75.9 %collective-permute-done.2 = bf16[256,2048]{1,0:T(8,128)(2,1)S(1)} collective-permute-done((bf16[256,2048]{1,0:T(8,128)(2,1)}, bf16[256,2048]{1,0:T(8,128)(2,1)S(1)}, u32[]{:S(2)}, u32[]{:S(2)}) %collective-permute-start.2) | collective-permute-done | bytes 1048608 | tf_op jit(solution)/shard_map/ppermute | solution.py:594
  102.7 37.9 %collective-permute-done.4 = bf16[512,2048]{1,0:T(8,128)(2,1)} collective-permute-done((bf16[512,2048]{1,0:T(8,128)(2,1)}, bf16[512,2048]{1,0:T(8,128)(2,1)}, u32[]{:S(2)}, u32[]{:S(2)}) %collective-permute-start.4) | collective-permute-done | bytes 2097184 | tf_op jit(solution)/shard_map/ppermute | solution.py:543
  140.6 6.2 maximum_select_fusion.1.own_ref
  165.5 18.8 %enter.2 = (bf16[2048,2048]{1,0:T(8,128)(2,1)}, f32[2048,1024]{1,0:T(8,128)}, f32[2048,1]{1,0:T(8,128)S(1)}, bf16[2048,512]{1,0:T(8,128)(2,1)S(1)}) custom-call(s32[4]{0:T(128)S(1)} %pad_add_fusion.1.spots, bf16[1024,2048]{1,0:T(8,128)(2,1)S(1)} %copy-done.15, bf16[1024,2048]{1,0:T(8,128)(2,1)} %collective-permute-done.6.other_ref, ...), custom_call_target="tpu_custom_call" | custom-call | flops 8589934592 | bytes 31465472 | tf_op jit(solution)/shard_map/enter/pallas_call | solution.py:244
  185.3 13.9 %collective-permute-done.7.refs_1_.refs_5_.refs_6_ = bf16[1024,1024]{1,0:T(8,128)(2,1)} collective-permute-done((bf16[1024,1024]{1,0:T(8,128)(2,1)}, bf16[1024,1024]{1,0:T(8,128)(2,1)}, u32[]{:S(2)}, u32[]{:S(2)}) %collective-permute-start.7) | collective-permute-done | bytes 2097184 | tf_op jit(solution)/shard_map/ppermute | solution.py:543
  202.0 14.2 %project.1.zv_ref = f32[2048,1024]{1,0:T(8,128)S(1)} custom-call(s32[4]{0:T(128)S(1)} %pad_add_fusion.1.spots, bf16[2048,2048]{1,0:T(8,128)(2,1)} %get-tuple-element.161.h_ref.left_ref, bf16[1024,1024]{1,0:T(8,128)(2,1)S(1)} %copy-done.40, bf16[1024,1024]{1,0:T(8,128)(2,1)} %collective-permute-done.7.refs_1_.refs_5_.refs_6_), custom_call_target="tpu_custom_call" | custom-call | flops 8589934592 | bytes 20971520 | tf_op jit(solution)/shard_map/project/pallas_call | solution.py:275
  219.6 12.3 %attend.1 = f32[2048,512]{1,0:T(8,128)S(1)} custom-call(f32[4]{0:T(128)S(1)} %dynamic_slice.118.rates, s32[2,2]{1,0:T(2,128)S(1)} %pad_add_fusion.ends, f32[2048,1024]{1,0:T(8,128)S(1)} %copy-done, f32[2048,1024]{1,0:T(8,128)S(1)} %copy-done, f32[2048,1024]{1,0:T(8,128)} %copy-done.1), custom_call_target="tpu_custom_call" | custom-call | flops 4294967296 | bytes 16777216 | tf_op jit(solution)/shard_map/attend/pallas_call | solution.py:98
  242.2 42.2 %collective-permute-done.12 = f32[2048]{0:T(1024)S(1)} collective-permute-done((f32[2048]{0:T(1024)S(1)}, f32[2048]{0:T(1024)S(1)}, u32[]{:S(2)}, u32[]{:S(2)}) %collective-permute-start.12) | collective-permute-done | bytes 8224 | tf_op jit(solution)/shard_map/ppermute | solution.py:543
  291.7 9.5 collective-permute-done.10.refs_1_.refs_3_.refs_4_
  310.4 9.9 fusion.21
  328.5 43.1 %collective-permute-done.16 = bf16[256,2048]{1,0:T(8,128)(2,1)S(1)} collective-permute-done((bf16[256,2048]{1,0:T(8,128)(2,1)S(1)}, bf16[256,2048]{1,0:T(8,128)(2,1)S(1)}, u32[]{:S(2)}, u32[]{:S(2)}) %collective-permute-start.16) | collective-permute-done | bytes 1048608 | tf_op jit(solution)/shard_map/ppermute | solution.py:594
  390.8 38.3 %gated_unit.1 = (bf16[2048,2048]{1,0:T(8,128)(2,1)}, bf16[2048,1408]{1,0:T(8,128)(2,1)}, bf16[2048,1408]{1,0:T(8,128)(2,1)}, bf16[2048,1408]{1,0:T(8,128)(2,1)}, f32[2048,1]{1,0:T(8,128)S(1)}) custom-call(s32[4]{0:T(128)S(1)} %pad_add_fusion.1.spots, bf16[2048,1024]{1,0:T(8,128)(2,1)} %maximum_select_fusion.3.own_ref, ...), custom_call_target="tpu_custom_call" | custom-call | flops 23622320128 | bytes 45621248 | tf_op jit(solution)/shard_map/gated_unit/pallas_call | solution.py:337
  438.2 6.8 collective-permute-done.20.other_ref
  451.7 9.2 gradient_rows.10
  462.4 10.5 all-gather.17.cloned.1.call-done.refs_0_.refs_1_.refs_2_
  476.3 22.5 %gated_unit_back.1 = (bf16[2048,1408]{1,0:T(8,128)(2,1)S(1)}, bf16[2048,1408]{1,0:T(8,128)(2,1)S(1)}, f32[2048,1]{1,0:T(8,128)S(1)}) custom-call(s32[4]{0:T(128)S(1)} %pad_add_fusion.1.spots, bf16[2048,2048]{1,0:T(8,128)(2,1)} %get-tuple-element.183.left_ref.dy_ref, bf16[2048,1408]{1,0:T(8,128)(2,1)} %get-tuple-element.187.one_ref, ...), custom_call_target="tpu_custom_call" | custom-call | flops 11811160064 | bytes 37232640 | tf_op jit(solution)/shard_map/gated_unit_back/pallas_call | solution.py:374
  504.8 19.8 %fold_half.6 = bf16[2048,1024]{1,0:T(8,128)(2,1)} custom-call(s32[4]{0:T(128)S(1)} %pad_add_fusion.1.spots, bf16[2048,1408]{1,0:T(8,128)(2,1)} %copy-done.50, bf16[2048,1408]{1,0:T(8,128)(2,1)} %copy-done.48, bf16[1024,1408]{1,0:T(8,128)(2,1)S(1)} %copy-done.30, bf16[1024,1408]{1,0:T(8,128)(2,1)} %collective-permute-done.10.refs_1_.refs_3_.refs_4_, ...), custom_call_target="tpu_custom_call" | custom-call | flops 11811160064 | bytes 21495808 | tf_op jit(solution)/shard_map/fold_half/pallas_call | solution.py:435
  530.6 11.4 fold_half.7
  542.0 9.3 gradient_rows.11
  572.9 21.8 %fold_half.8 = (bf16[2048,512]{1,0:T(8,128)(2,1)}, f32[2048,512]{1,0:T(8,128)}) custom-call(s32[4]{0:T(128)S(1)} %pad_add_fusion.1.spots, bf16[2048,1408]{1,0:T(8,128)(2,1)} %copy-done.50, bf16[2048,1408]{1,0:T(8,128)(2,1)} %copy-done.48, bf16[2048,1024]{1,0:T(8,128)(2,1)} %copy-done.90, bf16[1024,1408]{1,0:T(8,128)(2,1)S(1)} %copy-done.31, ...), custom_call_target="tpu_custom_call" | custom-call | flops 11811160064 | bytes 27787264 | tf_op jit(solution)/shard_map/fold_half/pallas_call | solution.py:435
  600.6 12.8 %fold_half.9 = (bf16[2048,512]{1,0:T(8,128)(2,1)S(1)}, f32[2048,512]{1,0:T(8,128)S(1)}) custom-call(s32[4]{0:T(128)S(1)} %pad_add_fusion.1.spots, bf16[2048,1408]{1,0:T(8,128)(2,1)} %get-tuple-element.206.right_ref.refs_0_, bf16[2048,1024]{1,0:T(8,128)(2,1)} %collective-permute-done.27.refs_1_, ...), custom_call_target="tpu_custom_call" | custom-call | flops 5905580032 | bytes 16252928 | tf_op jit(solution)/shard_map/fold_half/pallas_call | solution.py:435
  616.7 9.2 gradient_rows.12
  630.1 9.4 gradient_rows.13
  661.4 12.3 %convolution_convert_fusion.1 = bf16[2048,512]{1,0:T(8,128)(2,1)S(1)} fusion(f32[2048,512]{1,0:T(8,128)} %copy-done.52, f32[2048]{0:T(1024)S(1)} %add_rsqrt_fusion, bf16[2048,1024]{1,0:T(8,128)(2,1)} %collective-permute-done.13, bf16[2048,1024]{1,0:T(8,128)(2,1)} %maximum_select_fusion.2, pred[]{:T(512)S(6)} %eq.51), kind=kOutput, calls=%fused_computation.28 | convolution fusion | flops 4335861760 | bytes 14688257 | tf_op jit(solution)/shard_map/dot_general | solution.py:32
  685.8 15.4 %collective-permute-done.33 = bf16[640,1408]{1,0:T(8,128)(2,1)} collective-permute-done((bf16[640,1408]{1,0:T(8,128)(2,1)}, bf16[640,1408]{1,0:T(8,128)(2,1)}, u32[]{:S(2)}, u32[]{:S(2)}) %collective-permute-start.33) | collective-permute-done | bytes 1802272 | tf_op jit(solution)/shard_map/ppermute | solution.py:543
  701.3 5.9 collective-permute-done.31
  717.7 10.0 gradient_rows.14
  727.7 7.3 collective-permute-done.35
  735.0 18.6 %collective-permute-done.36 = f32[2048]{0:T(1024)S(1)} collective-permute-done((f32[2048]{0:T(1024)S(1)}, f32[2048]{0:T(1024)S(1)}, u32[]{:S(2)}, u32[]{:S(2)}) %collective-permute-start.36) | collective-permute-done | bytes 8224 | tf_op jit(solution)/shard_map/ppermute | solution.py:543
  763.7 21.3 %attend_back.1 = (bf16[2048,512]{1,0:T(8,128)(2,1)S(1)}, bf16[2048,512]{1,0:T(8,128)(2,1)S(1)}, bf16[2048,512]{1,0:T(8,128)(2,1)S(1)}) custom-call(f32[4]{0:T(128)S(1)} %copy-done.28, s32[2,2]{1,0:T(2,128)S(1)} %copy-done.26, f32[2048,1024]{1,0:T(8,128)} %get-tuple-element.160.zq_ref.zk_ref, f32[2048,1024]{1,0:T(8,128)} %get-tuple-element.160.zq_ref.zk_ref, ...), custom_call_target="tpu_custom_call" | custom-call | flops 10737418240 | bytes 20971520 | tf_op jit(solution)/shard_map/attend_back/pallas_call | solution.py:119
  785.7 7.8 gradient_rows.15
  799.2 10.0 gradient_rows.16
  827.6 8.1 gradient_rows.17
  840.3 13.9 %fold_half.10 = bf16[2048,1024]{1,0:T(8,128)(2,1)S(1)} custom-call(s32[4]{0:T(128)S(1)} %pad_add_fusion.1.spots, bf16[2048,1024]{1,0:T(8,128)(2,1)} %copy-done.7, bf16[2048,1024]{1,0:T(8,128)(2,1)} %pad_maximum_fusion.refs_1_.right_ref, bf16[1024,1024]{1,0:T(8,128)(2,1)S(1)} %copy-done.39, bf16[1024,1024]{1,0:T(8,128)(2,1)S(1)} %copy-done.44, ...), custom_call_target="tpu_custom_call" | custom-call | flops 8589934592 | bytes 16777216 | tf_op jit(solution)/shard_map/fold_half/pallas_call | solution.py:435
  854.2 14.4 %collective-permute-done.41 = bf16[512,1024]{1,0:T(8,128)(2,1)} collective-permute-done((bf16[512,1024]{1,0:T(8,128)(2,1)}, bf16[512,1024]{1,0:T(8,128)(2,1)}, u32[]{:S(2)}, u32[]{:S(2)}) %collective-permute-start.41) | collective-permute-done | bytes 1048608 | tf_op jit(solution)/shard_map/ppermute | solution.py:543
  868.7 15.4 %collective-permute-done.43 = bf16[256,1408]{1,0:T(8,128)(2,1)S(1)} collective-permute-done((bf16[256,1408]{1,0:T(8,128)(2,1)}, bf16[256,1408]{1,0:T(8,128)(2,1)S(1)}, u32[]{:S(2)}, u32[]{:S(2)}) %collective-permute-start.43) | collective-permute-done | bytes 720928 | tf_op jit(solution)/shard_map/ppermute | solution.py:543
  904.7 16.9 %fold_half.11 = (bf16[2048,512]{1,0:T(8,128)(2,1)}, f32[2048,512]{1,0:T(8,128)}) custom-call(s32[4]{0:T(128)S(1)} %pad_add_fusion.1.spots, bf16[2048,1024]{1,0:T(8,128)(2,1)} %copy-done.7, bf16[2048,1024]{1,0:T(8,128)(2,1)} %pad_maximum_fusion.refs_1_.right_ref, bf16[2048,1024]{1,0:T(8,128)(2,1)} %collective-permute-done.44.refs_2_, ...), custom_call_target="tpu_custom_call" | custom-call | flops 8589934592 | bytes 23068672 | tf_op jit(solution)/shard_map/fold_half/pallas_call | solution.py:435
  924.6 23.3 %collective-permute-done.48 = bf16[256,2048]{1,0:T(8,128)(2,1)S(1)} collective-permute-done((bf16[256,2048]{1,0:T(8,128)(2,1)}, bf16[256,2048]{1,0:T(8,128)(2,1)S(1)}, u32[]{:S(2)}, u32[]{:S(2)}) %collective-permute-start.48) | collective-permute-done | bytes 1048608 | tf_op jit(solution)/shard_map/ppermute | solution.py:602
  951.1 7.9 gradient_rows.19
  967.2 42.7 %collective-permute-done.52 = f32[2048]{0:T(1024)S(1)} collective-permute-done((f32[2048]{0:T(1024)S(1)}, f32[2048]{0:T(1024)S(1)}, u32[]{:S(2)}, u32[]{:S(2)}) %collective-permute-start.52) | collective-permute-done | bytes 8224 | tf_op jit(solution)/shard_map/ppermute | solution.py:543
  1012.2 7.4 gradient_rows.18
  1030.1 24.1 %collective-permute-done.54 = bf16[2,512,512]{2,1,0:T(8,128)(2,1)S(1)} collective-permute-done((bf16[2,512,512]{2,1,0:T(8,128)(2,1)S(1)}, bf16[2,512,512]{2,1,0:T(8,128)(2,1)S(1)}, u32[]{:S(2)}, u32[]{:S(2)}) %collective-permute-start.54) | collective-permute-done | bytes 1048608 | tf_op jit(solution)/shard_map/ppermute | solution.py:543
  1060.3 7.1 place_quarters.5
  1070.5 7.1 place_quarters.6
  1087.0 40.6 %collective-permute-done.59 = bf16[256,1024]{1,0:T(8,128)(2,1)S(1)} collective-permute-done((bf16[256,1024]{1,0:T(8,128)(2,1)S(1)}, bf16[256,1024]{1,0:T(8,128)(2,1)S(1)}, u32[]{:S(2)}, u32[]{:S(2)}) %collective-permute-start.59) | collective-permute-done | bytes 524320 | tf_op jit(solution)/shard_map/ppermute | solution.py:543
  1143.5 16.6 %collective-permute-done.65 = bf16[512,1024]{1,0:T(8,128)(2,1)} collective-permute-done((bf16[512,1024]{1,0:T(8,128)(2,1)}, bf16[512,1024]{1,0:T(8,128)(2,1)}, u32[]{:S(2)}, u32[]{:S(2)}) %collective-permute-start.65) | collective-permute-done | bytes 1048608 | tf_op jit(solution)/shard_map/ppermute | solution.py:543
  1163.3 7.8 place_quarters.9
  1176.4 6.2 place_quarters.7
  (489 shorter events, 344.3 us)
Async XLA Ops:
  8.0 88.9 %all-gather.7.cloned.1.call-start = ((), (), s32[]{:S(2)}) async-start(), calls=%async_computation.6 | async-start | bytes 2621440 | tf_op jit(solution)/shard_map/all_gather | solution.py:664
  10.3 136.6 %all-gather.9.cloned.1.call-start = ((), (), s32[]{:S(2)}) async-start(), calls=%async_computation.7 | async-start | bytes 2621440 | tf_op jit(solution)/shard_map/all_gather | solution.py:664
  12.5 172.8 %all-gather.11.cloned.1.call-start = ((), (), s32[]{:S(2)}) async-start(), calls=%async_computation.8 | async-start | bytes 1310720 | tf_op jit(solution)/shard_map/all_gather | solution.py:664
  13.7 80.9 %collective-permute-start.2 = (bf16[256,2048]{1,0:T(8,128)(2,1)}, bf16[256,2048]{1,0:T(8,128)(2,1)S(1)}, u32[]{:S(2)}, u32[]{:S(2)}) collective-permute-start(bf16[256,2048]{1,0:T(8,128)(2,1)} %get-tuple-element.326), channel_id=1, source_target_pairs={{0,0},{4,1},{1,2},{5,3},{2,4},{6,5},{3,6},{7,7},{8,8},{12,9},{9,10... | collective-permute-start | bytes 3145736 | tf_op jit(solution)/shard_map/ppermute | solution.py:594
  15.8 78.8 %collective-permute-start.3 = (bf16[256,2048]{1,0:T(8,128)(2,1)S(1)}, bf16[256,2048]{1,0:T(8,128)(2,1)S(1)}, u32[]{:S(2)}, u32[]{:S(2)}) collective-permute-start(bf16[256,2048]{1,0:T(8,128)(2,1)S(1)} %get-tuple-element.327), channel_id=1, source_target_pairs={{1,0},{5,1},{0,2},{4,3},{3,4},{7,5},{2,6},{6,7},{9,8},{13,9},{8,10... | collective-permute-start | bytes 3145736 | tf_op jit(solution)/shard_map/ppermute | solution.py:594
  96.9 43.7 %collective-permute-start.4 = (bf16[512,2048]{1,0:T(8,128)(2,1)}, bf16[512,2048]{1,0:T(8,128)(2,1)}, u32[]{:S(2)}, u32[]{:S(2)}) collective-permute-start(bf16[512,2048]{1,0:T(8,128)(2,1)} %maximum_select_fusion.6), channel_id=1, source_target_pairs={{0,8},{1,9},{2,10},{3,11},{4,12},{5,13},{6,14},{7,15},{8,0},{9,1},... | collective-permute-start | bytes 6291464 | tf_op jit(solution)/shard_map/ppermute | solution.py:543
  98.9 139.1 %all-gather.13.cloned.1.call-start = ((), (), s32[]{:S(2)}) async-start(), calls=%async_computation.9 | async-start | bytes 3604480 | tf_op jit(solution)/shard_map/all_gather | solution.py:664
  99.0 47.9 %collective-permute-start.5 = (bf16[1024,1024]{1,0:T(8,128)(2,1)}, bf16[1024,1024]{1,0:T(8,128)(2,1)S(1)}, u32[]{:S(2)}, u32[]{:S(2)}) collective-permute-start(bf16[1024,1024]{1,0:T(8,128)(2,1)} %all-gather.7.cloned.1.call-done.refs_0_.refs_2_.refs_3_), channel_id=1, source_target_pairs={{0,16},{1,17},{2,18},{3,19},{4,20},{5,21},{6,22},{7,23},{8,24},{9,... | collective-permute-start | bytes 6291464 | tf_op jit(solution)/shard_map/ppermute | solution.py:543
  102.7 189.0 %all-gather.15.cloned.1.call-start = ((), (), s32[]{:S(2)}) async-start(), calls=%async_computation.10 | async-start | bytes 3604480 | tf_op jit(solution)/shard_map/all_gather | solution.py:664
  151.6 47.5 %collective-permute-start.7 = (bf16[1024,1024]{1,0:T(8,128)(2,1)}, bf16[1024,1024]{1,0:T(8,128)(2,1)}, u32[]{:S(2)}, u32[]{:S(2)}) collective-permute-start(bf16[1024,1024]{1,0:T(8,128)(2,1)} %all-gather.9.cloned.1.call-done.refs_0_.refs_4_.refs_5_), channel_id=1, source_target_pairs={{0,16},{1,17},{2,18},{3,19},{4,20},{5,21},{6,22},{7,23},{8,24},{9,... | collective-permute-start | bytes 6291464 | tf_op jit(solution)/shard_map/ppermute | solution.py:543
  157.7 315.2 %all-gather.17.cloned.1.call-start = ((), (), s32[]{:S(2)}) async-start(), calls=%async_computation.11 | async-start | bytes 6488064 | tf_op jit(solution)/shard_map/all_gather | solution.py:668
  238.0 63.2 %collective-permute-start.10 = (bf16[1024,1408]{1,0:T(8,128)(2,1)}, bf16[1024,1408]{1,0:T(8,128)(2,1)}, u32[]{:S(2)}, u32[]{:S(2)}) collective-permute-start(bf16[1024,1408]{1,0:T(8,128)(2,1)} %all-gather.13.cloned.1.call-done.refs_0_.refs_2_.refs_3_), channel_id=1, source_target_pairs={{0,16},{1,17},{2,18},{3,19},{4,20},{5,21},{6,22},{7,23},{8,24},{9,... | collective-permute-start | bytes 8650760 | tf_op jit(solution)/shard_map/ppermute | solution.py:543
  238.2 46.2 %collective-permute-start.9 = (bf16[2048,512]{1,0:T(8,128)(2,1)}, bf16[2048,512]{1,0:T(8,128)(2,1)S(1)}, u32[]{:S(2)}, u32[]{:S(2)}) collective-permute-start(bf16[2048,512]{1,0:T(8,128)(2,1)} %get-tuple-element.164), channel_id=1, source_target_pairs={{0,8},{1,9},{2,10},{3,11},{4,12},{5,13},{6,14},{7,15},{8,0},{9,1},... | collective-permute-start | bytes 6291464 | tf_op jit(solution)/shard_map/ppermute | solution.py:543
  242.0 42.5 %collective-permute-start.12 = (f32[2048]{0:T(1024)S(1)}, f32[2048]{0:T(1024)S(1)}, u32[]{:S(2)}, u32[]{:S(2)}) collective-permute-start(f32[2048]{0:T(1024)S(1)} %add.256), channel_id=1, source_target_pairs={{0,8},{1,9},{2,10},{3,11},{4,12},{5,13},{6,14},{7,15},{8,0},{9,1},... | collective-permute-start | bytes 24584 | tf_op jit(solution)/shard_map/ppermute | solution.py:543
  307.4 69.2 %collective-permute-start.15 = (bf16[1024,1408]{1,0:T(8,128)(2,1)S(1)}, bf16[1024,1408]{1,0:T(8,128)(2,1)S(1)}, u32[]{:S(2)}, u32[]{:S(2)}) collective-permute-start(bf16[1024,1408]{1,0:T(8,128)(2,1)S(1)} %copy-done.32), channel_id=1, source_target_pairs={{0,16},{1,17},{2,18},{3,19},{4,20},{5,21},{6,22},{7,23},{8,24},{9,... | collective-permute-start | bytes 8650760 | tf_op jit(solution)/shard_map/ppermute | solution.py:543
  320.3 53.6 %collective-permute-start.14 = (bf16[2048,512]{1,0:T(8,128)(2,1)}, bf16[2048,512]{1,0:T(8,128)(2,1)S(1)}, u32[]{:S(2)}, u32[]{:S(2)}) collective-permute-start(bf16[2048,512]{1,0:T(8,128)(2,1)} %get-tuple-element.330), channel_id=1, source_target_pairs={{0,8},{1,9},{2,10},{3,11},{4,12},{5,13},{6,14},{7,15},{8,0},{9,1},... | collective-permute-start | bytes 6291464 | tf_op jit(solution)/shard_map/ppermute | solution.py:543
  323.3 48.3 %collective-permute-start.16 = (bf16[256,2048]{1,0:T(8,128)(2,1)S(1)}, bf16[256,2048]{1,0:T(8,128)(2,1)S(1)}, u32[]{:S(2)}, u32[]{:S(2)}) collective-permute-start(bf16[256,2048]{1,0:T(8,128)(2,1)S(1)} %get-tuple-element.322), channel_id=1, source_target_pairs={{0,0},{4,1},{1,2},{5,3},{2,4},{6,5},{3,6},{7,7},{8,8},{12,9},{9,10... | collective-permute-start | bytes 3145736 | tf_op jit(solution)/shard_map/ppermute | solution.py:594
  328.4 43.2 %collective-permute-start.17 = (bf16[256,2048]{1,0:T(8,128)(2,1)S(1)}, bf16[256,2048]{1,0:T(8,128)(2,1)S(1)}, u32[]{:S(2)}, u32[]{:S(2)}) collective-permute-start(bf16[256,2048]{1,0:T(8,128)(2,1)S(1)} %get-tuple-element.323), channel_id=1, source_target_pairs={{1,0},{5,1},{0,2},{4,3},{3,4},{7,5},{2,6},{6,7},{9,8},{13,9},{8,10... | collective-permute-start | bytes 3145736 | tf_op jit(solution)/shard_map/ppermute | solution.py:594
  384.0 369.7 %reduce-scatter.7.cloned.1.call-start = ((), (), s32[]{:S(2)}) async-start(), calls=%async_computation.12 | async-start | bytes 3604480 | tf_op jit(solution)/shard_map/reduce_scatter | solution.py:705
  384.6 47.6 %collective-permute-start.19 = (bf16[512,2048]{1,0:T(8,128)(2,1)}, bf16[512,2048]{1,0:T(8,128)(2,1)S(1)}, u32[]{:S(2)}, u32[]{:S(2)}) collective-permute-start(bf16[512,2048]{1,0:T(8,128)(2,1)} %maximum_select_fusion.8), channel_id=1, source_target_pairs={{0,8},{1,9},{2,10},{3,11},{4,12},{5,13},{6,14},{7,15},{8,0},{9,1},... | collective-permute-start | bytes 6291464 | tf_op jit(solution)/shard_map/ppermute | solution.py:543
  476.1 48.6 %collective-permute-start.21 = (bf16[768,1408]{1,0:T(8,128)(2,1)}, bf16[768,1408]{1,0:T(8,128)(2,1)}, u32[]{:S(2)}, u32[]{:S(2)}) collective-permute-start(bf16[768,1408]{1,0:T(8,128)(2,1)} %slice.120), channel_id=1, source_target_pairs={{0,16},{1,17},{2,18},{3,19},{4,20},{5,21},{6,22},{7,23},{8,24},{9,... | collective-permute-start | bytes 6488072 | tf_op jit(solution)/shard_map/ppermute | solution.py:543
  554.9 42.8 %collective-permute-start.27 = (bf16[2048,1024]{1,0:T(8,128)(2,1)}, bf16[2048,1024]{1,0:T(8,128)(2,1)}, u32[]{:S(2)}, u32[]{:S(2)}) collective-permute-start(bf16[2048,1024]{1,0:T(8,128)(2,1)} %fold_half.7), channel_id=1, source_target_pairs={{0,4},{1,5},{2,6},{3,7},{4,0},{5,1},{6,2},{7,3},{8,12},{9,13},{10,... | collective-permute-start | bytes 12582920 | tf_op jit(solution)/shard_map/ppermute | solution.py:543
  597.7 46.2 %collective-permute-start.28 = (bf16[2048,512]{1,0:T(8,128)(2,1)}, bf16[2048,512]{1,0:T(8,128)(2,1)}, u32[]{:S(2)}, u32[]{:S(2)}) collective-permute-start(bf16[2048,512]{1,0:T(8,128)(2,1)} %get-tuple-element.205), channel_id=1, source_target_pairs={{0,8},{1,9},{2,10},{3,11},{4,12},{5,13},{6,14},{7,15},{8,0},{9,1},... | collective-permute-start | bytes 6291464 | tf_op jit(solution)/shard_map/ppermute | solution.py:543
  598.0 47.3 %collective-permute-start.29 = (bf16[768,1408]{1,0:T(8,128)(2,1)}, bf16[768,1408]{1,0:T(8,128)(2,1)}, u32[]{:S(2)}, u32[]{:S(2)}) collective-permute-start(bf16[768,1408]{1,0:T(8,128)(2,1)} %slice.122), channel_id=1, source_target_pairs={{0,16},{1,17},{2,18},{3,19},{4,20},{5,21},{6,22},{7,23},{8,24},{9,... | collective-permute-start | bytes 6488072 | tf_op jit(solution)/shard_map/ppermute | solution.py:543
  656.9 178.8 %reduce-scatter.9.cloned.1.call-start = ((), (), s32[]{:S(2)}) async-start(), calls=%async_computation.13 | async-start | bytes 3604480 | tf_op jit(solution)/shard_map/reduce_scatter | solution.py:705
  660.1 47.0 %collective-permute-start.31 = (bf16[2048,512]{1,0:T(8,128)(2,1)S(1)}, bf16[2048,512]{1,0:T(8,128)(2,1)}, u32[]{:S(2)}, u32[]{:S(2)}) collective-permute-start(bf16[2048,512]{1,0:T(8,128)(2,1)S(1)} %copy-done.47), channel_id=1, source_target_pairs={{0,8},{1,9},{2,10},{3,11},{4,12},{5,13},{6,14},{7,15},{8,0},{9,1},... | collective-permute-start | bytes 6291464 | tf_op jit(solution)/shard_map/ppermute | solution.py:543
  707.1 46.5 %collective-permute-start.34 = (bf16[2048,512]{1,0:T(8,128)(2,1)}, bf16[2048,512]{1,0:T(8,128)(2,1)}, u32[]{:S(2)}, u32[]{:S(2)}) collective-permute-start(bf16[2048,512]{1,0:T(8,128)(2,1)} %dynamic-slice_convert_fusion), channel_id=1, source_target_pairs={{0,8},{1,9},{2,10},{3,11},{4,12},{5,13},{6,14},{7,15},{8,0},{9,1},... | collective-permute-start | bytes 6291464 | tf_op jit(solution)/shard_map/ppermute | solution.py:543
  753.7 212.9 %reduce-scatter.11.cloned.1.call-start = ((), (), s32[]{:S(2)}) async-start(), calls=%async_computation.14 | async-start | bytes 3604480 | tf_op jit(solution)/shard_map/reduce_scatter | solution.py:705
  753.7 55.5 %collective-permute-start.37 = (bf16[256,1408]{1,0:T(8,128)(2,1)}, bf16[256,1408]{1,0:T(8,128)(2,1)}, u32[]{:S(2)}, u32[]{:S(2)}) collective-permute-start(bf16[256,1408]{1,0:T(8,128)(2,1)} %reduce-scatter.7.cloned.1.call-done), channel_id=1, source_target_pairs={{0,16},{1,17},{2,18},{3,19},{4,20},{5,21},{6,22},{7,23},{8,24},{9,... | collective-permute-start | bytes 2162696 | tf_op jit(solution)/shard_map/ppermute | solution.py:543
  755.2 54.0 %collective-permute-start.39 = (bf16[1024,512]{1,0:T(8,128)(2,1)}, bf16[1024,512]{1,0:T(8,128)(2,1)}, u32[]{:S(2)}, u32[]{:S(2)}) collective-permute-start(bf16[1024,512]{1,0:T(8,128)(2,1)} %get-tuple-element.240), channel_id=1, source_target_pairs={{0,16},{1,17},{2,18},{3,19},{4,20},{5,21},{6,22},{7,23},{8,24},{9,... | collective-permute-start | bytes 3145736 | tf_op jit(solution)/shard_map/ppermute | solution.py:543
  756.7 52.5 %collective-permute-start.38 = (bf16[2,512,512]{2,1,0:T(8,128)(2,1)}, bf16[2,512,512]{2,1,0:T(8,128)(2,1)}, u32[]{:S(2)}, u32[]{:S(2)}) collective-permute-start(bf16[2,512,512]{2,1,0:T(8,128)(2,1)} %get-tuple-element.319), channel_id=1, source_target_pairs={{0,8},{1,9},{2,10},{3,11},{4,12},{5,13},{6,14},{7,15},{8,0},{9,1},... | collective-permute-start | bytes 3145736 | tf_op jit(solution)/shard_map/ppermute | solution.py:543
  809.2 211.7 %reduce-scatter.13.cloned.1.call-start = ((), (), s32[]{:S(2)}) async-start(), calls=%async_computation.15 | async-start | bytes 1310720 | tf_op jit(solution)/shard_map/reduce_scatter | solution.py:705
  819.7 49.0 %collective-permute-start.42 = (bf16[512,1408]{1,0:T(8,128)(2,1)}, bf16[512,1408]{1,0:T(8,128)(2,1)}, u32[]{:S(2)}, u32[]{:S(2)}) collective-permute-start(bf16[512,1408]{1,0:T(8,128)(2,1)} %maximum_select_fusion.16), channel_id=1, source_target_pairs={{0,8},{1,9},{2,10},{3,11},{4,12},{5,13},{6,14},{7,15},{8,0},{9,1},... | collective-permute-start | bytes 4325384 | tf_op jit(solution)/shard_map/ppermute | solution.py:543
  821.4 100.3 %collective-permute-start.45 = (bf16[512,1024]{1,0:T(8,128)(2,1)}, bf16[512,1024]{1,0:T(8,128)(2,1)}, u32[]{:S(2)}, u32[]{:S(2)}) collective-permute-start(bf16[512,1024]{1,0:T(8,128)(2,1)} %get-tuple-element.316), channel_id=1, source_target_pairs={{0,16},{1,17},{2,18},{3,19},{4,20},{5,21},{6,22},{7,23},{8,24},{9,... | collective-permute-start | bytes 3145736 | tf_op jit(solution)/shard_map/ppermute | solution.py:543
  822.8 45.8 %collective-permute-start.41 = (bf16[512,1024]{1,0:T(8,128)(2,1)}, bf16[512,1024]{1,0:T(8,128)(2,1)}, u32[]{:S(2)}, u32[]{:S(2)}) collective-permute-start(bf16[512,1024]{1,0:T(8,128)(2,1)} %get-tuple-element.317), channel_id=1, source_target_pairs={{0,16},{1,17},{2,18},{3,19},{4,20},{5,21},{6,22},{7,23},{8,24},{9,... | collective-permute-start | bytes 3145736 | tf_op jit(solution)/shard_map/ppermute | solution.py:543
  825.4 231.7 %reduce-scatter.15.cloned.1.call-start = ((), (), s32[]{:S(2)}) async-start(), calls=%async_computation.16 | async-start | bytes 2621440 | tf_op jit(solution)/shard_map/reduce_scatter | solution.py:705
  835.7 48.4 %collective-permute-start.43 = (bf16[256,1408]{1,0:T(8,128)(2,1)}, bf16[256,1408]{1,0:T(8,128)(2,1)S(1)}, u32[]{:S(2)}, u32[]{:S(2)}) collective-permute-start(bf16[256,1408]{1,0:T(8,128)(2,1)} %reduce-scatter.9.cloned.1.call-done), channel_id=1, source_target_pairs={{0,16},{1,17},{2,18},{3,19},{4,20},{5,21},{6,22},{7,23},{8,24},{9,... | collective-permute-start | bytes 2162696 | tf_op jit(solution)/shard_map/ppermute | solution.py:543
  894.8 53.1 %collective-permute-start.47 = (bf16[512,1408]{1,0:T(8,128)(2,1)S(1)}, bf16[512,1408]{1,0:T(8,128)(2,1)S(1)}, u32[]{:S(2)}, u32[]{:S(2)}) collective-permute-start(bf16[512,1408]{1,0:T(8,128)(2,1)S(1)} %maximum_select_fusion.17), channel_id=1, source_target_pairs={{0,8},{1,9},{2,10},{3,11},{4,12},{5,13},{6,14},{7,15},{8,0},{9,1},... | collective-permute-start | bytes 4325384 | tf_op jit(solution)/shard_map/ppermute | solution.py:543
  901.2 46.7 %collective-permute-start.48 = (bf16[256,2048]{1,0:T(8,128)(2,1)}, bf16[256,2048]{1,0:T(8,128)(2,1)S(1)}, u32[]{:S(2)}, u32[]{:S(2)}) collective-permute-start(bf16[256,2048]{1,0:T(8,128)(2,1)} %get-tuple-element.313), channel_id=1, source_target_pairs={{0,0},{1,4},{2,1},{3,5},{4,2},{5,6},{6,3},{7,7},{8,8},{9,12},{10,9... | collective-permute-start | bytes 3145736 | tf_op jit(solution)/shard_map/ppermute | solution.py:602
  959.0 118.7 %reduce-scatter.17.cloned.1.call-start = ((), (), s32[]{:S(2)}) async-start(), calls=%async_computation.17 | async-start | bytes 2621440 | tf_op jit(solution)/shard_map/reduce_scatter | solution.py:705
  962.1 47.7 %collective-permute-start.50 = (bf16[2048,512]{1,0:T(8,128)(2,1)}, bf16[2048,512]{1,0:T(8,128)(2,1)}, u32[]{:S(2)}, u32[]{:S(2)}) collective-permute-start(bf16[2048,512]{1,0:T(8,128)(2,1)} %get-tuple-element.259), channel_id=1, source_target_pairs={{0,8},{1,9},{2,10},{3,11},{4,12},{5,13},{6,14},{7,15},{8,0},{9,1},... | collective-permute-start | bytes 6291464 | tf_op jit(solution)/shard_map/ppermute | solution.py:543
  962.8 47.2 %collective-permute-start.51 = (bf16[1024,1024]{1,0:T(8,128)(2,1)}, bf16[1024,1024]{1,0:T(8,128)(2,1)}, u32[]{:S(2)}, u32[]{:S(2)}) collective-permute-start(bf16[1024,1024]{1,0:T(8,128)(2,1)} %gradient_rows.17), channel_id=1, source_target_pairs={{0,16},{1,17},{2,18},{3,19},{4,20},{5,21},{6,22},{7,23},{8,24},{9,... | collective-permute-start | bytes 6291464 | tf_op jit(solution)/shard_map/ppermute | solution.py:543
  964.0 45.9 %collective-permute-start.52 = (f32[2048]{0:T(1024)S(1)}, f32[2048]{0:T(1024)S(1)}, u32[]{:S(2)}, u32[]{:S(2)}) collective-permute-start(f32[2048]{0:T(1024)S(1)} %add.284), channel_id=1, source_target_pairs={{0,8},{1,9},{2,10},{3,11},{4,12},{5,13},{6,14},{7,15},{8,0},{9,1},... | collective-permute-start | bytes 24584 | tf_op jit(solution)/shard_map/ppermute | solution.py:543
  1022.5 48.0 %collective-permute-start.58 = (bf16[512,2816]{1,0:T(8,128)(2,1)}, bf16[512,2816]{1,0:T(8,128)(2,1)}, u32[]{:S(2)}, u32[]{:S(2)}) collective-permute-start(bf16[512,2816]{1,0:T(8,128)(2,1)} %pad_maximum_fusion.5.refs_0_.refs_1_), channel_id=1, source_target_pairs={{0,4},{1,5},{2,6},{3,7},{4,0},{5,1},{6,2},{7,3},{8,12},{9,13},{10,... | collective-permute-start | bytes 8650760 | tf_op jit(solution)/shard_map/ppermute | solution.py:543
  1079.5 48.1 %collective-permute-start.61 = (bf16[512,1408]{1,0:T(8,128)(2,1)S(1)}, bf16[512,1408]{1,0:T(8,128)(2,1)S(1)}, u32[]{:S(2)}, u32[]{:S(2)}) collective-permute-start(bf16[512,1408]{1,0:T(8,128)(2,1)S(1)} %maximum_select_fusion.18), channel_id=1, source_target_pairs={{0,8},{1,9},{2,10},{3,11},{4,12},{5,13},{6,14},{7,15},{8,0},{9,1},... | collective-permute-start | bytes 4325384 | tf_op jit(solution)/shard_map/ppermute | solution.py:543
  1081.4 47.1 %collective-permute-start.60 = (bf16[256,3072]{1,0:T(8,128)(2,1)S(1)}, bf16[256,3072]{1,0:T(8,128)(2,1)S(1)}, u32[]{:S(2)}, u32[]{:S(2)}) collective-permute-start(bf16[256,3072]{1,0:T(8,128)(2,1)S(1)} %constant_dynamic-update-slice_fusion.2), channel_id=1, source_target_pairs={{0,16},{1,17},{2,18},{3,19},{4,20},{5,21},{6,22},{7,23},{8,24},{9,... | collective-permute-start | bytes 4718600 | tf_op jit(solution)/shard_map/ppermute | solution.py:543
  1083.3 44.2 %collective-permute-start.63 = (bf16[256,2048]{1,0:T(8,128)(2,1)S(1)}, bf16[256,2048]{1,0:T(8,128)(2,1)S(1)}, u32[]{:S(2)}, u32[]{:S(2)}) collective-permute-start(bf16[256,2048]{1,0:T(8,128)(2,1)S(1)} %get-tuple-element.306), channel_id=1, source_target_pairs={{0,1},{1,5},{2,0},{3,4},{4,3},{5,7},{6,2},{7,6},{8,9},{9,13},{10,8... | collective-permute-start | bytes 3145736 | tf_op jit(solution)/shard_map/ppermute | solution.py:602
  1084.7 42.8 %collective-permute-start.62 = (bf16[256,2048]{1,0:T(8,128)(2,1)S(1)}, bf16[256,2048]{1,0:T(8,128)(2,1)S(1)}, u32[]{:S(2)}, u32[]{:S(2)}) collective-permute-start(bf16[256,2048]{1,0:T(8,128)(2,1)S(1)} %get-tuple-element.307), channel_id=1, source_target_pairs={{0,0},{1,4},{2,1},{3,5},{4,2},{5,6},{6,3},{7,7},{8,8},{9,12},{10,9... | collective-permute-start | bytes 3145736 | tf_op jit(solution)/shard_map/ppermute | solution.py:602
  (134 other events, 2240.6 us)
Sparse Core Ops, SparseCore 0:
  11.0 82.8 all-gather.6
  96.1 46.1 all-gather.8
  144.4 27.5 all-gather.10
  173.9 57.8 all-gather.12
  233.8 57.8 all-gather.14
  657.1 54.6 reduce-scatter.6
  753.8 57.5 reduce-scatter.8
  814.3 56.0 reduce-scatter.10
  872.6 25.7 reduce-scatter.12
  959.1 43.7 reduce-scatter.14
  1021.1 44.2 reduce-scatter.16
Sparse Core Ops, SparseCore 1:
  384.1 88.8 all-gather.16

commit v10 on v6

--- a/solution.py
+++ b/solution.py
@@ -497,8 +497,8 @@
                 out_ref[...] = refs[n][:, first : first + size].astype(F32)
 
 
-def place_quarters(spots, four, *cuts):
-    rows, columns = four[0][0].shape[0], four[0][2]
+def place_quarters(spots, pairs, *cuts):
+    rows, columns = pairs[0].shape[0], pairs[0].shape[1] // 2
     outs = [jax.ShapeDtypeStruct((rows, GROUP * size), F32) for _, size in cuts]
 
     def block(index):
@@ -510,13 +510,13 @@
         grid_spec=pltpu.PrefetchScalarGridSpec(
             num_scalar_prefetch=1,
             grid=(GROUP,),
-            in_specs=[block(index) for _, index, _ in four],
+            in_specs=[block(0), block(1), block(0), block(1)],
             out_specs=[pl.BlockSpec((rows, size), lambda q, s: (0, q)) for _, size in cuts],
         ),
         compiler_params=limit(40),
-        cost_estimate=estimate(0, *[x for x, _, _ in four], *outs),
+        cost_estimate=estimate(0, *pairs, *outs),
         name="place_quarters",
-    )(spots, *[x for x, _, _ in four])
+    )(spots, pairs[0], pairs[0], pairs[1], pairs[1])
 
 
 def tie(*values):
@@ -596,9 +596,9 @@
         ]
         return ordered(batch_of(place), *arrived, 0)
 
-    def bring_back(x):
+    def send_back(x):
         slots = natural(x).reshape(2, run, width)
-        arrived = [
+        return [
             lax.ppermute(
                 lax.dynamic_index_in_dim(slots, (batch_of(place) + p) % 2, 0, False),
                 AXES,
@@ -606,6 +606,8 @@
             )
             for p in range(2)
         ]
+
+    def as_batches(arrived):
         return ordered(place % 2, arrived[0][None], arrived[1][None], 0)
 
 
@@ -630,11 +632,19 @@
         sent = swap_b(columns(x, (1 - b) * own, own).astype(LOW))
         return columns(x, b * own, own) + sent.astype(F32)
 
+
+    pick = functools.partial(lax.dynamic_index_in_dim, keepdims=False)
+
+    def away_b(x):
+        cut = x.reshape(2, 2, -1, own)
+        return pick(cut, b, 0), swap_b(pick(cut, 1 - b, 0))
+
+    def away_c(mine, arrived):
+        both = ordered(b, mine, arrived, 2)
+        return pick(both, c, 0), swap_c(pick(both, 1 - c, 0))
+
     def to_runs(x):
-        cut = x.reshape(2, 2, -1, own)
-        pick = functools.partial(lax.dynamic_index_in_dim, keepdims=False)
-        both = ordered(b, pick(cut, b, 0), swap_b(pick(cut, 1 - b, 0)), 2)
-        return ordered(c, pick(both, c, 0), swap_c(pick(both, 1 - c, 0)), 1)
+        return ordered(c, *away_c(*away_b(x)), 1)
 
 
     def own_features(w):
@@ -707,11 +717,11 @@
         return jnp.concatenate([x, swap_b(x)], axis=1)
 
     def spread_c(pair):
-        other, size = swap_c(pair), pair.shape[1] // 2
-        return [(pair, 0, size), (pair, 1, size), (other, 0, size), (other, 1, size)]
-
-    def features_in_order(four, first, size):
-        cut = [x[:, index * full + first : index * full + first + size] for x, index, full in four]
+        return pair, swap_c(pair)
+
+    def features_in_order(pairs, first, size):
+        full = pairs[0].shape[1] // 2
+        cut = [x[:, i * full + first : i * full + first + size] for x in pairs for i in range(2)]
         pair = [ordered(b, cut[n], cut[n + 1], 1) for n in (0, 2)]
         return natural(ordered(c, pair[0], pair[1], 1)).astype(F32)
 
@@ -818,7 +828,7 @@
     arrived = swap_c(sent)
     r_result = swap_c(result)
     y_down = spread_a(f_down)
-    lean_o = total(lean_o)
+    lean_o = lean_o + swap_c(lean_o)
     p_out = cross_tokens(lifted, (o_scale * d_middle).astype(LOW)).astype(LOW)
     p_out = jnp.transpose(p_out.reshape(shards, spread, part, -1), (1, 0, 2, 3))
     p_out = p_out.reshape(spread, width // spread, -1)
@@ -829,9 +839,10 @@
     sent, mine, r_result, t_out, lean_o, y_down = tie(sent, mine, r_result, t_out, lean_o, y_down)
 
     crossed = swap_b(sent)
+    lean_b = swap_b(lean_o)
     r_out = sent_a(t_out[1:])
     result, result_mine = fold_half(spots, [product], [w_d], r_result)
-    crossed, result, r_out, lower = tie(crossed, result, r_out, lower)
+    crossed, result, r_out, lower, lean_b = tie(crossed, result, r_out, lower, lean_b)
 
     lower = sent_a(lower)
     result = swap_b(result)
@@ -839,7 +850,7 @@
     o_normed = attended * o_scale
     d_gated = mine + crossed.astype(F32)
     d_gate = (d_gated * o_normed).astype(LOW)
-    lean = lean_o[:, None] / width
+    lean = (lean_o + lean_b)[:, None] / width
     d_attended = (o_scale * (d_gated * gate - o_normed * lean)).astype(LOW)
     d_query, d_key, d_value = attend_back(rates, ends, z_qk, z_vg, d_attended)
     d_qk = joined(d_query, d_key)
@@ -859,53 +870,62 @@
 
     f_two = scattered(f_two)
     lower_qk = sent_a(lower_qk)
+    x_down = swap_b(y_down)
+    y_one = over_spread(f_one)
     arrived = swap_c(sent)
-    lean_x = total(
-        jnp.sum(z_qk * d_qk.astype(F32), axis=-1) + jnp.sum(z_vg * d_vg.astype(F32), axis=-1)
+    lean_x = jnp.sum(z_qk * d_qk.astype(F32), axis=-1) + jnp.sum(z_vg * d_vg.astype(F32), axis=-1)
+    sent, mine = fold_half(spots, [d_qk, d_vg], [w_qk, w_vg], arrived)
+    lean_x = lean_x + swap_c(lean_x)
+    sent, mine, lower_qk, t_vg, lean_x, x_down, y_one = tie(
+        sent, mine, lower_qk, t_vg, lean_x, x_down, y_one
     )
-    sent, mine = fold_half(spots, [d_qk, d_vg], [w_qk, w_vg], arrived)
-    sent, mine, lower_qk, t_vg, f_one, lean_x, y_down = tie(
-        sent, mine, lower_qk, t_vg, f_one, lean_x, y_down
-    )
 
     crossed = swap_b(sent)
+    lean_b = swap_b(lean_x)
     r_vg = sent_a(t_vg)
     f_qk = scattered(gradient_rows(spots, spread, 0, hidden_one, d_qk, stacked(upper_qk, lower_qk)))
-    output = bring_back(output)
-    x_one = spread_b(f_one)
-    crossed, d_vg, r_vg, x_one, output, y_down = tie(crossed, d_vg, r_vg, x_one, output, y_down)
+    four_down = spread_c(joined(y_down, x_down))
+    crossed, d_vg, r_vg, lean_b, four_down = tie(crossed, d_vg, r_vg, lean_b, four_down)
 
     f_vg = gradient_rows(spots, spread, 0, hidden_one, d_vg, r_vg)
-    f_vg, crossed, x_one, f_two, f_out, y_down = tie(f_vg, crossed, x_one, f_two, f_out, y_down)
+    f_vg, crossed, f_two, f_out = tie(f_vg, crossed, f_two, f_out)
 
     f_vg = scattered(f_vg)
     d_hidden = mine + crossed.astype(F32)
     x_normed = x_own.astype(F32) * x_scale
-    lean = lean_x[:, None] / width
+    lean = (lean_x + lean_b)[:, None] / width
     input_grad = to_runs((d_middle + x_scale * (d_hidden - x_normed * lean)).astype(LOW))
-    x_down = spread_b(y_down)
-    y_one = spread_a(x_one)
-    x_two = spread_b(f_two)
-    y_oqk = spread_a(joined(f_out, f_qk))
-    input_grad, x_down, y_one, x_two, y_oqk, f_vg = tie(input_grad, x_down, y_one, x_two, y_oqk, f_vg)
-
-    y_vg = spread_a(f_vg)
-    x_oqk = spread_b(y_oqk)
-    y_vg, x_oqk = tie(y_vg, x_oqk)
-
-    four_vg = spread_c(spread_b(y_vg))
-    input_grad = bring_back(input_grad)
-    four_two = spread_c(spread_a(x_two))
-    four_one = spread_c(y_one)
-    four_down = spread_c(x_down)
-    four_oqk = spread_c(x_oqk)
+    y_one = by_spread([f_one, *y_one])
+    x_one = swap_b(y_one)
+    f_oqk = joined(f_out, f_qk)
+    y_two = over_spread(f_two)
+    y_oqk = over_spread(f_oqk)
     units = f_one.shape[1]
+    [g_down] = place_quarters(spots, four_down, (0, units))
+    input_grad, x_one, y_two, y_oqk, f_vg, g_down = tie(input_grad, x_one, y_two, y_oqk, f_vg, g_down)
+
+    x_vg = swap_b(f_vg)
+    four_one = spread_c(joined(y_one, x_one))
+    x_vg, four_one = tie(x_vg, four_one)
+
+    f_vg = joined(f_vg, x_vg)
+    y_vg = over_spread(f_vg)
+    y_two = by_spread([f_two, *y_two])
+    x_two = swap_b(y_two)
+    y_oqk = by_spread([f_oqk, *y_oqk])
+    x_oqk = swap_b(y_oqk)
+    output, input_grad = send_back(output), send_back(input_grad)
+    [g_one] = place_quarters(spots, four_one, (0, units))
+    y_vg, x_two, x_oqk, g_one = tie(y_vg, x_two, x_oqk, g_one)
+
+    four_vg = spread_c(by_spread([f_vg, *y_vg]))
+    four_two = spread_c(joined(y_two, x_two))
+    four_oqk = spread_c(joined(y_oqk, x_oqk))
     g_query, g_key = place_quarters(spots, four_oqk, (own, own), (2 * own, own))
     g_value, g_gate = place_quarters(spots, four_vg, (0, own), (own, own))
-    [g_one] = place_quarters(spots, four_one, (0, units))
     [g_two] = place_quarters(spots, four_two, (0, units))
-    [g_down] = place_quarters(spots, four_down, (0, units))
     g_out = features_in_order(four_oqk, 0, own)
+    output, input_grad = as_batches(output), as_batches(input_grad)
     return output, input_grad, g_query, g_key, g_value, g_gate, g_out, g_one, g_two, g_down
 
 

time: 1210 us -> 1200 us (level)
  the two profiles are of different devices: /device:TPU:17 before, /device:TPU:0 now
where the time goes in v10:
time: 1200 us; the launch traced here: 1190 us
  waiting for transfers between devices  505 us (42%)
  Pallas kernels  345 us (29%)
  local copies, waits for them, and re-layouts  117 us (10%)
  other arithmetic  107 us (9%)
  starting transfers between devices  69.3 us (6%)
  matrix products  30.8 us (3%)
  between operations  17.1 us (1%)
    ppermute x56, waiting for transfers between devices, move(): return lax.ppermute(x, AXES, pairs)  358 us
    pallas_call x6, Pallas kernels, fold_half(): pl.pallas_call(functools.partial(fold_kernel, len(values), arrived is not...  98.8 us
    pallas_call x8, Pallas kernels, gradient_rows(): pl.pallas_call(gradient_kernel, out_shape=out, grid_spec=pltpu.PrefetchSc...  80.6 us
    unnamed x208, local copies, waits for them, and re-layouts  79.7 us
    ppermute x4, waiting for transfers between devices, bring(): lax.ppermute(lax.dynamic_index_in_dim(x, (place + p) % 2, 0, False), AXES...  65.6 us
    select_n x23, other arithmetic, ordered(): jnp.where(index == 0, jnp.concatenate([mine, other], axis), jnp.concatena...  51 us
    ppermute x56, starting transfers between devices, move(): return lax.ppermute(x, AXES, pairs)  43.4 us
    pallas_call x1, Pallas kernels, gated_unit(): pl.pallas_call(unit_kernel, out_shape=outs, grid_spec=pltpu.PrefetchScala...  38.5 us
  transfers between devices with their start and end apart: 76, of which 32 were waited for; matrix products, arithmetic and copies ran while one was open for 15% of the time, Pallas kernels for 28%

profile of v10, /device:TPU:0, one launch (start us, length us, event | category | flops | bytes accessed | tf_op | source)
XLA Modules:
  0.0 1192.2 jit_solution(6003029254272498809)
XLA Ops:
  21.6 43.2 %collective-permute-done.3 = bf16[256,2048]{1,0:T(8,128)(2,1)S(1)} collective-permute-done((bf16[256,2048]{1,0:T(8,128)(2,1)S(1)}, bf16[256,2048]{1,0:T(8,128)(2,1)S(1)}, u32[]{:S(2)}, u32[]{:S(2)}) %collective-permute-start.3) | collective-permute-done | bytes 1048608 | tf_op jit(solution)/shard_map/ppermute | solution.py:594
  67.1 31.3 %all-gather.7.cloned.1.call-done.refs_0_.refs_2_.refs_3_ = bf16[1024,1024]{1,0:T(8,128)(2,1)} async-done(((bf16[256,1024]{1,0:T(8,128)(2,1)}), bf16[1024,1024]{1,0:T(8,128)(2,1)}) %all-gather.7.cloned.1.call-update) | async-done | bytes 2097168 | tf_op jit(solution)/shard_map/all_gather | solution.py:664
  104.7 40.3 %collective-permute-done.4 = bf16[512,2048]{1,0:T(8,128)(2,1)} collective-permute-done((bf16[512,2048]{1,0:T(8,128)(2,1)}, bf16[512,2048]{1,0:T(8,128)(2,1)}, u32[]{:S(2)}, u32[]{:S(2)}) %collective-permute-start.4) | collective-permute-done | bytes 2097184 | tf_op jit(solution)/shard_map/ppermute | solution.py:543
  167.2 18.8 %enter.2 = (bf16[2048,2048]{1,0:T(8,128)(2,1)}, f32[2048,1024]{1,0:T(8,128)}, f32[2048,1]{1,0:T(8,128)S(1)}, bf16[2048,512]{1,0:T(8,128)(2,1)S(1)}) custom-call(s32[4]{0:T(128)S(1)} %pad_add_fusion.1.spots, bf16[1024,2048]{1,0:T(8,128)(2,1)S(1)} %copy-done.19, bf16[1024,2048]{1,0:T(8,128)(2,1)} %collective-permute-done.6.other_ref, ...), custom_call_target="tpu_custom_call" | custom-call | flops 8589934592 | bytes 31465472 | tf_op jit(solution)/shard_map/enter/pallas_call | solution.py:244
  186.0 15.3 %collective-permute-done.7.refs_1_.refs_5_.refs_6_ = bf16[1024,1024]{1,0:T(8,128)(2,1)} collective-permute-done((bf16[1024,1024]{1,0:T(8,128)(2,1)}, bf16[1024,1024]{1,0:T(8,128)(2,1)}, u32[]{:S(2)}, u32[]{:S(2)}) %collective-permute-start.7) | collective-permute-done | bytes 2097184 | tf_op jit(solution)/shard_map/ppermute | solution.py:543
  204.4 14.2 %project.1.zv_ref = f32[2048,1024]{1,0:T(8,128)S(1)} custom-call(s32[4]{0:T(128)S(1)} %pad_add_fusion.1.spots, bf16[2048,2048]{1,0:T(8,128)(2,1)} %get-tuple-element.147.h_ref.left_ref, bf16[1024,1024]{1,0:T(8,128)(2,1)S(1)} %copy-done.43, bf16[1024,1024]{1,0:T(8,128)(2,1)} %collective-permute-done.7.refs_1_.refs_5_.refs_6_), custom_call_target="tpu_custom_call" | custom-call | flops 8589934592 | bytes 20971520 | tf_op jit(solution)/shard_map/project/pallas_call | solution.py:275
  222.1 12.3 %attend.1 = f32[2048,512]{1,0:T(8,128)S(1)} custom-call(f32[4]{0:T(128)S(1)} %dynamic_slice.118.rates, s32[2,2]{1,0:T(2,128)S(1)} %pad_add_fusion.ends, f32[2048,1024]{1,0:T(8,128)S(1)} %copy-done, f32[2048,1024]{1,0:T(8,128)S(1)} %copy-done, f32[2048,1024]{1,0:T(8,128)} %copy-done.1), custom_call_target="tpu_custom_call" | custom-call | flops 4294967296 | bytes 16777216 | tf_op jit(solution)/shard_map/attend/pallas_call | solution.py:98
  244.2 43.4 %collective-permute-done.12 = f32[2048]{0:T(1024)S(1)} collective-permute-done((f32[2048]{0:T(1024)S(1)}, f32[2048]{0:T(1024)S(1)}, u32[]{:S(2)}, u32[]{:S(2)}) %collective-permute-start.12) | collective-permute-done | bytes 8224 | tf_op jit(solution)/shard_map/ppermute | solution.py:543
  294.6 9.5 collective-permute-done.10.refs_1_.refs_3_.refs_4_
  311.6 9.7 fusion.21
  329.0 22.4 %collective-permute-done.17 = bf16[256,2048]{1,0:T(8,128)(2,1)S(1)} collective-permute-done((bf16[256,2048]{1,0:T(8,128)(2,1)S(1)}, bf16[256,2048]{1,0:T(8,128)(2,1)S(1)}, u32[]{:S(2)}, u32[]{:S(2)}) %collective-permute-start.17) | collective-permute-done | bytes 1048608 | tf_op jit(solution)/shard_map/ppermute | solution.py:594
  353.7 15.5 %collective-permute-done.14 = bf16[2048,512]{1,0:T(8,128)(2,1)S(1)} collective-permute-done((bf16[2048,512]{1,0:T(8,128)(2,1)}, bf16[2048,512]{1,0:T(8,128)(2,1)S(1)}, u32[]{:S(2)}, u32[]{:S(2)}) %collective-permute-start.14) | collective-permute-done | bytes 2097184 | tf_op jit(solution)/shard_map/ppermute | solution.py:543
  388.4 38.5 %gated_unit.1 = (bf16[2048,2048]{1,0:T(8,128)(2,1)}, bf16[2048,1408]{1,0:T(8,128)(2,1)}, bf16[2048,1408]{1,0:T(8,128)(2,1)}, bf16[2048,1408]{1,0:T(8,128)(2,1)}, f32[2048,1]{1,0:T(8,128)S(1)}) custom-call(s32[4]{0:T(128)S(1)} %pad_add_fusion.1.spots, bf16[2048,1024]{1,0:T(8,128)(2,1)} %maximum_select_fusion.3.own_ref, ...), custom_call_target="tpu_custom_call" | custom-call | flops 23622320128 | bytes 45621248 | tf_op jit(solution)/shard_map/gated_unit/pallas_call | solution.py:337
  432.5 7.1 collective-permute-done.20.other_ref
  446.4 16.6 %gradient_rows.8 = bf16[2048,1408]{1,0:T(8,128)(2,1)S(1)} custom-call(s32[4]{0:T(128)S(1)} %pad_add_fusion.1.spots, bf16[2048,2048]{1,0:T(8,128)(2,1)} %get-tuple-element.169.left_ref.dy_ref, bf16[2048,1408]{1,0:T(8,128)(2,1)S(1)} %bitcast.63), custom_call_target="tpu_custom_call" | custom-call | flops 11811160064 | bytes 17301504 | tf_op jit(solution)/shard_map/gradient_rows/pallas_call | solution.py:470
  465.5 10.0 all-gather.17.cloned.1.call-done.refs_0_.refs_1_.refs_2_
  475.7 22.4 %gated_unit_back.1 = (bf16[2048,1408]{1,0:T(8,128)(2,1)S(1)}, bf16[2048,1408]{1,0:T(8,128)(2,1)S(1)}, f32[2048,1]{1,0:T(8,128)S(1)}) custom-call(s32[4]{0:T(128)S(1)} %pad_add_fusion.1.spots, bf16[2048,2048]{1,0:T(8,128)(2,1)} %get-tuple-element.169.left_ref.dy_ref, bf16[2048,1408]{1,0:T(8,128)(2,1)} %get-tuple-element.173.one_ref, ...), custom_call_target="tpu_custom_call" | custom-call | flops 11811160064 | bytes 37232640 | tf_op jit(solution)/shard_map/gated_unit_back/pallas_call | solution.py:374
  504.0 21.5 %fold_half.6 = bf16[2048,1024]{1,0:T(8,128)(2,1)} custom-call(s32[4]{0:T(128)S(1)} %pad_add_fusion.1.spots, bf16[2048,1408]{1,0:T(8,128)(2,1)} %copy-done.55, bf16[2048,1408]{1,0:T(8,128)(2,1)} %copy-done.52, bf16[1024,1408]{1,0:T(8,128)(2,1)S(1)} %copy-done.32, bf16[1024,1408]{1,0:T(8,128)(2,1)} %collective-permute-done.10.refs_1_.refs_3_.refs_4_, ...), custom_call_target="tpu_custom_call" | custom-call | flops 11811160064 | bytes 21495808 | tf_op jit(solution)/shard_map/fold_half/pallas_call | solution.py:435
  537.0 9.4 gradient_rows.9
  546.4 20.3 %fold_half.7 = (bf16[2048,512]{1,0:T(8,128)(2,1)}, f32[2048,512]{1,0:T(8,128)}) custom-call(s32[4]{0:T(128)S(1)} %pad_add_fusion.1.spots, bf16[2048,1408]{1,0:T(8,128)(2,1)} %copy-done.55, bf16[2048,1408]{1,0:T(8,128)(2,1)} %copy-done.52, bf16[2048,1024]{1,0:T(8,128)(2,1)} %collective-permute-done.21.refs_2_, bf16[1024,1408]{1,0:T(8,128)(2,1)S(1)} %copy-done.33, ...), custom_call_target="tpu_custom_call" | custom-call | flops 11811160064 | bytes 27787264 | tf_op jit(solution)/shard_map/fold_half/pallas_call | solution.py:435
  572.4 11.4 fold_half.8
  586.5 16.4 %gradient_rows.10 = bf16[2048,1408]{1,0:T(8,128)(2,1)S(1)} custom-call(s32[4]{0:T(128)S(1)} %pad_add_fusion.1.spots, bf16[2048,2048]{1,0:T(8,128)(2,1)} %get-tuple-element.183.left_ref, bf16[2048,1408]{1,0:T(8,128)(2,1)S(1)} %copy-done.56), custom_call_target="tpu_custom_call" | custom-call | flops 11811160064 | bytes 17301504 | tf_op jit(solution)/shard_map/gradient_rows/pallas_call | solution.py:470
  605.5 9.8 collective-permute-done.24
  615.6 6.4 multiply_reduce_fusion.2
  627.1 11.9 convolution_convert_fusion.1
  640.7 8.0 collective-permute-done.29
  661.3 15.1 %fold_half.9 = (bf16[2048,512]{1,0:T(8,128)(2,1)}, f32[2048,512]{1,0:T(8,128)S(1)}) custom-call(s32[4]{0:T(128)S(1)} %pad_add_fusion.1.spots, bf16[2048,1408]{1,0:T(8,128)(2,1)} %get-tuple-element.187.right_ref.refs_0_, bf16[2048,1024]{1,0:T(8,128)(2,1)} %collective-permute-done.27.refs_1_, ...), custom_call_target="tpu_custom_call" | custom-call | flops 5905580032 | bytes 16252928 | tf_op jit(solution)/shard_map/fold_half/pallas_call | solution.py:435
  676.4 28.7 %collective-permute-done.32 = f32[2048]{0:T(1024)S(1)} collective-permute-done((f32[2048]{0:T(1024)S(1)}, f32[2048]{0:T(1024)S(1)}, u32[]{:S(2)}, u32[]{:S(2)}) %collective-permute-start.32) | collective-permute-done | bytes 8224 | tf_op jit(solution)/shard_map/ppermute | solution.py:543
  712.9 21.3 %attend_back.1 = (bf16[2048,512]{1,0:T(8,128)(2,1)S(1)}, bf16[2048,512]{1,0:T(8,128)(2,1)S(1)}, bf16[2048,512]{1,0:T(8,128)(2,1)S(1)}) custom-call(f32[4]{0:T(128)S(1)} %dynamic_slice.118.rates, s32[2,2]{1,0:T(2,128)S(1)} %pad_add_fusion.ends, f32[2048,1024]{1,0:T(8,128)} %get-tuple-element.146.zq_ref.zk_ref, f32[2048,1024]{1,0:T(8,128)} %get-tuple-element.146.zq_ref.zk_ref, ...), custom_call_target="tpu_custom_call" | custom-call | flops 10737418240 | bytes 20971520 | tf_op jit(solution)/shard_map/attend_back/pallas_call | solution.py:119
  749.3 7.9 gradient_rows.11
  763.9 9.1 gradient_rows.13
  778.7 6.6 collective-permute-done.35
  789.8 7.2 gradient_rows.12
  797.1 15.3 %fold_half.10 = bf16[2048,1024]{1,0:T(8,128)(2,1)S(1)} custom-call(s32[4]{0:T(128)S(1)} %pad_add_fusion.1.spots, bf16[2048,1024]{1,0:T(8,128)(2,1)} %copy-done.6, bf16[2048,1024]{1,0:T(8,128)(2,1)} %pad_maximum_fusion.refs_1_.right_ref, bf16[1024,1024]{1,0:T(8,128)(2,1)S(1)} %copy-done.41, bf16[1024,1024]{1,0:T(8,128)(2,1)S(1)} %copy-done.48, ...), custom_call_target="tpu_custom_call" | custom-call | flops 8589934592 | bytes 16777216 | tf_op jit(solution)/shard_map/fold_half/pallas_call | solution.py:435
  835.4 15.2 %fold_half.11 = (bf16[2048,512]{1,0:T(8,128)(2,1)S(1)}, f32[2048,512]{1,0:T(8,128)}) custom-call(s32[4]{0:T(128)S(1)} %pad_add_fusion.1.spots, bf16[2048,1024]{1,0:T(8,128)(2,1)} %copy-done.6, bf16[2048,1024]{1,0:T(8,128)(2,1)} %pad_maximum_fusion.refs_1_.right_ref, bf16[2048,1024]{1,0:T(8,128)(2,1)} %collective-permute-done.40.refs_2_, ...), custom_call_target="tpu_custom_call" | custom-call | flops 8589934592 | bytes 23068672 | tf_op jit(solution)/shard_map/fold_half/pallas_call | solution.py:435
  860.7 6.9 gradient_rows.15
  876.5 46.0 %collective-permute-done.47 = f32[2048]{0:T(1024)S(1)} collective-permute-done((f32[2048]{0:T(1024)S(1)}, f32[2048]{0:T(1024)S(1)}, u32[]{:S(2)}, u32[]{:S(2)}) %collective-permute-start.47) | collective-permute-done | bytes 8224 | tf_op jit(solution)/shard_map/ppermute | solution.py:543
  925.4 6.9 gradient_rows.14
  943.4 21.7 %collective-permute-done.49 = bf16[2,512,512]{2,1,0:T(8,128)(2,1)S(1)} collective-permute-done((bf16[2,512,512]{2,1,0:T(8,128)(2,1)S(1)}, bf16[2,512,512]{2,1,0:T(8,128)(2,1)S(1)}, u32[]{:S(2)}, u32[]{:S(2)}) %collective-permute-start.49) | collective-permute-done | bytes 1048608 | tf_op jit(solution)/shard_map/ppermute | solution.py:543
  983.1 11.7 collective-permute-done.51
  994.8 10.9 collective-permute-done.52
  1023.3 7.5 collective-permute-done.56
  1035.9 7.1 place_quarters.6
  1043.0 52.0 %collective-permute-done.59 = bf16[512,1408]{1,0:T(8,128)(2,1)S(1)} collective-permute-done((bf16[512,1408]{1,0:T(8,128)(2,1)S(1)}, bf16[512,1408]{1,0:T(8,128)(2,1)S(1)}, u32[]{:S(2)}, u32[]{:S(2)}) %collective-permute-start.59) | collective-permute-done | bytes 1441824 | tf_op jit(solution)/shard_map/ppermute | solution.py:543
  1102.5 9.7 collective-permute-start.54
  1117.3 37.5 %collective-permute-done.55 = bf16[256,2048]{1,0:T(8,128)(2,1)} collective-permute-done((bf16[256,2048]{1,0:T(8,128)(2,1)}, bf16[256,2048]{1,0:T(8,128)(2,1)}, u32[]{:S(2)}, u32[]{:S(2)}) %collective-permute-start.55) | collective-permute-done | bytes 1048608 | tf_op jit(solution)/shard_map/ppermute | solution.py:602
  1159.2 6.3 place_quarters.8
  1165.6 7.8 place_quarters.9
  (450 shorter events, 330.5 us)
Async XLA Ops:
  8.0 90.4 %all-gather.7.cloned.1.call-start = ((), (), s32[]{:S(2)}) async-start(), calls=%async_computation.6 | async-start | bytes 2621440 | tf_op jit(solution)/shard_map/all_gather | solution.py:664
  10.3 140.9 %all-gather.9.cloned.1.call-start = ((), (), s32[]{:S(2)}) async-start(), calls=%async_computation.7 | async-start | bytes 2621440 | tf_op jit(solution)/shard_map/all_gather | solution.py:664
  12.5 173.6 %all-gather.11.cloned.1.call-start = ((), (), s32[]{:S(2)}) async-start(), calls=%async_computation.8 | async-start | bytes 1310720 | tf_op jit(solution)/shard_map/all_gather | solution.py:664
  15.6 49.2 %collective-permute-start.3 = (bf16[256,2048]{1,0:T(8,128)(2,1)S(1)}, bf16[256,2048]{1,0:T(8,128)(2,1)S(1)}, u32[]{:S(2)}, u32[]{:S(2)}) collective-permute-start(bf16[256,2048]{1,0:T(8,128)(2,1)S(1)} %get-tuple-element.299), channel_id=1, source_target_pairs={{1,0},{5,1},{0,2},{4,3},{3,4},{7,5},{2,6},{6,7},{9,8},{13,9},{8,10... | collective-permute-start | bytes 3145736 | tf_op jit(solution)/shard_map/ppermute | solution.py:594
  98.4 46.6 %collective-permute-start.4 = (bf16[512,2048]{1,0:T(8,128)(2,1)}, bf16[512,2048]{1,0:T(8,128)(2,1)}, u32[]{:S(2)}, u32[]{:S(2)}) collective-permute-start(bf16[512,2048]{1,0:T(8,128)(2,1)} %maximum_select_fusion.5), channel_id=1, source_target_pairs={{0,8},{1,9},{2,10},{3,11},{4,12},{5,13},{6,14},{7,15},{8,0},{9,1},... | collective-permute-start | bytes 6291464 | tf_op jit(solution)/shard_map/ppermute | solution.py:543
  100.7 139.8 %all-gather.13.cloned.1.call-start = ((), (), s32[]{:S(2)}) async-start(), calls=%async_computation.9 | async-start | bytes 3604480 | tf_op jit(solution)/shard_map/all_gather | solution.py:664
  100.7 50.4 %collective-permute-start.5 = (bf16[1024,1024]{1,0:T(8,128)(2,1)}, bf16[1024,1024]{1,0:T(8,128)(2,1)S(1)}, u32[]{:S(2)}, u32[]{:S(2)}) collective-permute-start(bf16[1024,1024]{1,0:T(8,128)(2,1)} %all-gather.7.cloned.1.call-done.refs_0_.refs_2_.refs_3_), channel_id=1, source_target_pairs={{0,16},{1,17},{2,18},{3,19},{4,20},{5,21},{6,22},{7,23},{8,24},{9,... | collective-permute-start | bytes 6291464 | tf_op jit(solution)/shard_map/ppermute | solution.py:543
  104.7 190.0 %all-gather.15.cloned.1.call-start = ((), (), s32[]{:S(2)}) async-start(), calls=%async_computation.10 | async-start | bytes 3604480 | tf_op jit(solution)/shard_map/all_gather | solution.py:664
  153.4 47.9 %collective-permute-start.7 = (bf16[1024,1024]{1,0:T(8,128)(2,1)}, bf16[1024,1024]{1,0:T(8,128)(2,1)}, u32[]{:S(2)}, u32[]{:S(2)}) collective-permute-start(bf16[1024,1024]{1,0:T(8,128)(2,1)} %all-gather.9.cloned.1.call-done.refs_0_.refs_4_.refs_5_), channel_id=1, source_target_pairs={{0,16},{1,17},{2,18},{3,19},{4,20},{5,21},{6,22},{7,23},{8,24},{9,... | collective-permute-start | bytes 6291464 | tf_op jit(solution)/shard_map/ppermute | solution.py:543
  159.9 315.7 %all-gather.17.cloned.1.call-start = ((), (), s32[]{:S(2)}) async-start(), calls=%async_computation.11 | async-start | bytes 6488064 | tf_op jit(solution)/shard_map/all_gather | solution.py:668
  201.3 39.1 %collective-permute-start.8 = (bf16[1024,512]{1,0:T(8,128)(2,1)}, bf16[1024,512]{1,0:T(8,128)(2,1)}, u32[]{:S(2)}, u32[]{:S(2)}) collective-permute-start(bf16[1024,512]{1,0:T(8,128)(2,1)} %all-gather.11.cloned.1.call-done), channel_id=1, source_target_pairs={{0,16},{1,17},{2,18},{3,19},{4,20},{5,21},{6,22},{7,23},{8,24},{9,... | collective-permute-start | bytes 3145736 | tf_op jit(solution)/shard_map/ppermute | solution.py:543
  240.4 63.7 %collective-permute-start.10 = (bf16[1024,1408]{1,0:T(8,128)(2,1)}, bf16[1024,1408]{1,0:T(8,128)(2,1)}, u32[]{:S(2)}, u32[]{:S(2)}) collective-permute-start(bf16[1024,1408]{1,0:T(8,128)(2,1)} %all-gather.13.cloned.1.call-done.refs_0_.refs_2_.refs_3_), channel_id=1, source_target_pairs={{0,16},{1,17},{2,18},{3,19},{4,20},{5,21},{6,22},{7,23},{8,24},{9,... | collective-permute-start | bytes 8650760 | tf_op jit(solution)/shard_map/ppermute | solution.py:543
  241.0 46.6 %collective-permute-start.9 = (bf16[2048,512]{1,0:T(8,128)(2,1)}, bf16[2048,512]{1,0:T(8,128)(2,1)S(1)}, u32[]{:S(2)}, u32[]{:S(2)}) collective-permute-start(bf16[2048,512]{1,0:T(8,128)(2,1)} %get-tuple-element.150), channel_id=1, source_target_pairs={{0,8},{1,9},{2,10},{3,11},{4,12},{5,13},{6,14},{7,15},{8,0},{9,1},... | collective-permute-start | bytes 6291464 | tf_op jit(solution)/shard_map/ppermute | solution.py:543
  243.4 44.1 %collective-permute-start.12 = (f32[2048]{0:T(1024)S(1)}, f32[2048]{0:T(1024)S(1)}, u32[]{:S(2)}, u32[]{:S(2)}) collective-permute-start(f32[2048]{0:T(1024)S(1)} %add.256), channel_id=1, source_target_pairs={{0,8},{1,9},{2,10},{3,11},{4,12},{5,13},{6,14},{7,15},{8,0},{9,1},... | collective-permute-start | bytes 24584 | tf_op jit(solution)/shard_map/ppermute | solution.py:543
  308.9 64.9 %collective-permute-start.15 = (bf16[1024,1408]{1,0:T(8,128)(2,1)S(1)}, bf16[1024,1408]{1,0:T(8,128)(2,1)S(1)}, u32[]{:S(2)}, u32[]{:S(2)}) collective-permute-start(bf16[1024,1408]{1,0:T(8,128)(2,1)S(1)} %copy-done.34), channel_id=1, source_target_pairs={{0,16},{1,17},{2,18},{3,19},{4,20},{5,21},{6,22},{7,23},{8,24},{9,... | collective-permute-start | bytes 8650760 | tf_op jit(solution)/shard_map/ppermute | solution.py:543
  321.3 47.9 %collective-permute-start.14 = (bf16[2048,512]{1,0:T(8,128)(2,1)}, bf16[2048,512]{1,0:T(8,128)(2,1)S(1)}, u32[]{:S(2)}, u32[]{:S(2)}) collective-permute-start(bf16[2048,512]{1,0:T(8,128)(2,1)} %get-tuple-element.302), channel_id=1, source_target_pairs={{0,8},{1,9},{2,10},{3,11},{4,12},{5,13},{6,14},{7,15},{8,0},{9,1},... | collective-permute-start | bytes 6291464 | tf_op jit(solution)/shard_map/ppermute | solution.py:543
  381.9 233.4 %reduce-scatter.7.cloned.1.call-start = ((), (), s32[]{:S(2)}) async-start(), calls=%async_computation.12 | async-start | bytes 6488064 | tf_op jit(solution)/shard_map/reduce_scatter | solution.py:708
  382.4 47.8 %collective-permute-start.19 = (bf16[512,2048]{1,0:T(8,128)(2,1)}, bf16[512,2048]{1,0:T(8,128)(2,1)S(1)}, u32[]{:S(2)}, u32[]{:S(2)}) collective-permute-start(bf16[512,2048]{1,0:T(8,128)(2,1)} %maximum_select_fusion.7), channel_id=1, source_target_pairs={{0,8},{1,9},{2,10},{3,11},{4,12},{5,13},{6,14},{7,15},{8,0},{9,1},... | collective-permute-start | bytes 6291464 | tf_op jit(solution)/shard_map/ppermute | solution.py:543
  475.6 353.1 %reduce-scatter.9.cloned.1.call-start = ((), (), s32[]{:S(2)}) async-start(), calls=%async_computation.13 | async-start | bytes 6488064 | tf_op jit(solution)/shard_map/reduce_scatter | solution.py:708
  566.7 48.6 %collective-permute-start.24 = (bf16[2048,512]{1,0:T(8,128)(2,1)}, bf16[2048,512]{1,0:T(8,128)(2,1)}, u32[]{:S(2)}, u32[]{:S(2)}) collective-permute-start(bf16[2048,512]{1,0:T(8,128)(2,1)} %get-tuple-element.186), channel_id=1, source_target_pairs={{0,8},{1,9},{2,10},{3,11},{4,12},{5,13},{6,14},{7,15},{8,0},{9,1},... | collective-permute-start | bytes 6291464 | tf_op jit(solution)/shard_map/ppermute | solution.py:543
  569.1 36.3 %collective-permute-start.25 = (bf16[512,1408]{1,0:T(8,128)(2,1)}, bf16[512,1408]{1,0:T(8,128)(2,1)}, u32[]{:S(2)}, u32[]{:S(2)}) collective-permute-start(bf16[512,1408]{1,0:T(8,128)(2,1)} %get-tuple-element.277), channel_id=1, source_target_pairs={{0,16},{1,17},{2,18},{3,19},{4,20},{5,21},{6,22},{7,23},{8,24},{9,... | collective-permute-start | bytes 4325384 | tf_op jit(solution)/shard_map/ppermute | solution.py:543
  615.3 318.4 %reduce-scatter.13.cloned.1.call-start = ((), (), s32[]{:S(2)}) async-start(), calls=%async_computation.15 | async-start | bytes 1310720 | tf_op jit(solution)/shard_map/reduce_scatter | solution.py:702
  659.3 45.8 %collective-permute-start.30 = (bf16[2048,512]{1,0:T(8,128)(2,1)}, bf16[2048,512]{1,0:T(8,128)(2,1)}, u32[]{:S(2)}, u32[]{:S(2)}) collective-permute-start(bf16[2048,512]{1,0:T(8,128)(2,1)} %dynamic-slice_convert_fusion), channel_id=1, source_target_pairs={{0,8},{1,9},{2,10},{3,11},{4,12},{5,13},{6,14},{7,15},{8,0},{9,1},... | collective-permute-start | bytes 6291464 | tf_op jit(solution)/shard_map/ppermute | solution.py:543
  659.4 45.7 %collective-permute-start.31 = (bf16[1024,512]{1,0:T(8,128)(2,1)}, bf16[1024,512]{1,0:T(8,128)(2,1)}, u32[]{:S(2)}, u32[]{:S(2)}) collective-permute-start(bf16[1024,512]{1,0:T(8,128)(2,1)} %get-tuple-element.203), channel_id=1, source_target_pairs={{0,16},{1,17},{2,18},{3,19},{4,20},{5,21},{6,22},{7,23},{8,24},{9,... | collective-permute-start | bytes 3145736 | tf_op jit(solution)/shard_map/ppermute | solution.py:543
  659.8 45.3 %collective-permute-start.32 = (f32[2048]{0:T(1024)S(1)}, f32[2048]{0:T(1024)S(1)}, u32[]{:S(2)}, u32[]{:S(2)}) collective-permute-start(f32[2048]{0:T(1024)S(1)} %add.275), channel_id=1, source_target_pairs={{0,8},{1,9},{2,10},{3,11},{4,12},{5,13},{6,14},{7,15},{8,0},{9,1},... | collective-permute-start | bytes 24584 | tf_op jit(solution)/shard_map/ppermute | solution.py:543
  705.1 52.1 %collective-permute-start.33 = (bf16[512,1408]{1,0:T(8,128)(2,1)}, bf16[512,1408]{1,0:T(8,128)(2,1)}, u32[]{:S(2)}, u32[]{:S(2)}) collective-permute-start(bf16[512,1408]{1,0:T(8,128)(2,1)} %get-tuple-element.210), channel_id=1, source_target_pairs={{0,16},{1,17},{2,18},{3,19},{4,20},{5,21},{6,22},{7,23},{8,24},{9,... | collective-permute-start | bytes 4325384 | tf_op jit(solution)/shard_map/ppermute | solution.py:543
  705.7 51.5 %collective-permute-start.34 = (bf16[2048,512]{1,0:T(8,128)(2,1)}, bf16[2048,512]{1,0:T(8,128)(2,1)}, u32[]{:S(2)}, u32[]{:S(2)}) collective-permute-start(bf16[2048,512]{1,0:T(8,128)(2,1)} %get-tuple-element.211), channel_id=1, source_target_pairs={{0,8},{1,9},{2,10},{3,11},{4,12},{5,13},{6,14},{7,15},{8,0},{9,1},... | collective-permute-start | bytes 6291464 | tf_op jit(solution)/shard_map/ppermute | solution.py:543
  740.7 193.0 %reduce-scatter.11.cloned.1.call-start = ((), (), s32[]{:S(2)}) async-start(), calls=%async_computation.14 | async-start | bytes 3604480 | tf_op jit(solution)/shard_map/reduce_scatter | solution.py:702
  777.4 39.1 %collective-permute-start.37 = (bf16[512,1024]{1,0:T(8,128)(2,1)S(1)}, bf16[512,1024]{1,0:T(8,128)(2,1)}, u32[]{:S(2)}, u32[]{:S(2)}) collective-permute-start(bf16[512,1024]{1,0:T(8,128)(2,1)S(1)} %get-tuple-element.287), channel_id=1, source_target_pairs={{0,16},{1,17},{2,18},{3,19},{4,20},{5,21},{6,22},{7,23},{8,24},{9,... | collective-permute-start | bytes 3145736 | tf_op jit(solution)/shard_map/ppermute | solution.py:543
  816.6 151.4 %reduce-scatter.15.cloned.1.call-start = ((), (), s32[]{:S(2)}) async-start(), calls=%async_computation.16 | async-start | bytes 2621440 | tf_op jit(solution)/shard_map/reduce_scatter | solution.py:702
  816.7 35.2 %collective-permute-start.43 = (bf16[512,1408]{1,0:T(8,128)(2,1)}, bf16[512,1408]{1,0:T(8,128)(2,1)}, u32[]{:S(2)}, u32[]{:S(2)}) collective-permute-start(bf16[512,1408]{1,0:T(8,128)(2,1)} %maximum_select_fusion.17), channel_id=1, source_target_pairs={{0,8},{1,9},{2,10},{3,11},{4,12},{5,13},{6,14},{7,15},{8,0},{9,1},... | collective-permute-start | bytes 4325384 | tf_op jit(solution)/shard_map/ppermute | solution.py:543
  869.0 136.7 %reduce-scatter.17.cloned.1.call-start = ((), (), s32[]{:S(2)}) async-start(), calls=%async_computation.17 | async-start | bytes 2621440 | tf_op jit(solution)/shard_map/reduce_scatter | solution.py:702
  872.5 51.3 %collective-permute-start.48 = (bf16[512,2816]{1,0:T(8,128)(2,1)S(1)}, bf16[512,2816]{1,0:T(8,128)(2,1)S(1)}, u32[]{:S(2)}, u32[]{:S(2)}) collective-permute-start(bf16[512,2816]{1,0:T(8,128)(2,1)S(1)} %constant_dynamic-update-slice_fusion.2.refs_0_.refs_1_), channel_id=1, source_target_pairs={{0,4},{1,5},{2,6},{3,7},{4,0},{5,1},{6,2},{7,3},{8,12},{9,13},{10,... | collective-permute-start | bytes 8650760 | tf_op jit(solution)/shard_map/ppermute | solution.py:543
  874.1 48.4 %collective-permute-start.45 = (bf16[2048,512]{1,0:T(8,128)(2,1)}, bf16[2048,512]{1,0:T(8,128)(2,1)S(1)}, u32[]{:S(2)}, u32[]{:S(2)}) collective-permute-start(bf16[2048,512]{1,0:T(8,128)(2,1)} %copy-done.51), channel_id=1, source_target_pairs={{0,8},{1,9},{2,10},{3,11},{4,12},{5,13},{6,14},{7,15},{8,0},{9,1},... | collective-permute-start | bytes 6291464 | tf_op jit(solution)/shard_map/ppermute | solution.py:543
  875.8 48.0 %collective-permute-start.46 = (bf16[1024,1024]{1,0:T(8,128)(2,1)}, bf16[1024,1024]{1,0:T(8,128)(2,1)S(1)}, u32[]{:S(2)}, u32[]{:S(2)}) collective-permute-start(bf16[1024,1024]{1,0:T(8,128)(2,1)} %copy-done.50), channel_id=1, source_target_pairs={{0,16},{1,17},{2,18},{3,19},{4,20},{5,21},{6,22},{7,23},{8,24},{9,... | collective-permute-start | bytes 6291464 | tf_op jit(solution)/shard_map/ppermute | solution.py:543
  876.1 46.4 %collective-permute-start.47 = (f32[2048]{0:T(1024)S(1)}, f32[2048]{0:T(1024)S(1)}, u32[]{:S(2)}, u32[]{:S(2)}) collective-permute-start(f32[2048]{0:T(1024)S(1)} %add.290), channel_id=1, source_target_pairs={{0,8},{1,9},{2,10},{3,11},{4,12},{5,13},{6,14},{7,15},{8,0},{9,1},... | collective-permute-start | bytes 24584 | tf_op jit(solution)/shard_map/ppermute | solution.py:543
  942.3 52.5 %collective-permute-start.51 = (bf16[512,1408]{1,0:T(8,128)(2,1)}, bf16[512,1408]{1,0:T(8,128)(2,1)}, u32[]{:S(2)}, u32[]{:S(2)}) collective-permute-start(bf16[512,1408]{1,0:T(8,128)(2,1)} %maximum_select_fusion.18), channel_id=1, source_target_pairs={{0,8},{1,9},{2,10},{3,11},{4,12},{5,13},{6,14},{7,15},{8,0},{9,1},... | collective-permute-start | bytes 4325384 | tf_op jit(solution)/shard_map/ppermute | solution.py:543
  970.0 35.7 %collective-permute-start.53 = (bf16[256,1536]{1,0:T(8,128)(2,1)}, bf16[256,1536]{1,0:T(8,128)(2,1)}, u32[]{:S(2)}, u32[]{:S(2)}) collective-permute-start(bf16[256,1536]{1,0:T(8,128)(2,1)} %constant_dynamic-update-slice_fusion.4), channel_id=1, source_target_pairs={{0,16},{1,17},{2,18},{3,19},{4,20},{5,21},{6,22},{7,23},{8,24},{9,... | collective-permute-start | bytes 2359304 | tf_op jit(solution)/shard_map/ppermute | solution.py:543
  970.3 35.4 %collective-permute-start.52 = (bf16[256,1408]{1,0:T(8,128)(2,1)}, bf16[256,1408]{1,0:T(8,128)(2,1)}, u32[]{:S(2)}, u32[]{:S(2)}) collective-permute-start(bf16[256,1408]{1,0:T(8,128)(2,1)} %reduce-scatter.11.cloned.1.call-done), channel_id=1, source_target_pairs={{0,16},{1,17},{2,18},{3,19},{4,20},{5,21},{6,22},{7,23},{8,24},{9,... | collective-permute-start | bytes 2162696 | tf_op jit(solution)/shard_map/ppermute | solution.py:543
  1019.4 75.6 %collective-permute-start.60 = (bf16[512,1536]{1,0:T(8,128)(2,1)S(1)}, bf16[512,1536]{1,0:T(8,128)(2,1)S(1)}, u32[]{:S(2)}, u32[]{:S(2)}) collective-permute-start(bf16[512,1536]{1,0:T(8,128)(2,1)S(1)} %maximum_select_fusion.16), channel_id=1, source_target_pairs={{0,8},{1,9},{2,10},{3,11},{4,12},{5,13},{6,14},{7,15},{8,0},{9,1},... | collective-permute-start | bytes 4718600 | tf_op jit(solution)/shard_map/ppermute | solution.py:543
  1021.6 73.4 %collective-permute-start.59 = (bf16[512,1408]{1,0:T(8,128)(2,1)S(1)}, bf16[512,1408]{1,0:T(8,128)(2,1)S(1)}, u32[]{:S(2)}, u32[]{:S(2)}) collective-permute-start(bf16[512,1408]{1,0:T(8,128)(2,1)S(1)} %maximum_select_fusion.19), channel_id=1, source_target_pairs={{0,8},{1,9},{2,10},{3,11},{4,12},{5,13},{6,14},{7,15},{8,0},{9,1},... | collective-permute-start | bytes 4325384 | tf_op jit(solution)/shard_map/ppermute | solution.py:543
  1030.9 64.1 %collective-permute-start.58 = (bf16[256,2048]{1,0:T(8,128)(2,1)S(1)}, bf16[256,2048]{1,0:T(8,128)(2,1)S(1)}, u32[]{:S(2)}, u32[]{:S(2)}) collective-permute-start(bf16[256,2048]{1,0:T(8,128)(2,1)S(1)} %constant_dynamic-update-slice_fusion.6), channel_id=1, source_target_pairs={{0,16},{1,17},{2,18},{3,19},{4,20},{5,21},{6,22},{7,23},{8,24},{9,... | collective-permute-start | bytes 3145736 | tf_op jit(solution)/shard_map/ppermute | solution.py:543
  1031.6 70.9 %collective-permute-start.38 = (bf16[256,2048]{1,0:T(8,128)(2,1)S(1)}, bf16[256,2048]{1,0:T(8,128)(2,1)}, u32[]{:S(2)}, u32[]{:S(2)}) collective-permute-start(bf16[256,2048]{1,0:T(8,128)(2,1)S(1)} %get-tuple-element.284), channel_id=1, source_target_pairs={{0,0},{1,4},{2,1},{3,5},{4,2},{5,6},{6,3},{7,7},{8,8},{9,12},{10,9... | collective-permute-start | bytes 3145736 | tf_op jit(solution)/shard_map/ppermute | solution.py:602
  1033.2 79.0 %collective-permute-start.39 = (bf16[256,2048]{1,0:T(8,128)(2,1)S(1)}, bf16[256,2048]{1,0:T(8,128)(2,1)}, u32[]{:S(2)}, u32[]{:S(2)}) collective-permute-start(bf16[256,2048]{1,0:T(8,128)(2,1)S(1)} %get-tuple-element.285), channel_id=1, source_target_pairs={{0,1},{1,5},{2,0},{3,4},{4,3},{5,7},{6,2},{7,6},{8,9},{9,13},{10,8... | collective-permute-start | bytes 3145736 | tf_op jit(solution)/shard_map/ppermute | solution.py:602
  1096.1 77.2 %collective-permute-start.61 = (bf16[512,3072]{1,0:T(8,128)(2,1)S(1)}, bf16[512,3072]{1,0:T(8,128)(2,1)}, u32[]{:S(2)}, u32[]{:S(2)}) collective-permute-start(bf16[512,3072]{1,0:T(8,128)(2,1)S(1)} %pad_maximum_fusion.1.refs_0_.refs_1_), channel_id=1, source_target_pairs={{0,4},{1,5},{2,6},{3,7},{4,0},{5,1},{6,2},{7,3},{8,12},{9,13},{10,... | collective-permute-start | bytes 9437192 | tf_op jit(solution)/shard_map/ppermute | solution.py:543
  1097.9 67.7 %collective-permute-start.63 = (bf16[512,2816]{1,0:T(8,128)(2,1)}, bf16[512,2816]{1,0:T(8,128)(2,1)}, u32[]{:S(2)}, u32[]{:S(2)}) collective-permute-start(bf16[512,2816]{1,0:T(8,128)(2,1)} %pad_maximum_fusion.4.refs_0_.refs_1_), channel_id=1, source_target_pairs={{0,4},{1,5},{2,6},{3,7},{4,0},{5,1},{6,2},{7,3},{8,12},{9,13},{10,... | collective-permute-start | bytes 8650760 | tf_op jit(solution)/shard_map/ppermute | solution.py:543
  1100.8 58.4 %collective-permute-start.62 = (bf16[512,2048]{1,0:T(8,128)(2,1)}, bf16[512,2048]{1,0:T(8,128)(2,1)}, u32[]{:S(2)}, u32[]{:S(2)}) collective-permute-start(bf16[512,2048]{1,0:T(8,128)(2,1)} %maximum_select_fusion.14.refs_0_.refs_1_), channel_id=1, source_target_pairs={{0,4},{1,5},{2,6},{3,7},{4,0},{5,1},{6,2},{7,3},{8,12},{9,13},{10,... | collective-permute-start | bytes 6291464 | tf_op jit(solution)/shard_map/ppermute | solution.py:543
  1112.2 42.7 %collective-permute-start.55 = (bf16[256,2048]{1,0:T(8,128)(2,1)}, bf16[256,2048]{1,0:T(8,128)(2,1)}, u32[]{:S(2)}, u32[]{:S(2)}) collective-permute-start(bf16[256,2048]{1,0:T(8,128)(2,1)} %get-tuple-element.279), channel_id=1, source_target_pairs={{0,1},{1,5},{2,0},{3,4},{4,3},{5,7},{6,2},{7,6},{8,9},{9,13},{10,8... | collective-permute-start | bytes 3145736 | tf_op jit(solution)/shard_map/ppermute | solution.py:602
  (120 other events, 1466.0 us)
Sparse Core Ops, SparseCore 0:
  11.0 87.3 all-gather.6
  100.6 44.6 all-gather.8
  147.4 26.6 all-gather.10
  176.0 58.6 all-gather.12
  236.8 57.8 all-gather.14
Sparse Core Ops, SparseCore 1:
  382.0 93.6 all-gather.16
  479.1 108.3 reduce-scatter.6
  615.4 126.4 reduce-scatter.8
  744.2 25.7 reduce-scatter.12
  816.7 56.5 reduce-scatter.10
  876.2 43.2 reduce-scatter.14
  933.8 44.9 reduce-scatter.16

commit v11 on v10

--- a/solution.py
+++ b/solution.py
@@ -804,21 +804,24 @@
 
     arrived = swap_c(sent)
     t_two = away(hidden_two, d_two)
-    lean_m = total(lean_m[:, 0])
+    lean_m = lean_m[:, 0]
+    lean_c = swap_c(lean_m)
     sent, mine = fold_half(spots, [d_one, d_two], [w_1, w_2], arrived)
-    sent, d_one, t_two, product, lean_m = tie(sent, d_one, t_two, product, lean_m)
+    sent, d_one, t_two, product, lean_c = tie(sent, d_one, t_two, product, lean_c)
 
     crossed = swap_b(sent)
+    lean_m = lean_m + lean_c
+    lean_b = swap_b(lean_m)
     upper, lower = in_two(t_two)
     upper = sent_a(upper)
     f_one = whole_rows(hidden_two, d_one)
     result = fold_half(spots, [product], [w_d])
-    crossed, result, f_one, upper, f_down = tie(crossed, result, f_one, upper, f_down)
+    crossed, result, f_one, upper, f_down, lean_b = tie(crossed, result, f_one, upper, f_down, lean_b)
 
     f_one = scattered_all(f_one)
     d_hidden = mine + crossed.astype(F32)
     m_normed = middle * m_scale
-    lean = lean_m[:, None] * (2.0 / width)
+    lean = (lean_m + lean_b)[:, None] * (2.0 / width)
     d_middle = dy_own.astype(F32) + m_scale * (d_hidden - m_normed * lean)
     d_branch = d_middle.astype(LOW)
     lean_o = jnp.sum(d_middle * branch, axis=-1)
@@ -895,14 +898,17 @@
     x_normed = x_own.astype(F32) * x_scale
     lean = (lean_x + lean_b)[:, None] / width
     input_grad = to_runs((d_middle + x_scale * (d_hidden - x_normed * lean)).astype(LOW))
+    output = send_back(output)
     y_one = by_spread([f_one, *y_one])
     x_one = swap_b(y_one)
     f_oqk = joined(f_out, f_qk)
+    x_oqk = swap_b(f_oqk)
     y_two = over_spread(f_two)
-    y_oqk = over_spread(f_oqk)
     units = f_one.shape[1]
     [g_down] = place_quarters(spots, four_down, (0, units))
-    input_grad, x_one, y_two, y_oqk, f_vg, g_down = tie(input_grad, x_one, y_two, y_oqk, f_vg, g_down)
+    input_grad, output, x_one, y_two, x_oqk, f_vg, g_down = tie(
+        input_grad, output, x_one, y_two, x_oqk, f_vg, g_down
+    )
 
     x_vg = swap_b(f_vg)
     four_one = spread_c(joined(y_one, x_one))
@@ -912,15 +918,15 @@
     y_vg = over_spread(f_vg)
     y_two = by_spread([f_two, *y_two])
     x_two = swap_b(y_two)
-    y_oqk = by_spread([f_oqk, *y_oqk])
-    x_oqk = swap_b(y_oqk)
-    output, input_grad = send_back(output), send_back(input_grad)
+    f_oqk = joined(f_oqk, x_oqk)
+    y_oqk = over_spread(f_oqk)
+    input_grad = send_back(input_grad)
     [g_one] = place_quarters(spots, four_one, (0, units))
-    y_vg, x_two, x_oqk, g_one = tie(y_vg, x_two, x_oqk, g_one)
+    y_vg, x_two, y_oqk, input_grad, g_one = tie(y_vg, x_two, y_oqk, input_grad, g_one)
 
     four_vg = spread_c(by_spread([f_vg, *y_vg]))
     four_two = spread_c(joined(y_two, x_two))
-    four_oqk = spread_c(joined(y_oqk, x_oqk))
+    four_oqk = spread_c(by_spread([f_oqk, *y_oqk]))
     g_query, g_key = place_quarters(spots, four_oqk, (own, own), (2 * own, own))
     g_value, g_gate = place_quarters(spots, four_vg, (0, own), (own, own))
     [g_two] = place_quarters(spots, four_two, (0, units))

time: 1200 us -> 1140 us (0.950)
  the two profiles are of different devices: /device:TPU:0 before, /device:TPU:17 now
where the time goes in v11:
time: 1140 us; the launch traced here: 1130 us
  waiting for transfers between devices  450 us (39%)
  Pallas kernels  347 us (30%)
  local copies, waits for them, and re-layouts  108 us (9%)
  other arithmetic  103 us (9%)
  starting transfers between devices  75.4 us (7%)
  matrix products  30.8 us (3%)
  between operations  17 us (1%)
    ppermute x56, waiting for transfers between devices, move(): return lax.ppermute(x, AXES, pairs)  258 us
    ppermute x4, waiting for transfers between devices, bring(): lax.ppermute(lax.dynamic_index_in_dim(x, (place + p) % 2, 0, False), AXES...  119 us
    pallas_call x6, Pallas kernels, fold_half(): pl.pallas_call(functools.partial(fold_kernel, len(values), arrived is not...  99.1 us
    pallas_call x8, Pallas kernels, gradient_rows(): pl.pallas_call(gradient_kernel, out_shape=out, grid_spec=pltpu.PrefetchSc...  81.7 us
    unnamed x201, local copies, waits for them, and re-layouts  73.3 us
    ppermute x4, waiting for transfers between devices, send_back(): lax.ppermute(lax.dynamic_index_in_dim(slots, (batch_of(place) + p) % 2, 0...  65.2 us
    ppermute x56, starting transfers between devices, move(): return lax.ppermute(x, AXES, pairs)  55.2 us
    select_n x23, other arithmetic, ordered(): jnp.where(index == 0, jnp.concatenate([mine, other], axis), jnp.concatena...  47 us
  transfers between devices with their start and end apart: 76, of which 30 were waited for; matrix products, arithmetic and copies ran while one was open for 15% of the time, Pallas kernels for 30%

profile of v11, /device:TPU:17, one launch (start us, length us, event | category | flops | bytes accessed | tf_op | source)
XLA Modules:
  0.0 1130.5 jit_solution(8810865165534488823)
XLA Ops:
  18.7 75.9 %collective-permute-done = bf16[256,2048]{1,0:T(8,128)(2,1)S(1)} collective-permute-done((bf16[256,2048]{1,0:T(8,128)(2,1)}, bf16[256,2048]{1,0:T(8,128)(2,1)S(1)}, u32[]{:S(2)}, u32[]{:S(2)}) %collective-permute-start) | collective-permute-done | bytes 1048608 | tf_op jit(solution)/shard_map/ppermute | solution.py:594
  102.8 37.9 %collective-permute-done.2 = bf16[512,2048]{1,0:T(8,128)(2,1)} collective-permute-done((bf16[512,2048]{1,0:T(8,128)(2,1)}, bf16[512,2048]{1,0:T(8,128)(2,1)}, u32[]{:S(2)}, u32[]{:S(2)}) %collective-permute-start.2) | collective-permute-done | bytes 2097184 | tf_op jit(solution)/shard_map/ppermute | solution.py:543
  140.6 6.0 maximum_select_fusion.1.own_ref
  165.2 18.8 %enter.2 = (bf16[2048,2048]{1,0:T(8,128)(2,1)}, f32[2048,1024]{1,0:T(8,128)}, f32[2048,1]{1,0:T(8,128)S(1)}, bf16[2048,512]{1,0:T(8,128)(2,1)S(1)}) custom-call(s32[4]{0:T(128)S(1)} %pad_add_fusion.1.spots, bf16[1024,2048]{1,0:T(8,128)(2,1)S(1)} %copy-done.15, bf16[1024,2048]{1,0:T(8,128)(2,1)} %collective-permute-done.4.other_ref, ...), custom_call_target="tpu_custom_call" | custom-call | flops 8589934592 | bytes 31465472 | tf_op jit(solution)/shard_map/enter/pallas_call | solution.py:244
  184.1 14.9 %collective-permute-done.7.refs_1_.refs_5_.refs_6_ = bf16[1024,1024]{1,0:T(8,128)(2,1)} collective-permute-done((bf16[1024,1024]{1,0:T(8,128)(2,1)}, bf16[1024,1024]{1,0:T(8,128)(2,1)}, u32[]{:S(2)}, u32[]{:S(2)}) %collective-permute-start.7) | collective-permute-done | bytes 2097184 | tf_op jit(solution)/shard_map/ppermute | solution.py:543
  201.8 14.2 %project.1.zv_ref = f32[2048,1024]{1,0:T(8,128)S(1)} custom-call(s32[4]{0:T(128)S(1)} %pad_add_fusion.1.spots, bf16[2048,2048]{1,0:T(8,128)(2,1)} %get-tuple-element.153.h_ref.left_ref, bf16[1024,1024]{1,0:T(8,128)(2,1)S(1)} %copy-done.39, bf16[1024,1024]{1,0:T(8,128)(2,1)} %collective-permute-done.7.refs_1_.refs_5_.refs_6_), custom_call_target="tpu_custom_call" | custom-call | flops 8589934592 | bytes 20971520 | tf_op jit(solution)/shard_map/project/pallas_call | solution.py:275
  219.4 12.3 %attend.1 = f32[2048,512]{1,0:T(8,128)S(1)} custom-call(f32[4]{0:T(128)S(1)} %dynamic_slice.126.rates, s32[2,2]{1,0:T(2,128)S(1)} %pad_add_fusion.ends, f32[2048,1024]{1,0:T(8,128)S(1)} %copy-done, f32[2048,1024]{1,0:T(8,128)S(1)} %copy-done, f32[2048,1024]{1,0:T(8,128)} %copy-done.1), custom_call_target="tpu_custom_call" | custom-call | flops 4294967296 | bytes 16777216 | tf_op jit(solution)/shard_map/attend/pallas_call | solution.py:98
  242.0 42.2 %collective-permute-done.12 = f32[2048]{0:T(1024)S(1)} collective-permute-done((f32[2048]{0:T(1024)S(1)}, f32[2048]{0:T(1024)S(1)}, u32[]{:S(2)}, u32[]{:S(2)}) %collective-permute-start.12) | collective-permute-done | bytes 8224 | tf_op jit(solution)/shard_map/ppermute | solution.py:543
  291.7 9.2 collective-permute-done.10.refs_1_.refs_3_.refs_4_
  310.1 9.7 fusion.21
  328.0 43.1 %collective-permute-done.16 = bf16[256,2048]{1,0:T(8,128)(2,1)S(1)} collective-permute-done((bf16[256,2048]{1,0:T(8,128)(2,1)S(1)}, bf16[256,2048]{1,0:T(8,128)(2,1)S(1)}, u32[]{:S(2)}, u32[]{:S(2)}) %collective-permute-start.16) | collective-permute-done | bytes 1048608 | tf_op jit(solution)/shard_map/ppermute | solution.py:594
  390.2 38.3 %gated_unit.1 = (bf16[2048,2048]{1,0:T(8,128)(2,1)}, bf16[2048,1408]{1,0:T(8,128)(2,1)}, bf16[2048,1408]{1,0:T(8,128)(2,1)}, bf16[2048,1408]{1,0:T(8,128)(2,1)}, f32[2048,1]{1,0:T(8,128)S(1)}) custom-call(s32[4]{0:T(128)S(1)} %pad_add_fusion.1.spots, bf16[2048,1024]{1,0:T(8,128)(2,1)} %maximum_select_fusion.3.own_ref, ...), custom_call_target="tpu_custom_call" | custom-call | flops 23622320128 | bytes 45621248 | tf_op jit(solution)/shard_map/gated_unit/pallas_call | solution.py:337
  434.6 6.8 collective-permute-done.20.other_ref
  448.2 16.6 %gradient_rows.8 = bf16[2048,1408]{1,0:T(8,128)(2,1)S(1)} custom-call(s32[4]{0:T(128)S(1)} %pad_add_fusion.1.spots, bf16[2048,2048]{1,0:T(8,128)(2,1)} %get-tuple-element.174.left_ref.dy_ref, bf16[2048,1408]{1,0:T(8,128)(2,1)S(1)} %bitcast.63), custom_call_target="tpu_custom_call" | custom-call | flops 11811160064 | bytes 17301504 | tf_op jit(solution)/shard_map/gradient_rows/pallas_call | solution.py:470
  472.5 22.4 %gated_unit_back.1 = (bf16[2048,1408]{1,0:T(8,128)(2,1)S(1)}, bf16[2048,1408]{1,0:T(8,128)(2,1)S(1)}, f32[2048,1]{1,0:T(8,128)S(1)}) custom-call(s32[4]{0:T(128)S(1)} %pad_add_fusion.1.spots, bf16[2048,2048]{1,0:T(8,128)(2,1)} %get-tuple-element.174.left_ref.dy_ref, bf16[2048,1408]{1,0:T(8,128)(2,1)} %get-tuple-element.178.one_ref, ...), custom_call_target="tpu_custom_call" | custom-call | flops 11811160064 | bytes 37232640 | tf_op jit(solution)/shard_map/gated_unit_back/pallas_call | solution.py:374
  500.8 19.8 %fold_half.6 = bf16[2048,1024]{1,0:T(8,128)(2,1)} custom-call(s32[4]{0:T(128)S(1)} %pad_add_fusion.1.spots, bf16[2048,1408]{1,0:T(8,128)(2,1)} %copy-done.49, bf16[2048,1408]{1,0:T(8,128)(2,1)} %copy-done.46, bf16[1024,1408]{1,0:T(8,128)(2,1)S(1)} %copy-done.28, bf16[1024,1408]{1,0:T(8,128)(2,1)} %collective-permute-done.10.refs_1_.refs_3_.refs_4_, ...), custom_call_target="tpu_custom_call" | custom-call | flops 11811160064 | bytes 21495808 | tf_op jit(solution)/shard_map/fold_half/pallas_call | solution.py:435
  529.6 9.5 gradient_rows.9
  539.1 22.0 %fold_half.7 = (bf16[2048,512]{1,0:T(8,128)(2,1)}, f32[2048,512]{1,0:T(8,128)}) custom-call(s32[4]{0:T(128)S(1)} %pad_add_fusion.1.spots, bf16[2048,1408]{1,0:T(8,128)(2,1)} %copy-done.49, bf16[2048,1408]{1,0:T(8,128)(2,1)} %copy-done.46, bf16[2048,1024]{1,0:T(8,128)(2,1)} %collective-permute-done.21.refs_2_, bf16[1024,1408]{1,0:T(8,128)(2,1)S(1)} %copy-done.29, ...), custom_call_target="tpu_custom_call" | custom-call | flops 11811160064 | bytes 27787264 | tf_op jit(solution)/shard_map/fold_half/pallas_call | solution.py:435
  567.1 16.5 %gradient_rows.10 = bf16[2048,1408]{1,0:T(8,128)(2,1)S(1)} custom-call(s32[4]{0:T(128)S(1)} %pad_add_fusion.1.spots, bf16[2048,2048]{1,0:T(8,128)(2,1)} %get-tuple-element.188.left_ref, bf16[2048,1408]{1,0:T(8,128)(2,1)S(1)} %copy-done.50), custom_call_target="tpu_custom_call" | custom-call | flops 11811160064 | bytes 17301504 | tf_op jit(solution)/shard_map/gradient_rows/pallas_call | solution.py:470
  588.7 11.4 %fold_half.8 = bf16[2048,1024]{1,0:T(8,128)(2,1)} custom-call(s32[4]{0:T(128)S(1)} %pad_add_fusion.1.spots, bf16[2048,1408]{1,0:T(8,128)(2,1)S(1)} %copy-done.48, bf16[2048,1408]{1,0:T(8,128)(2,1)} %all-gather.17.cloned.1.call-done.refs_0_.refs_1_.refs_2_), custom_call_target="tpu_custom_call" | custom-call | flops 5905580032 | bytes 9961472 | tf_op jit(solution)/shard_map/fold_half/pallas_call | solution.py:435
  600.1 9.5 collective-permute-done.23
  609.9 6.0 multiply_reduce_fusion.2
  620.9 11.9 %convolution_convert_fusion.1 = bf16[2048,512]{1,0:T(8,128)(2,1)S(1)} fusion(f32[2048,512]{1,0:T(8,128)} %copy-done.51, f32[2048]{0:T(1024)S(1)} %add_rsqrt_fusion, bf16[2048,1024]{1,0:T(8,128)(2,1)} %collective-permute-done.13, bf16[2048,1024]{1,0:T(8,128)(2,1)} %maximum_select_fusion.2, pred[]{:T(512)S(6)} %eq.51), kind=kOutput, calls=%fused_computation.28 | convolution fusion | flops 4335861760 | bytes 14688257 | tf_op jit(solution)/shard_map/dot_general | solution.py:32
  634.9 7.4 collective-permute-done.29
  654.8 15.0 %fold_half.9 = (bf16[2048,512]{1,0:T(8,128)(2,1)}, f32[2048,512]{1,0:T(8,128)S(1)}) custom-call(s32[4]{0:T(128)S(1)} %pad_add_fusion.1.spots, bf16[2048,1408]{1,0:T(8,128)(2,1)} %get-tuple-element.192.right_ref.refs_0_, bf16[2048,1024]{1,0:T(8,128)(2,1)} %collective-permute-done.27.refs_1_, ...), custom_call_target="tpu_custom_call" | custom-call | flops 5905580032 | bytes 16252928 | tf_op jit(solution)/shard_map/fold_half/pallas_call | solution.py:435
  669.8 29.5 %collective-permute-done.32 = f32[2048]{0:T(1024)S(1)} collective-permute-done((f32[2048]{0:T(1024)S(1)}, f32[2048]{0:T(1024)S(1)}, u32[]{:S(2)}, u32[]{:S(2)}) %collective-permute-start.32) | collective-permute-done | bytes 8224 | tf_op jit(solution)/shard_map/ppermute | solution.py:543
  706.2 21.3 %attend_back.1 = (bf16[2048,512]{1,0:T(8,128)(2,1)S(1)}, bf16[2048,512]{1,0:T(8,128)(2,1)S(1)}, bf16[2048,512]{1,0:T(8,128)(2,1)S(1)}) custom-call(f32[4]{0:T(128)S(1)} %dynamic_slice.126.rates, s32[2,2]{1,0:T(2,128)S(1)} %pad_add_fusion.ends, f32[2048,1024]{1,0:T(8,128)} %get-tuple-element.152.zq_ref.zk_ref, f32[2048,1024]{1,0:T(8,128)} %get-tuple-element.152.zq_ref.zk_ref, ...), custom_call_target="tpu_custom_call" | custom-call | flops 10737418240 | bytes 20971520 | tf_op jit(solution)/shard_map/attend_back/pallas_call | solution.py:119
  742.6 8.0 gradient_rows.11
  757.6 9.1 gradient_rows.13
  772.0 5.7 collective-permute-done.35
  783.7 7.9 gradient_rows.12
  791.5 13.9 %fold_half.10 = bf16[2048,1024]{1,0:T(8,128)(2,1)S(1)} custom-call(s32[4]{0:T(128)S(1)} %pad_add_fusion.1.spots, bf16[2048,1024]{1,0:T(8,128)(2,1)} %copy-done.6, bf16[2048,1024]{1,0:T(8,128)(2,1)} %pad_maximum_fusion.refs_1_.right_ref, bf16[1024,1024]{1,0:T(8,128)(2,1)S(1)} %copy-done.37, bf16[1024,1024]{1,0:T(8,128)(2,1)S(1)} %copy-done.44, ...), custom_call_target="tpu_custom_call" | custom-call | flops 8589934592 | bytes 16777216 | tf_op jit(solution)/shard_map/fold_half/pallas_call | solution.py:435
  813.9 5.5 multiply_reduce_fusion
  831.6 17.0 %fold_half.11 = (bf16[2048,512]{1,0:T(8,128)(2,1)}, f32[2048,512]{1,0:T(8,128)}) custom-call(s32[4]{0:T(128)S(1)} %pad_add_fusion.1.spots, bf16[2048,1024]{1,0:T(8,128)(2,1)} %copy-done.6, bf16[2048,1024]{1,0:T(8,128)(2,1)} %pad_maximum_fusion.refs_1_.right_ref, bf16[2048,1024]{1,0:T(8,128)(2,1)} %collective-permute-done.38.refs_2_, ...), custom_call_target="tpu_custom_call" | custom-call | flops 8589934592 | bytes 23068672 | tf_op jit(solution)/shard_map/fold_half/pallas_call | solution.py:435
  856.7 7.0 gradient_rows.15
  876.5 42.5 %collective-permute-done.45 = f32[2048]{0:T(1024)S(1)} collective-permute-done((f32[2048]{0:T(1024)S(1)}, f32[2048]{0:T(1024)S(1)}, u32[]{:S(2)}, u32[]{:S(2)}) %collective-permute-start.45) | collective-permute-done | bytes 8224 | tf_op jit(solution)/shard_map/ppermute | solution.py:543
  921.9 7.2 gradient_rows.14
  937.5 21.4 %collective-permute-done.47 = bf16[2,512,512]{2,1,0:T(8,128)(2,1)S(1)} collective-permute-done((bf16[2,512,512]{2,1,0:T(8,128)(2,1)S(1)}, bf16[2,512,512]{2,1,0:T(8,128)(2,1)S(1)}, u32[]{:S(2)}, u32[]{:S(2)}) %collective-permute-start.47) | collective-permute-done | bytes 1048608 | tf_op jit(solution)/shard_map/ppermute | solution.py:543
  973.2 7.8 place_quarters.5
  984.0 11.0 collective-permute-done.50
  995.0 21.7 %collective-permute-done.49 = bf16[256,2048]{1,0:T(8,128)(2,1)} collective-permute-done((bf16[256,2048]{1,0:T(8,128)(2,1)}, bf16[256,2048]{1,0:T(8,128)(2,1)}, u32[]{:S(2)}, u32[]{:S(2)}) %collective-permute-start.49) | collective-permute-done | bytes 1048608 | tf_op jit(solution)/shard_map/ppermute | solution.py:602
  1035.8 5.6 place_quarters.6
  1041.3 9.8 collective-permute-done.60
  1051.2 22.6 %collective-permute-done.59 = bf16[256,2048]{1,0:T(8,128)(2,1)S(1)} collective-permute-done((bf16[256,2048]{1,0:T(8,128)(2,1)S(1)}, bf16[256,2048]{1,0:T(8,128)(2,1)S(1)}, u32[]{:S(2)}, u32[]{:S(2)}) %collective-permute-start.59) | collective-permute-done | bytes 1048608 | tf_op jit(solution)/shard_map/ppermute | solution.py:602
  1073.8 7.7 collective-permute-done.56
  1097.6 6.3 place_quarters.8
  1103.9 7.8 place_quarters.9
  1117.0 6.2 place_quarters.7
  (440 shorter events, 313.7 us)
Async XLA Ops:
  8.0 88.9 %all-gather.7.cloned.1.call-start = ((), (), s32[]{:S(2)}) async-start(), calls=%async_computation.6 | async-start | bytes 2621440 | tf_op jit(solution)/shard_map/all_gather | solution.py:664
  10.3 136.4 %all-gather.9.cloned.1.call-start = ((), (), s32[]{:S(2)}) async-start(), calls=%async_computation.7 | async-start | bytes 2621440 | tf_op jit(solution)/shard_map/all_gather | solution.py:664
  12.5 171.6 %all-gather.11.cloned.1.call-start = ((), (), s32[]{:S(2)}) async-start(), calls=%async_computation.8 | async-start | bytes 1310720 | tf_op jit(solution)/shard_map/all_gather | solution.py:664
  13.7 80.9 %collective-permute-start = (bf16[256,2048]{1,0:T(8,128)(2,1)}, bf16[256,2048]{1,0:T(8,128)(2,1)S(1)}, u32[]{:S(2)}, u32[]{:S(2)}) collective-permute-start(bf16[256,2048]{1,0:T(8,128)(2,1)} %get-tuple-element.310), channel_id=1, source_target_pairs={{0,0},{4,1},{1,2},{5,3},{2,4},{6,5},{3,6},{7,7},{8,8},{12,9},{9,10... | collective-permute-start | bytes 3145736 | tf_op jit(solution)/shard_map/ppermute | solution.py:594
  15.8 78.8 %collective-permute-start.1 = (bf16[256,2048]{1,0:T(8,128)(2,1)S(1)}, bf16[256,2048]{1,0:T(8,128)(2,1)S(1)}, u32[]{:S(2)}, u32[]{:S(2)}) collective-permute-start(bf16[256,2048]{1,0:T(8,128)(2,1)S(1)} %get-tuple-element.311), channel_id=1, source_target_pairs={{1,0},{5,1},{0,2},{4,3},{3,4},{7,5},{2,6},{6,7},{9,8},{13,9},{8,10... | collective-permute-start | bytes 3145736 | tf_op jit(solution)/shard_map/ppermute | solution.py:594
  96.9 43.7 %collective-permute-start.2 = (bf16[512,2048]{1,0:T(8,128)(2,1)}, bf16[512,2048]{1,0:T(8,128)(2,1)}, u32[]{:S(2)}, u32[]{:S(2)}) collective-permute-start(bf16[512,2048]{1,0:T(8,128)(2,1)} %maximum_select_fusion.6), channel_id=1, source_target_pairs={{0,8},{1,9},{2,10},{3,11},{4,12},{5,13},{6,14},{7,15},{8,0},{9,1},... | collective-permute-start | bytes 6291464 | tf_op jit(solution)/shard_map/ppermute | solution.py:543
  98.9 138.9 %all-gather.13.cloned.1.call-start = ((), (), s32[]{:S(2)}) async-start(), calls=%async_computation.9 | async-start | bytes 3604480 | tf_op jit(solution)/shard_map/all_gather | solution.py:664
  99.0 47.7 %collective-permute-start.3 = (bf16[1024,1024]{1,0:T(8,128)(2,1)}, bf16[1024,1024]{1,0:T(8,128)(2,1)S(1)}, u32[]{:S(2)}, u32[]{:S(2)}) collective-permute-start(bf16[1024,1024]{1,0:T(8,128)(2,1)} %all-gather.7.cloned.1.call-done.refs_0_.refs_2_.refs_3_), channel_id=1, source_target_pairs={{0,16},{1,17},{2,18},{3,19},{4,20},{5,21},{6,22},{7,23},{8,24},{9,... | collective-permute-start | bytes 6291464 | tf_op jit(solution)/shard_map/ppermute | solution.py:543
  102.7 189.0 %all-gather.15.cloned.1.call-start = ((), (), s32[]{:S(2)}) async-start(), calls=%async_computation.10 | async-start | bytes 3604480 | tf_op jit(solution)/shard_map/all_gather | solution.py:664
  151.4 47.5 %collective-permute-start.7 = (bf16[1024,1024]{1,0:T(8,128)(2,1)}, bf16[1024,1024]{1,0:T(8,128)(2,1)}, u32[]{:S(2)}, u32[]{:S(2)}) collective-permute-start(bf16[1024,1024]{1,0:T(8,128)(2,1)} %all-gather.9.cloned.1.call-done.refs_0_.refs_4_.refs_5_), channel_id=1, source_target_pairs={{0,16},{1,17},{2,18},{3,19},{4,20},{5,21},{6,22},{7,23},{8,24},{9,... | collective-permute-start | bytes 6291464 | tf_op jit(solution)/shard_map/ppermute | solution.py:543
  157.6 314.8 %all-gather.17.cloned.1.call-start = ((), (), s32[]{:S(2)}) async-start(), calls=%async_computation.11 | async-start | bytes 6488064 | tf_op jit(solution)/shard_map/all_gather | solution.py:668
  198.9 38.8 %collective-permute-start.8 = (bf16[1024,512]{1,0:T(8,128)(2,1)}, bf16[1024,512]{1,0:T(8,128)(2,1)}, u32[]{:S(2)}, u32[]{:S(2)}) collective-permute-start(bf16[1024,512]{1,0:T(8,128)(2,1)} %all-gather.11.cloned.1.call-done), channel_id=1, source_target_pairs={{0,16},{1,17},{2,18},{3,19},{4,20},{5,21},{6,22},{7,23},{8,24},{9,... | collective-permute-start | bytes 3145736 | tf_op jit(solution)/shard_map/ppermute | solution.py:543
  237.8 63.2 %collective-permute-start.10 = (bf16[1024,1408]{1,0:T(8,128)(2,1)}, bf16[1024,1408]{1,0:T(8,128)(2,1)}, u32[]{:S(2)}, u32[]{:S(2)}) collective-permute-start(bf16[1024,1408]{1,0:T(8,128)(2,1)} %all-gather.13.cloned.1.call-done.refs_0_.refs_2_.refs_3_), channel_id=1, source_target_pairs={{0,16},{1,17},{2,18},{3,19},{4,20},{5,21},{6,22},{7,23},{8,24},{9,... | collective-permute-start | bytes 8650760 | tf_op jit(solution)/shard_map/ppermute | solution.py:543
  238.0 46.2 %collective-permute-start.9 = (bf16[2048,512]{1,0:T(8,128)(2,1)}, bf16[2048,512]{1,0:T(8,128)(2,1)S(1)}, u32[]{:S(2)}, u32[]{:S(2)}) collective-permute-start(bf16[2048,512]{1,0:T(8,128)(2,1)} %get-tuple-element.156), channel_id=1, source_target_pairs={{0,8},{1,9},{2,10},{3,11},{4,12},{5,13},{6,14},{7,15},{8,0},{9,1},... | collective-permute-start | bytes 6291464 | tf_op jit(solution)/shard_map/ppermute | solution.py:543
  241.8 42.5 %collective-permute-start.12 = (f32[2048]{0:T(1024)S(1)}, f32[2048]{0:T(1024)S(1)}, u32[]{:S(2)}, u32[]{:S(2)}) collective-permute-start(f32[2048]{0:T(1024)S(1)} %add.256), channel_id=1, source_target_pairs={{0,8},{1,9},{2,10},{3,11},{4,12},{5,13},{6,14},{7,15},{8,0},{9,1},... | collective-permute-start | bytes 24584 | tf_op jit(solution)/shard_map/ppermute | solution.py:543
  307.8 68.4 %collective-permute-start.15 = (bf16[1024,1408]{1,0:T(8,128)(2,1)S(1)}, bf16[1024,1408]{1,0:T(8,128)(2,1)S(1)}, u32[]{:S(2)}, u32[]{:S(2)}) collective-permute-start(bf16[1024,1408]{1,0:T(8,128)(2,1)S(1)} %copy-done.30), channel_id=1, source_target_pairs={{0,16},{1,17},{2,18},{3,19},{4,20},{5,21},{6,22},{7,23},{8,24},{9,... | collective-permute-start | bytes 8650760 | tf_op jit(solution)/shard_map/ppermute | solution.py:543
  319.8 53.6 %collective-permute-start.14 = (bf16[2048,512]{1,0:T(8,128)(2,1)}, bf16[2048,512]{1,0:T(8,128)(2,1)S(1)}, u32[]{:S(2)}, u32[]{:S(2)}) collective-permute-start(bf16[2048,512]{1,0:T(8,128)(2,1)} %get-tuple-element.314), channel_id=1, source_target_pairs={{0,8},{1,9},{2,10},{3,11},{4,12},{5,13},{6,14},{7,15},{8,0},{9,1},... | collective-permute-start | bytes 6291464 | tf_op jit(solution)/shard_map/ppermute | solution.py:543
  322.8 48.3 %collective-permute-start.16 = (bf16[256,2048]{1,0:T(8,128)(2,1)S(1)}, bf16[256,2048]{1,0:T(8,128)(2,1)S(1)}, u32[]{:S(2)}, u32[]{:S(2)}) collective-permute-start(bf16[256,2048]{1,0:T(8,128)(2,1)S(1)} %get-tuple-element.306), channel_id=1, source_target_pairs={{0,0},{4,1},{1,2},{5,3},{2,4},{6,5},{3,6},{7,7},{8,8},{12,9},{9,10... | collective-permute-start | bytes 3145736 | tf_op jit(solution)/shard_map/ppermute | solution.py:594
  327.9 43.2 %collective-permute-start.17 = (bf16[256,2048]{1,0:T(8,128)(2,1)S(1)}, bf16[256,2048]{1,0:T(8,128)(2,1)S(1)}, u32[]{:S(2)}, u32[]{:S(2)}) collective-permute-start(bf16[256,2048]{1,0:T(8,128)(2,1)S(1)} %get-tuple-element.307), channel_id=1, source_target_pairs={{1,0},{5,1},{0,2},{4,3},{3,4},{7,5},{2,6},{6,7},{9,8},{13,9},{8,10... | collective-permute-start | bytes 3145736 | tf_op jit(solution)/shard_map/ppermute | solution.py:594
  383.5 226.1 %reduce-scatter.7.cloned.1.call-start = ((), (), s32[]{:S(2)}) async-start(), calls=%async_computation.12 | async-start | bytes 6488064 | tf_op jit(solution)/shard_map/reduce_scatter | solution.py:708
  384.0 47.6 %collective-permute-start.19 = (bf16[512,2048]{1,0:T(8,128)(2,1)}, bf16[512,2048]{1,0:T(8,128)(2,1)S(1)}, u32[]{:S(2)}, u32[]{:S(2)}) collective-permute-start(bf16[512,2048]{1,0:T(8,128)(2,1)} %maximum_select_fusion.8), channel_id=1, source_target_pairs={{0,8},{1,9},{2,10},{3,11},{4,12},{5,13},{6,14},{7,15},{8,0},{9,1},... | collective-permute-start | bytes 6291464 | tf_op jit(solution)/shard_map/ppermute | solution.py:543
  472.4 353.0 %reduce-scatter.9.cloned.1.call-start = ((), (), s32[]{:S(2)}) async-start(), calls=%async_computation.13 | async-start | bytes 6488064 | tf_op jit(solution)/shard_map/reduce_scatter | solution.py:708
  561.1 39.0 %collective-permute-start.25 = (f32[2048]{0:T(1024)S(1)}, f32[2048]{0:T(1024)S(1)}, u32[]{:S(2)}, u32[]{:S(2)}) collective-permute-start(f32[2048]{0:T(1024)S(1)} %add.261), channel_id=1, source_target_pairs={{0,8},{1,9},{2,10},{3,11},{4,12},{5,13},{6,14},{7,15},{8,0},{9,1},... | collective-permute-start | bytes 24584 | tf_op jit(solution)/shard_map/ppermute | solution.py:543
  562.4 47.2 %collective-permute-start.23 = (bf16[2048,512]{1,0:T(8,128)(2,1)}, bf16[2048,512]{1,0:T(8,128)(2,1)}, u32[]{:S(2)}, u32[]{:S(2)}) collective-permute-start(bf16[2048,512]{1,0:T(8,128)(2,1)} %get-tuple-element.191), channel_id=1, source_target_pairs={{0,8},{1,9},{2,10},{3,11},{4,12},{5,13},{6,14},{7,15},{8,0},{9,1},... | collective-permute-start | bytes 6291464 | tf_op jit(solution)/shard_map/ppermute | solution.py:543
  564.5 35.7 %collective-permute-start.24 = (bf16[512,1408]{1,0:T(8,128)(2,1)}, bf16[512,1408]{1,0:T(8,128)(2,1)}, u32[]{:S(2)}, u32[]{:S(2)}) collective-permute-start(bf16[512,1408]{1,0:T(8,128)(2,1)} %get-tuple-element.289), channel_id=1, source_target_pairs={{0,16},{1,17},{2,18},{3,19},{4,20},{5,21},{6,22},{7,23},{8,24},{9,... | collective-permute-start | bytes 4325384 | tf_op jit(solution)/shard_map/ppermute | solution.py:543
  609.6 320.8 %reduce-scatter.13.cloned.1.call-start = ((), (), s32[]{:S(2)}) async-start(), calls=%async_computation.15 | async-start | bytes 1310720 | tf_op jit(solution)/shard_map/reduce_scatter | solution.py:702
  652.8 46.5 %collective-permute-start.30 = (bf16[2048,512]{1,0:T(8,128)(2,1)}, bf16[2048,512]{1,0:T(8,128)(2,1)}, u32[]{:S(2)}, u32[]{:S(2)}) collective-permute-start(bf16[2048,512]{1,0:T(8,128)(2,1)} %dynamic-slice_convert_fusion), channel_id=1, source_target_pairs={{0,8},{1,9},{2,10},{3,11},{4,12},{5,13},{6,14},{7,15},{8,0},{9,1},... | collective-permute-start | bytes 6291464 | tf_op jit(solution)/shard_map/ppermute | solution.py:543
  654.0 45.4 %collective-permute-start.31 = (bf16[1024,512]{1,0:T(8,128)(2,1)}, bf16[1024,512]{1,0:T(8,128)(2,1)}, u32[]{:S(2)}, u32[]{:S(2)}) collective-permute-start(bf16[1024,512]{1,0:T(8,128)(2,1)} %get-tuple-element.210), channel_id=1, source_target_pairs={{0,16},{1,17},{2,18},{3,19},{4,20},{5,21},{6,22},{7,23},{8,24},{9,... | collective-permute-start | bytes 3145736 | tf_op jit(solution)/shard_map/ppermute | solution.py:543
  654.6 44.7 %collective-permute-start.32 = (f32[2048]{0:T(1024)S(1)}, f32[2048]{0:T(1024)S(1)}, u32[]{:S(2)}, u32[]{:S(2)}) collective-permute-start(f32[2048]{0:T(1024)S(1)} %add.275), channel_id=1, source_target_pairs={{0,8},{1,9},{2,10},{3,11},{4,12},{5,13},{6,14},{7,15},{8,0},{9,1},... | collective-permute-start | bytes 24584 | tf_op jit(solution)/shard_map/ppermute | solution.py:543
  699.4 51.2 %collective-permute-start.33 = (bf16[512,1408]{1,0:T(8,128)(2,1)}, bf16[512,1408]{1,0:T(8,128)(2,1)}, u32[]{:S(2)}, u32[]{:S(2)}) collective-permute-start(bf16[512,1408]{1,0:T(8,128)(2,1)} %get-tuple-element.217), channel_id=1, source_target_pairs={{0,16},{1,17},{2,18},{3,19},{4,20},{5,21},{6,22},{7,23},{8,24},{9,... | collective-permute-start | bytes 4325384 | tf_op jit(solution)/shard_map/ppermute | solution.py:543
  700.1 50.4 %collective-permute-start.34 = (bf16[2048,512]{1,0:T(8,128)(2,1)}, bf16[2048,512]{1,0:T(8,128)(2,1)}, u32[]{:S(2)}, u32[]{:S(2)}) collective-permute-start(bf16[2048,512]{1,0:T(8,128)(2,1)} %get-tuple-element.218), channel_id=1, source_target_pairs={{0,8},{1,9},{2,10},{3,11},{4,12},{5,13},{6,14},{7,15},{8,0},{9,1},... | collective-permute-start | bytes 6291464 | tf_op jit(solution)/shard_map/ppermute | solution.py:543
  734.0 196.4 %reduce-scatter.11.cloned.1.call-start = ((), (), s32[]{:S(2)}) async-start(), calls=%async_computation.14 | async-start | bytes 3604480 | tf_op jit(solution)/shard_map/reduce_scatter | solution.py:702
  771.1 38.4 %collective-permute-start.37 = (bf16[512,1024]{1,0:T(8,128)(2,1)S(1)}, bf16[512,1024]{1,0:T(8,128)(2,1)}, u32[]{:S(2)}, u32[]{:S(2)}) collective-permute-start(bf16[512,1024]{1,0:T(8,128)(2,1)S(1)} %get-tuple-element.299), channel_id=1, source_target_pairs={{0,16},{1,17},{2,18},{3,19},{4,20},{5,21},{6,22},{7,23},{8,24},{9,... | collective-permute-start | bytes 3145736 | tf_op jit(solution)/shard_map/ppermute | solution.py:543
  809.6 161.4 %reduce-scatter.15.cloned.1.call-start = ((), (), s32[]{:S(2)}) async-start(), calls=%async_computation.16 | async-start | bytes 2621440 | tf_op jit(solution)/shard_map/reduce_scatter | solution.py:702
  813.6 35.0 %collective-permute-start.41 = (bf16[512,1408]{1,0:T(8,128)(2,1)}, bf16[512,1408]{1,0:T(8,128)(2,1)}, u32[]{:S(2)}, u32[]{:S(2)}) collective-permute-start(bf16[512,1408]{1,0:T(8,128)(2,1)} %maximum_select_fusion.17), channel_id=1, source_target_pairs={{0,8},{1,9},{2,10},{3,11},{4,12},{5,13},{6,14},{7,15},{8,0},{9,1},... | collective-permute-start | bytes 4325384 | tf_op jit(solution)/shard_map/ppermute | solution.py:543
  865.0 151.8 %reduce-scatter.17.cloned.1.call-start = ((), (), s32[]{:S(2)}) async-start(), calls=%async_computation.17 | async-start | bytes 2621440 | tf_op jit(solution)/shard_map/reduce_scatter | solution.py:702
  870.2 49.5 %collective-permute-start.46 = (bf16[512,2816]{1,0:T(8,128)(2,1)}, bf16[512,2816]{1,0:T(8,128)(2,1)}, u32[]{:S(2)}, u32[]{:S(2)}) collective-permute-start(bf16[512,2816]{1,0:T(8,128)(2,1)} %constant_dynamic-update-slice_fusion.2.refs_0_.refs_1_), channel_id=1, source_target_pairs={{0,4},{1,5},{2,6},{3,7},{4,0},{5,1},{6,2},{7,3},{8,12},{9,13},{10,... | collective-permute-start | bytes 8650760 | tf_op jit(solution)/shard_map/ppermute | solution.py:543
  871.3 47.8 %collective-permute-start.43 = (bf16[2048,512]{1,0:T(8,128)(2,1)}, bf16[2048,512]{1,0:T(8,128)(2,1)}, u32[]{:S(2)}, u32[]{:S(2)}) collective-permute-start(bf16[2048,512]{1,0:T(8,128)(2,1)} %get-tuple-element.236), channel_id=1, source_target_pairs={{0,8},{1,9},{2,10},{3,11},{4,12},{5,13},{6,14},{7,15},{8,0},{9,1},... | collective-permute-start | bytes 6291464 | tf_op jit(solution)/shard_map/ppermute | solution.py:543
  872.4 47.3 %collective-permute-start.44 = (bf16[1024,1024]{1,0:T(8,128)(2,1)}, bf16[1024,1024]{1,0:T(8,128)(2,1)}, u32[]{:S(2)}, u32[]{:S(2)}) collective-permute-start(bf16[1024,1024]{1,0:T(8,128)(2,1)} %gradient_rows.12), channel_id=1, source_target_pairs={{0,16},{1,17},{2,18},{3,19},{4,20},{5,21},{6,22},{7,23},{8,24},{9,... | collective-permute-start | bytes 6291464 | tf_op jit(solution)/shard_map/ppermute | solution.py:543
  874.5 44.5 %collective-permute-start.45 = (f32[2048]{0:T(1024)S(1)}, f32[2048]{0:T(1024)S(1)}, u32[]{:S(2)}, u32[]{:S(2)}) collective-permute-start(f32[2048]{0:T(1024)S(1)} %add.285), channel_id=1, source_target_pairs={{0,8},{1,9},{2,10},{3,11},{4,12},{5,13},{6,14},{7,15},{8,0},{9,1},... | collective-permute-start | bytes 24584 | tf_op jit(solution)/shard_map/ppermute | solution.py:543
  963.6 53.2 %collective-permute-start.51 = (bf16[512,1408]{1,0:T(8,128)(2,1)}, bf16[512,1408]{1,0:T(8,128)(2,1)}, u32[]{:S(2)}, u32[]{:S(2)}) collective-permute-start(bf16[512,1408]{1,0:T(8,128)(2,1)} %maximum_select_fusion.18), channel_id=1, source_target_pairs={{0,8},{1,9},{2,10},{3,11},{4,12},{5,13},{6,14},{7,15},{8,0},{9,1},... | collective-permute-start | bytes 4325384 | tf_op jit(solution)/shard_map/ppermute | solution.py:543
  967.0 49.7 %collective-permute-start.49 = (bf16[256,2048]{1,0:T(8,128)(2,1)}, bf16[256,2048]{1,0:T(8,128)(2,1)}, u32[]{:S(2)}, u32[]{:S(2)}) collective-permute-start(bf16[256,2048]{1,0:T(8,128)(2,1)} %get-tuple-element.293), channel_id=1, source_target_pairs={{0,0},{1,4},{2,1},{3,5},{4,2},{5,6},{6,3},{7,7},{8,8},{9,12},{10,9... | collective-permute-start | bytes 3145736 | tf_op jit(solution)/shard_map/ppermute | solution.py:602
  972.1 44.6 %collective-permute-start.53 = (bf16[256,1536]{1,0:T(8,128)(2,1)S(1)}, bf16[256,1536]{1,0:T(8,128)(2,1)}, u32[]{:S(2)}, u32[]{:S(2)}) collective-permute-start(bf16[256,1536]{1,0:T(8,128)(2,1)S(1)} %pad_maximum_fusion.5), channel_id=1, source_target_pairs={{0,8},{1,9},{2,10},{3,11},{4,12},{5,13},{6,14},{7,15},{8,0},{9,1},... | collective-permute-start | bytes 2359304 | tf_op jit(solution)/shard_map/ppermute | solution.py:543
  973.2 43.6 %collective-permute-start.52 = (bf16[256,1408]{1,0:T(8,128)(2,1)}, bf16[256,1408]{1,0:T(8,128)(2,1)}, u32[]{:S(2)}, u32[]{:S(2)}) collective-permute-start(bf16[256,1408]{1,0:T(8,128)(2,1)} %reduce-scatter.11.cloned.1.call-done), channel_id=1, source_target_pairs={{0,16},{1,17},{2,18},{3,19},{4,20},{5,21},{6,22},{7,23},{8,24},{9,... | collective-permute-start | bytes 2162696 | tf_op jit(solution)/shard_map/ppermute | solution.py:543
  1022.4 51.3 %collective-permute-start.57 = (bf16[512,1408]{1,0:T(8,128)(2,1)S(1)}, bf16[512,1408]{1,0:T(8,128)(2,1)S(1)}, u32[]{:S(2)}, u32[]{:S(2)}) collective-permute-start(bf16[512,1408]{1,0:T(8,128)(2,1)S(1)} %maximum_select_fusion.19), channel_id=1, source_target_pairs={{0,8},{1,9},{2,10},{3,11},{4,12},{5,13},{6,14},{7,15},{8,0},{9,1},... | collective-permute-start | bytes 4325384 | tf_op jit(solution)/shard_map/ppermute | solution.py:543
  1024.0 49.7 %collective-permute-start.58 = (bf16[256,3072]{1,0:T(8,128)(2,1)S(1)}, bf16[256,3072]{1,0:T(8,128)(2,1)S(1)}, u32[]{:S(2)}, u32[]{:S(2)}) collective-permute-start(bf16[256,3072]{1,0:T(8,128)(2,1)S(1)} %constant_dynamic-update-slice_fusion.6), channel_id=1, source_target_pairs={{0,16},{1,17},{2,18},{3,19},{4,20},{5,21},{6,22},{7,23},{8,24},{9,... | collective-permute-start | bytes 4718600 | tf_op jit(solution)/shard_map/ppermute | solution.py:543
  1032.2 41.6 %collective-permute-start.59 = (bf16[256,2048]{1,0:T(8,128)(2,1)S(1)}, bf16[256,2048]{1,0:T(8,128)(2,1)S(1)}, u32[]{:S(2)}, u32[]{:S(2)}) collective-permute-start(bf16[256,2048]{1,0:T(8,128)(2,1)S(1)} %get-tuple-element.291), channel_id=1, source_target_pairs={{0,0},{1,4},{2,1},{3,5},{4,2},{5,6},{6,3},{7,7},{8,8},{9,12},{10,9... | collective-permute-start | bytes 3145736 | tf_op jit(solution)/shard_map/ppermute | solution.py:602
  1035.7 45.8 %collective-permute-start.56 = (bf16[256,2048]{1,0:T(8,128)(2,1)S(1)}, bf16[256,2048]{1,0:T(8,128)(2,1)S(1)}, u32[]{:S(2)}, u32[]{:S(2)}) collective-permute-start(bf16[256,2048]{1,0:T(8,128)(2,1)S(1)} %constant_dynamic-update-slice_fusion.4), channel_id=1, source_target_pairs={{0,16},{1,17},{2,18},{3,19},{4,20},{5,21},{6,22},{7,23},{8,24},{9,... | collective-permute-start | bytes 3145736 | tf_op jit(solution)/shard_map/ppermute | solution.py:543
  (115 other events, 1366.2 us)
Sparse Core Ops, SparseCore 0:
  11.0 82.8 all-gather.6
  96.1 46.1 all-gather.8
  144.4 27.5 all-gather.10
  173.9 57.9 all-gather.12
  233.8 57.8 all-gather.14
Sparse Core Ops, SparseCore 1:
  383.5 88.8 all-gather.16
  475.9 108.8 reduce-scatter.6
  609.7 126.2 reduce-scatter.8
  738.3 25.1 reduce-scatter.12
  809.6 58.7 reduce-scatter.10
  871.4 42.7 reduce-scatter.14
  930.5 45.8 reduce-scatter.16

commit v12 on v11

--- a/solution.py
+++ b/solution.py
@@ -596,16 +596,17 @@
         ]
         return ordered(batch_of(place), *arrived, 0)
 
-    def send_back(x):
+    def back_slots(x):
         slots = natural(x).reshape(2, run, width)
         return [
-            lax.ppermute(
-                lax.dynamic_index_in_dim(slots, (batch_of(place) + p) % 2, 0, False),
-                AXES,
-                [(to, origin) for origin, to in routes(p)],
-            )
-            for p in range(2)
+            lax.dynamic_index_in_dim(slots, (batch_of(place) + p) % 2, 0, False) for p in range(2)
         ]
+
+    def send_slot(x, p):
+        return lax.ppermute(x, AXES, [(to, origin) for origin, to in routes(p)])
+
+    def send_back(x):
+        return [send_slot(slot, p) for p, slot in enumerate(back_slots(x))]
 
     def as_batches(arrived):
         return ordered(place % 2, arrived[0][None], arrived[1][None], 0)
@@ -789,34 +790,35 @@
     dy_other = swap_b(dy_run)
     w_1, w_2 = [g_1, *s_1], [g_2, *s_2]
     hidden_two, z_one, z_two, product, m_scale = gated_unit(spots, low_middle, other_middle, w_1, w_2)
-    z_one, z_two, product, dy_other = tie(z_one, z_two, product, dy_other)
+    z_one, z_two, product, dy_other, w_d[0] = tie(z_one, z_two, product, dy_other, w_d[0])
 
     dy_pair = ordered(b, dy_run, dy_other, 0)
     dy_all, dy_own = enter(spots, blocks, dy_pair, swap_c(dy_pair))
-    f_down = whole_rows(dy_all, product)
-    z_one, z_two, product, f_down, w_d[0] = tie(z_one, z_two, product, f_down, w_d[0])
-
-
-    f_down = scattered_all(f_down)
+
+
     d_one, d_two, lean_m = gated_unit_back(spots, dy_all, z_one, z_two, w_d)
     sent = fold_half(spots, [d_one, d_two], [w_1, w_2])
-    sent, d_two, lean_m = tie(sent, d_two, lean_m)
+    sent, product, lean_m, dy_all = tie(sent, product, lean_m, dy_all)
 
     arrived = swap_c(sent)
-    t_two = away(hidden_two, d_two)
+    f_down = whole_rows(dy_all, product)
+    arrived, f_down = tie(arrived, f_down)
+
+    f_down = scattered_all(f_down)
     lean_m = lean_m[:, 0]
     lean_c = swap_c(lean_m)
     sent, mine = fold_half(spots, [d_one, d_two], [w_1, w_2], arrived)
-    sent, d_one, t_two, product, lean_c = tie(sent, d_one, t_two, product, lean_c)
+    sent, d_one, d_two, product, lean_c = tie(sent, d_one, d_two, product, lean_c)
 
     crossed = swap_b(sent)
+    t_two = away(hidden_two, d_two)
     lean_m = lean_m + lean_c
     lean_b = swap_b(lean_m)
     upper, lower = in_two(t_two)
     upper = sent_a(upper)
     f_one = whole_rows(hidden_two, d_one)
     result = fold_half(spots, [product], [w_d])
-    crossed, result, f_one, upper, f_down, lean_b = tie(crossed, result, f_one, upper, f_down, lean_b)
+    crossed, result, f_one, upper, lean_b = tie(crossed, result, f_one, upper, lean_b)
 
     f_one = scattered_all(f_one)
     d_hidden = mine + crossed.astype(F32)
@@ -830,7 +832,6 @@
 
     arrived = swap_c(sent)
     r_result = swap_c(result)
-    y_down = spread_a(f_down)
     lean_o = lean_o + swap_c(lean_o)
     p_out = cross_tokens(lifted, (o_scale * d_middle).astype(LOW)).astype(LOW)
     p_out = jnp.transpose(p_out.reshape(shards, spread, part, -1), (1, 0, 2, 3))
@@ -839,15 +840,16 @@
     d_gated = times_transposed(d_branch, row_half(w_o, c)) + arrived.astype(F32)
     sent = columns(d_gated, (1 - b) * own, own).astype(LOW)
     mine = columns(d_gated, b * own, own)
-    sent, mine, r_result, t_out, lean_o, y_down = tie(sent, mine, r_result, t_out, lean_o, y_down)
+    sent, mine, r_result, t_out, lean_o = tie(sent, mine, r_result, t_out, lean_o)
 
     crossed = swap_b(sent)
     lean_b = swap_b(lean_o)
     r_out = sent_a(t_out[1:])
     result, result_mine = fold_half(spots, [product], [w_d], r_result)
-    crossed, result, r_out, lower, lean_b = tie(crossed, result, r_out, lower, lean_b)
+    crossed, result, r_out, lower, lean_b, f_down = tie(crossed, result, r_out, lower, lean_b, f_down)
 
     lower = sent_a(lower)
+    y_down = over_spread(f_down)
     result = swap_b(result)
     f_out = scattered(sum([x.astype(F32) for x in r_out], t_out[0].astype(F32)).astype(LOW))
     o_normed = attended * o_scale
@@ -859,7 +861,7 @@
     d_qk = joined(d_query, d_key)
     d_vg = joined(d_value, d_gate)
     t_qk = away(hidden_one, d_qk)
-    d_qk, d_vg, t_qk, lower, result = tie(d_qk, d_vg, t_qk, lower, result)
+    d_qk, d_vg, t_qk, lower, result, y_down = tie(d_qk, d_vg, t_qk, lower, result, y_down)
 
     upper_qk, lower_qk = in_two(t_qk)
     upper_qk = sent_a(upper_qk)
@@ -873,6 +875,7 @@
 
     f_two = scattered(f_two)
     lower_qk = sent_a(lower_qk)
+    y_down = by_spread([f_down, *y_down])
     x_down = swap_b(y_down)
     y_one = over_spread(f_one)
     arrived = swap_c(sent)
@@ -910,28 +913,33 @@
         input_grad, output, x_one, y_two, x_oqk, f_vg, g_down
     )
 
-    x_vg = swap_b(f_vg)
-    four_one = spread_c(joined(y_one, x_one))
-    x_vg, four_one = tie(x_vg, four_one)
-
-    f_vg = joined(f_vg, x_vg)
     y_vg = over_spread(f_vg)
     y_two = by_spread([f_two, *y_two])
     x_two = swap_b(y_two)
     f_oqk = joined(f_oqk, x_oqk)
-    y_oqk = over_spread(f_oqk)
-    input_grad = send_back(input_grad)
-    [g_one] = place_quarters(spots, four_one, (0, units))
-    y_vg, x_two, y_oqk, input_grad, g_one = tie(y_vg, x_two, y_oqk, input_grad, g_one)
-
-    four_vg = spread_c(by_spread([f_vg, *y_vg]))
-    four_two = spread_c(joined(y_two, x_two))
-    four_oqk = spread_c(by_spread([f_oqk, *y_oqk]))
+    upper, lower = in_two([f_oqk])
+    upper = over_spread(upper[0])
+    back_one, back_two = back_slots(input_grad)
+    back_one = send_slot(back_one, 0)
+    output = as_batches(output)
+    [g_one] = place_quarters(spots, spread_c(joined(y_one, x_one)), (0, units))
+    y_vg, x_two, upper, lower, back_one, back_two, output, g_one = tie(
+        y_vg, x_two, upper, lower, back_one, back_two, output, g_one
+    )
+
+    y_vg = by_spread([f_vg, *y_vg])
+    x_vg = swap_b(y_vg)
+    lower = over_spread(lower[0])
+    back_two = send_slot(back_two, 1)
+    [g_two] = place_quarters(spots, spread_c(joined(y_two, x_two)), (0, units))
+    x_vg, lower, back_two, g_two = tie(x_vg, lower, back_two, g_two)
+
+    four_vg = spread_c(joined(y_vg, x_vg))
+    four_oqk = spread_c(by_spread([f_oqk, *stacked(upper, lower)]))
+    g_value, g_gate = place_quarters(spots, four_vg, (0, own), (own, own))
     g_query, g_key = place_quarters(spots, four_oqk, (own, own), (2 * own, own))
-    g_value, g_gate = place_quarters(spots, four_vg, (0, own), (own, own))
-    [g_two] = place_quarters(spots, four_two, (0, units))
     g_out = features_in_order(four_oqk, 0, own)
-    output, input_grad = as_batches(output), as_batches(input_grad)
+    input_grad = as_batches([back_one, back_two])
     return output, input_grad, g_query, g_key, g_value, g_gate, g_out, g_one, g_two, g_down
 
 

time: 1140 us -> 1200 us (1.053)
  waiting for transfers between devices: 450 us -> 491 us
  other arithmetic: 103 us -> 115 us
    ppermute x4, waiting for transfers between devices: 119 us -> 159 us  [bring(): lax.ppermute(lax.dynamic_index_in_dim(x, (place + p) % 2, 0, False), AXES...]
    ppermute x56 -> x57, waiting for transfers between devices: 258 us -> 297 us  [move(): return lax.ppermute(x, AXES, pairs)]
    ppermute x4, waiting for transfers between devices: 65.2 us -> 31.4 us  [send_slot(): return lax.ppermute(x, AXES, [(to, origin) for origin, to in routes(p)])]
    ppermute x56 -> x57, starting transfers between devices: 55.2 us -> 59.7 us  [move(): return lax.ppermute(x, AXES, pairs)]
  transfers between devices with their start and end apart: 76 -> 77, of which waited for: 30 -> 28; matrix products, arithmetic and copies ran while one was open for 15% -> 14% of each run, Pallas kernels for 30% -> 25%
where the time goes in v12:
time: 1200 us; the launch traced here: 1180 us
  waiting for transfers between devices  491 us (41%)
  Pallas kernels  341 us (28%)
  other arithmetic  115 us (10%)
  local copies, waits for them, and re-layouts  109 us (9%)
  starting transfers between devices  74.8 us (6%)
  matrix products  30.6 us (3%)
  between operations  17 us (1%)
    ppermute x57, waiting for transfers between devices, move(): return lax.ppermute(x, AXES, pairs)  297 us
    ppermute x4, waiting for transfers between devices, bring(): lax.ppermute(lax.dynamic_index_in_dim(x, (place + p) % 2, 0, False), AXES...  159 us
    pallas_call x6, Pallas kernels, fold_half(): pl.pallas_call(functools.partial(fold_kernel, len(values), arrived is not...  97.2 us
    pallas_call x8, Pallas kernels, gradient_rows(): pl.pallas_call(gradient_kernel, out_shape=out, grid_spec=pltpu.PrefetchSc...  82.9 us
    unnamed x201, local copies, waits for them, and re-layouts  74.2 us
    ppermute x57, starting transfers between devices, move(): return lax.ppermute(x, AXES, pairs)  59.7 us
    select_n x23, other arithmetic, ordered(): jnp.where(index == 0, jnp.concatenate([mine, other], axis), jnp.concatena...  53.9 us
    pallas_call x1, Pallas kernels, gated_unit(): pl.pallas_call(unit_kernel, out_shape=outs, grid_spec=pltpu.PrefetchScala...  38 us
  transfers between devices with their start and end apart: 77, of which 28 were waited for; matrix products, arithmetic and copies ran while one was open for 14% of the time, Pallas kernels for 25%

profile of v12, /device:TPU:17, one launch (start us, length us, event | category | flops | bytes accessed | tf_op | source)
XLA Modules:
  0.0 1178.8 jit_solution(7671821439212379981)
XLA Ops:
  18.7 75.9 %collective-permute-done = bf16[256,2048]{1,0:T(8,128)(2,1)S(1)} collective-permute-done((bf16[256,2048]{1,0:T(8,128)(2,1)}, bf16[256,2048]{1,0:T(8,128)(2,1)S(1)}, u32[]{:S(2)}, u32[]{:S(2)}) %collective-permute-start) | collective-permute-done | bytes 1048608 | tf_op jit(solution)/shard_map/ppermute | solution.py:594
  102.7 37.9 %collective-permute-done.2 = bf16[512,2048]{1,0:T(8,128)(2,1)} collective-permute-done((bf16[512,2048]{1,0:T(8,128)(2,1)}, bf16[512,2048]{1,0:T(8,128)(2,1)}, u32[]{:S(2)}, u32[]{:S(2)}) %collective-permute-start.2) | collective-permute-done | bytes 2097184 | tf_op jit(solution)/shard_map/ppermute | solution.py:543
  140.6 6.0 maximum_select_fusion.1.own_ref
  165.0 18.8 %enter.2 = (bf16[2048,2048]{1,0:T(8,128)(2,1)}, f32[2048,1024]{1,0:T(8,128)}, f32[2048,1]{1,0:T(8,128)S(1)}, bf16[2048,512]{1,0:T(8,128)(2,1)S(1)}) custom-call(s32[4]{0:T(128)S(1)} %pad_add_fusion.1.spots, bf16[1024,2048]{1,0:T(8,128)(2,1)S(1)} %copy-done.14, bf16[1024,2048]{1,0:T(8,128)(2,1)} %collective-permute-done.4.other_ref, ...), custom_call_target="tpu_custom_call" | custom-call | flops 8589934592 | bytes 31465472 | tf_op jit(solution)/shard_map/enter/pallas_call | solution.py:244
  184.8 14.2 %collective-permute-done.7.refs_1_.refs_5_.refs_6_ = bf16[1024,1024]{1,0:T(8,128)(2,1)} collective-permute-done((bf16[1024,1024]{1,0:T(8,128)(2,1)}, bf16[1024,1024]{1,0:T(8,128)(2,1)}, u32[]{:S(2)}, u32[]{:S(2)}) %collective-permute-start.7) | collective-permute-done | bytes 2097184 | tf_op jit(solution)/shard_map/ppermute | solution.py:543
  201.8 14.2 %project.1.zv_ref = f32[2048,1024]{1,0:T(8,128)S(1)} custom-call(s32[4]{0:T(128)S(1)} %pad_add_fusion.1.spots, bf16[2048,2048]{1,0:T(8,128)(2,1)} %get-tuple-element.155.h_ref.left_ref, bf16[1024,1024]{1,0:T(8,128)(2,1)S(1)} %copy-done.41, bf16[1024,1024]{1,0:T(8,128)(2,1)} %collective-permute-done.7.refs_1_.refs_5_.refs_6_), custom_call_target="tpu_custom_call" | custom-call | flops 8589934592 | bytes 20971520 | tf_op jit(solution)/shard_map/project/pallas_call | solution.py:275
  219.4 12.3 %attend.1 = f32[2048,512]{1,0:T(8,128)S(1)} custom-call(f32[4]{0:T(128)S(1)} %dynamic_slice.126.rates, s32[2,2]{1,0:T(2,128)S(1)} %pad_add_fusion.ends, f32[2048,1024]{1,0:T(8,128)S(1)} %copy-done, f32[2048,1024]{1,0:T(8,128)S(1)} %copy-done, f32[2048,1024]{1,0:T(8,128)} %copy-done.1), custom_call_target="tpu_custom_call" | custom-call | flops 4294967296 | bytes 16777216 | tf_op jit(solution)/shard_map/attend/pallas_call | solution.py:98
  242.0 42.2 %collective-permute-done.12 = f32[2048]{0:T(1024)S(1)} collective-permute-done((f32[2048]{0:T(1024)S(1)}, f32[2048]{0:T(1024)S(1)}, u32[]{:S(2)}, u32[]{:S(2)}) %collective-permute-start.12) | collective-permute-done | bytes 8224 | tf_op jit(solution)/shard_map/ppermute | solution.py:543
  291.7 9.2 collective-permute-done.10.refs_1_.refs_3_.refs_4_
  310.1 9.6 fusion.21
  327.9 83.5 %collective-permute-done.16 = bf16[256,2048]{1,0:T(8,128)(2,1)S(1)} collective-permute-done((bf16[256,2048]{1,0:T(8,128)(2,1)S(1)}, bf16[256,2048]{1,0:T(8,128)(2,1)S(1)}, u32[]{:S(2)}, u32[]{:S(2)}) %collective-permute-start.16) | collective-permute-done | bytes 1048608 | tf_op jit(solution)/shard_map/ppermute | solution.py:594
  418.6 6.6 collective-permute-done.18.other_ref
  425.2 38.0 %gated_unit.1 = (bf16[2048,2048]{1,0:T(8,128)(2,1)}, bf16[2048,1408]{1,0:T(8,128)(2,1)}, bf16[2048,1408]{1,0:T(8,128)(2,1)}, bf16[2048,1408]{1,0:T(8,128)(2,1)}, f32[2048,1]{1,0:T(8,128)S(1)}) custom-call(s32[4]{0:T(128)S(1)} %pad_add_fusion.1.spots, bf16[2048,1024]{1,0:T(8,128)(2,1)} %copy-done.67, bf16[2048,1024]{1,0:T(8,128)(2,1)} %collective-permute-done.18.other_ref, ...), custom_call_target="tpu_custom_call" | custom-call | flops 23622320128 | bytes 45621248 | tf_op jit(solution)/shard_map/gated_unit/pallas_call | solution.py:337
  471.4 6.8 collective-permute-done.20.other_ref
  485.0 22.4 %gated_unit_back.1 = (bf16[2048,1408]{1,0:T(8,128)(2,1)S(1)}, bf16[2048,1408]{1,0:T(8,128)(2,1)S(1)}, f32[2048,1]{1,0:T(8,128)S(1)}) custom-call(s32[4]{0:T(128)S(1)} %pad_add_fusion.1.spots, bf16[2048,2048]{1,0:T(8,128)(2,1)} %get-tuple-element.185.dy_ref.left_ref, bf16[2048,1408]{1,0:T(8,128)(2,1)} %get-tuple-element.177.one_ref, ...), custom_call_target="tpu_custom_call" | custom-call | flops 11811160064 | bytes 37232640 | tf_op jit(solution)/shard_map/gated_unit_back/pallas_call | solution.py:374
  513.4 19.8 %fold_half.6 = bf16[2048,1024]{1,0:T(8,128)(2,1)} custom-call(s32[4]{0:T(128)S(1)} %pad_add_fusion.1.spots, bf16[2048,1408]{1,0:T(8,128)(2,1)} %copy-done.53, bf16[2048,1408]{1,0:T(8,128)(2,1)} %copy-done.49, bf16[1024,1408]{1,0:T(8,128)(2,1)S(1)} %copy-done.31, bf16[1024,1408]{1,0:T(8,128)(2,1)} %collective-permute-done.10.refs_1_.refs_3_.refs_4_, ...), custom_call_target="tpu_custom_call" | custom-call | flops 11811160064 | bytes 21495808 | tf_op jit(solution)/shard_map/fold_half/pallas_call | solution.py:435
  537.9 16.5 %gradient_rows.8 = bf16[2048,1408]{1,0:T(8,128)(2,1)S(1)} custom-call(s32[4]{0:T(128)S(1)} %pad_add_fusion.1.spots, bf16[2048,2048]{1,0:T(8,128)(2,1)} %get-tuple-element.185.dy_ref.left_ref, bf16[2048,1408]{1,0:T(8,128)(2,1)S(1)} %copy-done.51), custom_call_target="tpu_custom_call" | custom-call | flops 11811160064 | bytes 17301504 | tf_op jit(solution)/shard_map/gradient_rows/pallas_call | solution.py:470
  564.8 21.9 %fold_half.7 = (bf16[2048,512]{1,0:T(8,128)(2,1)}, f32[2048,512]{1,0:T(8,128)}) custom-call(s32[4]{0:T(128)S(1)} %pad_add_fusion.1.spots, bf16[2048,1408]{1,0:T(8,128)(2,1)} %copy-done.53, bf16[2048,1408]{1,0:T(8,128)(2,1)} %copy-done.49, bf16[2048,1024]{1,0:T(8,128)(2,1)} %collective-permute-done.21.refs_2_, bf16[1024,1408]{1,0:T(8,128)(2,1)S(1)} %copy-done.32, ...), custom_call_target="tpu_custom_call" | custom-call | flops 11811160064 | bytes 27787264 | tf_op jit(solution)/shard_map/fold_half/pallas_call | solution.py:435
  591.0 9.1 gradient_rows.10
  603.8 16.4 %gradient_rows.9 = bf16[2048,1408]{1,0:T(8,128)(2,1)S(1)} custom-call(s32[4]{0:T(128)S(1)} %pad_add_fusion.1.spots, bf16[2048,2048]{1,0:T(8,128)(2,1)} %get-tuple-element.193.left_ref, bf16[2048,1408]{1,0:T(8,128)(2,1)S(1)} %copy-done.54), custom_call_target="tpu_custom_call" | custom-call | flops 11811160064 | bytes 17301504 | tf_op jit(solution)/shard_map/gradient_rows/pallas_call | solution.py:470
  625.4 11.5 fold_half.8
  636.8 14.0 %collective-permute-done.24 = bf16[512,1408]{1,0:T(8,128)(2,1)} collective-permute-done((bf16[512,1408]{1,0:T(8,128)(2,1)}, bf16[512,1408]{1,0:T(8,128)(2,1)}, u32[]{:S(2)}, u32[]{:S(2)}) %collective-permute-start.24) | collective-permute-done | bytes 1441824 | tf_op jit(solution)/shard_map/ppermute | solution.py:543
  651.1 6.5 multiply_reduce_fusion.2
  662.9 11.8 %convolution_convert_fusion.1 = bf16[2048,512]{1,0:T(8,128)(2,1)S(1)} fusion(f32[2048,512]{1,0:T(8,128)} %copy-done.55, f32[2048]{0:T(1024)S(1)} %add_rsqrt_fusion, bf16[2048,1024]{1,0:T(8,128)(2,1)} %collective-permute-done.13, bf16[2048,1024]{1,0:T(8,128)(2,1)} %maximum_select_fusion.2, pred[]{:T(512)S(6)} %eq.50), kind=kOutput, calls=%fused_computation.28 | convolution fusion | flops 4335861760 | bytes 14688257 | tf_op jit(solution)/shard_map/dot_general | solution.py:32
  688.7 13.1 %fold_half.9 = (bf16[2048,512]{1,0:T(8,128)(2,1)S(1)}, f32[2048,512]{1,0:T(8,128)S(1)}) custom-call(s32[4]{0:T(128)S(1)} %pad_add_fusion.1.spots, bf16[2048,1408]{1,0:T(8,128)(2,1)} %get-tuple-element.192.right_ref.refs_0_, bf16[2048,1024]{1,0:T(8,128)(2,1)} %collective-permute-done.27.refs_1_, ...), custom_call_target="tpu_custom_call" | custom-call | flops 5905580032 | bytes 16252928 | tf_op jit(solution)/shard_map/fold_half/pallas_call | solution.py:435
  705.2 29.1 %collective-permute-done.31 = f32[2048]{0:T(1024)S(1)} collective-permute-done((f32[2048]{0:T(1024)S(1)}, f32[2048]{0:T(1024)S(1)}, u32[]{:S(2)}, u32[]{:S(2)}) %collective-permute-start.31) | collective-permute-done | bytes 8224 | tf_op jit(solution)/shard_map/ppermute | solution.py:543
  736.9 7.6 multiply_convert_fusion
  744.5 21.5 %attend_back.1 = (bf16[2048,512]{1,0:T(8,128)(2,1)S(1)}, bf16[2048,512]{1,0:T(8,128)(2,1)S(1)}, bf16[2048,512]{1,0:T(8,128)(2,1)S(1)}) custom-call(f32[4]{0:T(128)S(1)} %copy-done.28, s32[2,2]{1,0:T(2,128)S(1)} %copy-done.26, f32[2048,1024]{1,0:T(8,128)} %get-tuple-element.154.zq_ref.zk_ref, f32[2048,1024]{1,0:T(8,128)} %get-tuple-element.154.zq_ref.zk_ref, ...), custom_call_target="tpu_custom_call" | custom-call | flops 10737418240 | bytes 20971520 | tf_op jit(solution)/shard_map/attend_back/pallas_call | solution.py:119
  779.9 7.9 gradient_rows.11
  787.8 16.6 %collective-permute-done.32 = bf16[512,1408]{1,0:T(8,128)(2,1)} collective-permute-done((bf16[512,1408]{1,0:T(8,128)(2,1)}, bf16[512,1408]{1,0:T(8,128)(2,1)}, u32[]{:S(2)}, u32[]{:S(2)}) %collective-permute-start.32) | collective-permute-done | bytes 1441824 | tf_op jit(solution)/shard_map/ppermute | solution.py:543
  811.5 10.0 gradient_rows.13
  823.1 6.9 collective-permute-done.35
  836.5 7.9 gradient_rows.12
  844.4 13.9 %fold_half.10 = bf16[2048,1024]{1,0:T(8,128)(2,1)S(1)} custom-call(s32[4]{0:T(128)S(1)} %pad_add_fusion.1.spots, bf16[2048,1024]{1,0:T(8,128)(2,1)} %copy-done.5, bf16[2048,1024]{1,0:T(8,128)(2,1)} %pad_maximum_fusion.refs_1_.right_ref, bf16[1024,1024]{1,0:T(8,128)(2,1)S(1)} %copy-done.40, bf16[1024,1024]{1,0:T(8,128)(2,1)S(1)} %copy-done.46, ...), custom_call_target="tpu_custom_call" | custom-call | flops 8589934592 | bytes 16777216 | tf_op jit(solution)/shard_map/fold_half/pallas_call | solution.py:435
  871.3 5.9 multiply_reduce_fusion
  886.6 17.0 %fold_half.11 = (bf16[2048,512]{1,0:T(8,128)(2,1)}, f32[2048,512]{1,0:T(8,128)}) custom-call(s32[4]{0:T(128)S(1)} %pad_add_fusion.1.spots, bf16[2048,1024]{1,0:T(8,128)(2,1)} %copy-done.5, bf16[2048,1024]{1,0:T(8,128)(2,1)} %pad_maximum_fusion.refs_1_.right_ref, bf16[2048,1024]{1,0:T(8,128)(2,1)} %collective-permute-done.38.refs_2_, ...), custom_call_target="tpu_custom_call" | custom-call | flops 8589934592 | bytes 23068672 | tf_op jit(solution)/shard_map/fold_half/pallas_call | solution.py:435
  903.6 7.6 collective-permute-done.42
  913.9 7.9 gradient_rows.15
  931.4 41.2 %collective-permute-done.45 = f32[2048]{0:T(1024)S(1)} collective-permute-done((f32[2048]{0:T(1024)S(1)}, f32[2048]{0:T(1024)S(1)}, u32[]{:S(2)}, u32[]{:S(2)}) %collective-permute-start.45) | collective-permute-done | bytes 8224 | tf_op jit(solution)/shard_map/ppermute | solution.py:543
  974.8 7.2 gradient_rows.14
  991.4 21.5 %collective-permute-done.47 = bf16[2,512,512]{2,1,0:T(8,128)(2,1)S(1)} collective-permute-done((bf16[2,512,512]{2,1,0:T(8,128)(2,1)S(1)}, bf16[2,512,512]{2,1,0:T(8,128)(2,1)S(1)}, u32[]{:S(2)}, u32[]{:S(2)}) %collective-permute-start.47) | collective-permute-done | bytes 1048608 | tf_op jit(solution)/shard_map/ppermute | solution.py:543
  1025.4 7.1 place_quarters.5
  1037.8 10.5 collective-permute-done.50
  1048.3 20.6 %collective-permute-done.49 = bf16[256,2048]{1,0:T(8,128)(2,1)} collective-permute-done((bf16[256,2048]{1,0:T(8,128)(2,1)}, bf16[256,2048]{1,0:T(8,128)(2,1)}, u32[]{:S(2)}, u32[]{:S(2)}) %collective-permute-start.49) | collective-permute-done | bytes 1048608 | tf_op jit(solution)/shard_map/ppermute | solution.py:606
  1089.7 7.1 place_quarters.6
  1096.8 16.5 %collective-permute-done.54 = bf16[256,1024]{1,0:T(8,128)(2,1)} collective-permute-done((bf16[256,1024]{1,0:T(8,128)(2,1)}, bf16[256,1024]{1,0:T(8,128)(2,1)}, u32[]{:S(2)}, u32[]{:S(2)}) %collective-permute-start.54) | collective-permute-done | bytes 524320 | tf_op jit(solution)/shard_map/ppermute | solution.py:543
  1128.5 9.1 collective-permute-done.60
  1137.6 7.3 collective-permute-done.59
  (442 shorter events, 315.5 us)
Async XLA Ops:
  8.0 88.9 %all-gather.7.cloned.1.call-start = ((), (), s32[]{:S(2)}) async-start(), calls=%async_computation.6 | async-start | bytes 2621440 | tf_op jit(solution)/shard_map/all_gather | solution.py:665
  10.3 136.4 %all-gather.9.cloned.1.call-start = ((), (), s32[]{:S(2)}) async-start(), calls=%async_computation.7 | async-start | bytes 2621440 | tf_op jit(solution)/shard_map/all_gather | solution.py:665
  12.5 172.3 %all-gather.11.cloned.1.call-start = ((), (), s32[]{:S(2)}) async-start(), calls=%async_computation.8 | async-start | bytes 1310720 | tf_op jit(solution)/shard_map/all_gather | solution.py:665
  13.7 80.9 %collective-permute-start = (bf16[256,2048]{1,0:T(8,128)(2,1)}, bf16[256,2048]{1,0:T(8,128)(2,1)S(1)}, u32[]{:S(2)}, u32[]{:S(2)}) collective-permute-start(bf16[256,2048]{1,0:T(8,128)(2,1)} %get-tuple-element.314), channel_id=1, source_target_pairs={{0,0},{4,1},{1,2},{5,3},{2,4},{6,5},{3,6},{7,7},{8,8},{12,9},{9,10... | collective-permute-start | bytes 3145736 | tf_op jit(solution)/shard_map/ppermute | solution.py:594
  15.8 78.8 %collective-permute-start.1 = (bf16[256,2048]{1,0:T(8,128)(2,1)S(1)}, bf16[256,2048]{1,0:T(8,128)(2,1)S(1)}, u32[]{:S(2)}, u32[]{:S(2)}) collective-permute-start(bf16[256,2048]{1,0:T(8,128)(2,1)S(1)} %get-tuple-element.315), channel_id=1, source_target_pairs={{1,0},{5,1},{0,2},{4,3},{3,4},{7,5},{2,6},{6,7},{9,8},{13,9},{8,10... | collective-permute-start | bytes 3145736 | tf_op jit(solution)/shard_map/ppermute | solution.py:594
  96.9 43.7 %collective-permute-start.2 = (bf16[512,2048]{1,0:T(8,128)(2,1)}, bf16[512,2048]{1,0:T(8,128)(2,1)}, u32[]{:S(2)}, u32[]{:S(2)}) collective-permute-start(bf16[512,2048]{1,0:T(8,128)(2,1)} %maximum_select_fusion.6), channel_id=1, source_target_pairs={{0,8},{1,9},{2,10},{3,11},{4,12},{5,13},{6,14},{7,15},{8,0},{9,1},... | collective-permute-start | bytes 6291464 | tf_op jit(solution)/shard_map/ppermute | solution.py:543
  98.9 138.9 %all-gather.13.cloned.1.call-start = ((), (), s32[]{:S(2)}) async-start(), calls=%async_computation.9 | async-start | bytes 3604480 | tf_op jit(solution)/shard_map/all_gather | solution.py:665
  99.0 47.7 %collective-permute-start.3 = (bf16[1024,1024]{1,0:T(8,128)(2,1)}, bf16[1024,1024]{1,0:T(8,128)(2,1)S(1)}, u32[]{:S(2)}, u32[]{:S(2)}) collective-permute-start(bf16[1024,1024]{1,0:T(8,128)(2,1)} %all-gather.7.cloned.1.call-done.refs_0_.refs_2_.refs_3_), channel_id=1, source_target_pairs={{0,16},{1,17},{2,18},{3,19},{4,20},{5,21},{6,22},{7,23},{8,24},{9,... | collective-permute-start | bytes 6291464 | tf_op jit(solution)/shard_map/ppermute | solution.py:543
  102.7 189.1 %all-gather.15.cloned.1.call-start = ((), (), s32[]{:S(2)}) async-start(), calls=%async_computation.10 | async-start | bytes 3604480 | tf_op jit(solution)/shard_map/all_gather | solution.py:665
  151.4 47.5 %collective-permute-start.7 = (bf16[1024,1024]{1,0:T(8,128)(2,1)}, bf16[1024,1024]{1,0:T(8,128)(2,1)}, u32[]{:S(2)}, u32[]{:S(2)}) collective-permute-start(bf16[1024,1024]{1,0:T(8,128)(2,1)} %all-gather.9.cloned.1.call-done.refs_0_.refs_4_.refs_5_), channel_id=1, source_target_pairs={{0,16},{1,17},{2,18},{3,19},{4,20},{5,21},{6,22},{7,23},{8,24},{9,... | collective-permute-start | bytes 6291464 | tf_op jit(solution)/shard_map/ppermute | solution.py:543
  157.5 305.7 %all-gather.17.cloned.1.call-start = ((), (), s32[]{:S(2)}) async-start(), calls=%async_computation.11 | async-start | bytes 6488064 | tf_op jit(solution)/shard_map/all_gather | solution.py:669
  198.9 38.8 %collective-permute-start.8 = (bf16[1024,512]{1,0:T(8,128)(2,1)}, bf16[1024,512]{1,0:T(8,128)(2,1)}, u32[]{:S(2)}, u32[]{:S(2)}) collective-permute-start(bf16[1024,512]{1,0:T(8,128)(2,1)} %all-gather.11.cloned.1.call-done), channel_id=1, source_target_pairs={{0,16},{1,17},{2,18},{3,19},{4,20},{5,21},{6,22},{7,23},{8,24},{9,... | collective-permute-start | bytes 3145736 | tf_op jit(solution)/shard_map/ppermute | solution.py:543
  237.8 63.2 %collective-permute-start.10 = (bf16[1024,1408]{1,0:T(8,128)(2,1)}, bf16[1024,1408]{1,0:T(8,128)(2,1)}, u32[]{:S(2)}, u32[]{:S(2)}) collective-permute-start(bf16[1024,1408]{1,0:T(8,128)(2,1)} %all-gather.13.cloned.1.call-done.refs_0_.refs_2_.refs_3_), channel_id=1, source_target_pairs={{0,16},{1,17},{2,18},{3,19},{4,20},{5,21},{6,22},{7,23},{8,24},{9,... | collective-permute-start | bytes 8650760 | tf_op jit(solution)/shard_map/ppermute | solution.py:543
  238.0 46.2 %collective-permute-start.9 = (bf16[2048,512]{1,0:T(8,128)(2,1)}, bf16[2048,512]{1,0:T(8,128)(2,1)S(1)}, u32[]{:S(2)}, u32[]{:S(2)}) collective-permute-start(bf16[2048,512]{1,0:T(8,128)(2,1)} %get-tuple-element.158), channel_id=1, source_target_pairs={{0,8},{1,9},{2,10},{3,11},{4,12},{5,13},{6,14},{7,15},{8,0},{9,1},... | collective-permute-start | bytes 6291464 | tf_op jit(solution)/shard_map/ppermute | solution.py:543
  241.8 42.5 %collective-permute-start.12 = (f32[2048]{0:T(1024)S(1)}, f32[2048]{0:T(1024)S(1)}, u32[]{:S(2)}, u32[]{:S(2)}) collective-permute-start(f32[2048]{0:T(1024)S(1)} %add.256), channel_id=1, source_target_pairs={{0,8},{1,9},{2,10},{3,11},{4,12},{5,13},{6,14},{7,15},{8,0},{9,1},... | collective-permute-start | bytes 24584 | tf_op jit(solution)/shard_map/ppermute | solution.py:543
  305.4 428.9 %reduce-scatter.7.cloned.1.call-start = ((), (), s32[]{:S(2)}) async-start(), calls=%async_computation.12 | async-start | bytes 6488064 | tf_op jit(solution)/shard_map/reduce_scatter | solution.py:709
  309.9 105.4 %collective-permute-start.15 = (bf16[1024,1408]{1,0:T(8,128)(2,1)S(1)}, bf16[1024,1408]{1,0:T(8,128)(2,1)S(1)}, u32[]{:S(2)}, u32[]{:S(2)}) collective-permute-start(bf16[1024,1408]{1,0:T(8,128)(2,1)S(1)} %copy-done.33), channel_id=1, source_target_pairs={{0,16},{1,17},{2,18},{3,19},{4,20},{5,21},{6,22},{7,23},{8,24},{9,... | collective-permute-start | bytes 8650760 | tf_op jit(solution)/shard_map/ppermute | solution.py:543
  319.8 94.1 %collective-permute-start.14 = (bf16[2048,512]{1,0:T(8,128)(2,1)}, bf16[2048,512]{1,0:T(8,128)(2,1)S(1)}, u32[]{:S(2)}, u32[]{:S(2)}) collective-permute-start(bf16[2048,512]{1,0:T(8,128)(2,1)} %get-tuple-element.320), channel_id=1, source_target_pairs={{0,8},{1,9},{2,10},{3,11},{4,12},{5,13},{6,14},{7,15},{8,0},{9,1},... | collective-permute-start | bytes 6291464 | tf_op jit(solution)/shard_map/ppermute | solution.py:543
  322.8 88.7 %collective-permute-start.16 = (bf16[256,2048]{1,0:T(8,128)(2,1)S(1)}, bf16[256,2048]{1,0:T(8,128)(2,1)S(1)}, u32[]{:S(2)}, u32[]{:S(2)}) collective-permute-start(bf16[256,2048]{1,0:T(8,128)(2,1)S(1)} %get-tuple-element.310), channel_id=1, source_target_pairs={{0,0},{4,1},{1,2},{5,3},{2,4},{6,5},{3,6},{7,7},{8,8},{12,9},{9,10... | collective-permute-start | bytes 3145736 | tf_op jit(solution)/shard_map/ppermute | solution.py:594
  327.9 83.6 %collective-permute-start.17 = (bf16[256,2048]{1,0:T(8,128)(2,1)S(1)}, bf16[256,2048]{1,0:T(8,128)(2,1)S(1)}, u32[]{:S(2)}, u32[]{:S(2)}) collective-permute-start(bf16[256,2048]{1,0:T(8,128)(2,1)S(1)} %get-tuple-element.311), channel_id=1, source_target_pairs={{1,0},{5,1},{0,2},{4,3},{3,4},{7,5},{2,6},{6,7},{9,8},{13,9},{8,10... | collective-permute-start | bytes 3145736 | tf_op jit(solution)/shard_map/ppermute | solution.py:594
  418.3 47.5 %collective-permute-start.19 = (bf16[512,2048]{1,0:T(8,128)(2,1)}, bf16[512,2048]{1,0:T(8,128)(2,1)}, u32[]{:S(2)}, u32[]{:S(2)}) collective-permute-start(bf16[512,2048]{1,0:T(8,128)(2,1)} %maximum_select_fusion.8), channel_id=1, source_target_pairs={{0,8},{1,9},{2,10},{3,11},{4,12},{5,13},{6,14},{7,15},{8,0},{9,1},... | collective-permute-start | bytes 6291464 | tf_op jit(solution)/shard_map/ppermute | solution.py:543
  556.8 324.9 %reduce-scatter.9.cloned.1.call-start = ((), (), s32[]{:S(2)}) async-start(), calls=%async_computation.13 | async-start | bytes 6488064 | tf_op jit(solution)/shard_map/reduce_scatter | solution.py:709
  586.7 50.1 %collective-permute-start.25 = (f32[2048]{0:T(1024)S(1)}, f32[2048]{0:T(1024)S(1)}, u32[]{:S(2)}, u32[]{:S(2)}) collective-permute-start(f32[2048]{0:T(1024)S(1)} %add.261), channel_id=1, source_target_pairs={{0,8},{1,9},{2,10},{3,11},{4,12},{5,13},{6,14},{7,15},{8,0},{9,1},... | collective-permute-start | bytes 24584 | tf_op jit(solution)/shard_map/ppermute | solution.py:543
  587.5 63.4 %collective-permute-start.23 = (bf16[2048,512]{1,0:T(8,128)(2,1)}, bf16[2048,512]{1,0:T(8,128)(2,1)}, u32[]{:S(2)}, u32[]{:S(2)}) collective-permute-start(bf16[2048,512]{1,0:T(8,128)(2,1)} %get-tuple-element.191), channel_id=1, source_target_pairs={{0,8},{1,9},{2,10},{3,11},{4,12},{5,13},{6,14},{7,15},{8,0},{9,1},... | collective-permute-start | bytes 6291464 | tf_op jit(solution)/shard_map/ppermute | solution.py:543
  601.9 48.9 %collective-permute-start.24 = (bf16[512,1408]{1,0:T(8,128)(2,1)}, bf16[512,1408]{1,0:T(8,128)(2,1)}, u32[]{:S(2)}, u32[]{:S(2)}) collective-permute-start(bf16[512,1408]{1,0:T(8,128)(2,1)} %get-tuple-element.293), channel_id=1, source_target_pairs={{0,16},{1,17},{2,18},{3,19},{4,20},{5,21},{6,22},{7,23},{8,24},{9,... | collective-permute-start | bytes 4325384 | tf_op jit(solution)/shard_map/ppermute | solution.py:543
  650.8 332.5 %reduce-scatter.13.cloned.1.call-start = ((), (), s32[]{:S(2)}) async-start(), calls=%async_computation.15 | async-start | bytes 1310720 | tf_op jit(solution)/shard_map/reduce_scatter | solution.py:703
  687.2 47.1 %collective-permute-start.29 = (bf16[2048,512]{1,0:T(8,128)(2,1)}, bf16[2048,512]{1,0:T(8,128)(2,1)}, u32[]{:S(2)}, u32[]{:S(2)}) collective-permute-start(bf16[2048,512]{1,0:T(8,128)(2,1)} %dynamic-slice_convert_fusion), channel_id=1, source_target_pairs={{0,8},{1,9},{2,10},{3,11},{4,12},{5,13},{6,14},{7,15},{8,0},{9,1},... | collective-permute-start | bytes 6291464 | tf_op jit(solution)/shard_map/ppermute | solution.py:543
  687.9 46.4 %collective-permute-start.30 = (bf16[1024,512]{1,0:T(8,128)(2,1)}, bf16[1024,512]{1,0:T(8,128)(2,1)S(1)}, u32[]{:S(2)}, u32[]{:S(2)}) collective-permute-start(bf16[1024,512]{1,0:T(8,128)(2,1)} %get-tuple-element.209), channel_id=1, source_target_pairs={{0,16},{1,17},{2,18},{3,19},{4,20},{5,21},{6,22},{7,23},{8,24},{9,... | collective-permute-start | bytes 3145736 | tf_op jit(solution)/shard_map/ppermute | solution.py:543
  687.9 46.4 %collective-permute-start.31 = (f32[2048]{0:T(1024)S(1)}, f32[2048]{0:T(1024)S(1)}, u32[]{:S(2)}, u32[]{:S(2)}) collective-permute-start(f32[2048]{0:T(1024)S(1)} %add.275), channel_id=1, source_target_pairs={{0,8},{1,9},{2,10},{3,11},{4,12},{5,13},{6,14},{7,15},{8,0},{9,1},... | collective-permute-start | bytes 24584 | tf_op jit(solution)/shard_map/ppermute | solution.py:543
  734.4 53.4 %collective-permute-start.34 = (bf16[256,1408]{1,0:T(8,128)(2,1)}, bf16[256,1408]{1,0:T(8,128)(2,1)}, u32[]{:S(2)}, u32[]{:S(2)}) collective-permute-start(bf16[256,1408]{1,0:T(8,128)(2,1)} %reduce-scatter.7.cloned.1.call-done), channel_id=1, source_target_pairs={{0,16},{1,17},{2,18},{3,19},{4,20},{5,21},{6,22},{7,23},{8,24},{9,... | collective-permute-start | bytes 2162696 | tf_op jit(solution)/shard_map/ppermute | solution.py:543
  734.4 69.9 %collective-permute-start.32 = (bf16[512,1408]{1,0:T(8,128)(2,1)}, bf16[512,1408]{1,0:T(8,128)(2,1)}, u32[]{:S(2)}, u32[]{:S(2)}) collective-permute-start(bf16[512,1408]{1,0:T(8,128)(2,1)} %get-tuple-element.217), channel_id=1, source_target_pairs={{0,16},{1,17},{2,18},{3,19},{4,20},{5,21},{6,22},{7,23},{8,24},{9,... | collective-permute-start | bytes 4325384 | tf_op jit(solution)/shard_map/ppermute | solution.py:543
  735.9 68.5 %collective-permute-start.33 = (bf16[2048,512]{1,0:T(8,128)(2,1)}, bf16[2048,512]{1,0:T(8,128)(2,1)}, u32[]{:S(2)}, u32[]{:S(2)}) collective-permute-start(bf16[2048,512]{1,0:T(8,128)(2,1)} %copy-done.48), channel_id=1, source_target_pairs={{0,8},{1,9},{2,10},{3,11},{4,12},{5,13},{6,14},{7,15},{8,0},{9,1},... | collective-permute-start | bytes 6291464 | tf_op jit(solution)/shard_map/ppermute | solution.py:543
  771.3 212.1 %reduce-scatter.11.cloned.1.call-start = ((), (), s32[]{:S(2)}) async-start(), calls=%async_computation.14 | async-start | bytes 3604480 | tf_op jit(solution)/shard_map/reduce_scatter | solution.py:703
  822.7 39.7 %collective-permute-start.37 = (bf16[512,1024]{1,0:T(8,128)(2,1)S(1)}, bf16[512,1024]{1,0:T(8,128)(2,1)}, u32[]{:S(2)}, u32[]{:S(2)}) collective-permute-start(bf16[512,1024]{1,0:T(8,128)(2,1)S(1)} %get-tuple-element.303), channel_id=1, source_target_pairs={{0,16},{1,17},{2,18},{3,19},{4,20},{5,21},{6,22},{7,23},{8,24},{9,... | collective-permute-start | bytes 3145736 | tf_op jit(solution)/shard_map/ppermute | solution.py:543
  862.5 161.2 %reduce-scatter.15.cloned.1.call-start = ((), (), s32[]{:S(2)}) async-start(), calls=%async_computation.16 | async-start | bytes 2621440 | tf_op jit(solution)/shard_map/reduce_scatter | solution.py:703
  869.9 41.4 %collective-permute-start.41 = (bf16[512,1408]{1,0:T(8,128)(2,1)}, bf16[512,1408]{1,0:T(8,128)(2,1)}, u32[]{:S(2)}, u32[]{:S(2)}) collective-permute-start(bf16[512,1408]{1,0:T(8,128)(2,1)} %maximum_select_fusion.16), channel_id=1, source_target_pairs={{0,8},{1,9},{2,10},{3,11},{4,12},{5,13},{6,14},{7,15},{8,0},{9,1},... | collective-permute-start | bytes 4325384 | tf_op jit(solution)/shard_map/ppermute | solution.py:543
  871.2 40.0 %collective-permute-start.39 = (bf16[512,1024]{1,0:T(8,128)(2,1)S(1)}, bf16[512,1024]{1,0:T(8,128)(2,1)}, u32[]{:S(2)}, u32[]{:S(2)}) collective-permute-start(bf16[512,1024]{1,0:T(8,128)(2,1)S(1)} %copy-done.78), channel_id=1, source_target_pairs={{0,16},{1,17},{2,18},{3,19},{4,20},{5,21},{6,22},{7,23},{8,24},{9,... | collective-permute-start | bytes 3145736 | tf_op jit(solution)/shard_map/ppermute | solution.py:543
  921.8 147.1 %reduce-scatter.17.cloned.1.call-start = ((), (), s32[]{:S(2)}) async-start(), calls=%async_computation.17 | async-start | bytes 2621440 | tf_op jit(solution)/shard_map/reduce_scatter | solution.py:703
  923.8 48.8 %collective-permute-start.46 = (bf16[512,2816]{1,0:T(8,128)(2,1)S(1)}, bf16[512,2816]{1,0:T(8,128)(2,1)}, u32[]{:S(2)}, u32[]{:S(2)}) collective-permute-start(bf16[512,2816]{1,0:T(8,128)(2,1)S(1)} %pad_maximum_fusion.2.refs_0_.refs_1_), channel_id=1, source_target_pairs={{0,4},{1,5},{2,6},{3,7},{4,0},{5,1},{6,2},{7,3},{8,12},{9,13},{10,... | collective-permute-start | bytes 8650760 | tf_op jit(solution)/shard_map/ppermute | solution.py:543
  924.9 47.7 %collective-permute-start.43 = (bf16[2048,512]{1,0:T(8,128)(2,1)}, bf16[2048,512]{1,0:T(8,128)(2,1)}, u32[]{:S(2)}, u32[]{:S(2)}) collective-permute-start(bf16[2048,512]{1,0:T(8,128)(2,1)} %get-tuple-element.237), channel_id=1, source_target_pairs={{0,8},{1,9},{2,10},{3,11},{4,12},{5,13},{6,14},{7,15},{8,0},{9,1},... | collective-permute-start | bytes 6291464 | tf_op jit(solution)/shard_map/ppermute | solution.py:543
  925.0 47.6 %collective-permute-start.44 = (bf16[1024,1024]{1,0:T(8,128)(2,1)}, bf16[1024,1024]{1,0:T(8,128)(2,1)}, u32[]{:S(2)}, u32[]{:S(2)}) collective-permute-start(bf16[1024,1024]{1,0:T(8,128)(2,1)} %gradient_rows.12), channel_id=1, source_target_pairs={{0,16},{1,17},{2,18},{3,19},{4,20},{5,21},{6,22},{7,23},{8,24},{9,... | collective-permute-start | bytes 6291464 | tf_op jit(solution)/shard_map/ppermute | solution.py:543
  928.4 44.3 %collective-permute-start.45 = (f32[2048]{0:T(1024)S(1)}, f32[2048]{0:T(1024)S(1)}, u32[]{:S(2)}, u32[]{:S(2)}) collective-permute-start(f32[2048]{0:T(1024)S(1)} %add.285), channel_id=1, source_target_pairs={{0,8},{1,9},{2,10},{3,11},{4,12},{5,13},{6,14},{7,15},{8,0},{9,1},... | collective-permute-start | bytes 24584 | tf_op jit(solution)/shard_map/ppermute | solution.py:543
  1018.4 50.5 %collective-permute-start.51 = (bf16[512,1408]{1,0:T(8,128)(2,1)}, bf16[512,1408]{1,0:T(8,128)(2,1)}, u32[]{:S(2)}, u32[]{:S(2)}) collective-permute-start(bf16[512,1408]{1,0:T(8,128)(2,1)} %maximum_select_fusion.17), channel_id=1, source_target_pairs={{0,8},{1,9},{2,10},{3,11},{4,12},{5,13},{6,14},{7,15},{8,0},{9,1},... | collective-permute-start | bytes 4325384 | tf_op jit(solution)/shard_map/ppermute | solution.py:543
  1021.6 47.3 %collective-permute-start.49 = (bf16[256,2048]{1,0:T(8,128)(2,1)}, bf16[256,2048]{1,0:T(8,128)(2,1)}, u32[]{:S(2)}, u32[]{:S(2)}) collective-permute-start(bf16[256,2048]{1,0:T(8,128)(2,1)} %get-tuple-element.297), channel_id=1, source_target_pairs={{0,0},{1,4},{2,1},{3,5},{4,2},{5,6},{6,3},{7,7},{8,8},{9,12},{10,9... | collective-permute-start | bytes 3145736 | tf_op jit(solution)/shard_map/ppermute | solution.py:606
  1024.8 44.1 %collective-permute-start.53 = (bf16[256,1536]{1,0:T(8,128)(2,1)S(1)}, bf16[256,1536]{1,0:T(8,128)(2,1)}, u32[]{:S(2)}, u32[]{:S(2)}) collective-permute-start(bf16[256,1536]{1,0:T(8,128)(2,1)S(1)} %pad_maximum_fusion.7), channel_id=1, source_target_pairs={{0,8},{1,9},{2,10},{3,11},{4,12},{5,13},{6,14},{7,15},{8,0},{9,1},... | collective-permute-start | bytes 2359304 | tf_op jit(solution)/shard_map/ppermute | solution.py:543
  1025.4 43.5 %collective-permute-start.52 = (bf16[256,1408]{1,0:T(8,128)(2,1)}, bf16[256,1408]{1,0:T(8,128)(2,1)}, u32[]{:S(2)}, u32[]{:S(2)}) collective-permute-start(bf16[256,1408]{1,0:T(8,128)(2,1)} %reduce-scatter.11.cloned.1.call-done), channel_id=1, source_target_pairs={{0,16},{1,17},{2,18},{3,19},{4,20},{5,21},{6,22},{7,23},{8,24},{9,... | collective-permute-start | bytes 2162696 | tf_op jit(solution)/shard_map/ppermute | solution.py:543
  1073.9 39.4 %collective-permute-start.55 = (bf16[512,1408]{1,0:T(8,128)(2,1)}, bf16[512,1408]{1,0:T(8,128)(2,1)}, u32[]{:S(2)}, u32[]{:S(2)}) collective-permute-start(bf16[512,1408]{1,0:T(8,128)(2,1)} %maximum_select_fusion.18), channel_id=1, source_target_pairs={{0,8},{1,9},{2,10},{3,11},{4,12},{5,13},{6,14},{7,15},{8,0},{9,1},... | collective-permute-start | bytes 4325384 | tf_op jit(solution)/shard_map/ppermute | solution.py:543
  1077.7 35.6 %collective-permute-start.57 = (bf16[256,2048]{1,0:T(8,128)(2,1)}, bf16[256,2048]{1,0:T(8,128)(2,1)}, u32[]{:S(2)}, u32[]{:S(2)}) collective-permute-start(bf16[256,2048]{1,0:T(8,128)(2,1)} %get-tuple-element.295), channel_id=1, source_target_pairs={{0,0},{1,4},{2,1},{3,5},{4,2},{5,6},{6,3},{7,7},{8,8},{9,12},{10,9... | collective-permute-start | bytes 3145736 | tf_op jit(solution)/shard_map/ppermute | solution.py:606
  (117 other events, 2020.4 us)
Sparse Core Ops, SparseCore 0:
  11.0 82.8 all-gather.6
  96.1 46.1 all-gather.8
  144.4 27.5 all-gather.10
  173.9 57.9 all-gather.12
  233.9 57.8 all-gather.14
Sparse Core Ops, SparseCore 1:
  305.5 125.1 all-gather.16
  556.9 123.6 reduce-scatter.6
  684.1 133.2 reduce-scatter.8
  819.6 25.9 reduce-scatter.12
  862.6 58.0 reduce-scatter.10
  923.6 42.7 reduce-scatter.14
  983.5 44.2 reduce-scatter.16

commit v13 on v11

--- a/solution.py
+++ b/solution.py
@@ -861,78 +861,76 @@
     t_qk = away(hidden_one, d_qk)
     d_qk, d_vg, t_qk, lower, result = tie(d_qk, d_vg, t_qk, lower, result)
 
-    upper_qk, lower_qk = in_two(t_qk)
-    upper_qk = sent_a(upper_qk)
+    qk_a, qk_b = in_two(t_qk)
+    qk_a = sent_a(qk_a)
     f_two = gradient_rows(spots, spread, 0, hidden_two, d_two, stacked(upper, lower))
-    output = to_runs((middle + (result_mine + result.astype(F32))).astype(LOW))
+    output, out_b = away_b((middle + (result_mine + result.astype(F32))).astype(LOW))
+    f_two, qk_a, qk_b, out_b, d_qk, d_vg = tie(f_two, qk_a, qk_b, out_b, d_qk, d_vg)
+
+    f_two = scattered(f_two)
+    qk_b = sent_a(qk_b)
+    output, out_c = away_c(output, out_b)
     t_vg = away(hidden_one, d_vg)
     sent = fold_half(spots, [d_qk, d_vg], [w_qk, w_vg])
-    sent, t_vg, d_qk, d_vg, f_two, output, upper_qk, lower_qk = tie(
-        sent, t_vg, d_qk, d_vg, f_two, output, upper_qk, lower_qk
-    )
-
-    f_two = scattered(f_two)
-    lower_qk = sent_a(lower_qk)
+    sent, t_vg, d_qk, d_vg, out_c, qk_b = tie(sent, t_vg, d_qk, d_vg, out_c, qk_b)
+
+    arrived = swap_c(sent)
+    vg_a, vg_b = in_two(t_vg)
+    vg_a = sent_a(vg_a)
+    f_qk = gradient_rows(spots, spread, 0, hidden_one, d_qk, stacked(qk_a, qk_b))
+    lean_x = jnp.sum(z_qk * d_qk.astype(F32), axis=-1) + jnp.sum(z_vg * d_vg.astype(F32), axis=-1)
+    arrived, vg_a, vg_b, f_qk, lean_x = tie(arrived, vg_a, vg_b, f_qk, lean_x)
+
+    f_qk = scattered(f_qk)
+    vg_b = sent_a(vg_b)
     x_down = swap_b(y_down)
-    y_one = over_spread(f_one)
-    arrived = swap_c(sent)
-    lean_x = jnp.sum(z_qk * d_qk.astype(F32), axis=-1) + jnp.sum(z_vg * d_vg.astype(F32), axis=-1)
+    lean_x = lean_x + swap_c(lean_x)
     sent, mine = fold_half(spots, [d_qk, d_vg], [w_qk, w_vg], arrived)
-    lean_x = lean_x + swap_c(lean_x)
-    sent, mine, lower_qk, t_vg, lean_x, x_down, y_one = tie(
-        sent, mine, lower_qk, t_vg, lean_x, x_down, y_one
-    )
+    sent, mine, vg_b, lean_x, x_down, d_vg, f_one = tie(sent, mine, vg_b, lean_x, x_down, d_vg, f_one)
 
     crossed = swap_b(sent)
     lean_b = swap_b(lean_x)
-    r_vg = sent_a(t_vg)
-    f_qk = scattered(gradient_rows(spots, spread, 0, hidden_one, d_qk, stacked(upper_qk, lower_qk)))
+    f_vg = scattered(gradient_rows(spots, spread, 0, hidden_one, d_vg, stacked(vg_a, vg_b)))
+    y_one = over_spread(f_one)
     four_down = spread_c(joined(y_down, x_down))
-    crossed, d_vg, r_vg, lean_b, four_down = tie(crossed, d_vg, r_vg, lean_b, four_down)
-
-    f_vg = gradient_rows(spots, spread, 0, hidden_one, d_vg, r_vg)
-    f_vg, crossed, f_two, f_out = tie(f_vg, crossed, f_two, f_out)
-
-    f_vg = scattered(f_vg)
+    crossed, lean_b, y_one, four_down, f_two, f_out = tie(crossed, lean_b, y_one, four_down, f_two, f_out)
+
     d_hidden = mine + crossed.astype(F32)
     x_normed = x_own.astype(F32) * x_scale
     lean = (lean_x + lean_b)[:, None] / width
     input_grad = to_runs((d_middle + x_scale * (d_hidden - x_normed * lean)).astype(LOW))
-    output = send_back(output)
+    output = send_back(ordered(c, output, out_c, 1))
     y_one = by_spread([f_one, *y_one])
     x_one = swap_b(y_one)
     f_oqk = joined(f_out, f_qk)
     x_oqk = swap_b(f_oqk)
     y_two = over_spread(f_two)
+    y_vg = over_spread(f_vg)
     units = f_one.shape[1]
     [g_down] = place_quarters(spots, four_down, (0, units))
-    input_grad, output, x_one, y_two, x_oqk, f_vg, g_down = tie(
-        input_grad, output, x_one, y_two, x_oqk, f_vg, g_down
+    input_grad, output, x_one, y_two, x_oqk, y_vg, g_down = tie(
+        input_grad, output, x_one, y_two, x_oqk, y_vg, g_down
     )
 
-    x_vg = swap_b(f_vg)
-    four_one = spread_c(joined(y_one, x_one))
-    x_vg, four_one = tie(x_vg, four_one)
-
-    f_vg = joined(f_vg, x_vg)
-    y_vg = over_spread(f_vg)
+    y_vg = by_spread([f_vg, *y_vg])
+    x_vg = swap_b(y_vg)
     y_two = by_spread([f_two, *y_two])
     x_two = swap_b(y_two)
     f_oqk = joined(f_oqk, x_oqk)
     y_oqk = over_spread(f_oqk)
     input_grad = send_back(input_grad)
-    [g_one] = place_quarters(spots, four_one, (0, units))
-    y_vg, x_two, y_oqk, input_grad, g_one = tie(y_vg, x_two, y_oqk, input_grad, g_one)
-
-    four_vg = spread_c(by_spread([f_vg, *y_vg]))
+    output = as_batches(output)
+    [g_one] = place_quarters(spots, spread_c(joined(y_one, x_one)), (0, units))
+    x_vg, x_two, y_oqk, input_grad, output, g_one = tie(x_vg, x_two, y_oqk, input_grad, output, g_one)
+
+    four_vg = spread_c(joined(y_vg, x_vg))
     four_two = spread_c(joined(y_two, x_two))
     four_oqk = spread_c(by_spread([f_oqk, *y_oqk]))
     g_query, g_key = place_quarters(spots, four_oqk, (own, own), (2 * own, own))
     g_value, g_gate = place_quarters(spots, four_vg, (0, own), (own, own))
     [g_two] = place_quarters(spots, four_two, (0, units))
     g_out = features_in_order(four_oqk, 0, own)
-    output, input_grad = as_batches(output), as_batches(input_grad)
-    return output, input_grad, g_query, g_key, g_value, g_gate, g_out, g_one, g_two, g_down
+    return output, as_batches(input_grad), g_query, g_key, g_value, g_gate, g_out, g_one, g_two, g_down
 
 
 def solution(mesh):

time: 1140 us -> 1120 us (0.982)
  waiting for transfers between devices: 450 us -> 424 us
    ppermute x4, waiting for transfers between devices: 65.2 us -> 40.9 us  [send_back(): lax.ppermute(lax.dynamic_index_in_dim(slots, (batch_of(place) + p) % 2, 0...]
    unnamed x201 -> x202, local copies, waits for them, and re-layouts: 73.3 us -> 77.1 us
    ppermute x56 -> x57, starting transfers between devices: 55.2 us -> 53.4 us  [move(): return lax.ppermute(x, AXES, pairs)]
    ppermute x56 -> x57, waiting for transfers between devices: 258 us -> 259 us  [move(): return lax.ppermute(x, AXES, pairs)]
  transfers between devices with their start and end apart: 76 -> 77, of which waited for: 30 -> 28; matrix products, arithmetic and copies ran while one was open for 15% -> 16% of each run, Pallas kernels for 30% -> 30%
where the time goes in v13:
time: 1120 us; the launch traced here: 1110 us
  waiting for transfers between devices  424 us (38%)
  Pallas kernels  341 us (30%)
  local copies, waits for them, and re-layouts  117 us (10%)
  other arithmetic  112 us (10%)
  starting transfers between devices  71.9 us (6%)
  matrix products  31.2 us (3%)
  between operations  17 us (2%)
    ppermute x57, waiting for transfers between devices, move(): return lax.ppermute(x, AXES, pairs)  259 us
    ppermute x4, waiting for transfers between devices, bring(): lax.ppermute(lax.dynamic_index_in_dim(x, (place + p) % 2, 0, False), AXES...  119 us
    pallas_call x6, Pallas kernels, fold_half(): pl.pallas_call(functools.partial(fold_kernel, len(values), arrived is not...  99.4 us
    pallas_call x8, Pallas kernels, gradient_rows(): pl.pallas_call(gradient_kernel, out_shape=out, grid_spec=pltpu.PrefetchSc...  81.5 us
    unnamed x202, local copies, waits for them, and re-layouts  77.1 us
    select_n x23, other arithmetic, ordered(): jnp.where(index == 0, jnp.concatenate([mine, other], axis), jnp.concatena...  56.1 us
    ppermute x57, starting transfers between devices, move(): return lax.ppermute(x, AXES, pairs)  53.4 us
    ppermute x4, waiting for transfers between devices, send_back(): lax.ppermute(lax.dynamic_index_in_dim(slots, (batch_of(place) + p) % 2, 0...  40.9 us
  transfers between devices with their start and end apart: 77, of which 28 were waited for; matrix products, arithmetic and copies ran while one was open for 16% of the time, Pallas kernels for 30%

profile of v13, /device:TPU:17, one launch (start us, length us, event | category | flops | bytes accessed | tf_op | source)
XLA Modules:
  0.0 1113.3 jit_solution(10983348819029524949)
XLA Ops:
  18.8 75.9 %collective-permute-done = bf16[256,2048]{1,0:T(8,128)(2,1)S(1)} collective-permute-done((bf16[256,2048]{1,0:T(8,128)(2,1)}, bf16[256,2048]{1,0:T(8,128)(2,1)S(1)}, u32[]{:S(2)}, u32[]{:S(2)}) %collective-permute-start) | collective-permute-done | bytes 1048608 | tf_op jit(solution)/shard_map/ppermute | solution.py:594
  102.9 37.9 %collective-permute-done.2 = bf16[512,2048]{1,0:T(8,128)(2,1)} collective-permute-done((bf16[512,2048]{1,0:T(8,128)(2,1)}, bf16[512,2048]{1,0:T(8,128)(2,1)}, u32[]{:S(2)}, u32[]{:S(2)}) %collective-permute-start.2) | collective-permute-done | bytes 2097184 | tf_op jit(solution)/shard_map/ppermute | solution.py:543
  140.8 6.1 maximum_select_fusion.1.own_ref
  165.5 18.8 %enter.2 = (bf16[2048,2048]{1,0:T(8,128)(2,1)}, f32[2048,1024]{1,0:T(8,128)}, f32[2048,1]{1,0:T(8,128)S(1)}, bf16[2048,512]{1,0:T(8,128)(2,1)S(1)}) custom-call(s32[4]{0:T(128)S(1)} %pad_add_fusion.1.spots, bf16[1024,2048]{1,0:T(8,128)(2,1)S(1)} %copy-done.18, bf16[1024,2048]{1,0:T(8,128)(2,1)} %collective-permute-done.4.other_ref, ...), custom_call_target="tpu_custom_call" | custom-call | flops 8589934592 | bytes 31465472 | tf_op jit(solution)/shard_map/enter/pallas_call | solution.py:244
  184.3 14.9 %collective-permute-done.5.refs_1_.refs_5_.refs_6_ = bf16[1024,1024]{1,0:T(8,128)(2,1)} collective-permute-done((bf16[1024,1024]{1,0:T(8,128)(2,1)}, bf16[1024,1024]{1,0:T(8,128)(2,1)}, u32[]{:S(2)}, u32[]{:S(2)}) %collective-permute-start.5) | collective-permute-done | bytes 2097184 | tf_op jit(solution)/shard_map/ppermute | solution.py:543
  202.0 14.2 %project.1.zv_ref = f32[2048,1024]{1,0:T(8,128)S(1)} custom-call(s32[4]{0:T(128)S(1)} %pad_add_fusion.1.spots, bf16[2048,2048]{1,0:T(8,128)(2,1)} %get-tuple-element.155.h_ref.left_ref, bf16[1024,1024]{1,0:T(8,128)(2,1)S(1)} %copy-done.42, bf16[1024,1024]{1,0:T(8,128)(2,1)} %collective-permute-done.5.refs_1_.refs_5_.refs_6_), custom_call_target="tpu_custom_call" | custom-call | flops 8589934592 | bytes 20971520 | tf_op jit(solution)/shard_map/project/pallas_call | solution.py:275
  219.7 12.3 %attend.1 = f32[2048,512]{1,0:T(8,128)S(1)} custom-call(f32[4]{0:T(128)S(1)} %dynamic_slice.129.rates, s32[2,2]{1,0:T(2,128)S(1)} %pad_add_fusion.ends, f32[2048,1024]{1,0:T(8,128)S(1)} %copy-done, f32[2048,1024]{1,0:T(8,128)S(1)} %copy-done, f32[2048,1024]{1,0:T(8,128)} %copy-done.1), custom_call_target="tpu_custom_call" | custom-call | flops 4294967296 | bytes 16777216 | tf_op jit(solution)/shard_map/attend/pallas_call | solution.py:98
  242.2 42.2 %collective-permute-done.12 = f32[2048]{0:T(1024)S(1)} collective-permute-done((f32[2048]{0:T(1024)S(1)}, f32[2048]{0:T(1024)S(1)}, u32[]{:S(2)}, u32[]{:S(2)}) %collective-permute-start.12) | collective-permute-done | bytes 8224 | tf_op jit(solution)/shard_map/ppermute | solution.py:543
  284.4 5.0 maximum_select_fusion.2
  291.8 9.4 collective-permute-done.10.refs_1_.refs_3_.refs_4_
  310.4 9.9 fusion.21
  323.2 5.0 collective-permute-start.16
  328.3 43.1 %collective-permute-done.16 = bf16[256,2048]{1,0:T(8,128)(2,1)S(1)} collective-permute-done((bf16[256,2048]{1,0:T(8,128)(2,1)S(1)}, bf16[256,2048]{1,0:T(8,128)(2,1)S(1)}, u32[]{:S(2)}, u32[]{:S(2)}) %collective-permute-start.16) | collective-permute-done | bytes 1048608 | tf_op jit(solution)/shard_map/ppermute | solution.py:594
  390.6 38.3 %gated_unit.1 = (bf16[2048,2048]{1,0:T(8,128)(2,1)}, bf16[2048,1408]{1,0:T(8,128)(2,1)}, bf16[2048,1408]{1,0:T(8,128)(2,1)}, bf16[2048,1408]{1,0:T(8,128)(2,1)}, f32[2048,1]{1,0:T(8,128)S(1)}) custom-call(s32[4]{0:T(128)S(1)} %pad_add_fusion.1.spots, bf16[2048,1024]{1,0:T(8,128)(2,1)} %maximum_select_fusion.3.own_ref, ...), custom_call_target="tpu_custom_call" | custom-call | flops 23622320128 | bytes 45621248 | tf_op jit(solution)/shard_map/gated_unit/pallas_call | solution.py:337
  438.0 6.8 collective-permute-done.20.other_ref
  444.8 5.3 enter.3
  451.5 16.7 %gradient_rows.8 = bf16[2048,1408]{1,0:T(8,128)(2,1)S(1)} custom-call(s32[4]{0:T(128)S(1)} %pad_add_fusion.1.spots, bf16[2048,2048]{1,0:T(8,128)(2,1)} %get-tuple-element.177.left_ref.dy_ref, bf16[2048,1408]{1,0:T(8,128)(2,1)S(1)} %bitcast.63), custom_call_target="tpu_custom_call" | custom-call | flops 11811160064 | bytes 17301504 | tf_op jit(solution)/shard_map/gradient_rows/pallas_call | solution.py:470
  472.9 22.4 %gated_unit_back.1 = (bf16[2048,1408]{1,0:T(8,128)(2,1)S(1)}, bf16[2048,1408]{1,0:T(8,128)(2,1)S(1)}, f32[2048,1]{1,0:T(8,128)S(1)}) custom-call(s32[4]{0:T(128)S(1)} %pad_add_fusion.1.spots, bf16[2048,2048]{1,0:T(8,128)(2,1)} %get-tuple-element.177.left_ref.dy_ref, bf16[2048,1408]{1,0:T(8,128)(2,1)} %get-tuple-element.181.one_ref, ...), custom_call_target="tpu_custom_call" | custom-call | flops 11811160064 | bytes 37232640 | tf_op jit(solution)/shard_map/gated_unit_back/pallas_call | solution.py:374
  501.2 19.8 %fold_half.6 = bf16[2048,1024]{1,0:T(8,128)(2,1)} custom-call(s32[4]{0:T(128)S(1)} %pad_add_fusion.1.spots, bf16[2048,1408]{1,0:T(8,128)(2,1)} %copy-done.53, bf16[2048,1408]{1,0:T(8,128)(2,1)} %copy-done.49, bf16[1024,1408]{1,0:T(8,128)(2,1)S(1)} %copy-done.31, bf16[1024,1408]{1,0:T(8,128)(2,1)} %collective-permute-done.10.refs_1_.refs_3_.refs_4_, ...), custom_call_target="tpu_custom_call" | custom-call | flops 11811160064 | bytes 21495808 | tf_op jit(solution)/shard_map/fold_half/pallas_call | solution.py:435
  529.9 9.5 gradient_rows.9
  539.5 21.9 %fold_half.7 = (bf16[2048,512]{1,0:T(8,128)(2,1)}, f32[2048,512]{1,0:T(8,128)}) custom-call(s32[4]{0:T(128)S(1)} %pad_add_fusion.1.spots, bf16[2048,1408]{1,0:T(8,128)(2,1)} %copy-done.53, bf16[2048,1408]{1,0:T(8,128)(2,1)} %copy-done.49, bf16[2048,1024]{1,0:T(8,128)(2,1)} %collective-permute-done.21.refs_2_, bf16[1024,1408]{1,0:T(8,128)(2,1)S(1)} %copy-done.32, ...), custom_call_target="tpu_custom_call" | custom-call | flops 11811160064 | bytes 27787264 | tf_op jit(solution)/shard_map/fold_half/pallas_call | solution.py:435
  567.4 16.5 %gradient_rows.10 = bf16[2048,1408]{1,0:T(8,128)(2,1)S(1)} custom-call(s32[4]{0:T(128)S(1)} %pad_add_fusion.1.spots, bf16[2048,2048]{1,0:T(8,128)(2,1)} %get-tuple-element.171.left_ref, bf16[2048,1408]{1,0:T(8,128)(2,1)S(1)} %copy-done.54), custom_call_target="tpu_custom_call" | custom-call | flops 11811160064 | bytes 17301504 | tf_op jit(solution)/shard_map/gradient_rows/pallas_call | solution.py:470
  589.0 11.4 %fold_half.8 = bf16[2048,1024]{1,0:T(8,128)(2,1)} custom-call(s32[4]{0:T(128)S(1)} %pad_add_fusion.1.spots, bf16[2048,1408]{1,0:T(8,128)(2,1)S(1)} %copy-done.52, bf16[2048,1408]{1,0:T(8,128)(2,1)} %all-gather.17.cloned.1.call-done.refs_0_.refs_1_.refs_2_), custom_call_target="tpu_custom_call" | custom-call | flops 5905580032 | bytes 9961472 | tf_op jit(solution)/shard_map/fold_half/pallas_call | solution.py:435
  600.4 9.5 collective-permute-done.23
  610.2 6.0 multiply_reduce_fusion.2
  621.3 12.1 %convolution_convert_fusion.1 = bf16[2048,512]{1,0:T(8,128)(2,1)S(1)} fusion(f32[2048,512]{1,0:T(8,128)} %copy-done.55, f32[2048]{0:T(1024)S(1)} %add_rsqrt_fusion, bf16[2048,1024]{1,0:T(8,128)(2,1)} %collective-permute-done.13, bf16[2048,1024]{1,0:T(8,128)(2,1)} %maximum_select_fusion.2, pred[]{:T(512)S(6)} %eq.53), kind=kOutput, calls=%fused_computation.28 | convolution fusion | flops 4335861760 | bytes 14688257 | tf_op jit(solution)/shard_map/dot_general | solution.py:32
  635.5 7.2 collective-permute-done.29
  655.1 15.0 %fold_half.9 = (bf16[2048,512]{1,0:T(8,128)(2,1)}, f32[2048,512]{1,0:T(8,128)S(1)}) custom-call(s32[4]{0:T(128)S(1)} %pad_add_fusion.1.spots, bf16[2048,1408]{1,0:T(8,128)(2,1)} %get-tuple-element.193.right_ref.refs_0_, bf16[2048,1024]{1,0:T(8,128)(2,1)} %collective-permute-done.27.refs_1_, ...), custom_call_target="tpu_custom_call" | custom-call | flops 5905580032 | bytes 16252928 | tf_op jit(solution)/shard_map/fold_half/pallas_call | solution.py:435
  670.1 29.6 %collective-permute-done.32 = f32[2048]{0:T(1024)S(1)} collective-permute-done((f32[2048]{0:T(1024)S(1)}, f32[2048]{0:T(1024)S(1)}, u32[]{:S(2)}, u32[]{:S(2)}) %collective-permute-start.32) | collective-permute-done | bytes 8224 | tf_op jit(solution)/shard_map/ppermute | solution.py:543
  701.7 4.8 multiply_convert_fusion
  706.6 21.3 %attend_back.1 = (bf16[2048,512]{1,0:T(8,128)(2,1)S(1)}, bf16[2048,512]{1,0:T(8,128)(2,1)S(1)}, bf16[2048,512]{1,0:T(8,128)(2,1)S(1)}) custom-call(f32[4]{0:T(128)S(1)} %dynamic_slice.129.rates, s32[2,2]{1,0:T(2,128)S(1)} %pad_add_fusion.ends, f32[2048,1024]{1,0:T(8,128)} %get-tuple-element.157.zq_ref.zk_ref, f32[2048,1024]{1,0:T(8,128)} %get-tuple-element.157.zq_ref.zk_ref, ...), custom_call_target="tpu_custom_call" | custom-call | flops 10737418240 | bytes 20971520 | tf_op jit(solution)/shard_map/attend_back/pallas_call | solution.py:119
  743.1 7.5 gradient_rows.11
  761.7 9.1 gradient_rows.12
  787.7 8.2 gradient_rows.13
  798.8 14.2 %fold_half.10 = bf16[2048,1024]{1,0:T(8,128)(2,1)S(1)} custom-call(s32[4]{0:T(128)S(1)} %pad_add_fusion.1.spots, bf16[2048,1024]{1,0:T(8,128)(2,1)} %copy-done.7, bf16[2048,1024]{1,0:T(8,128)(2,1)} %pad_maximum_fusion.refs_1_.right_ref, bf16[1024,1024]{1,0:T(8,128)(2,1)S(1)} %copy-done.40, bf16[1024,1024]{1,0:T(8,128)(2,1)S(1)} %copy-done.47, ...), custom_call_target="tpu_custom_call" | custom-call | flops 8589934592 | bytes 16777216 | tf_op jit(solution)/shard_map/fold_half/pallas_call | solution.py:435
  829.8 7.0 gradient_rows.14
  838.2 8.2 collective-permute-done.40
  854.2 17.0 %fold_half.11 = (bf16[2048,512]{1,0:T(8,128)(2,1)}, f32[2048,512]{1,0:T(8,128)}) custom-call(s32[4]{0:T(128)S(1)} %pad_add_fusion.1.spots, bf16[2048,1024]{1,0:T(8,128)(2,1)} %copy-done.7, bf16[2048,1024]{1,0:T(8,128)(2,1)} %pad_maximum_fusion.refs_1_.right_ref, bf16[2048,1024]{1,0:T(8,128)(2,1)} %collective-permute-done.39.refs_2_, ...), custom_call_target="tpu_custom_call" | custom-call | flops 8589934592 | bytes 23068672 | tf_op jit(solution)/shard_map/fold_half/pallas_call | solution.py:435
  883.0 7.0 gradient_rows.15
  893.0 29.8 %collective-permute-done.45 = f32[2048]{0:T(1024)S(1)} collective-permute-done((f32[2048]{0:T(1024)S(1)}, f32[2048]{0:T(1024)S(1)}, u32[]{:S(2)}, u32[]{:S(2)}) %collective-permute-start.45) | collective-permute-done | bytes 8224 | tf_op jit(solution)/shard_map/ppermute | solution.py:543
  932.3 19.4 %collective-permute-done.48 = bf16[2,512,512]{2,1,0:T(8,128)(2,1)S(1)} collective-permute-done((bf16[2,512,512]{2,1,0:T(8,128)(2,1)S(1)}, bf16[2,512,512]{2,1,0:T(8,128)(2,1)S(1)}, u32[]{:S(2)}, u32[]{:S(2)}) %collective-permute-start.48) | collective-permute-done | bytes 1048608 | tf_op jit(solution)/shard_map/ppermute | solution.py:543
  967.0 7.1 place_quarters.5
  977.2 8.6 collective-permute-done.50
  985.8 22.7 %collective-permute-done.54 = bf16[256,1536]{1,0:T(8,128)(2,1)} collective-permute-done((bf16[256,1536]{1,0:T(8,128)(2,1)}, bf16[256,1536]{1,0:T(8,128)(2,1)}, u32[]{:S(2)}, u32[]{:S(2)}) %collective-permute-start.54) | collective-permute-done | bytes 786464 | tf_op jit(solution)/shard_map/ppermute | solution.py:543
  1032.0 5.6 place_quarters.6
  1038.9 7.8 collective-permute-done.60
  1046.8 24.5 %collective-permute-done.59 = bf16[256,2048]{1,0:T(8,128)(2,1)} collective-permute-done((bf16[256,2048]{1,0:T(8,128)(2,1)}, bf16[256,2048]{1,0:T(8,128)(2,1)}, u32[]{:S(2)}, u32[]{:S(2)}) %collective-permute-start.59) | collective-permute-done | bytes 1048608 | tf_op jit(solution)/shard_map/ppermute | solution.py:602
  1091.9 5.6 place_quarters.9
  (445 shorter events, 318.3 us)
Async XLA Ops:
  8.0 89.1 %all-gather.7.cloned.1.call-start = ((), (), s32[]{:S(2)}) async-start(), calls=%async_computation.6 | async-start | bytes 2621440 | tf_op jit(solution)/shard_map/all_gather | solution.py:664
  10.3 136.6 %all-gather.9.cloned.1.call-start = ((), (), s32[]{:S(2)}) async-start(), calls=%async_computation.7 | async-start | bytes 2621440 | tf_op jit(solution)/shard_map/all_gather | solution.py:664
  12.6 171.6 %all-gather.11.cloned.1.call-start = ((), (), s32[]{:S(2)}) async-start(), calls=%async_computation.8 | async-start | bytes 1310720 | tf_op jit(solution)/shard_map/all_gather | solution.py:664
  13.9 80.9 %collective-permute-start = (bf16[256,2048]{1,0:T(8,128)(2,1)}, bf16[256,2048]{1,0:T(8,128)(2,1)S(1)}, u32[]{:S(2)}, u32[]{:S(2)}) collective-permute-start(bf16[256,2048]{1,0:T(8,128)(2,1)} %get-tuple-element.320), channel_id=1, source_target_pairs={{0,0},{4,1},{1,2},{5,3},{2,4},{6,5},{3,6},{7,7},{8,8},{12,9},{9,10... | collective-permute-start | bytes 3145736 | tf_op jit(solution)/shard_map/ppermute | solution.py:594
  16.0 78.8 %collective-permute-start.1 = (bf16[256,2048]{1,0:T(8,128)(2,1)S(1)}, bf16[256,2048]{1,0:T(8,128)(2,1)S(1)}, u32[]{:S(2)}, u32[]{:S(2)}) collective-permute-start(bf16[256,2048]{1,0:T(8,128)(2,1)S(1)} %get-tuple-element.321), channel_id=1, source_target_pairs={{1,0},{5,1},{0,2},{4,3},{3,4},{7,5},{2,6},{6,7},{9,8},{13,9},{8,10... | collective-permute-start | bytes 3145736 | tf_op jit(solution)/shard_map/ppermute | solution.py:594
  97.1 43.7 %collective-permute-start.2 = (bf16[512,2048]{1,0:T(8,128)(2,1)}, bf16[512,2048]{1,0:T(8,128)(2,1)}, u32[]{:S(2)}, u32[]{:S(2)}) collective-permute-start(bf16[512,2048]{1,0:T(8,128)(2,1)} %maximum_select_fusion.6), channel_id=1, source_target_pairs={{0,8},{1,9},{2,10},{3,11},{4,12},{5,13},{6,14},{7,15},{8,0},{9,1},... | collective-permute-start | bytes 6291464 | tf_op jit(solution)/shard_map/ppermute | solution.py:543
  99.1 139.0 %all-gather.13.cloned.1.call-start = ((), (), s32[]{:S(2)}) async-start(), calls=%async_computation.9 | async-start | bytes 3604480 | tf_op jit(solution)/shard_map/all_gather | solution.py:664
  99.1 47.8 %collective-permute-start.3 = (bf16[1024,1024]{1,0:T(8,128)(2,1)}, bf16[1024,1024]{1,0:T(8,128)(2,1)S(1)}, u32[]{:S(2)}, u32[]{:S(2)}) collective-permute-start(bf16[1024,1024]{1,0:T(8,128)(2,1)} %all-gather.7.cloned.1.call-done.refs_0_.refs_2_.refs_3_), channel_id=1, source_target_pairs={{0,16},{1,17},{2,18},{3,19},{4,20},{5,21},{6,22},{7,23},{8,24},{9,... | collective-permute-start | bytes 6291464 | tf_op jit(solution)/shard_map/ppermute | solution.py:543
  102.8 189.0 %all-gather.15.cloned.1.call-start = ((), (), s32[]{:S(2)}) async-start(), calls=%async_computation.10 | async-start | bytes 3604480 | tf_op jit(solution)/shard_map/all_gather | solution.py:664
  151.7 47.5 %collective-permute-start.5 = (bf16[1024,1024]{1,0:T(8,128)(2,1)}, bf16[1024,1024]{1,0:T(8,128)(2,1)}, u32[]{:S(2)}, u32[]{:S(2)}) collective-permute-start(bf16[1024,1024]{1,0:T(8,128)(2,1)} %all-gather.9.cloned.1.call-done.refs_0_.refs_4_.refs_5_), channel_id=1, source_target_pairs={{0,16},{1,17},{2,18},{3,19},{4,20},{5,21},{6,22},{7,23},{8,24},{9,... | collective-permute-start | bytes 6291464 | tf_op jit(solution)/shard_map/ppermute | solution.py:543
  157.8 315.0 %all-gather.17.cloned.1.call-start = ((), (), s32[]{:S(2)}) async-start(), calls=%async_computation.11 | async-start | bytes 6488064 | tf_op jit(solution)/shard_map/all_gather | solution.py:668
  199.2 38.8 %collective-permute-start.8 = (bf16[1024,512]{1,0:T(8,128)(2,1)}, bf16[1024,512]{1,0:T(8,128)(2,1)}, u32[]{:S(2)}, u32[]{:S(2)}) collective-permute-start(bf16[1024,512]{1,0:T(8,128)(2,1)} %all-gather.11.cloned.1.call-done), channel_id=1, source_target_pairs={{0,16},{1,17},{2,18},{3,19},{4,20},{5,21},{6,22},{7,23},{8,24},{9,... | collective-permute-start | bytes 3145736 | tf_op jit(solution)/shard_map/ppermute | solution.py:543
  238.0 63.2 %collective-permute-start.10 = (bf16[1024,1408]{1,0:T(8,128)(2,1)}, bf16[1024,1408]{1,0:T(8,128)(2,1)}, u32[]{:S(2)}, u32[]{:S(2)}) collective-permute-start(bf16[1024,1408]{1,0:T(8,128)(2,1)} %all-gather.13.cloned.1.call-done.refs_0_.refs_2_.refs_3_), channel_id=1, source_target_pairs={{0,16},{1,17},{2,18},{3,19},{4,20},{5,21},{6,22},{7,23},{8,24},{9,... | collective-permute-start | bytes 8650760 | tf_op jit(solution)/shard_map/ppermute | solution.py:543
  238.2 46.2 %collective-permute-start.9 = (bf16[2048,512]{1,0:T(8,128)(2,1)}, bf16[2048,512]{1,0:T(8,128)(2,1)S(1)}, u32[]{:S(2)}, u32[]{:S(2)}) collective-permute-start(bf16[2048,512]{1,0:T(8,128)(2,1)} %get-tuple-element.160), channel_id=1, source_target_pairs={{0,8},{1,9},{2,10},{3,11},{4,12},{5,13},{6,14},{7,15},{8,0},{9,1},... | collective-permute-start | bytes 6291464 | tf_op jit(solution)/shard_map/ppermute | solution.py:543
  242.0 42.4 %collective-permute-start.12 = (f32[2048]{0:T(1024)S(1)}, f32[2048]{0:T(1024)S(1)}, u32[]{:S(2)}, u32[]{:S(2)}) collective-permute-start(f32[2048]{0:T(1024)S(1)} %add.256), channel_id=1, source_target_pairs={{0,8},{1,9},{2,10},{3,11},{4,12},{5,13},{6,14},{7,15},{8,0},{9,1},... | collective-permute-start | bytes 24584 | tf_op jit(solution)/shard_map/ppermute | solution.py:543
  308.0 68.5 %collective-permute-start.15 = (bf16[1024,1408]{1,0:T(8,128)(2,1)S(1)}, bf16[1024,1408]{1,0:T(8,128)(2,1)S(1)}, u32[]{:S(2)}, u32[]{:S(2)}) collective-permute-start(bf16[1024,1408]{1,0:T(8,128)(2,1)S(1)} %copy-done.33), channel_id=1, source_target_pairs={{0,16},{1,17},{2,18},{3,19},{4,20},{5,21},{6,22},{7,23},{8,24},{9,... | collective-permute-start | bytes 8650760 | tf_op jit(solution)/shard_map/ppermute | solution.py:543
  320.3 53.5 %collective-permute-start.14 = (bf16[2048,512]{1,0:T(8,128)(2,1)}, bf16[2048,512]{1,0:T(8,128)(2,1)S(1)}, u32[]{:S(2)}, u32[]{:S(2)}) collective-permute-start(bf16[2048,512]{1,0:T(8,128)(2,1)} %get-tuple-element.324), channel_id=1, source_target_pairs={{0,8},{1,9},{2,10},{3,11},{4,12},{5,13},{6,14},{7,15},{8,0},{9,1},... | collective-permute-start | bytes 6291464 | tf_op jit(solution)/shard_map/ppermute | solution.py:543
  323.2 48.2 %collective-permute-start.16 = (bf16[256,2048]{1,0:T(8,128)(2,1)S(1)}, bf16[256,2048]{1,0:T(8,128)(2,1)S(1)}, u32[]{:S(2)}, u32[]{:S(2)}) collective-permute-start(bf16[256,2048]{1,0:T(8,128)(2,1)S(1)} %get-tuple-element.316), channel_id=1, source_target_pairs={{0,0},{4,1},{1,2},{5,3},{2,4},{6,5},{3,6},{7,7},{8,8},{12,9},{9,10... | collective-permute-start | bytes 3145736 | tf_op jit(solution)/shard_map/ppermute | solution.py:594
  328.2 43.2 %collective-permute-start.17 = (bf16[256,2048]{1,0:T(8,128)(2,1)S(1)}, bf16[256,2048]{1,0:T(8,128)(2,1)S(1)}, u32[]{:S(2)}, u32[]{:S(2)}) collective-permute-start(bf16[256,2048]{1,0:T(8,128)(2,1)S(1)} %get-tuple-element.317), channel_id=1, source_target_pairs={{1,0},{5,1},{0,2},{4,3},{3,4},{7,5},{2,6},{6,7},{9,8},{13,9},{8,10... | collective-permute-start | bytes 3145736 | tf_op jit(solution)/shard_map/ppermute | solution.py:594
  383.8 226.1 %reduce-scatter.7.cloned.1.call-start = ((), (), s32[]{:S(2)}) async-start(), calls=%async_computation.12 | async-start | bytes 6488064 | tf_op jit(solution)/shard_map/reduce_scatter | solution.py:708
  384.4 47.6 %collective-permute-start.19 = (bf16[512,2048]{1,0:T(8,128)(2,1)}, bf16[512,2048]{1,0:T(8,128)(2,1)S(1)}, u32[]{:S(2)}, u32[]{:S(2)}) collective-permute-start(bf16[512,2048]{1,0:T(8,128)(2,1)} %maximum_select_fusion.8), channel_id=1, source_target_pairs={{0,8},{1,9},{2,10},{3,11},{4,12},{5,13},{6,14},{7,15},{8,0},{9,1},... | collective-permute-start | bytes 6291464 | tf_op jit(solution)/shard_map/ppermute | solution.py:543
  472.8 398.4 %reduce-scatter.9.cloned.1.call-start = ((), (), s32[]{:S(2)}) async-start(), calls=%async_computation.13 | async-start | bytes 6488064 | tf_op jit(solution)/shard_map/reduce_scatter | solution.py:708
  527.1 34.3 %collective-permute-start.22 = (f32[2048]{0:T(1024)S(1)}, f32[2048]{0:T(1024)S(1)}, u32[]{:S(2)}, u32[]{:S(2)}) collective-permute-start(f32[2048]{0:T(1024)S(1)} %reduce.1), channel_id=1, source_target_pairs={{0,4},{1,5},{2,6},{3,7},{4,0},{5,1},{6,2},{7,3},{8,12},{9,13},{10,... | collective-permute-start | bytes 24584 | tf_op jit(solution)/shard_map/ppermute | solution.py:543
  561.4 39.0 %collective-permute-start.25 = (f32[2048]{0:T(1024)S(1)}, f32[2048]{0:T(1024)S(1)}, u32[]{:S(2)}, u32[]{:S(2)}) collective-permute-start(f32[2048]{0:T(1024)S(1)} %add.261), channel_id=1, source_target_pairs={{0,8},{1,9},{2,10},{3,11},{4,12},{5,13},{6,14},{7,15},{8,0},{9,1},... | collective-permute-start | bytes 24584 | tf_op jit(solution)/shard_map/ppermute | solution.py:543
  562.7 47.3 %collective-permute-start.23 = (bf16[2048,512]{1,0:T(8,128)(2,1)}, bf16[2048,512]{1,0:T(8,128)(2,1)}, u32[]{:S(2)}, u32[]{:S(2)}) collective-permute-start(bf16[2048,512]{1,0:T(8,128)(2,1)} %get-tuple-element.192), channel_id=1, source_target_pairs={{0,8},{1,9},{2,10},{3,11},{4,12},{5,13},{6,14},{7,15},{8,0},{9,1},... | collective-permute-start | bytes 6291464 | tf_op jit(solution)/shard_map/ppermute | solution.py:543
  564.7 35.7 %collective-permute-start.24 = (bf16[512,1408]{1,0:T(8,128)(2,1)}, bf16[512,1408]{1,0:T(8,128)(2,1)}, u32[]{:S(2)}, u32[]{:S(2)}) collective-permute-start(bf16[512,1408]{1,0:T(8,128)(2,1)} %get-tuple-element.297), channel_id=1, source_target_pairs={{0,16},{1,17},{2,18},{3,19},{4,20},{5,21},{6,22},{7,23},{8,24},{9,... | collective-permute-start | bytes 4325384 | tf_op jit(solution)/shard_map/ppermute | solution.py:543
  610.0 283.0 %reduce-scatter.15.cloned.1.call-start = ((), (), s32[]{:S(2)}) async-start(), calls=%async_computation.16 | async-start | bytes 1310720 | tf_op jit(solution)/shard_map/reduce_scatter | solution.py:702
  621.1 32.1 %collective-permute-start.27 = (bf16[2048,1024]{1,0:T(8,128)(2,1)}, bf16[2048,1024]{1,0:T(8,128)(2,1)}, u32[]{:S(2)}, u32[]{:S(2)}) collective-permute-start(bf16[2048,1024]{1,0:T(8,128)(2,1)} %fold_half.8), channel_id=1, source_target_pairs={{0,4},{1,5},{2,6},{3,7},{4,0},{5,1},{6,2},{7,3},{8,12},{9,13},{10,... | collective-permute-start | bytes 12582920 | tf_op jit(solution)/shard_map/ppermute | solution.py:543
  653.2 46.5 %collective-permute-start.30 = (bf16[2048,512]{1,0:T(8,128)(2,1)}, bf16[2048,512]{1,0:T(8,128)(2,1)}, u32[]{:S(2)}, u32[]{:S(2)}) collective-permute-start(bf16[2048,512]{1,0:T(8,128)(2,1)} %dynamic-slice_convert_fusion), channel_id=1, source_target_pairs={{0,8},{1,9},{2,10},{3,11},{4,12},{5,13},{6,14},{7,15},{8,0},{9,1},... | collective-permute-start | bytes 6291464 | tf_op jit(solution)/shard_map/ppermute | solution.py:543
  654.3 45.4 %collective-permute-start.31 = (bf16[1024,512]{1,0:T(8,128)(2,1)}, bf16[1024,512]{1,0:T(8,128)(2,1)}, u32[]{:S(2)}, u32[]{:S(2)}) collective-permute-start(bf16[1024,512]{1,0:T(8,128)(2,1)} %get-tuple-element.214), channel_id=1, source_target_pairs={{0,16},{1,17},{2,18},{3,19},{4,20},{5,21},{6,22},{7,23},{8,24},{9,... | collective-permute-start | bytes 3145736 | tf_op jit(solution)/shard_map/ppermute | solution.py:543
  654.9 44.8 %collective-permute-start.32 = (f32[2048]{0:T(1024)S(1)}, f32[2048]{0:T(1024)S(1)}, u32[]{:S(2)}, u32[]{:S(2)}) collective-permute-start(f32[2048]{0:T(1024)S(1)} %add.275), channel_id=1, source_target_pairs={{0,8},{1,9},{2,10},{3,11},{4,12},{5,13},{6,14},{7,15},{8,0},{9,1},... | collective-permute-start | bytes 24584 | tf_op jit(solution)/shard_map/ppermute | solution.py:543
  699.7 50.9 %collective-permute-start.33 = (bf16[512,1408]{1,0:T(8,128)(2,1)}, bf16[512,1408]{1,0:T(8,128)(2,1)}, u32[]{:S(2)}, u32[]{:S(2)}) collective-permute-start(bf16[512,1408]{1,0:T(8,128)(2,1)} %get-tuple-element.221), channel_id=1, source_target_pairs={{0,16},{1,17},{2,18},{3,19},{4,20},{5,21},{6,22},{7,23},{8,24},{9,... | collective-permute-start | bytes 4325384 | tf_op jit(solution)/shard_map/ppermute | solution.py:543
  700.4 50.2 %collective-permute-start.34 = (bf16[2048,512]{1,0:T(8,128)(2,1)}, bf16[2048,512]{1,0:T(8,128)(2,1)}, u32[]{:S(2)}, u32[]{:S(2)}) collective-permute-start(bf16[2048,512]{1,0:T(8,128)(2,1)} %get-tuple-element.222), channel_id=1, source_target_pairs={{0,8},{1,9},{2,10},{3,11},{4,12},{5,13},{6,14},{7,15},{8,0},{9,1},... | collective-permute-start | bytes 6291464 | tf_op jit(solution)/shard_map/ppermute | solution.py:543
  734.4 158.6 %reduce-scatter.13.cloned.1.call-start = ((), (), s32[]{:S(2)}) async-start(), calls=%async_computation.15 | async-start | bytes 3604480 | tf_op jit(solution)/shard_map/reduce_scatter | solution.py:702
  778.7 183.6 %reduce-scatter.17.cloned.1.call-start = ((), (), s32[]{:S(2)}) async-start(), calls=%async_computation.17 | async-start | bytes 2621440 | tf_op jit(solution)/shard_map/reduce_scatter | solution.py:702
  817.3 53.9 %collective-permute-start.43 = (bf16[512,1408]{1,0:T(8,128)(2,1)}, bf16[512,1408]{1,0:T(8,128)(2,1)}, u32[]{:S(2)}, u32[]{:S(2)}) collective-permute-start(bf16[512,1408]{1,0:T(8,128)(2,1)} %maximum_select_fusion.16), channel_id=1, source_target_pairs={{0,8},{1,9},{2,10},{3,11},{4,12},{5,13},{6,14},{7,15},{8,0},{9,1},... | collective-permute-start | bytes 4325384 | tf_op jit(solution)/shard_map/ppermute | solution.py:543
  846.4 119.2 %reduce-scatter.11.cloned.1.call-start = ((), (), s32[]{:S(2)}) async-start(), calls=%async_computation.14 | async-start | bytes 2621440 | tf_op jit(solution)/shard_map/reduce_scatter | solution.py:702
  873.8 49.0 %collective-permute-start.47 = (bf16[512,2816]{1,0:T(8,128)(2,1)}, bf16[512,2816]{1,0:T(8,128)(2,1)}, u32[]{:S(2)}, u32[]{:S(2)}) collective-permute-start(bf16[512,2816]{1,0:T(8,128)(2,1)} %constant_dynamic-update-slice_fusion.2.refs_0_.refs_1_), channel_id=1, source_target_pairs={{0,4},{1,5},{2,6},{3,7},{4,0},{5,1},{6,2},{7,3},{8,12},{9,13},{10,... | collective-permute-start | bytes 8650760 | tf_op jit(solution)/shard_map/ppermute | solution.py:543
  875.0 47.8 %collective-permute-start.44 = (bf16[2048,512]{1,0:T(8,128)(2,1)}, bf16[2048,512]{1,0:T(8,128)(2,1)}, u32[]{:S(2)}, u32[]{:S(2)}) collective-permute-start(bf16[2048,512]{1,0:T(8,128)(2,1)} %get-tuple-element.251), channel_id=1, source_target_pairs={{0,8},{1,9},{2,10},{3,11},{4,12},{5,13},{6,14},{7,15},{8,0},{9,1},... | collective-permute-start | bytes 6291464 | tf_op jit(solution)/shard_map/ppermute | solution.py:543
  878.6 44.2 %collective-permute-start.45 = (f32[2048]{0:T(1024)S(1)}, f32[2048]{0:T(1024)S(1)}, u32[]{:S(2)}, u32[]{:S(2)}) collective-permute-start(f32[2048]{0:T(1024)S(1)} %add.284), channel_id=1, source_target_pairs={{0,8},{1,9},{2,10},{3,11},{4,12},{5,13},{6,14},{7,15},{8,0},{9,1},... | collective-permute-start | bytes 24584 | tf_op jit(solution)/shard_map/ppermute | solution.py:543
  880.1 42.6 %collective-permute-start.46 = (bf16[256,1408]{1,0:T(8,128)(2,1)S(1)}, bf16[256,1408]{1,0:T(8,128)(2,1)}, u32[]{:S(2)}, u32[]{:S(2)}) collective-permute-start(bf16[256,1408]{1,0:T(8,128)(2,1)S(1)} %copy-done.77), channel_id=1, source_target_pairs={{0,16},{1,17},{2,18},{3,19},{4,20},{5,21},{6,22},{7,23},{8,24},{9,... | collective-permute-start | bytes 2162696 | tf_op jit(solution)/shard_map/ppermute | solution.py:543
  931.4 34.1 %collective-permute-start.51 = (bf16[256,2048]{1,0:T(8,128)(2,1)}, bf16[256,2048]{1,0:T(8,128)(2,1)}, u32[]{:S(2)}, u32[]{:S(2)}) collective-permute-start(bf16[256,2048]{1,0:T(8,128)(2,1)} %get-tuple-element.300), channel_id=1, source_target_pairs={{0,1},{1,5},{2,0},{3,4},{4,3},{5,7},{6,2},{7,6},{8,9},{9,13},{10,8... | collective-permute-start | bytes 3145736 | tf_op jit(solution)/shard_map/ppermute | solution.py:602
  958.3 50.2 %collective-permute-start.52 = (bf16[512,1408]{1,0:T(8,128)(2,1)}, bf16[512,1408]{1,0:T(8,128)(2,1)}, u32[]{:S(2)}, u32[]{:S(2)}) collective-permute-start(bf16[512,1408]{1,0:T(8,128)(2,1)} %maximum_select_fusion.17), channel_id=1, source_target_pairs={{0,8},{1,9},{2,10},{3,11},{4,12},{5,13},{6,14},{7,15},{8,0},{9,1},... | collective-permute-start | bytes 4325384 | tf_op jit(solution)/shard_map/ppermute | solution.py:543
  964.3 44.2 %collective-permute-start.54 = (bf16[256,1536]{1,0:T(8,128)(2,1)}, bf16[256,1536]{1,0:T(8,128)(2,1)}, u32[]{:S(2)}, u32[]{:S(2)}) collective-permute-start(bf16[256,1536]{1,0:T(8,128)(2,1)} %pad_maximum_fusion.7), channel_id=1, source_target_pairs={{0,8},{1,9},{2,10},{3,11},{4,12},{5,13},{6,14},{7,15},{8,0},{9,1},... | collective-permute-start | bytes 2359304 | tf_op jit(solution)/shard_map/ppermute | solution.py:543
  965.7 42.8 %collective-permute-start.55 = (bf16[256,1024]{1,0:T(8,128)(2,1)}, bf16[256,1024]{1,0:T(8,128)(2,1)S(1)}, u32[]{:S(2)}, u32[]{:S(2)}) collective-permute-start(bf16[256,1024]{1,0:T(8,128)(2,1)} %reduce-scatter.11.cloned.1.call-done), channel_id=1, source_target_pairs={{0,16},{1,17},{2,18},{3,19},{4,20},{5,21},{6,22},{7,23},{8,24},{9,... | collective-permute-start | bytes 1572872 | tf_op jit(solution)/shard_map/ppermute | solution.py:543
  1016.8 54.4 %collective-permute-start.57 = (bf16[512,1408]{1,0:T(8,128)(2,1)}, bf16[512,1408]{1,0:T(8,128)(2,1)}, u32[]{:S(2)}, u32[]{:S(2)}) collective-permute-start(bf16[512,1408]{1,0:T(8,128)(2,1)} %maximum_select_fusion.18), channel_id=1, source_target_pairs={{0,8},{1,9},{2,10},{3,11},{4,12},{5,13},{6,14},{7,15},{8,0},{9,1},... | collective-permute-start | bytes 4325384 | tf_op jit(solution)/shard_map/ppermute | solution.py:543
  1020.2 51.0 %collective-permute-start.58 = (bf16[256,3072]{1,0:T(8,128)(2,1)}, bf16[256,3072]{1,0:T(8,128)(2,1)}, u32[]{:S(2)}, u32[]{:S(2)}) collective-permute-start(bf16[256,3072]{1,0:T(8,128)(2,1)} %constant_dynamic-update-slice_fusion.4), channel_id=1, source_target_pairs={{0,16},{1,17},{2,18},{3,19},{4,20},{5,21},{6,22},{7,23},{8,24},{9,... | collective-permute-start | bytes 4718600 | tf_op jit(solution)/shard_map/ppermute | solution.py:543
  1024.6 46.6 %collective-permute-start.59 = (bf16[256,2048]{1,0:T(8,128)(2,1)}, bf16[256,2048]{1,0:T(8,128)(2,1)}, u32[]{:S(2)}, u32[]{:S(2)}) collective-permute-start(bf16[256,2048]{1,0:T(8,128)(2,1)} %get-tuple-element.299), channel_id=1, source_target_pairs={{0,0},{1,4},{2,1},{3,5},{4,2},{5,6},{6,3},{7,7},{8,8},{9,12},{10,9... | collective-permute-start | bytes 3145736 | tf_op jit(solution)/shard_map/ppermute | solution.py:602
  (117 other events, 1395.1 us)
Sparse Core Ops, SparseCore 0:
  11.0 82.9 all-gather.6
  96.1 46.0 all-gather.8
  144.4 27.5 all-gather.10
  174.0 57.8 all-gather.12
  233.9 57.8 all-gather.14
Sparse Core Ops, SparseCore 1:
  383.9 88.8 all-gather.16
  476.3 108.7 reduce-scatter.6
  610.1 126.2 reduce-scatter.8
  738.6 25.1 reduce-scatter.14
  778.8 59.8 reduce-scatter.12
  846.5 43.0 reduce-scatter.16
  892.3 42.7 reduce-scatter.10

commit v14 on v13

--- a/solution.py
+++ b/solution.py
@@ -865,14 +865,18 @@
     qk_a = sent_a(qk_a)
     f_two = gradient_rows(spots, spread, 0, hidden_two, d_two, stacked(upper, lower))
     output, out_b = away_b((middle + (result_mine + result.astype(F32))).astype(LOW))
-    f_two, qk_a, qk_b, out_b, d_qk, d_vg = tie(f_two, qk_a, qk_b, out_b, d_qk, d_vg)
+    f_two, qk_a, qk_b, out_b, d_qk, d_vg, f_one = tie(f_two, qk_a, qk_b, out_b, d_qk, d_vg, f_one)
 
     f_two = scattered(f_two)
     qk_b = sent_a(qk_b)
     output, out_c = away_c(output, out_b)
+    x_down = swap_b(y_down)
+    y_one = over_spread(f_one)
     t_vg = away(hidden_one, d_vg)
     sent = fold_half(spots, [d_qk, d_vg], [w_qk, w_vg])
-    sent, t_vg, d_qk, d_vg, out_c, qk_b = tie(sent, t_vg, d_qk, d_vg, out_c, qk_b)
+    sent, t_vg, d_qk, d_vg, out_c, qk_b, x_down, y_one = tie(
+        sent, t_vg, d_qk, d_vg, out_c, qk_b, x_down, y_one
+    )
 
     arrived = swap_c(sent)
     vg_a, vg_b = in_two(t_vg)
@@ -883,33 +887,35 @@
 
     f_qk = scattered(f_qk)
     vg_b = sent_a(vg_b)
-    x_down = swap_b(y_down)
+    y_one = by_spread([f_one, *y_one])
+    x_one = swap_b(y_one)
     lean_x = lean_x + swap_c(lean_x)
     sent, mine = fold_half(spots, [d_qk, d_vg], [w_qk, w_vg], arrived)
-    sent, mine, vg_b, lean_x, x_down, d_vg, f_one = tie(sent, mine, vg_b, lean_x, x_down, d_vg, f_one)
+    sent, mine, vg_b, lean_x, x_one, d_vg = tie(sent, mine, vg_b, lean_x, x_one, d_vg)
 
     crossed = swap_b(sent)
     lean_b = swap_b(lean_x)
     f_vg = scattered(gradient_rows(spots, spread, 0, hidden_one, d_vg, stacked(vg_a, vg_b)))
-    y_one = over_spread(f_one)
     four_down = spread_c(joined(y_down, x_down))
-    crossed, lean_b, y_one, four_down, f_two, f_out = tie(crossed, lean_b, y_one, four_down, f_two, f_out)
+    four_one = spread_c(joined(y_one, x_one))
+    crossed, lean_b, four_one, four_down, f_two, f_out = tie(
+        crossed, lean_b, four_one, four_down, f_two, f_out
+    )
 
     d_hidden = mine + crossed.astype(F32)
     x_normed = x_own.astype(F32) * x_scale
     lean = (lean_x + lean_b)[:, None] / width
     input_grad = to_runs((d_middle + x_scale * (d_hidden - x_normed * lean)).astype(LOW))
     output = send_back(ordered(c, output, out_c, 1))
-    y_one = by_spread([f_one, *y_one])
-    x_one = swap_b(y_one)
     f_oqk = joined(f_out, f_qk)
     x_oqk = swap_b(f_oqk)
     y_two = over_spread(f_two)
     y_vg = over_spread(f_vg)
     units = f_one.shape[1]
     [g_down] = place_quarters(spots, four_down, (0, units))
-    input_grad, output, x_one, y_two, x_oqk, y_vg, g_down = tie(
-        input_grad, output, x_one, y_two, x_oqk, y_vg, g_down
+    [g_one] = place_quarters(spots, four_one, (0, units))
+    input_grad, output, y_two, x_oqk, y_vg, g_down, g_one = tie(
+        input_grad, output, y_two, x_oqk, y_vg, g_down, g_one
     )
 
     y_vg = by_spread([f_vg, *y_vg])
@@ -920,8 +926,7 @@
     y_oqk = over_spread(f_oqk)
     input_grad = send_back(input_grad)
     output = as_batches(output)
-    [g_one] = place_quarters(spots, spread_c(joined(y_one, x_one)), (0, units))
-    x_vg, x_two, y_oqk, input_grad, output, g_one = tie(x_vg, x_two, y_oqk, input_grad, output, g_one)
+    x_vg, x_two, y_oqk, input_grad, output = tie(x_vg, x_two, y_oqk, input_grad, output)
 
     four_vg = spread_c(joined(y_vg, x_vg))
     four_two = spread_c(joined(y_two, x_two))

time: 1120 us -> 1120 us (level)
  waiting for transfers between devices: 424 us -> 438 us
  local copies, waits for them, and re-layouts: 117 us -> 104 us
    unnamed x202 -> x208, local copies, waits for them, and re-layouts: 77.1 us -> 66.9 us
  transfers between devices with their start and end apart: 77 -> 77, of which waited for: 28 -> 31; matrix products, arithmetic and copies ran while one was open for 16% -> 15% of each run, Pallas kernels for 30% -> 31%
where the time goes in v14:
time: 1120 us; the launch traced here: 1110 us
  waiting for transfers between devices  438 us (39%)
  Pallas kernels  344 us (31%)
  local copies, waits for them, and re-layouts  104 us (9%)
  other arithmetic  102 us (9%)
  starting transfers between devices  76 us (7%)
  matrix products  30.7 us (3%)
  between operations  17 us (2%)
    ppermute x57, waiting for transfers between devices, move(): return lax.ppermute(x, AXES, pairs)  269 us
    ppermute x4, waiting for transfers between devices, bring(): lax.ppermute(lax.dynamic_index_in_dim(x, (place + p) % 2, 0, False), AXES...  119 us
    pallas_call x6, Pallas kernels, fold_half(): pl.pallas_call(functools.partial(fold_kernel, len(values), arrived is not...  100 us
    pallas_call x8, Pallas kernels, gradient_rows(): pl.pallas_call(gradient_kernel, out_shape=out, grid_spec=pltpu.PrefetchSc...  82 us
    unnamed x208, local copies, waits for them, and re-layouts  66.9 us
    ppermute x57, starting transfers between devices, move(): return lax.ppermute(x, AXES, pairs)  61 us
    select_n x23, other arithmetic, ordered(): jnp.where(index == 0, jnp.concatenate([mine, other], axis), jnp.concatena...  52.2 us
    ppermute x4, waiting for transfers between devices, send_back(): lax.ppermute(lax.dynamic_index_in_dim(slots, (batch_of(place) + p) % 2, 0...  42.2 us
  transfers between devices with their start and end apart: 77, of which 31 were waited for; matrix products, arithmetic and copies ran while one was open for 15% of the time, Pallas kernels for 31%

profile of v14, /device:TPU:17, one launch (start us, length us, event | category | flops | bytes accessed | tf_op | source)
XLA Modules:
  0.0 1112.2 jit_solution(1331272249982748079)
XLA Ops:
  18.8 75.9 %collective-permute-done = bf16[256,2048]{1,0:T(8,128)(2,1)S(1)} collective-permute-done((bf16[256,2048]{1,0:T(8,128)(2,1)}, bf16[256,2048]{1,0:T(8,128)(2,1)S(1)}, u32[]{:S(2)}, u32[]{:S(2)}) %collective-permute-start) | collective-permute-done | bytes 1048608 | tf_op jit(solution)/shard_map/ppermute | solution.py:594
  102.9 37.9 %collective-permute-done.2 = bf16[512,2048]{1,0:T(8,128)(2,1)} collective-permute-done((bf16[512,2048]{1,0:T(8,128)(2,1)}, bf16[512,2048]{1,0:T(8,128)(2,1)}, u32[]{:S(2)}, u32[]{:S(2)}) %collective-permute-start.2) | collective-permute-done | bytes 2097184 | tf_op jit(solution)/shard_map/ppermute | solution.py:543
  140.8 6.2 maximum_select_fusion.1.own_ref
  165.5 18.8 %enter.2 = (bf16[2048,2048]{1,0:T(8,128)(2,1)}, f32[2048,1024]{1,0:T(8,128)}, f32[2048,1]{1,0:T(8,128)S(1)}, bf16[2048,512]{1,0:T(8,128)(2,1)S(1)}) custom-call(s32[4]{0:T(128)S(1)} %pad_add_fusion.1.spots, bf16[1024,2048]{1,0:T(8,128)(2,1)S(1)} %copy-done.15, bf16[1024,2048]{1,0:T(8,128)(2,1)} %collective-permute-done.4.other_ref, ...), custom_call_target="tpu_custom_call" | custom-call | flops 8589934592 | bytes 31465472 | tf_op jit(solution)/shard_map/enter/pallas_call | solution.py:244
  185.3 14.0 %collective-permute-done.5.refs_1_.refs_5_.refs_6_ = bf16[1024,1024]{1,0:T(8,128)(2,1)} collective-permute-done((bf16[1024,1024]{1,0:T(8,128)(2,1)}, bf16[1024,1024]{1,0:T(8,128)(2,1)}, u32[]{:S(2)}, u32[]{:S(2)}) %collective-permute-start.5) | collective-permute-done | bytes 2097184 | tf_op jit(solution)/shard_map/ppermute | solution.py:543
  202.1 14.2 %project.1.zv_ref = f32[2048,1024]{1,0:T(8,128)S(1)} custom-call(s32[4]{0:T(128)S(1)} %pad_add_fusion.1.spots, bf16[2048,2048]{1,0:T(8,128)(2,1)} %get-tuple-element.157.h_ref.left_ref, bf16[1024,1024]{1,0:T(8,128)(2,1)S(1)} %copy-done.42, bf16[1024,1024]{1,0:T(8,128)(2,1)} %collective-permute-done.5.refs_1_.refs_5_.refs_6_), custom_call_target="tpu_custom_call" | custom-call | flops 8589934592 | bytes 20971520 | tf_op jit(solution)/shard_map/project/pallas_call | solution.py:275
  219.8 12.3 %attend.1 = f32[2048,512]{1,0:T(8,128)S(1)} custom-call(f32[4]{0:T(128)S(1)} %dynamic_slice.129.rates, s32[2,2]{1,0:T(2,128)S(1)} %pad_add_fusion.ends, f32[2048,1024]{1,0:T(8,128)S(1)} %copy-done, f32[2048,1024]{1,0:T(8,128)S(1)} %copy-done, f32[2048,1024]{1,0:T(8,128)} %copy-done.1), custom_call_target="tpu_custom_call" | custom-call | flops 4294967296 | bytes 16777216 | tf_op jit(solution)/shard_map/attend/pallas_call | solution.py:98
  242.3 42.2 %collective-permute-done.12 = f32[2048]{0:T(1024)S(1)} collective-permute-done((f32[2048]{0:T(1024)S(1)}, f32[2048]{0:T(1024)S(1)}, u32[]{:S(2)}, u32[]{:S(2)}) %collective-permute-start.12) | collective-permute-done | bytes 8224 | tf_op jit(solution)/shard_map/ppermute | solution.py:543
  291.8 9.5 collective-permute-done.10.refs_1_.refs_3_.refs_4_
  310.5 9.8 fusion.21
  328.3 43.1 %collective-permute-done.16 = bf16[256,2048]{1,0:T(8,128)(2,1)S(1)} collective-permute-done((bf16[256,2048]{1,0:T(8,128)(2,1)S(1)}, bf16[256,2048]{1,0:T(8,128)(2,1)S(1)}, u32[]{:S(2)}, u32[]{:S(2)}) %collective-permute-start.16) | collective-permute-done | bytes 1048608 | tf_op jit(solution)/shard_map/ppermute | solution.py:594
  390.6 38.3 %gated_unit.1 = (bf16[2048,2048]{1,0:T(8,128)(2,1)}, bf16[2048,1408]{1,0:T(8,128)(2,1)}, bf16[2048,1408]{1,0:T(8,128)(2,1)}, bf16[2048,1408]{1,0:T(8,128)(2,1)}, f32[2048,1]{1,0:T(8,128)S(1)}) custom-call(s32[4]{0:T(128)S(1)} %pad_add_fusion.1.spots, bf16[2048,1024]{1,0:T(8,128)(2,1)} %maximum_select_fusion.3.own_ref, ...), custom_call_target="tpu_custom_call" | custom-call | flops 23622320128 | bytes 45621248 | tf_op jit(solution)/shard_map/gated_unit/pallas_call | solution.py:337
  435.0 6.8 collective-permute-done.20.other_ref
  441.7 5.5 enter.3
  448.6 16.7 %gradient_rows.8 = bf16[2048,1408]{1,0:T(8,128)(2,1)S(1)} custom-call(s32[4]{0:T(128)S(1)} %pad_add_fusion.1.spots, bf16[2048,2048]{1,0:T(8,128)(2,1)} %get-tuple-element.179.left_ref.dy_ref, bf16[2048,1408]{1,0:T(8,128)(2,1)S(1)} %bitcast.65), custom_call_target="tpu_custom_call" | custom-call | flops 11811160064 | bytes 17301504 | tf_op jit(solution)/shard_map/gradient_rows/pallas_call | solution.py:470
  472.9 22.4 %gated_unit_back.1 = (bf16[2048,1408]{1,0:T(8,128)(2,1)S(1)}, bf16[2048,1408]{1,0:T(8,128)(2,1)S(1)}, f32[2048,1]{1,0:T(8,128)S(1)}) custom-call(s32[4]{0:T(128)S(1)} %pad_add_fusion.1.spots, bf16[2048,2048]{1,0:T(8,128)(2,1)} %get-tuple-element.179.left_ref.dy_ref, bf16[2048,1408]{1,0:T(8,128)(2,1)} %get-tuple-element.183.one_ref, ...), custom_call_target="tpu_custom_call" | custom-call | flops 11811160064 | bytes 37232640 | tf_op jit(solution)/shard_map/gated_unit_back/pallas_call | solution.py:374
  501.3 19.8 %fold_half.6 = bf16[2048,1024]{1,0:T(8,128)(2,1)} custom-call(s32[4]{0:T(128)S(1)} %pad_add_fusion.1.spots, bf16[2048,1408]{1,0:T(8,128)(2,1)} %copy-done.53, bf16[2048,1408]{1,0:T(8,128)(2,1)} %copy-done.49, bf16[1024,1408]{1,0:T(8,128)(2,1)S(1)} %copy-done.31, bf16[1024,1408]{1,0:T(8,128)(2,1)} %collective-permute-done.10.refs_1_.refs_3_.refs_4_, ...), custom_call_target="tpu_custom_call" | custom-call | flops 11811160064 | bytes 21495808 | tf_op jit(solution)/shard_map/fold_half/pallas_call | solution.py:435
  528.8 9.4 gradient_rows.9
  538.2 22.0 %fold_half.7 = (bf16[2048,512]{1,0:T(8,128)(2,1)}, f32[2048,512]{1,0:T(8,128)}) custom-call(s32[4]{0:T(128)S(1)} %pad_add_fusion.1.spots, bf16[2048,1408]{1,0:T(8,128)(2,1)} %copy-done.53, bf16[2048,1408]{1,0:T(8,128)(2,1)} %copy-done.49, bf16[2048,1024]{1,0:T(8,128)(2,1)} %collective-permute-done.21.refs_2_, bf16[1024,1408]{1,0:T(8,128)(2,1)S(1)} %copy-done.32, ...), custom_call_target="tpu_custom_call" | custom-call | flops 11811160064 | bytes 27787264 | tf_op jit(solution)/shard_map/fold_half/pallas_call | solution.py:435
  566.3 16.4 %gradient_rows.10 = bf16[2048,1408]{1,0:T(8,128)(2,1)S(1)} custom-call(s32[4]{0:T(128)S(1)} %pad_add_fusion.1.spots, bf16[2048,2048]{1,0:T(8,128)(2,1)} %get-tuple-element.173.left_ref, bf16[2048,1408]{1,0:T(8,128)(2,1)S(1)} %copy-done.54), custom_call_target="tpu_custom_call" | custom-call | flops 11811160064 | bytes 17301504 | tf_op jit(solution)/shard_map/gradient_rows/pallas_call | solution.py:470
  587.9 11.4 %fold_half.8 = bf16[2048,1024]{1,0:T(8,128)(2,1)} custom-call(s32[4]{0:T(128)S(1)} %pad_add_fusion.1.spots, bf16[2048,1408]{1,0:T(8,128)(2,1)S(1)} %copy-done.52, bf16[2048,1408]{1,0:T(8,128)(2,1)} %all-gather.17.cloned.1.call-done.refs_0_.refs_1_.refs_2_), custom_call_target="tpu_custom_call" | custom-call | flops 5905580032 | bytes 9961472 | tf_op jit(solution)/shard_map/fold_half/pallas_call | solution.py:435
  600.2 8.6 collective-permute-done.23
  609.1 6.0 multiply_reduce_fusion.2
  620.1 11.8 %convolution_convert_fusion.1 = bf16[2048,512]{1,0:T(8,128)(2,1)S(1)} fusion(f32[2048,512]{1,0:T(8,128)} %copy-done.55, f32[2048]{0:T(1024)S(1)} %add_rsqrt_fusion, bf16[2048,1024]{1,0:T(8,128)(2,1)} %collective-permute-done.13, bf16[2048,1024]{1,0:T(8,128)(2,1)} %maximum_select_fusion.2, pred[]{:T(512)S(6)} %eq.53), kind=kOutput, calls=%fused_computation.28 | convolution fusion | flops 4335861760 | bytes 14688257 | tf_op jit(solution)/shard_map/dot_general | solution.py:32
  633.8 7.7 collective-permute-done.29
  655.2 15.0 %fold_half.9 = (bf16[2048,512]{1,0:T(8,128)(2,1)}, f32[2048,512]{1,0:T(8,128)S(1)}) custom-call(s32[4]{0:T(128)S(1)} %pad_add_fusion.1.spots, bf16[2048,1408]{1,0:T(8,128)(2,1)} %get-tuple-element.195.right_ref.refs_0_, bf16[2048,1024]{1,0:T(8,128)(2,1)} %collective-permute-done.27.refs_1_, ...), custom_call_target="tpu_custom_call" | custom-call | flops 5905580032 | bytes 16252928 | tf_op jit(solution)/shard_map/fold_half/pallas_call | solution.py:435
  670.2 29.5 %collective-permute-done.32 = f32[2048]{0:T(1024)S(1)} collective-permute-done((f32[2048]{0:T(1024)S(1)}, f32[2048]{0:T(1024)S(1)}, u32[]{:S(2)}, u32[]{:S(2)}) %collective-permute-start.32) | collective-permute-done | bytes 8224 | tf_op jit(solution)/shard_map/ppermute | solution.py:543
  706.9 21.3 %attend_back.1 = (bf16[2048,512]{1,0:T(8,128)(2,1)S(1)}, bf16[2048,512]{1,0:T(8,128)(2,1)S(1)}, bf16[2048,512]{1,0:T(8,128)(2,1)S(1)}) custom-call(f32[4]{0:T(128)S(1)} %copy-done.29, s32[2,2]{1,0:T(2,128)S(1)} %copy-done.27, f32[2048,1024]{1,0:T(8,128)} %get-tuple-element.159.zq_ref.zk_ref, f32[2048,1024]{1,0:T(8,128)} %get-tuple-element.159.zq_ref.zk_ref, ...), custom_call_target="tpu_custom_call" | custom-call | flops 10737418240 | bytes 20971520 | tf_op jit(solution)/shard_map/attend_back/pallas_call | solution.py:119
  743.4 7.4 gradient_rows.11
  761.7 10.0 gradient_rows.12
  780.1 5.4 collective-permute-start.37
  786.1 7.3 gradient_rows.13
  794.8 14.9 %fold_half.10 = bf16[2048,1024]{1,0:T(8,128)(2,1)} custom-call(s32[4]{0:T(128)S(1)} %pad_add_fusion.1.spots, bf16[2048,1024]{1,0:T(8,128)(2,1)} %copy-done.7, bf16[2048,1024]{1,0:T(8,128)(2,1)} %pad_maximum_fusion.refs_1_.right_ref, bf16[1024,1024]{1,0:T(8,128)(2,1)S(1)} %copy-done.40, bf16[1024,1024]{1,0:T(8,128)(2,1)S(1)} %copy-done.47, ...), custom_call_target="tpu_custom_call" | custom-call | flops 8589934592 | bytes 16777216 | tf_op jit(solution)/shard_map/fold_half/pallas_call | solution.py:435
  813.2 5.6 collective-permute-start.41
  830.2 7.9 gradient_rows.14
  838.1 11.4 %collective-permute-done.42 = bf16[512,1024]{1,0:T(8,128)(2,1)S(1)} collective-permute-done((bf16[512,1024]{1,0:T(8,128)(2,1)}, bf16[512,1024]{1,0:T(8,128)(2,1)S(1)}, u32[]{:S(2)}, u32[]{:S(2)}) %collective-permute-start.42) | collective-permute-done | bytes 1048608 | tf_op jit(solution)/shard_map/ppermute | solution.py:543
  857.7 17.2 %fold_half.11 = (bf16[2048,512]{1,0:T(8,128)(2,1)}, f32[2048,512]{1,0:T(8,128)}) custom-call(s32[4]{0:T(128)S(1)} %pad_add_fusion.1.spots, bf16[2048,1024]{1,0:T(8,128)(2,1)} %copy-done.7, bf16[2048,1024]{1,0:T(8,128)(2,1)} %pad_maximum_fusion.refs_1_.right_ref, bf16[2048,1024]{1,0:T(8,128)(2,1)} %collective-permute-done.41.refs_2_, ...), custom_call_target="tpu_custom_call" | custom-call | flops 8589934592 | bytes 23068672 | tf_op jit(solution)/shard_map/fold_half/pallas_call | solution.py:435
  890.5 6.9 gradient_rows.15
  900.5 29.4 %collective-permute-done.47 = f32[2048]{0:T(1024)S(1)} collective-permute-done((f32[2048]{0:T(1024)S(1)}, f32[2048]{0:T(1024)S(1)}, u32[]{:S(2)}, u32[]{:S(2)}) %collective-permute-start.47) | collective-permute-done | bytes 8224 | tf_op jit(solution)/shard_map/ppermute | solution.py:543
  937.7 21.7 %collective-permute-done.50 = bf16[2,512,512]{2,1,0:T(8,128)(2,1)S(1)} collective-permute-done((bf16[2,512,512]{2,1,0:T(8,128)(2,1)S(1)}, bf16[2,512,512]{2,1,0:T(8,128)(2,1)S(1)}, u32[]{:S(2)}, u32[]{:S(2)}) %collective-permute-start.50) | collective-permute-done | bytes 1048608 | tf_op jit(solution)/shard_map/ppermute | solution.py:543
  972.5 7.8 place_quarters.5
  980.3 7.1 place_quarters.6
  991.4 22.4 %collective-permute-done.52 = bf16[256,2048]{1,0:T(8,128)(2,1)} collective-permute-done((bf16[256,2048]{1,0:T(8,128)(2,1)}, bf16[256,2048]{1,0:T(8,128)(2,1)}, u32[]{:S(2)}, u32[]{:S(2)}) %collective-permute-start.52) | collective-permute-done | bytes 1048608 | tf_op jit(solution)/shard_map/ppermute | solution.py:602
  1028.5 13.0 %collective-permute-done.57 = bf16[512,1024]{1,0:T(8,128)(2,1)} collective-permute-done((bf16[512,1024]{1,0:T(8,128)(2,1)S(1)}, bf16[512,1024]{1,0:T(8,128)(2,1)}, u32[]{:S(2)}, u32[]{:S(2)}) %collective-permute-start.57) | collective-permute-done | bytes 1048608 | tf_op jit(solution)/shard_map/ppermute | solution.py:543
  1041.5 5.3 collective-permute-done.61
  1046.8 14.4 %collective-permute-done.60 = bf16[256,2048]{1,0:T(8,128)(2,1)} collective-permute-done((bf16[256,2048]{1,0:T(8,128)(2,1)}, bf16[256,2048]{1,0:T(8,128)(2,1)}, u32[]{:S(2)}, u32[]{:S(2)}) %collective-permute-start.60) | collective-permute-done | bytes 1048608 | tf_op jit(solution)/shard_map/ppermute | solution.py:602
  1061.2 8.7 collective-permute-done.58
  1090.7 5.6 place_quarters.9
  (452 shorter events, 313.3 us)
Async XLA Ops:
  8.0 89.1 %all-gather.7.cloned.1.call-start = ((), (), s32[]{:S(2)}) async-start(), calls=%async_computation.6 | async-start | bytes 2621440 | tf_op jit(solution)/shard_map/all_gather | solution.py:664
  10.3 136.7 %all-gather.9.cloned.1.call-start = ((), (), s32[]{:S(2)}) async-start(), calls=%async_computation.7 | async-start | bytes 2621440 | tf_op jit(solution)/shard_map/all_gather | solution.py:664
  12.6 172.6 %all-gather.11.cloned.1.call-start = ((), (), s32[]{:S(2)}) async-start(), calls=%async_computation.8 | async-start | bytes 1310720 | tf_op jit(solution)/shard_map/all_gather | solution.py:664
  13.9 80.9 %collective-permute-start = (bf16[256,2048]{1,0:T(8,128)(2,1)}, bf16[256,2048]{1,0:T(8,128)(2,1)S(1)}, u32[]{:S(2)}, u32[]{:S(2)}) collective-permute-start(bf16[256,2048]{1,0:T(8,128)(2,1)} %get-tuple-element.324), channel_id=1, source_target_pairs={{0,0},{4,1},{1,2},{5,3},{2,4},{6,5},{3,6},{7,7},{8,8},{12,9},{9,10... | collective-permute-start | bytes 3145736 | tf_op jit(solution)/shard_map/ppermute | solution.py:594
  16.0 78.8 %collective-permute-start.1 = (bf16[256,2048]{1,0:T(8,128)(2,1)S(1)}, bf16[256,2048]{1,0:T(8,128)(2,1)S(1)}, u32[]{:S(2)}, u32[]{:S(2)}) collective-permute-start(bf16[256,2048]{1,0:T(8,128)(2,1)S(1)} %get-tuple-element.325), channel_id=1, source_target_pairs={{1,0},{5,1},{0,2},{4,3},{3,4},{7,5},{2,6},{6,7},{9,8},{13,9},{8,10... | collective-permute-start | bytes 3145736 | tf_op jit(solution)/shard_map/ppermute | solution.py:594
  97.1 43.7 %collective-permute-start.2 = (bf16[512,2048]{1,0:T(8,128)(2,1)}, bf16[512,2048]{1,0:T(8,128)(2,1)}, u32[]{:S(2)}, u32[]{:S(2)}) collective-permute-start(bf16[512,2048]{1,0:T(8,128)(2,1)} %maximum_select_fusion.6), channel_id=1, source_target_pairs={{0,8},{1,9},{2,10},{3,11},{4,12},{5,13},{6,14},{7,15},{8,0},{9,1},... | collective-permute-start | bytes 6291464 | tf_op jit(solution)/shard_map/ppermute | solution.py:543
  99.0 139.1 %all-gather.13.cloned.1.call-start = ((), (), s32[]{:S(2)}) async-start(), calls=%async_computation.9 | async-start | bytes 3604480 | tf_op jit(solution)/shard_map/all_gather | solution.py:664
  99.1 47.9 %collective-permute-start.3 = (bf16[1024,1024]{1,0:T(8,128)(2,1)}, bf16[1024,1024]{1,0:T(8,128)(2,1)S(1)}, u32[]{:S(2)}, u32[]{:S(2)}) collective-permute-start(bf16[1024,1024]{1,0:T(8,128)(2,1)} %all-gather.7.cloned.1.call-done.refs_0_.refs_2_.refs_3_), channel_id=1, source_target_pairs={{0,16},{1,17},{2,18},{3,19},{4,20},{5,21},{6,22},{7,23},{8,24},{9,... | collective-permute-start | bytes 6291464 | tf_op jit(solution)/shard_map/ppermute | solution.py:543
  102.8 189.0 %all-gather.15.cloned.1.call-start = ((), (), s32[]{:S(2)}) async-start(), calls=%async_computation.10 | async-start | bytes 3604480 | tf_op jit(solution)/shard_map/all_gather | solution.py:664
  151.7 47.5 %collective-permute-start.5 = (bf16[1024,1024]{1,0:T(8,128)(2,1)}, bf16[1024,1024]{1,0:T(8,128)(2,1)}, u32[]{:S(2)}, u32[]{:S(2)}) collective-permute-start(bf16[1024,1024]{1,0:T(8,128)(2,1)} %all-gather.9.cloned.1.call-done.refs_0_.refs_4_.refs_5_), channel_id=1, source_target_pairs={{0,16},{1,17},{2,18},{3,19},{4,20},{5,21},{6,22},{7,23},{8,24},{9,... | collective-permute-start | bytes 6291464 | tf_op jit(solution)/shard_map/ppermute | solution.py:543
  157.9 315.0 %all-gather.17.cloned.1.call-start = ((), (), s32[]{:S(2)}) async-start(), calls=%async_computation.11 | async-start | bytes 6488064 | tf_op jit(solution)/shard_map/all_gather | solution.py:668
  199.2 38.9 %collective-permute-start.8 = (bf16[1024,512]{1,0:T(8,128)(2,1)}, bf16[1024,512]{1,0:T(8,128)(2,1)}, u32[]{:S(2)}, u32[]{:S(2)}) collective-permute-start(bf16[1024,512]{1,0:T(8,128)(2,1)} %all-gather.11.cloned.1.call-done), channel_id=1, source_target_pairs={{0,16},{1,17},{2,18},{3,19},{4,20},{5,21},{6,22},{7,23},{8,24},{9,... | collective-permute-start | bytes 3145736 | tf_op jit(solution)/shard_map/ppermute | solution.py:543
  238.1 63.1 %collective-permute-start.10 = (bf16[1024,1408]{1,0:T(8,128)(2,1)}, bf16[1024,1408]{1,0:T(8,128)(2,1)}, u32[]{:S(2)}, u32[]{:S(2)}) collective-permute-start(bf16[1024,1408]{1,0:T(8,128)(2,1)} %all-gather.13.cloned.1.call-done.refs_0_.refs_2_.refs_3_), channel_id=1, source_target_pairs={{0,16},{1,17},{2,18},{3,19},{4,20},{5,21},{6,22},{7,23},{8,24},{9,... | collective-permute-start | bytes 8650760 | tf_op jit(solution)/shard_map/ppermute | solution.py:543
  238.3 46.2 %collective-permute-start.9 = (bf16[2048,512]{1,0:T(8,128)(2,1)}, bf16[2048,512]{1,0:T(8,128)(2,1)S(1)}, u32[]{:S(2)}, u32[]{:S(2)}) collective-permute-start(bf16[2048,512]{1,0:T(8,128)(2,1)} %get-tuple-element.162), channel_id=1, source_target_pairs={{0,8},{1,9},{2,10},{3,11},{4,12},{5,13},{6,14},{7,15},{8,0},{9,1},... | collective-permute-start | bytes 6291464 | tf_op jit(solution)/shard_map/ppermute | solution.py:543
  242.1 42.5 %collective-permute-start.12 = (f32[2048]{0:T(1024)S(1)}, f32[2048]{0:T(1024)S(1)}, u32[]{:S(2)}, u32[]{:S(2)}) collective-permute-start(f32[2048]{0:T(1024)S(1)} %add.256), channel_id=1, source_target_pairs={{0,8},{1,9},{2,10},{3,11},{4,12},{5,13},{6,14},{7,15},{8,0},{9,1},... | collective-permute-start | bytes 24584 | tf_op jit(solution)/shard_map/ppermute | solution.py:543
  307.5 69.0 %collective-permute-start.15 = (bf16[1024,1408]{1,0:T(8,128)(2,1)S(1)}, bf16[1024,1408]{1,0:T(8,128)(2,1)S(1)}, u32[]{:S(2)}, u32[]{:S(2)}) collective-permute-start(bf16[1024,1408]{1,0:T(8,128)(2,1)S(1)} %copy-done.33), channel_id=1, source_target_pairs={{0,16},{1,17},{2,18},{3,19},{4,20},{5,21},{6,22},{7,23},{8,24},{9,... | collective-permute-start | bytes 8650760 | tf_op jit(solution)/shard_map/ppermute | solution.py:543
  320.2 53.6 %collective-permute-start.14 = (bf16[2048,512]{1,0:T(8,128)(2,1)}, bf16[2048,512]{1,0:T(8,128)(2,1)S(1)}, u32[]{:S(2)}, u32[]{:S(2)}) collective-permute-start(bf16[2048,512]{1,0:T(8,128)(2,1)} %get-tuple-element.328), channel_id=1, source_target_pairs={{0,8},{1,9},{2,10},{3,11},{4,12},{5,13},{6,14},{7,15},{8,0},{9,1},... | collective-permute-start | bytes 6291464 | tf_op jit(solution)/shard_map/ppermute | solution.py:543
  323.2 48.2 %collective-permute-start.16 = (bf16[256,2048]{1,0:T(8,128)(2,1)S(1)}, bf16[256,2048]{1,0:T(8,128)(2,1)S(1)}, u32[]{:S(2)}, u32[]{:S(2)}) collective-permute-start(bf16[256,2048]{1,0:T(8,128)(2,1)S(1)} %get-tuple-element.320), channel_id=1, source_target_pairs={{0,0},{4,1},{1,2},{5,3},{2,4},{6,5},{3,6},{7,7},{8,8},{12,9},{9,10... | collective-permute-start | bytes 3145736 | tf_op jit(solution)/shard_map/ppermute | solution.py:594
  328.2 43.2 %collective-permute-start.17 = (bf16[256,2048]{1,0:T(8,128)(2,1)S(1)}, bf16[256,2048]{1,0:T(8,128)(2,1)S(1)}, u32[]{:S(2)}, u32[]{:S(2)}) collective-permute-start(bf16[256,2048]{1,0:T(8,128)(2,1)S(1)} %get-tuple-element.321), channel_id=1, source_target_pairs={{1,0},{5,1},{0,2},{4,3},{3,4},{7,5},{2,6},{6,7},{9,8},{13,9},{8,10... | collective-permute-start | bytes 3145736 | tf_op jit(solution)/shard_map/ppermute | solution.py:594
  383.8 225.0 %reduce-scatter.7.cloned.1.call-start = ((), (), s32[]{:S(2)}) async-start(), calls=%async_computation.12 | async-start | bytes 6488064 | tf_op jit(solution)/shard_map/reduce_scatter | solution.py:708
  384.4 47.6 %collective-permute-start.19 = (bf16[512,2048]{1,0:T(8,128)(2,1)}, bf16[512,2048]{1,0:T(8,128)(2,1)S(1)}, u32[]{:S(2)}, u32[]{:S(2)}) collective-permute-start(bf16[512,2048]{1,0:T(8,128)(2,1)} %maximum_select_fusion.8), channel_id=1, source_target_pairs={{0,8},{1,9},{2,10},{3,11},{4,12},{5,13},{6,14},{7,15},{8,0},{9,1},... | collective-permute-start | bytes 6291464 | tf_op jit(solution)/shard_map/ppermute | solution.py:543
  472.9 304.5 %reduce-scatter.9.cloned.1.call-start = ((), (), s32[]{:S(2)}) async-start(), calls=%async_computation.13 | async-start | bytes 6488064 | tf_op jit(solution)/shard_map/reduce_scatter | solution.py:708
  560.2 39.0 %collective-permute-start.25 = (f32[2048]{0:T(1024)S(1)}, f32[2048]{0:T(1024)S(1)}, u32[]{:S(2)}, u32[]{:S(2)}) collective-permute-start(f32[2048]{0:T(1024)S(1)} %add.261), channel_id=1, source_target_pairs={{0,8},{1,9},{2,10},{3,11},{4,12},{5,13},{6,14},{7,15},{8,0},{9,1},... | collective-permute-start | bytes 24584 | tf_op jit(solution)/shard_map/ppermute | solution.py:543
  561.5 47.4 %collective-permute-start.23 = (bf16[2048,512]{1,0:T(8,128)(2,1)}, bf16[2048,512]{1,0:T(8,128)(2,1)}, u32[]{:S(2)}, u32[]{:S(2)}) collective-permute-start(bf16[2048,512]{1,0:T(8,128)(2,1)} %get-tuple-element.194), channel_id=1, source_target_pairs={{0,8},{1,9},{2,10},{3,11},{4,12},{5,13},{6,14},{7,15},{8,0},{9,1},... | collective-permute-start | bytes 6291464 | tf_op jit(solution)/shard_map/ppermute | solution.py:543
  563.7 36.6 %collective-permute-start.24 = (bf16[512,1408]{1,0:T(8,128)(2,1)}, bf16[512,1408]{1,0:T(8,128)(2,1)}, u32[]{:S(2)}, u32[]{:S(2)}) collective-permute-start(bf16[512,1408]{1,0:T(8,128)(2,1)} %get-tuple-element.301), channel_id=1, source_target_pairs={{0,16},{1,17},{2,18},{3,19},{4,20},{5,21},{6,22},{7,23},{8,24},{9,... | collective-permute-start | bytes 4325384 | tf_op jit(solution)/shard_map/ppermute | solution.py:543
  608.9 291.6 %reduce-scatter.15.cloned.1.call-start = ((), (), s32[]{:S(2)}) async-start(), calls=%async_computation.16 | async-start | bytes 1310720 | tf_op jit(solution)/shard_map/reduce_scatter | solution.py:702
  653.3 46.5 %collective-permute-start.30 = (bf16[2048,512]{1,0:T(8,128)(2,1)}, bf16[2048,512]{1,0:T(8,128)(2,1)}, u32[]{:S(2)}, u32[]{:S(2)}) collective-permute-start(bf16[2048,512]{1,0:T(8,128)(2,1)} %dynamic-slice_convert_fusion), channel_id=1, source_target_pairs={{0,8},{1,9},{2,10},{3,11},{4,12},{5,13},{6,14},{7,15},{8,0},{9,1},... | collective-permute-start | bytes 6291464 | tf_op jit(solution)/shard_map/ppermute | solution.py:543
  654.4 45.3 %collective-permute-start.31 = (bf16[1024,512]{1,0:T(8,128)(2,1)S(1)}, bf16[1024,512]{1,0:T(8,128)(2,1)}, u32[]{:S(2)}, u32[]{:S(2)}) collective-permute-start(bf16[1024,512]{1,0:T(8,128)(2,1)S(1)} %get-tuple-element.216), channel_id=1, source_target_pairs={{0,16},{1,17},{2,18},{3,19},{4,20},{5,21},{6,22},{7,23},{8,24},{9,... | collective-permute-start | bytes 3145736 | tf_op jit(solution)/shard_map/ppermute | solution.py:543
  655.1 44.7 %collective-permute-start.32 = (f32[2048]{0:T(1024)S(1)}, f32[2048]{0:T(1024)S(1)}, u32[]{:S(2)}, u32[]{:S(2)}) collective-permute-start(f32[2048]{0:T(1024)S(1)} %add.275), channel_id=1, source_target_pairs={{0,8},{1,9},{2,10},{3,11},{4,12},{5,13},{6,14},{7,15},{8,0},{9,1},... | collective-permute-start | bytes 24584 | tf_op jit(solution)/shard_map/ppermute | solution.py:543
  699.8 51.0 %collective-permute-start.33 = (bf16[512,1408]{1,0:T(8,128)(2,1)}, bf16[512,1408]{1,0:T(8,128)(2,1)}, u32[]{:S(2)}, u32[]{:S(2)}) collective-permute-start(bf16[512,1408]{1,0:T(8,128)(2,1)} %get-tuple-element.223), channel_id=1, source_target_pairs={{0,16},{1,17},{2,18},{3,19},{4,20},{5,21},{6,22},{7,23},{8,24},{9,... | collective-permute-start | bytes 4325384 | tf_op jit(solution)/shard_map/ppermute | solution.py:543
  700.5 50.3 %collective-permute-start.34 = (bf16[2048,512]{1,0:T(8,128)(2,1)}, bf16[2048,512]{1,0:T(8,128)(2,1)}, u32[]{:S(2)}, u32[]{:S(2)}) collective-permute-start(bf16[2048,512]{1,0:T(8,128)(2,1)} %get-tuple-element.224), channel_id=1, source_target_pairs={{0,8},{1,9},{2,10},{3,11},{4,12},{5,13},{6,14},{7,15},{8,0},{9,1},... | collective-permute-start | bytes 6291464 | tf_op jit(solution)/shard_map/ppermute | solution.py:543
  734.7 165.8 %reduce-scatter.13.cloned.1.call-start = ((), (), s32[]{:S(2)}) async-start(), calls=%async_computation.15 | async-start | bytes 3604480 | tf_op jit(solution)/shard_map/reduce_scatter | solution.py:702
  755.7 54.1 %collective-permute-start.39 = (bf16[512,1408]{1,0:T(8,128)(2,1)}, bf16[512,1408]{1,0:T(8,128)(2,1)}, u32[]{:S(2)}, u32[]{:S(2)}) collective-permute-start(bf16[512,1408]{1,0:T(8,128)(2,1)} %maximum_select_fusion.16), channel_id=1, source_target_pairs={{0,8},{1,9},{2,10},{3,11},{4,12},{5,13},{6,14},{7,15},{8,0},{9,1},... | collective-permute-start | bytes 4325384 | tf_op jit(solution)/shard_map/ppermute | solution.py:543
  777.9 190.3 %reduce-scatter.17.cloned.1.call-start = ((), (), s32[]{:S(2)}) async-start(), calls=%async_computation.17 | async-start | bytes 2621440 | tf_op jit(solution)/shard_map/reduce_scatter | solution.py:702
  813.2 36.3 %collective-permute-start.41 = (bf16[2048,1024]{1,0:T(8,128)(2,1)}, bf16[2048,1024]{1,0:T(8,128)(2,1)}, u32[]{:S(2)}, u32[]{:S(2)}) collective-permute-start(bf16[2048,1024]{1,0:T(8,128)(2,1)} %fold_half.10), channel_id=1, source_target_pairs={{0,4},{1,5},{2,6},{3,7},{4,0},{5,1},{6,2},{7,3},{8,12},{9,13},{10,... | collective-permute-start | bytes 12582920 | tf_op jit(solution)/shard_map/ppermute | solution.py:543
  821.8 53.1 %collective-permute-start.45 = (bf16[512,1408]{1,0:T(8,128)(2,1)}, bf16[512,1408]{1,0:T(8,128)(2,1)}, u32[]{:S(2)}, u32[]{:S(2)}) collective-permute-start(bf16[512,1408]{1,0:T(8,128)(2,1)} %maximum_select_fusion.17), channel_id=1, source_target_pairs={{0,8},{1,9},{2,10},{3,11},{4,12},{5,13},{6,14},{7,15},{8,0},{9,1},... | collective-permute-start | bytes 4325384 | tf_op jit(solution)/shard_map/ppermute | solution.py:543
  850.5 120.8 %reduce-scatter.11.cloned.1.call-start = ((), (), s32[]{:S(2)}) async-start(), calls=%async_computation.14 | async-start | bytes 2621440 | tf_op jit(solution)/shard_map/reduce_scatter | solution.py:702
  856.5 44.0 %collective-permute-start.49 = (bf16[512,2816]{1,0:T(8,128)(2,1)}, bf16[512,2816]{1,0:T(8,128)(2,1)}, u32[]{:S(2)}, u32[]{:S(2)}) collective-permute-start(bf16[512,2816]{1,0:T(8,128)(2,1)} %constant_dynamic-update-slice_fusion.2.refs_0_.refs_1_), channel_id=1, source_target_pairs={{0,4},{1,5},{2,6},{3,7},{4,0},{5,1},{6,2},{7,3},{8,12},{9,13},{10,... | collective-permute-start | bytes 8650760 | tf_op jit(solution)/shard_map/ppermute | solution.py:543
  880.3 49.6 %collective-permute-start.48 = (bf16[512,2816]{1,0:T(8,128)(2,1)S(1)}, bf16[512,2816]{1,0:T(8,128)(2,1)}, u32[]{:S(2)}, u32[]{:S(2)}) collective-permute-start(bf16[512,2816]{1,0:T(8,128)(2,1)S(1)} %pad_maximum_fusion.2.refs_0_.refs_1_), channel_id=1, source_target_pairs={{0,4},{1,5},{2,6},{3,7},{4,0},{5,1},{6,2},{7,3},{8,12},{9,13},{10,... | collective-permute-start | bytes 8650760 | tf_op jit(solution)/shard_map/ppermute | solution.py:543
  882.2 47.7 %collective-permute-start.46 = (bf16[2048,512]{1,0:T(8,128)(2,1)}, bf16[2048,512]{1,0:T(8,128)(2,1)}, u32[]{:S(2)}, u32[]{:S(2)}) collective-permute-start(bf16[2048,512]{1,0:T(8,128)(2,1)} %get-tuple-element.255), channel_id=1, source_target_pairs={{0,8},{1,9},{2,10},{3,11},{4,12},{5,13},{6,14},{7,15},{8,0},{9,1},... | collective-permute-start | bytes 6291464 | tf_op jit(solution)/shard_map/ppermute | solution.py:543
  888.4 41.5 %collective-permute-start.47 = (f32[2048]{0:T(1024)S(1)}, f32[2048]{0:T(1024)S(1)}, u32[]{:S(2)}, u32[]{:S(2)}) collective-permute-start(f32[2048]{0:T(1024)S(1)} %add.284), channel_id=1, source_target_pairs={{0,8},{1,9},{2,10},{3,11},{4,12},{5,13},{6,14},{7,15},{8,0},{9,1},... | collective-permute-start | bytes 24584 | tf_op jit(solution)/shard_map/ppermute | solution.py:543
  964.9 48.9 %collective-permute-start.52 = (bf16[256,2048]{1,0:T(8,128)(2,1)}, bf16[256,2048]{1,0:T(8,128)(2,1)}, u32[]{:S(2)}, u32[]{:S(2)}) collective-permute-start(bf16[256,2048]{1,0:T(8,128)(2,1)} %get-tuple-element.305), channel_id=1, source_target_pairs={{0,0},{1,4},{2,1},{3,5},{4,2},{5,6},{6,3},{7,7},{8,8},{9,12},{10,9... | collective-permute-start | bytes 3145736 | tf_op jit(solution)/shard_map/ppermute | solution.py:602
  970.2 43.6 %collective-permute-start.55 = (bf16[256,1536]{1,0:T(8,128)(2,1)}, bf16[256,1536]{1,0:T(8,128)(2,1)}, u32[]{:S(2)}, u32[]{:S(2)}) collective-permute-start(bf16[256,1536]{1,0:T(8,128)(2,1)} %pad_maximum_fusion.7), channel_id=1, source_target_pairs={{0,8},{1,9},{2,10},{3,11},{4,12},{5,13},{6,14},{7,15},{8,0},{9,1},... | collective-permute-start | bytes 2359304 | tf_op jit(solution)/shard_map/ppermute | solution.py:543
  971.0 42.8 %collective-permute-start.54 = (bf16[256,1408]{1,0:T(8,128)(2,1)}, bf16[256,1408]{1,0:T(8,128)(2,1)}, u32[]{:S(2)}, u32[]{:S(2)}) collective-permute-start(bf16[256,1408]{1,0:T(8,128)(2,1)} %reduce-scatter.13.cloned.1.call-done), channel_id=1, source_target_pairs={{0,16},{1,17},{2,18},{3,19},{4,20},{5,21},{6,22},{7,23},{8,24},{9,... | collective-permute-start | bytes 2162696 | tf_op jit(solution)/shard_map/ppermute | solution.py:543
  971.4 42.5 %collective-permute-start.56 = (bf16[256,1024]{1,0:T(8,128)(2,1)}, bf16[256,1024]{1,0:T(8,128)(2,1)S(1)}, u32[]{:S(2)}, u32[]{:S(2)}) collective-permute-start(bf16[256,1024]{1,0:T(8,128)(2,1)} %reduce-scatter.11.cloned.1.call-done), channel_id=1, source_target_pairs={{0,16},{1,17},{2,18},{3,19},{4,20},{5,21},{6,22},{7,23},{8,24},{9,... | collective-permute-start | bytes 1572872 | tf_op jit(solution)/shard_map/ppermute | solution.py:543
  1017.0 53.0 %collective-permute-start.58 = (bf16[512,1408]{1,0:T(8,128)(2,1)S(1)}, bf16[512,1408]{1,0:T(8,128)(2,1)}, u32[]{:S(2)}, u32[]{:S(2)}) collective-permute-start(bf16[512,1408]{1,0:T(8,128)(2,1)S(1)} %maximum_select_fusion.18), channel_id=1, source_target_pairs={{0,8},{1,9},{2,10},{3,11},{4,12},{5,13},{6,14},{7,15},{8,0},{9,1},... | collective-permute-start | bytes 4325384 | tf_op jit(solution)/shard_map/ppermute | solution.py:543
  1019.7 50.3 %collective-permute-start.59 = (bf16[256,3072]{1,0:T(8,128)(2,1)}, bf16[256,3072]{1,0:T(8,128)(2,1)}, u32[]{:S(2)}, u32[]{:S(2)}) collective-permute-start(bf16[256,3072]{1,0:T(8,128)(2,1)} %constant_dynamic-update-slice_fusion.4), channel_id=1, source_target_pairs={{0,16},{1,17},{2,18},{3,19},{4,20},{5,21},{6,22},{7,23},{8,24},{9,... | collective-permute-start | bytes 4718600 | tf_op jit(solution)/shard_map/ppermute | solution.py:543
  1022.3 38.9 %collective-permute-start.60 = (bf16[256,2048]{1,0:T(8,128)(2,1)}, bf16[256,2048]{1,0:T(8,128)(2,1)}, u32[]{:S(2)}, u32[]{:S(2)}) collective-permute-start(bf16[256,2048]{1,0:T(8,128)(2,1)} %get-tuple-element.303), channel_id=1, source_target_pairs={{0,0},{1,4},{2,1},{3,5},{4,2},{5,6},{6,3},{7,7},{8,8},{9,12},{10,9... | collective-permute-start | bytes 3145736 | tf_op jit(solution)/shard_map/ppermute | solution.py:602
  (120 other events, 2167.5 us)
Sparse Core Ops, SparseCore 0:
  11.0 82.9 all-gather.6
  96.1 46.1 all-gather.8
  144.4 27.5 all-gather.10
  174.0 57.8 all-gather.12
  233.9 57.8 all-gather.14
Sparse Core Ops, SparseCore 1:
  383.9 88.8 all-gather.16
  476.3 107.8 reduce-scatter.6
  608.9 126.8 reduce-scatter.8
  738.1 25.1 reduce-scatter.14
  778.0 60.8 reduce-scatter.12
  850.6 43.0 reduce-scatter.16
  898.9 43.4 reduce-scatter.10

commit v15 on v14

--- a/solution.py
+++ b/solution.py
@@ -596,16 +596,17 @@
         ]
         return ordered(batch_of(place), *arrived, 0)
 
-    def send_back(x):
+    def back_slots(x):
         slots = natural(x).reshape(2, run, width)
         return [
-            lax.ppermute(
-                lax.dynamic_index_in_dim(slots, (batch_of(place) + p) % 2, 0, False),
-                AXES,
-                [(to, origin) for origin, to in routes(p)],
-            )
-            for p in range(2)
+            lax.dynamic_index_in_dim(slots, (batch_of(place) + p) % 2, 0, False) for p in range(2)
         ]
+
+    def send_slot(x, p):
+        return lax.ppermute(x, AXES, [(to, origin) for origin, to in routes(p)])
+
+    def send_back(x):
+        return [send_slot(slot, p) for p, slot in enumerate(back_slots(x))]
 
     def as_batches(arrived):
         return ordered(place % 2, arrived[0][None], arrived[1][None], 0)
@@ -898,25 +899,29 @@
     f_vg = scattered(gradient_rows(spots, spread, 0, hidden_one, d_vg, stacked(vg_a, vg_b)))
     four_down = spread_c(joined(y_down, x_down))
     four_one = spread_c(joined(y_one, x_one))
-    crossed, lean_b, four_one, four_down, f_two, f_out = tie(
-        crossed, lean_b, four_one, four_down, f_two, f_out
+    y_two = over_spread(f_two)
+    out_one, out_two = back_slots(ordered(c, output, out_c, 1))
+    crossed, lean_b, four_one, four_down, y_two, f_out, out_one, out_two = tie(
+        crossed, lean_b, four_one, four_down, y_two, f_out, out_one, out_two
     )
 
     d_hidden = mine + crossed.astype(F32)
     x_normed = x_own.astype(F32) * x_scale
     lean = (lean_x + lean_b)[:, None] / width
-    input_grad = to_runs((d_middle + x_scale * (d_hidden - x_normed * lean)).astype(LOW))
-    output = send_back(ordered(c, output, out_c, 1))
+    input_grad = (d_middle + x_scale * (d_hidden - x_normed * lean)).astype(LOW)
+    input_grad, grad_b = away_b(input_grad)
+    out_one = send_slot(out_one, 0)
+    input_grad, grad_b, out_one, out_two = tie(input_grad, grad_b, out_one, out_two)
+
+    input_grad, grad_c = away_c(input_grad, grad_b)
+    out_two = send_slot(out_two, 1)
     f_oqk = joined(f_out, f_qk)
     x_oqk = swap_b(f_oqk)
-    y_two = over_spread(f_two)
     y_vg = over_spread(f_vg)
     units = f_one.shape[1]
     [g_down] = place_quarters(spots, four_down, (0, units))
     [g_one] = place_quarters(spots, four_one, (0, units))
-    input_grad, output, y_two, x_oqk, y_vg, g_down, g_one = tie(
-        input_grad, output, y_two, x_oqk, y_vg, g_down, g_one
-    )
+    grad_c, out_two, x_oqk, y_vg, g_down, g_one = tie(grad_c, out_two, x_oqk, y_vg, g_down, g_one)
 
     y_vg = by_spread([f_vg, *y_vg])
     x_vg = swap_b(y_vg)
@@ -924,8 +929,8 @@
     x_two = swap_b(y_two)
     f_oqk = joined(f_oqk, x_oqk)
     y_oqk = over_spread(f_oqk)
-    input_grad = send_back(input_grad)
-    output = as_batches(output)
+    input_grad = send_back(ordered(c, input_grad, grad_c, 1))
+    output = as_batches([out_one, out_two])
     x_vg, x_two, y_oqk, input_grad, output = tie(x_vg, x_two, y_oqk, input_grad, output)
 
     four_vg = spread_c(joined(y_vg, x_vg))

time: 1120 us -> 1120 us (level)
  waiting for transfers between devices: 438 us -> 413 us
  starting transfers between devices: 76 us -> 98.4 us
    ppermute x4, waiting for transfers between devices: 42.2 us -> 10.8 us  [send_slot(): return lax.ppermute(x, AXES, [(to, origin) for origin, to in routes(p)])]
    reduce_scatter x2, starting transfers between devices: 0.55 us -> 13.8 us  [scattered_all(): return lax.psum_scatter(x, OWNERS, scatter_dimension=0, tiled=True)]
    ppermute x57, waiting for transfers between devices: 269 us -> 281 us  [move(): return lax.ppermute(x, AXES, pairs)]
    unnamed x208 -> x180, local copies, waits for them, and re-layouts: 66.9 us -> 60.8 us
  transfers between devices with their start and end apart: 77 -> 77, of which waited for: 31 -> 28; matrix products, arithmetic and copies ran while one was open for 15% -> 16% of each run, Pallas kernels for 31% -> 30%
where the time goes in v15:
time: 1120 us; the launch traced here: 1110 us
  waiting for transfers between devices  413 us (37%)
  Pallas kernels  342 us (31%)
  other arithmetic  107 us (10%)
  local copies, waits for them, and re-layouts  102 us (9%)
  starting transfers between devices  98.4 us (9%)
  matrix products  30.9 us (3%)
  between operations  17.1 us (2%)
    ppermute x57, waiting for transfers between devices, move(): return lax.ppermute(x, AXES, pairs)  281 us
    ppermute x4, waiting for transfers between devices, bring(): lax.ppermute(lax.dynamic_index_in_dim(x, (place + p) % 2, 0, False), AXES...  119 us
    pallas_call x6, Pallas kernels, fold_half(): pl.pallas_call(functools.partial(fold_kernel, len(values), arrived is not...  98.1 us
    pallas_call x8, Pallas kernels, gradient_rows(): pl.pallas_call(gradient_kernel, out_shape=out, grid_spec=pltpu.PrefetchSc...  81.8 us
    ppermute x57, starting transfers between devices, move(): return lax.ppermute(x, AXES, pairs)  68.5 us
    unnamed x180, local copies, waits for them, and re-layouts  60.8 us
    select_n x23, other arithmetic, ordered(): jnp.where(index == 0, jnp.concatenate([mine, other], axis), jnp.concatena...  48.4 us
    pallas_call x1, Pallas kernels, gated_unit(): pl.pallas_call(unit_kernel, out_shape=outs, grid_spec=pltpu.PrefetchScala...  38 us
  transfers between devices with their start and end apart: 77, of which 28 were waited for; matrix products, arithmetic and copies ran while one was open for 16% of the time, Pallas kernels for 30%

profile of v15, /device:TPU:17, one launch (start us, length us, event | category | flops | bytes accessed | tf_op | source)
XLA Modules:
  0.0 1110.0 jit_solution(647992858058698685)
XLA Ops:
  18.8 75.9 %collective-permute-done = bf16[256,2048]{1,0:T(8,128)(2,1)S(1)} collective-permute-done((bf16[256,2048]{1,0:T(8,128)(2,1)}, bf16[256,2048]{1,0:T(8,128)(2,1)S(1)}, u32[]{:S(2)}, u32[]{:S(2)}) %collective-permute-start) | collective-permute-done | bytes 1048608 | tf_op jit(solution)/shard_map/ppermute | solution.py:594
  102.9 37.9 %collective-permute-done.2 = bf16[512,2048]{1,0:T(8,128)(2,1)} collective-permute-done((bf16[512,2048]{1,0:T(8,128)(2,1)}, bf16[512,2048]{1,0:T(8,128)(2,1)}, u32[]{:S(2)}, u32[]{:S(2)}) %collective-permute-start.2) | collective-permute-done | bytes 2097184 | tf_op jit(solution)/shard_map/ppermute | solution.py:543
  140.8 6.0 maximum_select_fusion.1.own_ref
  165.5 18.8 %enter.2 = (bf16[2048,2048]{1,0:T(8,128)(2,1)}, f32[2048,1024]{1,0:T(8,128)}, f32[2048,1]{1,0:T(8,128)S(1)}, bf16[2048,512]{1,0:T(8,128)(2,1)S(1)}) custom-call(s32[4]{0:T(128)S(1)} %pad_add_fusion.1.spots, bf16[1024,2048]{1,0:T(8,128)(2,1)S(1)} %copy-done.13, bf16[1024,2048]{1,0:T(8,128)(2,1)} %collective-permute-done.4.other_ref, ...), custom_call_target="tpu_custom_call" | custom-call | flops 8589934592 | bytes 31465472 | tf_op jit(solution)/shard_map/enter/pallas_call | solution.py:244
  184.4 14.7 %collective-permute-done.5.refs_1_.refs_5_.refs_6_ = bf16[1024,1024]{1,0:T(8,128)(2,1)} collective-permute-done((bf16[1024,1024]{1,0:T(8,128)(2,1)}, bf16[1024,1024]{1,0:T(8,128)(2,1)}, u32[]{:S(2)}, u32[]{:S(2)}) %collective-permute-start.5) | collective-permute-done | bytes 2097184 | tf_op jit(solution)/shard_map/ppermute | solution.py:543
  201.9 14.2 %project.1.zv_ref = f32[2048,1024]{1,0:T(8,128)S(1)} custom-call(s32[4]{0:T(128)S(1)} %pad_add_fusion.1.spots, bf16[2048,2048]{1,0:T(8,128)(2,1)} %get-tuple-element.161.h_ref.left_ref, bf16[1024,1024]{1,0:T(8,128)(2,1)S(1)} %copy-done.29, bf16[1024,1024]{1,0:T(8,128)(2,1)} %collective-permute-done.5.refs_1_.refs_5_.refs_6_), custom_call_target="tpu_custom_call" | custom-call | flops 8589934592 | bytes 20971520 | tf_op jit(solution)/shard_map/project/pallas_call | solution.py:275
  219.6 12.3 %attend.1 = f32[2048,512]{1,0:T(8,128)S(1)} custom-call(f32[4]{0:T(128)S(1)} %dynamic_slice.129.rates, s32[2,2]{1,0:T(2,128)S(1)} %pad_add_fusion.ends, f32[2048,1024]{1,0:T(8,128)S(1)} %copy-done, f32[2048,1024]{1,0:T(8,128)S(1)} %copy-done, f32[2048,1024]{1,0:T(8,128)} %copy-done.1), custom_call_target="tpu_custom_call" | custom-call | flops 4294967296 | bytes 16777216 | tf_op jit(solution)/shard_map/attend/pallas_call | solution.py:98
  242.1 42.2 %collective-permute-done.12 = f32[2048]{0:T(1024)S(1)} collective-permute-done((f32[2048]{0:T(1024)S(1)}, f32[2048]{0:T(1024)S(1)}, u32[]{:S(2)}, u32[]{:S(2)}) %collective-permute-start.12) | collective-permute-done | bytes 8224 | tf_op jit(solution)/shard_map/ppermute | solution.py:543
  291.8 9.3 collective-permute-done.10.refs_1_.refs_3_.refs_4_
  310.3 9.6 fusion.21
  327.9 43.1 %collective-permute-done.16 = bf16[256,2048]{1,0:T(8,128)(2,1)S(1)} collective-permute-done((bf16[256,2048]{1,0:T(8,128)(2,1)S(1)}, bf16[256,2048]{1,0:T(8,128)(2,1)S(1)}, u32[]{:S(2)}, u32[]{:S(2)}) %collective-permute-start.16) | collective-permute-done | bytes 1048608 | tf_op jit(solution)/shard_map/ppermute | solution.py:594
  383.4 13.8 %reduce-scatter.7.cloned.1.call-start = ((), (), s32[]{:S(2)}) async-start(), calls=%async_computation.12 | async-start | bytes 6488064 | tf_op jit(solution)/shard_map/reduce_scatter | solution.py:709
  399.3 38.0 %gated_unit.1 = (bf16[2048,2048]{1,0:T(8,128)(2,1)}, bf16[2048,1408]{1,0:T(8,128)(2,1)}, bf16[2048,1408]{1,0:T(8,128)(2,1)}, bf16[2048,1408]{1,0:T(8,128)(2,1)}, f32[2048,1]{1,0:T(8,128)S(1)}) custom-call(s32[4]{0:T(128)S(1)} %pad_add_fusion.1.spots, bf16[2048,1024]{1,0:T(8,128)(2,1)} %maximum_select_fusion.3.own_ref, ...), custom_call_target="tpu_custom_call" | custom-call | flops 23622320128 | bytes 45621248 | tf_op jit(solution)/shard_map/gated_unit/pallas_call | solution.py:337
  438.4 6.5 collective-permute-done.19
  447.8 6.8 collective-permute-done.20.other_ref
  461.4 16.7 %gradient_rows.8 = bf16[2048,1408]{1,0:T(8,128)(2,1)S(1)} custom-call(s32[4]{0:T(128)S(1)} %pad_add_fusion.1.spots, bf16[2048,2048]{1,0:T(8,128)(2,1)} %get-tuple-element.183.left_ref.dy_ref, bf16[2048,1408]{1,0:T(8,128)(2,1)S(1)} %bitcast.63), custom_call_target="tpu_custom_call" | custom-call | flops 11811160064 | bytes 17301504 | tf_op jit(solution)/shard_map/gradient_rows/pallas_call | solution.py:470
  480.6 22.4 %gated_unit_back.1 = (bf16[2048,1408]{1,0:T(8,128)(2,1)S(1)}, bf16[2048,1408]{1,0:T(8,128)(2,1)S(1)}, f32[2048,1]{1,0:T(8,128)S(1)}) custom-call(s32[4]{0:T(128)S(1)} %pad_add_fusion.1.spots, bf16[2048,2048]{1,0:T(8,128)(2,1)} %get-tuple-element.183.left_ref.dy_ref, bf16[2048,1408]{1,0:T(8,128)(2,1)} %get-tuple-element.187.one_ref, ...), custom_call_target="tpu_custom_call" | custom-call | flops 11811160064 | bytes 37232640 | tf_op jit(solution)/shard_map/gated_unit_back/pallas_call | solution.py:374
  508.9 19.9 %fold_half.6 = bf16[2048,1024]{1,0:T(8,128)(2,1)} custom-call(s32[4]{0:T(128)S(1)} %pad_add_fusion.1.spots, bf16[2048,1408]{1,0:T(8,128)(2,1)} %copy-done.39, bf16[2048,1408]{1,0:T(8,128)(2,1)} %copy-done.36, bf16[1024,1408]{1,0:T(8,128)(2,1)S(1)} %copy-done.18, bf16[1024,1408]{1,0:T(8,128)(2,1)} %collective-permute-done.10.refs_1_.refs_3_.refs_4_, ...), custom_call_target="tpu_custom_call" | custom-call | flops 11811160064 | bytes 21495808 | tf_op jit(solution)/shard_map/fold_half/pallas_call | solution.py:435
  536.8 9.4 gradient_rows.9
  546.3 21.8 %fold_half.7 = (bf16[2048,512]{1,0:T(8,128)(2,1)}, f32[2048,512]{1,0:T(8,128)}) custom-call(s32[4]{0:T(128)S(1)} %pad_add_fusion.1.spots, bf16[2048,1408]{1,0:T(8,128)(2,1)} %copy-done.39, bf16[2048,1408]{1,0:T(8,128)(2,1)} %copy-done.36, bf16[2048,1024]{1,0:T(8,128)(2,1)} %collective-permute-done.21.refs_2_, bf16[1024,1408]{1,0:T(8,128)(2,1)S(1)} %copy-done.19, ...), custom_call_target="tpu_custom_call" | custom-call | flops 11811160064 | bytes 27787264 | tf_op jit(solution)/shard_map/fold_half/pallas_call | solution.py:435
  574.2 16.4 %gradient_rows.10 = bf16[2048,1408]{1,0:T(8,128)(2,1)S(1)} custom-call(s32[4]{0:T(128)S(1)} %pad_add_fusion.1.spots, bf16[2048,2048]{1,0:T(8,128)(2,1)} %get-tuple-element.177.left_ref, bf16[2048,1408]{1,0:T(8,128)(2,1)S(1)} %copy-done.40), custom_call_target="tpu_custom_call" | custom-call | flops 11811160064 | bytes 17301504 | tf_op jit(solution)/shard_map/gradient_rows/pallas_call | solution.py:470
  595.7 11.4 %fold_half.8 = bf16[2048,1024]{1,0:T(8,128)(2,1)} custom-call(s32[4]{0:T(128)S(1)} %pad_add_fusion.1.spots, bf16[2048,1408]{1,0:T(8,128)(2,1)S(1)} %copy-done.38, bf16[2048,1408]{1,0:T(8,128)(2,1)} %all-gather.17.cloned.1.call-done.refs_0_.refs_1_.refs_2_), custom_call_target="tpu_custom_call" | custom-call | flops 5905580032 | bytes 9961472 | tf_op jit(solution)/shard_map/fold_half/pallas_call | solution.py:435
  607.2 8.8 collective-permute-done.23
  616.0 6.0 multiply_reduce_fusion.2
  627.0 12.3 %convolution_convert_fusion.1 = bf16[2048,512]{1,0:T(8,128)(2,1)S(1)} fusion(f32[2048,512]{1,0:T(8,128)} %copy-done.41, f32[2048]{0:T(1024)S(1)} %add_rsqrt_fusion, bf16[2048,1024]{1,0:T(8,128)(2,1)} %collective-permute-done.13, bf16[2048,1024]{1,0:T(8,128)(2,1)} %maximum_select_fusion.2, pred[]{:T(512)S(6)} %eq.53), kind=kOutput, calls=%fused_computation.28 | convolution fusion | flops 4335861760 | bytes 14688257 | tf_op jit(solution)/shard_map/dot_general | solution.py:32
  641.6 10.7 collective-permute-done.29
  664.8 13.1 %fold_half.9 = (bf16[2048,512]{1,0:T(8,128)(2,1)S(1)}, f32[2048,512]{1,0:T(8,128)S(1)}) custom-call(s32[4]{0:T(128)S(1)} %pad_add_fusion.1.spots, bf16[2048,1408]{1,0:T(8,128)(2,1)} %get-tuple-element.199.right_ref.refs_0_, bf16[2048,1024]{1,0:T(8,128)(2,1)} %collective-permute-done.27.refs_1_, ...), custom_call_target="tpu_custom_call" | custom-call | flops 5905580032 | bytes 16252928 | tf_op jit(solution)/shard_map/fold_half/pallas_call | solution.py:435
  677.9 31.3 %collective-permute-done.32 = f32[2048]{0:T(1024)S(1)} collective-permute-done((f32[2048]{0:T(1024)S(1)}, f32[2048]{0:T(1024)S(1)}, u32[]{:S(2)}, u32[]{:S(2)}) %collective-permute-start.32) | collective-permute-done | bytes 8224 | tf_op jit(solution)/shard_map/ppermute | solution.py:543
  711.0 5.8 multiply_convert_fusion
  716.8 21.3 %attend_back.1 = (bf16[2048,512]{1,0:T(8,128)(2,1)S(1)}, bf16[2048,512]{1,0:T(8,128)(2,1)S(1)}, bf16[2048,512]{1,0:T(8,128)(2,1)S(1)}) custom-call(f32[4]{0:T(128)S(1)} %dynamic_slice.129.rates, s32[2,2]{1,0:T(2,128)S(1)} %pad_add_fusion.ends, f32[2048,1024]{1,0:T(8,128)} %get-tuple-element.163.zq_ref.zk_ref, f32[2048,1024]{1,0:T(8,128)} %get-tuple-element.163.zq_ref.zk_ref, ...), custom_call_target="tpu_custom_call" | custom-call | flops 10737418240 | bytes 20971520 | tf_op jit(solution)/shard_map/attend_back/pallas_call | solution.py:119
  743.3 7.4 gradient_rows.11
  763.9 10.0 gradient_rows.12
  773.9 7.3 collective-permute-done.36
  792.0 7.0 gradient_rows.13
  799.0 14.7 %fold_half.10 = bf16[2048,1024]{1,0:T(8,128)(2,1)} custom-call(s32[4]{0:T(128)S(1)} %pad_add_fusion.1.spots, bf16[2048,1024]{1,0:T(8,128)(2,1)} %copy-done.7, bf16[2048,1024]{1,0:T(8,128)(2,1)} %pad_maximum_fusion.refs_1_.right_ref, bf16[1024,1024]{1,0:T(8,128)(2,1)S(1)} %copy-done.27, bf16[1024,1024]{1,0:T(8,128)(2,1)S(1)} %copy-done.34, ...), custom_call_target="tpu_custom_call" | custom-call | flops 8589934592 | bytes 16777216 | tf_op jit(solution)/shard_map/fold_half/pallas_call | solution.py:435
  813.8 6.5 collective-permute-done.38
  842.5 7.9 gradient_rows.14
  866.6 17.2 %fold_half.11 = (bf16[2048,512]{1,0:T(8,128)(2,1)}, f32[2048,512]{1,0:T(8,128)}) custom-call(s32[4]{0:T(128)S(1)} %pad_add_fusion.1.spots, bf16[2048,1024]{1,0:T(8,128)(2,1)} %copy-done.7, bf16[2048,1024]{1,0:T(8,128)(2,1)} %pad_maximum_fusion.refs_1_.right_ref, bf16[2048,1024]{1,0:T(8,128)(2,1)} %collective-permute-done.41.refs_2_, ...), custom_call_target="tpu_custom_call" | custom-call | flops 8589934592 | bytes 23068672 | tf_op jit(solution)/shard_map/fold_half/pallas_call | solution.py:435
  883.8 7.7 collective-permute-done.45
  903.5 6.9 gradient_rows.15
  922.7 24.3 %collective-permute-done.47 = f32[2048]{0:T(1024)S(1)} collective-permute-done((f32[2048]{0:T(1024)S(1)}, f32[2048]{0:T(1024)S(1)}, u32[]{:S(2)}, u32[]{:S(2)}) %collective-permute-start.47) | collective-permute-done | bytes 8224 | tf_op jit(solution)/shard_map/ppermute | solution.py:543
  956.7 19.9 %collective-permute-done.51 = bf16[2,512,512]{2,1,0:T(8,128)(2,1)S(1)} collective-permute-done((bf16[2,512,512]{2,1,0:T(8,128)(2,1)S(1)}, bf16[2,512,512]{2,1,0:T(8,128)(2,1)S(1)}, u32[]{:S(2)}, u32[]{:S(2)}) %collective-permute-start.51) | collective-permute-done | bytes 1048608 | tf_op jit(solution)/shard_map/ppermute | solution.py:543
  988.2 11.7 %collective-permute-start.56 = (bf16[256,1024]{1,0:T(8,128)(2,1)}, bf16[256,1024]{1,0:T(8,128)(2,1)S(1)}, u32[]{:S(2)}, u32[]{:S(2)}) collective-permute-start(bf16[256,1024]{1,0:T(8,128)(2,1)} %reduce-scatter.11.cloned.1.call-done), channel_id=1, source_target_pairs={{0,16},{1,17},{2,18},{3,19},{4,20},{5,21},{6,22},{7,23},{8,24},{9,... | collective-permute-start | bytes 1572872 | tf_op jit(solution)/shard_map/ppermute | solution.py:543
  1003.2 7.8 place_quarters.5
  1010.9 7.1 place_quarters.6
  1037.4 22.5 %collective-permute-done.57 = bf16[512,1024]{1,0:T(8,128)(2,1)} collective-permute-done((bf16[512,1024]{1,0:T(8,128)(2,1)S(1)}, bf16[512,1024]{1,0:T(8,128)(2,1)}, u32[]{:S(2)}, u32[]{:S(2)}) %collective-permute-start.57) | collective-permute-done | bytes 1048608 | tf_op jit(solution)/shard_map/ppermute | solution.py:543
  1077.6 6.3 collective-permute-done.63.refs_2_.refs_3_
  1088.3 5.6 place_quarters.9
  (423 shorter events, 318.5 us)
Async XLA Ops:
  8.0 89.1 %all-gather.7.cloned.1.call-start = ((), (), s32[]{:S(2)}) async-start(), calls=%async_computation.6 | async-start | bytes 2621440 | tf_op jit(solution)/shard_map/all_gather | solution.py:665
  10.3 136.6 %all-gather.9.cloned.1.call-start = ((), (), s32[]{:S(2)}) async-start(), calls=%async_computation.7 | async-start | bytes 2621440 | tf_op jit(solution)/shard_map/all_gather | solution.py:665
  12.6 171.7 %all-gather.11.cloned.1.call-start = ((), (), s32[]{:S(2)}) async-start(), calls=%async_computation.8 | async-start | bytes 1310720 | tf_op jit(solution)/shard_map/all_gather | solution.py:665
  13.9 80.9 %collective-permute-start = (bf16[256,2048]{1,0:T(8,128)(2,1)}, bf16[256,2048]{1,0:T(8,128)(2,1)S(1)}, u32[]{:S(2)}, u32[]{:S(2)}) collective-permute-start(bf16[256,2048]{1,0:T(8,128)(2,1)} %get-tuple-element.332), channel_id=1, source_target_pairs={{0,0},{4,1},{1,2},{5,3},{2,4},{6,5},{3,6},{7,7},{8,8},{12,9},{9,10... | collective-permute-start | bytes 3145736 | tf_op jit(solution)/shard_map/ppermute | solution.py:594
  16.0 78.8 %collective-permute-start.1 = (bf16[256,2048]{1,0:T(8,128)(2,1)S(1)}, bf16[256,2048]{1,0:T(8,128)(2,1)S(1)}, u32[]{:S(2)}, u32[]{:S(2)}) collective-permute-start(bf16[256,2048]{1,0:T(8,128)(2,1)S(1)} %get-tuple-element.333), channel_id=1, source_target_pairs={{1,0},{5,1},{0,2},{4,3},{3,4},{7,5},{2,6},{6,7},{9,8},{13,9},{8,10... | collective-permute-start | bytes 3145736 | tf_op jit(solution)/shard_map/ppermute | solution.py:594
  97.1 43.7 %collective-permute-start.2 = (bf16[512,2048]{1,0:T(8,128)(2,1)}, bf16[512,2048]{1,0:T(8,128)(2,1)}, u32[]{:S(2)}, u32[]{:S(2)}) collective-permute-start(bf16[512,2048]{1,0:T(8,128)(2,1)} %maximum_select_fusion.6), channel_id=1, source_target_pairs={{0,8},{1,9},{2,10},{3,11},{4,12},{5,13},{6,14},{7,15},{8,0},{9,1},... | collective-permute-start | bytes 6291464 | tf_op jit(solution)/shard_map/ppermute | solution.py:543
  99.1 138.9 %all-gather.13.cloned.1.call-start = ((), (), s32[]{:S(2)}) async-start(), calls=%async_computation.9 | async-start | bytes 3604480 | tf_op jit(solution)/shard_map/all_gather | solution.py:665
  99.1 47.7 %collective-permute-start.3 = (bf16[1024,1024]{1,0:T(8,128)(2,1)}, bf16[1024,1024]{1,0:T(8,128)(2,1)S(1)}, u32[]{:S(2)}, u32[]{:S(2)}) collective-permute-start(bf16[1024,1024]{1,0:T(8,128)(2,1)} %all-gather.7.cloned.1.call-done.refs_0_.refs_2_.refs_3_), channel_id=1, source_target_pairs={{0,16},{1,17},{2,18},{3,19},{4,20},{5,21},{6,22},{7,23},{8,24},{9,... | collective-permute-start | bytes 6291464 | tf_op jit(solution)/shard_map/ppermute | solution.py:543
  102.8 188.9 %all-gather.15.cloned.1.call-start = ((), (), s32[]{:S(2)}) async-start(), calls=%async_computation.10 | async-start | bytes 3604480 | tf_op jit(solution)/shard_map/all_gather | solution.py:665
  151.6 47.5 %collective-permute-start.5 = (bf16[1024,1024]{1,0:T(8,128)(2,1)}, bf16[1024,1024]{1,0:T(8,128)(2,1)}, u32[]{:S(2)}, u32[]{:S(2)}) collective-permute-start(bf16[1024,1024]{1,0:T(8,128)(2,1)} %all-gather.9.cloned.1.call-done.refs_0_.refs_4_.refs_5_), channel_id=1, source_target_pairs={{0,16},{1,17},{2,18},{3,19},{4,20},{5,21},{6,22},{7,23},{8,24},{9,... | collective-permute-start | bytes 6291464 | tf_op jit(solution)/shard_map/ppermute | solution.py:543
  157.7 322.8 %all-gather.17.cloned.1.call-start = ((), (), s32[]{:S(2)}) async-start(), calls=%async_computation.11 | async-start | bytes 6488064 | tf_op jit(solution)/shard_map/all_gather | solution.py:669
  199.1 38.8 %collective-permute-start.8 = (bf16[1024,512]{1,0:T(8,128)(2,1)}, bf16[1024,512]{1,0:T(8,128)(2,1)}, u32[]{:S(2)}, u32[]{:S(2)}) collective-permute-start(bf16[1024,512]{1,0:T(8,128)(2,1)} %all-gather.11.cloned.1.call-done), channel_id=1, source_target_pairs={{0,16},{1,17},{2,18},{3,19},{4,20},{5,21},{6,22},{7,23},{8,24},{9,... | collective-permute-start | bytes 3145736 | tf_op jit(solution)/shard_map/ppermute | solution.py:543
  237.9 63.2 %collective-permute-start.10 = (bf16[1024,1408]{1,0:T(8,128)(2,1)}, bf16[1024,1408]{1,0:T(8,128)(2,1)}, u32[]{:S(2)}, u32[]{:S(2)}) collective-permute-start(bf16[1024,1408]{1,0:T(8,128)(2,1)} %all-gather.13.cloned.1.call-done.refs_0_.refs_2_.refs_3_), channel_id=1, source_target_pairs={{0,16},{1,17},{2,18},{3,19},{4,20},{5,21},{6,22},{7,23},{8,24},{9,... | collective-permute-start | bytes 8650760 | tf_op jit(solution)/shard_map/ppermute | solution.py:543
  238.2 46.2 %collective-permute-start.9 = (bf16[2048,512]{1,0:T(8,128)(2,1)}, bf16[2048,512]{1,0:T(8,128)(2,1)S(1)}, u32[]{:S(2)}, u32[]{:S(2)}) collective-permute-start(bf16[2048,512]{1,0:T(8,128)(2,1)} %get-tuple-element.166), channel_id=1, source_target_pairs={{0,8},{1,9},{2,10},{3,11},{4,12},{5,13},{6,14},{7,15},{8,0},{9,1},... | collective-permute-start | bytes 6291464 | tf_op jit(solution)/shard_map/ppermute | solution.py:543
  241.9 42.5 %collective-permute-start.12 = (f32[2048]{0:T(1024)S(1)}, f32[2048]{0:T(1024)S(1)}, u32[]{:S(2)}, u32[]{:S(2)}) collective-permute-start(f32[2048]{0:T(1024)S(1)} %add.256), channel_id=1, source_target_pairs={{0,8},{1,9},{2,10},{3,11},{4,12},{5,13},{6,14},{7,15},{8,0},{9,1},... | collective-permute-start | bytes 24584 | tf_op jit(solution)/shard_map/ppermute | solution.py:543
  307.9 68.1 %collective-permute-start.15 = (bf16[1024,1408]{1,0:T(8,128)(2,1)S(1)}, bf16[1024,1408]{1,0:T(8,128)(2,1)S(1)}, u32[]{:S(2)}, u32[]{:S(2)}) collective-permute-start(bf16[1024,1408]{1,0:T(8,128)(2,1)S(1)} %copy-done.20), channel_id=1, source_target_pairs={{0,16},{1,17},{2,18},{3,19},{4,20},{5,21},{6,22},{7,23},{8,24},{9,... | collective-permute-start | bytes 8650760 | tf_op jit(solution)/shard_map/ppermute | solution.py:543
  319.9 53.5 %collective-permute-start.14 = (bf16[2048,512]{1,0:T(8,128)(2,1)}, bf16[2048,512]{1,0:T(8,128)(2,1)S(1)}, u32[]{:S(2)}, u32[]{:S(2)}) collective-permute-start(bf16[2048,512]{1,0:T(8,128)(2,1)} %get-tuple-element.336), channel_id=1, source_target_pairs={{0,8},{1,9},{2,10},{3,11},{4,12},{5,13},{6,14},{7,15},{8,0},{9,1},... | collective-permute-start | bytes 6291464 | tf_op jit(solution)/shard_map/ppermute | solution.py:543
  322.8 48.2 %collective-permute-start.16 = (bf16[256,2048]{1,0:T(8,128)(2,1)S(1)}, bf16[256,2048]{1,0:T(8,128)(2,1)S(1)}, u32[]{:S(2)}, u32[]{:S(2)}) collective-permute-start(bf16[256,2048]{1,0:T(8,128)(2,1)S(1)} %get-tuple-element.328), channel_id=1, source_target_pairs={{0,0},{4,1},{1,2},{5,3},{2,4},{6,5},{3,6},{7,7},{8,8},{12,9},{9,10... | collective-permute-start | bytes 3145736 | tf_op jit(solution)/shard_map/ppermute | solution.py:594
  327.8 43.2 %collective-permute-start.17 = (bf16[256,2048]{1,0:T(8,128)(2,1)S(1)}, bf16[256,2048]{1,0:T(8,128)(2,1)S(1)}, u32[]{:S(2)}, u32[]{:S(2)}) collective-permute-start(bf16[256,2048]{1,0:T(8,128)(2,1)S(1)} %get-tuple-element.329), channel_id=1, source_target_pairs={{1,0},{5,1},{0,2},{4,3},{3,4},{7,5},{2,6},{6,7},{9,8},{13,9},{8,10... | collective-permute-start | bytes 3145736 | tf_op jit(solution)/shard_map/ppermute | solution.py:594
  383.4 232.6 %reduce-scatter.7.cloned.1.call-start = ((), (), s32[]{:S(2)}) async-start(), calls=%async_computation.12 | async-start | bytes 6488064 | tf_op jit(solution)/shard_map/reduce_scatter | solution.py:709
  397.2 47.6 %collective-permute-start.19 = (bf16[512,2048]{1,0:T(8,128)(2,1)}, bf16[512,2048]{1,0:T(8,128)(2,1)S(1)}, u32[]{:S(2)}, u32[]{:S(2)}) collective-permute-start(bf16[512,2048]{1,0:T(8,128)(2,1)} %maximum_select_fusion.8), channel_id=1, source_target_pairs={{0,8},{1,9},{2,10},{3,11},{4,12},{5,13},{6,14},{7,15},{8,0},{9,1},... | collective-permute-start | bytes 6291464 | tf_op jit(solution)/shard_map/ppermute | solution.py:543
  480.6 302.5 %reduce-scatter.9.cloned.1.call-start = ((), (), s32[]{:S(2)}) async-start(), calls=%async_computation.13 | async-start | bytes 6488064 | tf_op jit(solution)/shard_map/reduce_scatter | solution.py:709
  534.0 34.1 %collective-permute-start.22 = (f32[2048]{0:T(1024)S(1)}, f32[2048]{0:T(1024)S(1)}, u32[]{:S(2)}, u32[]{:S(2)}) collective-permute-start(f32[2048]{0:T(1024)S(1)} %reduce.1), channel_id=1, source_target_pairs={{0,4},{1,5},{2,6},{3,7},{4,0},{5,1},{6,2},{7,3},{8,12},{9,13},{10,... | collective-permute-start | bytes 24584 | tf_op jit(solution)/shard_map/ppermute | solution.py:543
  568.1 39.0 %collective-permute-start.25 = (f32[2048]{0:T(1024)S(1)}, f32[2048]{0:T(1024)S(1)}, u32[]{:S(2)}, u32[]{:S(2)}) collective-permute-start(f32[2048]{0:T(1024)S(1)} %add.261), channel_id=1, source_target_pairs={{0,8},{1,9},{2,10},{3,11},{4,12},{5,13},{6,14},{7,15},{8,0},{9,1},... | collective-permute-start | bytes 24584 | tf_op jit(solution)/shard_map/ppermute | solution.py:543
  568.6 47.4 %collective-permute-start.23 = (bf16[2048,512]{1,0:T(8,128)(2,1)}, bf16[2048,512]{1,0:T(8,128)(2,1)}, u32[]{:S(2)}, u32[]{:S(2)}) collective-permute-start(bf16[2048,512]{1,0:T(8,128)(2,1)} %get-tuple-element.198), channel_id=1, source_target_pairs={{0,8},{1,9},{2,10},{3,11},{4,12},{5,13},{6,14},{7,15},{8,0},{9,1},... | collective-permute-start | bytes 6291464 | tf_op jit(solution)/shard_map/ppermute | solution.py:543
  571.5 35.6 %collective-permute-start.24 = (bf16[512,1408]{1,0:T(8,128)(2,1)}, bf16[512,1408]{1,0:T(8,128)(2,1)}, u32[]{:S(2)}, u32[]{:S(2)}) collective-permute-start(bf16[512,1408]{1,0:T(8,128)(2,1)} %get-tuple-element.309), channel_id=1, source_target_pairs={{0,16},{1,17},{2,18},{3,19},{4,20},{5,21},{6,22},{7,23},{8,24},{9,... | collective-permute-start | bytes 4325384 | tf_op jit(solution)/shard_map/ppermute | solution.py:543
  626.8 36.1 %collective-permute-start.27 = (bf16[2048,1024]{1,0:T(8,128)(2,1)}, bf16[2048,1024]{1,0:T(8,128)(2,1)}, u32[]{:S(2)}, u32[]{:S(2)}) collective-permute-start(bf16[2048,1024]{1,0:T(8,128)(2,1)} %fold_half.8), channel_id=1, source_target_pairs={{0,4},{1,5},{2,6},{3,7},{4,0},{5,1},{6,2},{7,3},{8,12},{9,13},{10,... | collective-permute-start | bytes 12582920 | tf_op jit(solution)/shard_map/ppermute | solution.py:543
  626.9 288.2 %reduce-scatter.13.cloned.1.call-start = ((), (), s32[]{:S(2)}) async-start(), calls=%async_computation.15 | async-start | bytes 3604480 | tf_op jit(solution)/shard_map/reduce_scatter | solution.py:703
  662.9 46.4 %collective-permute-start.30 = (bf16[2048,512]{1,0:T(8,128)(2,1)}, bf16[2048,512]{1,0:T(8,128)(2,1)}, u32[]{:S(2)}, u32[]{:S(2)}) collective-permute-start(bf16[2048,512]{1,0:T(8,128)(2,1)} %dynamic-slice_convert_fusion), channel_id=1, source_target_pairs={{0,8},{1,9},{2,10},{3,11},{4,12},{5,13},{6,14},{7,15},{8,0},{9,1},... | collective-permute-start | bytes 6291464 | tf_op jit(solution)/shard_map/ppermute | solution.py:543
  663.9 45.3 %collective-permute-start.31 = (bf16[1024,512]{1,0:T(8,128)(2,1)}, bf16[1024,512]{1,0:T(8,128)(2,1)}, u32[]{:S(2)}, u32[]{:S(2)}) collective-permute-start(bf16[1024,512]{1,0:T(8,128)(2,1)} %get-tuple-element.220), channel_id=1, source_target_pairs={{0,16},{1,17},{2,18},{3,19},{4,20},{5,21},{6,22},{7,23},{8,24},{9,... | collective-permute-start | bytes 3145736 | tf_op jit(solution)/shard_map/ppermute | solution.py:543
  664.2 45.0 %collective-permute-start.32 = (f32[2048]{0:T(1024)S(1)}, f32[2048]{0:T(1024)S(1)}, u32[]{:S(2)}, u32[]{:S(2)}) collective-permute-start(f32[2048]{0:T(1024)S(1)} %add.275), channel_id=1, source_target_pairs={{0,8},{1,9},{2,10},{3,11},{4,12},{5,13},{6,14},{7,15},{8,0},{9,1},... | collective-permute-start | bytes 24584 | tf_op jit(solution)/shard_map/ppermute | solution.py:543
  709.2 41.6 %collective-permute-start.33 = (bf16[512,1408]{1,0:T(8,128)(2,1)S(1)}, bf16[512,1408]{1,0:T(8,128)(2,1)}, u32[]{:S(2)}, u32[]{:S(2)}) collective-permute-start(bf16[512,1408]{1,0:T(8,128)(2,1)S(1)} %copy-done.57), channel_id=1, source_target_pairs={{0,16},{1,17},{2,18},{3,19},{4,20},{5,21},{6,22},{7,23},{8,24},{9,... | collective-permute-start | bytes 4325384 | tf_op jit(solution)/shard_map/ppermute | solution.py:543
  710.2 45.3 %collective-permute-start.34 = (bf16[2048,512]{1,0:T(8,128)(2,1)S(1)}, bf16[2048,512]{1,0:T(8,128)(2,1)}, u32[]{:S(2)}, u32[]{:S(2)}) collective-permute-start(bf16[2048,512]{1,0:T(8,128)(2,1)S(1)} %get-tuple-element.228), channel_id=1, source_target_pairs={{0,8},{1,9},{2,10},{3,11},{4,12},{5,13},{6,14},{7,15},{8,0},{9,1},... | collective-permute-start | bytes 6291464 | tf_op jit(solution)/shard_map/ppermute | solution.py:543
  783.1 139.6 %reduce-scatter.15.cloned.1.call-start = ((), (), s32[]{:S(2)}) async-start(), calls=%async_computation.16 | async-start | bytes 1310720 | tf_op jit(solution)/shard_map/reduce_scatter | solution.py:703
  821.2 34.4 %collective-permute-start.41 = (bf16[2048,1024]{1,0:T(8,128)(2,1)}, bf16[2048,1024]{1,0:T(8,128)(2,1)}, u32[]{:S(2)}, u32[]{:S(2)}) collective-permute-start(bf16[2048,1024]{1,0:T(8,128)(2,1)} %fold_half.10), channel_id=1, source_target_pairs={{0,4},{1,5},{2,6},{3,7},{4,0},{5,1},{6,2},{7,3},{8,12},{9,13},{10,... | collective-permute-start | bytes 12582920 | tf_op jit(solution)/shard_map/ppermute | solution.py:543
  828.9 156.2 %reduce-scatter.17.cloned.1.call-start = ((), (), s32[]{:S(2)}) async-start(), calls=%async_computation.17 | async-start | bytes 2621440 | tf_op jit(solution)/shard_map/reduce_scatter | solution.py:703
  855.6 132.6 %reduce-scatter.11.cloned.1.call-start = ((), (), s32[]{:S(2)}) async-start(), calls=%async_computation.14 | async-start | bytes 2621440 | tf_op jit(solution)/shard_map/reduce_scatter | solution.py:703
  858.8 32.8 %collective-permute-start.45 = (bf16[512,1408]{1,0:T(8,128)(2,1)}, bf16[512,1408]{1,0:T(8,128)(2,1)}, u32[]{:S(2)}, u32[]{:S(2)}) collective-permute-start(bf16[512,1408]{1,0:T(8,128)(2,1)} %maximum_select_fusion.17), channel_id=1, source_target_pairs={{0,8},{1,9},{2,10},{3,11},{4,12},{5,13},{6,14},{7,15},{8,0},{9,1},... | collective-permute-start | bytes 4325384 | tf_op jit(solution)/shard_map/ppermute | solution.py:543
  865.3 57.4 %collective-permute-start.49 = (bf16[512,2816]{1,0:T(8,128)(2,1)}, bf16[512,2816]{1,0:T(8,128)(2,1)}, u32[]{:S(2)}, u32[]{:S(2)}) collective-permute-start(bf16[512,2816]{1,0:T(8,128)(2,1)} %constant_dynamic-update-slice_fusion.2.refs_0_.refs_1_), channel_id=1, source_target_pairs={{0,4},{1,5},{2,6},{3,7},{4,0},{5,1},{6,2},{7,3},{8,12},{9,13},{10,... | collective-permute-start | bytes 8650760 | tf_op jit(solution)/shard_map/ppermute | solution.py:543
  893.6 53.4 %collective-permute-start.48 = (bf16[512,2816]{1,0:T(8,128)(2,1)S(1)}, bf16[512,2816]{1,0:T(8,128)(2,1)}, u32[]{:S(2)}, u32[]{:S(2)}) collective-permute-start(bf16[512,2816]{1,0:T(8,128)(2,1)S(1)} %pad_maximum_fusion.2.refs_0_.refs_1_), channel_id=1, source_target_pairs={{0,4},{1,5},{2,6},{3,7},{4,0},{5,1},{6,2},{7,3},{8,12},{9,13},{10,... | collective-permute-start | bytes 8650760 | tf_op jit(solution)/shard_map/ppermute | solution.py:543
  899.3 47.7 %collective-permute-start.46 = (bf16[2048,512]{1,0:T(8,128)(2,1)}, bf16[2048,512]{1,0:T(8,128)(2,1)}, u32[]{:S(2)}, u32[]{:S(2)}) collective-permute-start(bf16[2048,512]{1,0:T(8,128)(2,1)} %get-tuple-element.259), channel_id=1, source_target_pairs={{0,8},{1,9},{2,10},{3,11},{4,12},{5,13},{6,14},{7,15},{8,0},{9,1},... | collective-permute-start | bytes 6291464 | tf_op jit(solution)/shard_map/ppermute | solution.py:543
  984.3 35.3 %collective-permute-start.53 = (bf16[512,1024]{1,0:T(8,128)(2,1)}, bf16[512,1024]{1,0:T(8,128)(2,1)}, u32[]{:S(2)}, u32[]{:S(2)}) collective-permute-start(bf16[512,1024]{1,0:T(8,128)(2,1)} %get-tuple-element.313), channel_id=1, source_target_pairs={{0,4},{1,5},{2,6},{3,7},{4,0},{5,1},{6,2},{7,3},{8,12},{9,13},{10,... | collective-permute-start | bytes 3145736 | tf_op jit(solution)/shard_map/ppermute | solution.py:543
  984.3 35.3 %collective-permute-start.54 = (bf16[256,2048]{1,0:T(8,128)(2,1)}, bf16[256,2048]{1,0:T(8,128)(2,1)}, u32[]{:S(2)}, u32[]{:S(2)}) collective-permute-start(bf16[256,2048]{1,0:T(8,128)(2,1)} %get-tuple-element.273), channel_id=1, source_target_pairs={{0,1},{1,5},{2,0},{3,4},{4,3},{5,7},{6,2},{7,6},{8,9},{9,13},{10,8... | collective-permute-start | bytes 3145736 | tf_op jit(solution)/shard_map/ppermute | solution.py:606
  987.1 32.6 %collective-permute-start.55 = (bf16[256,1536]{1,0:T(8,128)(2,1)}, bf16[256,1536]{1,0:T(8,128)(2,1)}, u32[]{:S(2)}, u32[]{:S(2)}) collective-permute-start(bf16[256,1536]{1,0:T(8,128)(2,1)} %pad_maximum_fusion.7), channel_id=1, source_target_pairs={{0,8},{1,9},{2,10},{3,11},{4,12},{5,13},{6,14},{7,15},{8,0},{9,1},... | collective-permute-start | bytes 2359304 | tf_op jit(solution)/shard_map/ppermute | solution.py:543
  1003.2 34.2 %collective-permute-start.58 = (bf16[512,1408]{1,0:T(8,128)(2,1)}, bf16[512,1408]{1,0:T(8,128)(2,1)}, u32[]{:S(2)}, u32[]{:S(2)}) collective-permute-start(bf16[512,1408]{1,0:T(8,128)(2,1)} %maximum_select_fusion.18), channel_id=1, source_target_pairs={{0,8},{1,9},{2,10},{3,11},{4,12},{5,13},{6,14},{7,15},{8,0},{9,1},... | collective-permute-start | bytes 4325384 | tf_op jit(solution)/shard_map/ppermute | solution.py:543
  1020.1 39.7 %collective-permute-start.57 = (bf16[512,1024]{1,0:T(8,128)(2,1)S(1)}, bf16[512,1024]{1,0:T(8,128)(2,1)}, u32[]{:S(2)}, u32[]{:S(2)}) collective-permute-start(bf16[512,1024]{1,0:T(8,128)(2,1)S(1)} %maximum_select_fusion.21), channel_id=1, source_target_pairs={{0,8},{1,9},{2,10},{3,11},{4,12},{5,13},{6,14},{7,15},{8,0},{9,1},... | collective-permute-start | bytes 3145736 | tf_op jit(solution)/shard_map/ppermute | solution.py:543
  1023.7 41.7 %collective-permute-start.59 = (bf16[256,3072]{1,0:T(8,128)(2,1)}, bf16[256,3072]{1,0:T(8,128)(2,1)}, u32[]{:S(2)}, u32[]{:S(2)}) collective-permute-start(bf16[256,3072]{1,0:T(8,128)(2,1)} %constant_dynamic-update-slice_fusion.4), channel_id=1, source_target_pairs={{0,16},{1,17},{2,18},{3,19},{4,20},{5,21},{6,22},{7,23},{8,24},{9,... | collective-permute-start | bytes 4718600 | tf_op jit(solution)/shard_map/ppermute | solution.py:543
  1029.0 36.4 %collective-permute-start.60 = (bf16[256,2048]{1,0:T(8,128)(2,1)}, bf16[256,2048]{1,0:T(8,128)(2,1)S(1)}, u32[]{:S(2)}, u32[]{:S(2)}) collective-permute-start(bf16[256,2048]{1,0:T(8,128)(2,1)} %get-tuple-element.311), channel_id=1, source_target_pairs={{0,0},{1,4},{2,1},{3,5},{4,2},{5,6},{6,3},{7,7},{8,8},{9,12},{10,9... | collective-permute-start | bytes 3145736 | tf_op jit(solution)/shard_map/ppermute | solution.py:606
  (106 other events, 1894.5 us)
Sparse Core Ops, SparseCore 0:
  11.0 82.9 all-gather.6
  96.1 46.0 all-gather.8
  144.4 27.5 all-gather.10
  174.0 57.8 all-gather.12
  233.9 57.8 all-gather.14
  783.2 58.6 reduce-scatter.12
  844.2 25.7 reduce-scatter.14
  872.4 43.2 reduce-scatter.16
  918.6 44.3 reduce-scatter.10
Sparse Core Ops, SparseCore 1:
  383.5 88.8 all-gather.16
  480.6 107.7 reduce-scatter.6
  627.0 126.3 reduce-scatter.8

commit v16 on v15

--- a/solution.py
+++ b/solution.py
@@ -920,8 +920,7 @@
     y_vg = over_spread(f_vg)
     units = f_one.shape[1]
     [g_down] = place_quarters(spots, four_down, (0, units))
-    [g_one] = place_quarters(spots, four_one, (0, units))
-    grad_c, out_two, x_oqk, y_vg, g_down, g_one = tie(grad_c, out_two, x_oqk, y_vg, g_down, g_one)
+    grad_c, out_two, x_oqk, y_vg, g_down, *four_one = tie(grad_c, out_two, x_oqk, y_vg, g_down, *four_one)
 
     y_vg = by_spread([f_vg, *y_vg])
     x_vg = swap_b(y_vg)
@@ -931,7 +930,8 @@
     y_oqk = over_spread(f_oqk)
     input_grad = send_back(ordered(c, input_grad, grad_c, 1))
     output = as_batches([out_one, out_two])
-    x_vg, x_two, y_oqk, input_grad, output = tie(x_vg, x_two, y_oqk, input_grad, output)
+    [g_one] = place_quarters(spots, four_one, (0, units))
+    x_vg, x_two, y_oqk, input_grad, output, g_one = tie(x_vg, x_two, y_oqk, input_grad, output, g_one)
 
     four_vg = spread_c(joined(y_vg, x_vg))
     four_two = spread_c(joined(y_two, x_two))

time: 1120 us -> 1120 us (level)
    unnamed x180 -> x182, local copies, waits for them, and re-layouts: 60.8 us -> 60.1 us
  transfers between devices with their start and end apart: 77 -> 77, of which waited for: 28 -> 27; matrix products, arithmetic and copies ran while one was open for 16% -> 16% of each run, Pallas kernels for 30% -> 30%
where the time goes in v16:
time: 1120 us; the launch traced here: 1110 us
  waiting for transfers between devices  403 us (36%)
  Pallas kernels  342 us (31%)
  other arithmetic  109 us (10%)
  starting transfers between devices  105 us (9%)
  local copies, waits for them, and re-layouts  101 us (9%)
  matrix products  31 us (3%)
  between operations  17.1 us (2%)
    ppermute x57, waiting for transfers between devices, move(): return lax.ppermute(x, AXES, pairs)  271 us
    ppermute x4, waiting for transfers between devices, bring(): lax.ppermute(lax.dynamic_index_in_dim(x, (place + p) % 2, 0, False), AXES...  119 us
    pallas_call x6, Pallas kernels, fold_half(): pl.pallas_call(functools.partial(fold_kernel, len(values), arrived is not...  98.2 us
    pallas_call x8, Pallas kernels, gradient_rows(): pl.pallas_call(gradient_kernel, out_shape=out, grid_spec=pltpu.PrefetchSc...  82 us
    ppermute x57, starting transfers between devices, move(): return lax.ppermute(x, AXES, pairs)  74.7 us
    unnamed x182, local copies, waits for them, and re-layouts  60.1 us
    select_n x23, other arithmetic, ordered(): jnp.where(index == 0, jnp.concatenate([mine, other], axis), jnp.concatena...  50.9 us
    pallas_call x1, Pallas kernels, gated_unit(): pl.pallas_call(unit_kernel, out_shape=outs, grid_spec=pltpu.PrefetchScala...  38 us
  transfers between devices with their start and end apart: 77, of which 27 were waited for; matrix products, arithmetic and copies ran while one was open for 16% of the time, Pallas kernels for 30%

profile of v16, /device:TPU:17, one launch (start us, length us, event | category | flops | bytes accessed | tf_op | source)
XLA Modules:
  0.0 1109.8 jit_solution(4277106985011949800)
XLA Ops:
  18.8 75.9 %collective-permute-done = bf16[256,2048]{1,0:T(8,128)(2,1)S(1)} collective-permute-done((bf16[256,2048]{1,0:T(8,128)(2,1)}, bf16[256,2048]{1,0:T(8,128)(2,1)S(1)}, u32[]{:S(2)}, u32[]{:S(2)}) %collective-permute-start) | collective-permute-done | bytes 1048608 | tf_op jit(solution)/shard_map/ppermute | solution.py:594
  102.9 37.9 %collective-permute-done.2 = bf16[512,2048]{1,0:T(8,128)(2,1)} collective-permute-done((bf16[512,2048]{1,0:T(8,128)(2,1)}, bf16[512,2048]{1,0:T(8,128)(2,1)}, u32[]{:S(2)}, u32[]{:S(2)}) %collective-permute-start.2) | collective-permute-done | bytes 2097184 | tf_op jit(solution)/shard_map/ppermute | solution.py:543
  140.8 6.0 maximum_select_fusion.1.own_ref
  165.5 18.8 %enter.2 = (bf16[2048,2048]{1,0:T(8,128)(2,1)}, f32[2048,1024]{1,0:T(8,128)}, f32[2048,1]{1,0:T(8,128)S(1)}, bf16[2048,512]{1,0:T(8,128)(2,1)S(1)}) custom-call(s32[4]{0:T(128)S(1)} %pad_add_fusion.1.spots, bf16[1024,2048]{1,0:T(8,128)(2,1)S(1)} %copy-done.13, bf16[1024,2048]{1,0:T(8,128)(2,1)} %collective-permute-done.4.other_ref, ...), custom_call_target="tpu_custom_call" | custom-call | flops 8589934592 | bytes 31465472 | tf_op jit(solution)/shard_map/enter/pallas_call | solution.py:244
  184.3 14.7 %collective-permute-done.5.refs_1_.refs_5_.refs_6_ = bf16[1024,1024]{1,0:T(8,128)(2,1)} collective-permute-done((bf16[1024,1024]{1,0:T(8,128)(2,1)}, bf16[1024,1024]{1,0:T(8,128)(2,1)}, u32[]{:S(2)}, u32[]{:S(2)}) %collective-permute-start.5) | collective-permute-done | bytes 2097184 | tf_op jit(solution)/shard_map/ppermute | solution.py:543
  201.9 14.2 %project.1.zv_ref = f32[2048,1024]{1,0:T(8,128)S(1)} custom-call(s32[4]{0:T(128)S(1)} %pad_add_fusion.1.spots, bf16[2048,2048]{1,0:T(8,128)(2,1)} %get-tuple-element.163.h_ref.left_ref, bf16[1024,1024]{1,0:T(8,128)(2,1)S(1)} %copy-done.29, bf16[1024,1024]{1,0:T(8,128)(2,1)} %collective-permute-done.5.refs_1_.refs_5_.refs_6_), custom_call_target="tpu_custom_call" | custom-call | flops 8589934592 | bytes 20971520 | tf_op jit(solution)/shard_map/project/pallas_call | solution.py:275
  219.5 12.3 %attend.1 = f32[2048,512]{1,0:T(8,128)S(1)} custom-call(f32[4]{0:T(128)S(1)} %dynamic_slice.129.rates, s32[2,2]{1,0:T(2,128)S(1)} %pad_add_fusion.ends, f32[2048,1024]{1,0:T(8,128)S(1)} %copy-done, f32[2048,1024]{1,0:T(8,128)S(1)} %copy-done, f32[2048,1024]{1,0:T(8,128)} %copy-done.1), custom_call_target="tpu_custom_call" | custom-call | flops 4294967296 | bytes 16777216 | tf_op jit(solution)/shard_map/attend/pallas_call | solution.py:98
  242.1 42.2 %collective-permute-done.12 = f32[2048]{0:T(1024)S(1)} collective-permute-done((f32[2048]{0:T(1024)S(1)}, f32[2048]{0:T(1024)S(1)}, u32[]{:S(2)}, u32[]{:S(2)}) %collective-permute-start.12) | collective-permute-done | bytes 8224 | tf_op jit(solution)/shard_map/ppermute | solution.py:543
  291.8 9.2 collective-permute-done.10.refs_1_.refs_3_.refs_4_
  310.2 9.6 fusion.21
  327.8 43.1 %collective-permute-done.16 = bf16[256,2048]{1,0:T(8,128)(2,1)S(1)} collective-permute-done((bf16[256,2048]{1,0:T(8,128)(2,1)S(1)}, bf16[256,2048]{1,0:T(8,128)(2,1)S(1)}, u32[]{:S(2)}, u32[]{:S(2)}) %collective-permute-start.16) | collective-permute-done | bytes 1048608 | tf_op jit(solution)/shard_map/ppermute | solution.py:594
  383.4 13.8 %reduce-scatter.7.cloned.1.call-start = ((), (), s32[]{:S(2)}) async-start(), calls=%async_computation.12 | async-start | bytes 6488064 | tf_op jit(solution)/shard_map/reduce_scatter | solution.py:709
  399.2 38.0 %gated_unit.1 = (bf16[2048,2048]{1,0:T(8,128)(2,1)}, bf16[2048,1408]{1,0:T(8,128)(2,1)}, bf16[2048,1408]{1,0:T(8,128)(2,1)}, bf16[2048,1408]{1,0:T(8,128)(2,1)}, f32[2048,1]{1,0:T(8,128)S(1)}) custom-call(s32[4]{0:T(128)S(1)} %pad_add_fusion.1.spots, bf16[2048,1024]{1,0:T(8,128)(2,1)} %maximum_select_fusion.3.own_ref, ...), custom_call_target="tpu_custom_call" | custom-call | flops 23622320128 | bytes 45621248 | tf_op jit(solution)/shard_map/gated_unit/pallas_call | solution.py:337
  438.3 6.5 collective-permute-done.19
  447.8 6.8 collective-permute-done.20.other_ref
  454.5 5.4 enter.3
  461.3 16.7 %gradient_rows.8 = bf16[2048,1408]{1,0:T(8,128)(2,1)S(1)} custom-call(s32[4]{0:T(128)S(1)} %pad_add_fusion.1.spots, bf16[2048,2048]{1,0:T(8,128)(2,1)} %get-tuple-element.185.left_ref.dy_ref, bf16[2048,1408]{1,0:T(8,128)(2,1)S(1)} %bitcast.63), custom_call_target="tpu_custom_call" | custom-call | flops 11811160064 | bytes 17301504 | tf_op jit(solution)/shard_map/gradient_rows/pallas_call | solution.py:470
  480.6 22.4 %gated_unit_back.1 = (bf16[2048,1408]{1,0:T(8,128)(2,1)S(1)}, bf16[2048,1408]{1,0:T(8,128)(2,1)S(1)}, f32[2048,1]{1,0:T(8,128)S(1)}) custom-call(s32[4]{0:T(128)S(1)} %pad_add_fusion.1.spots, bf16[2048,2048]{1,0:T(8,128)(2,1)} %get-tuple-element.185.left_ref.dy_ref, bf16[2048,1408]{1,0:T(8,128)(2,1)} %get-tuple-element.189.one_ref, ...), custom_call_target="tpu_custom_call" | custom-call | flops 11811160064 | bytes 37232640 | tf_op jit(solution)/shard_map/gated_unit_back/pallas_call | solution.py:374
  508.9 19.9 %fold_half.6 = bf16[2048,1024]{1,0:T(8,128)(2,1)} custom-call(s32[4]{0:T(128)S(1)} %pad_add_fusion.1.spots, bf16[2048,1408]{1,0:T(8,128)(2,1)} %copy-done.39, bf16[2048,1408]{1,0:T(8,128)(2,1)} %copy-done.36, bf16[1024,1408]{1,0:T(8,128)(2,1)S(1)} %copy-done.18, bf16[1024,1408]{1,0:T(8,128)(2,1)} %collective-permute-done.10.refs_1_.refs_3_.refs_4_, ...), custom_call_target="tpu_custom_call" | custom-call | flops 11811160064 | bytes 21495808 | tf_op jit(solution)/shard_map/fold_half/pallas_call | solution.py:435
  536.8 9.4 gradient_rows.9
  546.2 21.8 %fold_half.7 = (bf16[2048,512]{1,0:T(8,128)(2,1)}, f32[2048,512]{1,0:T(8,128)}) custom-call(s32[4]{0:T(128)S(1)} %pad_add_fusion.1.spots, bf16[2048,1408]{1,0:T(8,128)(2,1)} %copy-done.39, bf16[2048,1408]{1,0:T(8,128)(2,1)} %copy-done.36, bf16[2048,1024]{1,0:T(8,128)(2,1)} %collective-permute-done.21.refs_2_, bf16[1024,1408]{1,0:T(8,128)(2,1)S(1)} %copy-done.19, ...), custom_call_target="tpu_custom_call" | custom-call | flops 11811160064 | bytes 27787264 | tf_op jit(solution)/shard_map/fold_half/pallas_call | solution.py:435
  574.1 16.5 %gradient_rows.10 = bf16[2048,1408]{1,0:T(8,128)(2,1)S(1)} custom-call(s32[4]{0:T(128)S(1)} %pad_add_fusion.1.spots, bf16[2048,2048]{1,0:T(8,128)(2,1)} %get-tuple-element.179.left_ref, bf16[2048,1408]{1,0:T(8,128)(2,1)S(1)} %copy-done.40), custom_call_target="tpu_custom_call" | custom-call | flops 11811160064 | bytes 17301504 | tf_op jit(solution)/shard_map/gradient_rows/pallas_call | solution.py:470
  595.7 11.4 %fold_half.8 = bf16[2048,1024]{1,0:T(8,128)(2,1)} custom-call(s32[4]{0:T(128)S(1)} %pad_add_fusion.1.spots, bf16[2048,1408]{1,0:T(8,128)(2,1)S(1)} %copy-done.38, bf16[2048,1408]{1,0:T(8,128)(2,1)} %all-gather.17.cloned.1.call-done.refs_0_.refs_1_.refs_2_), custom_call_target="tpu_custom_call" | custom-call | flops 5905580032 | bytes 9961472 | tf_op jit(solution)/shard_map/fold_half/pallas_call | solution.py:435
  607.1 8.7 collective-permute-done.23
  615.8 6.0 multiply_reduce_fusion.2
  626.9 12.3 %convolution_convert_fusion.1 = bf16[2048,512]{1,0:T(8,128)(2,1)S(1)} fusion(f32[2048,512]{1,0:T(8,128)} %copy-done.41, f32[2048]{0:T(1024)S(1)} %add_rsqrt_fusion, bf16[2048,1024]{1,0:T(8,128)(2,1)} %collective-permute-done.13, bf16[2048,1024]{1,0:T(8,128)(2,1)} %maximum_select_fusion.2, pred[]{:T(512)S(6)} %eq.53), kind=kOutput, calls=%fused_computation.28 | convolution fusion | flops 4335861760 | bytes 14688257 | tf_op jit(solution)/shard_map/dot_general | solution.py:32
  641.4 10.8 collective-permute-done.29
  664.5 13.3 %fold_half.9 = (bf16[2048,512]{1,0:T(8,128)(2,1)S(1)}, f32[2048,512]{1,0:T(8,128)S(1)}) custom-call(s32[4]{0:T(128)S(1)} %pad_add_fusion.1.spots, bf16[2048,1408]{1,0:T(8,128)(2,1)} %get-tuple-element.201.right_ref.refs_0_, bf16[2048,1024]{1,0:T(8,128)(2,1)} %collective-permute-done.27.refs_1_, ...), custom_call_target="tpu_custom_call" | custom-call | flops 5905580032 | bytes 16252928 | tf_op jit(solution)/shard_map/fold_half/pallas_call | solution.py:435
  677.8 31.4 %collective-permute-done.32 = f32[2048]{0:T(1024)S(1)} collective-permute-done((f32[2048]{0:T(1024)S(1)}, f32[2048]{0:T(1024)S(1)}, u32[]{:S(2)}, u32[]{:S(2)}) %collective-permute-start.32) | collective-permute-done | bytes 8224 | tf_op jit(solution)/shard_map/ppermute | solution.py:543
  711.1 5.7 multiply_convert_fusion
  716.8 21.3 %attend_back.1 = (bf16[2048,512]{1,0:T(8,128)(2,1)S(1)}, bf16[2048,512]{1,0:T(8,128)(2,1)S(1)}, bf16[2048,512]{1,0:T(8,128)(2,1)S(1)}) custom-call(f32[4]{0:T(128)S(1)} %dynamic_slice.129.rates, s32[2,2]{1,0:T(2,128)S(1)} %pad_add_fusion.ends, f32[2048,1024]{1,0:T(8,128)} %get-tuple-element.165.zq_ref.zk_ref, f32[2048,1024]{1,0:T(8,128)} %get-tuple-element.165.zq_ref.zk_ref, ...), custom_call_target="tpu_custom_call" | custom-call | flops 10737418240 | bytes 20971520 | tf_op jit(solution)/shard_map/attend_back/pallas_call | solution.py:119
  743.3 7.5 gradient_rows.11
  763.9 10.0 gradient_rows.12
  773.9 6.9 collective-permute-done.36
  791.5 7.2 gradient_rows.13
  798.8 14.7 %fold_half.10 = bf16[2048,1024]{1,0:T(8,128)(2,1)} custom-call(s32[4]{0:T(128)S(1)} %pad_add_fusion.1.spots, bf16[2048,1024]{1,0:T(8,128)(2,1)} %copy-done.7, bf16[2048,1024]{1,0:T(8,128)(2,1)} %pad_maximum_fusion.refs_1_.right_ref, bf16[1024,1024]{1,0:T(8,128)(2,1)S(1)} %copy-done.27, bf16[1024,1024]{1,0:T(8,128)(2,1)S(1)} %copy-done.34, ...), custom_call_target="tpu_custom_call" | custom-call | flops 8589934592 | bytes 16777216 | tf_op jit(solution)/shard_map/fold_half/pallas_call | solution.py:435
  813.5 6.6 collective-permute-done.38
  842.3 7.9 gradient_rows.14
  866.7 17.2 %fold_half.11 = (bf16[2048,512]{1,0:T(8,128)(2,1)}, f32[2048,512]{1,0:T(8,128)}) custom-call(s32[4]{0:T(128)S(1)} %pad_add_fusion.1.spots, bf16[2048,1024]{1,0:T(8,128)(2,1)} %copy-done.7, bf16[2048,1024]{1,0:T(8,128)(2,1)} %pad_maximum_fusion.refs_1_.right_ref, bf16[2048,1024]{1,0:T(8,128)(2,1)} %collective-permute-done.41.refs_2_, ...), custom_call_target="tpu_custom_call" | custom-call | flops 8589934592 | bytes 23068672 | tf_op jit(solution)/shard_map/fold_half/pallas_call | solution.py:435
  883.9 7.4 collective-permute-done.45
  903.7 6.9 gradient_rows.15
  922.7 24.1 %collective-permute-done.47 = f32[2048]{0:T(1024)S(1)} collective-permute-done((f32[2048]{0:T(1024)S(1)}, f32[2048]{0:T(1024)S(1)}, u32[]{:S(2)}, u32[]{:S(2)}) %collective-permute-start.47) | collective-permute-done | bytes 8224 | tf_op jit(solution)/shard_map/ppermute | solution.py:543
  956.6 19.7 %collective-permute-done.51 = bf16[2,512,512]{2,1,0:T(8,128)(2,1)S(1)} collective-permute-done((bf16[2,512,512]{2,1,0:T(8,128)(2,1)S(1)}, bf16[2,512,512]{2,1,0:T(8,128)(2,1)S(1)}, u32[]{:S(2)}, u32[]{:S(2)}) %collective-permute-start.51) | collective-permute-done | bytes 1048608 | tf_op jit(solution)/shard_map/ppermute | solution.py:543
  988.0 11.7 %collective-permute-start.56 = (bf16[256,1024]{1,0:T(8,128)(2,1)}, bf16[256,1024]{1,0:T(8,128)(2,1)S(1)}, u32[]{:S(2)}, u32[]{:S(2)}) collective-permute-start(bf16[256,1024]{1,0:T(8,128)(2,1)} %reduce-scatter.11.cloned.1.call-done), channel_id=1, source_target_pairs={{0,16},{1,17},{2,18},{3,19},{4,20},{5,21},{6,22},{7,23},{8,24},{9,... | collective-permute-start | bytes 1572872 | tf_op jit(solution)/shard_map/ppermute | solution.py:543
  1003.0 7.8 place_quarters.5
  1030.9 7.1 place_quarters.6
  1041.2 18.5 %collective-permute-done.57 = bf16[512,1024]{1,0:T(8,128)(2,1)} collective-permute-done((bf16[512,1024]{1,0:T(8,128)(2,1)}, bf16[512,1024]{1,0:T(8,128)(2,1)}, u32[]{:S(2)}, u32[]{:S(2)}) %collective-permute-start.57) | collective-permute-done | bytes 1048608 | tf_op jit(solution)/shard_map/ppermute | solution.py:543
  1088.0 5.6 place_quarters.9
  (425 shorter events, 323.9 us)
Async XLA Ops:
  8.0 89.1 %all-gather.7.cloned.1.call-start = ((), (), s32[]{:S(2)}) async-start(), calls=%async_computation.6 | async-start | bytes 2621440 | tf_op jit(solution)/shard_map/all_gather | solution.py:665
  10.3 136.5 %all-gather.9.cloned.1.call-start = ((), (), s32[]{:S(2)}) async-start(), calls=%async_computation.7 | async-start | bytes 2621440 | tf_op jit(solution)/shard_map/all_gather | solution.py:665
  12.6 171.7 %all-gather.11.cloned.1.call-start = ((), (), s32[]{:S(2)}) async-start(), calls=%async_computation.8 | async-start | bytes 1310720 | tf_op jit(solution)/shard_map/all_gather | solution.py:665
  13.9 80.9 %collective-permute-start = (bf16[256,2048]{1,0:T(8,128)(2,1)}, bf16[256,2048]{1,0:T(8,128)(2,1)S(1)}, u32[]{:S(2)}, u32[]{:S(2)}) collective-permute-start(bf16[256,2048]{1,0:T(8,128)(2,1)} %get-tuple-element.336), channel_id=1, source_target_pairs={{0,0},{4,1},{1,2},{5,3},{2,4},{6,5},{3,6},{7,7},{8,8},{12,9},{9,10... | collective-permute-start | bytes 3145736 | tf_op jit(solution)/shard_map/ppermute | solution.py:594
  16.0 78.8 %collective-permute-start.1 = (bf16[256,2048]{1,0:T(8,128)(2,1)S(1)}, bf16[256,2048]{1,0:T(8,128)(2,1)S(1)}, u32[]{:S(2)}, u32[]{:S(2)}) collective-permute-start(bf16[256,2048]{1,0:T(8,128)(2,1)S(1)} %get-tuple-element.337), channel_id=1, source_target_pairs={{1,0},{5,1},{0,2},{4,3},{3,4},{7,5},{2,6},{6,7},{9,8},{13,9},{8,10... | collective-permute-start | bytes 3145736 | tf_op jit(solution)/shard_map/ppermute | solution.py:594
  97.1 43.7 %collective-permute-start.2 = (bf16[512,2048]{1,0:T(8,128)(2,1)}, bf16[512,2048]{1,0:T(8,128)(2,1)}, u32[]{:S(2)}, u32[]{:S(2)}) collective-permute-start(bf16[512,2048]{1,0:T(8,128)(2,1)} %maximum_select_fusion.6), channel_id=1, source_target_pairs={{0,8},{1,9},{2,10},{3,11},{4,12},{5,13},{6,14},{7,15},{8,0},{9,1},... | collective-permute-start | bytes 6291464 | tf_op jit(solution)/shard_map/ppermute | solution.py:543
  99.1 138.8 %all-gather.13.cloned.1.call-start = ((), (), s32[]{:S(2)}) async-start(), calls=%async_computation.9 | async-start | bytes 3604480 | tf_op jit(solution)/shard_map/all_gather | solution.py:665
  99.1 47.6 %collective-permute-start.3 = (bf16[1024,1024]{1,0:T(8,128)(2,1)}, bf16[1024,1024]{1,0:T(8,128)(2,1)S(1)}, u32[]{:S(2)}, u32[]{:S(2)}) collective-permute-start(bf16[1024,1024]{1,0:T(8,128)(2,1)} %all-gather.7.cloned.1.call-done.refs_0_.refs_2_.refs_3_), channel_id=1, source_target_pairs={{0,16},{1,17},{2,18},{3,19},{4,20},{5,21},{6,22},{7,23},{8,24},{9,... | collective-permute-start | bytes 6291464 | tf_op jit(solution)/shard_map/ppermute | solution.py:543
  102.8 189.0 %all-gather.15.cloned.1.call-start = ((), (), s32[]{:S(2)}) async-start(), calls=%async_computation.10 | async-start | bytes 3604480 | tf_op jit(solution)/shard_map/all_gather | solution.py:665
  151.5 47.5 %collective-permute-start.5 = (bf16[1024,1024]{1,0:T(8,128)(2,1)}, bf16[1024,1024]{1,0:T(8,128)(2,1)}, u32[]{:S(2)}, u32[]{:S(2)}) collective-permute-start(bf16[1024,1024]{1,0:T(8,128)(2,1)} %all-gather.9.cloned.1.call-done.refs_0_.refs_4_.refs_5_), channel_id=1, source_target_pairs={{0,16},{1,17},{2,18},{3,19},{4,20},{5,21},{6,22},{7,23},{8,24},{9,... | collective-permute-start | bytes 6291464 | tf_op jit(solution)/shard_map/ppermute | solution.py:543
  157.6 322.8 %all-gather.17.cloned.1.call-start = ((), (), s32[]{:S(2)}) async-start(), calls=%async_computation.11 | async-start | bytes 6488064 | tf_op jit(solution)/shard_map/all_gather | solution.py:669
  199.0 38.8 %collective-permute-start.8 = (bf16[1024,512]{1,0:T(8,128)(2,1)}, bf16[1024,512]{1,0:T(8,128)(2,1)}, u32[]{:S(2)}, u32[]{:S(2)}) collective-permute-start(bf16[1024,512]{1,0:T(8,128)(2,1)} %all-gather.11.cloned.1.call-done), channel_id=1, source_target_pairs={{0,16},{1,17},{2,18},{3,19},{4,20},{5,21},{6,22},{7,23},{8,24},{9,... | collective-permute-start | bytes 3145736 | tf_op jit(solution)/shard_map/ppermute | solution.py:543
  237.9 63.2 %collective-permute-start.10 = (bf16[1024,1408]{1,0:T(8,128)(2,1)}, bf16[1024,1408]{1,0:T(8,128)(2,1)}, u32[]{:S(2)}, u32[]{:S(2)}) collective-permute-start(bf16[1024,1408]{1,0:T(8,128)(2,1)} %all-gather.13.cloned.1.call-done.refs_0_.refs_2_.refs_3_), channel_id=1, source_target_pairs={{0,16},{1,17},{2,18},{3,19},{4,20},{5,21},{6,22},{7,23},{8,24},{9,... | collective-permute-start | bytes 8650760 | tf_op jit(solution)/shard_map/ppermute | solution.py:543
  238.1 46.2 %collective-permute-start.9 = (bf16[2048,512]{1,0:T(8,128)(2,1)}, bf16[2048,512]{1,0:T(8,128)(2,1)S(1)}, u32[]{:S(2)}, u32[]{:S(2)}) collective-permute-start(bf16[2048,512]{1,0:T(8,128)(2,1)} %get-tuple-element.168), channel_id=1, source_target_pairs={{0,8},{1,9},{2,10},{3,11},{4,12},{5,13},{6,14},{7,15},{8,0},{9,1},... | collective-permute-start | bytes 6291464 | tf_op jit(solution)/shard_map/ppermute | solution.py:543
  241.8 42.5 %collective-permute-start.12 = (f32[2048]{0:T(1024)S(1)}, f32[2048]{0:T(1024)S(1)}, u32[]{:S(2)}, u32[]{:S(2)}) collective-permute-start(f32[2048]{0:T(1024)S(1)} %add.256), channel_id=1, source_target_pairs={{0,8},{1,9},{2,10},{3,11},{4,12},{5,13},{6,14},{7,15},{8,0},{9,1},... | collective-permute-start | bytes 24584 | tf_op jit(solution)/shard_map/ppermute | solution.py:543
  307.8 68.1 %collective-permute-start.15 = (bf16[1024,1408]{1,0:T(8,128)(2,1)S(1)}, bf16[1024,1408]{1,0:T(8,128)(2,1)S(1)}, u32[]{:S(2)}, u32[]{:S(2)}) collective-permute-start(bf16[1024,1408]{1,0:T(8,128)(2,1)S(1)} %copy-done.20), channel_id=1, source_target_pairs={{0,16},{1,17},{2,18},{3,19},{4,20},{5,21},{6,22},{7,23},{8,24},{9,... | collective-permute-start | bytes 8650760 | tf_op jit(solution)/shard_map/ppermute | solution.py:543
  319.8 53.5 %collective-permute-start.14 = (bf16[2048,512]{1,0:T(8,128)(2,1)}, bf16[2048,512]{1,0:T(8,128)(2,1)S(1)}, u32[]{:S(2)}, u32[]{:S(2)}) collective-permute-start(bf16[2048,512]{1,0:T(8,128)(2,1)} %get-tuple-element.340), channel_id=1, source_target_pairs={{0,8},{1,9},{2,10},{3,11},{4,12},{5,13},{6,14},{7,15},{8,0},{9,1},... | collective-permute-start | bytes 6291464 | tf_op jit(solution)/shard_map/ppermute | solution.py:543
  322.7 48.2 %collective-permute-start.16 = (bf16[256,2048]{1,0:T(8,128)(2,1)S(1)}, bf16[256,2048]{1,0:T(8,128)(2,1)S(1)}, u32[]{:S(2)}, u32[]{:S(2)}) collective-permute-start(bf16[256,2048]{1,0:T(8,128)(2,1)S(1)} %get-tuple-element.332), channel_id=1, source_target_pairs={{0,0},{4,1},{1,2},{5,3},{2,4},{6,5},{3,6},{7,7},{8,8},{12,9},{9,10... | collective-permute-start | bytes 3145736 | tf_op jit(solution)/shard_map/ppermute | solution.py:594
  327.7 43.2 %collective-permute-start.17 = (bf16[256,2048]{1,0:T(8,128)(2,1)S(1)}, bf16[256,2048]{1,0:T(8,128)(2,1)S(1)}, u32[]{:S(2)}, u32[]{:S(2)}) collective-permute-start(bf16[256,2048]{1,0:T(8,128)(2,1)S(1)} %get-tuple-element.333), channel_id=1, source_target_pairs={{1,0},{5,1},{0,2},{4,3},{3,4},{7,5},{2,6},{6,7},{9,8},{13,9},{8,10... | collective-permute-start | bytes 3145736 | tf_op jit(solution)/shard_map/ppermute | solution.py:594
  383.4 232.4 %reduce-scatter.7.cloned.1.call-start = ((), (), s32[]{:S(2)}) async-start(), calls=%async_computation.12 | async-start | bytes 6488064 | tf_op jit(solution)/shard_map/reduce_scatter | solution.py:709
  397.1 47.6 %collective-permute-start.19 = (bf16[512,2048]{1,0:T(8,128)(2,1)}, bf16[512,2048]{1,0:T(8,128)(2,1)S(1)}, u32[]{:S(2)}, u32[]{:S(2)}) collective-permute-start(bf16[512,2048]{1,0:T(8,128)(2,1)} %maximum_select_fusion.8), channel_id=1, source_target_pairs={{0,8},{1,9},{2,10},{3,11},{4,12},{5,13},{6,14},{7,15},{8,0},{9,1},... | collective-permute-start | bytes 6291464 | tf_op jit(solution)/shard_map/ppermute | solution.py:543
  480.5 302.7 %reduce-scatter.9.cloned.1.call-start = ((), (), s32[]{:S(2)}) async-start(), calls=%async_computation.13 | async-start | bytes 6488064 | tf_op jit(solution)/shard_map/reduce_scatter | solution.py:709
  533.9 34.1 %collective-permute-start.22 = (f32[2048]{0:T(1024)S(1)}, f32[2048]{0:T(1024)S(1)}, u32[]{:S(2)}, u32[]{:S(2)}) collective-permute-start(f32[2048]{0:T(1024)S(1)} %reduce.1), channel_id=1, source_target_pairs={{0,4},{1,5},{2,6},{3,7},{4,0},{5,1},{6,2},{7,3},{8,12},{9,13},{10,... | collective-permute-start | bytes 24584 | tf_op jit(solution)/shard_map/ppermute | solution.py:543
  568.1 39.0 %collective-permute-start.25 = (f32[2048]{0:T(1024)S(1)}, f32[2048]{0:T(1024)S(1)}, u32[]{:S(2)}, u32[]{:S(2)}) collective-permute-start(f32[2048]{0:T(1024)S(1)} %add.261), channel_id=1, source_target_pairs={{0,8},{1,9},{2,10},{3,11},{4,12},{5,13},{6,14},{7,15},{8,0},{9,1},... | collective-permute-start | bytes 24584 | tf_op jit(solution)/shard_map/ppermute | solution.py:543
  568.4 47.3 %collective-permute-start.23 = (bf16[2048,512]{1,0:T(8,128)(2,1)}, bf16[2048,512]{1,0:T(8,128)(2,1)}, u32[]{:S(2)}, u32[]{:S(2)}) collective-permute-start(bf16[2048,512]{1,0:T(8,128)(2,1)} %get-tuple-element.200), channel_id=1, source_target_pairs={{0,8},{1,9},{2,10},{3,11},{4,12},{5,13},{6,14},{7,15},{8,0},{9,1},... | collective-permute-start | bytes 6291464 | tf_op jit(solution)/shard_map/ppermute | solution.py:543
  571.5 35.6 %collective-permute-start.24 = (bf16[512,1408]{1,0:T(8,128)(2,1)}, bf16[512,1408]{1,0:T(8,128)(2,1)}, u32[]{:S(2)}, u32[]{:S(2)}) collective-permute-start(bf16[512,1408]{1,0:T(8,128)(2,1)} %get-tuple-element.313), channel_id=1, source_target_pairs={{0,16},{1,17},{2,18},{3,19},{4,20},{5,21},{6,22},{7,23},{8,24},{9,... | collective-permute-start | bytes 4325384 | tf_op jit(solution)/shard_map/ppermute | solution.py:543
  626.6 36.2 %collective-permute-start.27 = (bf16[2048,1024]{1,0:T(8,128)(2,1)}, bf16[2048,1024]{1,0:T(8,128)(2,1)}, u32[]{:S(2)}, u32[]{:S(2)}) collective-permute-start(bf16[2048,1024]{1,0:T(8,128)(2,1)} %fold_half.8), channel_id=1, source_target_pairs={{0,4},{1,5},{2,6},{3,7},{4,0},{5,1},{6,2},{7,3},{8,12},{9,13},{10,... | collective-permute-start | bytes 12582920 | tf_op jit(solution)/shard_map/ppermute | solution.py:543
  626.7 288.6 %reduce-scatter.13.cloned.1.call-start = ((), (), s32[]{:S(2)}) async-start(), calls=%async_computation.15 | async-start | bytes 3604480 | tf_op jit(solution)/shard_map/reduce_scatter | solution.py:703
  662.7 46.4 %collective-permute-start.30 = (bf16[2048,512]{1,0:T(8,128)(2,1)}, bf16[2048,512]{1,0:T(8,128)(2,1)}, u32[]{:S(2)}, u32[]{:S(2)}) collective-permute-start(bf16[2048,512]{1,0:T(8,128)(2,1)} %dynamic-slice_convert_fusion), channel_id=1, source_target_pairs={{0,8},{1,9},{2,10},{3,11},{4,12},{5,13},{6,14},{7,15},{8,0},{9,1},... | collective-permute-start | bytes 6291464 | tf_op jit(solution)/shard_map/ppermute | solution.py:543
  663.9 45.3 %collective-permute-start.31 = (bf16[1024,512]{1,0:T(8,128)(2,1)}, bf16[1024,512]{1,0:T(8,128)(2,1)}, u32[]{:S(2)}, u32[]{:S(2)}) collective-permute-start(bf16[1024,512]{1,0:T(8,128)(2,1)} %get-tuple-element.222), channel_id=1, source_target_pairs={{0,16},{1,17},{2,18},{3,19},{4,20},{5,21},{6,22},{7,23},{8,24},{9,... | collective-permute-start | bytes 3145736 | tf_op jit(solution)/shard_map/ppermute | solution.py:543
  664.2 44.9 %collective-permute-start.32 = (f32[2048]{0:T(1024)S(1)}, f32[2048]{0:T(1024)S(1)}, u32[]{:S(2)}, u32[]{:S(2)}) collective-permute-start(f32[2048]{0:T(1024)S(1)} %add.275), channel_id=1, source_target_pairs={{0,8},{1,9},{2,10},{3,11},{4,12},{5,13},{6,14},{7,15},{8,0},{9,1},... | collective-permute-start | bytes 24584 | tf_op jit(solution)/shard_map/ppermute | solution.py:543
  709.2 41.7 %collective-permute-start.33 = (bf16[512,1408]{1,0:T(8,128)(2,1)S(1)}, bf16[512,1408]{1,0:T(8,128)(2,1)}, u32[]{:S(2)}, u32[]{:S(2)}) collective-permute-start(bf16[512,1408]{1,0:T(8,128)(2,1)S(1)} %copy-done.57), channel_id=1, source_target_pairs={{0,16},{1,17},{2,18},{3,19},{4,20},{5,21},{6,22},{7,23},{8,24},{9,... | collective-permute-start | bytes 4325384 | tf_op jit(solution)/shard_map/ppermute | solution.py:543
  709.9 45.3 %collective-permute-start.34 = (bf16[2048,512]{1,0:T(8,128)(2,1)S(1)}, bf16[2048,512]{1,0:T(8,128)(2,1)}, u32[]{:S(2)}, u32[]{:S(2)}) collective-permute-start(bf16[2048,512]{1,0:T(8,128)(2,1)S(1)} %get-tuple-element.230), channel_id=1, source_target_pairs={{0,8},{1,9},{2,10},{3,11},{4,12},{5,13},{6,14},{7,15},{8,0},{9,1},... | collective-permute-start | bytes 6291464 | tf_op jit(solution)/shard_map/ppermute | solution.py:543
  783.2 139.5 %reduce-scatter.15.cloned.1.call-start = ((), (), s32[]{:S(2)}) async-start(), calls=%async_computation.16 | async-start | bytes 1310720 | tf_op jit(solution)/shard_map/reduce_scatter | solution.py:703
  783.3 30.2 %collective-permute-start.39 = (bf16[512,1408]{1,0:T(8,128)(2,1)}, bf16[512,1408]{1,0:T(8,128)(2,1)}, u32[]{:S(2)}, u32[]{:S(2)}) collective-permute-start(bf16[512,1408]{1,0:T(8,128)(2,1)} %maximum_select_fusion.16), channel_id=1, source_target_pairs={{0,8},{1,9},{2,10},{3,11},{4,12},{5,13},{6,14},{7,15},{8,0},{9,1},... | collective-permute-start | bytes 4325384 | tf_op jit(solution)/shard_map/ppermute | solution.py:543
  821.1 34.2 %collective-permute-start.41 = (bf16[2048,1024]{1,0:T(8,128)(2,1)}, bf16[2048,1024]{1,0:T(8,128)(2,1)}, u32[]{:S(2)}, u32[]{:S(2)}) collective-permute-start(bf16[2048,1024]{1,0:T(8,128)(2,1)} %fold_half.10), channel_id=1, source_target_pairs={{0,4},{1,5},{2,6},{3,7},{4,0},{5,1},{6,2},{7,3},{8,12},{9,13},{10,... | collective-permute-start | bytes 12582920 | tf_op jit(solution)/shard_map/ppermute | solution.py:543
  828.6 156.2 %reduce-scatter.17.cloned.1.call-start = ((), (), s32[]{:S(2)}) async-start(), calls=%async_computation.17 | async-start | bytes 2621440 | tf_op jit(solution)/shard_map/reduce_scatter | solution.py:703
  855.4 132.6 %reduce-scatter.11.cloned.1.call-start = ((), (), s32[]{:S(2)}) async-start(), calls=%async_computation.14 | async-start | bytes 2621440 | tf_op jit(solution)/shard_map/reduce_scatter | solution.py:703
  858.5 32.8 %collective-permute-start.45 = (bf16[512,1408]{1,0:T(8,128)(2,1)}, bf16[512,1408]{1,0:T(8,128)(2,1)}, u32[]{:S(2)}, u32[]{:S(2)}) collective-permute-start(bf16[512,1408]{1,0:T(8,128)(2,1)} %maximum_select_fusion.17), channel_id=1, source_target_pairs={{0,8},{1,9},{2,10},{3,11},{4,12},{5,13},{6,14},{7,15},{8,0},{9,1},... | collective-permute-start | bytes 4325384 | tf_op jit(solution)/shard_map/ppermute | solution.py:543
  865.4 57.3 %collective-permute-start.49 = (bf16[512,2816]{1,0:T(8,128)(2,1)}, bf16[512,2816]{1,0:T(8,128)(2,1)}, u32[]{:S(2)}, u32[]{:S(2)}) collective-permute-start(bf16[512,2816]{1,0:T(8,128)(2,1)} %constant_dynamic-update-slice_fusion.2.refs_0_.refs_1_), channel_id=1, source_target_pairs={{0,4},{1,5},{2,6},{3,7},{4,0},{5,1},{6,2},{7,3},{8,12},{9,13},{10,... | collective-permute-start | bytes 8650760 | tf_op jit(solution)/shard_map/ppermute | solution.py:543
  893.4 53.4 %collective-permute-start.48 = (bf16[512,2816]{1,0:T(8,128)(2,1)S(1)}, bf16[512,2816]{1,0:T(8,128)(2,1)}, u32[]{:S(2)}, u32[]{:S(2)}) collective-permute-start(bf16[512,2816]{1,0:T(8,128)(2,1)S(1)} %pad_maximum_fusion.2.refs_0_.refs_1_), channel_id=1, source_target_pairs={{0,4},{1,5},{2,6},{3,7},{4,0},{5,1},{6,2},{7,3},{8,12},{9,13},{10,... | collective-permute-start | bytes 8650760 | tf_op jit(solution)/shard_map/ppermute | solution.py:543
  899.1 47.7 %collective-permute-start.46 = (bf16[2048,512]{1,0:T(8,128)(2,1)}, bf16[2048,512]{1,0:T(8,128)(2,1)}, u32[]{:S(2)}, u32[]{:S(2)}) collective-permute-start(bf16[2048,512]{1,0:T(8,128)(2,1)} %get-tuple-element.261), channel_id=1, source_target_pairs={{0,8},{1,9},{2,10},{3,11},{4,12},{5,13},{6,14},{7,15},{8,0},{9,1},... | collective-permute-start | bytes 6291464 | tf_op jit(solution)/shard_map/ppermute | solution.py:543
  915.3 31.5 %collective-permute-start.50 = (bf16[256,1408]{1,0:T(8,128)(2,1)}, bf16[256,1408]{1,0:T(8,128)(2,1)}, u32[]{:S(2)}, u32[]{:S(2)}) collective-permute-start(bf16[256,1408]{1,0:T(8,128)(2,1)} %reduce-scatter.13.cloned.1.call-done), channel_id=1, source_target_pairs={{0,16},{1,17},{2,18},{3,19},{4,20},{5,21},{6,22},{7,23},{8,24},{9,... | collective-permute-start | bytes 2162696 | tf_op jit(solution)/shard_map/ppermute | solution.py:543
  1003.0 38.2 %collective-permute-start.58 = (bf16[512,1408]{1,0:T(8,128)(2,1)}, bf16[512,1408]{1,0:T(8,128)(2,1)}, u32[]{:S(2)}, u32[]{:S(2)}) collective-permute-start(bf16[512,1408]{1,0:T(8,128)(2,1)} %maximum_select_fusion.18), channel_id=1, source_target_pairs={{0,8},{1,9},{2,10},{3,11},{4,12},{5,13},{6,14},{7,15},{8,0},{9,1},... | collective-permute-start | bytes 4325384 | tf_op jit(solution)/shard_map/ppermute | solution.py:543
  1013.8 45.9 %collective-permute-start.57 = (bf16[512,1024]{1,0:T(8,128)(2,1)}, bf16[512,1024]{1,0:T(8,128)(2,1)}, u32[]{:S(2)}, u32[]{:S(2)}) collective-permute-start(bf16[512,1024]{1,0:T(8,128)(2,1)} %maximum_select_fusion.21), channel_id=1, source_target_pairs={{0,8},{1,9},{2,10},{3,11},{4,12},{5,13},{6,14},{7,15},{8,0},{9,1},... | collective-permute-start | bytes 3145736 | tf_op jit(solution)/shard_map/ppermute | solution.py:543
  1017.3 47.7 %collective-permute-start.59 = (bf16[256,3072]{1,0:T(8,128)(2,1)}, bf16[256,3072]{1,0:T(8,128)(2,1)}, u32[]{:S(2)}, u32[]{:S(2)}) collective-permute-start(bf16[256,3072]{1,0:T(8,128)(2,1)} %constant_dynamic-update-slice_fusion.4), channel_id=1, source_target_pairs={{0,16},{1,17},{2,18},{3,19},{4,20},{5,21},{6,22},{7,23},{8,24},{9,... | collective-permute-start | bytes 4718600 | tf_op jit(solution)/shard_map/ppermute | solution.py:543
  1026.9 32.8 %collective-permute-start.61 = (bf16[256,2048]{1,0:T(8,128)(2,1)}, bf16[256,2048]{1,0:T(8,128)(2,1)}, u32[]{:S(2)}, u32[]{:S(2)}) collective-permute-start(bf16[256,2048]{1,0:T(8,128)(2,1)} %get-tuple-element.314), channel_id=1, source_target_pairs={{0,1},{1,5},{2,0},{3,4},{4,3},{5,7},{6,2},{7,6},{8,9},{9,13},{10,8... | collective-permute-start | bytes 3145736 | tf_op jit(solution)/shard_map/ppermute | solution.py:606
  1028.7 36.3 %collective-permute-start.60 = (bf16[256,2048]{1,0:T(8,128)(2,1)}, bf16[256,2048]{1,0:T(8,128)(2,1)}, u32[]{:S(2)}, u32[]{:S(2)}) collective-permute-start(bf16[256,2048]{1,0:T(8,128)(2,1)} %get-tuple-element.315), channel_id=1, source_target_pairs={{0,0},{1,4},{2,1},{3,5},{4,2},{5,6},{6,3},{7,7},{8,8},{9,12},{10,9... | collective-permute-start | bytes 3145736 | tf_op jit(solution)/shard_map/ppermute | solution.py:606
  (107 other events, 1890.0 us)
Sparse Core Ops, SparseCore 0:
  11.0 82.9 all-gather.6
  96.1 46.0 all-gather.8
  144.4 27.5 all-gather.10
  174.0 57.9 all-gather.12
  233.9 57.8 all-gather.14
  783.3 58.6 reduce-scatter.12
  844.3 25.7 reduce-scatter.14
  872.5 43.1 reduce-scatter.16
  918.6 44.4 reduce-scatter.10
Sparse Core Ops, SparseCore 1:
  383.4 88.8 all-gather.16
  480.6 107.6 reduce-scatter.6
  626.8 126.3 reduce-scatter.8
